TPU v7x, 128 devices: a whole 4x4x4 slice. The times are simulated.
128 devices in a mesh: context: 32 (over z_hi, x, y), tensor: 4 (over z_lo, core).
Axes of the slice: x: 4, y: 4, z: 4 (z_hi: 2, z_lo: 2; z = z_hi * 2 + z_lo), core: 2. Of those that a mesh axis runs over, the one named last changes fastest.
Arguments:
- activations: bfloat16 [16384, 3072], P('context', 'tensor'), may hold values from -6 to 6
- qkv_weight: bfloat16 [3072, 3, 4096], P(None, None, 'tensor'), may hold values from -0.109375 to 0.109375
- log_decay: float32 [16384, 32], P('context', 'tensor'), may hold values from -1.5 to 0, as said below
- lengths: int32 [32], P('context'), may hold values from 256 to 512, as said below
- out_grad: bfloat16 [16384, 4096], P('context', 'tensor'), may hold values from -0.00036621094 to 0.00036621094
Outputs:
- weight_grad: float32 [3072, 3, 4096], P('context', None, 'tensor')
Inputs may be any that keep to these rules, and one draw needn't show every extreme that they name: `log_decay`: Negative; entries vary from token to token. `lengths`: each entry is a multiple of 256; the live tokens are the first slots of their shard; in every draw at least one shard is full.
All inputs are finite; a program needn't handle non-finite values.
Results may differ from a plain program's by a relative error of at most 0.015.
Values may be sent and summed in bfloat16 or wider, within the bound.
No kernel may reach another device: no remote copies, remote signals or barrier semaphores. Data moves between devices by JAX's collectives and lax.ppermute only.
A program may use at most 128 MiB of HBM per device.

v0:
```python
import jax
import jax.numpy as jnp
from jax import lax
from jax.sharding import Mesh
from jax.sharding import PartitionSpec as P

CONTEXT = ("context_0", "context_1", "context_2")


def nothing_yet(x, identity):
    return jax.tree.map(
        lambda a, e: jnp.broadcast_to(jnp.asarray(e, a.dtype), a.shape), x, identity
    )


def entering(x, axes, combine, identity, reverse):
    before = start = nothing_yet(x, identity)
    total = x
    for axis in reversed(axes):
        peers, here = (lax.axis_size(axis), lax.axis_index(axis))
        pieces = jax.tree.map(
            lambda part, kind: lax.all_gather(part.astype(kind), axis),
            total,
            (jnp.bfloat16, jnp.bfloat16),
        )
        inside, total = (start, start)
        for k in reversed(range(peers)) if reverse else range(peers):
            passed = k > here if reverse else k < here
            total = combine(
                total, jax.tree.map(lambda part, own: part[k].astype(own.dtype), pieces, x)
            )
            inside = jax.tree.map(lambda new, old: jnp.where(passed, new, old), total, inside)
        before = combine(inside, before)
    return before


def own_block(pieces, axes, sequence):
    inside = pieces.shape[1:]
    pieces = pieces.reshape(*(lax.axis_size(a) for a in axes), *inside)
    pieces = jnp.moveaxis(pieces, sequence, range(len(axes))).reshape(-1, *inside)
    for k in sequence:
        pieces = lax.psum_scatter(pieces, axes[k], scatter_dimension=0, tiled=True)
    return pieces[0]


def in_blocks(x, dim, peers):
    lengths = x.shape
    pieces = x.reshape(*lengths[:dim], peers, lengths[dim] // peers, *lengths[dim + 1 :])
    return jnp.moveaxis(pieces, dim, 0)


def sum_by_axis(x, axes, sequence, dim):
    peers = lax.axis_size(axes)
    return own_block(in_blocks(x, dim, peers), axes, sequence)


def combine_pair(earlier, later):
    return (earlier[0] + later[0], jnp.exp(later[0])[:, None, None] * earlier[1] + later[1])


def shards(activations, qkv_weight, log_decay, lengths, out_grad):
    features_all = lax.all_gather(activations, "tensor", axis=1, tiled=True)
    tokens = features_all.shape[0]
    head_count = log_decay.shape[1]
    col_width = out_grad.shape[1]
    head_dim = col_width // head_count
    score_scale_factor = head_dim ** (-0.5)
    token_position = jnp.arange(tokens, dtype=jnp.int32)
    is_live = (token_position < lengths[0]).astype(jnp.float32)
    projected = jnp.dot(
        features_all,
        qkv_weight.reshape(qkv_weight.shape[0], 3 * col_width),
        preferred_element_type=jnp.float32,
    ).astype(jnp.bfloat16)
    projected = (projected * is_live.astype(jnp.bfloat16)[:, None]).reshape(
        tokens, 3, head_count, head_dim
    )
    query_rows = projected[:, 0]
    key_matrix_rows = projected[:, 1]
    value_matrix_rows = projected[:, 2]
    output_gradient = out_grad.reshape(tokens, head_count, head_dim)
    run_sum = jnp.cumsum(log_decay * is_live[:, None], axis=0)
    shard_sum = run_sum[-1]
    until_finish = jnp.exp(shard_sum[None, :] - run_sum)
    since_beginning = jnp.exp(run_sum)
    decayed_key_rows = (key_matrix_rows.astype(jnp.float32) * until_finish[:, :, None]).astype(
        jnp.bfloat16
    )
    partition_state = jnp.einsum(
        "jla,jlu->lau", decayed_key_rows, value_matrix_rows, preferred_element_type=jnp.float32
    ).astype(jnp.bfloat16)
    decayed_query_rows = (
        query_rows.astype(jnp.float32) * (score_scale_factor * since_beginning)[:, :, None]
    ).astype(jnp.bfloat16)
    state_gradient = jnp.einsum(
        "jla,jlu->lau", decayed_query_rows, output_gradient, preferred_element_type=jnp.float32
    ).astype(jnp.bfloat16)
    shard_total = shard_sum.astype(jnp.bfloat16)
    shard_decay = shard_total.astype(jnp.float32)
    identity_pair = (jnp.zeros_like(shard_decay), jnp.zeros(partition_state.shape, jnp.float32))
    incoming = entering(
        (shard_decay, partition_state.astype(jnp.float32)),
        CONTEXT,
        combine_pair,
        identity_pair,
        False,
    )[1]
    from_later = entering(
        (shard_decay, state_gradient.astype(jnp.float32)),
        CONTEXT,
        combine_pair,
        identity_pair,
        True,
    )[1]
    causal = token_position[:, None] >= token_position[None, :]
    gap_matrix = run_sum.T[:, :, None] - run_sum.T[:, None, :]
    decay_matrix = jnp.exp(jnp.where(causal[None], gap_matrix, -jnp.inf))
    prob_matrix = (
        jnp.einsum("thd,shd->hts", query_rows, key_matrix_rows, preferred_element_type=jnp.float32)
        * score_scale_factor
        * decay_matrix
    ).astype(jnp.bfloat16)
    grad_score = (
        jnp.einsum(
            "thd,shd->hts", output_gradient, value_matrix_rows, preferred_element_type=jnp.float32
        )
        * decay_matrix
    ).astype(jnp.bfloat16)
    arriving_rounded = incoming.astype(jnp.bfloat16)
    subsequent_rounded = from_later.astype(jnp.bfloat16)
    query_gradient = score_scale_factor * (
        jnp.einsum("zmb,bzw->mzw", grad_score, key_matrix_rows, preferred_element_type=jnp.float32)
        + since_beginning[:, :, None]
        * jnp.einsum(
            "bzf,zof->bzo", output_gradient, arriving_rounded, preferred_element_type=jnp.float32
        )
    )
    key_gradient = score_scale_factor * jnp.einsum(
        "rvz,vrj->zrj", grad_score, query_rows, preferred_element_type=jnp.float32
    ) + until_finish[:, :, None] * jnp.einsum(
        "bzf,zof->bzo", value_matrix_rows, subsequent_rounded, preferred_element_type=jnp.float32
    )
    value_gradient = jnp.einsum(
        "rvz,vrj->zrj", prob_matrix, output_gradient, preferred_element_type=jnp.float32
    ) + until_finish[:, :, None] * jnp.einsum(
        "cnf,nfg->cng", key_matrix_rows, subsequent_rounded, preferred_element_type=jnp.float32
    )
    stacked = (
        jnp.stack([query_gradient, key_gradient, value_gradient], axis=1)
        * is_live[:, None, None, None]
    )
    qkv_grad = stacked.astype(jnp.bfloat16).reshape(tokens, 3 * col_width)
    rows_owned = qkv_weight.shape[0] // lax.axis_size(CONTEXT)
    weight_grad = sum_by_axis(
        jnp.einsum("td,tc->dc", features_all, qkv_grad, preferred_element_type=jnp.float32).astype(
            jnp.bfloat16
        ),
        CONTEXT,
        (1, 2, 0),
        0,
    ).astype(jnp.float32)
    return weight_grad.reshape(rows_owned, 3, col_width)


def solution(mesh):
    finer = Mesh(
        mesh.devices.reshape(2, 4, 4, mesh.shape["tensor"]),
        ("context_0", "context_1", "context_2", "tensor"),
    )
    placed = (
        P(CONTEXT, "tensor"),
        P(None, None, "tensor"),
        P(CONTEXT, "tensor"),
        P(CONTEXT),
        P(CONTEXT, "tensor"),
    )
    return jax.shard_map(
        shards, mesh=finer, in_specs=placed, out_specs=P(CONTEXT, None, "tensor"), check_vma=False
    )
```

profile of v0, /device:TPU:0, one launch (start us, length us, event | category | flops | bytes accessed | tf_op | source)
XLA Modules:
  0.0 495.0 jit_solution(3437501244132528728)
XLA Ops:
  6.5 0.7 all-gather.13.cloned.1.call-update
  8.0 0.7 multiply_bitcast_fusion
  8.7 1.1 reduce-window.6
  10.0 24.7 %copy.56 = bf16[3072,3,1024]{0,2,1:T(8,128)(2,1)} copy(bf16[3072,3,1024]{2,0,1:T(8,128)(2,1)} %param.6) | data formatting | bytes 37748736 | tf_op args[1]
  35.1 14.0 %all-gather.13.cloned.1.call-done = bf16[512,3072]{1,0:T(8,128)(2,1)} async-done(((bf16[512,768]{1,0:T(8,128)(2,1)}), bf16[512,3072]{1,0:T(8,128)(2,1)}) %all-gather.13.cloned.1.call-update) | async-done | bytes 3145744 | tf_op jit(solution)/shard_map/all_gather | solution.py:62
  49.0 14.8 %fusion.14 = bf16[64,8,24,128]{3,1,2,0:T(8,128)(2,1)S(1)} fusion(bf16[512,3072]{1,0:T(8,128)(2,1)} %all-gather.13.cloned.1.call-done, bf16[3072,3072]{0,1:T(8,128)(2,1)} %bitcast.462, bf16[512]{0:T(512)(128)(2,1)S(1)} %get-tuple-element.41), kind=kOutput, calls=%fused_computation.25 | convolution fusion | flops 9666822144 | bytes 25166848 | tf_op jit(solution)/shard_map/dot_general | solution.py:70
  63.9 0.9 copy.86
  64.8 1.5 fusion.166
  66.3 0.7 copy.82
  67.0 2.5 convolution_convert_fusion.3
  69.5 1.3 copy.85
  70.9 0.7 copy.84
  71.6 2.8 convolution_convert_fusion.2
  74.6 9.6 %all-gather.2 = bf16[4,1,8]{2,1,0:T(2,128)(2,1)S(1)} all-gather(bf16[1,1,8]{2,1,0:T(2,128)(2,1)S(1)} %bitcast.469), channel_id=1, replica_groups=mesh['context_0'=2,'context_1'=4,'context_2'=4,'tensor'=4] {'context_2'}, dimensions={0}, use_global_device_ids=true | all-gather | bytes 80 | tf_op jit(solution)/shard_map/all_gather | solution.py:22
  84.3 9.6 %all-gather.3 = bf16[4,1,8]{2,1,0:T(2,128)(2,1)S(1)} all-gather(bf16[1,1,8]{2,1,0:T(2,128)(2,1)S(1)} %get-tuple-element.25), channel_id=1, replica_groups=mesh['context_0'=2,'context_1'=4,'context_2'=4,'tensor'=4] {'context_1'}, dimensions={0}, use_global_device_ids=true | all-gather | bytes 80 | tf_op jit(solution)/shard_map/all_gather | solution.py:22
  93.9 6.9 %all-gather.5 = bf16[4,1,8]{2,1,0:T(2,128)(2,1)S(1)} all-gather(bf16[1,1,8]{2,1,0:T(2,128)(2,1)S(1)} %get-tuple-element.26), channel_id=1, replica_groups=mesh['context_0'=2,'context_1'=4,'context_2'=4,'tensor'=4] {'context_1'}, dimensions={0}, use_global_device_ids=true | all-gather | bytes 80 | tf_op jit(solution)/shard_map/all_gather | solution.py:22
  100.8 0.6 fusion.157
  101.4 19.4 %all-gather.21.cloned.1.call-done = bf16[32,128,128]{2,1,0:T(8,128)(2,1)} async-done(((bf16[8,128,128]{2,1,0:T(8,128)(2,1)}), bf16[32,128,128]{2,1,0:T(8,128)(2,1)}) %all-gather.21.cloned.1.call-update) | async-done | bytes 1048592 | tf_op jit(solution)/shard_map/all_gather | solution.py:22
  120.8 3.0 fusion.82
  123.9 5.7 %all-gather.4 = bf16[2,1,8]{2,1,0:T(2,128)(2,1)S(1)} all-gather(bf16[1,1,8]{2,1,0:T(2,128)(2,1)S(1)} %get-tuple-element.16), channel_id=1, replica_groups=mesh['context_0'=2,'context_1'=4,'context_2'=4,'tensor'=4] {'context_0'}, dimensions={0}, use_global_device_ids=true | all-gather | bytes 48 | tf_op jit(solution)/shard_map/all_gather | solution.py:22
  129.6 5.7 %all-gather.6 = bf16[2,1,8]{2,1,0:T(2,128)(2,1)S(1)} all-gather(bf16[1,1,8]{2,1,0:T(2,128)(2,1)S(1)} %get-tuple-element.27), channel_id=1, replica_groups=mesh['context_0'=2,'context_1'=4,'context_2'=4,'tensor'=4] {'context_0'}, dimensions={0}, use_global_device_ids=true | all-gather | bytes 48 | tf_op jit(solution)/shard_map/all_gather | solution.py:22
  135.4 0.6 exp.199
  136.0 0.5 exp.211
  136.6 0.7 fusion.150
  137.7 3.6 fusion
  141.3 1.5 fusion.18
  142.8 2.1 fusion.25
  144.9 3.4 all-gather.17.cloned.1.call-done
  148.2 1.6 fusion.73
  149.8 9.5 %all_gather.66 = bf16[2,8,128,128]{3,2,1,0:T(8,128)(2,1)} all-gather(bf16[1,8,128,128]{3,2,1,0:T(8,128)(2,1)S(1)} %fusion.73), channel_id=1, replica_groups=mesh['context_0'=2,'context_1'=4,'context_2'=4,'tensor'=4] {'context_0'}, dimensions={0}, use_global_device_ids=true | all-gather | bytes 786432 | tf_op jit(solution)/shard_map/all_gather | solution.py:22
  159.3 14.8 %all-gather.15.cloned.1.call-done = bf16[4,8,128,128]{3,2,1,0:T(8,128)(2,1)} async-done(((bf16[1,8,128,128]{3,2,1,0:T(8,128)(2,1)}), bf16[4,8,128,128]{3,2,1,0:T(8,128)(2,1)}) %all-gather.15.cloned.1.call-update) | async-done | bytes 1048592 | tf_op jit(solution)/shard_map/all_gather | solution.py:22
  174.1 1.6 fusion.58
  175.7 9.4 %all_gather.60 = bf16[2,8,128,128]{3,2,1,0:T(8,128)(2,1)} all-gather(bf16[1,8,128,128]{3,2,1,0:T(8,128)(2,1)S(1)} %fusion.58), channel_id=1, replica_groups=mesh['context_0'=2,'context_1'=4,'context_2'=4,'tensor'=4] {'context_0'}, dimensions={0}, use_global_device_ids=true | all-gather | bytes 786432 | tf_op jit(solution)/shard_map/all_gather | solution.py:22
  185.1 3.2 fusion.38
  188.3 1.8 fusion.20
  190.1 7.8 %fusion.8 = f32[512,1,8,128]{0,3,2,1:T(8,128)} fusion(f32[8,128,512]{2,1,0:T(8,128)} %fusion.20, bf16[512,8,128]{0,2,1:T(8,128)(2,1)} %bitcast.467, f32[8,512]{1,0:T(8,128)S(1)} %add_bitcast_fusion.1, pred[512,512]{0,1:T(8,128)(4,1)} %copy-done.8, bf16[512,1,8,128]{0,3,2,1:T(8,128)(2,1)} %copy-done, bf16[512,1,8,128]{0,3,2,1:T(8,128)(2,1)S(1)} %copy.82, ...), kind=kOutput, calls=%fused_computation.15 | convolution fusion | flops 1085276160 | bytes 7634944 | tf_op jit(solution)/shard_map/rvz,vrj->zrj/dot_general | solution.py:143
  197.9 1.9 fusion.10
  199.8 0.2 copy-done.6
  200.2 2.7 fusion.13
  202.9 1.1 pad_maximum_fusion
  204.0 0.9 fusion.1
  204.9 15.4 %convolution_convert_fusion = bf16[3072,3072]{0,1:T(8,128)(2,1)} fusion(bf16[512,3072]{0,1:T(8,128)(2,1)S(1)} %fusion.1, bf16[512,3072]{1,0:T(8,128)(2,1)} %all-gather.13.cloned.1.call-done), kind=kOutput, calls=%fused_computation | convolution fusion | flops 9673113600 | bytes 25165824 | tf_op jit(solution)/shard_map/td,tc->dc/dot_general | solution.py:155
  220.3 17.2 %copy.72 = bf16[2,4,4,96,3072]{4,3,0,2,1:T(8,128)(2,1)} copy(bf16[2,4,4,96,3072]{4,3,2,1,0:T(8,128)(2,1)} %bitcast.463) | data formatting | bytes 37748736 | tf_op jit(solution)/shard_map/reshape;reshape | solution.py:39
  237.6 165.3 %reduce-scatter.4.cloned.1.call-done = bf16[8,96,3072]{2,1,0:T(8,128)(2,1)} async-done(((bf16[32,96,3072]{2,1,0:T(8,128)(2,1)}), bf16[8,96,3072]{2,1,0:T(8,128)(2,1)}) %reduce-scatter.4.cloned.1.call-update) | async-done | bytes 4718608 | tf_op jit(solution)/shard_map/reduce_scatter | solution.py:42
  403.0 53.4 %reduce-scatter.6.cloned.1.call-done = bf16[2,96,3072]{2,1,0:T(8,128)(2,1)} async-done(((bf16[8,96,3072]{2,1,0:T(8,128)(2,1)}), bf16[2,96,3072]{2,1,0:T(8,128)(2,1)}) %reduce-scatter.6.cloned.1.call-update) | async-done | bytes 1179664 | tf_op jit(solution)/shard_map/reduce_scatter | solution.py:42
  456.4 28.1 %reduce-scatter.8.cloned.1.call-done = bf16[1,96,3072]{2,1,0:T(8,128)(2,1)} async-done(((bf16[2,96,3072]{2,1,0:T(8,128)(2,1)}), bf16[1,96,3072]{2,1,0:T(8,128)(2,1)}) %reduce-scatter.8.cloned.1.call-update) | async-done | bytes 589840 | tf_op jit(solution)/shard_map/reduce_scatter | solution.py:42
  484.5 2.0 reshape.413
  486.5 1.7 copy.73
  (60 shorter events, 1.7 us)
Async XLA Ops:
  6.5 42.5 %all-gather.13.cloned.1.call-start = ((), (), s32[]{:S(2)}) async-start(), calls=%async_computation.3 | async-start | bytes 3932160 | tf_op jit(solution)/shard_map/all_gather | solution.py:62
  7.3 94.2 %all-gather.19.cloned.1.call-start = ((), (), s32[]{:S(2)}) async-start(), calls=%async_computation.9 | async-start | bytes 1310720 | tf_op jit(solution)/shard_map/all_gather | solution.py:22
  66.9 2.6 copy-start.5
  69.5 51.4 %all-gather.21.cloned.1.call-start = ((), (), s32[]{:S(2)}) async-start(), calls=%async_computation.10 | async-start | bytes 1310720 | tf_op jit(solution)/shard_map/all_gather | solution.py:22
  71.6 65.8 %copy-start = (bf16[512,1,8,128]{0,3,2,1:T(8,128)(2,1)}, bf16[512,1,8,128]{0,3,2,1:T(8,128)(2,1)S(1)}, u32[]{:S(2)}) copy-start(bf16[512,1,8,128]{0,3,2,1:T(8,128)(2,1)S(1)} %copy.84) | copy-start | bytes 3145732
  71.6 66.1 %copy-start.2 = (bf16[512,1,8,128]{3,2,1,0:T(8,128)(2,1)S(1)}, bf16[512,1,8,128]{3,2,1,0:T(8,128)(2,1)}, u32[]{:S(2)}) copy-start(bf16[512,1,8,128]{3,2,1,0:T(8,128)(2,1)} %get-tuple-element.11) | copy-start | bytes 3145732
  74.4 73.8 %all-gather.17.cloned.1.call-start = ((), (), s32[]{:S(2)}) async-start(), calls=%async_computation.5 | async-start | bytes 1310720 | tf_op jit(solution)/shard_map/all_gather | solution.py:22
  123.8 50.2 %all-gather.15.cloned.1.call-start = ((), (), s32[]{:S(2)}) async-start(), calls=%async_computation.4 | async-start | bytes 1310720 | tf_op jit(solution)/shard_map/all_gather | solution.py:22
  136.6 4.7 copy-start.8
  137.4 265.5 %reduce-scatter.4.cloned.1.call-start = ((), (), s32[]{:S(2)}) async-start(), calls=%async_computation.6 | async-start | bytes 23592960 | tf_op jit(solution)/shard_map/reduce_scatter | solution.py:42
  137.7 3.7 copy-start.1
  144.9 40.2 %copy-start.9 = (f32[8]{0:T(128)S(1)}, f32[8]{0:T(128)}, u32[]{:S(2)}) copy-start(f32[8]{0:T(128)} %exp.211) | copy-start | bytes 100
  197.8 1.9 copy-start.3
  197.8 2.2 copy-start.6
  197.8 2.3 copy-start.7
  197.8 2.3 copy-start.10
  197.8 2.3 copy-start.11
  197.9 2.3 copy-start.12
  197.9 2.3 copy-start.13
  200.1 2.8 copy-start.4
  237.5 218.8 %reduce-scatter.6.cloned.1.call-start = ((), (), s32[]{:S(2)}) async-start(), calls=%async_computation.7 | async-start | bytes 5898240 | tf_op jit(solution)/shard_map/reduce_scatter | solution.py:42
  402.9 81.6 %reduce-scatter.8.cloned.1.call-start = ((), (), s32[]{:S(2)}) async-start(), calls=%async_computation.8 | async-start | bytes 1769472 | tf_op jit(solution)/shard_map/reduce_scatter | solution.py:42
Sparse Core Ops, SparseCore 0:
  9.0 39.9 all-gather.12
  69.6 25.1 all-gather.18
  96.5 24.2 all-gather.20
  124.0 24.2 all-gather.16
  149.7 24.2 all-gather.14
  237.6 165.2 reduce-scatter.3
  405.4 50.8 reduce-scatter.5
  458.8 25.6 reduce-scatter.7
where the time goes:
time: 497 us; the launch traced here: 495 us
  waiting for transfers between devices  299 us (60%)
  matrix products  56.9 us (11%)
  blocking collectives  56.5 us (11%)
  local copies, waits for them, and re-layouts  52.7 us (11%)
  other arithmetic  14.9 us (3%)
  between operations  14.4 us (3%)
    reduce_scatter x3, waiting for transfers between devices, own_block(): pieces = lax.psum_scatter(pieces, axes[k], scatter_dimension=0, tiled=True)  247 us
    all_gather x7, blocking collectives, entering(): lax.all_gather(part.astype(kind), axis)  56.5 us
    all_gather x4, waiting for transfers between devices, entering(): lax.all_gather(part.astype(kind), axis)  37.6 us
    unnamed x32, local copies, waits for them, and re-layouts  27.3 us
    another operation x1, local copies, waits for them, and re-layouts, own_block(): pieces = pieces.reshape(*(lax.axis_size(a) for a in axes), *inside)  17.2 us
    dot_general x1, matrix products, shards(): jnp.einsum('td,tc->dc', features_all, qkv_grad, preferred_element_type=jn...  15.4 us
    dot_general x1, matrix products, shards(): jnp.dot(features_all, qkv_weight.reshape(qkv_weight.shape[0], 3 * col_wid...  14.8 us
    all_gather x1, waiting for transfers between devices, shards(): features_all = lax.all_gather(activations, 'tensor', axis=1, tiled=True)  14 us
  transfers between devices with their start and end apart: 8, of which 7 were waited for; matrix products, arithmetic and copies ran while one was open for 9% of the time, Pallas kernels for 0%

commit v1 on v0

v1 whole, which is shorter than its diff:
```python
import jax
import jax.numpy as jnp
from jax import lax
from jax.experimental import pallas as pl
from jax.experimental.pallas import tpu as pltpu
from jax.sharding import Mesh
from jax.sharding import PartitionSpec as P

F32 = jnp.float32
BF16 = jnp.bfloat16
HEAD = 128
Z, X, Y, ZL, CO, TEN, LEN = range(7)
AB_T = (((1,), (1,)), ((), ()))
A_TB = (((0,), (0,)), ((), ()))


def dot(a, b):
    return jnp.dot(a, b, preferred_element_type=F32)


def shift(axis, by):
    n = lax.axis_size(axis)
    return [(i, (i + by) % n) for i in range(n)]


def send(x, axis, by):
    return lax.ppermute(x, axis, shift(axis, by))


def across(x):
    return lax.ppermute(x, ("c0", "zl"), [(0, 3), (1, 2), (2, 1), (3, 0)])


def whole(x):
    return pl.BlockSpec(x.shape, lambda *_, n=len(x.shape): (0,) * n)


def call(name, body, table, grid, operands, in_specs, outs, out_specs, mib, scratch=(), alias=None):
    return pl.pallas_call(
        body,
        grid_spec=pltpu.PrefetchScalarGridSpec(
            num_scalar_prefetch=1,
            grid=grid,
            in_specs=in_specs,
            out_specs=out_specs,
            scratch_shapes=scratch,
        ),
        out_shape=outs,
        input_output_aliases=alias or {},
        compiler_params=pltpu.CompilerParams(
            dimension_semantics=("arbitrary",) * len(grid), vmem_limit_bytes=mib << 20
        ),
        cost_estimate=pl.CostEstimate(flops=1, bytes_accessed=1, transcendentals=0),
        name=name,
    )(table, *operands)


def shape(dims, kind=BF16):
    return jax.ShapeDtypeStruct(dims, kind)


def project(table, shards, flips, weight, partial, last):
    n = len(shards)
    tokens, width = shards[0].shape
    cols = weight.shape[2] // 2

    def body(s, *refs):
        out = refs[-1]
        acc = dot(refs[0][...], refs[n][0])
        for i in range(1, n):
            acc += dot(refs[i][...], refs[n + i][0])
        if partial is not None:
            acc += refs[2 * n][0]
        if last:
            row = lax.broadcasted_iota(jnp.int32, acc.shape, 0)
            acc = jnp.where(row < s[LEN], acc, 0.0)
        out[0] = acc.astype(out.dtype)

    tile = pl.BlockSpec((1, tokens, cols), lambda g, s: (g, 0, 0))
    in_specs = [whole(x) for x in shards]
    for flip in flips:
        in_specs.append(
            pl.BlockSpec((1, width, cols), lambda g, s, flip=flip: (g, s[TEN] ^ flip, s[Z]))
        )
    operands = [*shards, *([weight] * n)]
    if partial is not None:
        in_specs.append(tile)
        operands.append(partial)
    out = shape((3, tokens, cols), BF16 if last else F32)
    return call("project", body, table, (3,), operands, in_specs, out, tile, 20)


def shard_states(table, qkvs, out_grads, cumul):
    tokens = qkvs[0].shape[1]
    heads = qkvs[0].shape[2] // HEAD
    scale = HEAD**-0.5

    def body(s, qkv_a, qkv_b, og_a, og_b, cum_ref, *outs):
        r = pl.program_id(0)
        who = (s[Y] + r) % 4
        blocks, totals = [], []
        for i, (qkv_ref, og_ref) in enumerate(((qkv_a, og_a), (qkv_b, og_b))):
            row = cum_ref[pl.ds(i * heads + who, 1), :]
            total = row[:, tokens - 1 : tokens]
            keys_t = qkv_ref[1].astype(F32).T
            query_t = qkv_ref[0].astype(F32).T
            keys_t = (keys_t * jnp.exp(total - row)).astype(BF16)
            query_t = (query_t * (scale * jnp.exp(row))).astype(BF16)
            blocks.append((dot(keys_t, qkv_ref[2]), dot(query_t, og_ref[...])))
            totals.append(total)
        at = lax.broadcasted_iota(jnp.int32, (16, HEAD), 0)
        tail = jnp.where(at == s[Z], totals[0], totals[1]).astype(BF16)
        for k, out in enumerate(outs):

            @pl.when(r == k)
            def _(out=out):
                for i in range(2):
                    for kind in range(2):
                        start = pl.multiple_of((2 * kind + (i ^ s[Z])) * HEAD, HEAD)
                        out[pl.ds(start, HEAD), :] = blocks[i][kind].astype(BF16)
                out[4 * HEAD :, :] = tail

    message = shape((4 * HEAD + 16, HEAD))
    qkv_tile = pl.BlockSpec((3, tokens, HEAD), lambda r, s: (0, 0, (s[Y] + r) % 4))
    og_tile = pl.BlockSpec((tokens, HEAD), lambda r, s: (0, (s[Y] + r) % 4))
    return call(
        "shard_states",
        body,
        table,
        (4,),
        (*qkvs, *out_grads, cumul),
        [qkv_tile, qkv_tile, og_tile, og_tile, whole(cumul)],
        [message] * 4,
        [whole(message)] * 4,
        12,
    )


def in_order(refs, place, held):
    for r, ref in enumerate(refs):
        held[(place - r + 4) % 4] = ref[...]


def spread(pair):
    wide = [jnp.broadcast_to(pair[i : i + 1, :], (HEAD, HEAD)) for i in range(2)]
    return jnp.concatenate(wide, axis=0)


def ring_y(table, messages):
    half = 2 * HEAD

    def body(s, a, b, c, d, before, after, prior, later, out, held):
        in_order((a, b, c, d), s[Y], held)
        totals = [held[t, 2 * half : 2 * half + 16, :].astype(F32)[:2] for t in range(4)]
        run = jnp.zeros((half, HEAD), F32)
        reach = jnp.zeros((2, HEAD), F32)
        for t in range(4):
            before[t] = run
            prior[t] = jnp.exp(reach)
            run = spread(jnp.exp(totals[t])) * run + held[t, :half, :].astype(F32)
            reach = reach + totals[t]
        out[:half, :] = run.astype(BF16)
        total = reach
        run = jnp.zeros((half, HEAD), F32)
        reach = jnp.zeros((2, HEAD), F32)
        for t in range(3, -1, -1):
            after[t] = run
            later[t] = jnp.exp(reach)
            run = spread(jnp.exp(totals[t])) * run + held[t, half : 2 * half, :].astype(F32)
            reach = reach + totals[t]
        out[half : 2 * half, :] = run.astype(BF16)
        high = total.astype(BF16).astype(F32)
        low = total - high
        at = lax.broadcasted_iota(jnp.int32, (16, HEAD), 0)
        tail = jnp.where(at == 0, high[0:1], high[1:2])
        tail = jnp.where(at == 2, low[0:1], tail)
        tail = jnp.where(at == 3, low[1:2], tail)
        out[2 * half :, :] = tail.astype(BF16)

    outs = [
        shape((4, half, HEAD), F32),
        shape((4, half, HEAD), F32),
        shape((4, 2, HEAD), F32),
        shape((4, 2, HEAD), F32),
        shape(messages[0].shape),
    ]
    return call(
        "ring_y",
        body,
        table,
        (1,),
        messages,
        [whole(m) for m in messages],
        outs,
        [whole(o) for o in outs],
        8,
        [pltpu.VMEM((4, *messages[0].shape), BF16)],
    )


def arrivals(table, messages, before, after, prior, later):
    half = 2 * HEAD

    def body(s, a, b, c, d, before_ref, after_ref, prior_ref, later_ref, *rest):
        outs, held, mine, edges = rest[:4], *rest[4:]
        in_order((a, b, c, d), s[X], held)
        tails = [held[t, 2 * half : 2 * half + 16, :].astype(F32) for t in range(4)]
        totals = [tail[0:2] + tail[2:4] for tail in tails]
        ends = []
        for kind, steps in ((0, range(4)), (1, range(3, -1, -1))):
            run = jnp.zeros((half, HEAD), F32)
            reach = jnp.zeros((2, HEAD), F32)
            for t in steps:

                @pl.when(s[X] == t)
                def _(run=run, reach=reach, kind=kind):
                    mine[kind] = run
                    edges[kind] = jnp.exp(reach)

                rows = held[t, kind * half : (kind + 1) * half, :].astype(F32)
                run = spread(jnp.exp(totals[t])) * run + rows
                reach = reach + totals[t]
            ends.append(run.astype(BF16).astype(F32))
        nothing = jnp.zeros((HEAD, HEAD), F32)
        across_up = jnp.concatenate([nothing, ends[0][:HEAD]], axis=0)
        across_down = jnp.concatenate([ends[1][HEAD:], nothing], axis=0)
        start = mine[0] + spread(edges[0]) * across_up
        finish = mine[1] + spread(edges[1]) * across_down
        for r, out in enumerate(outs):
            t = (s[Y] + r) % 4
            out[:half, :] = (before_ref[t] + spread(prior_ref[t]) * start).astype(BF16)
            out[half:, :] = (after_ref[t] + spread(later_ref[t]) * finish).astype(BF16)

    operands = (*messages, before, after, prior, later)
    message = shape((2 * half, HEAD))
    return call(
        "arrivals",
        body,
        table,
        (1,),
        operands,
        [whole(m) for m in operands],
        [message] * 4,
        [whole(message)] * 4,
        8,
        [
            pltpu.VMEM((4, *messages[0].shape), BF16),
            pltpu.VMEM((2, half, HEAD), F32),
            pltpu.VMEM((2, 2, HEAD), F32),
        ],
    )


def column_of(row):
    return jnp.broadcast_to(row, (HEAD, row.shape[1])).T


def local_grads(table, qkv, out_grad, cumul, which, first, count, so_far):
    tokens = qkv.shape[1]
    heads = qkv.shape[2] // HEAD
    scale = HEAD**-0.5
    size = tokens // 2

    def body(s, qkv_ref, og_ref, cum_ref, *refs):
        out, ready = refs[-2:]
        row = cum_ref[pl.ds(pl.program_id(0) + which * heads + first, 1), :]
        column = column_of(row)
        wide = jnp.concatenate([column] * (size // HEAD), axis=1)
        s_at = lax.broadcasted_iota(jnp.int32, (size, size), 0)
        t_at = lax.broadcasted_iota(jnp.int32, (size, size), 1)
        parts = [slice(0, size), slice(size, tokens)]

        def pair(t, s):
            gap = row[:, parts[t]] - wide[parts[s], :]
            if t == s:
                gap = jnp.where(s_at <= t_at, gap, -jnp.inf)
            decay = jnp.exp(gap)
            q, k, v = qkv_ref[0, parts[t], :], qkv_ref[1, parts[s], :], qkv_ref[2, parts[s], :]
            g = og_ref[parts[t], :]
            scores = lax.dot_general(k, q, AB_T, preferred_element_type=F32)
            grads = lax.dot_general(v, g, AB_T, preferred_element_type=F32)
            prob = (scores * scale * decay).astype(BF16)
            score = (grads * decay).astype(BF16)
            dq = lax.dot_general(score, k, A_TB, preferred_element_type=F32)
            return dq, dot(score, q), dot(prob, g)

        a, b, c = pair(0, 0), pair(1, 0), pair(1, 1)
        live = lax.broadcasted_iota(jnp.int32, (tokens, HEAD), 0) < s[LEN]
        grads = (
            jnp.concatenate([a[0], b[0] + c[0]], axis=0) * scale,
            jnp.concatenate([a[1] + b[1], c[1]], axis=0) * scale,
            jnp.concatenate([a[2] + b[2], c[2]], axis=0),
        )
        until = jnp.exp(row[:, tokens - 1 : tokens] - column)
        rows = (
            og_ref[...].astype(F32) * (scale * jnp.exp(column)),
            qkv_ref[2].astype(F32) * until,
            qkv_ref[1].astype(F32) * until,
        )
        for j in range(3):
            out[j] = jnp.where(live, grads[j], 0.0)
            ready[j] = jnp.where(live, rows[j], 0.0).astype(BF16)

    tile = pl.BlockSpec((3, tokens, HEAD), lambda h, s: (0, 0, h + first))
    in_specs = [tile, pl.BlockSpec((tokens, HEAD), lambda h, s: (0, h + first)), whole(cumul)]
    operands = [qkv, out_grad, cumul]
    if so_far is not None:
        in_specs += [pl.BlockSpec(memory_space=pl.ANY)] * 2
        operands += so_far
    return call(
        "local_grads",
        body,
        table,
        (count,),
        operands,
        in_specs,
        [shape(qkv.shape, F32), shape(qkv.shape)],
        [tile, tile],
        12,
        alias=None if so_far is None else {4: 0, 5: 1},
    )


def whole_grads(table, which, local, ready, states):
    tokens = local.shape[1]
    heads = local.shape[2] // HEAD

    def body(s, local_ref, ready_ref, a, b, c, d, left, right, held):
        h = pl.program_id(0)

        @pl.when(h == 0)
        def _():
            in_order((a, b, c, d), s[Y], held)

        base = pl.multiple_of((s[Z] ^ which) * HEAD, HEAD)
        coming = held[h, pl.ds(base, HEAD), :]
        later = held[h, pl.ds(2 * HEAD + base, HEAD), :]
        cross = (
            lax.dot_general(ready_ref[0], coming, AB_T, preferred_element_type=F32),
            lax.dot_general(ready_ref[1], later, AB_T, preferred_element_type=F32),
            dot(ready_ref[2], later),
        )
        grads = [(local_ref[j] + cross[j]).astype(BF16) for j in range(3)]
        for k in range(heads):

            @pl.when(h == k)
            def _(k=k):
                for j in range(3):
                    start = (2 * j + k % 2) * HEAD
                    (left, right)[k // 2][:, start : start + HEAD] = grads[j]

    tile = pl.BlockSpec((3, tokens, HEAD), lambda h, s: (0, 0, h))
    side = shape((tokens, 3 * heads * HEAD // 2))
    return call(
        "whole_grads",
        body,
        table,
        (heads,),
        (local, ready, *states),
        [tile, tile, *[whole(m) for m in states]],
        [side, side],
        [whole(side)] * 2,
        12,
        [pltpu.VMEM((4, *states[0].shape), BF16)],
    )


def turn(table, shards):
    tokens, width = shards[0].shape
    rows = 4 * width // 32

    def body(s, *refs):
        out = refs[-1]
        for k in range(4):

            @pl.when((pl.program_id(0) ^ s[TEN]) == k)
            def _(k=k):
                out[...] = refs[k][...].T.reshape(out.shape)

    out = shape((16, 2, rows, tokens))
    spec = pl.BlockSpec((8, 1, rows, tokens), lambda i, s: (i % 2, (i // 2) ^ s[Z], 0, 0))
    turned = call("turn", body, table, (4,), shards, [whole(x) for x in shards], out, spec, 12)
    return turned.reshape(4, 4, 2 * rows, tokens)


def weight_part(table, turned, lefts, rights, places, split):
    tokens, cols = lefts[0].shape
    rows = turned[0].shape[2]

    def body(s, own_x, own_y, pair_x, pair_y, left_a, left_b, right_a, right_b, *outs):
        r = pl.program_id(0)
        for side, (a, b, ga, gb) in enumerate(
            ((own_x, pair_x, left_a, left_b), (own_y, pair_y, right_a, right_b))
        ):
            acc = dot(a[...].reshape(4 * rows, tokens), ga[...])
            acc += dot(b[...].reshape(4 * rows, tokens), gb[...])
            acc = acc.astype(BF16)
            if split:
                outs[2 * side][...] = acc[: 2 * rows]
                outs[2 * side + 1][...] = acc[2 * rows :]
                continue
            for k in range(len(places)):

                @pl.when(r == k)
                def _(k=k, acc=acc, side=side):
                    outs[side * len(places) + k][...] = acc

    step = places[1] - places[0] if len(places) > 1 else 0
    by_x = pl.BlockSpec((1, 4, rows, tokens), lambda r, s: ((s[X] + places[0] + step * r) % 4, 0, 0, 0))
    by_y = pl.BlockSpec((4, 1, rows, tokens), lambda r, s: (0, (s[Y] + places[0] + step * r) % 4, 0, 0))
    outs = [shape((2 * rows if split else 4 * rows, cols))] * (4 if split else 2 * len(places))
    operands = (turned[0], turned[0], turned[1], turned[1], *lefts, *rights)
    return call(
        "weight_part",
        body,
        table,
        (len(places),),
        operands,
        [by_x, by_y, by_x, by_y, *[whole(x) for x in (*lefts, *rights)]],
        outs,
        [whole(o) for o in outs],
        40,
    )


def add_halves(table, near_up, near_down, up, down):
    n, cols = up.shape

    def body(s, a, b, u, d, out_a, out_b):
        out_a[...] = (a[...].astype(F32) + u[...].astype(F32)).astype(BF16)
        out_b[...] = (b[...].astype(F32) + d[...].astype(F32)).astype(BF16)

    first = pl.BlockSpec((n, cols), lambda i, s: (0, 0))
    second = pl.BlockSpec((n, cols), lambda i, s: (1, 0))
    return call(
        "add_halves",
        body,
        table,
        (1,),
        (near_up, near_down, up, down),
        [first, second, first, first],
        [shape(near_up.shape), shape(near_down.shape)],
        [first, second],
        12,
        alias={1: 0, 2: 1},
    )


def cut_blocks(table, axis, own, first, second):
    rows, cols = own.shape[0] // 4, own.shape[1]

    def body(s, a, b, c, far_up, far_down, one, three, here):
        def block(r):
            at = pl.ds(pl.multiple_of((s[axis] + r) % 4 * rows, rows), rows)
            return (a[at, :].astype(F32) + b[at, :].astype(F32) + c[at, :].astype(F32)).astype(BF16)

        far = block(2)
        far_up[...] = far[: rows // 2]
        far_down[...] = far[rows // 2 :]
        one[...] = block(1)
        three[...] = block(3)
        here[...] = block(0)

    outs = [shape((rows // 2, cols))] * 2 + [shape((rows, cols))] * 3
    operands = (own, first, second)
    return call(
        "cut_blocks",
        body,
        table,
        (1,),
        operands,
        [whole(x) for x in operands],
        outs,
        [whole(o) for o in outs],
        20,
    )


def final_sums(table, sides):
    rows, cols = sides[0][0].shape

    def body(s, *refs):
        here, there = refs[-2:]
        for k in range(2):
            a, b, c = refs[3 * k : 3 * k + 3]
            total = (a[...].astype(F32) + b[...].astype(F32) + c[...].astype(F32)).astype(BF16)
            here[k] = total[: rows // 2]
            there[k] = total[rows // 2 :]

    operands = [x for side in sides for x in side]
    outs = [shape((2, rows // 2, cols))] * 2
    return call(
        "final_sums",
        body,
        table,
        (1,),
        operands,
        [whole(x) for x in operands],
        outs,
        [whole(o) for o in outs],
        8,
    )


def finish(table, here, there):
    _, rows, cols = here.shape
    side = cols // 3

    def body(s, here_ref, there_ref, out):
        for ref, half in ((here_ref, s[Z]), (there_ref, 1 - s[Z])):
            for k in range(2):
                for j in range(3):
                    at = pl.ds(pl.multiple_of(half * 2 * side + k * side, side), side)
                    out[j, :, at] = ref[k, :, j * side : (j + 1) * side].astype(F32)

    out = shape((3, rows, 4 * side), F32)
    operands = (here, there)
    return call("finish", body, table, (1,), operands, [whole(here)] * 2, out, whole(out), 8)


def device_part(activations, qkv_weight, log_decay, lengths, out_grad):
    tied = lax.optimization_barrier
    tokens = activations.shape[0]
    heads = log_decay.shape[1]
    per = heads // 2
    index = [lax.axis_index(a) for a in ("c0", "c1", "c2", "zl", "co")]
    here_z = index[0]
    fixed = [*index, index[3] * 2 + index[4]]
    table = jnp.stack([*fixed, lengths[0]]).astype(jnp.int32)
    weight = pltpu.with_memory_space_constraint(jnp.transpose(qkv_weight, (1, 0, 2)), pltpu.HBM)

    near = send(activations, "zl", 1)
    side = across(activations)
    core = send(activations, "co", 1)

    live = (jnp.arange(tokens, dtype=jnp.int32) < lengths[0]).astype(F32)
    cumul = jnp.cumsum(log_decay.T * live[None, :], axis=1)
    size = jnp.broadcast_to(lengths.astype(F32)[:, None], (per, tokens))
    note = jnp.concatenate([lax.dynamic_slice_in_dim(cumul, (1 - here_z) * per, per), size])
    note = send(note, "c0", 1)
    width = per * HEAD
    og_own = lax.dynamic_slice_in_dim(out_grad, here_z * width, width, axis=1)
    og_other = lax.dynamic_slice_in_dim(out_grad, (1 - here_z) * width, width, axis=1)

    acc_own = project(table, [activations, core], (0, 1), weight, None, False)
    near, side, acc_own, note, og_other = tied((near, side, acc_own, note, og_other))
    cumul = jnp.concatenate([lax.dynamic_slice_in_dim(cumul, here_z * per, per), note[:per]])
    table_pair = jnp.stack([*fixed, note[per, 0].astype(jnp.int32)]).astype(jnp.int32)
    half = tokens // 2
    far = [send(side[:half], "zl", 1), across(near[half:])]
    near_core = send(near, "co", 1)
    side_core = send(side, "co", 1)
    acc_pair = project(table, [side], (2,), weight, None, False)
    near_core, side_core, acc_pair = tied((near_core, side_core, acc_pair))
    qkv_own = project(table, [near, near_core], (2, 3), weight, acc_own, True)
    *far, qkv_own = tied((*far, qkv_own))
    far = jnp.concatenate(far)
    far_core = send(far, "co", 1)
    og_pair = send(tied((og_other, far))[0], "c0", 1)
    acc_pair = project(table, [side_core, far], (3, 0), weight, acc_pair, False)
    far_core, acc_pair = tied((far_core, acc_pair))
    qkv_pair = project(table_pair, [far_core], (1,), weight, acc_pair, True)

    local_own = local_grads(table, qkv_own, og_own, cumul, 0, 0, per, None)
    og_pair, local_own, qkv_pair = tied((og_pair, local_own, qkv_pair))
    to_y = shard_states(table, (qkv_own, qkv_pair), (og_own, og_pair), cumul)
    at_y = [send(to_y[r], "c2", r) for r in (2, 1, 3)]
    local = local_grads(table_pair, qkv_pair, og_pair, cumul, 1, 0, per // 2, None)
    at_y, local = tied((at_y, local))
    before, after, prior, later, ring = ring_y(table, [to_y[0], at_y[1], at_y[0], at_y[2]])
    at_x = [send(ring, "c1", r) for r in (2, 1, 3)]
    local, _ = tied((local, ring))
    local = local_grads(table_pair, qkv_pair, og_pair, cumul, 1, per // 2, per // 2, local)
    at_x, local = tied((at_x, local))
    back = arrivals(table, [ring, at_x[1], at_x[0], at_x[2]], before, after, prior, later)
    states = [send(back[r], "c2", r) for r in (2, 1, 3)]
    first, second, _ = tied(([activations, core, near, near_core], [far, far_core, side, side_core], back[0]))
    turned = [turn(table, first), turn(table, second)]
    states, turned = tied((states, turned))
    states = [back[0], states[1], states[0], states[2]]

    left_own, right_own = whole_grads(table, 0, *local_own, states)
    left_pair, right_pair = whole_grads(table, 1, *local, states)
    lefts, rights = (left_own, left_pair), (right_own, right_pair)
    far_left, far_right = (
        lambda outs: (outs[:2], outs[2:])
    )(weight_part(table, turned, lefts, rights, (2,), True))
    l_half = [send(x, "c1", by) for x, by in zip(far_left, (1, -1))]
    r_half = [send(x, "c2", by) for x, by in zip(far_right, (1, -1))]
    turned, _ = tied((turned, far_left))
    pieces = weight_part(table, turned, lefts, rights, (1, 3), False)
    l_half, pieces = tied((l_half, pieces))
    l_near = add_halves(table, *pieces[:2], *l_half)
    l_got = [send(x, "c1", by) for x, by in zip(l_near, (1, -1))]
    r_half, _ = tied((r_half, l_near))
    r_near = add_halves(table, *pieces[2:], *r_half)
    r_got = [send(x, "c2", by) for x, by in zip(r_near, (1, -1))]
    turned, _ = tied((turned, r_near))
    own = weight_part(table, turned, lefts, rights, (0,), False)
    l_got, own = tied((l_got, own))
    l_cut = cut_blocks(table, Y, own[0], *l_got)
    r_got, _ = tied((r_got, l_cut))
    r_cut = cut_blocks(table, X, own[1], *r_got)
    l_half = [send(x, "c2", by) for x, by in zip(l_cut[:2], (1, -1))]
    r_half = [send(x, "c1", by) for x, by in zip(r_cut[:2], (1, -1))]
    l_near = add_halves(table, *l_cut[2:4], *l_half)
    l_got = [send(x, "c2", by) for x, by in zip(l_near, (1, -1))]
    r_half, _ = tied((r_half, l_near))
    r_near = add_halves(table, *r_cut[2:4], *r_half)
    r_got = [send(x, "c1", by) for x, by in zip(r_near, (1, -1))]
    here, there = final_sums(table, ((l_cut[4], *l_got), (r_cut[4], *r_got)))
    there = send(there, "c0", 1)
    return jnp.transpose(finish(table, here, there), (1, 0, 2))


def solution(mesh):
    finer = Mesh(mesh.devices.reshape(2, 4, 4, 2, 2), ("c0", "c1", "c2", "zl", "co"))
    context, tensor = ("c0", "c1", "c2"), ("zl", "co")
    placed = (
        P(context, tensor),
        P(None, None, tensor),
        P(context, tensor),
        P(context),
        P(context, tensor),
    )
    return jax.shard_map(
        device_part,
        mesh=finer,
        in_specs=placed,
        out_specs=P(context, None, tensor),
        check_vma=False,
    )
```

time: 497 us -> 189 us (0.38)
  waiting for transfers between devices: 299 us -> 40.2 us
  Pallas kernels: 0 us -> 79.1 us
  matrix products: 56.9 us -> 0 us
  blocking collectives: 56.5 us -> 0 us
  starting transfers between devices: 0.47 us -> 55.8 us
  local copies, waits for them, and re-layouts: 52.7 us -> 9.44 us
  other arithmetic: 14.9 us -> 2.04 us
  between operations: 14.4 us -> 1.78 us
    reduce_scatter x3 -> x0, waiting for transfers between devices: 247 us -> none  [own_block(): pieces = lax.psum_scatter(pieces, axes[k], scatter_dimension=0, tiled=True)]
    pallas_call x0 -> x26, Pallas kernels: none -> 79.1 us  [call(): pl.pallas_call(body, grid_spec=pltpu.PrefetchScalarGridSpec(num_scalar_pr...]
    dot_general x11 -> x0, matrix products: 56.9 us -> none  [the longest x1 15.4 us: shards(): jnp.einsum('td,tc->dc', features_all, qkv_grad, preferred_element_type=jn...]
    all_gather x7 -> x0, blocking collectives: 56.5 us -> none  [entering(): lax.all_gather(part.astype(kind), axis)]
    ppermute x0 -> x36, starting transfers between devices: none -> 55.8 us  [the longest x34 48.8 us: send(): return lax.ppermute(x, axis, shift(axis, by))]
    all_gather x5 -> x0, waiting for transfers between devices: 51.5 us -> none  [the longest x4 37.6 us: entering(): lax.all_gather(part.astype(kind), axis)]
    ppermute x0 -> x36, waiting for transfers between devices: none -> 40.2 us  [the longest x34 40.2 us: send(): return lax.ppermute(x, axis, shift(axis, by))]
    unnamed x32 -> x25, local copies, waits for them, and re-layouts: 27.3 us -> 5.47 us
  transfers between devices with their start and end apart: 8 -> 36, of which waited for: 7 -> 9; matrix products, arithmetic and copies ran while one was open for 9% -> 3% of each run, Pallas kernels for 0% -> 33%
where the time goes in v1:
time: 189 us; the launch traced here: 188 us
  Pallas kernels  79.1 us (42%)
  starting transfers between devices  55.8 us (30%)
  waiting for transfers between devices  40.2 us (21%)
  local copies, waits for them, and re-layouts  9.44 us (5%)
  other arithmetic  2.04 us (1%)
    pallas_call x26, Pallas kernels, call(): pl.pallas_call(body, grid_spec=pltpu.PrefetchScalarGridSpec(num_scalar_pr...  79.1 us
    ppermute x34, starting transfers between devices, send(): return lax.ppermute(x, axis, shift(axis, by))  48.8 us
    ppermute x34, waiting for transfers between devices, send(): return lax.ppermute(x, axis, shift(axis, by))  40.2 us
    ppermute x2, starting transfers between devices, across(): return lax.ppermute(x, ('c0', 'zl'), [(0, 3), (1, 2), (2, 1), (3, 0)])  7.06 us
    unnamed x25, local copies, waits for them, and re-layouts  5.47 us
  transfers between devices with their start and end apart: 36, of which 9 were waited for; matrix products, arithmetic and copies ran while one was open for 3% of the time, Pallas kernels for 33%

profile of v1, /device:TPU:0, one launch (start us, length us, event | category | flops | bytes accessed | tf_op | source)
XLA Modules:
  0.0 188.4 jit_solution(2740567769762426193)
XLA Ops:
  0.0 4.1 %collective-permute-start.1 = (bf16[512,768]{1,0:T(8,128)(2,1)}, bf16[512,768]{1,0:T(8,128)(2,1)S(1)}, u32[]{:S(2)}, u32[]{:S(2)}) collective-permute-start(bf16[512,768]{1,0:T(8,128)(2,1)} %refs_0_.2), channel_id=1, source_target_pairs={{0,66},{2,64},{64,2},{66,0},{1,67},{3,65},{65,3},{67,1},{4,70},{6,... | collective-permute-start | bytes 2359304 | tf_op jit(solution)/shard_map/ppermute | solution.py:31
  7.0 1.6 collective-permute-start.3
  8.7 2.2 %constant_dynamic-slice_fusion.1 = (bf16[512,512]{1,0:T(8,128)(2,1)}, bf16[512,512]{1,0:T(8,128)(2,1)}) fusion(bf16[512,1024]{1,0:T(8,128)(2,1)} %param.9, s32[]{:T(128)S(6)} %select_n.14, s32[]{:T(128)S(6)} %select_n.13), kind=kLoop, calls=%fused_computation.9 | loop fusion | bytes 2097160 | tf_op jit(solution)/shard_map/dynamic_slice | solution.py:542
  11.0 5.3 %project.5.refs_4_ = f32[3,512,512]{2,1,0:T(8,128)S(1)} custom-call(s32[7]{0:T(128)S(1)} %stack.39.s, bf16[512,768]{1,0:T(8,128)(2,1)S(1)} %copy-done.3, bf16[512,768]{1,0:T(8,128)(2,1)S(1)} %collective-permute-done.2.refs_1_, bf16[3,3072,1024]{2,1,0:T(8,128)(2,1)} %bitcast.32, bf16[3,3072,1024]{2,1,0:T(8,128)(2,1)} %bitcast.33), custom_call_target="tpu_custom_call" | custom-call | flops 1 | bytes 1 | tf_op jit(solution)/shard_map/project/pallas_call | solution.py:39
  16.3 7.8 %collective-permute-done.3 = f32[8,512]{1,0:T(8,128)S(1)} collective-permute-done((f32[8,512]{1,0:T(8,128)S(1)}, f32[8,512]{1,0:T(8,128)S(1)}, u32[]{:S(2)}, u32[]{:S(2)}) %collective-permute-start.3) | collective-permute-done | bytes 16416 | tf_op jit(solution)/shard_map/ppermute | solution.py:27
  24.8 2.9 %collective-permute-start.5 = (bf16[256,768]{1,0:T(8,128)(2,1)S(1)}, bf16[256,768]{1,0:T(8,128)(2,1)S(1)}, u32[]{:S(2)}, u32[]{:S(2)}) collective-permute-start(bf16[256,768]{1,0:T(8,128)(2,1)S(1)} %slice.21), channel_id=1, source_target_pairs={{0,66},{2,64},{64,2},{66,0},{1,67},{3,65},{65,3},{67,1},{4,70},{6,... | collective-permute-start | bytes 1179656 | tf_op jit(solution)/shard_map/ppermute | solution.py:31
  27.7 4.0 %project.6.refs_4_ = f32[3,512,512]{2,1,0:T(8,128)S(1)} custom-call(s32[7]{0:T(128)S(1)} %stack.39.s, bf16[512,768]{1,0:T(8,128)(2,1)S(1)} %collective-permute-done.1.refs_0_.refs_2_, bf16[3,3072,1024]{2,1,0:T(8,128)(2,1)} %bitcast.34), custom_call_target="tpu_custom_call" | custom-call | flops 1 | bytes 1 | tf_op jit(solution)/shard_map/project/pallas_call | solution.py:39
  31.7 1.6 copy-done
  33.3 5.3 %project.7.qkv_ref.qkv_a = bf16[3,512,512]{2,1,0:T(8,128)(2,1)S(1)} custom-call(s32[7]{0:T(128)S(1)} %stack.39.s, bf16[512,768]{1,0:T(8,128)(2,1)S(1)} %collective-permute-done.refs_0_.refs_2_, bf16[512,768]{1,0:T(8,128)(2,1)S(1)} %collective-permute-done.6.refs_1_.refs_3_, bf16[3,3072,1024]{2,1,0:T(8,128)(2,1)} %bitcast.35, ...), custom_call_target="tpu_custom_call" | custom-call | flops 1 | bytes 1 | tf_op jit(solution)/shard_map/project/pallas_call | solution.py:39
  40.3 1.8 collective-permute-start.8
  43.4 1.9 copy-done.1
  46.4 5.5 %project.8.refs_2_ = f32[3,512,512]{2,1,0:T(8,128)S(1)} custom-call(s32[7]{0:T(128)S(1)} %stack.39.s, bf16[512,768]{1,0:T(8,128)(2,1)S(1)} %copy-done.8, bf16[512,768]{1,0:T(8,128)(2,1)} %constant_dynamic-update-slice_fusion.refs_1_.refs_0_, bf16[3,3072,1024]{2,1,0:T(8,128)(2,1)} %bitcast.37, bf16[3,3072,1024]{2,1,0:T(8,128)(2,1)} %bitcast.38, ...), custom_call_target="tpu_custom_call" | custom-call | flops 1 | bytes 1 | tf_op jit(solution)/shard_map/project/pallas_call | solution.py:39
  52.0 6.3 %local_grads.3 = (f32[3,512,512]{2,1,0:T(8,128)S(1)}, bf16[3,512,512]{2,1,0:T(8,128)(2,1)S(1)}) custom-call(s32[7]{0:T(128)S(1)} %stack.39.s, bf16[3,512,512]{2,1,0:T(8,128)(2,1)S(1)} %project.7.qkv_ref.qkv_a, bf16[512,512]{1,0:T(8,128)(2,1)S(1)} %copy-done.2, f32[8,512]{1,0:T(8,128)S(1)} %pad_maximum_fusion.cum_ref), custom_call_target="tpu_custom_call" | custom-call | flops 1 | bytes 1 | tf_op jit(solution)/shard_map/local_grads/pallas_call | solution.py:39
  58.3 4.2 %project.9.qkv_b.qkv_ref = bf16[3,512,512]{2,1,0:T(8,128)(2,1)S(1)} custom-call(s32[7]{0:T(128)S(1)} %stack.41.s, bf16[512,768]{1,0:T(8,128)(2,1)} %collective-permute-done.9.refs_0_.refs_1_, bf16[3,3072,1024]{2,1,0:T(8,128)(2,1)} %bitcast.39, f32[3,512,512]{2,1,0:T(8,128)S(1)} %project.8.refs_2_), custom_call_target="tpu_custom_call" | custom-call | flops 1 | bytes 1 | tf_op jit(solution)/shard_map/project/pallas_call | solution.py:39
  62.5 4.3 %shard_states.1 = (bf16[528,128]{1,0:T(8,128)(2,1)S(1)}, bf16[528,128]{1,0:T(8,128)(2,1)S(1)}, bf16[528,128]{1,0:T(8,128)(2,1)S(1)}, bf16[528,128]{1,0:T(8,128)(2,1)S(1)}) custom-call(s32[7]{0:T(128)S(1)} %stack.39.s, bf16[3,512,512]{2,1,0:T(8,128)(2,1)S(1)} %project.7.qkv_ref.qkv_a, bf16[3,512,512]{2,1,0:T(8,128)(2,1)S(1)} %project.9.qkv_b.qkv_ref, ...), custom_call_target="tpu_custom_call" | custom-call | flops 1 | bytes 1 | tf_op jit(solution)/shard_map/shard_states/pallas_call | solution.py:39
  66.8 3.3 %collective-permute-start.10 = (bf16[528,128]{1,0:T(8,128)(2,1)S(1)}, bf16[528,128]{1,0:T(8,128)(2,1)S(1)}, u32[]{:S(2)}, u32[]{:S(2)}) collective-permute-start(bf16[528,128]{1,0:T(8,128)(2,1)S(1)} %get-tuple-element.140), channel_id=1, source_target_pairs={{0,8},{4,12},{8,0},{12,4},{1,9},{5,13},{9,1},{13,5},{2,10},{6,14},... | collective-permute-start | bytes 405512 | tf_op jit(solution)/shard_map/ppermute | solution.py:27
  70.7 2.6 %collective-permute-start.12 = (bf16[528,128]{1,0:T(8,128)(2,1)S(1)}, bf16[528,128]{1,0:T(8,128)(2,1)S(1)}, u32[]{:S(2)}, u32[]{:S(2)}) collective-permute-start(bf16[528,128]{1,0:T(8,128)(2,1)S(1)} %get-tuple-element.142), channel_id=1, source_target_pairs={{0,12},{4,0},{8,4},{12,8},{1,13},{5,1},{9,5},{13,9},{2,14},{6,2},{... | collective-permute-start | bytes 405512 | tf_op jit(solution)/shard_map/ppermute | solution.py:27
  73.3 4.2 %local_grads.4 = (f32[3,512,512]{2,1,0:T(8,128)S(1)}, bf16[3,512,512]{2,1,0:T(8,128)(2,1)S(1)}) custom-call(s32[7]{0:T(128)S(1)} %stack.41.s, bf16[3,512,512]{2,1,0:T(8,128)(2,1)S(1)} %project.9.qkv_b.qkv_ref, bf16[512,512]{1,0:T(8,128)(2,1)} %collective-permute-done.8.og_b.og_ref, f32[8,512]{1,0:T(8,128)S(1)} %pad_maximum_fusion.cum_ref), custom_call_target="tpu_custom_call" | custom-call | flops 1 | bytes 1 | tf_op jit(solution)/shard_map/local_grads/pallas_call | solution.py:39
  78.3 2.8 %collective-permute-start.15 = (bf16[528,128]{1,0:T(8,128)(2,1)S(1)}, bf16[528,128]{1,0:T(8,128)(2,1)S(1)}, u32[]{:S(2)}, u32[]{:S(2)}) collective-permute-start(bf16[528,128]{1,0:T(8,128)(2,1)S(1)} %get-tuple-element.148.a), channel_id=1, source_target_pairs={{0,48},{16,0},{32,16},{48,32},{1,49},{17,1},{33,17},{49,33},{2,50}... | collective-permute-start | bytes 405512 | tf_op jit(solution)/shard_map/ppermute | solution.py:27
  81.1 2.3 %collective-permute-start.13 = (bf16[528,128]{1,0:T(8,128)(2,1)S(1)}, bf16[528,128]{1,0:T(8,128)(2,1)S(1)}, u32[]{:S(2)}, u32[]{:S(2)}) collective-permute-start(bf16[528,128]{1,0:T(8,128)(2,1)S(1)} %get-tuple-element.148.a), channel_id=1, source_target_pairs={{0,32},{16,48},{32,0},{48,16},{1,33},{17,49},{33,1},{49,17},{2,34}... | collective-permute-start | bytes 405512 | tf_op jit(solution)/shard_map/ppermute | solution.py:27
  83.4 4.2 %local_grads.5 = (f32[3,512,512]{2,1,0:T(8,128)S(1)}, bf16[3,512,512]{2,1,0:T(8,128)(2,1)S(1)}) custom-call(s32[7]{0:T(128)S(1)} %stack.41.s, bf16[3,512,512]{2,1,0:T(8,128)(2,1)S(1)} %project.9.qkv_b.qkv_ref, bf16[512,512]{1,0:T(8,128)(2,1)} %collective-permute-done.8.og_b.og_ref, ...), custom_call_target="tpu_custom_call", output_to_operand_aliasing={{0}: (4, {}), {1}: (5, {})} | custom-call | flops 1 | bytes 1 | tf_op jit(solution)/shard_map/local_grads/pallas_call | solution.py:39
  87.6 2.2 %collective-permute-done.14.b = bf16[528,128]{1,0:T(8,128)(2,1)S(1)} collective-permute-done((bf16[528,128]{1,0:T(8,128)(2,1)S(1)}, bf16[528,128]{1,0:T(8,128)(2,1)S(1)}, u32[]{:S(2)}, u32[]{:S(2)}) %collective-permute-start.14) | collective-permute-done | bytes 135200 | tf_op jit(solution)/shard_map/ppermute | solution.py:27
  90.6 2.0 %collective-permute-start.16 = (bf16[512,128]{1,0:T(8,128)(2,1)S(1)}, bf16[512,128]{1,0:T(8,128)(2,1)S(1)}, u32[]{:S(2)}, u32[]{:S(2)}) collective-permute-start(bf16[512,128]{1,0:T(8,128)(2,1)S(1)} %get-tuple-element.162), channel_id=1, source_target_pairs={{0,8},{4,12},{8,0},{12,4},{1,9},{5,13},{9,1},{13,5},{2,10},{6,14},... | collective-permute-start | bytes 393224 | tf_op jit(solution)/shard_map/ppermute | solution.py:27
  92.6 1.5 collective-permute-start.17
  94.1 1.7 collective-permute-start.18
  95.9 2.0 %turn.2 = bf16[16,2,96,512]{3,2,1,0:T(8,128)(2,1)S(1)} custom-call(s32[7]{0:T(128)S(1)} %stack.39.s, bf16[512,768]{1,0:T(8,128)(2,1)S(1)} %copy-done.4, bf16[512,768]{1,0:T(8,128)(2,1)S(1)} %copy-done.6, bf16[512,768]{1,0:T(8,128)(2,1)S(1)} %collective-permute-done.refs_0_.refs_2_, bf16[512,768]{1,0:T(8,128)(2,1)S(1)} %copy-done.11), custom_call_target="tpu_custom_call" | custom-call | flops 1 | bytes 1 | tf_op jit(solution)/shard_map/turn/pallas_call | solution.py:39
  97.9 3.4 %turn.3 = bf16[16,2,96,512]{3,2,1,0:T(8,128)(2,1)S(1)} custom-call(s32[7]{0:T(128)S(1)} %stack.39.s, bf16[512,768]{1,0:T(8,128)(2,1)} %constant_dynamic-update-slice_fusion.refs_1_.refs_0_, bf16[512,768]{1,0:T(8,128)(2,1)} %collective-permute-done.9.refs_0_.refs_1_, bf16[512,768]{1,0:T(8,128)(2,1)S(1)} %collective-permute-done.1.refs_0_.refs_2_, ...), custom_call_target="tpu_custom_call" | custom-call | flops 1 | bytes 1 | tf_op jit(solution)/shard_map/turn/pallas_call | solution.py:39
  101.4 2.7 %whole_grads.3 = (bf16[512,768]{1,0:T(8,128)(2,1)S(1)}, bf16[512,768]{1,0:T(8,128)(2,1)S(1)}) custom-call(s32[7]{0:T(128)S(1)} %stack.39.s, f32[3,512,512]{2,1,0:T(8,128)S(1)} %get-tuple-element.182.local_ref, bf16[3,512,512]{2,1,0:T(8,128)(2,1)S(1)} %get-tuple-element.183.ready_ref, bf16[512,128]{1,0:T(8,128)(2,1)S(1)} %get-tuple-element.165.a, ...), custom_call_target="tpu_custom_call" | custom-call | flops 1 | bytes 1 | tf_op jit(solution)/shard_map/whole_grads/pallas_call | solution.py:39
  104.1 2.7 %whole_grads.2 = (bf16[512,768]{1,0:T(8,128)(2,1)S(1)}, bf16[512,768]{1,0:T(8,128)(2,1)S(1)}) custom-call(s32[7]{0:T(128)S(1)} %stack.39.s, f32[3,512,512]{2,1,0:T(8,128)S(1)} %get-tuple-element.176.local_ref, bf16[3,512,512]{2,1,0:T(8,128)(2,1)S(1)} %get-tuple-element.177.ready_ref, bf16[512,128]{1,0:T(8,128)(2,1)S(1)} %get-tuple-element.165.a, ...), custom_call_target="tpu_custom_call" | custom-call | flops 1 | bytes 1 | tf_op jit(solution)/shard_map/whole_grads/pallas_call | solution.py:39
  106.8 3.1 %weight_part.3 = (bf16[384,768]{1,0:T(8,128)(2,1)S(1)}, bf16[384,768]{1,0:T(8,128)(2,1)S(1)}, bf16[384,768]{1,0:T(8,128)(2,1)S(1)}, bf16[384,768]{1,0:T(8,128)(2,1)S(1)}) custom-call(s32[7]{0:T(128)S(1)} %stack.39.s, bf16[4,4,192,512]{3,2,1,0:T(8,128)(2,1)S(1)} %bitcast.20, bf16[4,4,192,512]{3,2,1,0:T(8,128)(2,1)S(1)} %bitcast.21, ...), custom_call_target="tpu_custom_call" | custom-call | flops 1 | bytes 1 | tf_op jit(solution)/shard_map/weight_part/pallas_call | solution.py:39
  110.0 3.2 %collective-permute-start.20 = (bf16[384,768]{1,0:T(8,128)(2,1)S(1)}, bf16[384,768]{1,0:T(8,128)(2,1)S(1)}, u32[]{:S(2)}, u32[]{:S(2)}) collective-permute-start(bf16[384,768]{1,0:T(8,128)(2,1)S(1)} %get-tuple-element.188), channel_id=1, source_target_pairs={{0,48},{16,0},{32,16},{48,32},{1,49},{17,1},{33,17},{49,33},{2,50}... | collective-permute-start | bytes 1769480 | tf_op jit(solution)/shard_map/ppermute | solution.py:27
  113.5 2.9 %collective-permute-start.24 = (bf16[384,768]{1,0:T(8,128)(2,1)S(1)}, bf16[384,768]{1,0:T(8,128)(2,1)S(1)}, u32[]{:S(2)}, u32[]{:S(2)}) collective-permute-start(bf16[384,768]{1,0:T(8,128)(2,1)S(1)} %get-tuple-element.204), channel_id=1, source_target_pairs={{0,12},{4,0},{8,4},{12,8},{1,13},{5,1},{9,5},{13,9},{2,14},{6,2},{... | collective-permute-start | bytes 1769480 | tf_op jit(solution)/shard_map/ppermute | solution.py:27
  116.5 8.4 %weight_part.4 = (bf16[768,768]{1,0:T(8,128)(2,1)S(1)}, bf16[768,768]{1,0:T(8,128)(2,1)S(1)}, bf16[768,768]{1,0:T(8,128)(2,1)S(1)}, bf16[768,768]{1,0:T(8,128)(2,1)S(1)}) custom-call(s32[7]{0:T(128)S(1)} %stack.39.s, bf16[4,4,192,512]{3,2,1,0:T(8,128)(2,1)S(1)} %bitcast.22, bf16[4,4,192,512]{3,2,1,0:T(8,128)(2,1)S(1)} %bitcast.23, ...), custom_call_target="tpu_custom_call" | custom-call | flops 1 | bytes 1 | tf_op jit(solution)/shard_map/weight_part/pallas_call | solution.py:39
  126.5 3.2 %collective-permute-start.22 = (bf16[768,768]{1,0:T(8,128)(2,1)S(1)}, bf16[768,768]{1,0:T(8,128)(2,1)S(1)}, u32[]{:S(2)}, u32[]{:S(2)}) collective-permute-start(bf16[768,768]{1,0:T(8,128)(2,1)S(1)} %get-tuple-element.200), channel_id=1, source_target_pairs={{0,48},{16,0},{32,16},{48,32},{1,49},{17,1},{33,17},{49,33},{2,50}... | collective-permute-start | bytes 3538952 | tf_op jit(solution)/shard_map/ppermute | solution.py:27
  131.2 3.2 %collective-permute-start.30 = (bf16[768,768]{1,0:T(8,128)(2,1)S(1)}, bf16[768,768]{1,0:T(8,128)(2,1)S(1)}, u32[]{:S(2)}, u32[]{:S(2)}) collective-permute-start(bf16[768,768]{1,0:T(8,128)(2,1)S(1)} %get-tuple-element.208), channel_id=1, source_target_pairs={{0,12},{4,0},{8,4},{12,8},{1,13},{5,1},{9,5},{13,9},{2,14},{6,2},{... | collective-permute-start | bytes 3538952 | tf_op jit(solution)/shard_map/ppermute | solution.py:27
  134.5 3.1 %weight_part.5 = (bf16[768,768]{1,0:T(8,128)(2,1)S(1)}, bf16[768,768]{1,0:T(8,128)(2,1)S(1)}) custom-call(s32[7]{0:T(128)S(1)} %stack.39.s, bf16[4,4,192,512]{3,2,1,0:T(8,128)(2,1)S(1)} %bitcast.24, bf16[4,4,192,512]{3,2,1,0:T(8,128)(2,1)S(1)} %bitcast.25, bf16[4,4,192,512]{3,2,1,0:T(8,128)(2,1)S(1)} %bitcast.30, bf16[4,4,192,512]{3,2,1,0:T(8,128)(2,1)S(1)} %bitcast.31, ...), custom_call_target="tpu_custom_call" | custom-call | flops 1 | bytes 1 | tf_op jit(solution)/shard_map/weight_part/pallas_call | solution.py:39
  137.6 13.6 %collective-permute-done.21.b = bf16[768,768]{1,0:T(8,128)(2,1)S(1)} collective-permute-done((bf16[768,768]{1,0:T(8,128)(2,1)S(1)}, bf16[768,768]{1,0:T(8,128)(2,1)S(1)}, u32[]{:S(2)}, u32[]{:S(2)}) %collective-permute-start.21) | collective-permute-done | bytes 1179680 | tf_op jit(solution)/shard_map/ppermute | solution.py:27
  152.3 3.2 %collective-permute-start.26 = (bf16[96,768]{1,0:T(8,128)(2,1)S(1)}, bf16[96,768]{1,0:T(8,128)(2,1)S(1)}, u32[]{:S(2)}, u32[]{:S(2)}) collective-permute-start(bf16[96,768]{1,0:T(8,128)(2,1)S(1)} %get-tuple-element.220), channel_id=1, source_target_pairs={{0,12},{4,0},{8,4},{12,8},{1,13},{5,1},{9,5},{13,9},{2,14},{6,2},{... | collective-permute-start | bytes 442376 | tf_op jit(solution)/shard_map/ppermute | solution.py:27
  155.5 1.5 collective-permute-done.29.b
  158.1 3.2 %collective-permute-start.32 = (bf16[96,768]{1,0:T(8,128)(2,1)S(1)}, bf16[96,768]{1,0:T(8,128)(2,1)S(1)}, u32[]{:S(2)}, u32[]{:S(2)}) collective-permute-start(bf16[96,768]{1,0:T(8,128)(2,1)S(1)} %get-tuple-element.230), channel_id=1, source_target_pairs={{0,48},{16,0},{32,16},{48,32},{1,49},{17,1},{33,17},{49,33},{2,50}... | collective-permute-start | bytes 442376 | tf_op jit(solution)/shard_map/ppermute | solution.py:27
  162.1 3.6 %collective-permute-done.31.u = bf16[96,768]{1,0:T(8,128)(2,1)S(1)} collective-permute-done((bf16[96,768]{1,0:T(8,128)(2,1)S(1)}, bf16[96,768]{1,0:T(8,128)(2,1)S(1)}, u32[]{:S(2)}, u32[]{:S(2)}) %collective-permute-start.31) | collective-permute-done | bytes 147488 | tf_op jit(solution)/shard_map/ppermute | solution.py:27
  166.5 3.2 %collective-permute-start.34 = (bf16[192,768]{1,0:T(8,128)(2,1)S(1)}, bf16[192,768]{1,0:T(8,128)(2,1)S(1)}, u32[]{:S(2)}, u32[]{:S(2)}) collective-permute-start(bf16[192,768]{1,0:T(8,128)(2,1)S(1)} %get-tuple-element.234), channel_id=1, source_target_pairs={{0,48},{16,0},{32,16},{48,32},{1,49},{17,1},{33,17},{49,33},{2,50}... | collective-permute-start | bytes 884744 | tf_op jit(solution)/shard_map/ppermute | solution.py:27
  169.7 3.2 %collective-permute-start.28 = (bf16[192,768]{1,0:T(8,128)(2,1)S(1)}, bf16[192,768]{1,0:T(8,128)(2,1)S(1)}, u32[]{:S(2)}, u32[]{:S(2)}) collective-permute-start(bf16[192,768]{1,0:T(8,128)(2,1)S(1)} %get-tuple-element.222), channel_id=1, source_target_pairs={{0,12},{4,0},{8,4},{12,8},{1,13},{5,1},{9,5},{13,9},{2,14},{6,2},{... | collective-permute-start | bytes 884744 | tf_op jit(solution)/shard_map/ppermute | solution.py:27
  173.0 1.5 collective-permute-done.33.refs_4_
  174.4 3.2 %collective-permute-done.27.refs_1_ = bf16[192,768]{1,0:T(8,128)(2,1)S(1)} collective-permute-done((bf16[192,768]{1,0:T(8,128)(2,1)S(1)}, bf16[192,768]{1,0:T(8,128)(2,1)S(1)}, u32[]{:S(2)}, u32[]{:S(2)}) %collective-permute-start.27) | collective-permute-done | bytes 294944 | tf_op jit(solution)/shard_map/ppermute | solution.py:27
  178.4 1.7 collective-permute-start.35
  180.1 6.6 %collective-permute-done.35.there_ref = bf16[2,96,768]{2,1,0:T(8,128)(2,1)S(1)} collective-permute-done((bf16[2,96,768]{2,1,0:T(8,128)(2,1)S(1)}, bf16[2,96,768]{2,1,0:T(8,128)(2,1)S(1)}, u32[]{:S(2)}, u32[]{:S(2)}) %collective-permute-start.35) | collective-permute-done | bytes 294944 | tf_op jit(solution)/shard_map/ppermute | solution.py:27
  186.7 1.6 finish.1
  (93 shorter events, 16.5 us)
Async XLA Ops:
  0.0 11.0 %collective-permute-start.2 = (bf16[512,768]{1,0:T(8,128)(2,1)}, bf16[512,768]{1,0:T(8,128)(2,1)S(1)}, u32[]{:S(2)}, u32[]{:S(2)}) collective-permute-start(bf16[512,768]{1,0:T(8,128)(2,1)} %refs_0_.2), channel_id=1, source_target_pairs={{0,1},{1,0},{2,3},{3,2},{4,5},{5,4},{6,7},{7,6},{8,9},{9,8},{10,11... | collective-permute-start | bytes 2359304 | tf_op jit(solution)/shard_map/ppermute | solution.py:27
  0.0 24.1 %collective-permute-start.1 = (bf16[512,768]{1,0:T(8,128)(2,1)}, bf16[512,768]{1,0:T(8,128)(2,1)S(1)}, u32[]{:S(2)}, u32[]{:S(2)}) collective-permute-start(bf16[512,768]{1,0:T(8,128)(2,1)} %refs_0_.2), channel_id=1, source_target_pairs={{0,66},{2,64},{64,2},{66,0},{1,67},{3,65},{65,3},{67,1},{4,70},{6,... | collective-permute-start | bytes 2359304 | tf_op jit(solution)/shard_map/ppermute | solution.py:31
  4.1 20.1 %collective-permute-start = (bf16[512,768]{1,0:T(8,128)(2,1)}, bf16[512,768]{1,0:T(8,128)(2,1)S(1)}, u32[]{:S(2)}, u32[]{:S(2)}) collective-permute-start(bf16[512,768]{1,0:T(8,128)(2,1)} %refs_0_.2), channel_id=1, source_target_pairs={{0,2},{2,0},{1,3},{3,1},{4,6},{6,4},{5,7},{7,5},{8,10},{10,8},{9,1... | collective-permute-start | bytes 2359304 | tf_op jit(solution)/shard_map/ppermute | solution.py:27
  4.8 6.2 %copy-start.3 = (bf16[512,768]{1,0:T(8,128)(2,1)S(1)}, bf16[512,768]{1,0:T(8,128)(2,1)}, u32[]{:S(2)}) copy-start(bf16[512,768]{1,0:T(8,128)(2,1)} %refs_0_.2) | copy-start | bytes 2359300
  7.0 17.1 %collective-permute-start.3 = (f32[8,512]{1,0:T(8,128)S(1)}, f32[8,512]{1,0:T(8,128)S(1)}, u32[]{:S(2)}, u32[]{:S(2)}) collective-permute-start(f32[8,512]{1,0:T(8,128)S(1)} %concatenate.9), channel_id=1, source_target_pairs={{0,64},{64,0},{1,65},{65,1},{2,66},{66,2},{3,67},{67,3},{4,68},{68... | collective-permute-start | bytes 49160 | tf_op jit(solution)/shard_map/ppermute | solution.py:27
  11.0 5.3 %copy-start.5 = (bf16[512,768]{1,0:T(8,128)(2,1)}, bf16[512,768]{1,0:T(8,128)(2,1)S(1)}, u32[]{:S(2)}) copy-start(bf16[512,768]{1,0:T(8,128)(2,1)S(1)} %collective-permute-done.2.refs_1_) | copy-start | bytes 2359300
  24.2 9.1 %collective-permute-start.7 = (bf16[512,768]{1,0:T(8,128)(2,1)S(1)}, bf16[512,768]{1,0:T(8,128)(2,1)S(1)}, u32[]{:S(2)}, u32[]{:S(2)}) collective-permute-start(bf16[512,768]{1,0:T(8,128)(2,1)S(1)} %collective-permute-done.1.refs_0_.refs_2_), channel_id=1, source_target_pairs={{0,1},{1,0},{2,3},{3,2},{4,5},{5,4},{6,7},{7,6},{8,9},{9,8},{10,11... | collective-permute-start | bytes 2359304 | tf_op jit(solution)/shard_map/ppermute | solution.py:27
  24.2 9.1 %collective-permute-start.6 = (bf16[512,768]{1,0:T(8,128)(2,1)S(1)}, bf16[512,768]{1,0:T(8,128)(2,1)S(1)}, u32[]{:S(2)}, u32[]{:S(2)}) collective-permute-start(bf16[512,768]{1,0:T(8,128)(2,1)S(1)} %collective-permute-done.refs_0_.refs_2_), channel_id=1, source_target_pairs={{0,1},{1,0},{2,3},{3,2},{4,5},{5,4},{6,7},{7,6},{8,9},{9,8},{10,11... | collective-permute-start | bytes 2359304 | tf_op jit(solution)/shard_map/ppermute | solution.py:27
  24.8 13.9 %collective-permute-start.5 = (bf16[256,768]{1,0:T(8,128)(2,1)S(1)}, bf16[256,768]{1,0:T(8,128)(2,1)S(1)}, u32[]{:S(2)}, u32[]{:S(2)}) collective-permute-start(bf16[256,768]{1,0:T(8,128)(2,1)S(1)} %slice.21), channel_id=1, source_target_pairs={{0,66},{2,64},{64,2},{66,0},{1,67},{3,65},{65,3},{67,1},{4,70},{6,... | collective-permute-start | bytes 1179656 | tf_op jit(solution)/shard_map/ppermute | solution.py:31
  27.7 11.0 %collective-permute-start.4 = (bf16[256,768]{1,0:T(8,128)(2,1)S(1)}, bf16[256,768]{1,0:T(8,128)(2,1)S(1)}, u32[]{:S(2)}, u32[]{:S(2)}) collective-permute-start(bf16[256,768]{1,0:T(8,128)(2,1)S(1)} %slice.20), channel_id=1, source_target_pairs={{0,2},{2,0},{1,3},{3,1},{4,6},{6,4},{5,7},{7,5},{8,10},{10,8},{9,1... | collective-permute-start | bytes 1179656 | tf_op jit(solution)/shard_map/ppermute | solution.py:27
  31.7 1.6 copy-start
  33.3 5.3 %copy-start.7 = (bf16[512,768]{1,0:T(8,128)(2,1)}, bf16[512,768]{1,0:T(8,128)(2,1)S(1)}, u32[]{:S(2)}) copy-start(bf16[512,768]{1,0:T(8,128)(2,1)S(1)} %collective-permute-done.7.refs_0_.refs_3_) | copy-start | bytes 2359300
  33.3 5.3 %copy-start.10 = (bf16[512,768]{1,0:T(8,128)(2,1)}, bf16[512,768]{1,0:T(8,128)(2,1)S(1)}, u32[]{:S(2)}) copy-start(bf16[512,768]{1,0:T(8,128)(2,1)S(1)} %collective-permute-done.6.refs_1_.refs_3_) | copy-start | bytes 2359300
  40.3 18.0 %collective-permute-start.9 = (bf16[512,768]{1,0:T(8,128)(2,1)}, bf16[512,768]{1,0:T(8,128)(2,1)}, u32[]{:S(2)}, u32[]{:S(2)}) collective-permute-start(bf16[512,768]{1,0:T(8,128)(2,1)} %constant_dynamic-update-slice_fusion.refs_1_.refs_0_), channel_id=1, source_target_pairs={{0,1},{1,0},{2,3},{3,2},{4,5},{5,4},{6,7},{7,6},{8,9},{9,8},{10,11... | collective-permute-start | bytes 2359304 | tf_op jit(solution)/shard_map/ppermute | solution.py:27
  40.3 22.2 %collective-permute-start.8 = (bf16[512,512]{1,0:T(8,128)(2,1)}, bf16[512,512]{1,0:T(8,128)(2,1)}, u32[]{:S(2)}, u32[]{:S(2)}) collective-permute-start(bf16[512,512]{1,0:T(8,128)(2,1)} %get-tuple-element.129), channel_id=1, source_target_pairs={{0,64},{64,0},{1,65},{65,1},{2,66},{66,2},{3,67},{67,3},{4,68},{68... | collective-permute-start | bytes 1572872 | tf_op jit(solution)/shard_map/ppermute | solution.py:27
  43.4 1.9 %copy-start.1 = (f32[3,512,512]{2,1,0:T(8,128)S(1)}, f32[3,512,512]{2,1,0:T(8,128)}, u32[]{:S(2)}) copy-start(f32[3,512,512]{2,1,0:T(8,128)} %copy-done) | copy-start | bytes 9437188
  45.3 1.1 copy-start.8
  46.4 5.6 %copy-start.2 = (bf16[512,512]{1,0:T(8,128)(2,1)S(1)}, bf16[512,512]{1,0:T(8,128)(2,1)}, u32[]{:S(2)}) copy-start(bf16[512,512]{1,0:T(8,128)(2,1)} %get-tuple-element.237.og_ref.og_a) | copy-start | bytes 1572868
  66.8 10.7 %collective-permute-start.10 = (bf16[528,128]{1,0:T(8,128)(2,1)S(1)}, bf16[528,128]{1,0:T(8,128)(2,1)S(1)}, u32[]{:S(2)}, u32[]{:S(2)}) collective-permute-start(bf16[528,128]{1,0:T(8,128)(2,1)S(1)} %get-tuple-element.140), channel_id=1, source_target_pairs={{0,8},{4,12},{8,0},{12,4},{1,9},{5,13},{9,1},{13,5},{2,10},{6,14},... | collective-permute-start | bytes 405512 | tf_op jit(solution)/shard_map/ppermute | solution.py:27
  70.1 7.4 %collective-permute-start.11 = (bf16[528,128]{1,0:T(8,128)(2,1)S(1)}, bf16[528,128]{1,0:T(8,128)(2,1)S(1)}, u32[]{:S(2)}, u32[]{:S(2)}) collective-permute-start(bf16[528,128]{1,0:T(8,128)(2,1)S(1)} %get-tuple-element.141), channel_id=1, source_target_pairs={{0,4},{4,8},{8,12},{12,0},{1,5},{5,9},{9,13},{13,1},{2,6},{6,10},{... | collective-permute-start | bytes 405512 | tf_op jit(solution)/shard_map/ppermute | solution.py:27
  70.7 6.8 %collective-permute-start.12 = (bf16[528,128]{1,0:T(8,128)(2,1)S(1)}, bf16[528,128]{1,0:T(8,128)(2,1)S(1)}, u32[]{:S(2)}, u32[]{:S(2)}) collective-permute-start(bf16[528,128]{1,0:T(8,128)(2,1)S(1)} %get-tuple-element.142), channel_id=1, source_target_pairs={{0,12},{4,0},{8,4},{12,8},{1,13},{5,1},{9,5},{13,9},{2,14},{6,2},{... | collective-permute-start | bytes 405512 | tf_op jit(solution)/shard_map/ppermute | solution.py:27
  78.3 9.3 %collective-permute-start.15 = (bf16[528,128]{1,0:T(8,128)(2,1)S(1)}, bf16[528,128]{1,0:T(8,128)(2,1)S(1)}, u32[]{:S(2)}, u32[]{:S(2)}) collective-permute-start(bf16[528,128]{1,0:T(8,128)(2,1)S(1)} %get-tuple-element.148.a), channel_id=1, source_target_pairs={{0,48},{16,0},{32,16},{48,32},{1,49},{17,1},{33,17},{49,33},{2,50}... | collective-permute-start | bytes 405512 | tf_op jit(solution)/shard_map/ppermute | solution.py:27
  81.1 8.7 %collective-permute-start.14 = (bf16[528,128]{1,0:T(8,128)(2,1)S(1)}, bf16[528,128]{1,0:T(8,128)(2,1)S(1)}, u32[]{:S(2)}, u32[]{:S(2)}) collective-permute-start(bf16[528,128]{1,0:T(8,128)(2,1)S(1)} %get-tuple-element.148.a), channel_id=1, source_target_pairs={{0,16},{16,32},{32,48},{48,0},{1,17},{17,33},{33,49},{49,1},{2,18}... | collective-permute-start | bytes 405512 | tf_op jit(solution)/shard_map/ppermute | solution.py:27
  81.1 8.7 %collective-permute-start.13 = (bf16[528,128]{1,0:T(8,128)(2,1)S(1)}, bf16[528,128]{1,0:T(8,128)(2,1)S(1)}, u32[]{:S(2)}, u32[]{:S(2)}) collective-permute-start(bf16[528,128]{1,0:T(8,128)(2,1)S(1)} %get-tuple-element.148.a), channel_id=1, source_target_pairs={{0,32},{16,48},{32,0},{48,16},{1,33},{17,49},{33,1},{49,17},{2,34}... | collective-permute-start | bytes 405512 | tf_op jit(solution)/shard_map/ppermute | solution.py:27
  83.4 12.5 %copy-start.11 = (bf16[512,768]{1,0:T(8,128)(2,1)S(1)}, bf16[512,768]{1,0:T(8,128)(2,1)}, u32[]{:S(2)}) copy-start(bf16[512,768]{1,0:T(8,128)(2,1)} %copy-done.10) | copy-start | bytes 2359300
  87.6 8.3 %copy-start.4 = (bf16[512,768]{1,0:T(8,128)(2,1)S(1)}, bf16[512,768]{1,0:T(8,128)(2,1)}, u32[]{:S(2)}) copy-start(bf16[512,768]{1,0:T(8,128)(2,1)} %refs_0_.2) | copy-start | bytes 2359300
  87.6 8.3 %copy-start.6 = (bf16[512,768]{1,0:T(8,128)(2,1)S(1)}, bf16[512,768]{1,0:T(8,128)(2,1)}, u32[]{:S(2)}) copy-start(bf16[512,768]{1,0:T(8,128)(2,1)} %copy-done.5) | copy-start | bytes 2359300
  90.6 10.7 %collective-permute-start.16 = (bf16[512,128]{1,0:T(8,128)(2,1)S(1)}, bf16[512,128]{1,0:T(8,128)(2,1)S(1)}, u32[]{:S(2)}, u32[]{:S(2)}) collective-permute-start(bf16[512,128]{1,0:T(8,128)(2,1)S(1)} %get-tuple-element.162), channel_id=1, source_target_pairs={{0,8},{4,12},{8,0},{12,4},{1,9},{5,13},{9,1},{13,5},{2,10},{6,14},... | collective-permute-start | bytes 393224 | tf_op jit(solution)/shard_map/ppermute | solution.py:27
  92.6 8.8 %collective-permute-start.17 = (bf16[512,128]{1,0:T(8,128)(2,1)S(1)}, bf16[512,128]{1,0:T(8,128)(2,1)S(1)}, u32[]{:S(2)}, u32[]{:S(2)}) collective-permute-start(bf16[512,128]{1,0:T(8,128)(2,1)S(1)} %get-tuple-element.163), channel_id=1, source_target_pairs={{0,4},{4,8},{8,12},{12,0},{1,5},{5,9},{9,13},{13,1},{2,6},{6,10},{... | collective-permute-start | bytes 393224 | tf_op jit(solution)/shard_map/ppermute | solution.py:27
  94.1 7.3 %collective-permute-start.18 = (bf16[512,128]{1,0:T(8,128)(2,1)S(1)}, bf16[512,128]{1,0:T(8,128)(2,1)S(1)}, u32[]{:S(2)}, u32[]{:S(2)}) collective-permute-start(bf16[512,128]{1,0:T(8,128)(2,1)S(1)} %get-tuple-element.164), channel_id=1, source_target_pairs={{0,12},{4,0},{8,4},{12,8},{1,13},{5,1},{9,5},{13,9},{2,14},{6,2},{... | collective-permute-start | bytes 393224 | tf_op jit(solution)/shard_map/ppermute | solution.py:27
  95.9 2.1 %copy-start.9 = (bf16[512,768]{1,0:T(8,128)(2,1)S(1)}, bf16[512,768]{1,0:T(8,128)(2,1)}, u32[]{:S(2)}) copy-start(bf16[512,768]{1,0:T(8,128)(2,1)} %copy-done.7) | copy-start | bytes 2359300
  109.9 15.0 %collective-permute-start.19 = (bf16[384,768]{1,0:T(8,128)(2,1)S(1)}, bf16[384,768]{1,0:T(8,128)(2,1)S(1)}, u32[]{:S(2)}, u32[]{:S(2)}) collective-permute-start(bf16[384,768]{1,0:T(8,128)(2,1)S(1)} %get-tuple-element.187), channel_id=1, source_target_pairs={{0,16},{16,32},{32,48},{48,0},{1,17},{17,33},{33,49},{49,1},{2,18}... | collective-permute-start | bytes 1769480 | tf_op jit(solution)/shard_map/ppermute | solution.py:27
  110.0 14.9 %collective-permute-start.20 = (bf16[384,768]{1,0:T(8,128)(2,1)S(1)}, bf16[384,768]{1,0:T(8,128)(2,1)S(1)}, u32[]{:S(2)}, u32[]{:S(2)}) collective-permute-start(bf16[384,768]{1,0:T(8,128)(2,1)S(1)} %get-tuple-element.188), channel_id=1, source_target_pairs={{0,48},{16,0},{32,16},{48,32},{1,49},{17,1},{33,17},{49,33},{2,50}... | collective-permute-start | bytes 1769480 | tf_op jit(solution)/shard_map/ppermute | solution.py:27
  113.2 16.5 %collective-permute-start.23 = (bf16[384,768]{1,0:T(8,128)(2,1)S(1)}, bf16[384,768]{1,0:T(8,128)(2,1)S(1)}, u32[]{:S(2)}, u32[]{:S(2)}) collective-permute-start(bf16[384,768]{1,0:T(8,128)(2,1)S(1)} %get-tuple-element.203), channel_id=1, source_target_pairs={{0,4},{4,8},{8,12},{12,0},{1,5},{5,9},{9,13},{13,1},{2,6},{6,10},{... | collective-permute-start | bytes 1769480 | tf_op jit(solution)/shard_map/ppermute | solution.py:27
  113.5 16.2 %collective-permute-start.24 = (bf16[384,768]{1,0:T(8,128)(2,1)S(1)}, bf16[384,768]{1,0:T(8,128)(2,1)S(1)}, u32[]{:S(2)}, u32[]{:S(2)}) collective-permute-start(bf16[384,768]{1,0:T(8,128)(2,1)S(1)} %get-tuple-element.204), channel_id=1, source_target_pairs={{0,12},{4,0},{8,4},{12,8},{1,13},{5,1},{9,5},{13,9},{2,14},{6,2},{... | collective-permute-start | bytes 1769480 | tf_op jit(solution)/shard_map/ppermute | solution.py:27
  126.4 24.9 %collective-permute-start.21 = (bf16[768,768]{1,0:T(8,128)(2,1)S(1)}, bf16[768,768]{1,0:T(8,128)(2,1)S(1)}, u32[]{:S(2)}, u32[]{:S(2)}) collective-permute-start(bf16[768,768]{1,0:T(8,128)(2,1)S(1)} %get-tuple-element.199), channel_id=1, source_target_pairs={{0,16},{16,32},{32,48},{48,0},{1,17},{17,33},{33,49},{49,1},{2,18}... | collective-permute-start | bytes 3538952 | tf_op jit(solution)/shard_map/ppermute | solution.py:27
  126.5 24.8 %collective-permute-start.22 = (bf16[768,768]{1,0:T(8,128)(2,1)S(1)}, bf16[768,768]{1,0:T(8,128)(2,1)S(1)}, u32[]{:S(2)}, u32[]{:S(2)}) collective-permute-start(bf16[768,768]{1,0:T(8,128)(2,1)S(1)} %get-tuple-element.200), channel_id=1, source_target_pairs={{0,48},{16,0},{32,16},{48,32},{1,49},{17,1},{33,17},{49,33},{2,50}... | collective-permute-start | bytes 3538952 | tf_op jit(solution)/shard_map/ppermute | solution.py:27
  131.2 25.9 %collective-permute-start.29 = (bf16[768,768]{1,0:T(8,128)(2,1)S(1)}, bf16[768,768]{1,0:T(8,128)(2,1)S(1)}, u32[]{:S(2)}, u32[]{:S(2)}) collective-permute-start(bf16[768,768]{1,0:T(8,128)(2,1)S(1)} %get-tuple-element.207), channel_id=1, source_target_pairs={{0,4},{4,8},{8,12},{12,0},{1,5},{5,9},{9,13},{13,1},{2,6},{6,10},{... | collective-permute-start | bytes 3538952 | tf_op jit(solution)/shard_map/ppermute | solution.py:27
  131.2 25.8 %collective-permute-start.30 = (bf16[768,768]{1,0:T(8,128)(2,1)S(1)}, bf16[768,768]{1,0:T(8,128)(2,1)S(1)}, u32[]{:S(2)}, u32[]{:S(2)}) collective-permute-start(bf16[768,768]{1,0:T(8,128)(2,1)S(1)} %get-tuple-element.208), channel_id=1, source_target_pairs={{0,12},{4,0},{8,4},{12,8},{1,13},{5,1},{9,5},{13,9},{2,14},{6,2},{... | collective-permute-start | bytes 3538952 | tf_op jit(solution)/shard_map/ppermute | solution.py:27
  152.2 9.1 %collective-permute-start.25 = (bf16[96,768]{1,0:T(8,128)(2,1)S(1)}, bf16[96,768]{1,0:T(8,128)(2,1)S(1)}, u32[]{:S(2)}, u32[]{:S(2)}) collective-permute-start(bf16[96,768]{1,0:T(8,128)(2,1)S(1)} %get-tuple-element.219), channel_id=1, source_target_pairs={{0,4},{4,8},{8,12},{12,0},{1,5},{5,9},{9,13},{13,1},{2,6},{6,10},{... | collective-permute-start | bytes 442376 | tf_op jit(solution)/shard_map/ppermute | solution.py:27
  152.3 9.0 %collective-permute-start.26 = (bf16[96,768]{1,0:T(8,128)(2,1)S(1)}, bf16[96,768]{1,0:T(8,128)(2,1)S(1)}, u32[]{:S(2)}, u32[]{:S(2)}) collective-permute-start(bf16[96,768]{1,0:T(8,128)(2,1)S(1)} %get-tuple-element.220), channel_id=1, source_target_pairs={{0,12},{4,0},{8,4},{12,8},{1,13},{5,1},{9,5},{13,9},{2,14},{6,2},{... | collective-permute-start | bytes 442376 | tf_op jit(solution)/shard_map/ppermute | solution.py:27
  158.0 7.7 %collective-permute-start.31 = (bf16[96,768]{1,0:T(8,128)(2,1)S(1)}, bf16[96,768]{1,0:T(8,128)(2,1)S(1)}, u32[]{:S(2)}, u32[]{:S(2)}) collective-permute-start(bf16[96,768]{1,0:T(8,128)(2,1)S(1)} %get-tuple-element.229), channel_id=1, source_target_pairs={{0,16},{16,32},{32,48},{48,0},{1,17},{17,33},{33,49},{49,1},{2,18}... | collective-permute-start | bytes 442376 | tf_op jit(solution)/shard_map/ppermute | solution.py:27
  158.1 7.6 %collective-permute-start.32 = (bf16[96,768]{1,0:T(8,128)(2,1)S(1)}, bf16[96,768]{1,0:T(8,128)(2,1)S(1)}, u32[]{:S(2)}, u32[]{:S(2)}) collective-permute-start(bf16[96,768]{1,0:T(8,128)(2,1)S(1)} %get-tuple-element.230), channel_id=1, source_target_pairs={{0,48},{16,0},{32,16},{48,32},{1,49},{17,1},{33,17},{49,33},{2,50}... | collective-permute-start | bytes 442376 | tf_op jit(solution)/shard_map/ppermute | solution.py:27
  166.4 8.0 %collective-permute-start.33 = (bf16[192,768]{1,0:T(8,128)(2,1)S(1)}, bf16[192,768]{1,0:T(8,128)(2,1)S(1)}, u32[]{:S(2)}, u32[]{:S(2)}) collective-permute-start(bf16[192,768]{1,0:T(8,128)(2,1)S(1)} %get-tuple-element.233), channel_id=1, source_target_pairs={{0,16},{16,32},{32,48},{48,0},{1,17},{17,33},{33,49},{49,1},{2,18}... | collective-permute-start | bytes 884744 | tf_op jit(solution)/shard_map/ppermute | solution.py:27
  166.5 7.9 %collective-permute-start.34 = (bf16[192,768]{1,0:T(8,128)(2,1)S(1)}, bf16[192,768]{1,0:T(8,128)(2,1)S(1)}, u32[]{:S(2)}, u32[]{:S(2)}) collective-permute-start(bf16[192,768]{1,0:T(8,128)(2,1)S(1)} %get-tuple-element.234), channel_id=1, source_target_pairs={{0,48},{16,0},{32,16},{48,32},{1,49},{17,1},{33,17},{49,33},{2,50}... | collective-permute-start | bytes 884744 | tf_op jit(solution)/shard_map/ppermute | solution.py:27
  169.7 7.9 %collective-permute-start.27 = (bf16[192,768]{1,0:T(8,128)(2,1)S(1)}, bf16[192,768]{1,0:T(8,128)(2,1)S(1)}, u32[]{:S(2)}, u32[]{:S(2)}) collective-permute-start(bf16[192,768]{1,0:T(8,128)(2,1)S(1)} %get-tuple-element.221), channel_id=1, source_target_pairs={{0,4},{4,8},{8,12},{12,0},{1,5},{5,9},{9,13},{13,1},{2,6},{6,10},{... | collective-permute-start | bytes 884744 | tf_op jit(solution)/shard_map/ppermute | solution.py:27
  169.7 7.9 %collective-permute-start.28 = (bf16[192,768]{1,0:T(8,128)(2,1)S(1)}, bf16[192,768]{1,0:T(8,128)(2,1)S(1)}, u32[]{:S(2)}, u32[]{:S(2)}) collective-permute-start(bf16[192,768]{1,0:T(8,128)(2,1)S(1)} %get-tuple-element.222), channel_id=1, source_target_pairs={{0,12},{4,0},{8,4},{12,8},{1,13},{5,1},{9,5},{13,9},{2,14},{6,2},{... | collective-permute-start | bytes 884744 | tf_op jit(solution)/shard_map/ppermute | solution.py:27
  178.4 8.3 %collective-permute-start.35 = (bf16[2,96,768]{2,1,0:T(8,128)(2,1)S(1)}, bf16[2,96,768]{2,1,0:T(8,128)(2,1)S(1)}, u32[]{:S(2)}, u32[]{:S(2)}) collective-permute-start(bf16[2,96,768]{2,1,0:T(8,128)(2,1)S(1)} %get-tuple-element.236), channel_id=1, source_target_pairs={{0,64},{64,0},{1,65},{65,1},{2,66},{66,2},{3,67},{67,3},{4,68},{68... | collective-permute-start | bytes 884744 | tf_op jit(solution)/shard_map/ppermute | solution.py:27

commit v2 on v1

--- a/solution.py
+++ b/solution.py
@@ -18,13 +18,8 @@
     return jnp.dot(a, b, preferred_element_type=F32)
 
 
-def shift(axis, by):
-    n = lax.axis_size(axis)
-    return [(i, (i + by) % n) for i in range(n)]
-
-
 def send(x, axis, by):
-    return lax.ppermute(x, axis, shift(axis, by))
+    return lax.ppermute(x, axis, [(i, i ^ by) for i in range(lax.axis_size(axis))])
 
 
 def across(x):
@@ -76,60 +71,70 @@
             acc = jnp.where(row < s[LEN], acc, 0.0)
         out[0] = acc.astype(out.dtype)
 
-    tile = pl.BlockSpec((1, tokens, cols), lambda g, s: (g, 0, 0))
+    block = cols // 2
+    tile = pl.BlockSpec((1, tokens, block), lambda g, j, s: (g, 0, j))
     in_specs = [whole(x) for x in shards]
     for flip in flips:
         in_specs.append(
-            pl.BlockSpec((1, width, cols), lambda g, s, flip=flip: (g, s[TEN] ^ flip, s[Z]))
+            pl.BlockSpec(
+                (1, width, block), lambda g, j, s, flip=flip: (g, s[TEN] ^ flip, 2 * s[Z] + j)
+            )
         )
     operands = [*shards, *([weight] * n)]
     if partial is not None:
         in_specs.append(tile)
         operands.append(partial)
     out = shape((3, tokens, cols), BF16 if last else F32)
-    return call("project", body, table, (3,), operands, in_specs, out, tile, 20)
-
-
-def shard_states(table, qkvs, out_grads, cumul):
-    tokens = qkvs[0].shape[1]
-    heads = qkvs[0].shape[2] // HEAD
+    return call("project", body, table, (3, 2), operands, in_specs, out, tile, 20)
+
+
+def shard_states(table, qkv, out_grad, cumul, which, so_far):
+    tokens = qkv.shape[1]
+    heads = qkv.shape[2] // HEAD
     scale = HEAD**-0.5
 
-    def body(s, qkv_a, qkv_b, og_a, og_b, cum_ref, *outs):
+    def body(s, qkv_ref, og_ref, cum_ref, *refs):
+        outs = refs[-4:]
         r = pl.program_id(0)
-        who = (s[Y] + r) % 4
-        blocks, totals = [], []
-        for i, (qkv_ref, og_ref) in enumerate(((qkv_a, og_a), (qkv_b, og_b))):
-            row = cum_ref[pl.ds(i * heads + who, 1), :]
-            total = row[:, tokens - 1 : tokens]
-            keys_t = qkv_ref[1].astype(F32).T
-            query_t = qkv_ref[0].astype(F32).T
-            keys_t = (keys_t * jnp.exp(total - row)).astype(BF16)
-            query_t = (query_t * (scale * jnp.exp(row))).astype(BF16)
-            blocks.append((dot(keys_t, qkv_ref[2]), dot(query_t, og_ref[...])))
-            totals.append(total)
+        row = cum_ref[pl.ds(which * heads + (s[Y] ^ r), 1), :]
+        total = row[:, tokens - 1 : tokens]
+        keys_t = qkv_ref[1].T.astype(F32)
+        query_t = qkv_ref[0].T.astype(F32)
+        keys_t = (keys_t * jnp.exp(total - row)).astype(BF16)
+        query_t = (query_t * (scale * jnp.exp(row))).astype(BF16)
+        states = (dot(keys_t, qkv_ref[2]), dot(query_t, og_ref[...]))
         at = lax.broadcasted_iota(jnp.int32, (16, HEAD), 0)
-        tail = jnp.where(at == s[Z], totals[0], totals[1]).astype(BF16)
+        tail = jnp.broadcast_to(total, (16, HEAD)).astype(BF16)
         for k, out in enumerate(outs):
 
             @pl.when(r == k)
-            def _(out=out):
-                for i in range(2):
-                    for kind in range(2):
-                        start = pl.multiple_of((2 * kind + (i ^ s[Z])) * HEAD, HEAD)
-                        out[pl.ds(start, HEAD), :] = blocks[i][kind].astype(BF16)
-                out[4 * HEAD :, :] = tail
+            def _(k=k, out=out):
+                here = s[Z] ^ which
+                if so_far is not None:
+                    out[...] = refs[k][...]
+                for kind in range(2):
+                    start = pl.multiple_of((2 * kind + here) * HEAD, HEAD)
+                    out[pl.ds(start, HEAD), :] = states[kind].astype(BF16)
+                if so_far is None:
+                    out[4 * HEAD :, :] = tail
+                else:
+                    out[4 * HEAD :, :] = jnp.where(at == here, tail, refs[k][4 * HEAD :, :])
 
     message = shape((4 * HEAD + 16, HEAD))
-    qkv_tile = pl.BlockSpec((3, tokens, HEAD), lambda r, s: (0, 0, (s[Y] + r) % 4))
-    og_tile = pl.BlockSpec((tokens, HEAD), lambda r, s: (0, (s[Y] + r) % 4))
+    operands = [qkv, out_grad, cumul, *(so_far or ())]
+    in_specs = [
+        pl.BlockSpec((3, tokens, HEAD), lambda r, s: (0, 0, s[Y] ^ r)),
+        pl.BlockSpec((tokens, HEAD), lambda r, s: (0, s[Y] ^ r)),
+        whole(cumul),
+        *[whole(m) for m in so_far or ()],
+    ]
     return call(
         "shard_states",
         body,
         table,
         (4,),
-        (*qkvs, *out_grads, cumul),
-        [qkv_tile, qkv_tile, og_tile, og_tile, whole(cumul)],
+        operands,
+        in_specs,
         [message] * 4,
         [whole(message)] * 4,
         12,
@@ -138,7 +143,7 @@
 
 def in_order(refs, place, held):
     for r, ref in enumerate(refs):
-        held[(place - r + 4) % 4] = ref[...]
+        held[place ^ r] = ref[...]
 
 
 def spread(pair):
@@ -227,7 +232,7 @@
         start = mine[0] + spread(edges[0]) * across_up
         finish = mine[1] + spread(edges[1]) * across_down
         for r, out in enumerate(outs):
-            t = (s[Y] + r) % 4
+            t = s[Y] ^ r
             out[:half, :] = (before_ref[t] + spread(prior_ref[t]) * start).astype(BF16)
             out[half:, :] = (after_ref[t] + spread(later_ref[t]) * finish).astype(BF16)
 
@@ -406,8 +411,8 @@
                     outs[side * len(places) + k][...] = acc
 
     step = places[1] - places[0] if len(places) > 1 else 0
-    by_x = pl.BlockSpec((1, 4, rows, tokens), lambda r, s: ((s[X] + places[0] + step * r) % 4, 0, 0, 0))
-    by_y = pl.BlockSpec((4, 1, rows, tokens), lambda r, s: (0, (s[Y] + places[0] + step * r) % 4, 0, 0))
+    by_x = pl.BlockSpec((1, 4, rows, tokens), lambda r, s: (s[X] ^ (places[0] + step * r), 0, 0, 0))
+    by_y = pl.BlockSpec((4, 1, rows, tokens), lambda r, s: (0, s[Y] ^ (places[0] + step * r), 0, 0))
     outs = [shape((2 * rows if split else 4 * rows, cols))] * (4 if split else 2 * len(places))
     operands = (turned[0], turned[0], turned[1], turned[1], *lefts, *rights)
     return call(
@@ -423,7 +428,9 @@
     )
 
 
-def add_halves(table, near_up, near_down, up, down):
+def add_halves(table, third, first_place, halves):
+    up, down = halves
+    near_up, near_down = third, first_place
     n, cols = up.shape
 
     def body(s, a, b, u, d, out_a, out_b):
@@ -451,7 +458,7 @@
 
     def body(s, a, b, c, far_up, far_down, one, three, here):
         def block(r):
-            at = pl.ds(pl.multiple_of((s[axis] + r) % 4 * rows, rows), rows)
+            at = pl.ds(pl.multiple_of((s[axis] ^ r) * rows, rows), rows)
             return (a[at, :].astype(F32) + b[at, :].astype(F32) + c[at, :].astype(F32)).astype(BF16)
 
         far = block(2)
@@ -516,6 +523,12 @@
     out = shape((3, rows, 4 * side), F32)
     operands = (here, there)
     return call("finish", body, table, (1,), operands, [whole(here)] * 2, out, whole(out), 8)
+
+
+def swaps(pieces, left, right):
+    a, c = send(pieces[0], left, 1), send(pieces[2], right, 1)
+    b, d = send(pieces[1], left, 3), send(pieces[3], right, 3)
+    return [a, b], [c, d]
 
 
 def device_part(activations, qkv_weight, log_decay, lengths, out_grad):
@@ -543,71 +556,71 @@
     og_other = lax.dynamic_slice_in_dim(out_grad, (1 - here_z) * width, width, axis=1)
 
     acc_own = project(table, [activations, core], (0, 1), weight, None, False)
-    near, side, acc_own, note, og_other = tied((near, side, acc_own, note, og_other))
+    near, side, acc_own = tied((near, side, acc_own))
+    half = tokens // 2
+    near_core = send(near, "co", 1)
+    side_core = send(side, "co", 1)
+    far = [send(side[:half], "zl", 1), across(near[half:])]
+    qkv_own = project(table, [near, near_core], (2, 3), weight, acc_own, True)
+    side_core, note, og_other, qkv_own = tied((side_core, note, og_other, qkv_own))
+    acc_pair = project(table, [side, side_core], (2, 3), weight, None, False)
     cumul = jnp.concatenate([lax.dynamic_slice_in_dim(cumul, here_z * per, per), note[:per]])
     table_pair = jnp.stack([*fixed, note[per, 0].astype(jnp.int32)]).astype(jnp.int32)
-    half = tokens // 2
-    far = [send(side[:half], "zl", 1), across(near[half:])]
-    near_core = send(near, "co", 1)
-    side_core = send(side, "co", 1)
-    acc_pair = project(table, [side], (2,), weight, None, False)
-    near_core, side_core, acc_pair = tied((near_core, side_core, acc_pair))
-    qkv_own = project(table, [near, near_core], (2, 3), weight, acc_own, True)
-    *far, qkv_own = tied((*far, qkv_own))
+    *far, acc_pair = tied((*far, acc_pair))
     far = jnp.concatenate(far)
     far_core = send(far, "co", 1)
     og_pair = send(tied((og_other, far))[0], "c0", 1)
-    acc_pair = project(table, [side_core, far], (3, 0), weight, acc_pair, False)
-    far_core, acc_pair = tied((far_core, acc_pair))
-    qkv_pair = project(table_pair, [far_core], (1,), weight, acc_pair, True)
-
+    first, _ = tied(([activations, core, near, near_core], far))
+    turned = [turn(table, first)]
+    to_y = shard_states(table, qkv_own, og_own, cumul, 0, None)
+    far_core, acc_pair, to_y, turned = tied((far_core, acc_pair, to_y, turned))
+    qkv_pair = project(table_pair, [far, far_core], (0, 1), weight, acc_pair, True)
+
+    to_y = shard_states(table, qkv_pair, og_pair, cumul, 1, to_y)
+    at_y = [send(to_y[r], "c2", r) for r in (1, 3, 2)]
+    qkv_own, _ = tied((qkv_own, to_y[0]))
     local_own = local_grads(table, qkv_own, og_own, cumul, 0, 0, per, None)
-    og_pair, local_own, qkv_pair = tied((og_pair, local_own, qkv_pair))
-    to_y = shard_states(table, (qkv_own, qkv_pair), (og_own, og_pair), cumul)
-    at_y = [send(to_y[r], "c2", r) for r in (2, 1, 3)]
+    at_y, local_own = tied((at_y, local_own))
+    before, after, prior, later, ring = ring_y(table, [to_y[0], at_y[0], at_y[2], at_y[1]])
+    at_x = [send(ring, "c1", r) for r in (1, 3, 2)]
+    qkv_pair, _ = tied((qkv_pair, ring))
     local = local_grads(table_pair, qkv_pair, og_pair, cumul, 1, 0, per // 2, None)
-    at_y, local = tied((at_y, local))
-    before, after, prior, later, ring = ring_y(table, [to_y[0], at_y[1], at_y[0], at_y[2]])
-    at_x = [send(ring, "c1", r) for r in (2, 1, 3)]
-    local, _ = tied((local, ring))
+    at_x, local = tied((at_x, local))
+    back = arrivals(table, [ring, at_x[0], at_x[2], at_x[1]], before, after, prior, later)
+    states = [send(back[r], "c2", r) for r in (1, 3, 2)]
+    local, _ = tied((local, back[0]))
     local = local_grads(table_pair, qkv_pair, og_pair, cumul, 1, per // 2, per // 2, local)
-    at_x, local = tied((at_x, local))
-    back = arrivals(table, [ring, at_x[1], at_x[0], at_x[2]], before, after, prior, later)
-    states = [send(back[r], "c2", r) for r in (2, 1, 3)]
-    first, second, _ = tied(([activations, core, near, near_core], [far, far_core, side, side_core], back[0]))
-    turned = [turn(table, first), turn(table, second)]
-    states, turned = tied((states, turned))
-    states = [back[0], states[1], states[0], states[2]]
+    second, _ = tied(([far, far_core, side, side_core], back[0]))
+    turned.append(turn(table, second))
+    states, turned, local = tied((states, turned, local))
+    states = [back[0], states[0], states[2], states[1]]
 
     left_own, right_own = whole_grads(table, 0, *local_own, states)
     left_pair, right_pair = whole_grads(table, 1, *local, states)
     lefts, rights = (left_own, left_pair), (right_own, right_pair)
-    far_left, far_right = (
-        lambda outs: (outs[:2], outs[2:])
-    )(weight_part(table, turned, lefts, rights, (2,), True))
-    l_half = [send(x, "c1", by) for x, by in zip(far_left, (1, -1))]
-    r_half = [send(x, "c2", by) for x, by in zip(far_right, (1, -1))]
-    turned, _ = tied((turned, far_left))
-    pieces = weight_part(table, turned, lefts, rights, (1, 3), False)
-    l_half, pieces = tied((l_half, pieces))
-    l_near = add_halves(table, *pieces[:2], *l_half)
-    l_got = [send(x, "c1", by) for x, by in zip(l_near, (1, -1))]
-    r_half, _ = tied((r_half, l_near))
-    r_near = add_halves(table, *pieces[2:], *r_half)
-    r_got = [send(x, "c2", by) for x, by in zip(r_near, (1, -1))]
-    turned, _ = tied((turned, r_near))
+    far_piece = weight_part(table, turned, lefts, rights, (2,), True)
+    l_half, r_half = swaps(far_piece, "c1", "c2")
+    turned, _ = tied((turned, far_piece[0]))
+    l_one, l_three, r_one, r_three = weight_part(table, turned, lefts, rights, (1, 3), False)
+    l_half, l_one = tied((l_half, l_one))
+    l_three, l_one = add_halves(table, l_three, l_one, l_half)
+    l_got = [send(l_one, "c1", 1), send(l_three, "c1", 3)]
+    r_half, _ = tied((r_half, l_one))
+    r_three, r_one = add_halves(table, r_three, r_one, r_half)
+    r_got = [send(r_one, "c2", 1), send(r_three, "c2", 3)]
+    turned, _ = tied((turned, r_one))
     own = weight_part(table, turned, lefts, rights, (0,), False)
     l_got, own = tied((l_got, own))
     l_cut = cut_blocks(table, Y, own[0], *l_got)
     r_got, _ = tied((r_got, l_cut))
     r_cut = cut_blocks(table, X, own[1], *r_got)
-    l_half = [send(x, "c2", by) for x, by in zip(l_cut[:2], (1, -1))]
-    r_half = [send(x, "c1", by) for x, by in zip(r_cut[:2], (1, -1))]
-    l_near = add_halves(table, *l_cut[2:4], *l_half)
-    l_got = [send(x, "c2", by) for x, by in zip(l_near, (1, -1))]
-    r_half, _ = tied((r_half, l_near))
-    r_near = add_halves(table, *r_cut[2:4], *r_half)
-    r_got = [send(x, "c1", by) for x, by in zip(r_near, (1, -1))]
+    l_half = [send(x, "c2", by) for x, by in zip(l_cut[:2], (1, 3))]
+    r_half = [send(x, "c1", by) for x, by in zip(r_cut[:2], (1, 3))]
+    l_three, l_one = add_halves(table, l_cut[3], l_cut[2], l_half)
+    l_got = [send(l_one, "c2", 1), send(l_three, "c2", 3)]
+    r_half, _ = tied((r_half, l_one))
+    r_three, r_one = add_halves(table, r_cut[3], r_cut[2], r_half)
+    r_got = [send(r_one, "c1", 1), send(r_three, "c1", 3)]
     here, there = final_sums(table, ((l_cut[4], *l_got), (r_cut[4], *r_got)))
     there = send(there, "c0", 1)
     return jnp.transpose(finish(table, here, there), (1, 0, 2))

time: 189 us -> 203 us (1.074)
  starting transfers between devices: 55.8 us -> 45.3 us
  waiting for transfers between devices: 40.2 us -> 49.3 us
  local copies, waits for them, and re-layouts: 9.44 us -> 17.9 us
  Pallas kernels: 79.1 us -> 86.1 us
    ppermute x34, starting transfers between devices: 48.8 us -> 39.7 us  [send(): lax.ppermute(x, axis, [(i, i ^ by) for i in range(lax.axis_size(axis))])]
    ppermute x2, waiting for transfers between devices: 0.01 us -> 8.04 us  [across(): return lax.ppermute(x, ('c0', 'zl'), [(0, 3), (1, 2), (2, 1), (3, 0)])]
    pallas_call x26, Pallas kernels: 79.1 us -> 86.1 us  [call(): pl.pallas_call(body, grid_spec=pltpu.PrefetchScalarGridSpec(num_scalar_pr...]
    slice x2, local copies, waits for them, and re-layouts: 0.05 us -> 3.6 us  [device_part(): far = [send(side[:half], 'zl', 1), across(near[half:])]]
    unnamed x25 -> x35, local copies, waits for them, and re-layouts: 5.47 us -> 8.45 us
  transfers between devices with their start and end apart: 36 -> 36, of which waited for: 9 -> 17; matrix products, arithmetic and copies ran while one was open for 3% -> 5% of each run, Pallas kernels for 33% -> 34%
where the time goes in v2:
time: 203 us; the launch traced here: 202 us
  Pallas kernels  86.1 us (42%)
  waiting for transfers between devices  49.3 us (24%)
  starting transfers between devices  45.3 us (22%)
  local copies, waits for them, and re-layouts  17.9 us (9%)
    pallas_call x26, Pallas kernels, call(): pl.pallas_call(body, grid_spec=pltpu.PrefetchScalarGridSpec(num_scalar_pr...  86.1 us
    ppermute x34, waiting for transfers between devices, send(): lax.ppermute(x, axis, [(i, i ^ by) for i in range(lax.axis_size(axis))])  41.3 us
    ppermute x34, starting transfers between devices, send(): lax.ppermute(x, axis, [(i, i ^ by) for i in range(lax.axis_size(axis))])  39.7 us
    unnamed x35, local copies, waits for them, and re-layouts  8.45 us
    ppermute x2, waiting for transfers between devices, across(): return lax.ppermute(x, ('c0', 'zl'), [(0, 3), (1, 2), (2, 1), (3, 0)])  8.04 us
    ppermute x2, starting transfers between devices, across(): return lax.ppermute(x, ('c0', 'zl'), [(0, 3), (1, 2), (2, 1), (3, 0)])  5.61 us
  transfers between devices with their start and end apart: 36, of which 17 were waited for; matrix products, arithmetic and copies ran while one was open for 5% of the time, Pallas kernels for 34%

profile of v2, /device:TPU:0, one launch (start us, length us, event | category | flops | bytes accessed | tf_op | source)
XLA Modules:
  0.0 202.3 jit_solution(1372870183613433606)
XLA Ops:
  0.0 4.1 %collective-permute-start.1 = (bf16[512,768]{1,0:T(8,128)(2,1)}, bf16[512,768]{1,0:T(8,128)(2,1)}, u32[]{:S(2)}, u32[]{:S(2)}) collective-permute-start(bf16[512,768]{1,0:T(8,128)(2,1)} %refs_0_.2), channel_id=1, source_target_pairs={{0,66},{2,64},{64,2},{66,0},{1,67},{3,65},{65,3},{67,1},{4,70},{6,... | collective-permute-start | bytes 2359304 | tf_op jit(solution)/shard_map/ppermute | solution.py:26
  8.0 6.6 %project.4.refs_4_ = f32[3,512,512]{2,1,0:T(8,128)S(1)} custom-call(s32[7]{0:T(128)S(1)} %stack.39.s, bf16[512,768]{1,0:T(8,128)(2,1)S(1)} %copy-done.6, bf16[512,768]{1,0:T(8,128)(2,1)S(1)} %copy-done.9, bf16[3,3072,1024]{2,1,0:T(8,128)(2,1)} %bitcast.32, bf16[3,3072,1024]{2,1,0:T(8,128)(2,1)} %bitcast.33), custom_call_target="tpu_custom_call" | custom-call | flops 1 | bytes 1 | tf_op jit(solution)/shard_map/project/pallas_call | solution.py:34
  14.6 8.0 %collective-permute-done.1.refs_0_.refs_2_ = bf16[512,768]{1,0:T(8,128)(2,1)} collective-permute-done((bf16[512,768]{1,0:T(8,128)(2,1)}, bf16[512,768]{1,0:T(8,128)(2,1)}, u32[]{:S(2)}, u32[]{:S(2)}) %collective-permute-start.1) | collective-permute-done | bytes 786464 | tf_op jit(solution)/shard_map/ppermute | solution.py:26
  22.7 1.5 collective-permute-done.refs_0_.refs_2_
  26.0 1.8 slice.21
  27.8 1.8 slice.22
  29.6 1.5 collective-permute-start.7
  32.5 3.2 %collective-permute-start.4 = (f32[8,512]{1,0:T(8,128)}, f32[8,512]{1,0:T(8,128)}, u32[]{:S(2)}, u32[]{:S(2)}) collective-permute-start(f32[8,512]{1,0:T(8,128)} %concatenate.9), channel_id=1, source_target_pairs={{0,64},{64,0},{1,65},{65,1},{2,66},{66,2},{3,67},{67,3},{4,68},{68... | collective-permute-start | bytes 49160 | tf_op jit(solution)/shard_map/ppermute | solution.py:22
  35.7 2.1 %constant_dynamic-slice_fusion.1 = (bf16[512,512]{1,0:T(8,128)(2,1)S(1)}, bf16[512,512]{1,0:T(8,128)(2,1)}) fusion(bf16[512,1024]{1,0:T(8,128)(2,1)} %param.9, s32[]{:T(128)S(6)} %select_n.14, s32[]{:T(128)S(6)} %select_n.13), kind=kLoop, calls=%fused_computation.9 | loop fusion | bytes 2097160 | tf_op jit(solution)/shard_map/dynamic_slice | solution.py:555
  37.7 7.1 %project.5.qkv_ref = bf16[3,512,512]{2,1,0:T(8,128)(2,1)S(1)} custom-call(s32[7]{0:T(128)S(1)} %stack.39.s, bf16[512,768]{1,0:T(8,128)(2,1)} %collective-permute-done.refs_0_.refs_2_, bf16[512,768]{1,0:T(8,128)(2,1)} %collective-permute-done.5.refs_1_.refs_3_, bf16[3,3072,1024]{2,1,0:T(8,128)(2,1)} %bitcast.34, bf16[3,3072,1024]{2,1,0:T(8,128)(2,1)} %bitcast.35, ...), custom_call_target="tpu_custom_call" | custom-call | flops 1 | bytes 1 | tf_op jit(solution)/shard_map/project/pallas_call | solution.py:34
  44.9 7.1 %project.6.refs_4_ = f32[3,512,512]{2,1,0:T(8,128)S(1)} custom-call(s32[7]{0:T(128)S(1)} %stack.39.s, bf16[512,768]{1,0:T(8,128)(2,1)} %collective-permute-done.1.refs_0_.refs_2_, bf16[512,768]{1,0:T(8,128)(2,1)} %collective-permute-done.3.refs_1_.refs_3_, bf16[3,3072,1024]{2,1,0:T(8,128)(2,1)} %bitcast.36, bf16[3,3072,1024]{2,1,0:T(8,128)(2,1)} %bitcast.37), custom_call_target="tpu_custom_call" | custom-call | flops 1 | bytes 1 | tf_op jit(solution)/shard_map/project/pallas_call | solution.py:34
  52.0 2.1 %constant_dynamic-update-slice_fusion.1 = bf16[512,768]{1,0:T(8,128)(2,1)} fusion(bf16[256,768]{1,0:T(8,128)(2,1)} %collective-permute-done.6), kind=kLoop, calls=%fused_computation.5 | loop fusion | bytes 786432
  56.1 2.3 %shard_states.2 = (bf16[528,128]{1,0:T(8,128)(2,1)S(1)}, bf16[528,128]{1,0:T(8,128)(2,1)S(1)}, bf16[528,128]{1,0:T(8,128)(2,1)S(1)}, bf16[528,128]{1,0:T(8,128)(2,1)S(1)}) custom-call(s32[7]{0:T(128)S(1)} %stack.39.s, bf16[3,512,512]{2,1,0:T(8,128)(2,1)S(1)} %project.5.qkv_ref, bf16[512,512]{1,0:T(8,128)(2,1)S(1)} %get-tuple-element.247.og_ref, ...), custom_call_target="tpu_custom_call" | custom-call | flops 1 | bytes 1 | tf_op jit(solution)/shard_map/shard_states/pallas_call | solution.py:34
  59.7 3.4 %turn.2 = bf16[16,2,96,512]{3,2,1,0:T(8,128)(2,1)S(1)} custom-call(s32[7]{0:T(128)S(1)} %stack.39.s, bf16[512,768]{1,0:T(8,128)(2,1)S(1)} %copy-done.7, bf16[512,768]{1,0:T(8,128)(2,1)S(1)} %copy-done.10, bf16[512,768]{1,0:T(8,128)(2,1)} %collective-permute-done.refs_0_.refs_2_, bf16[512,768]{1,0:T(8,128)(2,1)} %collective-permute-done.5.refs_1_.refs_3_), custom_call_target="tpu_custom_call" | custom-call | flops 1 | bytes 1 | tf_op jit(solution)/shard_map/turn/pallas_call | solution.py:34
  65.1 1.9 copy-done.3
  67.0 7.1 %project.7.qkv_ref = bf16[3,512,512]{2,1,0:T(8,128)(2,1)S(1)} custom-call(s32[7]{0:T(128)S(1)} %stack.41.s, bf16[512,768]{1,0:T(8,128)(2,1)} %constant_dynamic-update-slice_fusion.refs_0_, bf16[512,768]{1,0:T(8,128)(2,1)} %collective-permute-done.8.refs_1_, bf16[3,3072,1024]{2,1,0:T(8,128)(2,1)} %bitcast.38, bf16[3,3072,1024]{2,1,0:T(8,128)(2,1)} %bitcast.39, ...), custom_call_target="tpu_custom_call" | custom-call | flops 1 | bytes 1 | tf_op jit(solution)/shard_map/project/pallas_call | solution.py:34
  74.1 3.6 %shard_states.3 = (bf16[528,128]{1,0:T(8,128)(2,1)S(1)}, bf16[528,128]{1,0:T(8,128)(2,1)S(1)}, bf16[528,128]{1,0:T(8,128)(2,1)S(1)}, bf16[528,128]{1,0:T(8,128)(2,1)S(1)}) custom-call(s32[7]{0:T(128)S(1)} %stack.39.s, bf16[3,512,512]{2,1,0:T(8,128)(2,1)S(1)} %project.7.qkv_ref, bf16[512,512]{1,0:T(8,128)(2,1)} %collective-permute-done.9.og_ref, ...), custom_call_target="tpu_custom_call" | custom-call | flops 1 | bytes 1 | tf_op jit(solution)/shard_map/shard_states/pallas_call | solution.py:34
  77.8 1.7 collective-permute-start.10
  79.4 2.2 %collective-permute-start.11 = (bf16[528,128]{1,0:T(8,128)(2,1)S(1)}, bf16[528,128]{1,0:T(8,128)(2,1)S(1)}, u32[]{:S(2)}, u32[]{:S(2)}) collective-permute-start(bf16[528,128]{1,0:T(8,128)(2,1)S(1)} %get-tuple-element.153), channel_id=1, source_target_pairs={{0,12},{4,8},{8,4},{12,0},{1,13},{5,9},{9,5},{13,1},{2,14},{6,10},... | collective-permute-start | bytes 405512 | tf_op jit(solution)/shard_map/ppermute | solution.py:22
  82.3 6.3 %local_grads.3 = (f32[3,512,512]{2,1,0:T(8,128)S(1)}, bf16[3,512,512]{2,1,0:T(8,128)(2,1)S(1)}) custom-call(s32[7]{0:T(128)S(1)} %stack.39.s, bf16[3,512,512]{2,1,0:T(8,128)(2,1)S(1)} %copy-done.1, bf16[512,512]{1,0:T(8,128)(2,1)S(1)} %copy-done.5, f32[8,512]{1,0:T(8,128)S(1)} %pad_maximum_fusion.cum_ref), custom_call_target="tpu_custom_call" | custom-call | flops 1 | bytes 1 | tf_op jit(solution)/shard_map/local_grads/pallas_call | solution.py:34
  89.6 3.1 %collective-permute-start.15 = (bf16[528,128]{1,0:T(8,128)(2,1)S(1)}, bf16[528,128]{1,0:T(8,128)(2,1)S(1)}, u32[]{:S(2)}, u32[]{:S(2)}) collective-permute-start(bf16[528,128]{1,0:T(8,128)(2,1)S(1)} %get-tuple-element.161.a), channel_id=1, source_target_pairs={{0,32},{16,48},{32,0},{48,16},{1,33},{17,49},{33,1},{49,17},{2,34}... | collective-permute-start | bytes 405512 | tf_op jit(solution)/shard_map/ppermute | solution.py:22
  93.8 4.2 %local_grads.4 = (f32[3,512,512]{2,1,0:T(8,128)S(1)}, bf16[3,512,512]{2,1,0:T(8,128)(2,1)S(1)}) custom-call(s32[7]{0:T(128)S(1)} %stack.41.s, bf16[3,512,512]{2,1,0:T(8,128)(2,1)S(1)} %project.7.qkv_ref, bf16[512,512]{1,0:T(8,128)(2,1)} %collective-permute-done.9.og_ref, f32[8,512]{1,0:T(8,128)S(1)} %pad_maximum_fusion.cum_ref), custom_call_target="tpu_custom_call" | custom-call | flops 1 | bytes 1 | tf_op jit(solution)/shard_map/local_grads/pallas_call | solution.py:34
  101.1 2.2 %collective-permute-start.17 = (bf16[512,128]{1,0:T(8,128)(2,1)S(1)}, bf16[512,128]{1,0:T(8,128)(2,1)S(1)}, u32[]{:S(2)}, u32[]{:S(2)}) collective-permute-start(bf16[512,128]{1,0:T(8,128)(2,1)S(1)} %get-tuple-element.173), channel_id=1, source_target_pairs={{0,12},{4,8},{8,4},{12,0},{1,13},{5,9},{9,5},{13,1},{2,14},{6,10},... | collective-permute-start | bytes 393224 | tf_op jit(solution)/shard_map/ppermute | solution.py:22
  104.1 3.9 %turn.3 = bf16[16,2,96,512]{3,2,1,0:T(8,128)(2,1)S(1)} custom-call(s32[7]{0:T(128)S(1)} %stack.39.s, bf16[512,768]{1,0:T(8,128)(2,1)} %constant_dynamic-update-slice_fusion.refs_0_, bf16[512,768]{1,0:T(8,128)(2,1)} %collective-permute-done.8.refs_1_, bf16[512,768]{1,0:T(8,128)(2,1)} %collective-permute-done.1.refs_0_.refs_2_, ...), custom_call_target="tpu_custom_call" | custom-call | flops 1 | bytes 1 | tf_op jit(solution)/shard_map/turn/pallas_call | solution.py:34
  108.1 4.2 %local_grads.5 = (f32[3,512,512]{2,1,0:T(8,128)S(1)}, bf16[3,512,512]{2,1,0:T(8,128)(2,1)S(1)}) custom-call(s32[7]{0:T(128)S(1)} %stack.41.s, bf16[3,512,512]{2,1,0:T(8,128)(2,1)S(1)} %project.7.qkv_ref, bf16[512,512]{1,0:T(8,128)(2,1)} %collective-permute-done.9.og_ref, ...), custom_call_target="tpu_custom_call", output_to_operand_aliasing={{0}: (4, {}), {1}: (5, {})} | custom-call | flops 1 | bytes 1 | tf_op jit(solution)/shard_map/local_grads/pallas_call | solution.py:34
  112.3 2.7 %whole_grads.2 = (bf16[512,768]{1,0:T(8,128)(2,1)S(1)}, bf16[512,768]{1,0:T(8,128)(2,1)S(1)}) custom-call(s32[7]{0:T(128)S(1)} %stack.39.s, f32[3,512,512]{2,1,0:T(8,128)S(1)} %get-tuple-element.189.local_ref, bf16[3,512,512]{2,1,0:T(8,128)(2,1)S(1)} %get-tuple-element.190.ready_ref, bf16[512,128]{1,0:T(8,128)(2,1)S(1)} %get-tuple-element.176.a, ...), custom_call_target="tpu_custom_call" | custom-call | flops 1 | bytes 1 | tf_op jit(solution)/shard_map/whole_grads/pallas_call | solution.py:34
  115.0 2.7 %whole_grads.3 = (bf16[512,768]{1,0:T(8,128)(2,1)S(1)}, bf16[512,768]{1,0:T(8,128)(2,1)S(1)}) custom-call(s32[7]{0:T(128)S(1)} %stack.39.s, f32[3,512,512]{2,1,0:T(8,128)S(1)} %get-tuple-element.195.local_ref, bf16[3,512,512]{2,1,0:T(8,128)(2,1)S(1)} %get-tuple-element.196.ready_ref, bf16[512,128]{1,0:T(8,128)(2,1)S(1)} %get-tuple-element.176.a, ...), custom_call_target="tpu_custom_call" | custom-call | flops 1 | bytes 1 | tf_op jit(solution)/shard_map/whole_grads/pallas_call | solution.py:34
  117.7 3.2 %weight_part.3 = (bf16[384,768]{1,0:T(8,128)(2,1)S(1)}, bf16[384,768]{1,0:T(8,128)(2,1)S(1)}, bf16[384,768]{1,0:T(8,128)(2,1)S(1)}, bf16[384,768]{1,0:T(8,128)(2,1)S(1)}) custom-call(s32[7]{0:T(128)S(1)} %stack.39.s, bf16[4,4,192,512]{3,2,1,0:T(8,128)(2,1)S(1)} %bitcast.20, bf16[4,4,192,512]{3,2,1,0:T(8,128)(2,1)S(1)} %bitcast.21, ...), custom_call_target="tpu_custom_call" | custom-call | flops 1 | bytes 1 | tf_op jit(solution)/shard_map/weight_part/pallas_call | solution.py:34
  120.8 2.6 %collective-permute-start.20 = (bf16[384,768]{1,0:T(8,128)(2,1)S(1)}, bf16[384,768]{1,0:T(8,128)(2,1)S(1)}, u32[]{:S(2)}, u32[]{:S(2)}) collective-permute-start(bf16[384,768]{1,0:T(8,128)(2,1)S(1)} %get-tuple-element.204), channel_id=1, source_target_pairs={{0,48},{16,32},{32,16},{48,0},{1,49},{17,33},{33,17},{49,1},{2,50}... | collective-permute-start | bytes 1769480 | tf_op jit(solution)/shard_map/ppermute | solution.py:22
  124.3 2.2 %collective-permute-start.24 = (bf16[384,768]{1,0:T(8,128)(2,1)S(1)}, bf16[384,768]{1,0:T(8,128)(2,1)S(1)}, u32[]{:S(2)}, u32[]{:S(2)}) collective-permute-start(bf16[384,768]{1,0:T(8,128)(2,1)S(1)} %get-tuple-element.214), channel_id=1, source_target_pairs={{0,12},{4,8},{8,4},{12,0},{1,13},{5,9},{9,5},{13,1},{2,14},{6,10},... | collective-permute-start | bytes 1769480 | tf_op jit(solution)/shard_map/ppermute | solution.py:22
  126.5 8.4 %weight_part.4 = (bf16[768,768]{1,0:T(8,128)(2,1)S(1)}, bf16[768,768]{1,0:T(8,128)(2,1)S(1)}, bf16[768,768]{1,0:T(8,128)(2,1)S(1)}, bf16[768,768]{1,0:T(8,128)(2,1)S(1)}) custom-call(s32[7]{0:T(128)S(1)} %stack.39.s, bf16[4,4,192,512]{3,2,1,0:T(8,128)(2,1)S(1)} %bitcast.22, bf16[4,4,192,512]{3,2,1,0:T(8,128)(2,1)S(1)} %bitcast.23, ...), custom_call_target="tpu_custom_call" | custom-call | flops 1 | bytes 1 | tf_op jit(solution)/shard_map/weight_part/pallas_call | solution.py:34
  138.4 1.6 collective-permute-start.22
  140.0 1.5 add_halves.5
  141.5 2.3 %collective-permute-start.30 = (bf16[768,768]{1,0:T(8,128)(2,1)S(1)}, bf16[768,768]{1,0:T(8,128)(2,1)S(1)}, u32[]{:S(2)}, u32[]{:S(2)}) collective-permute-start(bf16[768,768]{1,0:T(8,128)(2,1)S(1)} %get-tuple-element.233), channel_id=1, source_target_pairs={{0,12},{4,8},{8,4},{12,0},{1,13},{5,9},{9,5},{13,1},{2,14},{6,10},... | collective-permute-start | bytes 3538952 | tf_op jit(solution)/shard_map/ppermute | solution.py:22
  144.0 3.2 %weight_part.5 = (bf16[768,768]{1,0:T(8,128)(2,1)S(1)}, bf16[768,768]{1,0:T(8,128)(2,1)S(1)}) custom-call(s32[7]{0:T(128)S(1)} %stack.39.s, bf16[4,4,192,512]{3,2,1,0:T(8,128)(2,1)S(1)} %bitcast.24, bf16[4,4,192,512]{3,2,1,0:T(8,128)(2,1)S(1)} %bitcast.25, bf16[4,4,192,512]{3,2,1,0:T(8,128)(2,1)S(1)} %bitcast.30, bf16[4,4,192,512]{3,2,1,0:T(8,128)(2,1)S(1)} %bitcast.31, ...), custom_call_target="tpu_custom_call" | custom-call | flops 1 | bytes 1 | tf_op jit(solution)/shard_map/weight_part/pallas_call | solution.py:34
  147.1 17.9 %collective-permute-done.22.c = bf16[768,768]{1,0:T(8,128)(2,1)S(1)} collective-permute-done((bf16[768,768]{1,0:T(8,128)(2,1)S(1)}, bf16[768,768]{1,0:T(8,128)(2,1)S(1)}, u32[]{:S(2)}, u32[]{:S(2)}) %collective-permute-start.22) | collective-permute-done | bytes 1179680 | tf_op jit(solution)/shard_map/ppermute | solution.py:22
  167.1 2.2 %collective-permute-start.26 = (bf16[96,768]{1,0:T(8,128)(2,1)S(1)}, bf16[96,768]{1,0:T(8,128)(2,1)S(1)}, u32[]{:S(2)}, u32[]{:S(2)}) collective-permute-start(bf16[96,768]{1,0:T(8,128)(2,1)S(1)} %get-tuple-element.229), channel_id=1, source_target_pairs={{0,12},{4,8},{8,4},{12,0},{1,13},{5,9},{9,5},{13,1},{2,14},{6,10},... | collective-permute-start | bytes 442376 | tf_op jit(solution)/shard_map/ppermute | solution.py:22
  171.3 1.8 collective-permute-start.31
  173.1 1.5 collective-permute-start.32
  175.3 1.9 collective-permute-done.31.u
  177.3 3.8 %collective-permute-done.32.d = bf16[96,768]{1,0:T(8,128)(2,1)S(1)} collective-permute-done((bf16[96,768]{1,0:T(8,128)(2,1)S(1)}, bf16[96,768]{1,0:T(8,128)(2,1)S(1)}, u32[]{:S(2)}, u32[]{:S(2)}) %collective-permute-start.32) | collective-permute-done | bytes 147488 | tf_op jit(solution)/shard_map/ppermute | solution.py:22
  181.9 1.5 collective-permute-start.34
  183.4 1.5 collective-permute-start.28
  184.9 3.7 %collective-permute-done.33.refs_4_ = bf16[192,768]{1,0:T(8,128)(2,1)S(1)} collective-permute-done((bf16[192,768]{1,0:T(8,128)(2,1)S(1)}, bf16[192,768]{1,0:T(8,128)(2,1)S(1)}, u32[]{:S(2)}, u32[]{:S(2)}) %collective-permute-start.33) | collective-permute-done | bytes 294944 | tf_op jit(solution)/shard_map/ppermute | solution.py:22
  189.9 1.5 collective-permute-done.28.refs_2_
  192.4 3.5 %collective-permute-start.35 = (bf16[2,96,768]{2,1,0:T(8,128)(2,1)S(1)}, bf16[2,96,768]{2,1,0:T(8,128)(2,1)S(1)}, u32[]{:S(2)}, u32[]{:S(2)}) collective-permute-start(bf16[2,96,768]{2,1,0:T(8,128)(2,1)S(1)} %get-tuple-element.246), channel_id=1, source_target_pairs={{0,64},{64,0},{1,65},{65,1},{2,66},{66,2},{3,67},{67,3},{4,68},{68... | collective-permute-start | bytes 884744 | tf_op jit(solution)/shard_map/ppermute | solution.py:22
  195.9 4.8 %collective-permute-done.35.there_ref = bf16[2,96,768]{2,1,0:T(8,128)(2,1)S(1)} collective-permute-done((bf16[2,96,768]{2,1,0:T(8,128)(2,1)S(1)}, bf16[2,96,768]{2,1,0:T(8,128)(2,1)S(1)}, u32[]{:S(2)}, u32[]{:S(2)}) %collective-permute-start.35) | collective-permute-done | bytes 294944 | tf_op jit(solution)/shard_map/ppermute | solution.py:22
  200.7 1.6 finish.1
  (103 shorter events, 30.4 us)
Async XLA Ops:
  0.0 4.9 %collective-permute-start.2 = (bf16[512,768]{1,0:T(8,128)(2,1)}, bf16[512,768]{1,0:T(8,128)(2,1)S(1)}, u32[]{:S(2)}, u32[]{:S(2)}) collective-permute-start(bf16[512,768]{1,0:T(8,128)(2,1)} %refs_0_.2), channel_id=1, source_target_pairs={{0,1},{1,0},{2,3},{3,2},{4,5},{5,4},{6,7},{7,6},{8,9},{9,8},{10,11... | collective-permute-start | bytes 2359304 | tf_op jit(solution)/shard_map/ppermute | solution.py:22
  0.0 22.6 %collective-permute-start.1 = (bf16[512,768]{1,0:T(8,128)(2,1)}, bf16[512,768]{1,0:T(8,128)(2,1)}, u32[]{:S(2)}, u32[]{:S(2)}) collective-permute-start(bf16[512,768]{1,0:T(8,128)(2,1)} %refs_0_.2), channel_id=1, source_target_pairs={{0,66},{2,64},{64,2},{66,0},{1,67},{3,65},{65,3},{67,1},{4,70},{6,... | collective-permute-start | bytes 2359304 | tf_op jit(solution)/shard_map/ppermute | solution.py:26
  4.1 20.0 %collective-permute-start = (bf16[512,768]{1,0:T(8,128)(2,1)}, bf16[512,768]{1,0:T(8,128)(2,1)}, u32[]{:S(2)}, u32[]{:S(2)}) collective-permute-start(bf16[512,768]{1,0:T(8,128)(2,1)} %refs_0_.2), channel_id=1, source_target_pairs={{0,2},{2,0},{1,3},{3,1},{4,6},{6,4},{5,7},{7,5},{8,10},{10,8},{9,1... | collective-permute-start | bytes 2359304 | tf_op jit(solution)/shard_map/ppermute | solution.py:22
  8.0 16.6 %copy-start.16 = (f32[512,8]{0,1:T(8,128)S(1)}, f32[512,8]{0,1:T(8,128)}, u32[]{:S(2)}) copy-start(f32[512,8]{0,1:T(8,128)} %param.7) | copy-start | bytes 49156
  24.1 20.8 %collective-permute-start.3 = (bf16[512,768]{1,0:T(8,128)(2,1)}, bf16[512,768]{1,0:T(8,128)(2,1)}, u32[]{:S(2)}, u32[]{:S(2)}) collective-permute-start(bf16[512,768]{1,0:T(8,128)(2,1)} %collective-permute-done.1.refs_0_.refs_2_), channel_id=1, source_target_pairs={{0,1},{1,0},{2,3},{3,2},{4,5},{5,4},{6,7},{7,6},{8,9},{9,8},{10,11... | collective-permute-start | bytes 2359304 | tf_op jit(solution)/shard_map/ppermute | solution.py:22
  24.1 13.6 %collective-permute-start.5 = (bf16[512,768]{1,0:T(8,128)(2,1)}, bf16[512,768]{1,0:T(8,128)(2,1)}, u32[]{:S(2)}, u32[]{:S(2)}) collective-permute-start(bf16[512,768]{1,0:T(8,128)(2,1)} %collective-permute-done.refs_0_.refs_2_), channel_id=1, source_target_pairs={{0,1},{1,0},{2,3},{3,2},{4,5},{5,4},{6,7},{7,6},{8,9},{9,8},{10,11... | collective-permute-start | bytes 2359304 | tf_op jit(solution)/shard_map/ppermute | solution.py:22
  25.8 2.0 copy-start.15
  29.6 22.4 %collective-permute-start.7 = (bf16[256,768]{1,0:T(8,128)(2,1)}, bf16[256,768]{1,0:T(8,128)(2,1)S(1)}, u32[]{:S(2)}, u32[]{:S(2)}) collective-permute-start(bf16[256,768]{1,0:T(8,128)(2,1)} %slice.22), channel_id=1, source_target_pairs={{0,66},{2,64},{64,2},{66,0},{1,67},{3,65},{65,3},{67,1},{4,70},{6,... | collective-permute-start | bytes 1179656 | tf_op jit(solution)/shard_map/ppermute | solution.py:26
  31.1 20.9 %collective-permute-start.6 = (bf16[256,768]{1,0:T(8,128)(2,1)}, bf16[256,768]{1,0:T(8,128)(2,1)}, u32[]{:S(2)}, u32[]{:S(2)}) collective-permute-start(bf16[256,768]{1,0:T(8,128)(2,1)} %slice.21), channel_id=1, source_target_pairs={{0,2},{2,0},{1,3},{3,1},{4,6},{6,4},{5,7},{7,5},{8,10},{10,8},{9,1... | collective-permute-start | bytes 1179656 | tf_op jit(solution)/shard_map/ppermute | solution.py:22
  32.5 12.4 %collective-permute-start.4 = (f32[8,512]{1,0:T(8,128)}, f32[8,512]{1,0:T(8,128)}, u32[]{:S(2)}, u32[]{:S(2)}) collective-permute-start(f32[8,512]{1,0:T(8,128)} %concatenate.9), channel_id=1, source_target_pairs={{0,64},{64,0},{1,65},{65,1},{2,66},{66,2},{3,67},{67,3},{4,68},{68... | collective-permute-start | bytes 49160 | tf_op jit(solution)/shard_map/ppermute | solution.py:22
  37.7 18.3 %copy-start.4 = (bf16[512,512]{1,0:T(8,128)(2,1)}, bf16[512,512]{1,0:T(8,128)(2,1)S(1)}, u32[]{:S(2)}) copy-start(bf16[512,512]{1,0:T(8,128)(2,1)S(1)} %get-tuple-element.247.og_ref) | copy-start | bytes 1572868
  44.9 11.2 %copy-start = (bf16[3,512,512]{2,1,0:T(8,128)(2,1)}, bf16[3,512,512]{2,1,0:T(8,128)(2,1)S(1)}, u32[]{:S(2)}) copy-start(bf16[3,512,512]{2,1,0:T(8,128)(2,1)S(1)} %project.5.qkv_ref) | copy-start | bytes 4718596
  52.0 6.4 %copy-start.2 = (f32[3,512,512]{2,1,0:T(8,128)}, f32[3,512,512]{2,1,0:T(8,128)S(1)}, u32[]{:S(2)}) copy-start(f32[3,512,512]{2,1,0:T(8,128)S(1)} %project.6.refs_4_) | copy-start | bytes 9437188
  54.9 4.8 %copy-start.7 = (bf16[512,768]{1,0:T(8,128)(2,1)S(1)}, bf16[512,768]{1,0:T(8,128)(2,1)}, u32[]{:S(2)}) copy-start(bf16[512,768]{1,0:T(8,128)(2,1)} %refs_0_.2) | copy-start | bytes 2359300
  54.9 4.8 %copy-start.10 = (bf16[512,768]{1,0:T(8,128)(2,1)S(1)}, bf16[512,768]{1,0:T(8,128)(2,1)}, u32[]{:S(2)}) copy-start(bf16[512,768]{1,0:T(8,128)(2,1)} %copy-done.8) | copy-start | bytes 2359300
  54.9 10.2 %collective-permute-start.8 = (bf16[512,768]{1,0:T(8,128)(2,1)}, bf16[512,768]{1,0:T(8,128)(2,1)}, u32[]{:S(2)}, u32[]{:S(2)}) collective-permute-start(bf16[512,768]{1,0:T(8,128)(2,1)} %constant_dynamic-update-slice_fusion.refs_0_), channel_id=1, source_target_pairs={{0,1},{1,0},{2,3},{3,2},{4,5},{5,4},{6,7},{7,6},{8,9},{9,8},{10,11... | collective-permute-start | bytes 2359304 | tf_op jit(solution)/shard_map/ppermute | solution.py:22
  54.9 19.2 %collective-permute-start.9 = (bf16[512,512]{1,0:T(8,128)(2,1)}, bf16[512,512]{1,0:T(8,128)(2,1)}, u32[]{:S(2)}, u32[]{:S(2)}) collective-permute-start(bf16[512,512]{1,0:T(8,128)(2,1)} %get-tuple-element.146), channel_id=1, source_target_pairs={{0,64},{64,0},{1,65},{65,1},{2,66},{66,2},{3,67},{67,3},{4,68},{68... | collective-permute-start | bytes 1572872 | tf_op jit(solution)/shard_map/ppermute | solution.py:22
  65.1 1.9 copy-start.3
  67.0 7.1 %copy-start.12 = (bf16[528,128]{1,0:T(8,128)(2,1)S(1)}, bf16[528,128]{1,0:T(8,128)(2,1)}, u32[]{:S(2)}) copy-start(bf16[528,128]{1,0:T(8,128)(2,1)} %copy-done.11) | copy-start | bytes 405508
  67.0 7.2 %copy-start.14 = (bf16[528,128]{1,0:T(8,128)(2,1)S(1)}, bf16[528,128]{1,0:T(8,128)(2,1)}, u32[]{:S(2)}) copy-start(bf16[528,128]{1,0:T(8,128)(2,1)} %copy-done.13) | copy-start | bytes 405508
  74.1 8.2 %copy-start.1 = (bf16[3,512,512]{2,1,0:T(8,128)(2,1)S(1)}, bf16[3,512,512]{2,1,0:T(8,128)(2,1)}, u32[]{:S(2)}) copy-start(bf16[3,512,512]{2,1,0:T(8,128)(2,1)} %copy-done) | copy-start | bytes 4718596
  74.1 8.2 %copy-start.5 = (bf16[512,512]{1,0:T(8,128)(2,1)S(1)}, bf16[512,512]{1,0:T(8,128)(2,1)}, u32[]{:S(2)}) copy-start(bf16[512,512]{1,0:T(8,128)(2,1)} %copy-done.4) | copy-start | bytes 1572868
  77.8 10.8 %collective-permute-start.10 = (bf16[528,128]{1,0:T(8,128)(2,1)S(1)}, bf16[528,128]{1,0:T(8,128)(2,1)S(1)}, u32[]{:S(2)}, u32[]{:S(2)}) collective-permute-start(bf16[528,128]{1,0:T(8,128)(2,1)S(1)} %get-tuple-element.152), channel_id=1, source_target_pairs={{0,4},{4,0},{8,12},{12,8},{1,5},{5,1},{9,13},{13,9},{2,6},{6,2},{1... | collective-permute-start | bytes 405512 | tf_op jit(solution)/shard_map/ppermute | solution.py:22
  79.4 9.2 %collective-permute-start.11 = (bf16[528,128]{1,0:T(8,128)(2,1)S(1)}, bf16[528,128]{1,0:T(8,128)(2,1)S(1)}, u32[]{:S(2)}, u32[]{:S(2)}) collective-permute-start(bf16[528,128]{1,0:T(8,128)(2,1)S(1)} %get-tuple-element.153), channel_id=1, source_target_pairs={{0,12},{4,8},{8,4},{12,0},{1,13},{5,9},{9,5},{13,1},{2,14},{6,10},... | collective-permute-start | bytes 405512 | tf_op jit(solution)/shard_map/ppermute | solution.py:22
  81.6 7.2 %collective-permute-start.12 = (bf16[528,128]{1,0:T(8,128)(2,1)S(1)}, bf16[528,128]{1,0:T(8,128)(2,1)S(1)}, u32[]{:S(2)}, u32[]{:S(2)}) collective-permute-start(bf16[528,128]{1,0:T(8,128)(2,1)S(1)} %get-tuple-element.154), channel_id=1, source_target_pairs={{0,8},{4,12},{8,0},{12,4},{1,9},{5,13},{9,1},{13,5},{2,10},{6,14},... | collective-permute-start | bytes 405512 | tf_op jit(solution)/shard_map/ppermute | solution.py:22
  89.6 8.4 %collective-permute-start.15 = (bf16[528,128]{1,0:T(8,128)(2,1)S(1)}, bf16[528,128]{1,0:T(8,128)(2,1)S(1)}, u32[]{:S(2)}, u32[]{:S(2)}) collective-permute-start(bf16[528,128]{1,0:T(8,128)(2,1)S(1)} %get-tuple-element.161.a), channel_id=1, source_target_pairs={{0,32},{16,48},{32,0},{48,16},{1,33},{17,49},{33,1},{49,17},{2,34}... | collective-permute-start | bytes 405512 | tf_op jit(solution)/shard_map/ppermute | solution.py:22
  92.7 6.4 %collective-permute-start.14 = (bf16[528,128]{1,0:T(8,128)(2,1)S(1)}, bf16[528,128]{1,0:T(8,128)(2,1)S(1)}, u32[]{:S(2)}, u32[]{:S(2)}) collective-permute-start(bf16[528,128]{1,0:T(8,128)(2,1)S(1)} %get-tuple-element.161.a), channel_id=1, source_target_pairs={{0,48},{16,32},{32,16},{48,0},{1,49},{17,33},{33,17},{49,1},{2,50}... | collective-permute-start | bytes 405512 | tf_op jit(solution)/shard_map/ppermute | solution.py:22
  93.8 5.3 %collective-permute-start.13 = (bf16[528,128]{1,0:T(8,128)(2,1)S(1)}, bf16[528,128]{1,0:T(8,128)(2,1)S(1)}, u32[]{:S(2)}, u32[]{:S(2)}) collective-permute-start(bf16[528,128]{1,0:T(8,128)(2,1)S(1)} %get-tuple-element.161.a), channel_id=1, source_target_pairs={{0,16},{16,0},{32,48},{48,32},{1,17},{17,1},{33,49},{49,33},{2,18}... | collective-permute-start | bytes 405512 | tf_op jit(solution)/shard_map/ppermute | solution.py:22
  100.0 12.3 %collective-permute-start.16 = (bf16[512,128]{1,0:T(8,128)(2,1)S(1)}, bf16[512,128]{1,0:T(8,128)(2,1)S(1)}, u32[]{:S(2)}, u32[]{:S(2)}) collective-permute-start(bf16[512,128]{1,0:T(8,128)(2,1)S(1)} %get-tuple-element.172), channel_id=1, source_target_pairs={{0,4},{4,0},{8,12},{12,8},{1,5},{5,1},{9,13},{13,9},{2,6},{6,2},{1... | collective-permute-start | bytes 393224 | tf_op jit(solution)/shard_map/ppermute | solution.py:22
  101.1 11.2 %collective-permute-start.17 = (bf16[512,128]{1,0:T(8,128)(2,1)S(1)}, bf16[512,128]{1,0:T(8,128)(2,1)S(1)}, u32[]{:S(2)}, u32[]{:S(2)}) collective-permute-start(bf16[512,128]{1,0:T(8,128)(2,1)S(1)} %get-tuple-element.173), channel_id=1, source_target_pairs={{0,12},{4,8},{8,4},{12,0},{1,13},{5,9},{9,5},{13,1},{2,14},{6,10},... | collective-permute-start | bytes 393224 | tf_op jit(solution)/shard_map/ppermute | solution.py:22
  103.2 9.1 %collective-permute-start.18 = (bf16[512,128]{1,0:T(8,128)(2,1)S(1)}, bf16[512,128]{1,0:T(8,128)(2,1)S(1)}, u32[]{:S(2)}, u32[]{:S(2)}) collective-permute-start(bf16[512,128]{1,0:T(8,128)(2,1)S(1)} %get-tuple-element.174), channel_id=1, source_target_pairs={{0,8},{4,12},{8,0},{12,4},{1,9},{5,13},{9,1},{13,5},{2,10},{6,14},... | collective-permute-start | bytes 393224 | tf_op jit(solution)/shard_map/ppermute | solution.py:22
  120.8 14.7 %collective-permute-start.20 = (bf16[384,768]{1,0:T(8,128)(2,1)S(1)}, bf16[384,768]{1,0:T(8,128)(2,1)S(1)}, u32[]{:S(2)}, u32[]{:S(2)}) collective-permute-start(bf16[384,768]{1,0:T(8,128)(2,1)S(1)} %get-tuple-element.204), channel_id=1, source_target_pairs={{0,48},{16,32},{32,16},{48,0},{1,49},{17,33},{33,17},{49,1},{2,50}... | collective-permute-start | bytes 1769480 | tf_op jit(solution)/shard_map/ppermute | solution.py:22
  123.4 13.6 %collective-permute-start.19 = (bf16[384,768]{1,0:T(8,128)(2,1)S(1)}, bf16[384,768]{1,0:T(8,128)(2,1)S(1)}, u32[]{:S(2)}, u32[]{:S(2)}) collective-permute-start(bf16[384,768]{1,0:T(8,128)(2,1)S(1)} %get-tuple-element.200), channel_id=1, source_target_pairs={{0,16},{16,0},{32,48},{48,32},{1,17},{17,1},{33,49},{49,33},{2,18}... | collective-permute-start | bytes 1769480 | tf_op jit(solution)/shard_map/ppermute | solution.py:22
  123.4 16.6 %collective-permute-start.23 = (bf16[384,768]{1,0:T(8,128)(2,1)S(1)}, bf16[384,768]{1,0:T(8,128)(2,1)S(1)}, u32[]{:S(2)}, u32[]{:S(2)}) collective-permute-start(bf16[384,768]{1,0:T(8,128)(2,1)S(1)} %get-tuple-element.213), channel_id=1, source_target_pairs={{0,4},{4,0},{8,12},{12,8},{1,5},{5,1},{9,13},{13,9},{2,6},{6,2},{1... | collective-permute-start | bytes 1769480 | tf_op jit(solution)/shard_map/ppermute | solution.py:22
  124.3 15.7 %collective-permute-start.24 = (bf16[384,768]{1,0:T(8,128)(2,1)S(1)}, bf16[384,768]{1,0:T(8,128)(2,1)S(1)}, u32[]{:S(2)}, u32[]{:S(2)}) collective-permute-start(bf16[384,768]{1,0:T(8,128)(2,1)S(1)} %get-tuple-element.214), channel_id=1, source_target_pairs={{0,12},{4,8},{8,4},{12,0},{1,13},{5,9},{9,5},{13,1},{2,14},{6,10},... | collective-permute-start | bytes 1769480 | tf_op jit(solution)/shard_map/ppermute | solution.py:22
  138.4 26.6 %collective-permute-start.22 = (bf16[768,768]{1,0:T(8,128)(2,1)S(1)}, bf16[768,768]{1,0:T(8,128)(2,1)S(1)}, u32[]{:S(2)}, u32[]{:S(2)}) collective-permute-start(bf16[768,768]{1,0:T(8,128)(2,1)S(1)} %get-tuple-element.210), channel_id=1, source_target_pairs={{0,48},{16,32},{32,16},{48,0},{1,49},{17,33},{33,17},{49,1},{2,50}... | collective-permute-start | bytes 3538952 | tf_op jit(solution)/shard_map/ppermute | solution.py:22
  140.0 25.3 %collective-permute-start.21 = (bf16[768,768]{1,0:T(8,128)(2,1)S(1)}, bf16[768,768]{1,0:T(8,128)(2,1)S(1)}, u32[]{:S(2)}, u32[]{:S(2)}) collective-permute-start(bf16[768,768]{1,0:T(8,128)(2,1)S(1)} %get-tuple-element.209), channel_id=1, source_target_pairs={{0,16},{16,0},{32,48},{48,32},{1,17},{17,1},{33,49},{49,33},{2,18}... | collective-permute-start | bytes 3538952 | tf_op jit(solution)/shard_map/ppermute | solution.py:22
  141.5 27.8 %collective-permute-start.30 = (bf16[768,768]{1,0:T(8,128)(2,1)S(1)}, bf16[768,768]{1,0:T(8,128)(2,1)S(1)}, u32[]{:S(2)}, u32[]{:S(2)}) collective-permute-start(bf16[768,768]{1,0:T(8,128)(2,1)S(1)} %get-tuple-element.233), channel_id=1, source_target_pairs={{0,12},{4,8},{8,4},{12,0},{1,13},{5,9},{9,5},{13,1},{2,14},{6,10},... | collective-permute-start | bytes 3538952 | tf_op jit(solution)/shard_map/ppermute | solution.py:22
  143.8 26.5 %collective-permute-start.29 = (bf16[768,768]{1,0:T(8,128)(2,1)S(1)}, bf16[768,768]{1,0:T(8,128)(2,1)S(1)}, u32[]{:S(2)}, u32[]{:S(2)}) collective-permute-start(bf16[768,768]{1,0:T(8,128)(2,1)S(1)} %get-tuple-element.217), channel_id=1, source_target_pairs={{0,4},{4,0},{8,12},{12,8},{1,5},{5,1},{9,13},{13,9},{2,6},{6,2},{1... | collective-permute-start | bytes 3538952 | tf_op jit(solution)/shard_map/ppermute | solution.py:22
  166.3 8.3 %collective-permute-start.25 = (bf16[96,768]{1,0:T(8,128)(2,1)S(1)}, bf16[96,768]{1,0:T(8,128)(2,1)S(1)}, u32[]{:S(2)}, u32[]{:S(2)}) collective-permute-start(bf16[96,768]{1,0:T(8,128)(2,1)S(1)} %get-tuple-element.228), channel_id=1, source_target_pairs={{0,4},{4,0},{8,12},{12,8},{1,5},{5,1},{9,13},{13,9},{2,6},{6,2},{1... | collective-permute-start | bytes 442376 | tf_op jit(solution)/shard_map/ppermute | solution.py:22
  167.1 7.5 %collective-permute-start.26 = (bf16[96,768]{1,0:T(8,128)(2,1)S(1)}, bf16[96,768]{1,0:T(8,128)(2,1)S(1)}, u32[]{:S(2)}, u32[]{:S(2)}) collective-permute-start(bf16[96,768]{1,0:T(8,128)(2,1)S(1)} %get-tuple-element.229), channel_id=1, source_target_pairs={{0,12},{4,8},{8,4},{12,0},{1,13},{5,9},{9,5},{13,1},{2,14},{6,10},... | collective-permute-start | bytes 442376 | tf_op jit(solution)/shard_map/ppermute | solution.py:22
  171.3 6.0 %collective-permute-start.31 = (bf16[96,768]{1,0:T(8,128)(2,1)S(1)}, bf16[96,768]{1,0:T(8,128)(2,1)S(1)}, u32[]{:S(2)}, u32[]{:S(2)}) collective-permute-start(bf16[96,768]{1,0:T(8,128)(2,1)S(1)} %get-tuple-element.239), channel_id=1, source_target_pairs={{0,16},{16,0},{32,48},{48,32},{1,17},{17,1},{33,49},{49,33},{2,18}... | collective-permute-start | bytes 442376 | tf_op jit(solution)/shard_map/ppermute | solution.py:22
  173.1 7.9 %collective-permute-start.32 = (bf16[96,768]{1,0:T(8,128)(2,1)S(1)}, bf16[96,768]{1,0:T(8,128)(2,1)S(1)}, u32[]{:S(2)}, u32[]{:S(2)}) collective-permute-start(bf16[96,768]{1,0:T(8,128)(2,1)S(1)} %get-tuple-element.240), channel_id=1, source_target_pairs={{0,48},{16,32},{32,16},{48,0},{1,49},{17,33},{33,17},{49,1},{2,50}... | collective-permute-start | bytes 442376 | tf_op jit(solution)/shard_map/ppermute | solution.py:22
  181.8 6.8 %collective-permute-start.33 = (bf16[192,768]{1,0:T(8,128)(2,1)S(1)}, bf16[192,768]{1,0:T(8,128)(2,1)S(1)}, u32[]{:S(2)}, u32[]{:S(2)}) collective-permute-start(bf16[192,768]{1,0:T(8,128)(2,1)S(1)} %get-tuple-element.243), channel_id=1, source_target_pairs={{0,16},{16,0},{32,48},{48,32},{1,17},{17,1},{33,49},{49,33},{2,18}... | collective-permute-start | bytes 884744 | tf_op jit(solution)/shard_map/ppermute | solution.py:22
  181.9 8.0 %collective-permute-start.34 = (bf16[192,768]{1,0:T(8,128)(2,1)S(1)}, bf16[192,768]{1,0:T(8,128)(2,1)S(1)}, u32[]{:S(2)}, u32[]{:S(2)}) collective-permute-start(bf16[192,768]{1,0:T(8,128)(2,1)S(1)} %get-tuple-element.244), channel_id=1, source_target_pairs={{0,48},{16,32},{32,16},{48,0},{1,49},{17,33},{33,17},{49,1},{2,50}... | collective-permute-start | bytes 884744 | tf_op jit(solution)/shard_map/ppermute | solution.py:22
  183.4 7.9 %collective-permute-start.28 = (bf16[192,768]{1,0:T(8,128)(2,1)S(1)}, bf16[192,768]{1,0:T(8,128)(2,1)S(1)}, u32[]{:S(2)}, u32[]{:S(2)}) collective-permute-start(bf16[192,768]{1,0:T(8,128)(2,1)S(1)} %get-tuple-element.231), channel_id=1, source_target_pairs={{0,12},{4,8},{8,4},{12,0},{1,13},{5,9},{9,5},{13,1},{2,14},{6,10},... | collective-permute-start | bytes 884744 | tf_op jit(solution)/shard_map/ppermute | solution.py:22
  184.9 6.7 %collective-permute-start.27 = (bf16[192,768]{1,0:T(8,128)(2,1)S(1)}, bf16[192,768]{1,0:T(8,128)(2,1)S(1)}, u32[]{:S(2)}, u32[]{:S(2)}) collective-permute-start(bf16[192,768]{1,0:T(8,128)(2,1)S(1)} %get-tuple-element.230), channel_id=1, source_target_pairs={{0,4},{4,0},{8,12},{12,8},{1,5},{5,1},{9,13},{13,9},{2,6},{6,2},{1... | collective-permute-start | bytes 884744 | tf_op jit(solution)/shard_map/ppermute | solution.py:22
  192.4 8.3 %collective-permute-start.35 = (bf16[2,96,768]{2,1,0:T(8,128)(2,1)S(1)}, bf16[2,96,768]{2,1,0:T(8,128)(2,1)S(1)}, u32[]{:S(2)}, u32[]{:S(2)}) collective-permute-start(bf16[2,96,768]{2,1,0:T(8,128)(2,1)S(1)} %get-tuple-element.246), channel_id=1, source_target_pairs={{0,64},{64,0},{1,65},{65,1},{2,66},{66,2},{3,67},{67,3},{4,68},{68... | collective-permute-start | bytes 884744 | tf_op jit(solution)/shard_map/ppermute | solution.py:22
  (5 other events, 4.5 us)

commit v3 on v2

--- a/solution.py
+++ b/solution.py
@@ -54,38 +54,43 @@
     return jax.ShapeDtypeStruct(dims, kind)
 
 
+def joined(refs):
+    parts = [ref[...] for ref in refs]
+    return parts[0] if len(parts) == 1 else jnp.concatenate(parts, axis=0)
+
+
 def project(table, shards, flips, weight, partial, last):
-    n = len(shards)
-    tokens, width = shards[0].shape
+    n, counts = len(shards), [len(x) for x in shards]
+    flat = [part for x in shards for part in x]
+    tokens, width = sum(part.shape[0] for part in shards[0]), flat[0].shape[1]
     cols = weight.shape[2] // 2
 
     def body(s, *refs):
-        out = refs[-1]
-        acc = dot(refs[0][...], refs[n][0])
-        for i in range(1, n):
-            acc += dot(refs[i][...], refs[n + i][0])
+        out, rest = refs[-1], list(refs)
+        acc = None
+        for i, count in enumerate(counts):
+            rows = joined([rest.pop(0) for _ in range(count)])
+            term = dot(rows, refs[len(flat) + i][0])
+            acc = term if acc is None else acc + term
         if partial is not None:
-            acc += refs[2 * n][0]
+            acc += refs[len(flat) + n][0]
         if last:
             row = lax.broadcasted_iota(jnp.int32, acc.shape, 0)
             acc = jnp.where(row < s[LEN], acc, 0.0)
         out[0] = acc.astype(out.dtype)
 
-    block = cols // 2
-    tile = pl.BlockSpec((1, tokens, block), lambda g, j, s: (g, 0, j))
-    in_specs = [whole(x) for x in shards]
+    tile = pl.BlockSpec((1, tokens, cols), lambda g, s: (g, 0, 0))
+    in_specs = [whole(x) for x in flat]
     for flip in flips:
         in_specs.append(
-            pl.BlockSpec(
-                (1, width, block), lambda g, j, s, flip=flip: (g, s[TEN] ^ flip, 2 * s[Z] + j)
-            )
+            pl.BlockSpec((1, width, cols), lambda g, s, flip=flip: (g, s[TEN] ^ flip, s[Z]))
         )
-    operands = [*shards, *([weight] * n)]
+    operands = [*flat, *([weight] * n)]
     if partial is not None:
         in_specs.append(tile)
         operands.append(partial)
     out = shape((3, tokens, cols), BF16 if last else F32)
-    return call("project", body, table, (3, 2), operands, in_specs, out, tile, 20)
+    return call("project", body, table, (3,), operands, in_specs, out, tile, 24)
 
 
 def shard_states(table, qkv, out_grad, cumul, which, so_far):
@@ -276,15 +281,19 @@
         parts = [slice(0, size), slice(size, tokens)]
 
         def pair(t, s):
-            gap = row[:, parts[t]] - wide[parts[s], :]
             if t == s:
-                gap = jnp.where(s_at <= t_at, gap, -jnp.inf)
-            decay = jnp.exp(gap)
+                gap = row[:, parts[t]] - wide[parts[s], :]
+                decay = jnp.exp(jnp.where(s_at <= t_at, gap, -jnp.inf))
+            else:
+                middle = row[:, size - 1 : size]
+                to_middle = jnp.exp(middle - column[parts[s], :])
+                decay = jnp.concatenate([to_middle] * (size // HEAD), axis=1)
+                decay *= jnp.exp(row[:, parts[t]] - middle)
             q, k, v = qkv_ref[0, parts[t], :], qkv_ref[1, parts[s], :], qkv_ref[2, parts[s], :]
             g = og_ref[parts[t], :]
             scores = lax.dot_general(k, q, AB_T, preferred_element_type=F32)
             grads = lax.dot_general(v, g, AB_T, preferred_element_type=F32)
-            prob = (scores * scale * decay).astype(BF16)
+            prob = (scores * decay).astype(BF16)
             score = (grads * decay).astype(BF16)
             dq = lax.dot_general(score, k, A_TB, preferred_element_type=F32)
             return dq, dot(score, q), dot(prob, g)
@@ -294,7 +303,7 @@
         grads = (
             jnp.concatenate([a[0], b[0] + c[0]], axis=0) * scale,
             jnp.concatenate([a[1] + b[1], c[1]], axis=0) * scale,
-            jnp.concatenate([a[2] + b[2], c[2]], axis=0),
+            jnp.concatenate([a[2] + b[2], c[2]], axis=0) * scale,
         )
         until = jnp.exp(row[:, tokens - 1 : tokens] - column)
         rows = (
@@ -371,20 +380,23 @@
 
 
 def turn(table, shards):
-    tokens, width = shards[0].shape
+    counts = [len(x) for x in shards]
+    flat = [part for x in shards for part in x]
+    tokens, width = sum(part.shape[0] for part in shards[0]), flat[0].shape[1]
     rows = 4 * width // 32
 
     def body(s, *refs):
-        out = refs[-1]
-        for k in range(4):
+        out, at = refs[-1], 0
+        for k, count in enumerate(counts):
+            mine, at = refs[at : at + count], at + count
 
             @pl.when((pl.program_id(0) ^ s[TEN]) == k)
-            def _(k=k):
-                out[...] = refs[k][...].T.reshape(out.shape)
+            def _(mine=mine):
+                out[...] = joined(mine).T.reshape(out.shape)
 
     out = shape((16, 2, rows, tokens))
     spec = pl.BlockSpec((8, 1, rows, tokens), lambda i, s: (i % 2, (i // 2) ^ s[Z], 0, 0))
-    turned = call("turn", body, table, (4,), shards, [whole(x) for x in shards], out, spec, 12)
+    turned = call("turn", body, table, (4,), flat, [whole(x) for x in flat], out, spec, 12)
     return turned.reshape(4, 4, 2 * rows, tokens)
 
 
@@ -424,7 +436,7 @@
         [by_x, by_y, by_x, by_y, *[whole(x) for x in (*lefts, *rights)]],
         outs,
         [whole(o) for o in outs],
-        40,
+        30,
     )
 
 
@@ -456,19 +468,13 @@
 def cut_blocks(table, axis, own, first, second):
     rows, cols = own.shape[0] // 4, own.shape[1]
 
-    def body(s, a, b, c, far_up, far_down, one, three, here):
-        def block(r):
+    def body(s, a, b, c, *outs):
+        for r, out in zip((1, 3, 2, 0), outs):
             at = pl.ds(pl.multiple_of((s[axis] ^ r) * rows, rows), rows)
-            return (a[at, :].astype(F32) + b[at, :].astype(F32) + c[at, :].astype(F32)).astype(BF16)
-
-        far = block(2)
-        far_up[...] = far[: rows // 2]
-        far_down[...] = far[rows // 2 :]
-        one[...] = block(1)
-        three[...] = block(3)
-        here[...] = block(0)
-
-    outs = [shape((rows // 2, cols))] * 2 + [shape((rows, cols))] * 3
+            total = a[at, :].astype(F32) + b[at, :].astype(F32) + c[at, :].astype(F32)
+            out[...] = total.astype(BF16)
+
+    outs = [shape((rows, cols))] * 4
     operands = (own, first, second)
     return call(
         "cut_blocks",
@@ -489,8 +495,7 @@
     def body(s, *refs):
         here, there = refs[-2:]
         for k in range(2):
-            a, b, c = refs[3 * k : 3 * k + 3]
-            total = (a[...].astype(F32) + b[...].astype(F32) + c[...].astype(F32)).astype(BF16)
+            total = sum(ref[...].astype(F32) for ref in refs[4 * k : 4 * k + 4]).astype(BF16)
             here[k] = total[: rows // 2]
             there[k] = total[rows // 2 :]
 
@@ -505,7 +510,7 @@
         [whole(x) for x in operands],
         outs,
         [whole(o) for o in outs],
-        8,
+        12,
     )
 
 
@@ -555,26 +560,25 @@
     og_own = lax.dynamic_slice_in_dim(out_grad, here_z * width, width, axis=1)
     og_other = lax.dynamic_slice_in_dim(out_grad, (1 - here_z) * width, width, axis=1)
 
-    acc_own = project(table, [activations, core], (0, 1), weight, None, False)
-    near, side, acc_own = tied((near, side, acc_own))
+    acc_own = project(table, [[activations], [core]], (0, 1), weight, None, False)
+    near, side, acc_own, note, og_other = tied((near, side, acc_own, note, og_other))
     half = tokens // 2
+    far = [send(side[:half], "zl", 1), across(near[half:])]
     near_core = send(near, "co", 1)
     side_core = send(side, "co", 1)
-    far = [send(side[:half], "zl", 1), across(near[half:])]
-    qkv_own = project(table, [near, near_core], (2, 3), weight, acc_own, True)
-    side_core, note, og_other, qkv_own = tied((side_core, note, og_other, qkv_own))
-    acc_pair = project(table, [side, side_core], (2, 3), weight, None, False)
     cumul = jnp.concatenate([lax.dynamic_slice_in_dim(cumul, here_z * per, per), note[:per]])
     table_pair = jnp.stack([*fixed, note[per, 0].astype(jnp.int32)]).astype(jnp.int32)
-    *far, acc_pair = tied((*far, acc_pair))
-    far = jnp.concatenate(far)
-    far_core = send(far, "co", 1)
+    acc_pair = project(table, [[side]], (2,), weight, None, False)
+    near_core, acc_pair = tied((near_core, acc_pair))
+    qkv_own = project(table, [[near], [near_core]], (2, 3), weight, acc_own, True)
+    far, side_core, qkv_own, table_pair, cumul = tied((far, side_core, qkv_own, table_pair, cumul))
+    far_core = [send(x, "co", 1) for x in far]
     og_pair = send(tied((og_other, far))[0], "c0", 1)
-    first, _ = tied(([activations, core, near, near_core], far))
-    turned = [turn(table, first)]
     to_y = shard_states(table, qkv_own, og_own, cumul, 0, None)
-    far_core, acc_pair, to_y, turned = tied((far_core, acc_pair, to_y, turned))
-    qkv_pair = project(table_pair, [far, far_core], (0, 1), weight, acc_pair, True)
+    far_core, to_y = tied((far_core, to_y))
+    qkv_pair = project(table_pair, [[side_core], far, far_core], (3, 0, 1), weight, acc_pair, True)
+    turned = [turn(table, tied(([[activations], [core], [near], [near_core]], qkv_pair))[0])]
+    og_pair, qkv_pair, turned = tied((og_pair, qkv_pair, turned))
 
     to_y = shard_states(table, qkv_pair, og_pair, cumul, 1, to_y)
     at_y = [send(to_y[r], "c2", r) for r in (1, 3, 2)]
@@ -590,7 +594,7 @@
     states = [send(back[r], "c2", r) for r in (1, 3, 2)]
     local, _ = tied((local, back[0]))
     local = local_grads(table_pair, qkv_pair, og_pair, cumul, 1, per // 2, per // 2, local)
-    second, _ = tied(([far, far_core, side, side_core], back[0]))
+    second, _ = tied(([far, far_core, [side], [side_core]], back[0]))
     turned.append(turn(table, second))
     states, turned, local = tied((states, turned, local))
     states = [back[0], states[0], states[2], states[1]]
@@ -614,14 +618,9 @@
     l_cut = cut_blocks(table, Y, own[0], *l_got)
     r_got, _ = tied((r_got, l_cut))
     r_cut = cut_blocks(table, X, own[1], *r_got)
-    l_half = [send(x, "c2", by) for x, by in zip(l_cut[:2], (1, 3))]
-    r_half = [send(x, "c1", by) for x, by in zip(r_cut[:2], (1, 3))]
-    l_three, l_one = add_halves(table, l_cut[3], l_cut[2], l_half)
-    l_got = [send(l_one, "c2", 1), send(l_three, "c2", 3)]
-    r_half, _ = tied((r_half, l_one))
-    r_three, r_one = add_halves(table, r_cut[3], r_cut[2], r_half)
-    r_got = [send(r_one, "c1", 1), send(r_three, "c1", 3)]
-    here, there = final_sums(table, ((l_cut[4], *l_got), (r_cut[4], *r_got)))
+    l_got = [send(x, "c2", by) for x, by in zip(l_cut, (1, 3, 2))]
+    r_got = [send(x, "c1", by) for x, by in zip(r_cut, (1, 3, 2))]
+    here, there = final_sums(table, ((l_cut[3], *l_got), (r_cut[3], *r_got)))
     there = send(there, "c0", 1)
     return jnp.transpose(finish(table, here, there), (1, 0, 2))
 

time: 203 us -> 182 us (0.90)
  Pallas kernels: 86.1 us -> 76 us
  local copies, waits for them, and re-layouts: 17.9 us -> 9.21 us
    pallas_call x26 -> x24, Pallas kernels: 86.1 us -> 76 us  [call(): pl.pallas_call(body, grid_spec=pltpu.PrefetchScalarGridSpec(num_scalar_pr...]
    ppermute x2, waiting for transfers between devices: 8.04 us -> 0.01 us  [across(): return lax.ppermute(x, ('c0', 'zl'), [(0, 3), (1, 2), (2, 1), (3, 0)])]
    unnamed x35 -> x20, local copies, waits for them, and re-layouts: 8.45 us -> 1.92 us
    ppermute x34 -> x33, waiting for transfers between devices: 41.3 us -> 47.3 us  [send(): lax.ppermute(x, axis, [(i, i ^ by) for i in range(lax.axis_size(axis))])]
    ppermute x34 -> x33, starting transfers between devices: 39.7 us -> 36.8 us  [send(): lax.ppermute(x, axis, [(i, i ^ by) for i in range(lax.axis_size(axis))])]
  transfers between devices with their start and end apart: 36 -> 35, of which waited for: 17 -> 15; matrix products, arithmetic and copies ran while one was open for 5% -> 6% of each run, Pallas kernels for 34% -> 33%
where the time goes in v3:
time: 182 us; the launch traced here: 181 us
  Pallas kernels  76 us (42%)
  waiting for transfers between devices  47.3 us (26%)
  starting transfers between devices  43.8 us (24%)
  local copies, waits for them, and re-layouts  9.21 us (5%)
  other arithmetic  2.74 us (2%)
    pallas_call x24, Pallas kernels, call(): pl.pallas_call(body, grid_spec=pltpu.PrefetchScalarGridSpec(num_scalar_pr...  76 us
    ppermute x33, waiting for transfers between devices, send(): lax.ppermute(x, axis, [(i, i ^ by) for i in range(lax.axis_size(axis))])  47.3 us
    ppermute x33, starting transfers between devices, send(): lax.ppermute(x, axis, [(i, i ^ by) for i in range(lax.axis_size(axis))])  36.8 us
    ppermute x2, starting transfers between devices, across(): return lax.ppermute(x, ('c0', 'zl'), [(0, 3), (1, 2), (2, 1), (3, 0)])  6.95 us
  transfers between devices with their start and end apart: 35, of which 15 were waited for; matrix products, arithmetic and copies ran while one was open for 6% of the time, Pallas kernels for 33%

profile of v3, /device:TPU:0, one launch (start us, length us, event | category | flops | bytes accessed | tf_op | source)
XLA Modules:
  0.0 180.6 jit_solution(12848668248311484277)
XLA Ops:
  0.0 4.1 %collective-permute-start.1 = (bf16[512,768]{1,0:T(8,128)(2,1)}, bf16[512,768]{1,0:T(8,128)(2,1)}, u32[]{:S(2)}, u32[]{:S(2)}) collective-permute-start(bf16[512,768]{1,0:T(8,128)(2,1)} %refs_0_.2), channel_id=1, source_target_pairs={{0,66},{2,64},{64,2},{66,0},{1,67},{3,65},{65,3},{67,1},{4,70},{6,... | collective-permute-start | bytes 2359304 | tf_op jit(solution)/shard_map/ppermute | solution.py:26
  7.6 1.5 collective-permute-start.3
  9.2 2.2 %constant_dynamic-slice_fusion = (bf16[512,512]{1,0:T(8,128)(2,1)}, bf16[512,512]{1,0:T(8,128)(2,1)}) fusion(bf16[512,1024]{1,0:T(8,128)(2,1)} %param.9, s32[]{:T(128)S(6)} %select_n.15, s32[]{:T(128)S(6)} %select_n.13), kind=kLoop, calls=%fused_computation.6 | loop fusion | bytes 2097160 | tf_op jit(solution)/shard_map/dynamic_slice | solution.py:560
  11.5 5.3 %project.4.refs_4_ = f32[3,512,512]{2,1,0:T(8,128)S(1)} custom-call(s32[7]{0:T(128)S(1)} %stack.39.s, bf16[512,768]{1,0:T(8,128)(2,1)S(1)} %copy-done.3, bf16[512,768]{1,0:T(8,128)(2,1)S(1)} %collective-permute-done.2.refs_1_, bf16[3,3072,1024]{2,1,0:T(8,128)(2,1)} %bitcast.32, bf16[3,3072,1024]{2,1,0:T(8,128)(2,1)} %bitcast.33), custom_call_target="tpu_custom_call" | custom-call | flops 1 | bytes 1 | tf_op jit(solution)/shard_map/project/pallas_call | solution.py:34
  16.8 7.3 %collective-permute-done.3 = f32[8,512]{1,0:T(8,128)S(1)} collective-permute-done((f32[8,512]{1,0:T(8,128)S(1)}, f32[8,512]{1,0:T(8,128)S(1)}, u32[]{:S(2)}, u32[]{:S(2)}) %collective-permute-start.3) | collective-permute-done | bytes 16416 | tf_op jit(solution)/shard_map/ppermute | solution.py:22
  24.8 1.8 slice.20
  26.6 1.8 slice.21
  28.4 2.8 %collective-permute-start.5 = (bf16[256,768]{1,0:T(8,128)(2,1)}, bf16[256,768]{1,0:T(8,128)(2,1)S(1)}, u32[]{:S(2)}, u32[]{:S(2)}) collective-permute-start(bf16[256,768]{1,0:T(8,128)(2,1)} %slice.21), channel_id=1, source_target_pairs={{0,66},{2,64},{64,2},{66,0},{1,67},{3,65},{65,3},{67,1},{4,70},{6,... | collective-permute-start | bytes 1179656 | tf_op jit(solution)/shard_map/ppermute | solution.py:26
  31.2 4.2 %project.5.refs_8_ = f32[3,512,512]{2,1,0:T(8,128)S(1)} custom-call(s32[7]{0:T(128)S(1)} %stack.39.s, bf16[512,768]{1,0:T(8,128)(2,1)} %collective-permute-done.1.refs_0_.refs_4_, bf16[3,3072,1024]{2,1,0:T(8,128)(2,1)} %bitcast.34), custom_call_target="tpu_custom_call" | custom-call | flops 1 | bytes 1 | tf_op jit(solution)/shard_map/project/pallas_call | solution.py:34
  37.4 1.9 %copy-done.1 = f32[3,512,512]{2,1,0:T(8,128)S(1)} copy-done((f32[3,512,512]{2,1,0:T(8,128)S(1)}, f32[3,512,512]{2,1,0:T(8,128)}, u32[]{:S(2)}) %copy-start.1) | copy-done | bytes 3145752
  39.3 5.8 %project.6.qkv_ref = bf16[3,512,512]{2,1,0:T(8,128)(2,1)S(1)} custom-call(s32[7]{0:T(128)S(1)} %stack.39.s, bf16[512,768]{1,0:T(8,128)(2,1)} %collective-permute-done.refs_0_.refs_2_, bf16[512,768]{1,0:T(8,128)(2,1)} %collective-permute-done.7.refs_1_.refs_3_, bf16[3,3072,1024]{2,1,0:T(8,128)(2,1)} %bitcast.35, bf16[3,3072,1024]{2,1,0:T(8,128)(2,1)} %bitcast.36, ...), custom_call_target="tpu_custom_call" | custom-call | flops 1 | bytes 1 | tf_op jit(solution)/shard_map/project/pallas_call | solution.py:34
  45.1 1.9 %collective-permute-start.8 = (bf16[512,512]{1,0:T(8,128)(2,1)S(1)}, bf16[512,512]{1,0:T(8,128)(2,1)S(1)}, u32[]{:S(2)}, u32[]{:S(2)}) collective-permute-start(bf16[512,512]{1,0:T(8,128)(2,1)S(1)} %copy-done.7), channel_id=1, source_target_pairs={{0,64},{64,0},{1,65},{65,1},{2,66},{66,2},{3,67},{67,3},{4,68},{68... | collective-permute-start | bytes 1572872 | tf_op jit(solution)/shard_map/ppermute | solution.py:22
  47.6 2.3 %shard_states.2 = (bf16[528,128]{1,0:T(8,128)(2,1)S(1)}, bf16[528,128]{1,0:T(8,128)(2,1)S(1)}, bf16[528,128]{1,0:T(8,128)(2,1)S(1)}, bf16[528,128]{1,0:T(8,128)(2,1)S(1)}) custom-call(s32[7]{0:T(128)S(1)} %stack.39.s, bf16[3,512,512]{2,1,0:T(8,128)(2,1)S(1)} %project.6.qkv_ref, bf16[512,512]{1,0:T(8,128)(2,1)S(1)} %copy-done.2, ...), custom_call_target="tpu_custom_call" | custom-call | flops 1 | bytes 1 | tf_op jit(solution)/shard_map/shard_states/pallas_call | solution.py:34
  49.9 7.2 %project.7.qkv_ref = bf16[3,512,512]{2,1,0:T(8,128)(2,1)S(1)} custom-call(s32[7]{0:T(128)S(1)} %stack.41.s, bf16[512,768]{1,0:T(8,128)(2,1)} %collective-permute-done.6.refs_0_.refs_5_, bf16[256,768]{1,0:T(8,128)(2,1)} %collective-permute-done.4.refs_1_.refs_0_, bf16[256,768]{1,0:T(8,128)(2,1)S(1)} %collective-permute-done.5.refs_2_.refs_1_, ...), custom_call_target="tpu_custom_call" | custom-call | flops 1 | bytes 1 | tf_op jit(solution)/shard_map/project/pallas_call | solution.py:34
  57.1 3.4 %turn.2 = bf16[16,2,96,512]{3,2,1,0:T(8,128)(2,1)S(1)} custom-call(s32[7]{0:T(128)S(1)} %stack.39.s, bf16[512,768]{1,0:T(8,128)(2,1)S(1)} %copy-done.4, bf16[512,768]{1,0:T(8,128)(2,1)S(1)} %copy-done.6, bf16[512,768]{1,0:T(8,128)(2,1)} %collective-permute-done.refs_0_.refs_2_, bf16[512,768]{1,0:T(8,128)(2,1)} %collective-permute-done.7.refs_1_.refs_3_), custom_call_target="tpu_custom_call" | custom-call | flops 1 | bytes 1 | tf_op jit(solution)/shard_map/turn/pallas_call | solution.py:34
  60.6 2.3 %shard_states.3 = (bf16[528,128]{1,0:T(8,128)(2,1)S(1)}, bf16[528,128]{1,0:T(8,128)(2,1)S(1)}, bf16[528,128]{1,0:T(8,128)(2,1)S(1)}, bf16[528,128]{1,0:T(8,128)(2,1)S(1)}) custom-call(s32[7]{0:T(128)S(1)} %stack.39.s, bf16[3,512,512]{2,1,0:T(8,128)(2,1)S(1)} %project.7.qkv_ref, bf16[512,512]{1,0:T(8,128)(2,1)S(1)} %collective-permute-done.8.og_ref, ...), custom_call_target="tpu_custom_call" | custom-call | flops 1 | bytes 1 | tf_op jit(solution)/shard_map/shard_states/pallas_call | solution.py:34
  62.9 1.7 collective-permute-start.11
  64.6 2.2 %collective-permute-start.12 = (bf16[528,128]{1,0:T(8,128)(2,1)S(1)}, bf16[528,128]{1,0:T(8,128)(2,1)S(1)}, u32[]{:S(2)}, u32[]{:S(2)}) collective-permute-start(bf16[528,128]{1,0:T(8,128)(2,1)S(1)} %get-tuple-element.157), channel_id=1, source_target_pairs={{0,12},{4,8},{8,4},{12,0},{1,13},{5,9},{9,5},{13,1},{2,14},{6,10},... | collective-permute-start | bytes 405512 | tf_op jit(solution)/shard_map/ppermute | solution.py:22
  67.5 6.1 %local_grads.3 = (f32[3,512,512]{2,1,0:T(8,128)S(1)}, bf16[3,512,512]{2,1,0:T(8,128)(2,1)S(1)}) custom-call(s32[7]{0:T(128)S(1)} %stack.39.s, bf16[3,512,512]{2,1,0:T(8,128)(2,1)S(1)} %project.6.qkv_ref, bf16[512,512]{1,0:T(8,128)(2,1)S(1)} %copy-done.2, f32[8,512]{1,0:T(8,128)S(1)} %pad_maximum_fusion.cum_ref), custom_call_target="tpu_custom_call" | custom-call | flops 1 | bytes 1 | tf_op jit(solution)/shard_map/local_grads/pallas_call | solution.py:34
  74.6 3.1 %collective-permute-start.16 = (bf16[528,128]{1,0:T(8,128)(2,1)S(1)}, bf16[528,128]{1,0:T(8,128)(2,1)S(1)}, u32[]{:S(2)}, u32[]{:S(2)}) collective-permute-start(bf16[528,128]{1,0:T(8,128)(2,1)S(1)} %get-tuple-element.165.a), channel_id=1, source_target_pairs={{0,32},{16,48},{32,0},{48,16},{1,33},{17,49},{33,1},{49,17},{2,34}... | collective-permute-start | bytes 405512 | tf_op jit(solution)/shard_map/ppermute | solution.py:22
  78.8 3.3 %local_grads.4 = (f32[3,512,512]{2,1,0:T(8,128)S(1)}, bf16[3,512,512]{2,1,0:T(8,128)(2,1)S(1)}) custom-call(s32[7]{0:T(128)S(1)} %stack.41.s, bf16[3,512,512]{2,1,0:T(8,128)(2,1)S(1)} %project.7.qkv_ref, bf16[512,512]{1,0:T(8,128)(2,1)S(1)} %collective-permute-done.8.og_ref, f32[8,512]{1,0:T(8,128)S(1)} %pad_maximum_fusion.cum_ref), custom_call_target="tpu_custom_call" | custom-call | flops 1 | bytes 1 | tf_op jit(solution)/shard_map/local_grads/pallas_call | solution.py:34
  82.2 1.9 %collective-permute-done.15.d = bf16[528,128]{1,0:T(8,128)(2,1)S(1)} collective-permute-done((bf16[528,128]{1,0:T(8,128)(2,1)S(1)}, bf16[528,128]{1,0:T(8,128)(2,1)S(1)}, u32[]{:S(2)}, u32[]{:S(2)}) %collective-permute-start.15) | collective-permute-done | bytes 135200 | tf_op jit(solution)/shard_map/ppermute | solution.py:22
  86.2 2.2 %collective-permute-start.18 = (bf16[512,128]{1,0:T(8,128)(2,1)S(1)}, bf16[512,128]{1,0:T(8,128)(2,1)S(1)}, u32[]{:S(2)}, u32[]{:S(2)}) collective-permute-start(bf16[512,128]{1,0:T(8,128)(2,1)S(1)} %get-tuple-element.177), channel_id=1, source_target_pairs={{0,12},{4,8},{8,4},{12,0},{1,13},{5,9},{9,5},{13,1},{2,14},{6,10},... | collective-permute-start | bytes 393224 | tf_op jit(solution)/shard_map/ppermute | solution.py:22
  89.3 3.3 %local_grads.5 = (f32[3,512,512]{2,1,0:T(8,128)S(1)}, bf16[3,512,512]{2,1,0:T(8,128)(2,1)S(1)}) custom-call(s32[7]{0:T(128)S(1)} %stack.41.s, bf16[3,512,512]{2,1,0:T(8,128)(2,1)S(1)} %project.7.qkv_ref, bf16[512,512]{1,0:T(8,128)(2,1)S(1)} %collective-permute-done.8.og_ref, ...), custom_call_target="tpu_custom_call", output_to_operand_aliasing={{0}: (4, {}), {1}: (5, {})} | custom-call | flops 1 | bytes 1 | tf_op jit(solution)/shard_map/local_grads/pallas_call | solution.py:34
  92.7 3.6 %turn.3 = bf16[16,2,96,512]{3,2,1,0:T(8,128)(2,1)S(1)} custom-call(s32[7]{0:T(128)S(1)} %stack.39.s, bf16[256,768]{1,0:T(8,128)(2,1)} %collective-permute-done.4.refs_1_.refs_0_, bf16[256,768]{1,0:T(8,128)(2,1)S(1)} %collective-permute-done.5.refs_2_.refs_1_, bf16[256,768]{1,0:T(8,128)(2,1)S(1)} %collective-permute-done.9.refs_3_.refs_2_, ...), custom_call_target="tpu_custom_call" | custom-call | flops 1 | bytes 1 | tf_op jit(solution)/shard_map/turn/pallas_call | solution.py:34
  96.3 2.7 %whole_grads.2 = (bf16[512,768]{1,0:T(8,128)(2,1)S(1)}, bf16[512,768]{1,0:T(8,128)(2,1)S(1)}) custom-call(s32[7]{0:T(128)S(1)} %stack.39.s, f32[3,512,512]{2,1,0:T(8,128)S(1)} %get-tuple-element.195.local_ref, bf16[3,512,512]{2,1,0:T(8,128)(2,1)S(1)} %get-tuple-element.196.ready_ref, bf16[512,128]{1,0:T(8,128)(2,1)S(1)} %get-tuple-element.180.a, ...), custom_call_target="tpu_custom_call" | custom-call | flops 1 | bytes 1 | tf_op jit(solution)/shard_map/whole_grads/pallas_call | solution.py:34
  99.0 2.7 %whole_grads.3 = (bf16[512,768]{1,0:T(8,128)(2,1)S(1)}, bf16[512,768]{1,0:T(8,128)(2,1)S(1)}) custom-call(s32[7]{0:T(128)S(1)} %stack.39.s, f32[3,512,512]{2,1,0:T(8,128)S(1)} %get-tuple-element.201.local_ref, bf16[3,512,512]{2,1,0:T(8,128)(2,1)S(1)} %get-tuple-element.202.ready_ref, bf16[512,128]{1,0:T(8,128)(2,1)S(1)} %get-tuple-element.180.a, ...), custom_call_target="tpu_custom_call" | custom-call | flops 1 | bytes 1 | tf_op jit(solution)/shard_map/whole_grads/pallas_call | solution.py:34
  101.6 3.2 %weight_part.3 = (bf16[384,768]{1,0:T(8,128)(2,1)S(1)}, bf16[384,768]{1,0:T(8,128)(2,1)S(1)}, bf16[384,768]{1,0:T(8,128)(2,1)S(1)}, bf16[384,768]{1,0:T(8,128)(2,1)S(1)}) custom-call(s32[7]{0:T(128)S(1)} %stack.39.s, bf16[4,4,192,512]{3,2,1,0:T(8,128)(2,1)S(1)} %bitcast.20, bf16[4,4,192,512]{3,2,1,0:T(8,128)(2,1)S(1)} %bitcast.21, ...), custom_call_target="tpu_custom_call" | custom-call | flops 1 | bytes 1 | tf_op jit(solution)/shard_map/weight_part/pallas_call | solution.py:34
  104.8 2.4 %collective-permute-start.21 = (bf16[384,768]{1,0:T(8,128)(2,1)S(1)}, bf16[384,768]{1,0:T(8,128)(2,1)S(1)}, u32[]{:S(2)}, u32[]{:S(2)}) collective-permute-start(bf16[384,768]{1,0:T(8,128)(2,1)S(1)} %get-tuple-element.210), channel_id=1, source_target_pairs={{0,48},{16,32},{32,16},{48,0},{1,49},{17,33},{33,17},{49,1},{2,50}... | collective-permute-start | bytes 1769480 | tf_op jit(solution)/shard_map/ppermute | solution.py:22
  108.2 2.2 %collective-permute-start.25 = (bf16[384,768]{1,0:T(8,128)(2,1)S(1)}, bf16[384,768]{1,0:T(8,128)(2,1)S(1)}, u32[]{:S(2)}, u32[]{:S(2)}) collective-permute-start(bf16[384,768]{1,0:T(8,128)(2,1)S(1)} %get-tuple-element.220), channel_id=1, source_target_pairs={{0,12},{4,8},{8,4},{12,0},{1,13},{5,9},{9,5},{13,1},{2,14},{6,10},... | collective-permute-start | bytes 1769480 | tf_op jit(solution)/shard_map/ppermute | solution.py:22
  110.3 8.4 %weight_part.4 = (bf16[768,768]{1,0:T(8,128)(2,1)S(1)}, bf16[768,768]{1,0:T(8,128)(2,1)S(1)}, bf16[768,768]{1,0:T(8,128)(2,1)S(1)}, bf16[768,768]{1,0:T(8,128)(2,1)S(1)}) custom-call(s32[7]{0:T(128)S(1)} %stack.39.s, bf16[4,4,192,512]{3,2,1,0:T(8,128)(2,1)S(1)} %bitcast.22, bf16[4,4,192,512]{3,2,1,0:T(8,128)(2,1)S(1)} %bitcast.23, ...), custom_call_target="tpu_custom_call" | custom-call | flops 1 | bytes 1 | tf_op jit(solution)/shard_map/weight_part/pallas_call | solution.py:34
  120.6 1.5 add_halves.2
  122.1 1.6 collective-permute-start.23
  123.6 1.5 add_halves.3
  125.1 2.4 %collective-permute-start.30 = (bf16[768,768]{1,0:T(8,128)(2,1)S(1)}, bf16[768,768]{1,0:T(8,128)(2,1)S(1)}, u32[]{:S(2)}, u32[]{:S(2)}) collective-permute-start(bf16[768,768]{1,0:T(8,128)(2,1)S(1)} %get-tuple-element.236), channel_id=1, source_target_pairs={{0,12},{4,8},{8,4},{12,0},{1,13},{5,9},{9,5},{13,1},{2,14},{6,10},... | collective-permute-start | bytes 3538952 | tf_op jit(solution)/shard_map/ppermute | solution.py:22
  127.6 3.2 %weight_part.5 = (bf16[768,768]{1,0:T(8,128)(2,1)S(1)}, bf16[768,768]{1,0:T(8,128)(2,1)S(1)}) custom-call(s32[7]{0:T(128)S(1)} %stack.39.s, bf16[4,4,192,512]{3,2,1,0:T(8,128)(2,1)S(1)} %bitcast.24, bf16[4,4,192,512]{3,2,1,0:T(8,128)(2,1)S(1)} %bitcast.25, bf16[4,4,192,512]{3,2,1,0:T(8,128)(2,1)S(1)} %bitcast.30, bf16[4,4,192,512]{3,2,1,0:T(8,128)(2,1)S(1)} %bitcast.31, ...), custom_call_target="tpu_custom_call" | custom-call | flops 1 | bytes 1 | tf_op jit(solution)/shard_map/weight_part/pallas_call | solution.py:34
  130.8 17.6 %collective-permute-done.23.c = bf16[768,768]{1,0:T(8,128)(2,1)S(1)} collective-permute-done((bf16[768,768]{1,0:T(8,128)(2,1)S(1)}, bf16[768,768]{1,0:T(8,128)(2,1)S(1)}, u32[]{:S(2)}, u32[]{:S(2)}) %collective-permute-start.23) | collective-permute-done | bytes 1179680 | tf_op jit(solution)/shard_map/ppermute | solution.py:22
  149.7 1.8 collective-permute-done.30.c
  153.2 2.2 %collective-permute-start.31 = (bf16[192,768]{1,0:T(8,128)(2,1)S(1)}, bf16[192,768]{1,0:T(8,128)(2,1)S(1)}, u32[]{:S(2)}, u32[]{:S(2)}) collective-permute-start(bf16[192,768]{1,0:T(8,128)(2,1)S(1)} %get-tuple-element.240), channel_id=1, source_target_pairs={{0,16},{16,0},{32,48},{48,32},{1,17},{17,1},{33,49},{49,33},{2,18}... | collective-permute-start | bytes 884744 | tf_op jit(solution)/shard_map/ppermute | solution.py:22
  155.5 1.7 collective-permute-start.32
  157.7 1.2 collective-permute-start.27
  158.9 2.5 %collective-permute-done.31.refs_5_ = bf16[192,768]{1,0:T(8,128)(2,1)S(1)} collective-permute-done((bf16[192,768]{1,0:T(8,128)(2,1)S(1)}, bf16[192,768]{1,0:T(8,128)(2,1)S(1)}, u32[]{:S(2)}, u32[]{:S(2)}) %collective-permute-start.31) | collective-permute-done | bytes 294944 | tf_op jit(solution)/shard_map/ppermute | solution.py:22
  161.3 2.3 %collective-permute-start.28 = (bf16[192,768]{1,0:T(8,128)(2,1)S(1)}, bf16[192,768]{1,0:T(8,128)(2,1)S(1)}, u32[]{:S(2)}, u32[]{:S(2)}) collective-permute-start(bf16[192,768]{1,0:T(8,128)(2,1)S(1)} %get-tuple-element.234), channel_id=1, source_target_pairs={{0,8},{4,12},{8,0},{12,4},{1,9},{5,13},{9,1},{13,5},{2,10},{6,14},... | collective-permute-start | bytes 884744 | tf_op jit(solution)/shard_map/ppermute | solution.py:22
  163.7 3.3 %collective-permute-done.32.refs_6_ = bf16[192,768]{1,0:T(8,128)(2,1)S(1)} collective-permute-done((bf16[192,768]{1,0:T(8,128)(2,1)S(1)}, bf16[192,768]{1,0:T(8,128)(2,1)S(1)}, u32[]{:S(2)}, u32[]{:S(2)}) %collective-permute-start.32) | collective-permute-done | bytes 294944 | tf_op jit(solution)/shard_map/ppermute | solution.py:22
  167.0 2.9 %collective-permute-done.27.refs_2_ = bf16[192,768]{1,0:T(8,128)(2,1)S(1)} collective-permute-done((bf16[192,768]{1,0:T(8,128)(2,1)S(1)}, bf16[192,768]{1,0:T(8,128)(2,1)S(1)}, u32[]{:S(2)}, u32[]{:S(2)}) %collective-permute-start.27) | collective-permute-done | bytes 294944 | tf_op jit(solution)/shard_map/ppermute | solution.py:22
  170.7 1.7 collective-permute-start.34
  172.4 6.6 %collective-permute-done.34.there_ref = bf16[2,96,768]{2,1,0:T(8,128)(2,1)S(1)} collective-permute-done((bf16[2,96,768]{2,1,0:T(8,128)(2,1)S(1)}, bf16[2,96,768]{2,1,0:T(8,128)(2,1)S(1)}, u32[]{:S(2)}, u32[]{:S(2)}) %collective-permute-start.34) | collective-permute-done | bytes 294944 | tf_op jit(solution)/shard_map/ppermute | solution.py:22
  179.0 1.6 finish.1
  (84 shorter events, 18.8 us)
Async XLA Ops:
  0.0 11.5 %collective-permute-start.2 = (bf16[512,768]{1,0:T(8,128)(2,1)}, bf16[512,768]{1,0:T(8,128)(2,1)S(1)}, u32[]{:S(2)}, u32[]{:S(2)}) collective-permute-start(bf16[512,768]{1,0:T(8,128)(2,1)} %refs_0_.2), channel_id=1, source_target_pairs={{0,1},{1,0},{2,3},{3,2},{4,5},{5,4},{6,7},{7,6},{8,9},{9,8},{10,11... | collective-permute-start | bytes 2359304 | tf_op jit(solution)/shard_map/ppermute | solution.py:22
  0.0 24.1 %collective-permute-start.1 = (bf16[512,768]{1,0:T(8,128)(2,1)}, bf16[512,768]{1,0:T(8,128)(2,1)}, u32[]{:S(2)}, u32[]{:S(2)}) collective-permute-start(bf16[512,768]{1,0:T(8,128)(2,1)} %refs_0_.2), channel_id=1, source_target_pairs={{0,66},{2,64},{64,2},{66,0},{1,67},{3,65},{65,3},{67,1},{4,70},{6,... | collective-permute-start | bytes 2359304 | tf_op jit(solution)/shard_map/ppermute | solution.py:26
  4.1 20.2 %collective-permute-start = (bf16[512,768]{1,0:T(8,128)(2,1)}, bf16[512,768]{1,0:T(8,128)(2,1)}, u32[]{:S(2)}, u32[]{:S(2)}) collective-permute-start(bf16[512,768]{1,0:T(8,128)(2,1)} %refs_0_.2), channel_id=1, source_target_pairs={{0,2},{2,0},{1,3},{3,1},{4,6},{6,4},{5,7},{7,5},{8,10},{10,8},{9,1... | collective-permute-start | bytes 2359304 | tf_op jit(solution)/shard_map/ppermute | solution.py:22
  4.8 6.7 %copy-start.3 = (bf16[512,768]{1,0:T(8,128)(2,1)S(1)}, bf16[512,768]{1,0:T(8,128)(2,1)}, u32[]{:S(2)}) copy-start(bf16[512,768]{1,0:T(8,128)(2,1)} %refs_0_.2) | copy-start | bytes 2359300
  7.6 16.5 %collective-permute-start.3 = (f32[8,512]{1,0:T(8,128)S(1)}, f32[8,512]{1,0:T(8,128)S(1)}, u32[]{:S(2)}, u32[]{:S(2)}) collective-permute-start(f32[8,512]{1,0:T(8,128)S(1)} %concatenate.6), channel_id=1, source_target_pairs={{0,64},{64,0},{1,65},{65,1},{2,66},{66,2},{3,67},{67,3},{4,68},{68... | collective-permute-start | bytes 49160 | tf_op jit(solution)/shard_map/ppermute | solution.py:22
  11.5 5.3 %copy-start.5 = (bf16[512,768]{1,0:T(8,128)(2,1)}, bf16[512,768]{1,0:T(8,128)(2,1)S(1)}, u32[]{:S(2)}) copy-start(bf16[512,768]{1,0:T(8,128)(2,1)S(1)} %collective-permute-done.2.refs_1_) | copy-start | bytes 2359300
  16.8 18.7 %copy-start = (f32[3,512,512]{2,1,0:T(8,128)}, f32[3,512,512]{2,1,0:T(8,128)S(1)}, u32[]{:S(2)}) copy-start(f32[3,512,512]{2,1,0:T(8,128)S(1)} %project.4.refs_4_) | copy-start | bytes 9437188
  24.1 7.1 %copy-start.8 = (f32[8,512]{1,0:T(8,128)}, f32[8,512]{1,0:T(8,128)S(1)}, u32[]{:S(2)}) copy-start(f32[8,512]{1,0:T(8,128)S(1)} %collective-permute-done.3) | copy-start | bytes 49156
  24.3 13.1 %collective-permute-start.7 = (bf16[512,768]{1,0:T(8,128)(2,1)}, bf16[512,768]{1,0:T(8,128)(2,1)}, u32[]{:S(2)}, u32[]{:S(2)}) collective-permute-start(bf16[512,768]{1,0:T(8,128)(2,1)} %collective-permute-done.refs_0_.refs_2_), channel_id=1, source_target_pairs={{0,1},{1,0},{2,3},{3,2},{4,5},{5,4},{6,7},{7,6},{8,9},{9,8},{10,11... | collective-permute-start | bytes 2359304 | tf_op jit(solution)/shard_map/ppermute | solution.py:22
  24.3 20.8 %collective-permute-start.6 = (bf16[512,768]{1,0:T(8,128)(2,1)}, bf16[512,768]{1,0:T(8,128)(2,1)}, u32[]{:S(2)}, u32[]{:S(2)}) collective-permute-start(bf16[512,768]{1,0:T(8,128)(2,1)} %collective-permute-done.1.refs_0_.refs_4_), channel_id=1, source_target_pairs={{0,1},{1,0},{2,3},{3,2},{4,5},{5,4},{6,7},{7,6},{8,9},{9,8},{10,11... | collective-permute-start | bytes 2359304 | tf_op jit(solution)/shard_map/ppermute | solution.py:22
  28.4 16.7 %collective-permute-start.5 = (bf16[256,768]{1,0:T(8,128)(2,1)}, bf16[256,768]{1,0:T(8,128)(2,1)S(1)}, u32[]{:S(2)}, u32[]{:S(2)}) collective-permute-start(bf16[256,768]{1,0:T(8,128)(2,1)} %slice.21), channel_id=1, source_target_pairs={{0,66},{2,64},{64,2},{66,0},{1,67},{3,65},{65,3},{67,1},{4,70},{6,... | collective-permute-start | bytes 1179656 | tf_op jit(solution)/shard_map/ppermute | solution.py:26
  31.2 13.8 %collective-permute-start.4 = (bf16[256,768]{1,0:T(8,128)(2,1)}, bf16[256,768]{1,0:T(8,128)(2,1)}, u32[]{:S(2)}, u32[]{:S(2)}) collective-permute-start(bf16[256,768]{1,0:T(8,128)(2,1)} %slice.20), channel_id=1, source_target_pairs={{0,2},{2,0},{1,3},{3,1},{4,6},{6,4},{5,7},{7,5},{8,10},{10,8},{9,1... | collective-permute-start | bytes 1179656 | tf_op jit(solution)/shard_map/ppermute | solution.py:22
  31.2 4.3 %copy-start.9 = (f32[8,512]{1,0:T(8,128)S(1)}, f32[8,512]{1,0:T(8,128)}, u32[]{:S(2)}) copy-start(f32[8,512]{1,0:T(8,128)} %copy-done.8) | copy-start | bytes 49156
  31.2 5.4 %slice-start = ((f32[8,512]{1,0:T(8,128)}), f32[4,512]{1,0:T(4,128)S(1)}, s32[]{:S(2)}) async-start(f32[8,512]{1,0:T(8,128)} %copy-done.8), calls=%async_computation | async-start | bytes 16384 | tf_op jit(solution)/shard_map/slice | solution.py:569
  37.4 1.9 %copy-start.1 = (f32[3,512,512]{2,1,0:T(8,128)S(1)}, f32[3,512,512]{2,1,0:T(8,128)}, u32[]{:S(2)}) copy-start(f32[3,512,512]{2,1,0:T(8,128)} %copy-done) | copy-start | bytes 9437188
  39.3 5.8 %copy-start.7 = (bf16[512,512]{1,0:T(8,128)(2,1)S(1)}, bf16[512,512]{1,0:T(8,128)(2,1)}, u32[]{:S(2)}) copy-start(bf16[512,512]{1,0:T(8,128)(2,1)} %get-tuple-element.133) | copy-start | bytes 1572868
  39.3 8.3 %copy-start.2 = (bf16[512,512]{1,0:T(8,128)(2,1)S(1)}, bf16[512,512]{1,0:T(8,128)(2,1)}, u32[]{:S(2)}) copy-start(bf16[512,512]{1,0:T(8,128)(2,1)} %get-tuple-element.245.og_ref) | copy-start | bytes 1572868
  45.1 15.5 %collective-permute-start.8 = (bf16[512,512]{1,0:T(8,128)(2,1)S(1)}, bf16[512,512]{1,0:T(8,128)(2,1)S(1)}, u32[]{:S(2)}, u32[]{:S(2)}) collective-permute-start(bf16[512,512]{1,0:T(8,128)(2,1)S(1)} %copy-done.7), channel_id=1, source_target_pairs={{0,64},{64,0},{1,65},{65,1},{2,66},{66,2},{3,67},{67,3},{4,68},{68... | collective-permute-start | bytes 1572872 | tf_op jit(solution)/shard_map/ppermute | solution.py:22
  47.0 2.8 %collective-permute-start.9 = (bf16[256,768]{1,0:T(8,128)(2,1)}, bf16[256,768]{1,0:T(8,128)(2,1)S(1)}, u32[]{:S(2)}, u32[]{:S(2)}) collective-permute-start(bf16[256,768]{1,0:T(8,128)(2,1)} %collective-permute-done.4.refs_1_.refs_0_), channel_id=1, source_target_pairs={{0,1},{1,0},{2,3},{3,2},{4,5},{5,4},{6,7},{7,6},{8,9},{9,8},{10,11... | collective-permute-start | bytes 1179656 | tf_op jit(solution)/shard_map/ppermute | solution.py:22
  47.0 2.8 %collective-permute-start.10 = (bf16[256,768]{1,0:T(8,128)(2,1)S(1)}, bf16[256,768]{1,0:T(8,128)(2,1)S(1)}, u32[]{:S(2)}, u32[]{:S(2)}) collective-permute-start(bf16[256,768]{1,0:T(8,128)(2,1)S(1)} %collective-permute-done.5.refs_2_.refs_1_), channel_id=1, source_target_pairs={{0,1},{1,0},{2,3},{3,2},{4,5},{5,4},{6,7},{7,6},{8,9},{9,8},{10,11... | collective-permute-start | bytes 1179656 | tf_op jit(solution)/shard_map/ppermute | solution.py:22
  49.9 7.2 %copy-start.4 = (bf16[512,768]{1,0:T(8,128)(2,1)S(1)}, bf16[512,768]{1,0:T(8,128)(2,1)}, u32[]{:S(2)}) copy-start(bf16[512,768]{1,0:T(8,128)(2,1)} %refs_0_.2) | copy-start | bytes 2359300
  49.9 7.2 %copy-start.6 = (bf16[512,768]{1,0:T(8,128)(2,1)S(1)}, bf16[512,768]{1,0:T(8,128)(2,1)}, u32[]{:S(2)}) copy-start(bf16[512,768]{1,0:T(8,128)(2,1)} %copy-done.5) | copy-start | bytes 2359300
  62.9 10.7 %collective-permute-start.11 = (bf16[528,128]{1,0:T(8,128)(2,1)S(1)}, bf16[528,128]{1,0:T(8,128)(2,1)S(1)}, u32[]{:S(2)}, u32[]{:S(2)}) collective-permute-start(bf16[528,128]{1,0:T(8,128)(2,1)S(1)} %get-tuple-element.156), channel_id=1, source_target_pairs={{0,4},{4,0},{8,12},{12,8},{1,5},{5,1},{9,13},{13,9},{2,6},{6,2},{1... | collective-permute-start | bytes 405512 | tf_op jit(solution)/shard_map/ppermute | solution.py:22
  64.6 9.0 %collective-permute-start.12 = (bf16[528,128]{1,0:T(8,128)(2,1)S(1)}, bf16[528,128]{1,0:T(8,128)(2,1)S(1)}, u32[]{:S(2)}, u32[]{:S(2)}) collective-permute-start(bf16[528,128]{1,0:T(8,128)(2,1)S(1)} %get-tuple-element.157), channel_id=1, source_target_pairs={{0,12},{4,8},{8,4},{12,0},{1,13},{5,9},{9,5},{13,1},{2,14},{6,10},... | collective-permute-start | bytes 405512 | tf_op jit(solution)/shard_map/ppermute | solution.py:22
  66.7 7.1 %collective-permute-start.13 = (bf16[528,128]{1,0:T(8,128)(2,1)S(1)}, bf16[528,128]{1,0:T(8,128)(2,1)S(1)}, u32[]{:S(2)}, u32[]{:S(2)}) collective-permute-start(bf16[528,128]{1,0:T(8,128)(2,1)S(1)} %get-tuple-element.158), channel_id=1, source_target_pairs={{0,8},{4,12},{8,0},{12,4},{1,9},{5,13},{9,1},{13,5},{2,10},{6,14},... | collective-permute-start | bytes 405512 | tf_op jit(solution)/shard_map/ppermute | solution.py:22
  74.6 7.6 %collective-permute-start.16 = (bf16[528,128]{1,0:T(8,128)(2,1)S(1)}, bf16[528,128]{1,0:T(8,128)(2,1)S(1)}, u32[]{:S(2)}, u32[]{:S(2)}) collective-permute-start(bf16[528,128]{1,0:T(8,128)(2,1)S(1)} %get-tuple-element.165.a), channel_id=1, source_target_pairs={{0,32},{16,48},{32,0},{48,16},{1,33},{17,49},{33,1},{49,17},{2,34}... | collective-permute-start | bytes 405512 | tf_op jit(solution)/shard_map/ppermute | solution.py:22
  77.7 6.4 %collective-permute-start.15 = (bf16[528,128]{1,0:T(8,128)(2,1)S(1)}, bf16[528,128]{1,0:T(8,128)(2,1)S(1)}, u32[]{:S(2)}, u32[]{:S(2)}) collective-permute-start(bf16[528,128]{1,0:T(8,128)(2,1)S(1)} %get-tuple-element.165.a), channel_id=1, source_target_pairs={{0,48},{16,32},{32,16},{48,0},{1,49},{17,33},{33,17},{49,1},{2,50}... | collective-permute-start | bytes 405512 | tf_op jit(solution)/shard_map/ppermute | solution.py:22
  78.8 5.3 %collective-permute-start.14 = (bf16[528,128]{1,0:T(8,128)(2,1)S(1)}, bf16[528,128]{1,0:T(8,128)(2,1)S(1)}, u32[]{:S(2)}, u32[]{:S(2)}) collective-permute-start(bf16[528,128]{1,0:T(8,128)(2,1)S(1)} %get-tuple-element.165.a), channel_id=1, source_target_pairs={{0,16},{16,0},{32,48},{48,32},{1,17},{17,1},{33,49},{49,33},{2,18}... | collective-permute-start | bytes 405512 | tf_op jit(solution)/shard_map/ppermute | solution.py:22
  85.2 11.1 %collective-permute-start.17 = (bf16[512,128]{1,0:T(8,128)(2,1)S(1)}, bf16[512,128]{1,0:T(8,128)(2,1)S(1)}, u32[]{:S(2)}, u32[]{:S(2)}) collective-permute-start(bf16[512,128]{1,0:T(8,128)(2,1)S(1)} %get-tuple-element.176), channel_id=1, source_target_pairs={{0,4},{4,0},{8,12},{12,8},{1,5},{5,1},{9,13},{13,9},{2,6},{6,2},{1... | collective-permute-start | bytes 393224 | tf_op jit(solution)/shard_map/ppermute | solution.py:22
  86.2 10.1 %collective-permute-start.18 = (bf16[512,128]{1,0:T(8,128)(2,1)S(1)}, bf16[512,128]{1,0:T(8,128)(2,1)S(1)}, u32[]{:S(2)}, u32[]{:S(2)}) collective-permute-start(bf16[512,128]{1,0:T(8,128)(2,1)S(1)} %get-tuple-element.177), channel_id=1, source_target_pairs={{0,12},{4,8},{8,4},{12,0},{1,13},{5,9},{9,5},{13,1},{2,14},{6,10},... | collective-permute-start | bytes 393224 | tf_op jit(solution)/shard_map/ppermute | solution.py:22
  88.4 7.9 %collective-permute-start.19 = (bf16[512,128]{1,0:T(8,128)(2,1)S(1)}, bf16[512,128]{1,0:T(8,128)(2,1)S(1)}, u32[]{:S(2)}, u32[]{:S(2)}) collective-permute-start(bf16[512,128]{1,0:T(8,128)(2,1)S(1)} %get-tuple-element.178), channel_id=1, source_target_pairs={{0,8},{4,12},{8,0},{12,4},{1,9},{5,13},{9,1},{13,5},{2,10},{6,14},... | collective-permute-start | bytes 393224 | tf_op jit(solution)/shard_map/ppermute | solution.py:22
  104.8 14.6 %collective-permute-start.21 = (bf16[384,768]{1,0:T(8,128)(2,1)S(1)}, bf16[384,768]{1,0:T(8,128)(2,1)S(1)}, u32[]{:S(2)}, u32[]{:S(2)}) collective-permute-start(bf16[384,768]{1,0:T(8,128)(2,1)S(1)} %get-tuple-element.210), channel_id=1, source_target_pairs={{0,48},{16,32},{32,16},{48,0},{1,49},{17,33},{33,17},{49,1},{2,50}... | collective-permute-start | bytes 1769480 | tf_op jit(solution)/shard_map/ppermute | solution.py:22
  107.2 13.4 %collective-permute-start.20 = (bf16[384,768]{1,0:T(8,128)(2,1)S(1)}, bf16[384,768]{1,0:T(8,128)(2,1)S(1)}, u32[]{:S(2)}, u32[]{:S(2)}) collective-permute-start(bf16[384,768]{1,0:T(8,128)(2,1)S(1)} %get-tuple-element.206), channel_id=1, source_target_pairs={{0,16},{16,0},{32,48},{48,32},{1,17},{17,1},{33,49},{49,33},{2,18}... | collective-permute-start | bytes 1769480 | tf_op jit(solution)/shard_map/ppermute | solution.py:22
  107.3 16.4 %collective-permute-start.24 = (bf16[384,768]{1,0:T(8,128)(2,1)S(1)}, bf16[384,768]{1,0:T(8,128)(2,1)S(1)}, u32[]{:S(2)}, u32[]{:S(2)}) collective-permute-start(bf16[384,768]{1,0:T(8,128)(2,1)S(1)} %get-tuple-element.219), channel_id=1, source_target_pairs={{0,4},{4,0},{8,12},{12,8},{1,5},{5,1},{9,13},{13,9},{2,6},{6,2},{1... | collective-permute-start | bytes 1769480 | tf_op jit(solution)/shard_map/ppermute | solution.py:22
  108.2 15.5 %collective-permute-start.25 = (bf16[384,768]{1,0:T(8,128)(2,1)S(1)}, bf16[384,768]{1,0:T(8,128)(2,1)S(1)}, u32[]{:S(2)}, u32[]{:S(2)}) collective-permute-start(bf16[384,768]{1,0:T(8,128)(2,1)S(1)} %get-tuple-element.220), channel_id=1, source_target_pairs={{0,12},{4,8},{8,4},{12,0},{1,13},{5,9},{9,5},{13,1},{2,14},{6,10},... | collective-permute-start | bytes 1769480 | tf_op jit(solution)/shard_map/ppermute | solution.py:22
  122.1 26.4 %collective-permute-start.23 = (bf16[768,768]{1,0:T(8,128)(2,1)S(1)}, bf16[768,768]{1,0:T(8,128)(2,1)S(1)}, u32[]{:S(2)}, u32[]{:S(2)}) collective-permute-start(bf16[768,768]{1,0:T(8,128)(2,1)S(1)} %get-tuple-element.216), channel_id=1, source_target_pairs={{0,48},{16,32},{32,16},{48,0},{1,49},{17,33},{33,17},{49,1},{2,50}... | collective-permute-start | bytes 3538952 | tf_op jit(solution)/shard_map/ppermute | solution.py:22
  123.6 25.1 %collective-permute-start.22 = (bf16[768,768]{1,0:T(8,128)(2,1)S(1)}, bf16[768,768]{1,0:T(8,128)(2,1)S(1)}, u32[]{:S(2)}, u32[]{:S(2)}) collective-permute-start(bf16[768,768]{1,0:T(8,128)(2,1)S(1)} %get-tuple-element.215), channel_id=1, source_target_pairs={{0,16},{16,0},{32,48},{48,32},{1,17},{17,1},{33,49},{49,33},{2,18}... | collective-permute-start | bytes 3538952 | tf_op jit(solution)/shard_map/ppermute | solution.py:22
  125.1 26.4 %collective-permute-start.30 = (bf16[768,768]{1,0:T(8,128)(2,1)S(1)}, bf16[768,768]{1,0:T(8,128)(2,1)S(1)}, u32[]{:S(2)}, u32[]{:S(2)}) collective-permute-start(bf16[768,768]{1,0:T(8,128)(2,1)S(1)} %get-tuple-element.236), channel_id=1, source_target_pairs={{0,12},{4,8},{8,4},{12,0},{1,13},{5,9},{9,5},{13,1},{2,14},{6,10},... | collective-permute-start | bytes 3538952 | tf_op jit(solution)/shard_map/ppermute | solution.py:22
  127.5 24.7 %collective-permute-start.29 = (bf16[768,768]{1,0:T(8,128)(2,1)S(1)}, bf16[768,768]{1,0:T(8,128)(2,1)S(1)}, u32[]{:S(2)}, u32[]{:S(2)}) collective-permute-start(bf16[768,768]{1,0:T(8,128)(2,1)S(1)} %get-tuple-element.223), channel_id=1, source_target_pairs={{0,4},{4,0},{8,12},{12,8},{1,5},{5,1},{9,13},{13,9},{2,6},{6,2},{1... | collective-permute-start | bytes 3538952 | tf_op jit(solution)/shard_map/ppermute | solution.py:22
  153.2 8.1 %collective-permute-start.31 = (bf16[192,768]{1,0:T(8,128)(2,1)S(1)}, bf16[192,768]{1,0:T(8,128)(2,1)S(1)}, u32[]{:S(2)}, u32[]{:S(2)}) collective-permute-start(bf16[192,768]{1,0:T(8,128)(2,1)S(1)} %get-tuple-element.240), channel_id=1, source_target_pairs={{0,16},{16,0},{32,48},{48,32},{1,17},{17,1},{33,49},{49,33},{2,18}... | collective-permute-start | bytes 884744 | tf_op jit(solution)/shard_map/ppermute | solution.py:22
  155.4 11.6 %collective-permute-start.26 = (bf16[192,768]{1,0:T(8,128)(2,1)S(1)}, bf16[192,768]{1,0:T(8,128)(2,1)S(1)}, u32[]{:S(2)}, u32[]{:S(2)}) collective-permute-start(bf16[192,768]{1,0:T(8,128)(2,1)S(1)} %get-tuple-element.232), channel_id=1, source_target_pairs={{0,4},{4,0},{8,12},{12,8},{1,5},{5,1},{9,13},{13,9},{2,6},{6,2},{1... | collective-permute-start | bytes 884744 | tf_op jit(solution)/shard_map/ppermute | solution.py:22
  155.5 11.5 %collective-permute-start.32 = (bf16[192,768]{1,0:T(8,128)(2,1)S(1)}, bf16[192,768]{1,0:T(8,128)(2,1)S(1)}, u32[]{:S(2)}, u32[]{:S(2)}) collective-permute-start(bf16[192,768]{1,0:T(8,128)(2,1)S(1)} %get-tuple-element.241), channel_id=1, source_target_pairs={{0,48},{16,32},{32,16},{48,0},{1,49},{17,33},{33,17},{49,1},{2,50}... | collective-permute-start | bytes 884744 | tf_op jit(solution)/shard_map/ppermute | solution.py:22
  157.2 9.8 %collective-permute-start.33 = (bf16[192,768]{1,0:T(8,128)(2,1)S(1)}, bf16[192,768]{1,0:T(8,128)(2,1)S(1)}, u32[]{:S(2)}, u32[]{:S(2)}) collective-permute-start(bf16[192,768]{1,0:T(8,128)(2,1)S(1)} %get-tuple-element.242), channel_id=1, source_target_pairs={{0,32},{16,48},{32,0},{48,16},{1,33},{17,49},{33,1},{49,17},{2,34}... | collective-permute-start | bytes 884744 | tf_op jit(solution)/shard_map/ppermute | solution.py:22
  157.7 12.2 %collective-permute-start.27 = (bf16[192,768]{1,0:T(8,128)(2,1)S(1)}, bf16[192,768]{1,0:T(8,128)(2,1)S(1)}, u32[]{:S(2)}, u32[]{:S(2)}) collective-permute-start(bf16[192,768]{1,0:T(8,128)(2,1)S(1)} %get-tuple-element.233), channel_id=1, source_target_pairs={{0,12},{4,8},{8,4},{12,0},{1,13},{5,9},{9,5},{13,1},{2,14},{6,10},... | collective-permute-start | bytes 884744 | tf_op jit(solution)/shard_map/ppermute | solution.py:22
  161.3 8.5 %collective-permute-start.28 = (bf16[192,768]{1,0:T(8,128)(2,1)S(1)}, bf16[192,768]{1,0:T(8,128)(2,1)S(1)}, u32[]{:S(2)}, u32[]{:S(2)}) collective-permute-start(bf16[192,768]{1,0:T(8,128)(2,1)S(1)} %get-tuple-element.234), channel_id=1, source_target_pairs={{0,8},{4,12},{8,0},{12,4},{1,9},{5,13},{9,1},{13,5},{2,10},{6,14},... | collective-permute-start | bytes 884744 | tf_op jit(solution)/shard_map/ppermute | solution.py:22
  170.7 8.3 %collective-permute-start.34 = (bf16[2,96,768]{2,1,0:T(8,128)(2,1)S(1)}, bf16[2,96,768]{2,1,0:T(8,128)(2,1)S(1)}, u32[]{:S(2)}, u32[]{:S(2)}) collective-permute-start(bf16[2,96,768]{2,1,0:T(8,128)(2,1)S(1)} %get-tuple-element.244), channel_id=1, source_target_pairs={{0,64},{64,0},{1,65},{65,1},{2,66},{66,2},{3,67},{67,3},{4,68},{68... | collective-permute-start | bytes 884744 | tf_op jit(solution)/shard_map/ppermute | solution.py:22

commit v4 on v3

--- a/solution.py
+++ b/solution.py
@@ -50,6 +50,10 @@
     )(table, *operands)
 
 
+def in_hbm(xs):
+    return [pltpu.with_memory_space_constraint(x, pltpu.HBM) for x in xs]
+
+
 def shape(dims, kind=BF16):
     return jax.ShapeDtypeStruct(dims, kind)
 
@@ -63,7 +67,7 @@
     n, counts = len(shards), [len(x) for x in shards]
     flat = [part for x in shards for part in x]
     tokens, width = sum(part.shape[0] for part in shards[0]), flat[0].shape[1]
-    cols = weight.shape[2] // 2
+    cols = weight.shape[2]
 
     def body(s, *refs):
         out, rest = refs[-1], list(refs)
@@ -83,14 +87,14 @@
     in_specs = [whole(x) for x in flat]
     for flip in flips:
         in_specs.append(
-            pl.BlockSpec((1, width, cols), lambda g, s, flip=flip: (g, s[TEN] ^ flip, s[Z]))
+            pl.BlockSpec((1, width, cols), lambda g, s, flip=flip: (g, s[TEN] ^ flip, 0))
         )
     operands = [*flat, *([weight] * n)]
     if partial is not None:
         in_specs.append(tile)
         operands.append(partial)
-    out = shape((3, tokens, cols), BF16 if last else F32)
-    return call("project", body, table, (3,), operands, in_specs, out, tile, 24)
+    out = shape((3, tokens, cols)) if last else pltpu.HBM((3, tokens, cols), F32)
+    return call("project", body, table, (3,), in_hbm(operands), in_specs, out, tile, 24)
 
 
 def shard_states(table, qkv, out_grad, cumul, which, so_far):
@@ -312,7 +316,7 @@
             qkv_ref[1].astype(F32) * until,
         )
         for j in range(3):
-            out[j] = jnp.where(live, grads[j], 0.0)
+            out[j] = jnp.where(live, grads[j], 0.0).astype(BF16)
             ready[j] = jnp.where(live, rows[j], 0.0).astype(BF16)
 
     tile = pl.BlockSpec((3, tokens, HEAD), lambda h, s: (0, 0, h + first))
@@ -328,7 +332,7 @@
         (count,),
         operands,
         in_specs,
-        [shape(qkv.shape, F32), shape(qkv.shape)],
+        [shape(qkv.shape), shape(qkv.shape)],
         [tile, tile],
         12,
         alias=None if so_far is None else {4: 0, 5: 1},
@@ -354,7 +358,7 @@
             lax.dot_general(ready_ref[1], later, AB_T, preferred_element_type=F32),
             dot(ready_ref[2], later),
         )
-        grads = [(local_ref[j] + cross[j]).astype(BF16) for j in range(3)]
+        grads = [(local_ref[j].astype(F32) + cross[j]).astype(BF16) for j in range(3)]
         for k in range(heads):
 
             @pl.when(h == k)
@@ -379,25 +383,40 @@
     )
 
 
-def turn(table, shards):
-    counts = [len(x) for x in shards]
-    flat = [part for x in shards for part in x]
-    tokens, width = sum(part.shape[0] for part in shards[0]), flat[0].shape[1]
-    rows = 4 * width // 32
+def turn(table, shards, base, so_far):
+    tokens, width = shards[0].shape
+    n, rows = len(shards), 4 * width // 32
 
     def body(s, *refs):
-        out, at = refs[-1], 0
-        for k, count in enumerate(counts):
-            mine, at = refs[at : at + count], at + count
-
-            @pl.when((pl.program_id(0) ^ s[TEN]) == k)
-            def _(mine=mine):
-                out[...] = joined(mine).T.reshape(out.shape)
+        out = refs[-1]
+        for k in range(n):
+
+            @pl.when(pl.program_id(0) == k)
+            def _(k=k):
+                out[...] = refs[k][...].T.reshape(out.shape)
+
+    def place(i, s):
+        i = s[TEN] ^ (base + i)
+        return i % 2, (i // 2) ^ s[Z], 0, 0
 
     out = shape((16, 2, rows, tokens))
-    spec = pl.BlockSpec((8, 1, rows, tokens), lambda i, s: (i % 2, (i // 2) ^ s[Z], 0, 0))
-    turned = call("turn", body, table, (4,), flat, [whole(x) for x in flat], out, spec, 12)
-    return turned.reshape(4, 4, 2 * rows, tokens)
+    spec = pl.BlockSpec((8, 1, rows, tokens), place)
+    operands, in_specs = in_hbm(shards), [whole(x) for x in shards]
+    if so_far is not None:
+        operands.append(so_far)
+        in_specs.append(pl.BlockSpec(memory_space=pl.ANY))
+    return call(
+        "turn",
+        body,
+        table,
+        (n,),
+        operands,
+        in_specs,
+        out,
+        spec,
+        12,
+        alias=None if so_far is None else {n + 1: 0},
+    )
 
 
 def weight_part(table, turned, lefts, rights, places, split):
@@ -465,18 +484,20 @@
     )
 
 
-def cut_blocks(table, axis, own, first, second):
-    rows, cols = own.shape[0] // 4, own.shape[1]
-
-    def body(s, a, b, c, *outs):
-        for r, out in zip((1, 3, 2, 0), outs):
-            at = pl.ds(pl.multiple_of((s[axis] ^ r) * rows, rows), rows)
-            total = a[at, :].astype(F32) + b[at, :].astype(F32) + c[at, :].astype(F32)
-            out[...] = total.astype(BF16)
-
-    outs = [shape((rows, cols))] * 4
-    operands = (own, first, second)
-    return call(
+def cut_blocks(table, left, right):
+    rows, cols = left[0].shape[0] // 4, left[0].shape[1]
+
+    def body(s, *refs):
+        for k, axis in enumerate((Y, X)):
+            a, b, c = refs[3 * k : 3 * k + 3]
+            for r, out in zip((1, 3, 2, 0), refs[6 + 4 * k : 10 + 4 * k]):
+                at = pl.ds(pl.multiple_of((s[axis] ^ r) * rows, rows), rows)
+                total = a[at, :].astype(F32) + b[at, :].astype(F32) + c[at, :].astype(F32)
+                out[...] = total.astype(BF16)
+
+    outs = [shape((rows, cols))] * 8
+    operands = (*left, *right)
+    cut = call(
         "cut_blocks",
         body,
         table,
@@ -485,8 +506,9 @@
         [whole(x) for x in operands],
         outs,
         [whole(o) for o in outs],
-        20,
-    )
+        24,
+    )
+    return cut[:4], cut[4:]
 
 
 def final_sums(table, sides):
@@ -545,7 +567,9 @@
     here_z = index[0]
     fixed = [*index, index[3] * 2 + index[4]]
     table = jnp.stack([*fixed, lengths[0]]).astype(jnp.int32)
-    weight = pltpu.with_memory_space_constraint(jnp.transpose(qkv_weight, (1, 0, 2)), pltpu.HBM)
+    weight = jnp.transpose(qkv_weight, (1, 0, 2))
+    width = per * HEAD
+    weight = lax.dynamic_slice_in_dim(weight, here_z * width, width, axis=2)
 
     near = send(activations, "zl", 1)
     side = across(activations)
@@ -555,30 +579,29 @@
     cumul = jnp.cumsum(log_decay.T * live[None, :], axis=1)
     size = jnp.broadcast_to(lengths.astype(F32)[:, None], (per, tokens))
     note = jnp.concatenate([lax.dynamic_slice_in_dim(cumul, (1 - here_z) * per, per), size])
-    note = send(note, "c0", 1)
-    width = per * HEAD
     og_own = lax.dynamic_slice_in_dim(out_grad, here_z * width, width, axis=1)
     og_other = lax.dynamic_slice_in_dim(out_grad, (1 - here_z) * width, width, axis=1)
 
     acc_own = project(table, [[activations], [core]], (0, 1), weight, None, False)
-    near, side, acc_own, note, og_other = tied((near, side, acc_own, note, og_other))
-    half = tokens // 2
-    far = [send(side[:half], "zl", 1), across(near[half:])]
+    turned = turn(table, [activations, core], 0, None)
+    near, side, acc_own, note, og_other, turned = tied((near, side, acc_own, note, og_other, turned))
+    note = send(note, "c0", 1)
     near_core = send(near, "co", 1)
     side_core = send(side, "co", 1)
-    cumul = jnp.concatenate([lax.dynamic_slice_in_dim(cumul, here_z * per, per), note[:per]])
-    table_pair = jnp.stack([*fixed, note[per, 0].astype(jnp.int32)]).astype(jnp.int32)
+    far = send(tied((activations, near, side))[0], "c0", 1)
     acc_pair = project(table, [[side]], (2,), weight, None, False)
     near_core, acc_pair = tied((near_core, acc_pair))
     qkv_own = project(table, [[near], [near_core]], (2, 3), weight, acc_own, True)
-    far, side_core, qkv_own, table_pair, cumul = tied((far, side_core, qkv_own, table_pair, cumul))
-    far_core = [send(x, "co", 1) for x in far]
+    turned = [turn(table, tied(([near, near_core], qkv_own))[0], 2, turned)]
+    note, side_core, qkv_own, far, turned = tied((note, side_core, qkv_own, far, turned))
+    cumul = jnp.concatenate([lax.dynamic_slice_in_dim(cumul, here_z * per, per), note[:per]])
+    table_pair = jnp.stack([*fixed, note[per, 0].astype(jnp.int32)]).astype(jnp.int32)
+    far_core = send(far, "co", 1)
     og_pair = send(tied((og_other, far))[0], "c0", 1)
     to_y = shard_states(table, qkv_own, og_own, cumul, 0, None)
     far_core, to_y = tied((far_core, to_y))
-    qkv_pair = project(table_pair, [[side_core], far, far_core], (3, 0, 1), weight, acc_pair, True)
-    turned = [turn(table, tied(([[activations], [core], [near], [near_core]], qkv_pair))[0])]
-    og_pair, qkv_pair, turned = tied((og_pair, qkv_pair, turned))
+    qkv_pair = project(table_pair, [[side_core], [far], [far_core]], (3, 0, 1), weight, acc_pair, True)
+    og_pair, qkv_pair = tied((og_pair, qkv_pair))
 
     to_y = shard_states(table, qkv_pair, og_pair, cumul, 1, to_y)
     at_y = [send(to_y[r], "c2", r) for r in (1, 3, 2)]
@@ -594,10 +617,11 @@
     states = [send(back[r], "c2", r) for r in (1, 3, 2)]
     local, _ = tied((local, back[0]))
     local = local_grads(table_pair, qkv_pair, og_pair, cumul, 1, per // 2, per // 2, local)
-    second, _ = tied(([far, far_core, [side], [side_core]], back[0]))
-    turned.append(turn(table, second))
+    second, _ = tied(([far, far_core, side, side_core], back[0]))
+    turned.append(turn(table, second, 0, None))
     states, turned, local = tied((states, turned, local))
     states = [back[0], states[0], states[2], states[1]]
+    turned = [t.reshape(4, 4, -1, tokens) for t in turned]
 
     left_own, right_own = whole_grads(table, 0, *local_own, states)
     left_pair, right_pair = whole_grads(table, 1, *local, states)
@@ -615,9 +639,7 @@
     turned, _ = tied((turned, r_one))
     own = weight_part(table, turned, lefts, rights, (0,), False)
     l_got, own = tied((l_got, own))
-    l_cut = cut_blocks(table, Y, own[0], *l_got)
-    r_got, _ = tied((r_got, l_cut))
-    r_cut = cut_blocks(table, X, own[1], *r_got)
+    l_cut, r_cut = cut_blocks(table, (own[0], *l_got), (own[1], *r_got))
     l_got = [send(x, "c2", by) for x, by in zip(l_cut, (1, 3, 2))]
     r_got = [send(x, "c1", by) for x, by in zip(r_cut, (1, 3, 2))]
     here, there = final_sums(table, ((l_cut[3], *l_got), (r_cut[3], *r_got)))

time: 182 us -> 186 us (1.022)
  Pallas kernels: 76 us -> 85.4 us
  waiting for transfers between devices: 47.3 us -> 41.1 us
  local copies, waits for them, and re-layouts: 9.21 us -> 13.3 us
    pallas_call x24, Pallas kernels: 76 us -> 85.4 us  [call(): pl.pallas_call(body, grid_spec=pltpu.PrefetchScalarGridSpec(num_scalar_pr...]
    dynamic_slice x0 -> x1, local copies, waits for them, and re-layouts: none -> 7.94 us  [device_part(): weight = lax.dynamic_slice_in_dim(weight, here_z * width, width, axis=2)]
    ppermute x33 -> x32, waiting for transfers between devices: 47.3 us -> 41.1 us  [send(): lax.ppermute(x, axis, [(i, i ^ by) for i in range(lax.axis_size(axis))])]
    ppermute x2 -> x1, starting transfers between devices: 6.95 us -> 2.52 us  [across(): return lax.ppermute(x, ('c0', 'zl'), [(0, 3), (1, 2), (2, 1), (3, 0)])]
    slice x3 -> x1, local copies, waits for them, and re-layouts: 3.75 us -> 0.16 us  [the longest x2 3.59 us: device_part(): far = [send(side[:half], 'zl', 1), across(near[half:])]]
    ppermute x33 -> x32, starting transfers between devices: 36.8 us -> 39.6 us  [send(): lax.ppermute(x, axis, [(i, i ^ by) for i in range(lax.axis_size(axis))])]
  transfers between devices with their start and end apart: 35 -> 33, of which waited for: 15 -> 14; matrix products, arithmetic and copies ran while one was open for 6% -> 7% of each run, Pallas kernels for 33% -> 37%
where the time goes in v4:
time: 186 us
  Pallas kernels  85.4 us (46%)
  starting transfers between devices  42.1 us (23%)
  waiting for transfers between devices  41.1 us (22%)
  local copies, waits for them, and re-layouts  13.3 us (7%)
  other arithmetic  1.98 us (1%)
    pallas_call x24, Pallas kernels, call(): pl.pallas_call(body, grid_spec=pltpu.PrefetchScalarGridSpec(num_scalar_pr...  85.4 us
    ppermute x32, waiting for transfers between devices, send(): lax.ppermute(x, axis, [(i, i ^ by) for i in range(lax.axis_size(axis))])  41.1 us
    ppermute x32, starting transfers between devices, send(): lax.ppermute(x, axis, [(i, i ^ by) for i in range(lax.axis_size(axis))])  39.6 us
    dynamic_slice x1, local copies, waits for them, and re-layouts, device_part(): weight = lax.dynamic_slice_in_dim(weight, here_z * width, width, axis=2)  7.94 us
  transfers between devices with their start and end apart: 33, of which 14 were waited for; matrix products, arithmetic and copies ran while one was open for 7% of the time, Pallas kernels for 37%

profile of v4, /device:TPU:0, one launch (start us, length us, event | category | flops | bytes accessed | tf_op | source)
XLA Modules:
  0.0 185.5 jit_solution(9356267185203824238)
XLA Ops:
  0.0 2.0 %collective-permute-start = (bf16[512,768]{1,0:T(8,128)(2,1)}, bf16[512,768]{1,0:T(8,128)(2,1)}, u32[]{:S(2)}, u32[]{:S(2)}) collective-permute-start(bf16[512,768]{1,0:T(8,128)(2,1)} %refs_0_.3), channel_id=1, source_target_pairs={{0,2},{2,0},{1,3},{3,1},{4,6},{6,4},{5,7},{7,5},{8,10},{10,8},{9,1... | collective-permute-start | bytes 2359304 | tf_op jit(solution)/shard_map/ppermute | solution.py:22
  2.0 2.5 %collective-permute-start.1 = (bf16[512,768]{1,0:T(8,128)(2,1)}, bf16[512,768]{1,0:T(8,128)(2,1)}, u32[]{:S(2)}, u32[]{:S(2)}) collective-permute-start(bf16[512,768]{1,0:T(8,128)(2,1)} %refs_0_.3), channel_id=1, source_target_pairs={{0,66},{2,64},{64,2},{66,0},{1,67},{3,65},{65,3},{67,1},{4,70},{6,... | collective-permute-start | bytes 2359304 | tf_op jit(solution)/shard_map/ppermute | solution.py:26
  7.4 2.3 %constant_dynamic-slice_fusion.1 = (bf16[512,512]{1,0:T(8,128)(2,1)}, bf16[512,512]{1,0:T(8,128)(2,1)}) fusion(bf16[512,1024]{1,0:T(8,128)(2,1)} %param.9, s32[]{:T(128)S(6)} %select_n.13, s32[]{:T(128)S(6)} %select_n.15), kind=kLoop, calls=%fused_computation.8 | loop fusion | bytes 2097160 | tf_op jit(solution)/shard_map/dynamic_slice | solution.py:582
  9.7 7.9 %dynamic-slice_bitcast_fusion.refs_2_.refs_3_.refs_1_.refs_4_.refs_5_ = bf16[3,3072,512]{2,1,0:T(8,128)(2,1)} fusion(bf16[3072,3,1024]{2,0,1:T(8,128)(2,1)} %param.6, s32[]{:T(128)S(6)} %select_n.13), kind=kLoop, calls=%fused_computation | loop fusion | bytes 18874372 | tf_op jit(solution)/shard_map/dynamic_slice | solution.py:572
  17.6 2.7 %turn.3.refs_2_ = bf16[16,2,96,512]{3,2,1,0:T(8,128)(2,1)S(1)} custom-call(s32[7]{0:T(128)S(1)} %stack.39.s, bf16[512,768]{1,0:T(8,128)(2,1)} %refs_0_.3, bf16[512,768]{1,0:T(8,128)(2,1)} %collective-permute-done.2.refs_1_), custom_call_target="tpu_custom_call" | custom-call | flops 1 | bytes 1 | tf_op jit(solution)/shard_map/turn/pallas_call | solution.py:34
  20.3 7.3 %project.4.refs_4_ = f32[3,512,512]{2,1,0:T(8,128)} custom-call(s32[7]{0:T(128)S(1)} %stack.39.s, bf16[512,768]{1,0:T(8,128)(2,1)} %refs_0_.3, bf16[512,768]{1,0:T(8,128)(2,1)} %collective-permute-done.2.refs_1_, bf16[3,3072,512]{2,1,0:T(8,128)(2,1)} %dynamic-slice_bitcast_fusion.refs_2_.refs_3_.refs_1_.refs_4_.refs_5_, ...), custom_call_target="tpu_custom_call" | custom-call | flops 1 | bytes 1 | tf_op jit(solution)/shard_map/project/pallas_call | solution.py:34
  29.0 2.5 %collective-permute-start.3 = (f32[8,512]{1,0:T(8,128)S(1)}, f32[8,512]{1,0:T(8,128)S(1)}, u32[]{:S(2)}, u32[]{:S(2)}) collective-permute-start(f32[8,512]{1,0:T(8,128)S(1)} %concatenate.6), channel_id=1, source_target_pairs={{0,64},{64,0},{1,65},{65,1},{2,66},{66,2},{3,67},{67,3},{4,68},{68... | collective-permute-start | bytes 49160 | tf_op jit(solution)/shard_map/ppermute | solution.py:22
  31.5 5.7 %project.5.refs_6_ = f32[3,512,512]{2,1,0:T(8,128)} custom-call(s32[7]{0:T(128)S(1)} %stack.39.s, bf16[512,768]{1,0:T(8,128)(2,1)} %collective-permute-done.1.refs_0_.refs_2_, bf16[3,3072,512]{2,1,0:T(8,128)(2,1)} %dynamic-slice_bitcast_fusion.refs_2_.refs_3_.refs_1_.refs_4_.refs_5_), custom_call_target="tpu_custom_call" | custom-call | flops 1 | bytes 1 | tf_op jit(solution)/shard_map/project/pallas_call | solution.py:34
  38.1 6.7 %project.6.qkv_ref = bf16[3,512,512]{2,1,0:T(8,128)(2,1)S(1)} custom-call(s32[7]{0:T(128)S(1)} %stack.39.s, bf16[512,768]{1,0:T(8,128)(2,1)} %collective-permute-done.refs_0_, bf16[512,768]{1,0:T(8,128)(2,1)} %copy-done.9, bf16[3,3072,512]{2,1,0:T(8,128)(2,1)} %dynamic-slice_bitcast_fusion.refs_2_.refs_3_.refs_1_.refs_4_.refs_5_, ...), custom_call_target="tpu_custom_call" | custom-call | flops 1 | bytes 1 | tf_op jit(solution)/shard_map/project/pallas_call | solution.py:34
  44.8 2.8 %turn.4 = bf16[16,2,96,512]{3,2,1,0:T(8,128)(2,1)S(1)} custom-call(s32[7]{0:T(128)S(1)} %stack.39.s, bf16[512,768]{1,0:T(8,128)(2,1)} %collective-permute-done.refs_0_, bf16[512,768]{1,0:T(8,128)(2,1)} %copy-done.9, bf16[16,2,96,512]{3,2,1,0:T(8,128)(2,1)S(1)} %turn.3.refs_2_), custom_call_target="tpu_custom_call", output_to_operand_aliasing={{}: (3, {})} | custom-call | flops 1 | bytes 1 | tf_op jit(solution)/shard_map/turn/pallas_call | solution.py:34
  47.6 2.0 %collective-permute-done.3 = f32[8,512]{1,0:T(8,128)S(1)} collective-permute-done((f32[8,512]{1,0:T(8,128)S(1)}, f32[8,512]{1,0:T(8,128)S(1)}, u32[]{:S(2)}, u32[]{:S(2)}) %collective-permute-start.3) | collective-permute-done | bytes 16416 | tf_op jit(solution)/shard_map/ppermute | solution.py:22
  50.8 2.3 %shard_states.2 = (bf16[528,128]{1,0:T(8,128)(2,1)S(1)}, bf16[528,128]{1,0:T(8,128)(2,1)S(1)}, bf16[528,128]{1,0:T(8,128)(2,1)S(1)}, bf16[528,128]{1,0:T(8,128)(2,1)S(1)}) custom-call(s32[7]{0:T(128)S(1)} %stack.39.s, bf16[3,512,512]{2,1,0:T(8,128)(2,1)S(1)} %project.6.qkv_ref, bf16[512,512]{1,0:T(8,128)(2,1)S(1)} %copy-done.2, ...), custom_call_target="tpu_custom_call" | custom-call | flops 1 | bytes 1 | tf_op jit(solution)/shard_map/shard_states/pallas_call | solution.py:34
  55.6 8.2 %project.7.qkv_ref = bf16[3,512,512]{2,1,0:T(8,128)(2,1)S(1)} custom-call(s32[7]{0:T(128)S(1)} %stack.41.s, bf16[512,768]{1,0:T(8,128)(2,1)} %copy-done.10, bf16[512,768]{1,0:T(8,128)(2,1)} %collective-permute-done.6.refs_1_.refs_0_, bf16[512,768]{1,0:T(8,128)(2,1)} %collective-permute-done.8.refs_2_.refs_1_, ...), custom_call_target="tpu_custom_call" | custom-call | flops 1 | bytes 1 | tf_op jit(solution)/shard_map/project/pallas_call | solution.py:34
  63.8 2.0 %collective-permute-done.7.og_ref = bf16[512,512]{1,0:T(8,128)(2,1)} collective-permute-done((bf16[512,512]{1,0:T(8,128)(2,1)}, bf16[512,512]{1,0:T(8,128)(2,1)}, u32[]{:S(2)}, u32[]{:S(2)}) %collective-permute-start.7) | collective-permute-done | bytes 524320 | tf_op jit(solution)/shard_map/ppermute | solution.py:22
  65.8 3.6 %shard_states.3 = (bf16[528,128]{1,0:T(8,128)(2,1)S(1)}, bf16[528,128]{1,0:T(8,128)(2,1)S(1)}, bf16[528,128]{1,0:T(8,128)(2,1)S(1)}, bf16[528,128]{1,0:T(8,128)(2,1)S(1)}) custom-call(s32[7]{0:T(128)S(1)} %stack.39.s, bf16[3,512,512]{2,1,0:T(8,128)(2,1)S(1)} %project.7.qkv_ref, bf16[512,512]{1,0:T(8,128)(2,1)} %collective-permute-done.7.og_ref, ...), custom_call_target="tpu_custom_call" | custom-call | flops 1 | bytes 1 | tf_op jit(solution)/shard_map/shard_states/pallas_call | solution.py:34
  69.5 3.1 %collective-permute-start.10 = (bf16[528,128]{1,0:T(8,128)(2,1)S(1)}, bf16[528,128]{1,0:T(8,128)(2,1)S(1)}, u32[]{:S(2)}, u32[]{:S(2)}) collective-permute-start(bf16[528,128]{1,0:T(8,128)(2,1)S(1)} %get-tuple-element.147), channel_id=1, source_target_pairs={{0,12},{4,8},{8,4},{12,0},{1,13},{5,9},{9,5},{13,1},{2,14},{6,10},... | collective-permute-start | bytes 405512 | tf_op jit(solution)/shard_map/ppermute | solution.py:22
  73.6 6.0 %local_grads.3 = (bf16[3,512,512]{2,1,0:T(8,128)(2,1)S(1)}, bf16[3,512,512]{2,1,0:T(8,128)(2,1)S(1)}) custom-call(s32[7]{0:T(128)S(1)} %stack.39.s, bf16[3,512,512]{2,1,0:T(8,128)(2,1)S(1)} %copy-done.1, bf16[512,512]{1,0:T(8,128)(2,1)S(1)} %copy-done.3, f32[8,512]{1,0:T(8,128)S(1)} %pad_maximum_fusion.cum_ref), custom_call_target="tpu_custom_call" | custom-call | flops 1 | bytes 1 | tf_op jit(solution)/shard_map/local_grads/pallas_call | solution.py:34
  81.1 1.6 collective-permute-start.12
  82.7 2.1 %collective-permute-start.13 = (bf16[528,128]{1,0:T(8,128)(2,1)S(1)}, bf16[528,128]{1,0:T(8,128)(2,1)S(1)}, u32[]{:S(2)}, u32[]{:S(2)}) collective-permute-start(bf16[528,128]{1,0:T(8,128)(2,1)S(1)} %get-tuple-element.155.a), channel_id=1, source_target_pairs={{0,48},{16,32},{32,16},{48,0},{1,49},{17,33},{33,17},{49,1},{2,50}... | collective-permute-start | bytes 405512 | tf_op jit(solution)/shard_map/ppermute | solution.py:22
  85.4 4.0 %local_grads.4 = (bf16[3,512,512]{2,1,0:T(8,128)(2,1)S(1)}, bf16[3,512,512]{2,1,0:T(8,128)(2,1)S(1)}) custom-call(s32[7]{0:T(128)S(1)} %stack.41.s, bf16[3,512,512]{2,1,0:T(8,128)(2,1)S(1)} %project.7.qkv_ref, bf16[512,512]{1,0:T(8,128)(2,1)} %collective-permute-done.7.og_ref, f32[8,512]{1,0:T(8,128)S(1)} %pad_maximum_fusion.cum_ref), custom_call_target="tpu_custom_call" | custom-call | flops 1 | bytes 1 | tf_op jit(solution)/shard_map/local_grads/pallas_call | solution.py:34
  89.7 1.5 collective-permute-done.14.c
  92.3 1.3 collective-permute-start.15
  93.5 2.2 %collective-permute-start.16 = (bf16[512,128]{1,0:T(8,128)(2,1)S(1)}, bf16[512,128]{1,0:T(8,128)(2,1)S(1)}, u32[]{:S(2)}, u32[]{:S(2)}) collective-permute-start(bf16[512,128]{1,0:T(8,128)(2,1)S(1)} %get-tuple-element.167), channel_id=1, source_target_pairs={{0,12},{4,8},{8,4},{12,0},{1,13},{5,9},{9,5},{13,1},{2,14},{6,10},... | collective-permute-start | bytes 393224 | tf_op jit(solution)/shard_map/ppermute | solution.py:22
  96.4 4.0 %local_grads.5 = (bf16[3,512,512]{2,1,0:T(8,128)(2,1)S(1)}, bf16[3,512,512]{2,1,0:T(8,128)(2,1)S(1)}) custom-call(s32[7]{0:T(128)S(1)} %stack.41.s, bf16[3,512,512]{2,1,0:T(8,128)(2,1)S(1)} %project.7.qkv_ref, bf16[512,512]{1,0:T(8,128)(2,1)} %collective-permute-done.7.og_ref, ...), custom_call_target="tpu_custom_call", output_to_operand_aliasing={{0}: (4, {}), {1}: (5, {})} | custom-call | flops 1 | bytes 1 | tf_op jit(solution)/shard_map/local_grads/pallas_call | solution.py:34
  100.5 3.9 %turn.5 = bf16[16,2,96,512]{3,2,1,0:T(8,128)(2,1)S(1)} custom-call(s32[7]{0:T(128)S(1)} %stack.39.s, bf16[512,768]{1,0:T(8,128)(2,1)} %collective-permute-done.6.refs_1_.refs_0_, bf16[512,768]{1,0:T(8,128)(2,1)} %collective-permute-done.8.refs_2_.refs_1_, bf16[512,768]{1,0:T(8,128)(2,1)} %collective-permute-done.1.refs_0_.refs_2_, bf16[512,768]{1,0:T(8,128)(2,1)} %copy-done.10), custom_call_target="tpu_custom_call" | custom-call | flops 1 | bytes 1 | tf_op jit(solution)/shard_map/turn/pallas_call | solution.py:34
  104.4 2.5 %whole_grads.3 = (bf16[512,768]{1,0:T(8,128)(2,1)S(1)}, bf16[512,768]{1,0:T(8,128)(2,1)S(1)}) custom-call(s32[7]{0:T(128)S(1)} %stack.39.s, bf16[3,512,512]{2,1,0:T(8,128)(2,1)S(1)} %get-tuple-element.189.local_ref, bf16[3,512,512]{2,1,0:T(8,128)(2,1)S(1)} %get-tuple-element.190.ready_ref, bf16[512,128]{1,0:T(8,128)(2,1)S(1)} %get-tuple-element.170.a, ...), custom_call_target="tpu_custom_call" | custom-call | flops 1 | bytes 1 | tf_op jit(solution)/shard_map/whole_grads/pallas_call | solution.py:34
  107.0 2.5 %whole_grads.2 = (bf16[512,768]{1,0:T(8,128)(2,1)S(1)}, bf16[512,768]{1,0:T(8,128)(2,1)S(1)}) custom-call(s32[7]{0:T(128)S(1)} %stack.39.s, bf16[3,512,512]{2,1,0:T(8,128)(2,1)S(1)} %get-tuple-element.183.local_ref, bf16[3,512,512]{2,1,0:T(8,128)(2,1)S(1)} %get-tuple-element.184.ready_ref, bf16[512,128]{1,0:T(8,128)(2,1)S(1)} %get-tuple-element.170.a, ...), custom_call_target="tpu_custom_call" | custom-call | flops 1 | bytes 1 | tf_op jit(solution)/shard_map/whole_grads/pallas_call | solution.py:34
  109.5 3.2 %weight_part.3 = (bf16[384,768]{1,0:T(8,128)(2,1)S(1)}, bf16[384,768]{1,0:T(8,128)(2,1)S(1)}, bf16[384,768]{1,0:T(8,128)(2,1)S(1)}, bf16[384,768]{1,0:T(8,128)(2,1)S(1)}) custom-call(s32[7]{0:T(128)S(1)} %stack.39.s, bf16[4,4,192,512]{3,2,1,0:T(8,128)(2,1)S(1)} %bitcast.21, bf16[4,4,192,512]{3,2,1,0:T(8,128)(2,1)S(1)} %bitcast.22, ...), custom_call_target="tpu_custom_call" | custom-call | flops 1 | bytes 1 | tf_op jit(solution)/shard_map/weight_part/pallas_call | solution.py:34
  115.8 2.2 %collective-permute-start.23 = (bf16[384,768]{1,0:T(8,128)(2,1)S(1)}, bf16[384,768]{1,0:T(8,128)(2,1)S(1)}, u32[]{:S(2)}, u32[]{:S(2)}) collective-permute-start(bf16[384,768]{1,0:T(8,128)(2,1)S(1)} %get-tuple-element.208), channel_id=1, source_target_pairs={{0,12},{4,8},{8,4},{12,0},{1,13},{5,9},{9,5},{13,1},{2,14},{6,10},... | collective-permute-start | bytes 1769480 | tf_op jit(solution)/shard_map/ppermute | solution.py:22
  117.9 8.4 %weight_part.4 = (bf16[768,768]{1,0:T(8,128)(2,1)S(1)}, bf16[768,768]{1,0:T(8,128)(2,1)S(1)}, bf16[768,768]{1,0:T(8,128)(2,1)S(1)}, bf16[768,768]{1,0:T(8,128)(2,1)S(1)}) custom-call(s32[7]{0:T(128)S(1)} %stack.39.s, bf16[4,4,192,512]{3,2,1,0:T(8,128)(2,1)S(1)} %bitcast.23, bf16[4,4,192,512]{3,2,1,0:T(8,128)(2,1)S(1)} %bitcast.24, ...), custom_call_target="tpu_custom_call" | custom-call | flops 1 | bytes 1 | tf_op jit(solution)/shard_map/weight_part/pallas_call | solution.py:34
  126.9 1.5 add_halves.2
  129.1 1.6 collective-permute-start.21
  130.8 1.5 add_halves.3
  133.0 1.7 collective-permute-start.25
  134.7 3.2 %weight_part.5 = (bf16[768,768]{1,0:T(8,128)(2,1)S(1)}, bf16[768,768]{1,0:T(8,128)(2,1)S(1)}) custom-call(s32[7]{0:T(128)S(1)} %stack.39.s, bf16[4,4,192,512]{3,2,1,0:T(8,128)(2,1)S(1)} %bitcast.25, bf16[4,4,192,512]{3,2,1,0:T(8,128)(2,1)S(1)} %bitcast.26, bf16[4,4,192,512]{3,2,1,0:T(8,128)(2,1)S(1)} %bitcast.31, bf16[4,4,192,512]{3,2,1,0:T(8,128)(2,1)S(1)} %bitcast.32, ...), custom_call_target="tpu_custom_call" | custom-call | flops 1 | bytes 1 | tf_op jit(solution)/shard_map/weight_part/pallas_call | solution.py:34
  137.8 14.6 %collective-permute-done.20.refs_1_ = bf16[768,768]{1,0:T(8,128)(2,1)S(1)} collective-permute-done((bf16[768,768]{1,0:T(8,128)(2,1)S(1)}, bf16[768,768]{1,0:T(8,128)(2,1)S(1)}, u32[]{:S(2)}, u32[]{:S(2)}) %collective-permute-start.20) | collective-permute-done | bytes 1179680 | tf_op jit(solution)/shard_map/ppermute | solution.py:22
  152.4 1.6 collective-permute-done.21.refs_2_
  154.0 1.7 collective-permute-done.24.refs_4_
  155.8 1.8 collective-permute-done.25.refs_5_
  157.5 1.4 cut_blocks.1
  159.0 1.8 collective-permute-start.27
  160.8 2.3 %collective-permute-start.28 = (bf16[192,768]{1,0:T(8,128)(2,1)S(1)}, bf16[192,768]{1,0:T(8,128)(2,1)S(1)}, u32[]{:S(2)}, u32[]{:S(2)}) collective-permute-start(bf16[192,768]{1,0:T(8,128)(2,1)S(1)} %get-tuple-element.224), channel_id=1, source_target_pairs={{0,8},{4,12},{8,0},{12,4},{1,9},{5,13},{9,1},{13,5},{2,10},{6,14},... | collective-permute-start | bytes 884744 | tf_op jit(solution)/shard_map/ppermute | solution.py:22
  163.6 2.0 %collective-permute-start.30 = (bf16[192,768]{1,0:T(8,128)(2,1)S(1)}, bf16[192,768]{1,0:T(8,128)(2,1)S(1)}, u32[]{:S(2)}, u32[]{:S(2)}) collective-permute-start(bf16[192,768]{1,0:T(8,128)(2,1)S(1)} %get-tuple-element.227), channel_id=1, source_target_pairs={{0,48},{16,32},{32,16},{48,0},{1,49},{17,33},{33,17},{49,1},{2,50}... | collective-permute-start | bytes 884744 | tf_op jit(solution)/shard_map/ppermute | solution.py:22
  165.7 2.0 %collective-permute-start.31 = (bf16[192,768]{1,0:T(8,128)(2,1)S(1)}, bf16[192,768]{1,0:T(8,128)(2,1)S(1)}, u32[]{:S(2)}, u32[]{:S(2)}) collective-permute-start(bf16[192,768]{1,0:T(8,128)(2,1)S(1)} %get-tuple-element.228), channel_id=1, source_target_pairs={{0,32},{16,48},{32,0},{48,16},{1,33},{17,49},{33,1},{49,17},{2,34}... | collective-permute-start | bytes 884744 | tf_op jit(solution)/shard_map/ppermute | solution.py:22
  167.7 2.5 %collective-permute-done.27.refs_2_ = bf16[192,768]{1,0:T(8,128)(2,1)S(1)} collective-permute-done((bf16[192,768]{1,0:T(8,128)(2,1)S(1)}, bf16[192,768]{1,0:T(8,128)(2,1)S(1)}, u32[]{:S(2)}, u32[]{:S(2)}) %collective-permute-start.27) | collective-permute-done | bytes 294944 | tf_op jit(solution)/shard_map/ppermute | solution.py:22
  170.2 4.5 %collective-permute-done.30.refs_6_ = bf16[192,768]{1,0:T(8,128)(2,1)S(1)} collective-permute-done((bf16[192,768]{1,0:T(8,128)(2,1)S(1)}, bf16[192,768]{1,0:T(8,128)(2,1)S(1)}, u32[]{:S(2)}, u32[]{:S(2)}) %collective-permute-start.30) | collective-permute-done | bytes 294944 | tf_op jit(solution)/shard_map/ppermute | solution.py:22
  176.7 7.2 %collective-permute-done.32.there_ref = bf16[2,96,768]{2,1,0:T(8,128)(2,1)S(1)} collective-permute-done((bf16[2,96,768]{2,1,0:T(8,128)(2,1)S(1)}, bf16[2,96,768]{2,1,0:T(8,128)(2,1)S(1)}, u32[]{:S(2)}, u32[]{:S(2)}) %collective-permute-start.32) | collective-permute-done | bytes 294944 | tf_op jit(solution)/shard_map/ppermute | solution.py:22
  183.9 1.6 finish.1
  (80 shorter events, 20.6 us)
Async XLA Ops:
  0.0 17.6 %collective-permute-start.2 = (bf16[512,768]{1,0:T(8,128)(2,1)}, bf16[512,768]{1,0:T(8,128)(2,1)}, u32[]{:S(2)}, u32[]{:S(2)}) collective-permute-start(bf16[512,768]{1,0:T(8,128)(2,1)} %refs_0_.3), channel_id=1, source_target_pairs={{0,1},{1,0},{2,3},{3,2},{4,5},{5,4},{6,7},{7,6},{8,9},{9,8},{10,11... | collective-permute-start | bytes 2359304 | tf_op jit(solution)/shard_map/ppermute | solution.py:22
  0.0 27.6 %collective-permute-start = (bf16[512,768]{1,0:T(8,128)(2,1)}, bf16[512,768]{1,0:T(8,128)(2,1)}, u32[]{:S(2)}, u32[]{:S(2)}) collective-permute-start(bf16[512,768]{1,0:T(8,128)(2,1)} %refs_0_.3), channel_id=1, source_target_pairs={{0,2},{2,0},{1,3},{3,1},{4,6},{6,4},{5,7},{7,5},{8,10},{10,8},{9,1... | collective-permute-start | bytes 2359304 | tf_op jit(solution)/shard_map/ppermute | solution.py:22
  2.0 25.6 %collective-permute-start.1 = (bf16[512,768]{1,0:T(8,128)(2,1)}, bf16[512,768]{1,0:T(8,128)(2,1)}, u32[]{:S(2)}, u32[]{:S(2)}) collective-permute-start(bf16[512,768]{1,0:T(8,128)(2,1)} %refs_0_.3), channel_id=1, source_target_pairs={{0,66},{2,64},{64,2},{66,0},{1,67},{3,65},{65,3},{67,1},{4,70},{6,... | collective-permute-start | bytes 2359304 | tf_op jit(solution)/shard_map/ppermute | solution.py:26
  20.3 7.4 %copy-start.8 = (bf16[512,768]{1,0:T(8,128)(2,1)S(1)}, bf16[512,768]{1,0:T(8,128)(2,1)}, u32[]{:S(2)}) copy-start(bf16[512,768]{1,0:T(8,128)(2,1)} %refs_0_.3) | copy-start | bytes 2359300
  27.6 9.6 %collective-permute-start.5 = (bf16[512,768]{1,0:T(8,128)(2,1)}, bf16[512,768]{1,0:T(8,128)(2,1)S(1)}, u32[]{:S(2)}, u32[]{:S(2)}) collective-permute-start(bf16[512,768]{1,0:T(8,128)(2,1)} %collective-permute-done.refs_0_), channel_id=1, source_target_pairs={{0,1},{1,0},{2,3},{3,2},{4,5},{5,4},{6,7},{7,6},{8,9},{9,8},{10,11... | collective-permute-start | bytes 2359304 | tf_op jit(solution)/shard_map/ppermute | solution.py:22
  27.7 21.8 %collective-permute-start.6 = (bf16[512,768]{1,0:T(8,128)(2,1)S(1)}, bf16[512,768]{1,0:T(8,128)(2,1)}, u32[]{:S(2)}, u32[]{:S(2)}) collective-permute-start(bf16[512,768]{1,0:T(8,128)(2,1)S(1)} %copy-done.8), channel_id=1, source_target_pairs={{0,64},{64,0},{1,65},{65,1},{2,66},{66,2},{3,67},{67,3},{4,68},{68... | collective-permute-start | bytes 2359304 | tf_op jit(solution)/shard_map/ppermute | solution.py:22
  29.0 20.5 %collective-permute-start.4 = (bf16[512,768]{1,0:T(8,128)(2,1)}, bf16[512,768]{1,0:T(8,128)(2,1)S(1)}, u32[]{:S(2)}, u32[]{:S(2)}) collective-permute-start(bf16[512,768]{1,0:T(8,128)(2,1)} %collective-permute-done.1.refs_0_.refs_2_), channel_id=1, source_target_pairs={{0,1},{1,0},{2,3},{3,2},{4,5},{5,4},{6,7},{7,6},{8,9},{9,8},{10,11... | collective-permute-start | bytes 2359304 | tf_op jit(solution)/shard_map/ppermute | solution.py:22
  29.0 20.5 %collective-permute-start.3 = (f32[8,512]{1,0:T(8,128)S(1)}, f32[8,512]{1,0:T(8,128)S(1)}, u32[]{:S(2)}, u32[]{:S(2)}) collective-permute-start(f32[8,512]{1,0:T(8,128)S(1)} %concatenate.6), channel_id=1, source_target_pairs={{0,64},{64,0},{1,65},{65,1},{2,66},{66,2},{3,67},{67,3},{4,68},{68... | collective-permute-start | bytes 49160 | tf_op jit(solution)/shard_map/ppermute | solution.py:22
  37.2 0.9 copy-start.9
  44.8 6.0 %copy-start = (bf16[3,512,512]{2,1,0:T(8,128)(2,1)}, bf16[3,512,512]{2,1,0:T(8,128)(2,1)S(1)}, u32[]{:S(2)}) copy-start(bf16[3,512,512]{2,1,0:T(8,128)(2,1)S(1)} %project.6.qkv_ref) | copy-start | bytes 4718596
  44.8 6.0 %copy-start.2 = (bf16[512,512]{1,0:T(8,128)(2,1)S(1)}, bf16[512,512]{1,0:T(8,128)(2,1)}, u32[]{:S(2)}) copy-start(bf16[512,512]{1,0:T(8,128)(2,1)} %get-tuple-element.231.og_ref) | copy-start | bytes 1572868
  49.6 5.9 %copy-start.10 = (bf16[512,768]{1,0:T(8,128)(2,1)}, bf16[512,768]{1,0:T(8,128)(2,1)S(1)}, u32[]{:S(2)}) copy-start(bf16[512,768]{1,0:T(8,128)(2,1)S(1)} %collective-permute-done.4.refs_0_.refs_3_) | copy-start | bytes 2359300
  49.6 6.0 %collective-permute-start.8 = (bf16[512,768]{1,0:T(8,128)(2,1)}, bf16[512,768]{1,0:T(8,128)(2,1)}, u32[]{:S(2)}, u32[]{:S(2)}) collective-permute-start(bf16[512,768]{1,0:T(8,128)(2,1)} %collective-permute-done.6.refs_1_.refs_0_), channel_id=1, source_target_pairs={{0,1},{1,0},{2,3},{3,2},{4,5},{5,4},{6,7},{7,6},{8,9},{9,8},{10,11... | collective-permute-start | bytes 2359304 | tf_op jit(solution)/shard_map/ppermute | solution.py:22
  49.7 16.2 %collective-permute-start.7 = (bf16[512,512]{1,0:T(8,128)(2,1)}, bf16[512,512]{1,0:T(8,128)(2,1)}, u32[]{:S(2)}, u32[]{:S(2)}) collective-permute-start(bf16[512,512]{1,0:T(8,128)(2,1)} %get-tuple-element.129), channel_id=1, source_target_pairs={{0,64},{64,0},{1,65},{65,1},{2,66},{66,2},{3,67},{67,3},{4,68},{68... | collective-permute-start | bytes 1572872 | tf_op jit(solution)/shard_map/ppermute | solution.py:22
  53.1 0.7 copy-start.4
  53.8 0.7 copy-start.6
  55.6 10.2 %copy-start.5 = (bf16[528,128]{1,0:T(8,128)(2,1)S(1)}, bf16[528,128]{1,0:T(8,128)(2,1)}, u32[]{:S(2)}) copy-start(bf16[528,128]{1,0:T(8,128)(2,1)} %copy-done.4) | copy-start | bytes 405508
  55.6 10.2 %copy-start.7 = (bf16[528,128]{1,0:T(8,128)(2,1)S(1)}, bf16[528,128]{1,0:T(8,128)(2,1)}, u32[]{:S(2)}) copy-start(bf16[528,128]{1,0:T(8,128)(2,1)} %copy-done.6) | copy-start | bytes 405508
  63.8 9.8 %copy-start.1 = (bf16[3,512,512]{2,1,0:T(8,128)(2,1)S(1)}, bf16[3,512,512]{2,1,0:T(8,128)(2,1)}, u32[]{:S(2)}) copy-start(bf16[3,512,512]{2,1,0:T(8,128)(2,1)} %copy-done) | copy-start | bytes 4718596
  63.8 9.8 %copy-start.3 = (bf16[512,512]{1,0:T(8,128)(2,1)S(1)}, bf16[512,512]{1,0:T(8,128)(2,1)}, u32[]{:S(2)}) copy-start(bf16[512,512]{1,0:T(8,128)(2,1)} %get-tuple-element.231.og_ref) | copy-start | bytes 1572868
  69.5 10.2 %collective-permute-start.10 = (bf16[528,128]{1,0:T(8,128)(2,1)S(1)}, bf16[528,128]{1,0:T(8,128)(2,1)S(1)}, u32[]{:S(2)}, u32[]{:S(2)}) collective-permute-start(bf16[528,128]{1,0:T(8,128)(2,1)S(1)} %get-tuple-element.147), channel_id=1, source_target_pairs={{0,12},{4,8},{8,4},{12,0},{1,13},{5,9},{9,5},{13,1},{2,14},{6,10},... | collective-permute-start | bytes 405512 | tf_op jit(solution)/shard_map/ppermute | solution.py:22
  72.5 7.8 %collective-permute-start.11 = (bf16[528,128]{1,0:T(8,128)(2,1)S(1)}, bf16[528,128]{1,0:T(8,128)(2,1)S(1)}, u32[]{:S(2)}, u32[]{:S(2)}) collective-permute-start(bf16[528,128]{1,0:T(8,128)(2,1)S(1)} %get-tuple-element.148), channel_id=1, source_target_pairs={{0,8},{4,12},{8,0},{12,4},{1,9},{5,13},{9,1},{13,5},{2,10},{6,14},... | collective-permute-start | bytes 405512 | tf_op jit(solution)/shard_map/ppermute | solution.py:22
  73.2 7.2 %collective-permute-start.9 = (bf16[528,128]{1,0:T(8,128)(2,1)S(1)}, bf16[528,128]{1,0:T(8,128)(2,1)S(1)}, u32[]{:S(2)}, u32[]{:S(2)}) collective-permute-start(bf16[528,128]{1,0:T(8,128)(2,1)S(1)} %get-tuple-element.146), channel_id=1, source_target_pairs={{0,4},{4,0},{8,12},{12,8},{1,5},{5,1},{9,13},{13,9},{2,6},{6,2},{1... | collective-permute-start | bytes 405512 | tf_op jit(solution)/shard_map/ppermute | solution.py:22
  81.1 8.4 %collective-permute-start.12 = (bf16[528,128]{1,0:T(8,128)(2,1)S(1)}, bf16[528,128]{1,0:T(8,128)(2,1)S(1)}, u32[]{:S(2)}, u32[]{:S(2)}) collective-permute-start(bf16[528,128]{1,0:T(8,128)(2,1)S(1)} %get-tuple-element.155.a), channel_id=1, source_target_pairs={{0,16},{16,0},{32,48},{48,32},{1,17},{17,1},{33,49},{49,33},{2,18}... | collective-permute-start | bytes 405512 | tf_op jit(solution)/shard_map/ppermute | solution.py:22
  82.7 7.1 %collective-permute-start.13 = (bf16[528,128]{1,0:T(8,128)(2,1)S(1)}, bf16[528,128]{1,0:T(8,128)(2,1)S(1)}, u32[]{:S(2)}, u32[]{:S(2)}) collective-permute-start(bf16[528,128]{1,0:T(8,128)(2,1)S(1)} %get-tuple-element.155.a), channel_id=1, source_target_pairs={{0,48},{16,32},{32,16},{48,0},{1,49},{17,33},{33,17},{49,1},{2,50}... | collective-permute-start | bytes 405512 | tf_op jit(solution)/shard_map/ppermute | solution.py:22
  84.7 6.5 %collective-permute-start.14 = (bf16[528,128]{1,0:T(8,128)(2,1)S(1)}, bf16[528,128]{1,0:T(8,128)(2,1)S(1)}, u32[]{:S(2)}, u32[]{:S(2)}) collective-permute-start(bf16[528,128]{1,0:T(8,128)(2,1)S(1)} %get-tuple-element.155.a), channel_id=1, source_target_pairs={{0,32},{16,48},{32,0},{48,16},{1,33},{17,49},{33,1},{49,17},{2,34}... | collective-permute-start | bytes 405512 | tf_op jit(solution)/shard_map/ppermute | solution.py:22
  92.3 12.1 %collective-permute-start.15 = (bf16[512,128]{1,0:T(8,128)(2,1)S(1)}, bf16[512,128]{1,0:T(8,128)(2,1)S(1)}, u32[]{:S(2)}, u32[]{:S(2)}) collective-permute-start(bf16[512,128]{1,0:T(8,128)(2,1)S(1)} %get-tuple-element.166), channel_id=1, source_target_pairs={{0,4},{4,0},{8,12},{12,8},{1,5},{5,1},{9,13},{13,9},{2,6},{6,2},{1... | collective-permute-start | bytes 393224 | tf_op jit(solution)/shard_map/ppermute | solution.py:22
  93.5 10.9 %collective-permute-start.16 = (bf16[512,128]{1,0:T(8,128)(2,1)S(1)}, bf16[512,128]{1,0:T(8,128)(2,1)S(1)}, u32[]{:S(2)}, u32[]{:S(2)}) collective-permute-start(bf16[512,128]{1,0:T(8,128)(2,1)S(1)} %get-tuple-element.167), channel_id=1, source_target_pairs={{0,12},{4,8},{8,4},{12,0},{1,13},{5,9},{9,5},{13,1},{2,14},{6,10},... | collective-permute-start | bytes 393224 | tf_op jit(solution)/shard_map/ppermute | solution.py:22
  95.7 8.7 %collective-permute-start.17 = (bf16[512,128]{1,0:T(8,128)(2,1)S(1)}, bf16[512,128]{1,0:T(8,128)(2,1)S(1)}, u32[]{:S(2)}, u32[]{:S(2)}) collective-permute-start(bf16[512,128]{1,0:T(8,128)(2,1)S(1)} %get-tuple-element.168), channel_id=1, source_target_pairs={{0,8},{4,12},{8,0},{12,4},{1,9},{5,13},{9,1},{13,5},{2,10},{6,14},... | collective-permute-start | bytes 393224 | tf_op jit(solution)/shard_map/ppermute | solution.py:22
  112.7 13.7 %collective-permute-start.18 = (bf16[384,768]{1,0:T(8,128)(2,1)S(1)}, bf16[384,768]{1,0:T(8,128)(2,1)S(1)}, u32[]{:S(2)}, u32[]{:S(2)}) collective-permute-start(bf16[384,768]{1,0:T(8,128)(2,1)S(1)} %get-tuple-element.194), channel_id=1, source_target_pairs={{0,16},{16,0},{32,48},{48,32},{1,17},{17,1},{33,49},{49,33},{2,18}... | collective-permute-start | bytes 1769480 | tf_op jit(solution)/shard_map/ppermute | solution.py:22
  113.3 13.5 %collective-permute-start.19 = (bf16[384,768]{1,0:T(8,128)(2,1)S(1)}, bf16[384,768]{1,0:T(8,128)(2,1)S(1)}, u32[]{:S(2)}, u32[]{:S(2)}) collective-permute-start(bf16[384,768]{1,0:T(8,128)(2,1)S(1)} %get-tuple-element.198), channel_id=1, source_target_pairs={{0,48},{16,32},{32,16},{48,0},{1,49},{17,33},{33,17},{49,1},{2,50}... | collective-permute-start | bytes 1769480 | tf_op jit(solution)/shard_map/ppermute | solution.py:22
  114.5 14.6 %collective-permute-start.22 = (bf16[384,768]{1,0:T(8,128)(2,1)S(1)}, bf16[384,768]{1,0:T(8,128)(2,1)S(1)}, u32[]{:S(2)}, u32[]{:S(2)}) collective-permute-start(bf16[384,768]{1,0:T(8,128)(2,1)S(1)} %get-tuple-element.207), channel_id=1, source_target_pairs={{0,4},{4,0},{8,12},{12,8},{1,5},{5,1},{9,13},{13,9},{2,6},{6,2},{1... | collective-permute-start | bytes 1769480 | tf_op jit(solution)/shard_map/ppermute | solution.py:22
  115.8 13.4 %collective-permute-start.23 = (bf16[384,768]{1,0:T(8,128)(2,1)S(1)}, bf16[384,768]{1,0:T(8,128)(2,1)S(1)}, u32[]{:S(2)}, u32[]{:S(2)}) collective-permute-start(bf16[384,768]{1,0:T(8,128)(2,1)S(1)} %get-tuple-element.208), channel_id=1, source_target_pairs={{0,12},{4,8},{8,4},{12,0},{1,13},{5,9},{9,5},{13,1},{2,14},{6,10},... | collective-permute-start | bytes 1769480 | tf_op jit(solution)/shard_map/ppermute | solution.py:22
  128.3 24.1 %collective-permute-start.20 = (bf16[768,768]{1,0:T(8,128)(2,1)S(1)}, bf16[768,768]{1,0:T(8,128)(2,1)S(1)}, u32[]{:S(2)}, u32[]{:S(2)}) collective-permute-start(bf16[768,768]{1,0:T(8,128)(2,1)S(1)} %get-tuple-element.203), channel_id=1, source_target_pairs={{0,16},{16,0},{32,48},{48,32},{1,17},{17,1},{33,49},{49,33},{2,18}... | collective-permute-start | bytes 3538952 | tf_op jit(solution)/shard_map/ppermute | solution.py:22
  129.1 24.9 %collective-permute-start.21 = (bf16[768,768]{1,0:T(8,128)(2,1)S(1)}, bf16[768,768]{1,0:T(8,128)(2,1)S(1)}, u32[]{:S(2)}, u32[]{:S(2)}) collective-permute-start(bf16[768,768]{1,0:T(8,128)(2,1)S(1)} %get-tuple-element.204), channel_id=1, source_target_pairs={{0,48},{16,32},{32,16},{48,0},{1,49},{17,33},{33,17},{49,1},{2,50}... | collective-permute-start | bytes 3538952 | tf_op jit(solution)/shard_map/ppermute | solution.py:22
  132.2 23.6 %collective-permute-start.24 = (bf16[768,768]{1,0:T(8,128)(2,1)S(1)}, bf16[768,768]{1,0:T(8,128)(2,1)S(1)}, u32[]{:S(2)}, u32[]{:S(2)}) collective-permute-start(bf16[768,768]{1,0:T(8,128)(2,1)S(1)} %get-tuple-element.211), channel_id=1, source_target_pairs={{0,4},{4,0},{8,12},{12,8},{1,5},{5,1},{9,13},{13,9},{2,6},{6,2},{1... | collective-permute-start | bytes 3538952 | tf_op jit(solution)/shard_map/ppermute | solution.py:22
  133.0 24.6 %collective-permute-start.25 = (bf16[768,768]{1,0:T(8,128)(2,1)S(1)}, bf16[768,768]{1,0:T(8,128)(2,1)S(1)}, u32[]{:S(2)}, u32[]{:S(2)}) collective-permute-start(bf16[768,768]{1,0:T(8,128)(2,1)S(1)} %get-tuple-element.220), channel_id=1, source_target_pairs={{0,12},{4,8},{8,4},{12,0},{1,13},{5,9},{9,5},{13,1},{2,14},{6,10},... | collective-permute-start | bytes 3538952 | tf_op jit(solution)/shard_map/ppermute | solution.py:22
  158.9 6.8 %collective-permute-start.26 = (bf16[192,768]{1,0:T(8,128)(2,1)S(1)}, bf16[192,768]{1,0:T(8,128)(2,1)S(1)}, u32[]{:S(2)}, u32[]{:S(2)}) collective-permute-start(bf16[192,768]{1,0:T(8,128)(2,1)S(1)} %get-tuple-element.222), channel_id=1, source_target_pairs={{0,4},{4,0},{8,12},{12,8},{1,5},{5,1},{9,13},{13,9},{2,6},{6,2},{1... | collective-permute-start | bytes 884744 | tf_op jit(solution)/shard_map/ppermute | solution.py:22
  159.0 11.2 %collective-permute-start.27 = (bf16[192,768]{1,0:T(8,128)(2,1)S(1)}, bf16[192,768]{1,0:T(8,128)(2,1)S(1)}, u32[]{:S(2)}, u32[]{:S(2)}) collective-permute-start(bf16[192,768]{1,0:T(8,128)(2,1)S(1)} %get-tuple-element.223), channel_id=1, source_target_pairs={{0,12},{4,8},{8,4},{12,0},{1,13},{5,9},{9,5},{13,1},{2,14},{6,10},... | collective-permute-start | bytes 884744 | tf_op jit(solution)/shard_map/ppermute | solution.py:22
  160.8 9.4 %collective-permute-start.28 = (bf16[192,768]{1,0:T(8,128)(2,1)S(1)}, bf16[192,768]{1,0:T(8,128)(2,1)S(1)}, u32[]{:S(2)}, u32[]{:S(2)}) collective-permute-start(bf16[192,768]{1,0:T(8,128)(2,1)S(1)} %get-tuple-element.224), channel_id=1, source_target_pairs={{0,8},{4,12},{8,0},{12,4},{1,9},{5,13},{9,1},{13,5},{2,10},{6,14},... | collective-permute-start | bytes 884744 | tf_op jit(solution)/shard_map/ppermute | solution.py:22
  163.1 7.1 %collective-permute-start.29 = (bf16[192,768]{1,0:T(8,128)(2,1)S(1)}, bf16[192,768]{1,0:T(8,128)(2,1)S(1)}, u32[]{:S(2)}, u32[]{:S(2)}) collective-permute-start(bf16[192,768]{1,0:T(8,128)(2,1)S(1)} %get-tuple-element.226), channel_id=1, source_target_pairs={{0,16},{16,0},{32,48},{48,32},{1,17},{17,1},{33,49},{49,33},{2,18}... | collective-permute-start | bytes 884744 | tf_op jit(solution)/shard_map/ppermute | solution.py:22
  163.6 11.1 %collective-permute-start.30 = (bf16[192,768]{1,0:T(8,128)(2,1)S(1)}, bf16[192,768]{1,0:T(8,128)(2,1)S(1)}, u32[]{:S(2)}, u32[]{:S(2)}) collective-permute-start(bf16[192,768]{1,0:T(8,128)(2,1)S(1)} %get-tuple-element.227), channel_id=1, source_target_pairs={{0,48},{16,32},{32,16},{48,0},{1,49},{17,33},{33,17},{49,1},{2,50}... | collective-permute-start | bytes 884744 | tf_op jit(solution)/shard_map/ppermute | solution.py:22
  165.7 9.0 %collective-permute-start.31 = (bf16[192,768]{1,0:T(8,128)(2,1)S(1)}, bf16[192,768]{1,0:T(8,128)(2,1)S(1)}, u32[]{:S(2)}, u32[]{:S(2)}) collective-permute-start(bf16[192,768]{1,0:T(8,128)(2,1)S(1)} %get-tuple-element.228), channel_id=1, source_target_pairs={{0,32},{16,48},{32,0},{48,16},{1,33},{17,49},{33,1},{49,17},{2,34}... | collective-permute-start | bytes 884744 | tf_op jit(solution)/shard_map/ppermute | solution.py:22
  175.6 8.3 %collective-permute-start.32 = (bf16[2,96,768]{2,1,0:T(8,128)(2,1)S(1)}, bf16[2,96,768]{2,1,0:T(8,128)(2,1)S(1)}, u32[]{:S(2)}, u32[]{:S(2)}) collective-permute-start(bf16[2,96,768]{2,1,0:T(8,128)(2,1)S(1)} %get-tuple-element.230), channel_id=1, source_target_pairs={{0,64},{64,0},{1,65},{65,1},{2,66},{66,2},{3,67},{67,3},{4,68},{68... | collective-permute-start | bytes 884744 | tf_op jit(solution)/shard_map/ppermute | solution.py:22

commit v5 on v4

--- a/solution.py
+++ b/solution.py
@@ -9,6 +9,7 @@
 F32 = jnp.float32
 BF16 = jnp.bfloat16
 HEAD = 128
+PROJ = 24
 Z, X, Y, ZL, CO, TEN, LEN = range(7)
 AB_T = (((1,), (1,)), ((), ()))
 A_TB = (((0,), (0,)), ((), ()))
@@ -50,10 +51,6 @@
     )(table, *operands)
 
 
-def in_hbm(xs):
-    return [pltpu.with_memory_space_constraint(x, pltpu.HBM) for x in xs]
-
-
 def shape(dims, kind=BF16):
     return jax.ShapeDtypeStruct(dims, kind)
 
@@ -67,7 +64,7 @@
     n, counts = len(shards), [len(x) for x in shards]
     flat = [part for x in shards for part in x]
     tokens, width = sum(part.shape[0] for part in shards[0]), flat[0].shape[1]
-    cols = weight.shape[2]
+    cols = weight.shape[2] // 2
 
     def body(s, *refs):
         out, rest = refs[-1], list(refs)
@@ -87,14 +84,14 @@
     in_specs = [whole(x) for x in flat]
     for flip in flips:
         in_specs.append(
-            pl.BlockSpec((1, width, cols), lambda g, s, flip=flip: (g, s[TEN] ^ flip, 0))
+            pl.BlockSpec((1, width, cols), lambda g, s, flip=flip: (g, s[TEN] ^ flip, s[Z]))
         )
     operands = [*flat, *([weight] * n)]
     if partial is not None:
         in_specs.append(tile)
         operands.append(partial)
-    out = shape((3, tokens, cols)) if last else pltpu.HBM((3, tokens, cols), F32)
-    return call("project", body, table, (3,), in_hbm(operands), in_specs, out, tile, 24)
+    out = shape((3, tokens, cols), BF16 if last else F32)
+    return call("project", body, table, (3,), operands, in_specs, out, tile, PROJ)
 
 
 def shard_states(table, qkv, out_grad, cumul, which, so_far):
@@ -384,16 +381,18 @@
 
 
 def turn(table, shards, base, so_far):
-    tokens, width = shards[0].shape
+    flat = [part for x in shards for part in x]
+    tokens, width = sum(part.shape[0] for part in shards[0]), flat[0].shape[1]
     n, rows = len(shards), 4 * width // 32
 
     def body(s, *refs):
-        out = refs[-1]
-        for k in range(n):
+        out, at = refs[-1], 0
+        for k, x in enumerate(shards):
+            mine, at = refs[at : at + len(x)], at + len(x)
 
             @pl.when(pl.program_id(0) == k)
-            def _(k=k):
-                out[...] = refs[k][...].T.reshape(out.shape)
+            def _(mine=mine):
+                out[...] = joined(mine).T.reshape(out.shape)
 
     def place(i, s):
         i = s[TEN] ^ (base + i)
@@ -401,7 +400,7 @@
 
     out = shape((16, 2, rows, tokens))
     spec = pl.BlockSpec((8, 1, rows, tokens), place)
-    operands, in_specs = in_hbm(shards), [whole(x) for x in shards]
+    operands, in_specs = list(flat), [whole(x) for x in flat]
     if so_far is not None:
         operands.append(so_far)
         in_specs.append(pl.BlockSpec(memory_space=pl.ANY))
@@ -415,7 +414,7 @@
         out,
         spec,
         12,
-        alias=None if so_far is None else {n + 1: 0},
+        alias=None if so_far is None else {len(flat) + 1: 0},
     )
 
 
@@ -567,12 +566,13 @@
     here_z = index[0]
     fixed = [*index, index[3] * 2 + index[4]]
     table = jnp.stack([*fixed, lengths[0]]).astype(jnp.int32)
-    weight = jnp.transpose(qkv_weight, (1, 0, 2))
+    weight = pltpu.with_memory_space_constraint(jnp.transpose(qkv_weight, (1, 0, 2)), pltpu.HBM)
     width = per * HEAD
-    weight = lax.dynamic_slice_in_dim(weight, here_z * width, width, axis=2)
-
-    near = send(activations, "zl", 1)
-    side = across(activations)
+
+    half = tokens // 2
+    rows = [activations[:half], activations[half:]]
+    near = [send(x, "zl", 1) for x in rows]
+    side = [across(x) for x in rows]
     core = send(activations, "co", 1)
 
     live = (jnp.arange(tokens, dtype=jnp.int32) < lengths[0]).astype(F32)
@@ -583,25 +583,25 @@
     og_other = lax.dynamic_slice_in_dim(out_grad, (1 - here_z) * width, width, axis=1)
 
     acc_own = project(table, [[activations], [core]], (0, 1), weight, None, False)
-    turned = turn(table, [activations, core], 0, None)
+    turned = turn(table, [[activations], [core]], 0, None)
     near, side, acc_own, note, og_other, turned = tied((near, side, acc_own, note, og_other, turned))
     note = send(note, "c0", 1)
-    near_core = send(near, "co", 1)
-    side_core = send(side, "co", 1)
-    far = send(tied((activations, near, side))[0], "c0", 1)
-    acc_pair = project(table, [[side]], (2,), weight, None, False)
-    near_core, acc_pair = tied((near_core, acc_pair))
-    qkv_own = project(table, [[near], [near_core]], (2, 3), weight, acc_own, True)
-    turned = [turn(table, tied(([near, near_core], qkv_own))[0], 2, turned)]
-    note, side_core, qkv_own, far, turned = tied((note, side_core, qkv_own, far, turned))
+    far = [send(side[0], "zl", 1), across(near[1])]
+    near_core = [send(x, "co", 1) for x in near]
+    side_core = [send(x, "co", 1) for x in side]
+    qkv_own = project(table, [near, near_core], (2, 3), weight, acc_own, True)
+    side_core, qkv_own = tied((side_core, qkv_own))
+    acc_pair = project(table, [side, side_core], (2, 3), weight, None, False)
+    note, far, acc_pair = tied((note, far, acc_pair))
     cumul = jnp.concatenate([lax.dynamic_slice_in_dim(cumul, here_z * per, per), note[:per]])
     table_pair = jnp.stack([*fixed, note[per, 0].astype(jnp.int32)]).astype(jnp.int32)
-    far_core = send(far, "co", 1)
+    far_core = [send(x, "co", 1) for x in far]
     og_pair = send(tied((og_other, far))[0], "c0", 1)
     to_y = shard_states(table, qkv_own, og_own, cumul, 0, None)
     far_core, to_y = tied((far_core, to_y))
-    qkv_pair = project(table_pair, [[side_core], [far], [far_core]], (3, 0, 1), weight, acc_pair, True)
-    og_pair, qkv_pair = tied((og_pair, qkv_pair))
+    qkv_pair = project(table_pair, [far, far_core], (0, 1), weight, acc_pair, True)
+    turned = [turn(table, tied(([near, near_core], qkv_pair))[0], 2, turned)]
+    og_pair, qkv_pair, turned = tied((og_pair, qkv_pair, turned))
 
     to_y = shard_states(table, qkv_pair, og_pair, cumul, 1, to_y)
     at_y = [send(to_y[r], "c2", r) for r in (1, 3, 2)]

time: 186 us -> 188 us (1.011)
  Pallas kernels: 85.4 us -> 77.5 us
  starting transfers between devices: 42.1 us -> 45.8 us
  local copies, waits for them, and re-layouts: 13.3 us -> 16.5 us
  waiting for transfers between devices: 41.1 us -> 44.1 us
    unnamed x22 -> x70, local copies, waits for them, and re-layouts: 2.24 us -> 10.6 us
    pallas_call x24, Pallas kernels: 85.4 us -> 77.5 us  [call(): pl.pallas_call(body, grid_spec=pltpu.PrefetchScalarGridSpec(num_scalar_pr...]
    dynamic_slice x1 -> x0, local copies, waits for them, and re-layouts: 7.94 us -> none  [device_part(): weight = lax.dynamic_slice_in_dim(weight, here_z * width, width, axis=2)]
    ppermute x1 -> x3, starting transfers between devices: 2.52 us -> 6.13 us  [across(): return lax.ppermute(x, ('c0', 'zl'), [(0, 3), (1, 2), (2, 1), (3, 0)])]
    slice x1 -> x2, local copies, waits for them, and re-layouts: 0.16 us -> 2.39 us  [the longest x1 2.23 us: device_part(): rows = [activations[:half], activations[half:]]]
    ppermute x32 -> x36, waiting for transfers between devices: 41.1 us -> 42.4 us  [send(): lax.ppermute(x, axis, [(i, i ^ by) for i in range(lax.axis_size(axis))])]
    ppermute x32 -> x36, starting transfers between devices: 39.6 us -> 39.7 us  [send(): lax.ppermute(x, axis, [(i, i ^ by) for i in range(lax.axis_size(axis))])]
  transfers between devices with their start and end apart: 33 -> 39, of which waited for: 14 -> 16; matrix products, arithmetic and copies ran while one was open for 7% -> 3% of each run, Pallas kernels for 37% -> 32%
where the time goes in v5:
time: 188 us; the launch traced here: 187 us
  Pallas kernels  77.5 us (41%)
  starting transfers between devices  45.8 us (24%)
  waiting for transfers between devices  44.1 us (23%)
  local copies, waits for them, and re-layouts  16.5 us (9%)
  between operations  1.92 us (1%)
    pallas_call x24, Pallas kernels, call(): pl.pallas_call(body, grid_spec=pltpu.PrefetchScalarGridSpec(num_scalar_pr...  77.5 us
    ppermute x36, waiting for transfers between devices, send(): lax.ppermute(x, axis, [(i, i ^ by) for i in range(lax.axis_size(axis))])  42.4 us
    ppermute x36, starting transfers between devices, send(): lax.ppermute(x, axis, [(i, i ^ by) for i in range(lax.axis_size(axis))])  39.7 us
    unnamed x70, local copies, waits for them, and re-layouts  10.6 us
    ppermute x3, starting transfers between devices, across(): return lax.ppermute(x, ('c0', 'zl'), [(0, 3), (1, 2), (2, 1), (3, 0)])  6.13 us
  transfers between devices with their start and end apart: 39, of which 16 were waited for; matrix products, arithmetic and copies ran while one was open for 3% of the time, Pallas kernels for 32%

profile of v5, /device:TPU:0, one launch (start us, length us, event | category | flops | bytes accessed | tf_op | source)
XLA Modules:
  0.0 187.1 jit_solution(11681702967273370292)
XLA Ops:
  0.0 2.2 %fusion.1 = (bf16[256,768]{1,0:T(8,128)(2,1)}, bf16[256,768]{1,0:T(8,128)(2,1)}) fusion(bf16[512,768]{1,0:T(8,128)(2,1)} %refs_0_.3), kind=kLoop, calls=%fused_computation.10 | loop fusion | bytes 1572864 | tf_op jit(solution)/shard_map/slice | solution.py:573
  2.2 4.1 %collective-permute-start.3 = (bf16[256,768]{1,0:T(8,128)(2,1)}, bf16[256,768]{1,0:T(8,128)(2,1)}, u32[]{:S(2)}, u32[]{:S(2)}) collective-permute-start(bf16[256,768]{1,0:T(8,128)(2,1)} %get-tuple-element.251), channel_id=1, source_target_pairs={{0,66},{2,64},{64,2},{66,0},{1,67},{3,65},{65,3},{67,1},{4,70},{6,... | collective-permute-start | bytes 1179656 | tf_op jit(solution)/shard_map/ppermute | solution.py:27
  6.9 1.5 collective-permute-start
  15.9 1.3 turn.3.refs_4_
  17.2 5.3 %project.4.refs_6_ = f32[3,512,512]{2,1,0:T(8,128)S(1)} custom-call(s32[7]{0:T(128)S(1)} %stack.39.s, bf16[512,768]{1,0:T(8,128)(2,1)S(1)} %copy-done.6, bf16[512,768]{1,0:T(8,128)(2,1)S(1)} %copy-done.10, bf16[3,3072,1024]{2,1,0:T(8,128)(2,1)} %bitcast.32, bf16[3,3072,1024]{2,1,0:T(8,128)(2,1)} %bitcast.33), custom_call_target="tpu_custom_call" | custom-call | flops 1 | bytes 1 | tf_op jit(solution)/shard_map/project/pallas_call | solution.py:35
  22.5 1.7 collective-permute-done.2.refs_0_.refs_4_
  24.2 1.5 collective-permute-done.refs_0_
  28.1 1.5 collective-permute-start.7
  30.9 5.4 %project.5.qkv_ref = bf16[3,512,512]{2,1,0:T(8,128)(2,1)S(1)} custom-call(s32[7]{0:T(128)S(1)} %stack.39.s, bf16[256,768]{1,0:T(8,128)(2,1)} %collective-permute-done.refs_0_, bf16[256,768]{1,0:T(8,128)(2,1)S(1)} %collective-permute-done.1.refs_1_, bf16[256,768]{1,0:T(8,128)(2,1)S(1)} %collective-permute-done.10.refs_2_, ...), custom_call_target="tpu_custom_call" | custom-call | flops 1 | bytes 1 | tf_op jit(solution)/shard_map/project/pallas_call | solution.py:35
  36.4 5.7 %project.6.refs_6_ = f32[3,512,512]{2,1,0:T(8,128)S(1)} custom-call(s32[7]{0:T(128)S(1)} %stack.39.s, bf16[256,768]{1,0:T(8,128)(2,1)} %collective-permute-done.2.refs_0_.refs_4_, bf16[256,768]{1,0:T(8,128)(2,1)} %collective-permute-done.3.refs_1_.refs_5_, bf16[256,768]{1,0:T(8,128)(2,1)S(1)} %collective-permute-done.8.refs_2_.refs_6_, ...), custom_call_target="tpu_custom_call" | custom-call | flops 1 | bytes 1 | tf_op jit(solution)/shard_map/project/pallas_call | solution.py:35
  42.1 1.6 copy-done.2
  43.8 2.4 %collective-permute-start.12 = (bf16[512,512]{1,0:T(8,128)(2,1)}, bf16[512,512]{1,0:T(8,128)(2,1)}, u32[]{:S(2)}, u32[]{:S(2)}) collective-permute-start(bf16[512,512]{1,0:T(8,128)(2,1)} %get-tuple-element.138), channel_id=1, source_target_pairs={{0,64},{64,0},{1,65},{65,1},{2,66},{66,2},{3,67},{67,3},{4,68},{68... | collective-permute-start | bytes 1572872 | tf_op jit(solution)/shard_map/ppermute | solution.py:23
  47.4 2.3 %shard_states.2 = (bf16[528,128]{1,0:T(8,128)(2,1)S(1)}, bf16[528,128]{1,0:T(8,128)(2,1)S(1)}, bf16[528,128]{1,0:T(8,128)(2,1)S(1)}, bf16[528,128]{1,0:T(8,128)(2,1)S(1)}) custom-call(s32[7]{0:T(128)S(1)} %copy-done.20, bf16[3,512,512]{2,1,0:T(8,128)(2,1)S(1)} %project.5.qkv_ref, bf16[512,512]{1,0:T(8,128)(2,1)S(1)} %get-tuple-element.249.og_ref, ...), custom_call_target="tpu_custom_call" | custom-call | flops 1 | bytes 1 | tf_op jit(solution)/shard_map/shard_states/pallas_call | solution.py:35
  54.2 1.9 %copy-done.3 = f32[3,512,512]{2,1,0:T(8,128)S(1)} copy-done((f32[3,512,512]{2,1,0:T(8,128)S(1)}, f32[3,512,512]{2,1,0:T(8,128)}, u32[]{:S(2)}) %copy-start.3) | copy-done | bytes 3145752
  56.8 5.8 %project.7.qkv_ref = bf16[3,512,512]{2,1,0:T(8,128)(2,1)S(1)} custom-call(s32[7]{0:T(128)S(1)} %copy-done.30, bf16[256,768]{1,0:T(8,128)(2,1)} %collective-permute-done.6.refs_0_, bf16[256,768]{1,0:T(8,128)(2,1)} %collective-permute-done.7.refs_1_, bf16[256,768]{1,0:T(8,128)(2,1)} %collective-permute-done.13.refs_2_, ...), custom_call_target="tpu_custom_call" | custom-call | flops 1 | bytes 1 | tf_op jit(solution)/shard_map/project/pallas_call | solution.py:35
  62.6 2.3 %turn.4 = bf16[16,2,96,512]{3,2,1,0:T(8,128)(2,1)S(1)} custom-call(s32[7]{0:T(128)S(1)} %copy-done.21, bf16[256,768]{1,0:T(8,128)(2,1)} %collective-permute-done.refs_0_, bf16[256,768]{1,0:T(8,128)(2,1)S(1)} %collective-permute-done.1.refs_1_, bf16[256,768]{1,0:T(8,128)(2,1)S(1)} %copy-done.12, ...), custom_call_target="tpu_custom_call", output_to_operand_aliasing={{}: (5, {})} | custom-call | flops 1 | bytes 1 | tf_op jit(solution)/shard_map/turn/pallas_call | solution.py:35
  65.0 3.6 %shard_states.3 = (bf16[528,128]{1,0:T(8,128)(2,1)S(1)}, bf16[528,128]{1,0:T(8,128)(2,1)S(1)}, bf16[528,128]{1,0:T(8,128)(2,1)S(1)}, bf16[528,128]{1,0:T(8,128)(2,1)S(1)}) custom-call(s32[7]{0:T(128)S(1)} %copy-done.21, bf16[3,512,512]{2,1,0:T(8,128)(2,1)S(1)} %project.7.qkv_ref, bf16[512,512]{1,0:T(8,128)(2,1)} %collective-permute-done.12.og_ref, ...), custom_call_target="tpu_custom_call" | custom-call | flops 1 | bytes 1 | tf_op jit(solution)/shard_map/shard_states/pallas_call | solution.py:35
  68.6 1.7 collective-permute-start.15
  70.3 2.2 %collective-permute-start.16 = (bf16[528,128]{1,0:T(8,128)(2,1)S(1)}, bf16[528,128]{1,0:T(8,128)(2,1)S(1)}, u32[]{:S(2)}, u32[]{:S(2)}) collective-permute-start(bf16[528,128]{1,0:T(8,128)(2,1)S(1)} %get-tuple-element.161), channel_id=1, source_target_pairs={{0,12},{4,8},{8,4},{12,0},{1,13},{5,9},{9,5},{13,1},{2,14},{6,10},... | collective-permute-start | bytes 405512 | tf_op jit(solution)/shard_map/ppermute | solution.py:23
  73.2 5.9 %local_grads.3 = (bf16[3,512,512]{2,1,0:T(8,128)(2,1)S(1)}, bf16[3,512,512]{2,1,0:T(8,128)(2,1)S(1)}) custom-call(s32[7]{0:T(128)S(1)} %copy-done.21, bf16[3,512,512]{2,1,0:T(8,128)(2,1)S(1)} %copy-done.1, bf16[512,512]{1,0:T(8,128)(2,1)S(1)} %copy-done.8, f32[8,512]{1,0:T(8,128)S(1)} %pad_maximum_fusion.cum_ref), custom_call_target="tpu_custom_call" | custom-call | flops 1 | bytes 1 | tf_op jit(solution)/shard_map/local_grads/pallas_call | solution.py:35
  80.3 3.1 %collective-permute-start.20 = (bf16[528,128]{1,0:T(8,128)(2,1)S(1)}, bf16[528,128]{1,0:T(8,128)(2,1)S(1)}, u32[]{:S(2)}, u32[]{:S(2)}) collective-permute-start(bf16[528,128]{1,0:T(8,128)(2,1)S(1)} %get-tuple-element.169.a), channel_id=1, source_target_pairs={{0,32},{16,48},{32,0},{48,16},{1,33},{17,49},{33,1},{49,17},{2,34}... | collective-permute-start | bytes 405512 | tf_op jit(solution)/shard_map/ppermute | solution.py:23
  84.6 4.0 %local_grads.4 = (bf16[3,512,512]{2,1,0:T(8,128)(2,1)S(1)}, bf16[3,512,512]{2,1,0:T(8,128)(2,1)S(1)}) custom-call(s32[7]{0:T(128)S(1)} %copy-done.30, bf16[3,512,512]{2,1,0:T(8,128)(2,1)S(1)} %project.7.qkv_ref, bf16[512,512]{1,0:T(8,128)(2,1)} %collective-permute-done.12.og_ref, f32[8,512]{1,0:T(8,128)S(1)} %pad_maximum_fusion.cum_ref), custom_call_target="tpu_custom_call" | custom-call | flops 1 | bytes 1 | tf_op jit(solution)/shard_map/local_grads/pallas_call | solution.py:35
  91.6 2.2 %collective-permute-start.22 = (bf16[512,128]{1,0:T(8,128)(2,1)S(1)}, bf16[512,128]{1,0:T(8,128)(2,1)S(1)}, u32[]{:S(2)}, u32[]{:S(2)}) collective-permute-start(bf16[512,128]{1,0:T(8,128)(2,1)S(1)} %get-tuple-element.181), channel_id=1, source_target_pairs={{0,12},{4,8},{8,4},{12,0},{1,13},{5,9},{9,5},{13,1},{2,14},{6,10},... | collective-permute-start | bytes 393224 | tf_op jit(solution)/shard_map/ppermute | solution.py:23
  94.9 4.0 %local_grads.5 = (bf16[3,512,512]{2,1,0:T(8,128)(2,1)S(1)}, bf16[3,512,512]{2,1,0:T(8,128)(2,1)S(1)}) custom-call(s32[7]{0:T(128)S(1)} %copy-done.30, bf16[3,512,512]{2,1,0:T(8,128)(2,1)S(1)} %project.7.qkv_ref, bf16[512,512]{1,0:T(8,128)(2,1)} %collective-permute-done.12.og_ref, ...), custom_call_target="tpu_custom_call", output_to_operand_aliasing={{0}: (4, {}), {1}: (5, {})} | custom-call | flops 1 | bytes 1 | tf_op jit(solution)/shard_map/local_grads/pallas_call | solution.py:35
  99.0 3.7 %turn.5 = bf16[16,2,96,512]{3,2,1,0:T(8,128)(2,1)S(1)} custom-call(s32[7]{0:T(128)S(1)} %copy-done.21, bf16[256,768]{1,0:T(8,128)(2,1)} %collective-permute-done.6.refs_0_, bf16[256,768]{1,0:T(8,128)(2,1)} %collective-permute-done.7.refs_1_, bf16[256,768]{1,0:T(8,128)(2,1)} %collective-permute-done.13.refs_2_, ...), custom_call_target="tpu_custom_call" | custom-call | flops 1 | bytes 1 | tf_op jit(solution)/shard_map/turn/pallas_call | solution.py:35
  102.7 2.5 %whole_grads.2 = (bf16[512,768]{1,0:T(8,128)(2,1)S(1)}, bf16[512,768]{1,0:T(8,128)(2,1)S(1)}) custom-call(s32[7]{0:T(128)S(1)} %copy-done.21, bf16[3,512,512]{2,1,0:T(8,128)(2,1)S(1)} %get-tuple-element.201.local_ref, bf16[3,512,512]{2,1,0:T(8,128)(2,1)S(1)} %get-tuple-element.202.ready_ref, bf16[512,128]{1,0:T(8,128)(2,1)S(1)} %get-tuple-element.184.a, ...), custom_call_target="tpu_custom_call" | custom-call | flops 1 | bytes 1 | tf_op jit(solution)/shard_map/whole_grads/pallas_call | solution.py:35
  105.3 2.5 %whole_grads.3 = (bf16[512,768]{1,0:T(8,128)(2,1)S(1)}, bf16[512,768]{1,0:T(8,128)(2,1)S(1)}) custom-call(s32[7]{0:T(128)S(1)} %copy-done.21, bf16[3,512,512]{2,1,0:T(8,128)(2,1)S(1)} %get-tuple-element.207.local_ref, bf16[3,512,512]{2,1,0:T(8,128)(2,1)S(1)} %get-tuple-element.208.ready_ref, bf16[512,128]{1,0:T(8,128)(2,1)S(1)} %get-tuple-element.184.a, ...), custom_call_target="tpu_custom_call" | custom-call | flops 1 | bytes 1 | tf_op jit(solution)/shard_map/whole_grads/pallas_call | solution.py:35
  107.8 3.2 %weight_part.3 = (bf16[384,768]{1,0:T(8,128)(2,1)S(1)}, bf16[384,768]{1,0:T(8,128)(2,1)S(1)}, bf16[384,768]{1,0:T(8,128)(2,1)S(1)}, bf16[384,768]{1,0:T(8,128)(2,1)S(1)}) custom-call(s32[7]{0:T(128)S(1)} %copy-done.21, bf16[4,4,192,512]{3,2,1,0:T(8,128)(2,1)S(1)} %bitcast.20, bf16[4,4,192,512]{3,2,1,0:T(8,128)(2,1)S(1)} %bitcast.21, ...), custom_call_target="tpu_custom_call" | custom-call | flops 1 | bytes 1 | tf_op jit(solution)/shard_map/weight_part/pallas_call | solution.py:35
  111.0 2.4 %collective-permute-start.25 = (bf16[384,768]{1,0:T(8,128)(2,1)S(1)}, bf16[384,768]{1,0:T(8,128)(2,1)S(1)}, u32[]{:S(2)}, u32[]{:S(2)}) collective-permute-start(bf16[384,768]{1,0:T(8,128)(2,1)S(1)} %get-tuple-element.216), channel_id=1, source_target_pairs={{0,48},{16,32},{32,16},{48,0},{1,49},{17,33},{33,17},{49,1},{2,50}... | collective-permute-start | bytes 1769480 | tf_op jit(solution)/shard_map/ppermute | solution.py:23
  114.2 2.2 %collective-permute-start.29 = (bf16[384,768]{1,0:T(8,128)(2,1)S(1)}, bf16[384,768]{1,0:T(8,128)(2,1)S(1)}, u32[]{:S(2)}, u32[]{:S(2)}) collective-permute-start(bf16[384,768]{1,0:T(8,128)(2,1)S(1)} %get-tuple-element.226), channel_id=1, source_target_pairs={{0,12},{4,8},{8,4},{12,0},{1,13},{5,9},{9,5},{13,1},{2,14},{6,10},... | collective-permute-start | bytes 1769480 | tf_op jit(solution)/shard_map/ppermute | solution.py:23
  116.3 8.4 %weight_part.4 = (bf16[768,768]{1,0:T(8,128)(2,1)S(1)}, bf16[768,768]{1,0:T(8,128)(2,1)S(1)}, bf16[768,768]{1,0:T(8,128)(2,1)S(1)}, bf16[768,768]{1,0:T(8,128)(2,1)S(1)}) custom-call(s32[7]{0:T(128)S(1)} %copy-done.21, bf16[4,4,192,512]{3,2,1,0:T(8,128)(2,1)S(1)} %bitcast.22, bf16[4,4,192,512]{3,2,1,0:T(8,128)(2,1)S(1)} %bitcast.23, ...), custom_call_target="tpu_custom_call" | custom-call | flops 1 | bytes 1 | tf_op jit(solution)/shard_map/weight_part/pallas_call | solution.py:35
  126.6 1.5 add_halves.2
  128.5 1.3 collective-permute-start.27
  129.8 1.5 add_halves.3
  131.2 2.4 %collective-permute-start.31 = (bf16[768,768]{1,0:T(8,128)(2,1)S(1)}, bf16[768,768]{1,0:T(8,128)(2,1)S(1)}, u32[]{:S(2)}, u32[]{:S(2)}) collective-permute-start(bf16[768,768]{1,0:T(8,128)(2,1)S(1)} %get-tuple-element.238), channel_id=1, source_target_pairs={{0,12},{4,8},{8,4},{12,0},{1,13},{5,9},{9,5},{13,1},{2,14},{6,10},... | collective-permute-start | bytes 3538952 | tf_op jit(solution)/shard_map/ppermute | solution.py:23
  133.8 3.2 %weight_part.5 = (bf16[768,768]{1,0:T(8,128)(2,1)S(1)}, bf16[768,768]{1,0:T(8,128)(2,1)S(1)}) custom-call(s32[7]{0:T(128)S(1)} %copy-done.21, bf16[4,4,192,512]{3,2,1,0:T(8,128)(2,1)S(1)} %bitcast.24, bf16[4,4,192,512]{3,2,1,0:T(8,128)(2,1)S(1)} %bitcast.25, bf16[4,4,192,512]{3,2,1,0:T(8,128)(2,1)S(1)} %bitcast.30, bf16[4,4,192,512]{3,2,1,0:T(8,128)(2,1)S(1)} %bitcast.31, ...), custom_call_target="tpu_custom_call" | custom-call | flops 1 | bytes 1 | tf_op jit(solution)/shard_map/weight_part/pallas_call | solution.py:35
  137.0 17.7 %collective-permute-done.27.refs_2_ = bf16[768,768]{1,0:T(8,128)(2,1)S(1)} collective-permute-done((bf16[768,768]{1,0:T(8,128)(2,1)S(1)}, bf16[768,768]{1,0:T(8,128)(2,1)S(1)}, u32[]{:S(2)}, u32[]{:S(2)}) %collective-permute-start.27) | collective-permute-done | bytes 1179680 | tf_op jit(solution)/shard_map/ppermute | solution.py:23
  154.7 2.8 %collective-permute-done.31.refs_5_ = bf16[768,768]{1,0:T(8,128)(2,1)S(1)} collective-permute-done((bf16[768,768]{1,0:T(8,128)(2,1)S(1)}, bf16[768,768]{1,0:T(8,128)(2,1)S(1)}, u32[]{:S(2)}, u32[]{:S(2)}) %collective-permute-start.31) | collective-permute-done | bytes 1179680 | tf_op jit(solution)/shard_map/ppermute | solution.py:23
  158.5 1.4 cut_blocks.1
  160.2 1.3 collective-permute-start.33
  161.5 2.5 %collective-permute-start.34 = (bf16[192,768]{1,0:T(8,128)(2,1)S(1)}, bf16[192,768]{1,0:T(8,128)(2,1)S(1)}, u32[]{:S(2)}, u32[]{:S(2)}) collective-permute-start(bf16[192,768]{1,0:T(8,128)(2,1)S(1)} %get-tuple-element.242), channel_id=1, source_target_pairs={{0,8},{4,12},{8,0},{12,4},{1,9},{5,13},{9,1},{13,5},{2,10},{6,14},... | collective-permute-start | bytes 884744 | tf_op jit(solution)/shard_map/ppermute | solution.py:23
  165.2 1.7 collective-permute-start.36
  168.1 1.8 collective-permute-start.37
  169.9 2.8 %collective-permute-done.33.refs_2_ = bf16[192,768]{1,0:T(8,128)(2,1)S(1)} collective-permute-done((bf16[192,768]{1,0:T(8,128)(2,1)S(1)}, bf16[192,768]{1,0:T(8,128)(2,1)S(1)}, u32[]{:S(2)}, u32[]{:S(2)}) %collective-permute-start.33) | collective-permute-done | bytes 294944 | tf_op jit(solution)/shard_map/ppermute | solution.py:23
  173.1 3.2 %collective-permute-done.37.refs_7_ = bf16[192,768]{1,0:T(8,128)(2,1)S(1)} collective-permute-done((bf16[192,768]{1,0:T(8,128)(2,1)S(1)}, bf16[192,768]{1,0:T(8,128)(2,1)S(1)}, u32[]{:S(2)}, u32[]{:S(2)}) %collective-permute-start.37) | collective-permute-done | bytes 294944 | tf_op jit(solution)/shard_map/ppermute | solution.py:23
  177.2 1.3 collective-permute-start.38
  178.4 7.0 %collective-permute-done.38.there_ref = bf16[2,96,768]{2,1,0:T(8,128)(2,1)S(1)} collective-permute-done((bf16[2,96,768]{2,1,0:T(8,128)(2,1)S(1)}, bf16[2,96,768]{2,1,0:T(8,128)(2,1)S(1)}, u32[]{:S(2)}, u32[]{:S(2)}) %collective-permute-start.38) | collective-permute-done | bytes 294944 | tf_op jit(solution)/shard_map/ppermute | solution.py:23
  185.5 1.6 finish.1
  (140 shorter events, 32.0 us)
Async XLA Ops:
  0.0 8.4 %copy-start.4 = (bf16[512,768]{1,0:T(8,128)(2,1)S(1)}, bf16[512,768]{1,0:T(8,128)(2,1)}, u32[]{:S(2)}) copy-start(bf16[512,768]{1,0:T(8,128)(2,1)} %refs_0_.3) | copy-start | bytes 2359300
  0.0 9.1 %copy-start.33 = (f32[512,8]{0,1:T(8,128)S(1)}, f32[512,8]{0,1:T(8,128)}, u32[]{:S(2)}) copy-start(f32[512,8]{0,1:T(8,128)} %param.7) | copy-start | bytes 49156
  0.0 11.8 %copy-start.31 = (bf16[512,1024]{1,0:T(8,128)(2,1)S(1)}, bf16[512,1024]{1,0:T(8,128)(2,1)}, u32[]{:S(2)}) copy-start(bf16[512,1024]{1,0:T(8,128)(2,1)} %param.9) | copy-start | bytes 3145732
  2.2 20.3 %collective-permute-start.3 = (bf16[256,768]{1,0:T(8,128)(2,1)}, bf16[256,768]{1,0:T(8,128)(2,1)}, u32[]{:S(2)}, u32[]{:S(2)}) collective-permute-start(bf16[256,768]{1,0:T(8,128)(2,1)} %get-tuple-element.251), channel_id=1, source_target_pairs={{0,66},{2,64},{64,2},{66,0},{1,67},{3,65},{65,3},{67,1},{4,70},{6,... | collective-permute-start | bytes 1179656 | tf_op jit(solution)/shard_map/ppermute | solution.py:27
  6.4 16.1 %collective-permute-start.1 = (bf16[256,768]{1,0:T(8,128)(2,1)}, bf16[256,768]{1,0:T(8,128)(2,1)S(1)}, u32[]{:S(2)}, u32[]{:S(2)}) collective-permute-start(bf16[256,768]{1,0:T(8,128)(2,1)} %get-tuple-element.251), channel_id=1, source_target_pairs={{0,2},{2,0},{1,3},{3,1},{4,6},{6,4},{5,7},{7,5},{8,10},{10,8},{9,1... | collective-permute-start | bytes 1179656 | tf_op jit(solution)/shard_map/ppermute | solution.py:23
  6.4 17.9 %collective-permute-start.2 = (bf16[256,768]{1,0:T(8,128)(2,1)}, bf16[256,768]{1,0:T(8,128)(2,1)}, u32[]{:S(2)}, u32[]{:S(2)}) collective-permute-start(bf16[256,768]{1,0:T(8,128)(2,1)} %get-tuple-element.252), channel_id=1, source_target_pairs={{0,66},{2,64},{64,2},{66,0},{1,67},{3,65},{65,3},{67,1},{4,70},{6,... | collective-permute-start | bytes 1179656 | tf_op jit(solution)/shard_map/ppermute | solution.py:27
  6.9 18.8 %collective-permute-start = (bf16[256,768]{1,0:T(8,128)(2,1)}, bf16[256,768]{1,0:T(8,128)(2,1)}, u32[]{:S(2)}, u32[]{:S(2)}) collective-permute-start(bf16[256,768]{1,0:T(8,128)(2,1)} %get-tuple-element.252), channel_id=1, source_target_pairs={{0,2},{2,0},{1,3},{3,1},{4,6},{6,4},{5,7},{7,5},{8,10},{10,8},{9,1... | collective-permute-start | bytes 1179656 | tf_op jit(solution)/shard_map/ppermute | solution.py:23
  8.4 4.3 %collective-permute-start.4 = (bf16[512,768]{1,0:T(8,128)(2,1)S(1)}, bf16[512,768]{1,0:T(8,128)(2,1)S(1)}, u32[]{:S(2)}, u32[]{:S(2)}) collective-permute-start(bf16[512,768]{1,0:T(8,128)(2,1)S(1)} %copy-done.4), channel_id=1, source_target_pairs={{0,1},{1,0},{2,3},{3,2},{4,5},{5,4},{6,7},{7,6},{8,9},{9,8},{10,11... | collective-permute-start | bytes 2359304 | tf_op jit(solution)/shard_map/ppermute | solution.py:23
  11.8 24.6 %copy-start.19 = (s32[7]{0:T(128)}, s32[7]{0:T(128)S(1)}, u32[]{:S(2)}) copy-start(s32[7]{0:T(128)S(1)} %stack.39.s) | copy-start | bytes 88
  12.7 34.0 %copy-start.7 = (bf16[512,512]{1,0:T(8,128)(2,1)}, bf16[512,512]{1,0:T(8,128)(2,1)S(1)}, u32[]{:S(2)}) copy-start(bf16[512,512]{1,0:T(8,128)(2,1)S(1)} %get-tuple-element.249.og_ref) | copy-start | bytes 1572868
  17.2 12.5 %copy-start.34 = (f32[8,512]{1,0:T(8,128)S(1)}, f32[8,512]{1,0:T(8,128)}, u32[]{:S(2)}) copy-start(f32[8,512]{1,0:T(8,128)} %concatenate.6) | copy-start | bytes 49156
  25.7 2.5 %collective-permute-start.10 = (bf16[256,768]{1,0:T(8,128)(2,1)}, bf16[256,768]{1,0:T(8,128)(2,1)S(1)}, u32[]{:S(2)}, u32[]{:S(2)}) collective-permute-start(bf16[256,768]{1,0:T(8,128)(2,1)} %collective-permute-done.refs_0_), channel_id=1, source_target_pairs={{0,1},{1,0},{2,3},{3,2},{4,5},{5,4},{6,7},{7,6},{8,9},{9,8},{10,11... | collective-permute-start | bytes 1179656 | tf_op jit(solution)/shard_map/ppermute | solution.py:23
  25.7 4.0 %collective-permute-start.11 = (bf16[256,768]{1,0:T(8,128)(2,1)S(1)}, bf16[256,768]{1,0:T(8,128)(2,1)S(1)}, u32[]{:S(2)}, u32[]{:S(2)}) collective-permute-start(bf16[256,768]{1,0:T(8,128)(2,1)S(1)} %collective-permute-done.1.refs_1_), channel_id=1, source_target_pairs={{0,1},{1,0},{2,3},{3,2},{4,5},{5,4},{6,7},{7,6},{8,9},{9,8},{10,11... | collective-permute-start | bytes 1179656 | tf_op jit(solution)/shard_map/ppermute | solution.py:23
  26.2 10.2 %collective-permute-start.9 = (bf16[256,768]{1,0:T(8,128)(2,1)}, bf16[256,768]{1,0:T(8,128)(2,1)S(1)}, u32[]{:S(2)}, u32[]{:S(2)}) collective-permute-start(bf16[256,768]{1,0:T(8,128)(2,1)} %collective-permute-done.3.refs_1_.refs_5_), channel_id=1, source_target_pairs={{0,1},{1,0},{2,3},{3,2},{4,5},{5,4},{6,7},{7,6},{8,9},{9,8},{10,11... | collective-permute-start | bytes 1179656 | tf_op jit(solution)/shard_map/ppermute | solution.py:23
  26.2 10.2 %collective-permute-start.8 = (bf16[256,768]{1,0:T(8,128)(2,1)}, bf16[256,768]{1,0:T(8,128)(2,1)S(1)}, u32[]{:S(2)}, u32[]{:S(2)}) collective-permute-start(bf16[256,768]{1,0:T(8,128)(2,1)} %collective-permute-done.2.refs_0_.refs_4_), channel_id=1, source_target_pairs={{0,1},{1,0},{2,3},{3,2},{4,5},{5,4},{6,7},{7,6},{8,9},{9,8},{10,11... | collective-permute-start | bytes 1179656 | tf_op jit(solution)/shard_map/ppermute | solution.py:23
  26.7 17.1 %collective-permute-start.6 = (bf16[256,768]{1,0:T(8,128)(2,1)}, bf16[256,768]{1,0:T(8,128)(2,1)}, u32[]{:S(2)}, u32[]{:S(2)}) collective-permute-start(bf16[256,768]{1,0:T(8,128)(2,1)} %collective-permute-done.2.refs_0_.refs_4_), channel_id=1, source_target_pairs={{0,2},{2,0},{1,3},{3,1},{4,6},{6,4},{5,7},{7,5},{8,10},{10,8},{9,1... | collective-permute-start | bytes 1179656 | tf_op jit(solution)/shard_map/ppermute | solution.py:23
  28.1 15.6 %collective-permute-start.7 = (bf16[256,768]{1,0:T(8,128)(2,1)S(1)}, bf16[256,768]{1,0:T(8,128)(2,1)}, u32[]{:S(2)}, u32[]{:S(2)}) collective-permute-start(bf16[256,768]{1,0:T(8,128)(2,1)S(1)} %collective-permute-done.1.refs_1_), channel_id=1, source_target_pairs={{0,66},{2,64},{64,2},{66,0},{1,67},{3,65},{65,3},{67,1},{4,70},{6,... | collective-permute-start | bytes 1179656 | tf_op jit(solution)/shard_map/ppermute | solution.py:27
  29.6 14.1 %collective-permute-start.5 = (f32[8,512]{1,0:T(8,128)S(1)}, f32[8,512]{1,0:T(8,128)S(1)}, u32[]{:S(2)}, u32[]{:S(2)}) collective-permute-start(f32[8,512]{1,0:T(8,128)S(1)} %copy-done.34), channel_id=1, source_target_pairs={{0,64},{64,0},{1,65},{65,1},{2,66},{66,2},{3,67},{67,3},{4,68},{68... | collective-permute-start | bytes 49160 | tf_op jit(solution)/shard_map/ppermute | solution.py:23
  36.3 10.4 %copy-start = (bf16[3,512,512]{2,1,0:T(8,128)(2,1)}, bf16[3,512,512]{2,1,0:T(8,128)(2,1)S(1)}, u32[]{:S(2)}) copy-start(bf16[3,512,512]{2,1,0:T(8,128)(2,1)S(1)} %project.5.qkv_ref) | copy-start | bytes 4718596
  36.3 10.4 %copy-start.32 = (f32[4,512]{1,0:T(4,128)S(1)}, f32[4,512]{1,0:T(4,128)}, u32[]{:S(2)}) copy-start(f32[4,512]{1,0:T(4,128)} %get-tuple-element.253) | copy-start | bytes 24580
  43.8 21.2 %collective-permute-start.12 = (bf16[512,512]{1,0:T(8,128)(2,1)}, bf16[512,512]{1,0:T(8,128)(2,1)}, u32[]{:S(2)}, u32[]{:S(2)}) collective-permute-start(bf16[512,512]{1,0:T(8,128)(2,1)} %get-tuple-element.138), channel_id=1, source_target_pairs={{0,64},{64,0},{1,65},{65,1},{2,66},{66,2},{3,67},{67,3},{4,68},{68... | collective-permute-start | bytes 1572872 | tf_op jit(solution)/shard_map/ppermute | solution.py:23
  46.2 8.0 %collective-permute-start.13 = (bf16[256,768]{1,0:T(8,128)(2,1)}, bf16[256,768]{1,0:T(8,128)(2,1)}, u32[]{:S(2)}, u32[]{:S(2)}) collective-permute-start(bf16[256,768]{1,0:T(8,128)(2,1)} %collective-permute-done.6.refs_0_), channel_id=1, source_target_pairs={{0,1},{1,0},{2,3},{3,2},{4,5},{5,4},{6,7},{7,6},{8,9},{9,8},{10,11... | collective-permute-start | bytes 1179656 | tf_op jit(solution)/shard_map/ppermute | solution.py:23
  46.2 8.0 %collective-permute-start.14 = (bf16[256,768]{1,0:T(8,128)(2,1)}, bf16[256,768]{1,0:T(8,128)(2,1)}, u32[]{:S(2)}, u32[]{:S(2)}) collective-permute-start(bf16[256,768]{1,0:T(8,128)(2,1)} %collective-permute-done.7.refs_1_), channel_id=1, source_target_pairs={{0,1},{1,0},{2,3},{3,2},{4,5},{5,4},{6,7},{7,6},{8,9},{9,8},{10,11... | collective-permute-start | bytes 1179656 | tf_op jit(solution)/shard_map/ppermute | solution.py:23
  64.9 8.3 %copy-start.1 = (bf16[3,512,512]{2,1,0:T(8,128)(2,1)S(1)}, bf16[3,512,512]{2,1,0:T(8,128)(2,1)}, u32[]{:S(2)}) copy-start(bf16[3,512,512]{2,1,0:T(8,128)(2,1)} %copy-done) | copy-start | bytes 4718596
  68.6 10.5 %collective-permute-start.15 = (bf16[528,128]{1,0:T(8,128)(2,1)S(1)}, bf16[528,128]{1,0:T(8,128)(2,1)S(1)}, u32[]{:S(2)}, u32[]{:S(2)}) collective-permute-start(bf16[528,128]{1,0:T(8,128)(2,1)S(1)} %get-tuple-element.160), channel_id=1, source_target_pairs={{0,4},{4,0},{8,12},{12,8},{1,5},{5,1},{9,13},{13,9},{2,6},{6,2},{1... | collective-permute-start | bytes 405512 | tf_op jit(solution)/shard_map/ppermute | solution.py:23
  70.3 8.9 %collective-permute-start.16 = (bf16[528,128]{1,0:T(8,128)(2,1)S(1)}, bf16[528,128]{1,0:T(8,128)(2,1)S(1)}, u32[]{:S(2)}, u32[]{:S(2)}) collective-permute-start(bf16[528,128]{1,0:T(8,128)(2,1)S(1)} %get-tuple-element.161), channel_id=1, source_target_pairs={{0,12},{4,8},{8,4},{12,0},{1,13},{5,9},{9,5},{13,1},{2,14},{6,10},... | collective-permute-start | bytes 405512 | tf_op jit(solution)/shard_map/ppermute | solution.py:23
  72.4 7.2 %collective-permute-start.17 = (bf16[528,128]{1,0:T(8,128)(2,1)S(1)}, bf16[528,128]{1,0:T(8,128)(2,1)S(1)}, u32[]{:S(2)}, u32[]{:S(2)}) collective-permute-start(bf16[528,128]{1,0:T(8,128)(2,1)S(1)} %get-tuple-element.162), channel_id=1, source_target_pairs={{0,8},{4,12},{8,0},{12,4},{1,9},{5,13},{9,1},{13,5},{2,10},{6,14},... | collective-permute-start | bytes 405512 | tf_op jit(solution)/shard_map/ppermute | solution.py:23
  80.3 8.3 %collective-permute-start.20 = (bf16[528,128]{1,0:T(8,128)(2,1)S(1)}, bf16[528,128]{1,0:T(8,128)(2,1)S(1)}, u32[]{:S(2)}, u32[]{:S(2)}) collective-permute-start(bf16[528,128]{1,0:T(8,128)(2,1)S(1)} %get-tuple-element.169.a), channel_id=1, source_target_pairs={{0,32},{16,48},{32,0},{48,16},{1,33},{17,49},{33,1},{49,17},{2,34}... | collective-permute-start | bytes 405512 | tf_op jit(solution)/shard_map/ppermute | solution.py:23
  83.4 6.4 %collective-permute-start.19 = (bf16[528,128]{1,0:T(8,128)(2,1)S(1)}, bf16[528,128]{1,0:T(8,128)(2,1)S(1)}, u32[]{:S(2)}, u32[]{:S(2)}) collective-permute-start(bf16[528,128]{1,0:T(8,128)(2,1)S(1)} %get-tuple-element.169.a), channel_id=1, source_target_pairs={{0,48},{16,32},{32,16},{48,0},{1,49},{17,33},{33,17},{49,1},{2,50}... | collective-permute-start | bytes 405512 | tf_op jit(solution)/shard_map/ppermute | solution.py:23
  84.6 5.4 %collective-permute-start.18 = (bf16[528,128]{1,0:T(8,128)(2,1)S(1)}, bf16[528,128]{1,0:T(8,128)(2,1)S(1)}, u32[]{:S(2)}, u32[]{:S(2)}) collective-permute-start(bf16[528,128]{1,0:T(8,128)(2,1)S(1)} %get-tuple-element.169.a), channel_id=1, source_target_pairs={{0,16},{16,0},{32,48},{48,32},{1,17},{17,1},{33,49},{49,33},{2,18}... | collective-permute-start | bytes 405512 | tf_op jit(solution)/shard_map/ppermute | solution.py:23
  90.7 11.9 %collective-permute-start.21 = (bf16[512,128]{1,0:T(8,128)(2,1)S(1)}, bf16[512,128]{1,0:T(8,128)(2,1)S(1)}, u32[]{:S(2)}, u32[]{:S(2)}) collective-permute-start(bf16[512,128]{1,0:T(8,128)(2,1)S(1)} %get-tuple-element.180), channel_id=1, source_target_pairs={{0,4},{4,0},{8,12},{12,8},{1,5},{5,1},{9,13},{13,9},{2,6},{6,2},{1... | collective-permute-start | bytes 393224 | tf_op jit(solution)/shard_map/ppermute | solution.py:23
  91.6 11.1 %collective-permute-start.22 = (bf16[512,128]{1,0:T(8,128)(2,1)S(1)}, bf16[512,128]{1,0:T(8,128)(2,1)S(1)}, u32[]{:S(2)}, u32[]{:S(2)}) collective-permute-start(bf16[512,128]{1,0:T(8,128)(2,1)S(1)} %get-tuple-element.181), channel_id=1, source_target_pairs={{0,12},{4,8},{8,4},{12,0},{1,13},{5,9},{9,5},{13,1},{2,14},{6,10},... | collective-permute-start | bytes 393224 | tf_op jit(solution)/shard_map/ppermute | solution.py:23
  93.8 8.9 %collective-permute-start.23 = (bf16[512,128]{1,0:T(8,128)(2,1)S(1)}, bf16[512,128]{1,0:T(8,128)(2,1)S(1)}, u32[]{:S(2)}, u32[]{:S(2)}) collective-permute-start(bf16[512,128]{1,0:T(8,128)(2,1)S(1)} %get-tuple-element.182), channel_id=1, source_target_pairs={{0,8},{4,12},{8,0},{12,4},{1,9},{5,13},{9,1},{13,5},{2,10},{6,14},... | collective-permute-start | bytes 393224 | tf_op jit(solution)/shard_map/ppermute | solution.py:23
  111.0 14.5 %collective-permute-start.25 = (bf16[384,768]{1,0:T(8,128)(2,1)S(1)}, bf16[384,768]{1,0:T(8,128)(2,1)S(1)}, u32[]{:S(2)}, u32[]{:S(2)}) collective-permute-start(bf16[384,768]{1,0:T(8,128)(2,1)S(1)} %get-tuple-element.216), channel_id=1, source_target_pairs={{0,48},{16,32},{32,16},{48,0},{1,49},{17,33},{33,17},{49,1},{2,50}... | collective-permute-start | bytes 1769480 | tf_op jit(solution)/shard_map/ppermute | solution.py:23
  113.3 13.3 %collective-permute-start.24 = (bf16[384,768]{1,0:T(8,128)(2,1)S(1)}, bf16[384,768]{1,0:T(8,128)(2,1)S(1)}, u32[]{:S(2)}, u32[]{:S(2)}) collective-permute-start(bf16[384,768]{1,0:T(8,128)(2,1)S(1)} %get-tuple-element.212), channel_id=1, source_target_pairs={{0,16},{16,0},{32,48},{48,32},{1,17},{17,1},{33,49},{49,33},{2,18}... | collective-permute-start | bytes 1769480 | tf_op jit(solution)/shard_map/ppermute | solution.py:23
  113.3 15.1 %collective-permute-start.28 = (bf16[384,768]{1,0:T(8,128)(2,1)S(1)}, bf16[384,768]{1,0:T(8,128)(2,1)S(1)}, u32[]{:S(2)}, u32[]{:S(2)}) collective-permute-start(bf16[384,768]{1,0:T(8,128)(2,1)S(1)} %get-tuple-element.225), channel_id=1, source_target_pairs={{0,4},{4,0},{8,12},{12,8},{1,5},{5,1},{9,13},{13,9},{2,6},{6,2},{1... | collective-permute-start | bytes 1769480 | tf_op jit(solution)/shard_map/ppermute | solution.py:23
  114.2 14.3 %collective-permute-start.29 = (bf16[384,768]{1,0:T(8,128)(2,1)S(1)}, bf16[384,768]{1,0:T(8,128)(2,1)S(1)}, u32[]{:S(2)}, u32[]{:S(2)}) collective-permute-start(bf16[384,768]{1,0:T(8,128)(2,1)S(1)} %get-tuple-element.226), channel_id=1, source_target_pairs={{0,12},{4,8},{8,4},{12,0},{1,13},{5,9},{9,5},{13,1},{2,14},{6,10},... | collective-permute-start | bytes 1769480 | tf_op jit(solution)/shard_map/ppermute | solution.py:23
  128.1 26.6 %collective-permute-start.26 = (bf16[768,768]{1,0:T(8,128)(2,1)S(1)}, bf16[768,768]{1,0:T(8,128)(2,1)S(1)}, u32[]{:S(2)}, u32[]{:S(2)}) collective-permute-start(bf16[768,768]{1,0:T(8,128)(2,1)S(1)} %get-tuple-element.221), channel_id=1, source_target_pairs={{0,16},{16,0},{32,48},{48,32},{1,17},{17,1},{33,49},{49,33},{2,18}... | collective-permute-start | bytes 3538952 | tf_op jit(solution)/shard_map/ppermute | solution.py:23
  128.5 26.2 %collective-permute-start.27 = (bf16[768,768]{1,0:T(8,128)(2,1)S(1)}, bf16[768,768]{1,0:T(8,128)(2,1)S(1)}, u32[]{:S(2)}, u32[]{:S(2)}) collective-permute-start(bf16[768,768]{1,0:T(8,128)(2,1)S(1)} %get-tuple-element.222), channel_id=1, source_target_pairs={{0,48},{16,32},{32,16},{48,0},{1,49},{17,33},{33,17},{49,1},{2,50}... | collective-permute-start | bytes 3538952 | tf_op jit(solution)/shard_map/ppermute | solution.py:23
  131.2 26.3 %collective-permute-start.31 = (bf16[768,768]{1,0:T(8,128)(2,1)S(1)}, bf16[768,768]{1,0:T(8,128)(2,1)S(1)}, u32[]{:S(2)}, u32[]{:S(2)}) collective-permute-start(bf16[768,768]{1,0:T(8,128)(2,1)S(1)} %get-tuple-element.238), channel_id=1, source_target_pairs={{0,12},{4,8},{8,4},{12,0},{1,13},{5,9},{9,5},{13,1},{2,14},{6,10},... | collective-permute-start | bytes 3538952 | tf_op jit(solution)/shard_map/ppermute | solution.py:23
  133.7 24.8 %collective-permute-start.30 = (bf16[768,768]{1,0:T(8,128)(2,1)S(1)}, bf16[768,768]{1,0:T(8,128)(2,1)S(1)}, u32[]{:S(2)}, u32[]{:S(2)}) collective-permute-start(bf16[768,768]{1,0:T(8,128)(2,1)S(1)} %get-tuple-element.229), channel_id=1, source_target_pairs={{0,4},{4,0},{8,12},{12,8},{1,5},{5,1},{9,13},{13,9},{2,6},{6,2},{1... | collective-permute-start | bytes 3538952 | tf_op jit(solution)/shard_map/ppermute | solution.py:23
  159.9 8.2 %collective-permute-start.32 = (bf16[192,768]{1,0:T(8,128)(2,1)S(1)}, bf16[192,768]{1,0:T(8,128)(2,1)S(1)}, u32[]{:S(2)}, u32[]{:S(2)}) collective-permute-start(bf16[192,768]{1,0:T(8,128)(2,1)S(1)} %get-tuple-element.240), channel_id=1, source_target_pairs={{0,4},{4,0},{8,12},{12,8},{1,5},{5,1},{9,13},{13,9},{2,6},{6,2},{1... | collective-permute-start | bytes 884744 | tf_op jit(solution)/shard_map/ppermute | solution.py:23
  160.2 12.5 %collective-permute-start.33 = (bf16[192,768]{1,0:T(8,128)(2,1)S(1)}, bf16[192,768]{1,0:T(8,128)(2,1)S(1)}, u32[]{:S(2)}, u32[]{:S(2)}) collective-permute-start(bf16[192,768]{1,0:T(8,128)(2,1)S(1)} %get-tuple-element.241), channel_id=1, source_target_pairs={{0,12},{4,8},{8,4},{12,0},{1,13},{5,9},{9,5},{13,1},{2,14},{6,10},... | collective-permute-start | bytes 884744 | tf_op jit(solution)/shard_map/ppermute | solution.py:23
  161.5 11.2 %collective-permute-start.34 = (bf16[192,768]{1,0:T(8,128)(2,1)S(1)}, bf16[192,768]{1,0:T(8,128)(2,1)S(1)}, u32[]{:S(2)}, u32[]{:S(2)}) collective-permute-start(bf16[192,768]{1,0:T(8,128)(2,1)S(1)} %get-tuple-element.242), channel_id=1, source_target_pairs={{0,8},{4,12},{8,0},{12,4},{1,9},{5,13},{9,1},{13,5},{2,10},{6,14},... | collective-permute-start | bytes 884744 | tf_op jit(solution)/shard_map/ppermute | solution.py:23
  164.0 8.7 %collective-permute-start.35 = (bf16[192,768]{1,0:T(8,128)(2,1)S(1)}, bf16[192,768]{1,0:T(8,128)(2,1)S(1)}, u32[]{:S(2)}, u32[]{:S(2)}) collective-permute-start(bf16[192,768]{1,0:T(8,128)(2,1)S(1)} %get-tuple-element.244), channel_id=1, source_target_pairs={{0,16},{16,0},{32,48},{48,32},{1,17},{17,1},{33,49},{49,33},{2,18}... | collective-permute-start | bytes 884744 | tf_op jit(solution)/shard_map/ppermute | solution.py:23
  165.2 7.9 %collective-permute-start.36 = (bf16[192,768]{1,0:T(8,128)(2,1)S(1)}, bf16[192,768]{1,0:T(8,128)(2,1)S(1)}, u32[]{:S(2)}, u32[]{:S(2)}) collective-permute-start(bf16[192,768]{1,0:T(8,128)(2,1)S(1)} %get-tuple-element.245), channel_id=1, source_target_pairs={{0,48},{16,32},{32,16},{48,0},{1,49},{17,33},{33,17},{49,1},{2,50}... | collective-permute-start | bytes 884744 | tf_op jit(solution)/shard_map/ppermute | solution.py:23
  168.1 8.2 %collective-permute-start.37 = (bf16[192,768]{1,0:T(8,128)(2,1)S(1)}, bf16[192,768]{1,0:T(8,128)(2,1)S(1)}, u32[]{:S(2)}, u32[]{:S(2)}) collective-permute-start(bf16[192,768]{1,0:T(8,128)(2,1)S(1)} %get-tuple-element.246), channel_id=1, source_target_pairs={{0,32},{16,48},{32,0},{48,16},{1,33},{17,49},{33,1},{49,17},{2,34}... | collective-permute-start | bytes 884744 | tf_op jit(solution)/shard_map/ppermute | solution.py:23
  177.2 8.3 %collective-permute-start.38 = (bf16[2,96,768]{2,1,0:T(8,128)(2,1)S(1)}, bf16[2,96,768]{2,1,0:T(8,128)(2,1)S(1)}, u32[]{:S(2)}, u32[]{:S(2)}) collective-permute-start(bf16[2,96,768]{2,1,0:T(8,128)(2,1)S(1)} %get-tuple-element.248), channel_id=1, source_target_pairs={{0,64},{64,0},{1,65},{65,1},{2,66},{66,2},{3,67},{67,3},{4,68},{68... | collective-permute-start | bytes 884744 | tf_op jit(solution)/shard_map/ppermute | solution.py:23
  (26 other events, 81.4 us)

commit v6 on v3

--- a/solution.py
+++ b/solution.py
@@ -312,7 +312,7 @@
             qkv_ref[1].astype(F32) * until,
         )
         for j in range(3):
-            out[j] = jnp.where(live, grads[j], 0.0)
+            out[j] = jnp.where(live, grads[j], 0.0).astype(BF16)
             ready[j] = jnp.where(live, rows[j], 0.0).astype(BF16)
 
     tile = pl.BlockSpec((3, tokens, HEAD), lambda h, s: (0, 0, h + first))
@@ -328,7 +328,7 @@
         (count,),
         operands,
         in_specs,
-        [shape(qkv.shape, F32), shape(qkv.shape)],
+        [shape(qkv.shape), shape(qkv.shape)],
         [tile, tile],
         12,
         alias=None if so_far is None else {4: 0, 5: 1},
@@ -354,7 +354,7 @@
             lax.dot_general(ready_ref[1], later, AB_T, preferred_element_type=F32),
             dot(ready_ref[2], later),
         )
-        grads = [(local_ref[j] + cross[j]).astype(BF16) for j in range(3)]
+        grads = [(local_ref[j].astype(F32) + cross[j]).astype(BF16) for j in range(3)]
         for k in range(heads):
 
             @pl.when(h == k)
@@ -465,18 +465,20 @@
     )
 
 
-def cut_blocks(table, axis, own, first, second):
-    rows, cols = own.shape[0] // 4, own.shape[1]
-
-    def body(s, a, b, c, *outs):
-        for r, out in zip((1, 3, 2, 0), outs):
-            at = pl.ds(pl.multiple_of((s[axis] ^ r) * rows, rows), rows)
-            total = a[at, :].astype(F32) + b[at, :].astype(F32) + c[at, :].astype(F32)
-            out[...] = total.astype(BF16)
-
-    outs = [shape((rows, cols))] * 4
-    operands = (own, first, second)
-    return call(
+def cut_blocks(table, left, right):
+    rows, cols = left[0].shape[0] // 4, left[0].shape[1]
+
+    def body(s, *refs):
+        for k, axis in enumerate((Y, X)):
+            a, b, c = refs[3 * k : 3 * k + 3]
+            for r, out in zip((1, 3, 2, 0), refs[6 + 4 * k : 10 + 4 * k]):
+                at = pl.ds(pl.multiple_of((s[axis] ^ r) * rows, rows), rows)
+                total = a[at, :].astype(F32) + b[at, :].astype(F32) + c[at, :].astype(F32)
+                out[...] = total.astype(BF16)
+
+    outs = [shape((rows, cols))] * 8
+    operands = (*left, *right)
+    cut = call(
         "cut_blocks",
         body,
         table,
@@ -485,8 +487,9 @@
         [whole(x) for x in operands],
         outs,
         [whole(o) for o in outs],
-        20,
-    )
+        24,
+    )
+    return cut[:4], cut[4:]
 
 
 def final_sums(table, sides):
@@ -568,22 +571,26 @@
     side_core = send(side, "co", 1)
     cumul = jnp.concatenate([lax.dynamic_slice_in_dim(cumul, here_z * per, per), note[:per]])
     table_pair = jnp.stack([*fixed, note[per, 0].astype(jnp.int32)]).astype(jnp.int32)
-    acc_pair = project(table, [[side]], (2,), weight, None, False)
-    near_core, acc_pair = tied((near_core, acc_pair))
     qkv_own = project(table, [[near], [near_core]], (2, 3), weight, acc_own, True)
-    far, side_core, qkv_own, table_pair, cumul = tied((far, side_core, qkv_own, table_pair, cumul))
+    turned = [turn(table, tied(([[activations], [core], [near], [near_core]], qkv_own))[0])]
+    far, side_core, qkv_own, table_pair, cumul, turned = tied(
+        (far, side_core, qkv_own, table_pair, cumul, turned)
+    )
     far_core = [send(x, "co", 1) for x in far]
     og_pair = send(tied((og_other, far))[0], "c0", 1)
+    local_own = local_grads(table, qkv_own, og_own, cumul, 0, 0, per // 2, None)
+    far_core, local_own = tied((far_core, local_own))
+    qkv_pair = project(
+        table_pair, [[side], [side_core], far, far_core], (2, 3, 0, 1), weight, None, True
+    )
+    qkv_own, _ = tied((qkv_own, qkv_pair))
     to_y = shard_states(table, qkv_own, og_own, cumul, 0, None)
-    far_core, to_y = tied((far_core, to_y))
-    qkv_pair = project(table_pair, [[side_core], far, far_core], (3, 0, 1), weight, acc_pair, True)
-    turned = [turn(table, tied(([[activations], [core], [near], [near_core]], qkv_pair))[0])]
-    og_pair, qkv_pair, turned = tied((og_pair, qkv_pair, turned))
+    og_pair, qkv_pair, to_y = tied((og_pair, qkv_pair, to_y))
 
     to_y = shard_states(table, qkv_pair, og_pair, cumul, 1, to_y)
     at_y = [send(to_y[r], "c2", r) for r in (1, 3, 2)]
     qkv_own, _ = tied((qkv_own, to_y[0]))
-    local_own = local_grads(table, qkv_own, og_own, cumul, 0, 0, per, None)
+    local_own = local_grads(table, qkv_own, og_own, cumul, 0, per // 2, per // 2, local_own)
     at_y, local_own = tied((at_y, local_own))
     before, after, prior, later, ring = ring_y(table, [to_y[0], at_y[0], at_y[2], at_y[1]])
     at_x = [send(ring, "c1", r) for r in (1, 3, 2)]
@@ -615,9 +622,7 @@
     turned, _ = tied((turned, r_one))
     own = weight_part(table, turned, lefts, rights, (0,), False)
     l_got, own = tied((l_got, own))
-    l_cut = cut_blocks(table, Y, own[0], *l_got)
-    r_got, _ = tied((r_got, l_cut))
-    r_cut = cut_blocks(table, X, own[1], *r_got)
+    l_cut, r_cut = cut_blocks(table, (own[0], *l_got), (own[1], *r_got))
     l_got = [send(x, "c2", by) for x, by in zip(l_cut, (1, 3, 2))]
     r_got = [send(x, "c1", by) for x, by in zip(r_cut, (1, 3, 2))]
     here, there = final_sums(table, ((l_cut[3], *l_got), (r_cut[3], *r_got)))

time: 182 us -> 180 us (0.989)
  Pallas kernels: 76 us -> 72.6 us
  local copies, waits for them, and re-layouts: 9.21 us -> 12.5 us
    pallas_call x24 -> x23, Pallas kernels: 76 us -> 72.6 us  [call(): pl.pallas_call(body, grid_spec=pltpu.PrefetchScalarGridSpec(num_scalar_pr...]
    ppermute x33, starting transfers between devices: 36.8 us -> 35 us  [send(): lax.ppermute(x, axis, [(i, i ^ by) for i in range(lax.axis_size(axis))])]
  transfers between devices with their start and end apart: 35 -> 35, of which waited for: 15 -> 15; matrix products, arithmetic and copies ran while one was open for 6% -> 7% of each run, Pallas kernels for 33% -> 32%
where the time goes in v6:
time: 180 us
  Pallas kernels  72.6 us (40%)
  waiting for transfers between devices  48.3 us (27%)
  starting transfers between devices  42 us (23%)
  local copies, waits for them, and re-layouts  12.5 us (7%)
  other arithmetic  2.67 us (1%)
    pallas_call x23, Pallas kernels, call(): pl.pallas_call(body, grid_spec=pltpu.PrefetchScalarGridSpec(num_scalar_pr...  72.6 us
    ppermute x33, waiting for transfers between devices, send(): lax.ppermute(x, axis, [(i, i ^ by) for i in range(lax.axis_size(axis))])  48.3 us
    ppermute x33, starting transfers between devices, send(): lax.ppermute(x, axis, [(i, i ^ by) for i in range(lax.axis_size(axis))])  35 us
    ppermute x2, starting transfers between devices, across(): return lax.ppermute(x, ('c0', 'zl'), [(0, 3), (1, 2), (2, 1), (3, 0)])  6.98 us
  transfers between devices with their start and end apart: 35, of which 15 were waited for; matrix products, arithmetic and copies ran while one was open for 7% of the time, Pallas kernels for 32%

profile of v6, /device:TPU:0, one launch (start us, length us, event | category | flops | bytes accessed | tf_op | source)
XLA Modules:
  0.0 179.7 jit_solution(10236894469008872776)
XLA Ops:
  0.0 4.1 %collective-permute-start.1 = (bf16[512,768]{1,0:T(8,128)(2,1)}, bf16[512,768]{1,0:T(8,128)(2,1)}, u32[]{:S(2)}, u32[]{:S(2)}) collective-permute-start(bf16[512,768]{1,0:T(8,128)(2,1)} %refs_0_.2), channel_id=1, source_target_pairs={{0,66},{2,64},{64,2},{66,0},{1,67},{3,65},{65,3},{67,1},{4,70},{6,... | collective-permute-start | bytes 2359304 | tf_op jit(solution)/shard_map/ppermute | solution.py:26
  8.1 1.5 collective-permute-start.3
  9.7 2.2 %constant_dynamic-slice_fusion = (bf16[512,512]{1,0:T(8,128)(2,1)}, bf16[512,512]{1,0:T(8,128)(2,1)}) fusion(bf16[512,1024]{1,0:T(8,128)(2,1)} %param.9, s32[]{:T(128)S(6)} %select_n.15, s32[]{:T(128)S(6)} %select_n.13), kind=kLoop, calls=%fused_computation.6 | loop fusion | bytes 2097160 | tf_op jit(solution)/shard_map/dynamic_slice | solution.py:563
  15.1 5.3 %project.3.refs_4_ = f32[3,512,512]{2,1,0:T(8,128)S(1)} custom-call(s32[7]{0:T(128)S(1)} %stack.39.s, bf16[512,768]{1,0:T(8,128)(2,1)S(1)} %copy-done.1, bf16[512,768]{1,0:T(8,128)(2,1)S(1)} %copy-done.4, bf16[3,3072,1024]{2,1,0:T(8,128)(2,1)} %bitcast.32, bf16[3,3072,1024]{2,1,0:T(8,128)(2,1)} %bitcast.33), custom_call_target="tpu_custom_call" | custom-call | flops 1 | bytes 1 | tf_op jit(solution)/shard_map/project/pallas_call | solution.py:34
  20.4 3.8 %collective-permute-done.3 = f32[8,512]{1,0:T(8,128)} collective-permute-done((f32[8,512]{1,0:T(8,128)}, f32[8,512]{1,0:T(8,128)}, u32[]{:S(2)}, u32[]{:S(2)}) %collective-permute-start.3) | collective-permute-done | bytes 16416 | tf_op jit(solution)/shard_map/ppermute | solution.py:22
  24.8 1.8 slice.20
  26.6 1.8 slice.21
  28.4 2.9 %collective-permute-start.5 = (bf16[256,768]{1,0:T(8,128)(2,1)}, bf16[256,768]{1,0:T(8,128)(2,1)S(1)}, u32[]{:S(2)}, u32[]{:S(2)}) collective-permute-start(bf16[256,768]{1,0:T(8,128)(2,1)} %slice.21), channel_id=1, source_target_pairs={{0,66},{2,64},{64,2},{66,0},{1,67},{3,65},{65,3},{67,1},{4,70},{6,... | collective-permute-start | bytes 1179656 | tf_op jit(solution)/shard_map/ppermute | solution.py:26
  34.7 5.8 %project.4.qkv_ref = bf16[3,512,512]{2,1,0:T(8,128)(2,1)S(1)} custom-call(s32[7]{0:T(128)S(1)} %stack.39.s, bf16[512,768]{1,0:T(8,128)(2,1)} %collective-permute-done.refs_0_.refs_2_, bf16[512,768]{1,0:T(8,128)(2,1)} %collective-permute-done.7.refs_1_.refs_3_, bf16[3,3072,1024]{2,1,0:T(8,128)(2,1)} %bitcast.34, bf16[3,3072,1024]{2,1,0:T(8,128)(2,1)} %bitcast.35, ...), custom_call_target="tpu_custom_call" | custom-call | flops 1 | bytes 1 | tf_op jit(solution)/shard_map/project/pallas_call | solution.py:34
  40.6 3.4 %turn.2 = bf16[16,2,96,512]{3,2,1,0:T(8,128)(2,1)S(1)} custom-call(s32[7]{0:T(128)S(1)} %stack.39.s, bf16[512,768]{1,0:T(8,128)(2,1)S(1)} %copy-done.2, bf16[512,768]{1,0:T(8,128)(2,1)S(1)} %copy-done.5, bf16[512,768]{1,0:T(8,128)(2,1)} %collective-permute-done.refs_0_.refs_2_, bf16[512,768]{1,0:T(8,128)(2,1)} %collective-permute-done.7.refs_1_.refs_3_), custom_call_target="tpu_custom_call" | custom-call | flops 1 | bytes 1 | tf_op jit(solution)/shard_map/turn/pallas_call | solution.py:34
  44.1 1.9 %collective-permute-start.8 = (bf16[512,512]{1,0:T(8,128)(2,1)S(1)}, bf16[512,512]{1,0:T(8,128)(2,1)S(1)}, u32[]{:S(2)}, u32[]{:S(2)}) collective-permute-start(bf16[512,512]{1,0:T(8,128)(2,1)S(1)} %copy-done.6), channel_id=1, source_target_pairs={{0,64},{64,0},{1,65},{65,1},{2,66},{66,2},{3,67},{67,3},{4,68},{68... | collective-permute-start | bytes 1572872 | tf_op jit(solution)/shard_map/ppermute | solution.py:22
  46.5 3.3 %local_grads.4 = (bf16[3,512,512]{2,1,0:T(8,128)(2,1)S(1)}, bf16[3,512,512]{2,1,0:T(8,128)(2,1)S(1)}) custom-call(s32[7]{0:T(128)S(1)} %stack.39.s, bf16[3,512,512]{2,1,0:T(8,128)(2,1)S(1)} %project.4.qkv_ref, bf16[512,512]{1,0:T(8,128)(2,1)S(1)} %copy-done, f32[8,512]{1,0:T(8,128)S(1)} %pad_maximum_fusion.cum_ref), custom_call_target="tpu_custom_call" | custom-call | flops 1 | bytes 1 | tf_op jit(solution)/shard_map/local_grads/pallas_call | solution.py:34
  49.8 8.8 %project.5.qkv_ref = bf16[3,512,512]{2,1,0:T(8,128)(2,1)S(1)} custom-call(s32[7]{0:T(128)S(1)} %stack.41.s, bf16[512,768]{1,0:T(8,128)(2,1)} %collective-permute-done.1.refs_0_.refs_4_, bf16[512,768]{1,0:T(8,128)(2,1)} %collective-permute-done.6.refs_1_.refs_5_, bf16[256,768]{1,0:T(8,128)(2,1)} %collective-permute-done.4.refs_2_.refs_0_, ...), custom_call_target="tpu_custom_call" | custom-call | flops 1 | bytes 1 | tf_op jit(solution)/shard_map/project/pallas_call | solution.py:34
  58.6 2.3 %shard_states.2 = (bf16[528,128]{1,0:T(8,128)(2,1)S(1)}, bf16[528,128]{1,0:T(8,128)(2,1)S(1)}, bf16[528,128]{1,0:T(8,128)(2,1)S(1)}, bf16[528,128]{1,0:T(8,128)(2,1)S(1)}) custom-call(s32[7]{0:T(128)S(1)} %stack.39.s, bf16[3,512,512]{2,1,0:T(8,128)(2,1)S(1)} %project.4.qkv_ref, bf16[512,512]{1,0:T(8,128)(2,1)S(1)} %copy-done, ...), custom_call_target="tpu_custom_call" | custom-call | flops 1 | bytes 1 | tf_op jit(solution)/shard_map/shard_states/pallas_call | solution.py:34
  60.9 2.3 %shard_states.3 = (bf16[528,128]{1,0:T(8,128)(2,1)S(1)}, bf16[528,128]{1,0:T(8,128)(2,1)S(1)}, bf16[528,128]{1,0:T(8,128)(2,1)S(1)}, bf16[528,128]{1,0:T(8,128)(2,1)S(1)}) custom-call(s32[7]{0:T(128)S(1)} %stack.39.s, bf16[3,512,512]{2,1,0:T(8,128)(2,1)S(1)} %project.5.qkv_ref, bf16[512,512]{1,0:T(8,128)(2,1)S(1)} %collective-permute-done.8.og_ref, ...), custom_call_target="tpu_custom_call" | custom-call | flops 1 | bytes 1 | tf_op jit(solution)/shard_map/shard_states/pallas_call | solution.py:34
  63.2 1.7 collective-permute-start.11
  64.9 2.2 %collective-permute-start.12 = (bf16[528,128]{1,0:T(8,128)(2,1)S(1)}, bf16[528,128]{1,0:T(8,128)(2,1)S(1)}, u32[]{:S(2)}, u32[]{:S(2)}) collective-permute-start(bf16[528,128]{1,0:T(8,128)(2,1)S(1)} %get-tuple-element.159), channel_id=1, source_target_pairs={{0,12},{4,8},{8,4},{12,0},{1,13},{5,9},{9,5},{13,1},{2,14},{6,10},... | collective-permute-start | bytes 405512 | tf_op jit(solution)/shard_map/ppermute | solution.py:22
  67.8 3.3 %local_grads.5 = (bf16[3,512,512]{2,1,0:T(8,128)(2,1)S(1)}, bf16[3,512,512]{2,1,0:T(8,128)(2,1)S(1)}) custom-call(s32[7]{0:T(128)S(1)} %stack.39.s, bf16[3,512,512]{2,1,0:T(8,128)(2,1)S(1)} %project.4.qkv_ref, bf16[512,512]{1,0:T(8,128)(2,1)S(1)} %copy-done, f32[8,512]{1,0:T(8,128)S(1)} %pad_maximum_fusion.cum_ref, ...), custom_call_target="tpu_custom_call", output_to_operand_aliasing={{0}: (4, {}), {1}: (5, {})} | custom-call | flops 1 | bytes 1 | tf_op jit(solution)/shard_map/local_grads/pallas_call | solution.py:34
  71.1 1.6 collective-permute-done.12.d
  72.7 1.5 collective-permute-done.13.c
  74.9 3.1 %collective-permute-start.16 = (bf16[528,128]{1,0:T(8,128)(2,1)S(1)}, bf16[528,128]{1,0:T(8,128)(2,1)S(1)}, u32[]{:S(2)}, u32[]{:S(2)}) collective-permute-start(bf16[528,128]{1,0:T(8,128)(2,1)S(1)} %get-tuple-element.169.a), channel_id=1, source_target_pairs={{0,32},{16,48},{32,0},{48,16},{1,33},{17,49},{33,1},{49,17},{2,34}... | collective-permute-start | bytes 405512 | tf_op jit(solution)/shard_map/ppermute | solution.py:22
  79.1 3.3 %local_grads.6 = (bf16[3,512,512]{2,1,0:T(8,128)(2,1)S(1)}, bf16[3,512,512]{2,1,0:T(8,128)(2,1)S(1)}) custom-call(s32[7]{0:T(128)S(1)} %stack.41.s, bf16[3,512,512]{2,1,0:T(8,128)(2,1)S(1)} %project.5.qkv_ref, bf16[512,512]{1,0:T(8,128)(2,1)S(1)} %collective-permute-done.8.og_ref, f32[8,512]{1,0:T(8,128)S(1)} %pad_maximum_fusion.cum_ref), custom_call_target="tpu_custom_call" | custom-call | flops 1 | bytes 1 | tf_op jit(solution)/shard_map/local_grads/pallas_call | solution.py:34
  82.4 2.0 %collective-permute-done.15.d = bf16[528,128]{1,0:T(8,128)(2,1)S(1)} collective-permute-done((bf16[528,128]{1,0:T(8,128)(2,1)S(1)}, bf16[528,128]{1,0:T(8,128)(2,1)S(1)}, u32[]{:S(2)}, u32[]{:S(2)}) %collective-permute-start.15) | collective-permute-done | bytes 135200 | tf_op jit(solution)/shard_map/ppermute | solution.py:22
  85.4 2.2 %collective-permute-start.18 = (bf16[512,128]{1,0:T(8,128)(2,1)S(1)}, bf16[512,128]{1,0:T(8,128)(2,1)S(1)}, u32[]{:S(2)}, u32[]{:S(2)}) collective-permute-start(bf16[512,128]{1,0:T(8,128)(2,1)S(1)} %get-tuple-element.181), channel_id=1, source_target_pairs={{0,12},{4,8},{8,4},{12,0},{1,13},{5,9},{9,5},{13,1},{2,14},{6,10},... | collective-permute-start | bytes 393224 | tf_op jit(solution)/shard_map/ppermute | solution.py:22
  87.6 1.9 %collective-permute-start.19 = (bf16[512,128]{1,0:T(8,128)(2,1)S(1)}, bf16[512,128]{1,0:T(8,128)(2,1)S(1)}, u32[]{:S(2)}, u32[]{:S(2)}) collective-permute-start(bf16[512,128]{1,0:T(8,128)(2,1)S(1)} %get-tuple-element.182), channel_id=1, source_target_pairs={{0,8},{4,12},{8,0},{12,4},{1,9},{5,13},{9,1},{13,5},{2,10},{6,14},... | collective-permute-start | bytes 393224 | tf_op jit(solution)/shard_map/ppermute | solution.py:22
  89.5 3.3 %local_grads.7 = (bf16[3,512,512]{2,1,0:T(8,128)(2,1)S(1)}, bf16[3,512,512]{2,1,0:T(8,128)(2,1)S(1)}) custom-call(s32[7]{0:T(128)S(1)} %stack.41.s, bf16[3,512,512]{2,1,0:T(8,128)(2,1)S(1)} %project.5.qkv_ref, bf16[512,512]{1,0:T(8,128)(2,1)S(1)} %collective-permute-done.8.og_ref, ...), custom_call_target="tpu_custom_call", output_to_operand_aliasing={{0}: (4, {}), {1}: (5, {})} | custom-call | flops 1 | bytes 1 | tf_op jit(solution)/shard_map/local_grads/pallas_call | solution.py:34
  92.8 3.6 %turn.3 = bf16[16,2,96,512]{3,2,1,0:T(8,128)(2,1)S(1)} custom-call(s32[7]{0:T(128)S(1)} %stack.39.s, bf16[256,768]{1,0:T(8,128)(2,1)} %collective-permute-done.4.refs_2_.refs_0_, bf16[256,768]{1,0:T(8,128)(2,1)S(1)} %collective-permute-done.5.refs_3_.refs_1_, bf16[256,768]{1,0:T(8,128)(2,1)S(1)} %collective-permute-done.9.refs_4_.refs_2_, ...), custom_call_target="tpu_custom_call" | custom-call | flops 1 | bytes 1 | tf_op jit(solution)/shard_map/turn/pallas_call | solution.py:34
  96.4 2.5 %whole_grads.2 = (bf16[512,768]{1,0:T(8,128)(2,1)S(1)}, bf16[512,768]{1,0:T(8,128)(2,1)S(1)}) custom-call(s32[7]{0:T(128)S(1)} %stack.39.s, bf16[3,512,512]{2,1,0:T(8,128)(2,1)S(1)} %get-tuple-element.199.local_ref, bf16[3,512,512]{2,1,0:T(8,128)(2,1)S(1)} %get-tuple-element.200.ready_ref, bf16[512,128]{1,0:T(8,128)(2,1)S(1)} %get-tuple-element.184.a, ...), custom_call_target="tpu_custom_call" | custom-call | flops 1 | bytes 1 | tf_op jit(solution)/shard_map/whole_grads/pallas_call | solution.py:34
  98.9 2.5 %whole_grads.3 = (bf16[512,768]{1,0:T(8,128)(2,1)S(1)}, bf16[512,768]{1,0:T(8,128)(2,1)S(1)}) custom-call(s32[7]{0:T(128)S(1)} %stack.39.s, bf16[3,512,512]{2,1,0:T(8,128)(2,1)S(1)} %get-tuple-element.205.local_ref, bf16[3,512,512]{2,1,0:T(8,128)(2,1)S(1)} %get-tuple-element.206.ready_ref, bf16[512,128]{1,0:T(8,128)(2,1)S(1)} %get-tuple-element.184.a, ...), custom_call_target="tpu_custom_call" | custom-call | flops 1 | bytes 1 | tf_op jit(solution)/shard_map/whole_grads/pallas_call | solution.py:34
  101.4 3.1 %weight_part.3 = (bf16[384,768]{1,0:T(8,128)(2,1)S(1)}, bf16[384,768]{1,0:T(8,128)(2,1)S(1)}, bf16[384,768]{1,0:T(8,128)(2,1)S(1)}, bf16[384,768]{1,0:T(8,128)(2,1)S(1)}) custom-call(s32[7]{0:T(128)S(1)} %stack.39.s, bf16[4,4,192,512]{3,2,1,0:T(8,128)(2,1)S(1)} %bitcast.20, bf16[4,4,192,512]{3,2,1,0:T(8,128)(2,1)S(1)} %bitcast.21, ...), custom_call_target="tpu_custom_call" | custom-call | flops 1 | bytes 1 | tf_op jit(solution)/shard_map/weight_part/pallas_call | solution.py:34
  104.6 2.3 %collective-permute-start.21 = (bf16[384,768]{1,0:T(8,128)(2,1)S(1)}, bf16[384,768]{1,0:T(8,128)(2,1)S(1)}, u32[]{:S(2)}, u32[]{:S(2)}) collective-permute-start(bf16[384,768]{1,0:T(8,128)(2,1)S(1)} %get-tuple-element.214), channel_id=1, source_target_pairs={{0,48},{16,32},{32,16},{48,0},{1,49},{17,33},{33,17},{49,1},{2,50}... | collective-permute-start | bytes 1769480 | tf_op jit(solution)/shard_map/ppermute | solution.py:22
  107.0 2.0 %collective-permute-start.25 = (bf16[384,768]{1,0:T(8,128)(2,1)S(1)}, bf16[384,768]{1,0:T(8,128)(2,1)S(1)}, u32[]{:S(2)}, u32[]{:S(2)}) collective-permute-start(bf16[384,768]{1,0:T(8,128)(2,1)S(1)} %get-tuple-element.224), channel_id=1, source_target_pairs={{0,12},{4,8},{8,4},{12,0},{1,13},{5,9},{9,5},{13,1},{2,14},{6,10},... | collective-permute-start | bytes 1769480 | tf_op jit(solution)/shard_map/ppermute | solution.py:22
  109.0 8.4 %weight_part.4 = (bf16[768,768]{1,0:T(8,128)(2,1)S(1)}, bf16[768,768]{1,0:T(8,128)(2,1)S(1)}, bf16[768,768]{1,0:T(8,128)(2,1)S(1)}, bf16[768,768]{1,0:T(8,128)(2,1)S(1)}) custom-call(s32[7]{0:T(128)S(1)} %stack.39.s, bf16[4,4,192,512]{3,2,1,0:T(8,128)(2,1)S(1)} %bitcast.22, bf16[4,4,192,512]{3,2,1,0:T(8,128)(2,1)S(1)} %bitcast.23, ...), custom_call_target="tpu_custom_call" | custom-call | flops 1 | bytes 1 | tf_op jit(solution)/shard_map/weight_part/pallas_call | solution.py:34
  117.4 1.6 collective-permute-done.21.d
  120.2 1.5 add_halves.2
  124.7 1.6 collective-permute-start.27
  126.3 3.1 %weight_part.5 = (bf16[768,768]{1,0:T(8,128)(2,1)S(1)}, bf16[768,768]{1,0:T(8,128)(2,1)S(1)}) custom-call(s32[7]{0:T(128)S(1)} %stack.39.s, bf16[4,4,192,512]{3,2,1,0:T(8,128)(2,1)S(1)} %bitcast.24, bf16[4,4,192,512]{3,2,1,0:T(8,128)(2,1)S(1)} %bitcast.25, bf16[4,4,192,512]{3,2,1,0:T(8,128)(2,1)S(1)} %bitcast.30, bf16[4,4,192,512]{3,2,1,0:T(8,128)(2,1)S(1)} %bitcast.31, ...), custom_call_target="tpu_custom_call" | custom-call | flops 1 | bytes 1 | tf_op jit(solution)/shard_map/weight_part/pallas_call | solution.py:34
  129.5 18.6 %collective-permute-done.23.refs_2_ = bf16[768,768]{1,0:T(8,128)(2,1)S(1)} collective-permute-done((bf16[768,768]{1,0:T(8,128)(2,1)S(1)}, bf16[768,768]{1,0:T(8,128)(2,1)S(1)}, u32[]{:S(2)}, u32[]{:S(2)}) %collective-permute-start.23) | collective-permute-done | bytes 1179680 | tf_op jit(solution)/shard_map/ppermute | solution.py:22
  148.1 2.8 %collective-permute-done.27.refs_5_ = bf16[768,768]{1,0:T(8,128)(2,1)S(1)} collective-permute-done((bf16[768,768]{1,0:T(8,128)(2,1)S(1)}, bf16[768,768]{1,0:T(8,128)(2,1)S(1)}, u32[]{:S(2)}, u32[]{:S(2)}) %collective-permute-start.27) | collective-permute-done | bytes 1179680 | tf_op jit(solution)/shard_map/ppermute | solution.py:22
  152.5 2.0 %collective-permute-start.29 = (bf16[192,768]{1,0:T(8,128)(2,1)S(1)}, bf16[192,768]{1,0:T(8,128)(2,1)S(1)}, u32[]{:S(2)}, u32[]{:S(2)}) collective-permute-start(bf16[192,768]{1,0:T(8,128)(2,1)S(1)} %get-tuple-element.239), channel_id=1, source_target_pairs={{0,12},{4,8},{8,4},{12,0},{1,13},{5,9},{9,5},{13,1},{2,14},{6,10},... | collective-permute-start | bytes 884744 | tf_op jit(solution)/shard_map/ppermute | solution.py:22
  154.5 2.1 %collective-permute-start.30 = (bf16[192,768]{1,0:T(8,128)(2,1)S(1)}, bf16[192,768]{1,0:T(8,128)(2,1)S(1)}, u32[]{:S(2)}, u32[]{:S(2)}) collective-permute-start(bf16[192,768]{1,0:T(8,128)(2,1)S(1)} %get-tuple-element.240), channel_id=1, source_target_pairs={{0,8},{4,12},{8,0},{12,4},{1,9},{5,13},{9,1},{13,5},{2,10},{6,14},... | collective-permute-start | bytes 884744 | tf_op jit(solution)/shard_map/ppermute | solution.py:22
  157.6 1.5 collective-permute-start.32
  159.0 1.7 collective-permute-done.28.refs_1_
  162.1 3.0 %collective-permute-done.29.refs_2_ = bf16[192,768]{1,0:T(8,128)(2,1)S(1)} collective-permute-done((bf16[192,768]{1,0:T(8,128)(2,1)S(1)}, bf16[192,768]{1,0:T(8,128)(2,1)S(1)}, u32[]{:S(2)}, u32[]{:S(2)}) %collective-permute-start.29) | collective-permute-done | bytes 294944 | tf_op jit(solution)/shard_map/ppermute | solution.py:22
  165.6 3.3 %collective-permute-done.33.refs_7_ = bf16[192,768]{1,0:T(8,128)(2,1)S(1)} collective-permute-done((bf16[192,768]{1,0:T(8,128)(2,1)S(1)}, bf16[192,768]{1,0:T(8,128)(2,1)S(1)}, u32[]{:S(2)}, u32[]{:S(2)}) %collective-permute-start.33) | collective-permute-done | bytes 294944 | tf_op jit(solution)/shard_map/ppermute | solution.py:22
  169.8 1.9 %collective-permute-start.34 = (bf16[2,96,768]{2,1,0:T(8,128)(2,1)S(1)}, bf16[2,96,768]{2,1,0:T(8,128)(2,1)S(1)}, u32[]{:S(2)}, u32[]{:S(2)}) collective-permute-start(bf16[2,96,768]{2,1,0:T(8,128)(2,1)S(1)} %get-tuple-element.246), channel_id=1, source_target_pairs={{0,64},{64,0},{1,65},{65,1},{2,66},{66,2},{3,67},{67,3},{4,68},{68... | collective-permute-start | bytes 884744 | tf_op jit(solution)/shard_map/ppermute | solution.py:22
  171.6 6.4 %collective-permute-done.34.there_ref = bf16[2,96,768]{2,1,0:T(8,128)(2,1)S(1)} collective-permute-done((bf16[2,96,768]{2,1,0:T(8,128)(2,1)S(1)}, bf16[2,96,768]{2,1,0:T(8,128)(2,1)S(1)}, u32[]{:S(2)}, u32[]{:S(2)}) %collective-permute-start.34) | collective-permute-done | bytes 294944 | tf_op jit(solution)/shard_map/ppermute | solution.py:22
  178.1 1.6 finish.1
  (76 shorter events, 23.6 us)
Async XLA Ops:
  0.0 12.0 %collective-permute-start.2 = (bf16[512,768]{1,0:T(8,128)(2,1)}, bf16[512,768]{1,0:T(8,128)(2,1)S(1)}, u32[]{:S(2)}, u32[]{:S(2)}) collective-permute-start(bf16[512,768]{1,0:T(8,128)(2,1)} %refs_0_.2), channel_id=1, source_target_pairs={{0,1},{1,0},{2,3},{3,2},{4,5},{5,4},{6,7},{7,6},{8,9},{9,8},{10,11... | collective-permute-start | bytes 2359304 | tf_op jit(solution)/shard_map/ppermute | solution.py:22
  0.0 24.2 %collective-permute-start.1 = (bf16[512,768]{1,0:T(8,128)(2,1)}, bf16[512,768]{1,0:T(8,128)(2,1)}, u32[]{:S(2)}, u32[]{:S(2)}) collective-permute-start(bf16[512,768]{1,0:T(8,128)(2,1)} %refs_0_.2), channel_id=1, source_target_pairs={{0,66},{2,64},{64,2},{66,0},{1,67},{3,65},{65,3},{67,1},{4,70},{6,... | collective-permute-start | bytes 2359304 | tf_op jit(solution)/shard_map/ppermute | solution.py:26
  4.1 20.2 %collective-permute-start = (bf16[512,768]{1,0:T(8,128)(2,1)}, bf16[512,768]{1,0:T(8,128)(2,1)}, u32[]{:S(2)}, u32[]{:S(2)}) collective-permute-start(bf16[512,768]{1,0:T(8,128)(2,1)} %refs_0_.2), channel_id=1, source_target_pairs={{0,2},{2,0},{1,3},{3,1},{4,6},{6,4},{5,7},{7,5},{8,10},{10,8},{9,1... | collective-permute-start | bytes 2359304 | tf_op jit(solution)/shard_map/ppermute | solution.py:22
  8.1 16.1 %collective-permute-start.3 = (f32[8,512]{1,0:T(8,128)}, f32[8,512]{1,0:T(8,128)}, u32[]{:S(2)}, u32[]{:S(2)}) collective-permute-start(f32[8,512]{1,0:T(8,128)} %concatenate.6), channel_id=1, source_target_pairs={{0,64},{64,0},{1,65},{65,1},{2,66},{66,2},{3,67},{67,3},{4,68},{68... | collective-permute-start | bytes 49160 | tf_op jit(solution)/shard_map/ppermute | solution.py:22
  12.0 0.9 copy-start.3
  12.9 1.1 copy-start.1
  14.0 1.1 copy-start.4
  24.3 10.4 %collective-permute-start.7 = (bf16[512,768]{1,0:T(8,128)(2,1)}, bf16[512,768]{1,0:T(8,128)(2,1)}, u32[]{:S(2)}, u32[]{:S(2)}) collective-permute-start(bf16[512,768]{1,0:T(8,128)(2,1)} %collective-permute-done.refs_0_.refs_2_), channel_id=1, source_target_pairs={{0,1},{1,0},{2,3},{3,2},{4,5},{5,4},{6,7},{7,6},{8,9},{9,8},{10,11... | collective-permute-start | bytes 2359304 | tf_op jit(solution)/shard_map/ppermute | solution.py:22
  24.3 19.8 %collective-permute-start.6 = (bf16[512,768]{1,0:T(8,128)(2,1)}, bf16[512,768]{1,0:T(8,128)(2,1)}, u32[]{:S(2)}, u32[]{:S(2)}) collective-permute-start(bf16[512,768]{1,0:T(8,128)(2,1)} %collective-permute-done.1.refs_0_.refs_4_), channel_id=1, source_target_pairs={{0,1},{1,0},{2,3},{3,2},{4,5},{5,4},{6,7},{7,6},{8,9},{9,8},{10,11... | collective-permute-start | bytes 2359304 | tf_op jit(solution)/shard_map/ppermute | solution.py:22
  28.4 15.7 %collective-permute-start.5 = (bf16[256,768]{1,0:T(8,128)(2,1)}, bf16[256,768]{1,0:T(8,128)(2,1)S(1)}, u32[]{:S(2)}, u32[]{:S(2)}) collective-permute-start(bf16[256,768]{1,0:T(8,128)(2,1)} %slice.21), channel_id=1, source_target_pairs={{0,66},{2,64},{64,2},{66,0},{1,67},{3,65},{65,3},{67,1},{4,70},{6,... | collective-permute-start | bytes 1179656 | tf_op jit(solution)/shard_map/ppermute | solution.py:26
  31.2 12.8 %collective-permute-start.4 = (bf16[256,768]{1,0:T(8,128)(2,1)}, bf16[256,768]{1,0:T(8,128)(2,1)}, u32[]{:S(2)}, u32[]{:S(2)}) collective-permute-start(bf16[256,768]{1,0:T(8,128)(2,1)} %slice.20), channel_id=1, source_target_pairs={{0,2},{2,0},{1,3},{3,1},{4,6},{6,4},{5,7},{7,5},{8,10},{10,8},{9,1... | collective-permute-start | bytes 1179656 | tf_op jit(solution)/shard_map/ppermute | solution.py:22
  34.7 5.8 %copy-start.2 = (bf16[512,768]{1,0:T(8,128)(2,1)S(1)}, bf16[512,768]{1,0:T(8,128)(2,1)}, u32[]{:S(2)}) copy-start(bf16[512,768]{1,0:T(8,128)(2,1)} %refs_0_.2) | copy-start | bytes 2359300
  34.7 5.8 %copy-start.5 = (bf16[512,768]{1,0:T(8,128)(2,1)S(1)}, bf16[512,768]{1,0:T(8,128)(2,1)}, u32[]{:S(2)}) copy-start(bf16[512,768]{1,0:T(8,128)(2,1)} %copy-done.3) | copy-start | bytes 2359300
  40.6 3.5 %copy-start.6 = (bf16[512,512]{1,0:T(8,128)(2,1)S(1)}, bf16[512,512]{1,0:T(8,128)(2,1)}, u32[]{:S(2)}) copy-start(bf16[512,512]{1,0:T(8,128)(2,1)} %get-tuple-element.137) | copy-start | bytes 1572868
  40.6 5.9 %copy-start = (bf16[512,512]{1,0:T(8,128)(2,1)S(1)}, bf16[512,512]{1,0:T(8,128)(2,1)}, u32[]{:S(2)}) copy-start(bf16[512,512]{1,0:T(8,128)(2,1)} %get-tuple-element.247.og_ref) | copy-start | bytes 1572868
  44.1 16.8 %collective-permute-start.8 = (bf16[512,512]{1,0:T(8,128)(2,1)S(1)}, bf16[512,512]{1,0:T(8,128)(2,1)S(1)}, u32[]{:S(2)}, u32[]{:S(2)}) collective-permute-start(bf16[512,512]{1,0:T(8,128)(2,1)S(1)} %copy-done.6), channel_id=1, source_target_pairs={{0,64},{64,0},{1,65},{65,1},{2,66},{66,2},{3,67},{67,3},{4,68},{68... | collective-permute-start | bytes 1572872 | tf_op jit(solution)/shard_map/ppermute | solution.py:22
  46.0 3.8 %collective-permute-start.9 = (bf16[256,768]{1,0:T(8,128)(2,1)}, bf16[256,768]{1,0:T(8,128)(2,1)S(1)}, u32[]{:S(2)}, u32[]{:S(2)}) collective-permute-start(bf16[256,768]{1,0:T(8,128)(2,1)} %collective-permute-done.4.refs_2_.refs_0_), channel_id=1, source_target_pairs={{0,1},{1,0},{2,3},{3,2},{4,5},{5,4},{6,7},{7,6},{8,9},{9,8},{10,11... | collective-permute-start | bytes 1179656 | tf_op jit(solution)/shard_map/ppermute | solution.py:22
  46.0 3.8 %collective-permute-start.10 = (bf16[256,768]{1,0:T(8,128)(2,1)S(1)}, bf16[256,768]{1,0:T(8,128)(2,1)S(1)}, u32[]{:S(2)}, u32[]{:S(2)}) collective-permute-start(bf16[256,768]{1,0:T(8,128)(2,1)S(1)} %collective-permute-done.5.refs_3_.refs_1_), channel_id=1, source_target_pairs={{0,1},{1,0},{2,3},{3,2},{4,5},{5,4},{6,7},{7,6},{8,9},{9,8},{10,11... | collective-permute-start | bytes 1179656 | tf_op jit(solution)/shard_map/ppermute | solution.py:22
  63.2 7.8 %collective-permute-start.11 = (bf16[528,128]{1,0:T(8,128)(2,1)S(1)}, bf16[528,128]{1,0:T(8,128)(2,1)S(1)}, u32[]{:S(2)}, u32[]{:S(2)}) collective-permute-start(bf16[528,128]{1,0:T(8,128)(2,1)S(1)} %get-tuple-element.158), channel_id=1, source_target_pairs={{0,4},{4,0},{8,12},{12,8},{1,5},{5,1},{9,13},{13,9},{2,6},{6,2},{1... | collective-permute-start | bytes 405512 | tf_op jit(solution)/shard_map/ppermute | solution.py:22
  64.9 7.8 %collective-permute-start.12 = (bf16[528,128]{1,0:T(8,128)(2,1)S(1)}, bf16[528,128]{1,0:T(8,128)(2,1)S(1)}, u32[]{:S(2)}, u32[]{:S(2)}) collective-permute-start(bf16[528,128]{1,0:T(8,128)(2,1)S(1)} %get-tuple-element.159), channel_id=1, source_target_pairs={{0,12},{4,8},{8,4},{12,0},{1,13},{5,9},{9,5},{13,1},{2,14},{6,10},... | collective-permute-start | bytes 405512 | tf_op jit(solution)/shard_map/ppermute | solution.py:22
  67.1 7.1 %collective-permute-start.13 = (bf16[528,128]{1,0:T(8,128)(2,1)S(1)}, bf16[528,128]{1,0:T(8,128)(2,1)S(1)}, u32[]{:S(2)}, u32[]{:S(2)}) collective-permute-start(bf16[528,128]{1,0:T(8,128)(2,1)S(1)} %get-tuple-element.160), channel_id=1, source_target_pairs={{0,8},{4,12},{8,0},{12,4},{1,9},{5,13},{9,1},{13,5},{2,10},{6,14},... | collective-permute-start | bytes 405512 | tf_op jit(solution)/shard_map/ppermute | solution.py:22
  74.9 7.5 %collective-permute-start.16 = (bf16[528,128]{1,0:T(8,128)(2,1)S(1)}, bf16[528,128]{1,0:T(8,128)(2,1)S(1)}, u32[]{:S(2)}, u32[]{:S(2)}) collective-permute-start(bf16[528,128]{1,0:T(8,128)(2,1)S(1)} %get-tuple-element.169.a), channel_id=1, source_target_pairs={{0,32},{16,48},{32,0},{48,16},{1,33},{17,49},{33,1},{49,17},{2,34}... | collective-permute-start | bytes 405512 | tf_op jit(solution)/shard_map/ppermute | solution.py:22
  78.0 6.4 %collective-permute-start.15 = (bf16[528,128]{1,0:T(8,128)(2,1)S(1)}, bf16[528,128]{1,0:T(8,128)(2,1)S(1)}, u32[]{:S(2)}, u32[]{:S(2)}) collective-permute-start(bf16[528,128]{1,0:T(8,128)(2,1)S(1)} %get-tuple-element.169.a), channel_id=1, source_target_pairs={{0,48},{16,32},{32,16},{48,0},{1,49},{17,33},{33,17},{49,1},{2,50}... | collective-permute-start | bytes 405512 | tf_op jit(solution)/shard_map/ppermute | solution.py:22
  79.1 5.4 %collective-permute-start.14 = (bf16[528,128]{1,0:T(8,128)(2,1)S(1)}, bf16[528,128]{1,0:T(8,128)(2,1)S(1)}, u32[]{:S(2)}, u32[]{:S(2)}) collective-permute-start(bf16[528,128]{1,0:T(8,128)(2,1)S(1)} %get-tuple-element.169.a), channel_id=1, source_target_pairs={{0,16},{16,0},{32,48},{48,32},{1,17},{17,1},{33,49},{49,33},{2,18}... | collective-permute-start | bytes 405512 | tf_op jit(solution)/shard_map/ppermute | solution.py:22
  85.3 11.0 %collective-permute-start.17 = (bf16[512,128]{1,0:T(8,128)(2,1)S(1)}, bf16[512,128]{1,0:T(8,128)(2,1)S(1)}, u32[]{:S(2)}, u32[]{:S(2)}) collective-permute-start(bf16[512,128]{1,0:T(8,128)(2,1)S(1)} %get-tuple-element.180), channel_id=1, source_target_pairs={{0,4},{4,0},{8,12},{12,8},{1,5},{5,1},{9,13},{13,9},{2,6},{6,2},{1... | collective-permute-start | bytes 393224 | tf_op jit(solution)/shard_map/ppermute | solution.py:22
  85.4 10.9 %collective-permute-start.18 = (bf16[512,128]{1,0:T(8,128)(2,1)S(1)}, bf16[512,128]{1,0:T(8,128)(2,1)S(1)}, u32[]{:S(2)}, u32[]{:S(2)}) collective-permute-start(bf16[512,128]{1,0:T(8,128)(2,1)S(1)} %get-tuple-element.181), channel_id=1, source_target_pairs={{0,12},{4,8},{8,4},{12,0},{1,13},{5,9},{9,5},{13,1},{2,14},{6,10},... | collective-permute-start | bytes 393224 | tf_op jit(solution)/shard_map/ppermute | solution.py:22
  87.6 8.7 %collective-permute-start.19 = (bf16[512,128]{1,0:T(8,128)(2,1)S(1)}, bf16[512,128]{1,0:T(8,128)(2,1)S(1)}, u32[]{:S(2)}, u32[]{:S(2)}) collective-permute-start(bf16[512,128]{1,0:T(8,128)(2,1)S(1)} %get-tuple-element.182), channel_id=1, source_target_pairs={{0,8},{4,12},{8,0},{12,4},{1,9},{5,13},{9,1},{13,5},{2,10},{6,14},... | collective-permute-start | bytes 393224 | tf_op jit(solution)/shard_map/ppermute | solution.py:22
  104.6 14.4 %collective-permute-start.21 = (bf16[384,768]{1,0:T(8,128)(2,1)S(1)}, bf16[384,768]{1,0:T(8,128)(2,1)S(1)}, u32[]{:S(2)}, u32[]{:S(2)}) collective-permute-start(bf16[384,768]{1,0:T(8,128)(2,1)S(1)} %get-tuple-element.214), channel_id=1, source_target_pairs={{0,48},{16,32},{32,16},{48,0},{1,49},{17,33},{33,17},{49,1},{2,50}... | collective-permute-start | bytes 1769480 | tf_op jit(solution)/shard_map/ppermute | solution.py:22
  106.9 13.2 %collective-permute-start.20 = (bf16[384,768]{1,0:T(8,128)(2,1)S(1)}, bf16[384,768]{1,0:T(8,128)(2,1)S(1)}, u32[]{:S(2)}, u32[]{:S(2)}) collective-permute-start(bf16[384,768]{1,0:T(8,128)(2,1)S(1)} %get-tuple-element.210), channel_id=1, source_target_pairs={{0,16},{16,0},{32,48},{48,32},{1,17},{17,1},{33,49},{49,33},{2,18}... | collective-permute-start | bytes 1769480 | tf_op jit(solution)/shard_map/ppermute | solution.py:22
  106.9 15.0 %collective-permute-start.24 = (bf16[384,768]{1,0:T(8,128)(2,1)S(1)}, bf16[384,768]{1,0:T(8,128)(2,1)S(1)}, u32[]{:S(2)}, u32[]{:S(2)}) collective-permute-start(bf16[384,768]{1,0:T(8,128)(2,1)S(1)} %get-tuple-element.223), channel_id=1, source_target_pairs={{0,4},{4,0},{8,12},{12,8},{1,5},{5,1},{9,13},{13,9},{2,6},{6,2},{1... | collective-permute-start | bytes 1769480 | tf_op jit(solution)/shard_map/ppermute | solution.py:22
  107.0 14.9 %collective-permute-start.25 = (bf16[384,768]{1,0:T(8,128)(2,1)S(1)}, bf16[384,768]{1,0:T(8,128)(2,1)S(1)}, u32[]{:S(2)}, u32[]{:S(2)}) collective-permute-start(bf16[384,768]{1,0:T(8,128)(2,1)S(1)} %get-tuple-element.224), channel_id=1, source_target_pairs={{0,12},{4,8},{8,4},{12,0},{1,13},{5,9},{9,5},{13,1},{2,14},{6,10},... | collective-permute-start | bytes 1769480 | tf_op jit(solution)/shard_map/ppermute | solution.py:22
  121.6 26.5 %collective-permute-start.22 = (bf16[768,768]{1,0:T(8,128)(2,1)S(1)}, bf16[768,768]{1,0:T(8,128)(2,1)S(1)}, u32[]{:S(2)}, u32[]{:S(2)}) collective-permute-start(bf16[768,768]{1,0:T(8,128)(2,1)S(1)} %get-tuple-element.219), channel_id=1, source_target_pairs={{0,16},{16,0},{32,48},{48,32},{1,17},{17,1},{33,49},{49,33},{2,18}... | collective-permute-start | bytes 3538952 | tf_op jit(solution)/shard_map/ppermute | solution.py:22
  122.0 26.1 %collective-permute-start.23 = (bf16[768,768]{1,0:T(8,128)(2,1)S(1)}, bf16[768,768]{1,0:T(8,128)(2,1)S(1)}, u32[]{:S(2)}, u32[]{:S(2)}) collective-permute-start(bf16[768,768]{1,0:T(8,128)(2,1)S(1)} %get-tuple-element.220), channel_id=1, source_target_pairs={{0,48},{16,32},{32,16},{48,0},{1,49},{17,33},{33,17},{49,1},{2,50}... | collective-permute-start | bytes 3538952 | tf_op jit(solution)/shard_map/ppermute | solution.py:22
  124.7 26.2 %collective-permute-start.27 = (bf16[768,768]{1,0:T(8,128)(2,1)S(1)}, bf16[768,768]{1,0:T(8,128)(2,1)S(1)}, u32[]{:S(2)}, u32[]{:S(2)}) collective-permute-start(bf16[768,768]{1,0:T(8,128)(2,1)S(1)} %get-tuple-element.236), channel_id=1, source_target_pairs={{0,12},{4,8},{8,4},{12,0},{1,13},{5,9},{9,5},{13,1},{2,14},{6,10},... | collective-permute-start | bytes 3538952 | tf_op jit(solution)/shard_map/ppermute | solution.py:22
  126.3 24.6 %collective-permute-start.26 = (bf16[768,768]{1,0:T(8,128)(2,1)S(1)}, bf16[768,768]{1,0:T(8,128)(2,1)S(1)}, u32[]{:S(2)}, u32[]{:S(2)}) collective-permute-start(bf16[768,768]{1,0:T(8,128)(2,1)S(1)} %get-tuple-element.227), channel_id=1, source_target_pairs={{0,4},{4,0},{8,12},{12,8},{1,5},{5,1},{9,13},{13,9},{2,6},{6,2},{1... | collective-permute-start | bytes 3538952 | tf_op jit(solution)/shard_map/ppermute | solution.py:22
  152.4 8.3 %collective-permute-start.28 = (bf16[192,768]{1,0:T(8,128)(2,1)S(1)}, bf16[192,768]{1,0:T(8,128)(2,1)S(1)}, u32[]{:S(2)}, u32[]{:S(2)}) collective-permute-start(bf16[192,768]{1,0:T(8,128)(2,1)S(1)} %get-tuple-element.238), channel_id=1, source_target_pairs={{0,4},{4,0},{8,12},{12,8},{1,5},{5,1},{9,13},{13,9},{2,6},{6,2},{1... | collective-permute-start | bytes 884744 | tf_op jit(solution)/shard_map/ppermute | solution.py:22
  152.5 12.7 %collective-permute-start.29 = (bf16[192,768]{1,0:T(8,128)(2,1)S(1)}, bf16[192,768]{1,0:T(8,128)(2,1)S(1)}, u32[]{:S(2)}, u32[]{:S(2)}) collective-permute-start(bf16[192,768]{1,0:T(8,128)(2,1)S(1)} %get-tuple-element.239), channel_id=1, source_target_pairs={{0,12},{4,8},{8,4},{12,0},{1,13},{5,9},{9,5},{13,1},{2,14},{6,10},... | collective-permute-start | bytes 884744 | tf_op jit(solution)/shard_map/ppermute | solution.py:22
  154.5 10.7 %collective-permute-start.30 = (bf16[192,768]{1,0:T(8,128)(2,1)S(1)}, bf16[192,768]{1,0:T(8,128)(2,1)S(1)}, u32[]{:S(2)}, u32[]{:S(2)}) collective-permute-start(bf16[192,768]{1,0:T(8,128)(2,1)S(1)} %get-tuple-element.240), channel_id=1, source_target_pairs={{0,8},{4,12},{8,0},{12,4},{1,9},{5,13},{9,1},{13,5},{2,10},{6,14},... | collective-permute-start | bytes 884744 | tf_op jit(solution)/shard_map/ppermute | solution.py:22
  156.5 8.6 %collective-permute-start.31 = (bf16[192,768]{1,0:T(8,128)(2,1)S(1)}, bf16[192,768]{1,0:T(8,128)(2,1)S(1)}, u32[]{:S(2)}, u32[]{:S(2)}) collective-permute-start(bf16[192,768]{1,0:T(8,128)(2,1)S(1)} %get-tuple-element.242), channel_id=1, source_target_pairs={{0,16},{16,0},{32,48},{48,32},{1,17},{17,1},{33,49},{49,33},{2,18}... | collective-permute-start | bytes 884744 | tf_op jit(solution)/shard_map/ppermute | solution.py:22
  157.6 8.0 %collective-permute-start.32 = (bf16[192,768]{1,0:T(8,128)(2,1)S(1)}, bf16[192,768]{1,0:T(8,128)(2,1)S(1)}, u32[]{:S(2)}, u32[]{:S(2)}) collective-permute-start(bf16[192,768]{1,0:T(8,128)(2,1)S(1)} %get-tuple-element.243), channel_id=1, source_target_pairs={{0,48},{16,32},{32,16},{48,0},{1,49},{17,33},{33,17},{49,1},{2,50}... | collective-permute-start | bytes 884744 | tf_op jit(solution)/shard_map/ppermute | solution.py:22
  160.7 8.2 %collective-permute-start.33 = (bf16[192,768]{1,0:T(8,128)(2,1)S(1)}, bf16[192,768]{1,0:T(8,128)(2,1)S(1)}, u32[]{:S(2)}, u32[]{:S(2)}) collective-permute-start(bf16[192,768]{1,0:T(8,128)(2,1)S(1)} %get-tuple-element.244), channel_id=1, source_target_pairs={{0,32},{16,48},{32,0},{48,16},{1,33},{17,49},{33,1},{49,17},{2,34}... | collective-permute-start | bytes 884744 | tf_op jit(solution)/shard_map/ppermute | solution.py:22
  169.8 8.3 %collective-permute-start.34 = (bf16[2,96,768]{2,1,0:T(8,128)(2,1)S(1)}, bf16[2,96,768]{2,1,0:T(8,128)(2,1)S(1)}, u32[]{:S(2)}, u32[]{:S(2)}) collective-permute-start(bf16[2,96,768]{2,1,0:T(8,128)(2,1)S(1)} %get-tuple-element.246), channel_id=1, source_target_pairs={{0,64},{64,0},{1,65},{65,1},{2,66},{66,2},{3,67},{67,3},{4,68},{68... | collective-permute-start | bytes 884744 | tf_op jit(solution)/shard_map/ppermute | solution.py:22

commit v7 on v6

--- a/solution.py
+++ b/solution.py
@@ -9,7 +9,8 @@
 F32 = jnp.float32
 BF16 = jnp.bfloat16
 HEAD = 128
-Z, X, Y, ZL, CO, TEN, LEN = range(7)
+HEADS = 4
+Z, X, Y, ZL, CO, TEN = range(6)
 AB_T = (((1,), (1,)), ((), ()))
 A_TB = (((0,), (0,)), ((), ()))
 
@@ -59,7 +60,13 @@
     return parts[0] if len(parts) == 1 else jnp.concatenate(parts, axis=0)
 
 
-def project(table, shards, flips, weight, partial, last):
+def living(info, dims):
+    row = lax.broadcasted_iota(jnp.int32, dims, 0).astype(F32)
+    return row < info[HEADS : HEADS + 1, :1]
+
+
+def project(table, shards, flips, weight, partial, info):
+    last = info is not None
     n, counts = len(shards), [len(x) for x in shards]
     flat = [part for x in shards for part in x]
     tokens, width = sum(part.shape[0] for part in shards[0]), flat[0].shape[1]
@@ -75,8 +82,7 @@
         if partial is not None:
             acc += refs[len(flat) + n][0]
         if last:
-            row = lax.broadcasted_iota(jnp.int32, acc.shape, 0)
-            acc = jnp.where(row < s[LEN], acc, 0.0)
+            acc = jnp.where(living(refs[-2], acc.shape), acc, 0.0)
         out[0] = acc.astype(out.dtype)
 
     tile = pl.BlockSpec((1, tokens, cols), lambda g, s: (g, 0, 0))
@@ -89,19 +95,21 @@
     if partial is not None:
         in_specs.append(tile)
         operands.append(partial)
+    if last:
+        in_specs.append(whole(info))
+        operands.append(info)
     out = shape((3, tokens, cols), BF16 if last else F32)
     return call("project", body, table, (3,), operands, in_specs, out, tile, 24)
 
 
 def shard_states(table, qkv, out_grad, cumul, which, so_far):
     tokens = qkv.shape[1]
-    heads = qkv.shape[2] // HEAD
     scale = HEAD**-0.5
 
     def body(s, qkv_ref, og_ref, cum_ref, *refs):
         outs = refs[-4:]
         r = pl.program_id(0)
-        row = cum_ref[pl.ds(which * heads + (s[Y] ^ r), 1), :]
+        row = cum_ref[pl.ds(s[Y] ^ r, 1), :]
         total = row[:, tokens - 1 : tokens]
         keys_t = qkv_ref[1].T.astype(F32)
         query_t = qkv_ref[0].T.astype(F32)
@@ -265,15 +273,14 @@
     return jnp.broadcast_to(row, (HEAD, row.shape[1])).T
 
 
-def local_grads(table, qkv, out_grad, cumul, which, first, count, so_far):
+def local_grads(table, qkv, out_grad, cumul, first, count, so_far):
     tokens = qkv.shape[1]
-    heads = qkv.shape[2] // HEAD
     scale = HEAD**-0.5
     size = tokens // 2
 
     def body(s, qkv_ref, og_ref, cum_ref, *refs):
         out, ready = refs[-2:]
-        row = cum_ref[pl.ds(pl.program_id(0) + which * heads + first, 1), :]
+        row = cum_ref[pl.ds(pl.program_id(0) + first, 1), :]
         column = column_of(row)
         wide = jnp.concatenate([column] * (size // HEAD), axis=1)
         s_at = lax.broadcasted_iota(jnp.int32, (size, size), 0)
@@ -299,7 +306,7 @@
             return dq, dot(score, q), dot(prob, g)
 
         a, b, c = pair(0, 0), pair(1, 0), pair(1, 1)
-        live = lax.broadcasted_iota(jnp.int32, (tokens, HEAD), 0) < s[LEN]
+        live = living(cum_ref, (tokens, HEAD))
         grads = (
             jnp.concatenate([a[0], b[0] + c[0]], axis=0) * scale,
             jnp.concatenate([a[1] + b[1], c[1]], axis=0) * scale,
@@ -379,6 +386,18 @@
     )
 
 
+def split(table, first, second):
+    tokens, width = first.shape
+
+    def body(s, a, b, out_a, out_b):
+        out_a[...] = a[...]
+        out_b[...] = b[...]
+
+    halves = [pl.BlockSpec((tokens // 2, width), lambda i, s, k=k: (k, 0)) for k in range(2)]
+    out = shape((tokens // 2, width))
+    return call("split", body, table, (1,), (first, second), halves, [out] * 2, [whole(out)] * 2, 8)
+
+
 def turn(table, shards):
     counts = [len(x) for x in shards]
     flat = [part for x in shards for part in x]
@@ -498,11 +517,11 @@
     def body(s, *refs):
         here, there = refs[-2:]
         for k in range(2):
-            total = sum(ref[...].astype(F32) for ref in refs[4 * k : 4 * k + 4]).astype(BF16)
+            total = sum(ref[...].astype(F32) for ref in refs[k:8:2]).astype(BF16)
             here[k] = total[: rows // 2]
             there[k] = total[rows // 2 :]
 
-    operands = [x for side in sides for x in side]
+    operands = [x for both in zip(*sides) for x in both]
     outs = [shape((2, rows // 2, cols))] * 2
     return call(
         "final_sums",
@@ -547,7 +566,7 @@
     index = [lax.axis_index(a) for a in ("c0", "c1", "c2", "zl", "co")]
     here_z = index[0]
     fixed = [*index, index[3] * 2 + index[4]]
-    table = jnp.stack([*fixed, lengths[0]]).astype(jnp.int32)
+    table = jnp.stack(fixed).astype(jnp.int32)
     weight = pltpu.with_memory_space_constraint(jnp.transpose(qkv_weight, (1, 0, 2)), pltpu.HBM)
 
     near = send(activations, "zl", 1)
@@ -557,52 +576,51 @@
     live = (jnp.arange(tokens, dtype=jnp.int32) < lengths[0]).astype(F32)
     cumul = jnp.cumsum(log_decay.T * live[None, :], axis=1)
     size = jnp.broadcast_to(lengths.astype(F32)[:, None], (per, tokens))
-    note = jnp.concatenate([lax.dynamic_slice_in_dim(cumul, (1 - here_z) * per, per), size])
+    info, note = (
+        jnp.concatenate([lax.dynamic_slice_in_dim(cumul, z * per, per), size])
+        for z in (here_z, 1 - here_z)
+    )
     note = send(note, "c0", 1)
     width = per * HEAD
     og_own = lax.dynamic_slice_in_dim(out_grad, here_z * width, width, axis=1)
     og_other = lax.dynamic_slice_in_dim(out_grad, (1 - here_z) * width, width, axis=1)
 
-    acc_own = project(table, [[activations], [core]], (0, 1), weight, None, False)
-    near, side, acc_own, note, og_other = tied((near, side, acc_own, note, og_other))
-    half = tokens // 2
-    far = [send(side[:half], "zl", 1), across(near[half:])]
+    acc_own = project(table, [[activations], [core]], (0, 1), weight, None, None)
+    near, side, acc_own, note, og_other, info = tied((near, side, acc_own, note, og_other, info))
+    far = split(table, side, near)
+    far = [send(far[0], "zl", 1), across(far[1])]
     near_core = send(near, "co", 1)
     side_core = send(side, "co", 1)
-    cumul = jnp.concatenate([lax.dynamic_slice_in_dim(cumul, here_z * per, per), note[:per]])
-    table_pair = jnp.stack([*fixed, note[per, 0].astype(jnp.int32)]).astype(jnp.int32)
-    qkv_own = project(table, [[near], [near_core]], (2, 3), weight, acc_own, True)
+    qkv_own = project(table, [[near], [near_core]], (2, 3), weight, acc_own, info)
     turned = [turn(table, tied(([[activations], [core], [near], [near_core]], qkv_own))[0])]
-    far, side_core, qkv_own, table_pair, cumul, turned = tied(
-        (far, side_core, qkv_own, table_pair, cumul, turned)
-    )
+    far, side_core, qkv_own, turned = tied((far, side_core, qkv_own, turned))
     far_core = [send(x, "co", 1) for x in far]
     og_pair = send(tied((og_other, far))[0], "c0", 1)
-    local_own = local_grads(table, qkv_own, og_own, cumul, 0, 0, per // 2, None)
+    local_own = local_grads(table, qkv_own, og_own, info, 0, per // 2, None)
     far_core, local_own = tied((far_core, local_own))
     qkv_pair = project(
-        table_pair, [[side], [side_core], far, far_core], (2, 3, 0, 1), weight, None, True
+        table, [[side], [side_core], far, far_core], (2, 3, 0, 1), weight, None, note
     )
     qkv_own, _ = tied((qkv_own, qkv_pair))
-    to_y = shard_states(table, qkv_own, og_own, cumul, 0, None)
+    to_y = shard_states(table, qkv_own, og_own, info, 0, None)
     og_pair, qkv_pair, to_y = tied((og_pair, qkv_pair, to_y))
 
-    to_y = shard_states(table, qkv_pair, og_pair, cumul, 1, to_y)
+    to_y = shard_states(table, qkv_pair, og_pair, note, 1, to_y)
     at_y = [send(to_y[r], "c2", r) for r in (1, 3, 2)]
     qkv_own, _ = tied((qkv_own, to_y[0]))
-    local_own = local_grads(table, qkv_own, og_own, cumul, 0, per // 2, per // 2, local_own)
-    at_y, local_own = tied((at_y, local_own))
+    local_own = local_grads(table, qkv_own, og_own, info, per // 2, per // 2, local_own)
+    second, _ = tied(([far, far_core, [side], [side_core]], to_y[0]))
+    turned.append(turn(table, second))
+    at_y, local_own, turned = tied((at_y, local_own, turned))
     before, after, prior, later, ring = ring_y(table, [to_y[0], at_y[0], at_y[2], at_y[1]])
     at_x = [send(ring, "c1", r) for r in (1, 3, 2)]
     qkv_pair, _ = tied((qkv_pair, ring))
-    local = local_grads(table_pair, qkv_pair, og_pair, cumul, 1, 0, per // 2, None)
+    local = local_grads(table, qkv_pair, og_pair, note, 0, per // 2, None)
     at_x, local = tied((at_x, local))
     back = arrivals(table, [ring, at_x[0], at_x[2], at_x[1]], before, after, prior, later)
     states = [send(back[r], "c2", r) for r in (1, 3, 2)]
     local, _ = tied((local, back[0]))
-    local = local_grads(table_pair, qkv_pair, og_pair, cumul, 1, per // 2, per // 2, local)
-    second, _ = tied(([far, far_core, [side], [side_core]], back[0]))
-    turned.append(turn(table, second))
+    local = local_grads(table, qkv_pair, og_pair, note, per // 2, per // 2, local)
     states, turned, local = tied((states, turned, local))
     states = [back[0], states[0], states[2], states[1]]
 
@@ -623,8 +641,10 @@
     own = weight_part(table, turned, lefts, rights, (0,), False)
     l_got, own = tied((l_got, own))
     l_cut, r_cut = cut_blocks(table, (own[0], *l_got), (own[1], *r_got))
-    l_got = [send(x, "c2", by) for x, by in zip(l_cut, (1, 3, 2))]
-    r_got = [send(x, "c1", by) for x, by in zip(r_cut, (1, 3, 2))]
+    l_got, r_got = [], []
+    for k, by in enumerate((1, 3, 2)):
+        l_got.append(send(l_cut[k], "c2", by))
+        r_got.append(send(r_cut[k], "c1", by))
     here, there = final_sums(table, ((l_cut[3], *l_got), (r_cut[3], *r_got)))
     there = send(there, "c0", 1)
     return jnp.transpose(finish(table, here, there), (1, 0, 2))

time: 180 us -> 174 us (0.967)
  local copies, waits for them, and re-layouts: 12.5 us -> 1.55 us
  waiting for transfers between devices: 48.3 us -> 55.7 us
  Pallas kernels: 72.6 us -> 70.1 us
    ppermute x33, waiting for transfers between devices: 48.3 us -> 54.9 us  [send(): lax.ppermute(x, axis, [(i, i ^ by) for i in range(lax.axis_size(axis))])]
    slice x5 -> x1, local copies, waits for them, and re-layouts: 5.72 us -> 0.16 us  [the longest x2 3.57 us: device_part(): far = [send(side[:half], 'zl', 1), across(near[half:])]]
    unnamed x14 -> x2, local copies, waits for them, and re-layouts: 3.16 us -> 0.01 us
    pallas_call x23 -> x24, Pallas kernels: 72.6 us -> 70.1 us  [call(): pl.pallas_call(body, grid_spec=pltpu.PrefetchScalarGridSpec(num_scalar_pr...]
  transfers between devices with their start and end apart: 35 -> 35, of which waited for: 15 -> 16; matrix products, arithmetic and copies ran while one was open for 7% -> 2% of each run, Pallas kernels for 32% -> 31%
where the time goes in v7:
time: 174 us
  Pallas kernels  70.1 us (40%)
  waiting for transfers between devices  55.7 us (32%)
  starting transfers between devices  43.3 us (25%)
  other arithmetic  1.96 us (1%)
    pallas_call x24, Pallas kernels, call(): pl.pallas_call(body, grid_spec=pltpu.PrefetchScalarGridSpec(num_scalar_pr...  70.1 us
    ppermute x33, waiting for transfers between devices, send(): lax.ppermute(x, axis, [(i, i ^ by) for i in range(lax.axis_size(axis))])  54.9 us
    ppermute x33, starting transfers between devices, send(): lax.ppermute(x, axis, [(i, i ^ by) for i in range(lax.axis_size(axis))])  36.6 us
    ppermute x2, starting transfers between devices, across(): return lax.ppermute(x, ('c0', 'zl'), [(0, 3), (1, 2), (2, 1), (3, 0)])  6.75 us
  transfers between devices with their start and end apart: 35, of which 16 were waited for; matrix products, arithmetic and copies ran while one was open for 2% of the time, Pallas kernels for 31%

profile of v7, /device:TPU:0, one launch (start us, length us, event | category | flops | bytes accessed | tf_op | source)
XLA Modules:
  0.0 173.7 jit_solution(11444217243879489144)
XLA Ops:
  0.0 4.1 %collective-permute-start.1 = (bf16[512,768]{1,0:T(8,128)(2,1)}, bf16[512,768]{1,0:T(8,128)(2,1)S(1)}, u32[]{:S(2)}, u32[]{:S(2)}) collective-permute-start(bf16[512,768]{1,0:T(8,128)(2,1)} %refs_0_.2), channel_id=1, source_target_pairs={{0,66},{2,64},{64,2},{66,0},{1,67},{3,65},{65,3},{67,1},{4,70},{6,... | collective-permute-start | bytes 2359304 | tf_op jit(solution)/shard_map/ppermute | solution.py:27
  7.0 1.6 collective-permute-start.3
  10.0 5.5 %project.3.refs_4_ = f32[3,512,512]{2,1,0:T(8,128)S(1)} custom-call(s32[6]{0:T(128)S(1)} %stack.27.s, bf16[512,768]{1,0:T(8,128)(2,1)S(1)} %copy-done, bf16[512,768]{1,0:T(8,128)(2,1)} %collective-permute-done.2.refs_1_, bf16[3,3072,1024]{2,1,0:T(8,128)(2,1)} %bitcast.31, bf16[3,3072,1024]{2,1,0:T(8,128)(2,1)} %bitcast.32), custom_call_target="tpu_custom_call" | custom-call | flops 1 | bytes 1 | tf_op jit(solution)/shard_map/project/pallas_call | solution.py:35
  15.5 8.6 %collective-permute-done.3.refs_10_.cum_ref = f32[8,512]{1,0:T(8,128)S(1)} collective-permute-done((f32[8,512]{1,0:T(8,128)S(1)}, f32[8,512]{1,0:T(8,128)S(1)}, u32[]{:S(2)}, u32[]{:S(2)}) %collective-permute-start.3) | collective-permute-done | bytes 16416 | tf_op jit(solution)/shard_map/ppermute | solution.py:23
  25.7 2.6 %collective-permute-start.5 = (bf16[256,768]{1,0:T(8,128)(2,1)S(1)}, bf16[256,768]{1,0:T(8,128)(2,1)S(1)}, u32[]{:S(2)}, u32[]{:S(2)}) collective-permute-start(bf16[256,768]{1,0:T(8,128)(2,1)S(1)} %get-tuple-element.133), channel_id=1, source_target_pairs={{0,66},{2,64},{64,2},{66,0},{1,67},{3,65},{65,3},{67,1},{4,70},{6,... | collective-permute-start | bytes 1179656 | tf_op jit(solution)/shard_map/ppermute | solution.py:27
  28.3 5.3 %project.4.qkv_ref = bf16[3,512,512]{2,1,0:T(8,128)(2,1)S(1)} custom-call(s32[6]{0:T(128)S(1)} %stack.27.s, bf16[512,768]{1,0:T(8,128)(2,1)S(1)} %collective-permute-done.b.refs_0_.refs_2_, bf16[512,768]{1,0:T(8,128)(2,1)S(1)} %collective-permute-done.7.refs_1_.refs_3_, bf16[3,3072,1024]{2,1,0:T(8,128)(2,1)} %bitcast.33, bf16[3,3072,1024]{2,1,0:T(8,128)(2,1)} %bitcast.34, ...), custom_call_target="tpu_custom_call" | custom-call | flops 1 | bytes 1 | tf_op jit(solution)/shard_map/project/pallas_call | solution.py:35
  33.6 3.2 %turn.2 = bf16[16,2,96,512]{3,2,1,0:T(8,128)(2,1)S(1)} custom-call(s32[6]{0:T(128)S(1)} %stack.27.s, bf16[512,768]{1,0:T(8,128)(2,1)S(1)} %copy-done, bf16[512,768]{1,0:T(8,128)(2,1)} %collective-permute-done.2.refs_1_, bf16[512,768]{1,0:T(8,128)(2,1)S(1)} %collective-permute-done.b.refs_0_.refs_2_, bf16[512,768]{1,0:T(8,128)(2,1)S(1)} %collective-permute-done.7.refs_1_.refs_3_), custom_call_target="tpu_custom_call" | custom-call | flops 1 | bytes 1 | tf_op jit(solution)/shard_map/turn/pallas_call | solution.py:35
  37.7 2.8 %collective-permute-start.8 = (bf16[512,512]{1,0:T(8,128)(2,1)S(1)}, bf16[512,512]{1,0:T(8,128)(2,1)S(1)}, u32[]{:S(2)}, u32[]{:S(2)}) collective-permute-start(bf16[512,512]{1,0:T(8,128)(2,1)S(1)} %get-tuple-element.142), channel_id=1, source_target_pairs={{0,64},{64,0},{1,65},{65,1},{2,66},{66,2},{3,67},{67,3},{4,68},{68... | collective-permute-start | bytes 1572872 | tf_op jit(solution)/shard_map/ppermute | solution.py:23
  41.0 3.2 %local_grads.4 = (bf16[3,512,512]{2,1,0:T(8,128)(2,1)S(1)}, bf16[3,512,512]{2,1,0:T(8,128)(2,1)S(1)}) custom-call(s32[6]{0:T(128)S(1)} %stack.27.s, bf16[3,512,512]{2,1,0:T(8,128)(2,1)S(1)} %project.4.qkv_ref, bf16[512,512]{1,0:T(8,128)(2,1)S(1)} %get-tuple-element.253.og_ref, f32[8,512]{1,0:T(8,128)S(1)} %concatenate.7.refs_5_.cum_ref), custom_call_target="tpu_custom_call" | custom-call | flops 1 | bytes 1 | tf_op jit(solution)/shard_map/local_grads/pallas_call | solution.py:35
  44.3 7.9 %project.5.qkv_ref = bf16[3,512,512]{2,1,0:T(8,128)(2,1)S(1)} custom-call(s32[6]{0:T(128)S(1)} %stack.27.s, bf16[512,768]{1,0:T(8,128)(2,1)S(1)} %collective-permute-done.1.a.refs_0_.refs_4_, bf16[512,768]{1,0:T(8,128)(2,1)S(1)} %collective-permute-done.6.refs_1_.refs_5_, bf16[256,768]{1,0:T(8,128)(2,1)S(1)} %collective-permute-done.4.refs_2_.refs_0_, ...), custom_call_target="tpu_custom_call" | custom-call | flops 1 | bytes 1 | tf_op jit(solution)/shard_map/project/pallas_call | solution.py:35
  52.2 2.3 %shard_states.2 = (bf16[528,128]{1,0:T(8,128)(2,1)S(1)}, bf16[528,128]{1,0:T(8,128)(2,1)S(1)}, bf16[528,128]{1,0:T(8,128)(2,1)S(1)}, bf16[528,128]{1,0:T(8,128)(2,1)S(1)}) custom-call(s32[6]{0:T(128)S(1)} %stack.27.s, bf16[3,512,512]{2,1,0:T(8,128)(2,1)S(1)} %project.4.qkv_ref, bf16[512,512]{1,0:T(8,128)(2,1)S(1)} %get-tuple-element.253.og_ref, ...), custom_call_target="tpu_custom_call" | custom-call | flops 1 | bytes 1 | tf_op jit(solution)/shard_map/shard_states/pallas_call | solution.py:35
  54.5 2.3 %shard_states.3 = (bf16[528,128]{1,0:T(8,128)(2,1)S(1)}, bf16[528,128]{1,0:T(8,128)(2,1)S(1)}, bf16[528,128]{1,0:T(8,128)(2,1)S(1)}, bf16[528,128]{1,0:T(8,128)(2,1)S(1)}) custom-call(s32[6]{0:T(128)S(1)} %stack.27.s, bf16[3,512,512]{2,1,0:T(8,128)(2,1)S(1)} %project.5.qkv_ref, bf16[512,512]{1,0:T(8,128)(2,1)S(1)} %collective-permute-done.8.og_ref, ...), custom_call_target="tpu_custom_call" | custom-call | flops 1 | bytes 1 | tf_op jit(solution)/shard_map/shard_states/pallas_call | solution.py:35
  56.8 1.7 collective-permute-start.11
  58.5 2.2 %collective-permute-start.12 = (bf16[528,128]{1,0:T(8,128)(2,1)S(1)}, bf16[528,128]{1,0:T(8,128)(2,1)S(1)}, u32[]{:S(2)}, u32[]{:S(2)}) collective-permute-start(bf16[528,128]{1,0:T(8,128)(2,1)S(1)} %get-tuple-element.163), channel_id=1, source_target_pairs={{0,12},{4,8},{8,4},{12,0},{1,13},{5,9},{9,5},{13,1},{2,14},{6,10},... | collective-permute-start | bytes 405512 | tf_op jit(solution)/shard_map/ppermute | solution.py:23
  61.4 3.2 %local_grads.5 = (bf16[3,512,512]{2,1,0:T(8,128)(2,1)S(1)}, bf16[3,512,512]{2,1,0:T(8,128)(2,1)S(1)}) custom-call(s32[6]{0:T(128)S(1)} %stack.27.s, bf16[3,512,512]{2,1,0:T(8,128)(2,1)S(1)} %project.4.qkv_ref, bf16[512,512]{1,0:T(8,128)(2,1)S(1)} %get-tuple-element.253.og_ref, ...), custom_call_target="tpu_custom_call", output_to_operand_aliasing={{0}: (4, {}), {1}: (5, {})} | custom-call | flops 1 | bytes 1 | tf_op jit(solution)/shard_map/local_grads/pallas_call | solution.py:35
  64.6 2.0 %turn.3 = bf16[16,2,96,512]{3,2,1,0:T(8,128)(2,1)S(1)} custom-call(s32[6]{0:T(128)S(1)} %stack.27.s, bf16[256,768]{1,0:T(8,128)(2,1)S(1)} %collective-permute-done.4.refs_2_.refs_0_, bf16[256,768]{1,0:T(8,128)(2,1)S(1)} %collective-permute-done.5.refs_3_.refs_1_, bf16[256,768]{1,0:T(8,128)(2,1)S(1)} %collective-permute-done.9.refs_4_.refs_2_, ...), custom_call_target="tpu_custom_call" | custom-call | flops 1 | bytes 1 | tf_op jit(solution)/shard_map/turn/pallas_call | solution.py:35
  68.6 3.1 %collective-permute-start.16 = (bf16[528,128]{1,0:T(8,128)(2,1)S(1)}, bf16[528,128]{1,0:T(8,128)(2,1)S(1)}, u32[]{:S(2)}, u32[]{:S(2)}) collective-permute-start(bf16[528,128]{1,0:T(8,128)(2,1)S(1)} %get-tuple-element.180.a), channel_id=1, source_target_pairs={{0,32},{16,48},{32,0},{48,16},{1,33},{17,49},{33,1},{49,17},{2,34}... | collective-permute-start | bytes 405512 | tf_op jit(solution)/shard_map/ppermute | solution.py:23
  72.8 3.2 %local_grads.6 = (bf16[3,512,512]{2,1,0:T(8,128)(2,1)S(1)}, bf16[3,512,512]{2,1,0:T(8,128)(2,1)S(1)}) custom-call(s32[6]{0:T(128)S(1)} %stack.27.s, bf16[3,512,512]{2,1,0:T(8,128)(2,1)S(1)} %project.5.qkv_ref, bf16[512,512]{1,0:T(8,128)(2,1)S(1)} %collective-permute-done.8.og_ref, f32[8,512]{1,0:T(8,128)S(1)} %collective-permute-done.3.refs_10_.cum_ref), custom_call_target="tpu_custom_call" | custom-call | flops 1 | bytes 1 | tf_op jit(solution)/shard_map/local_grads/pallas_call | solution.py:35
  76.0 2.0 %collective-permute-done.15.d = bf16[528,128]{1,0:T(8,128)(2,1)S(1)} collective-permute-done((bf16[528,128]{1,0:T(8,128)(2,1)S(1)}, bf16[528,128]{1,0:T(8,128)(2,1)S(1)}, u32[]{:S(2)}, u32[]{:S(2)}) %collective-permute-start.15) | collective-permute-done | bytes 135200 | tf_op jit(solution)/shard_map/ppermute | solution.py:23
  79.1 2.2 %collective-permute-start.18 = (bf16[512,128]{1,0:T(8,128)(2,1)S(1)}, bf16[512,128]{1,0:T(8,128)(2,1)S(1)}, u32[]{:S(2)}, u32[]{:S(2)}) collective-permute-start(bf16[512,128]{1,0:T(8,128)(2,1)S(1)} %get-tuple-element.192), channel_id=1, source_target_pairs={{0,12},{4,8},{8,4},{12,0},{1,13},{5,9},{9,5},{13,1},{2,14},{6,10},... | collective-permute-start | bytes 393224 | tf_op jit(solution)/shard_map/ppermute | solution.py:23
  81.3 1.8 %collective-permute-start.19 = (bf16[512,128]{1,0:T(8,128)(2,1)S(1)}, bf16[512,128]{1,0:T(8,128)(2,1)S(1)}, u32[]{:S(2)}, u32[]{:S(2)}) collective-permute-start(bf16[512,128]{1,0:T(8,128)(2,1)S(1)} %get-tuple-element.193), channel_id=1, source_target_pairs={{0,8},{4,12},{8,0},{12,4},{1,9},{5,13},{9,1},{13,5},{2,10},{6,14},... | collective-permute-start | bytes 393224 | tf_op jit(solution)/shard_map/ppermute | solution.py:23
  83.1 3.2 %local_grads.7 = (bf16[3,512,512]{2,1,0:T(8,128)(2,1)S(1)}, bf16[3,512,512]{2,1,0:T(8,128)(2,1)S(1)}) custom-call(s32[6]{0:T(128)S(1)} %stack.27.s, bf16[3,512,512]{2,1,0:T(8,128)(2,1)S(1)} %project.5.qkv_ref, bf16[512,512]{1,0:T(8,128)(2,1)S(1)} %collective-permute-done.8.og_ref, ...), custom_call_target="tpu_custom_call", output_to_operand_aliasing={{0}: (4, {}), {1}: (5, {})} | custom-call | flops 1 | bytes 1 | tf_op jit(solution)/shard_map/local_grads/pallas_call | solution.py:35
  86.6 1.4 collective-permute-done.19.c
  88.0 2.5 %whole_grads.2 = (bf16[512,768]{1,0:T(8,128)(2,1)S(1)}, bf16[512,768]{1,0:T(8,128)(2,1)S(1)}) custom-call(s32[6]{0:T(128)S(1)} %stack.27.s, bf16[3,512,512]{2,1,0:T(8,128)(2,1)S(1)} %get-tuple-element.205.local_ref, bf16[3,512,512]{2,1,0:T(8,128)(2,1)S(1)} %get-tuple-element.206.ready_ref, bf16[512,128]{1,0:T(8,128)(2,1)S(1)} %get-tuple-element.198.a, ...), custom_call_target="tpu_custom_call" | custom-call | flops 1 | bytes 1 | tf_op jit(solution)/shard_map/whole_grads/pallas_call | solution.py:35
  90.6 2.5 %whole_grads.3 = (bf16[512,768]{1,0:T(8,128)(2,1)S(1)}, bf16[512,768]{1,0:T(8,128)(2,1)S(1)}) custom-call(s32[6]{0:T(128)S(1)} %stack.27.s, bf16[3,512,512]{2,1,0:T(8,128)(2,1)S(1)} %get-tuple-element.211.local_ref, bf16[3,512,512]{2,1,0:T(8,128)(2,1)S(1)} %get-tuple-element.212.ready_ref, bf16[512,128]{1,0:T(8,128)(2,1)S(1)} %get-tuple-element.198.a, ...), custom_call_target="tpu_custom_call" | custom-call | flops 1 | bytes 1 | tf_op jit(solution)/shard_map/whole_grads/pallas_call | solution.py:35
  93.1 3.1 %weight_part.3 = (bf16[384,768]{1,0:T(8,128)(2,1)S(1)}, bf16[384,768]{1,0:T(8,128)(2,1)S(1)}, bf16[384,768]{1,0:T(8,128)(2,1)S(1)}, bf16[384,768]{1,0:T(8,128)(2,1)S(1)}) custom-call(s32[6]{0:T(128)S(1)} %stack.27.s, bf16[4,4,192,512]{3,2,1,0:T(8,128)(2,1)S(1)} %bitcast.19, bf16[4,4,192,512]{3,2,1,0:T(8,128)(2,1)S(1)} %bitcast.20, ...), custom_call_target="tpu_custom_call" | custom-call | flops 1 | bytes 1 | tf_op jit(solution)/shard_map/weight_part/pallas_call | solution.py:35
  96.3 2.6 %collective-permute-start.21 = (bf16[384,768]{1,0:T(8,128)(2,1)S(1)}, bf16[384,768]{1,0:T(8,128)(2,1)S(1)}, u32[]{:S(2)}, u32[]{:S(2)}) collective-permute-start(bf16[384,768]{1,0:T(8,128)(2,1)S(1)} %get-tuple-element.220), channel_id=1, source_target_pairs={{0,48},{16,32},{32,16},{48,0},{1,49},{17,33},{33,17},{49,1},{2,50}... | collective-permute-start | bytes 1769480 | tf_op jit(solution)/shard_map/ppermute | solution.py:23
  99.5 1.7 collective-permute-start.25
  101.2 8.4 %weight_part.4 = (bf16[768,768]{1,0:T(8,128)(2,1)S(1)}, bf16[768,768]{1,0:T(8,128)(2,1)S(1)}, bf16[768,768]{1,0:T(8,128)(2,1)S(1)}, bf16[768,768]{1,0:T(8,128)(2,1)S(1)}) custom-call(s32[6]{0:T(128)S(1)} %stack.27.s, bf16[4,4,192,512]{3,2,1,0:T(8,128)(2,1)S(1)} %bitcast.21, bf16[4,4,192,512]{3,2,1,0:T(8,128)(2,1)S(1)} %bitcast.22, ...), custom_call_target="tpu_custom_call" | custom-call | flops 1 | bytes 1 | tf_op jit(solution)/shard_map/weight_part/pallas_call | solution.py:35
  109.6 1.5 collective-permute-done.21.d
  111.2 1.5 collective-permute-done.20.u
  112.6 1.5 add_halves.2
  114.7 1.3 collective-permute-start.23
  116.0 1.5 add_halves.3
  117.4 1.3 collective-permute-start.27
  118.8 3.1 %weight_part.5 = (bf16[768,768]{1,0:T(8,128)(2,1)S(1)}, bf16[768,768]{1,0:T(8,128)(2,1)S(1)}) custom-call(s32[6]{0:T(128)S(1)} %stack.27.s, bf16[4,4,192,512]{3,2,1,0:T(8,128)(2,1)S(1)} %bitcast.23, bf16[4,4,192,512]{3,2,1,0:T(8,128)(2,1)S(1)} %bitcast.24, bf16[4,4,192,512]{3,2,1,0:T(8,128)(2,1)S(1)} %bitcast.29, bf16[4,4,192,512]{3,2,1,0:T(8,128)(2,1)S(1)} %bitcast.30, ...), custom_call_target="tpu_custom_call" | custom-call | flops 1 | bytes 1 | tf_op jit(solution)/shard_map/weight_part/pallas_call | solution.py:35
  121.9 19.5 %collective-permute-done.23.refs_2_ = bf16[768,768]{1,0:T(8,128)(2,1)S(1)} collective-permute-done((bf16[768,768]{1,0:T(8,128)(2,1)S(1)}, bf16[768,768]{1,0:T(8,128)(2,1)S(1)}, u32[]{:S(2)}, u32[]{:S(2)}) %collective-permute-start.23) | collective-permute-done | bytes 1179680 | tf_op jit(solution)/shard_map/ppermute | solution.py:23
  141.4 2.8 %collective-permute-done.27.refs_5_ = bf16[768,768]{1,0:T(8,128)(2,1)S(1)} collective-permute-done((bf16[768,768]{1,0:T(8,128)(2,1)S(1)}, bf16[768,768]{1,0:T(8,128)(2,1)S(1)}, u32[]{:S(2)}, u32[]{:S(2)}) %collective-permute-start.27) | collective-permute-done | bytes 1179680 | tf_op jit(solution)/shard_map/ppermute | solution.py:23
  144.3 1.4 cut_blocks.1
  146.9 1.9 %collective-permute-start.30 = (bf16[192,768]{1,0:T(8,128)(2,1)S(1)}, bf16[192,768]{1,0:T(8,128)(2,1)S(1)}, u32[]{:S(2)}, u32[]{:S(2)}) collective-permute-start(bf16[192,768]{1,0:T(8,128)(2,1)S(1)} %get-tuple-element.247), channel_id=1, source_target_pairs={{0,12},{4,8},{8,4},{12,0},{1,13},{5,9},{9,5},{13,1},{2,14},{6,10},... | collective-permute-start | bytes 884744 | tf_op jit(solution)/shard_map/ppermute | solution.py:23
  148.8 1.5 collective-permute-start.31
  150.2 2.1 %collective-permute-start.32 = (bf16[192,768]{1,0:T(8,128)(2,1)S(1)}, bf16[192,768]{1,0:T(8,128)(2,1)S(1)}, u32[]{:S(2)}, u32[]{:S(2)}) collective-permute-start(bf16[192,768]{1,0:T(8,128)(2,1)S(1)} %get-tuple-element.249), channel_id=1, source_target_pairs={{0,8},{4,12},{8,0},{12,4},{1,9},{5,13},{9,1},{13,5},{2,10},{6,14},... | collective-permute-start | bytes 884744 | tf_op jit(solution)/shard_map/ppermute | solution.py:23
  152.3 2.3 %collective-permute-done.28.refs_2_ = bf16[192,768]{1,0:T(8,128)(2,1)S(1)} collective-permute-done((bf16[192,768]{1,0:T(8,128)(2,1)S(1)}, bf16[192,768]{1,0:T(8,128)(2,1)S(1)}, u32[]{:S(2)}, u32[]{:S(2)}) %collective-permute-start.28) | collective-permute-done | bytes 294944 | tf_op jit(solution)/shard_map/ppermute | solution.py:23
  154.7 2.1 %collective-permute-start.33 = (bf16[192,768]{1,0:T(8,128)(2,1)S(1)}, bf16[192,768]{1,0:T(8,128)(2,1)S(1)}, u32[]{:S(2)}, u32[]{:S(2)}) collective-permute-start(bf16[192,768]{1,0:T(8,128)(2,1)S(1)} %get-tuple-element.250), channel_id=1, source_target_pairs={{0,32},{16,48},{32,0},{48,16},{1,33},{17,49},{33,1},{49,17},{2,34}... | collective-permute-start | bytes 884744 | tf_op jit(solution)/shard_map/ppermute | solution.py:23
  156.8 2.7 %collective-permute-done.30.refs_4_ = bf16[192,768]{1,0:T(8,128)(2,1)S(1)} collective-permute-done((bf16[192,768]{1,0:T(8,128)(2,1)S(1)}, bf16[192,768]{1,0:T(8,128)(2,1)S(1)}, u32[]{:S(2)}, u32[]{:S(2)}) %collective-permute-start.30) | collective-permute-done | bytes 294944 | tf_op jit(solution)/shard_map/ppermute | solution.py:23
  159.5 3.4 %collective-permute-done.33.refs_7_ = bf16[192,768]{1,0:T(8,128)(2,1)S(1)} collective-permute-done((bf16[192,768]{1,0:T(8,128)(2,1)S(1)}, bf16[192,768]{1,0:T(8,128)(2,1)S(1)}, u32[]{:S(2)}, u32[]{:S(2)}) %collective-permute-start.33) | collective-permute-done | bytes 294944 | tf_op jit(solution)/shard_map/ppermute | solution.py:23
  164.5 7.5 %collective-permute-done.34.there_ref = bf16[2,96,768]{2,1,0:T(8,128)(2,1)S(1)} collective-permute-done((bf16[2,96,768]{2,1,0:T(8,128)(2,1)S(1)}, bf16[2,96,768]{2,1,0:T(8,128)(2,1)S(1)}, u32[]{:S(2)}, u32[]{:S(2)}) %collective-permute-start.34) | collective-permute-done | bytes 294944 | tf_op jit(solution)/shard_map/ppermute | solution.py:23
  172.0 1.6 finish.1
  (60 shorter events, 15.6 us)
Async XLA Ops:
  0.0 10.0 %collective-permute-start.2 = (bf16[512,768]{1,0:T(8,128)(2,1)}, bf16[512,768]{1,0:T(8,128)(2,1)}, u32[]{:S(2)}, u32[]{:S(2)}) collective-permute-start(bf16[512,768]{1,0:T(8,128)(2,1)} %refs_0_.2), channel_id=1, source_target_pairs={{0,1},{1,0},{2,3},{3,2},{4,5},{5,4},{6,7},{7,6},{8,9},{9,8},{10,11... | collective-permute-start | bytes 2359304 | tf_op jit(solution)/shard_map/ppermute | solution.py:23
  0.0 24.1 %collective-permute-start.1 = (bf16[512,768]{1,0:T(8,128)(2,1)}, bf16[512,768]{1,0:T(8,128)(2,1)S(1)}, u32[]{:S(2)}, u32[]{:S(2)}) collective-permute-start(bf16[512,768]{1,0:T(8,128)(2,1)} %refs_0_.2), channel_id=1, source_target_pairs={{0,66},{2,64},{64,2},{66,0},{1,67},{3,65},{65,3},{67,1},{4,70},{6,... | collective-permute-start | bytes 2359304 | tf_op jit(solution)/shard_map/ppermute | solution.py:27
  4.1 20.1 %collective-permute-start = (bf16[512,768]{1,0:T(8,128)(2,1)}, bf16[512,768]{1,0:T(8,128)(2,1)S(1)}, u32[]{:S(2)}, u32[]{:S(2)}) collective-permute-start(bf16[512,768]{1,0:T(8,128)(2,1)} %refs_0_.2), channel_id=1, source_target_pairs={{0,2},{2,0},{1,3},{3,1},{4,6},{6,4},{5,7},{7,5},{8,10},{10,8},{9,1... | collective-permute-start | bytes 2359304 | tf_op jit(solution)/shard_map/ppermute | solution.py:23
  5.5 4.5 %copy-start = (bf16[512,768]{1,0:T(8,128)(2,1)S(1)}, bf16[512,768]{1,0:T(8,128)(2,1)}, u32[]{:S(2)}) copy-start(bf16[512,768]{1,0:T(8,128)(2,1)} %refs_0_.2) | copy-start | bytes 2359300
  7.0 17.1 %collective-permute-start.3 = (f32[8,512]{1,0:T(8,128)S(1)}, f32[8,512]{1,0:T(8,128)S(1)}, u32[]{:S(2)}, u32[]{:S(2)}) collective-permute-start(f32[8,512]{1,0:T(8,128)S(1)} %concatenate.6), channel_id=1, source_target_pairs={{0,64},{64,0},{1,65},{65,1},{2,66},{66,2},{3,67},{67,3},{4,68},{68... | collective-permute-start | bytes 49160 | tf_op jit(solution)/shard_map/ppermute | solution.py:23
  24.2 4.1 %collective-permute-start.7 = (bf16[512,768]{1,0:T(8,128)(2,1)S(1)}, bf16[512,768]{1,0:T(8,128)(2,1)S(1)}, u32[]{:S(2)}, u32[]{:S(2)}) collective-permute-start(bf16[512,768]{1,0:T(8,128)(2,1)S(1)} %collective-permute-done.b.refs_0_.refs_2_), channel_id=1, source_target_pairs={{0,1},{1,0},{2,3},{3,2},{4,5},{5,4},{6,7},{7,6},{8,9},{9,8},{10,11... | collective-permute-start | bytes 2359304 | tf_op jit(solution)/shard_map/ppermute | solution.py:23
  24.2 13.5 %collective-permute-start.6 = (bf16[512,768]{1,0:T(8,128)(2,1)S(1)}, bf16[512,768]{1,0:T(8,128)(2,1)S(1)}, u32[]{:S(2)}, u32[]{:S(2)}) collective-permute-start(bf16[512,768]{1,0:T(8,128)(2,1)S(1)} %collective-permute-done.1.a.refs_0_.refs_4_), channel_id=1, source_target_pairs={{0,1},{1,0},{2,3},{3,2},{4,5},{5,4},{6,7},{7,6},{8,9},{9,8},{10,11... | collective-permute-start | bytes 2359304 | tf_op jit(solution)/shard_map/ppermute | solution.py:23
  25.3 11.5 %collective-permute-start.4 = (bf16[256,768]{1,0:T(8,128)(2,1)S(1)}, bf16[256,768]{1,0:T(8,128)(2,1)S(1)}, u32[]{:S(2)}, u32[]{:S(2)}) collective-permute-start(bf16[256,768]{1,0:T(8,128)(2,1)S(1)} %get-tuple-element.132), channel_id=1, source_target_pairs={{0,2},{2,0},{1,3},{3,1},{4,6},{6,4},{5,7},{7,5},{8,10},{10,8},{9,1... | collective-permute-start | bytes 1179656 | tf_op jit(solution)/shard_map/ppermute | solution.py:23
  25.7 12.0 %collective-permute-start.5 = (bf16[256,768]{1,0:T(8,128)(2,1)S(1)}, bf16[256,768]{1,0:T(8,128)(2,1)S(1)}, u32[]{:S(2)}, u32[]{:S(2)}) collective-permute-start(bf16[256,768]{1,0:T(8,128)(2,1)S(1)} %get-tuple-element.133), channel_id=1, source_target_pairs={{0,66},{2,64},{64,2},{66,0},{1,67},{3,65},{65,3},{67,1},{4,70},{6,... | collective-permute-start | bytes 1179656 | tf_op jit(solution)/shard_map/ppermute | solution.py:27
  37.7 16.8 %collective-permute-start.8 = (bf16[512,512]{1,0:T(8,128)(2,1)S(1)}, bf16[512,512]{1,0:T(8,128)(2,1)S(1)}, u32[]{:S(2)}, u32[]{:S(2)}) collective-permute-start(bf16[512,512]{1,0:T(8,128)(2,1)S(1)} %get-tuple-element.142), channel_id=1, source_target_pairs={{0,64},{64,0},{1,65},{65,1},{2,66},{66,2},{3,67},{67,3},{4,68},{68... | collective-permute-start | bytes 1572872 | tf_op jit(solution)/shard_map/ppermute | solution.py:23
  40.5 3.7 %collective-permute-start.9 = (bf16[256,768]{1,0:T(8,128)(2,1)S(1)}, bf16[256,768]{1,0:T(8,128)(2,1)S(1)}, u32[]{:S(2)}, u32[]{:S(2)}) collective-permute-start(bf16[256,768]{1,0:T(8,128)(2,1)S(1)} %collective-permute-done.4.refs_2_.refs_0_), channel_id=1, source_target_pairs={{0,1},{1,0},{2,3},{3,2},{4,5},{5,4},{6,7},{7,6},{8,9},{9,8},{10,11... | collective-permute-start | bytes 1179656 | tf_op jit(solution)/shard_map/ppermute | solution.py:23
  40.5 3.7 %collective-permute-start.10 = (bf16[256,768]{1,0:T(8,128)(2,1)S(1)}, bf16[256,768]{1,0:T(8,128)(2,1)S(1)}, u32[]{:S(2)}, u32[]{:S(2)}) collective-permute-start(bf16[256,768]{1,0:T(8,128)(2,1)S(1)} %collective-permute-done.5.refs_3_.refs_1_), channel_id=1, source_target_pairs={{0,1},{1,0},{2,3},{3,2},{4,5},{5,4},{6,7},{7,6},{8,9},{9,8},{10,11... | collective-permute-start | bytes 1179656 | tf_op jit(solution)/shard_map/ppermute | solution.py:23
  56.8 9.8 %collective-permute-start.11 = (bf16[528,128]{1,0:T(8,128)(2,1)S(1)}, bf16[528,128]{1,0:T(8,128)(2,1)S(1)}, u32[]{:S(2)}, u32[]{:S(2)}) collective-permute-start(bf16[528,128]{1,0:T(8,128)(2,1)S(1)} %get-tuple-element.162), channel_id=1, source_target_pairs={{0,4},{4,0},{8,12},{12,8},{1,5},{5,1},{9,13},{13,9},{2,6},{6,2},{1... | collective-permute-start | bytes 405512 | tf_op jit(solution)/shard_map/ppermute | solution.py:23
  58.5 8.2 %collective-permute-start.12 = (bf16[528,128]{1,0:T(8,128)(2,1)S(1)}, bf16[528,128]{1,0:T(8,128)(2,1)S(1)}, u32[]{:S(2)}, u32[]{:S(2)}) collective-permute-start(bf16[528,128]{1,0:T(8,128)(2,1)S(1)} %get-tuple-element.163), channel_id=1, source_target_pairs={{0,12},{4,8},{8,4},{12,0},{1,13},{5,9},{9,5},{13,1},{2,14},{6,10},... | collective-permute-start | bytes 405512 | tf_op jit(solution)/shard_map/ppermute | solution.py:23
  60.7 7.1 %collective-permute-start.13 = (bf16[528,128]{1,0:T(8,128)(2,1)S(1)}, bf16[528,128]{1,0:T(8,128)(2,1)S(1)}, u32[]{:S(2)}, u32[]{:S(2)}) collective-permute-start(bf16[528,128]{1,0:T(8,128)(2,1)S(1)} %get-tuple-element.164), channel_id=1, source_target_pairs={{0,8},{4,12},{8,0},{12,4},{1,9},{5,13},{9,1},{13,5},{2,10},{6,14},... | collective-permute-start | bytes 405512 | tf_op jit(solution)/shard_map/ppermute | solution.py:23
  68.6 7.5 %collective-permute-start.16 = (bf16[528,128]{1,0:T(8,128)(2,1)S(1)}, bf16[528,128]{1,0:T(8,128)(2,1)S(1)}, u32[]{:S(2)}, u32[]{:S(2)}) collective-permute-start(bf16[528,128]{1,0:T(8,128)(2,1)S(1)} %get-tuple-element.180.a), channel_id=1, source_target_pairs={{0,32},{16,48},{32,0},{48,16},{1,33},{17,49},{33,1},{49,17},{2,34}... | collective-permute-start | bytes 405512 | tf_op jit(solution)/shard_map/ppermute | solution.py:23
  71.7 6.4 %collective-permute-start.15 = (bf16[528,128]{1,0:T(8,128)(2,1)S(1)}, bf16[528,128]{1,0:T(8,128)(2,1)S(1)}, u32[]{:S(2)}, u32[]{:S(2)}) collective-permute-start(bf16[528,128]{1,0:T(8,128)(2,1)S(1)} %get-tuple-element.180.a), channel_id=1, source_target_pairs={{0,48},{16,32},{32,16},{48,0},{1,49},{17,33},{33,17},{49,1},{2,50}... | collective-permute-start | bytes 405512 | tf_op jit(solution)/shard_map/ppermute | solution.py:23
  72.8 5.3 %collective-permute-start.14 = (bf16[528,128]{1,0:T(8,128)(2,1)S(1)}, bf16[528,128]{1,0:T(8,128)(2,1)S(1)}, u32[]{:S(2)}, u32[]{:S(2)}) collective-permute-start(bf16[528,128]{1,0:T(8,128)(2,1)S(1)} %get-tuple-element.180.a), channel_id=1, source_target_pairs={{0,16},{16,0},{32,48},{48,32},{1,17},{17,1},{33,49},{49,33},{2,18}... | collective-permute-start | bytes 405512 | tf_op jit(solution)/shard_map/ppermute | solution.py:23
  79.0 7.4 %collective-permute-start.17 = (bf16[512,128]{1,0:T(8,128)(2,1)S(1)}, bf16[512,128]{1,0:T(8,128)(2,1)S(1)}, u32[]{:S(2)}, u32[]{:S(2)}) collective-permute-start(bf16[512,128]{1,0:T(8,128)(2,1)S(1)} %get-tuple-element.191), channel_id=1, source_target_pairs={{0,4},{4,0},{8,12},{12,8},{1,5},{5,1},{9,13},{13,9},{2,6},{6,2},{1... | collective-permute-start | bytes 393224 | tf_op jit(solution)/shard_map/ppermute | solution.py:23
  79.1 7.5 %collective-permute-start.18 = (bf16[512,128]{1,0:T(8,128)(2,1)S(1)}, bf16[512,128]{1,0:T(8,128)(2,1)S(1)}, u32[]{:S(2)}, u32[]{:S(2)}) collective-permute-start(bf16[512,128]{1,0:T(8,128)(2,1)S(1)} %get-tuple-element.192), channel_id=1, source_target_pairs={{0,12},{4,8},{8,4},{12,0},{1,13},{5,9},{9,5},{13,1},{2,14},{6,10},... | collective-permute-start | bytes 393224 | tf_op jit(solution)/shard_map/ppermute | solution.py:23
  81.3 6.7 %collective-permute-start.19 = (bf16[512,128]{1,0:T(8,128)(2,1)S(1)}, bf16[512,128]{1,0:T(8,128)(2,1)S(1)}, u32[]{:S(2)}, u32[]{:S(2)}) collective-permute-start(bf16[512,128]{1,0:T(8,128)(2,1)S(1)} %get-tuple-element.193), channel_id=1, source_target_pairs={{0,8},{4,12},{8,0},{12,4},{1,9},{5,13},{9,1},{13,5},{2,10},{6,14},... | collective-permute-start | bytes 393224 | tf_op jit(solution)/shard_map/ppermute | solution.py:23
  96.3 14.9 %collective-permute-start.21 = (bf16[384,768]{1,0:T(8,128)(2,1)S(1)}, bf16[384,768]{1,0:T(8,128)(2,1)S(1)}, u32[]{:S(2)}, u32[]{:S(2)}) collective-permute-start(bf16[384,768]{1,0:T(8,128)(2,1)S(1)} %get-tuple-element.220), channel_id=1, source_target_pairs={{0,48},{16,32},{32,16},{48,0},{1,49},{17,33},{33,17},{49,1},{2,50}... | collective-permute-start | bytes 1769480 | tf_op jit(solution)/shard_map/ppermute | solution.py:23
  98.8 13.8 %collective-permute-start.20 = (bf16[384,768]{1,0:T(8,128)(2,1)S(1)}, bf16[384,768]{1,0:T(8,128)(2,1)S(1)}, u32[]{:S(2)}, u32[]{:S(2)}) collective-permute-start(bf16[384,768]{1,0:T(8,128)(2,1)S(1)} %get-tuple-element.216), channel_id=1, source_target_pairs={{0,16},{16,0},{32,48},{48,32},{1,17},{17,1},{33,49},{49,33},{2,18}... | collective-permute-start | bytes 1769480 | tf_op jit(solution)/shard_map/ppermute | solution.py:23
  98.8 15.8 %collective-permute-start.24 = (bf16[384,768]{1,0:T(8,128)(2,1)S(1)}, bf16[384,768]{1,0:T(8,128)(2,1)S(1)}, u32[]{:S(2)}, u32[]{:S(2)}) collective-permute-start(bf16[384,768]{1,0:T(8,128)(2,1)S(1)} %get-tuple-element.229), channel_id=1, source_target_pairs={{0,4},{4,0},{8,12},{12,8},{1,5},{5,1},{9,13},{13,9},{2,6},{6,2},{1... | collective-permute-start | bytes 1769480 | tf_op jit(solution)/shard_map/ppermute | solution.py:23
  99.5 15.2 %collective-permute-start.25 = (bf16[384,768]{1,0:T(8,128)(2,1)S(1)}, bf16[384,768]{1,0:T(8,128)(2,1)S(1)}, u32[]{:S(2)}, u32[]{:S(2)}) collective-permute-start(bf16[384,768]{1,0:T(8,128)(2,1)S(1)} %get-tuple-element.230), channel_id=1, source_target_pairs={{0,12},{4,8},{8,4},{12,0},{1,13},{5,9},{9,5},{13,1},{2,14},{6,10},... | collective-permute-start | bytes 1769480 | tf_op jit(solution)/shard_map/ppermute | solution.py:23
  114.1 27.3 %collective-permute-start.22 = (bf16[768,768]{1,0:T(8,128)(2,1)S(1)}, bf16[768,768]{1,0:T(8,128)(2,1)S(1)}, u32[]{:S(2)}, u32[]{:S(2)}) collective-permute-start(bf16[768,768]{1,0:T(8,128)(2,1)S(1)} %get-tuple-element.225), channel_id=1, source_target_pairs={{0,16},{16,0},{32,48},{48,32},{1,17},{17,1},{33,49},{49,33},{2,18}... | collective-permute-start | bytes 3538952 | tf_op jit(solution)/shard_map/ppermute | solution.py:23
  114.7 26.7 %collective-permute-start.23 = (bf16[768,768]{1,0:T(8,128)(2,1)S(1)}, bf16[768,768]{1,0:T(8,128)(2,1)S(1)}, u32[]{:S(2)}, u32[]{:S(2)}) collective-permute-start(bf16[768,768]{1,0:T(8,128)(2,1)S(1)} %get-tuple-element.226), channel_id=1, source_target_pairs={{0,48},{16,32},{32,16},{48,0},{1,49},{17,33},{33,17},{49,1},{2,50}... | collective-permute-start | bytes 3538952 | tf_op jit(solution)/shard_map/ppermute | solution.py:23
  117.4 26.8 %collective-permute-start.27 = (bf16[768,768]{1,0:T(8,128)(2,1)S(1)}, bf16[768,768]{1,0:T(8,128)(2,1)S(1)}, u32[]{:S(2)}, u32[]{:S(2)}) collective-permute-start(bf16[768,768]{1,0:T(8,128)(2,1)S(1)} %get-tuple-element.242), channel_id=1, source_target_pairs={{0,12},{4,8},{8,4},{12,0},{1,13},{5,9},{9,5},{13,1},{2,14},{6,10},... | collective-permute-start | bytes 3538952 | tf_op jit(solution)/shard_map/ppermute | solution.py:23
  118.7 25.5 %collective-permute-start.26 = (bf16[768,768]{1,0:T(8,128)(2,1)S(1)}, bf16[768,768]{1,0:T(8,128)(2,1)S(1)}, u32[]{:S(2)}, u32[]{:S(2)}) collective-permute-start(bf16[768,768]{1,0:T(8,128)(2,1)S(1)} %get-tuple-element.233), channel_id=1, source_target_pairs={{0,4},{4,0},{8,12},{12,8},{1,5},{5,1},{9,13},{13,9},{2,6},{6,2},{1... | collective-permute-start | bytes 3538952 | tf_op jit(solution)/shard_map/ppermute | solution.py:23
  145.6 9.0 %collective-permute-start.28 = (bf16[192,768]{1,0:T(8,128)(2,1)S(1)}, bf16[192,768]{1,0:T(8,128)(2,1)S(1)}, u32[]{:S(2)}, u32[]{:S(2)}) collective-permute-start(bf16[192,768]{1,0:T(8,128)(2,1)S(1)} %get-tuple-element.245), channel_id=1, source_target_pairs={{0,4},{4,0},{8,12},{12,8},{1,5},{5,1},{9,13},{13,9},{2,6},{6,2},{1... | collective-permute-start | bytes 884744 | tf_op jit(solution)/shard_map/ppermute | solution.py:23
  145.7 11.0 %collective-permute-start.29 = (bf16[192,768]{1,0:T(8,128)(2,1)S(1)}, bf16[192,768]{1,0:T(8,128)(2,1)S(1)}, u32[]{:S(2)}, u32[]{:S(2)}) collective-permute-start(bf16[192,768]{1,0:T(8,128)(2,1)S(1)} %get-tuple-element.246), channel_id=1, source_target_pairs={{0,16},{16,0},{32,48},{48,32},{1,17},{17,1},{33,49},{49,33},{2,18}... | collective-permute-start | bytes 884744 | tf_op jit(solution)/shard_map/ppermute | solution.py:23
  146.9 12.6 %collective-permute-start.30 = (bf16[192,768]{1,0:T(8,128)(2,1)S(1)}, bf16[192,768]{1,0:T(8,128)(2,1)S(1)}, u32[]{:S(2)}, u32[]{:S(2)}) collective-permute-start(bf16[192,768]{1,0:T(8,128)(2,1)S(1)} %get-tuple-element.247), channel_id=1, source_target_pairs={{0,12},{4,8},{8,4},{12,0},{1,13},{5,9},{9,5},{13,1},{2,14},{6,10},... | collective-permute-start | bytes 884744 | tf_op jit(solution)/shard_map/ppermute | solution.py:23
  148.8 10.7 %collective-permute-start.31 = (bf16[192,768]{1,0:T(8,128)(2,1)S(1)}, bf16[192,768]{1,0:T(8,128)(2,1)S(1)}, u32[]{:S(2)}, u32[]{:S(2)}) collective-permute-start(bf16[192,768]{1,0:T(8,128)(2,1)S(1)} %get-tuple-element.248), channel_id=1, source_target_pairs={{0,48},{16,32},{32,16},{48,0},{1,49},{17,33},{33,17},{49,1},{2,50}... | collective-permute-start | bytes 884744 | tf_op jit(solution)/shard_map/ppermute | solution.py:23
  150.2 9.2 %collective-permute-start.32 = (bf16[192,768]{1,0:T(8,128)(2,1)S(1)}, bf16[192,768]{1,0:T(8,128)(2,1)S(1)}, u32[]{:S(2)}, u32[]{:S(2)}) collective-permute-start(bf16[192,768]{1,0:T(8,128)(2,1)S(1)} %get-tuple-element.249), channel_id=1, source_target_pairs={{0,8},{4,12},{8,0},{12,4},{1,9},{5,13},{9,1},{13,5},{2,10},{6,14},... | collective-permute-start | bytes 884744 | tf_op jit(solution)/shard_map/ppermute | solution.py:23
  154.7 8.2 %collective-permute-start.33 = (bf16[192,768]{1,0:T(8,128)(2,1)S(1)}, bf16[192,768]{1,0:T(8,128)(2,1)S(1)}, u32[]{:S(2)}, u32[]{:S(2)}) collective-permute-start(bf16[192,768]{1,0:T(8,128)(2,1)S(1)} %get-tuple-element.250), channel_id=1, source_target_pairs={{0,32},{16,48},{32,0},{48,16},{1,33},{17,49},{33,1},{49,17},{2,34}... | collective-permute-start | bytes 884744 | tf_op jit(solution)/shard_map/ppermute | solution.py:23
  163.7 8.3 %collective-permute-start.34 = (bf16[2,96,768]{2,1,0:T(8,128)(2,1)S(1)}, bf16[2,96,768]{2,1,0:T(8,128)(2,1)S(1)}, u32[]{:S(2)}, u32[]{:S(2)}) collective-permute-start(bf16[2,96,768]{2,1,0:T(8,128)(2,1)S(1)} %get-tuple-element.252), channel_id=1, source_target_pairs={{0,64},{64,0},{1,65},{65,1},{2,66},{66,2},{3,67},{67,3},{4,68},{68... | collective-permute-start | bytes 884744 | tf_op jit(solution)/shard_map/ppermute | solution.py:23

commit v8 on v7

--- a/solution.py
+++ b/solution.py
@@ -342,46 +342,49 @@
     )
 
 
-def whole_grads(table, which, local, ready, states):
-    tokens = local.shape[1]
-    heads = local.shape[2] // HEAD
-
-    def body(s, local_ref, ready_ref, a, b, c, d, left, right, held):
-        h = pl.program_id(0)
-
-        @pl.when(h == 0)
+def whole_grads(table, own, pair, states):
+    tokens, heads = own[0].shape[1], HEADS
+
+    def body(s, local_a, ready_a, local_b, ready_b, a, b, c, d, *rest):
+        outs, held = rest[:4], rest[4]
+        i = pl.program_id(0)
+
+        @pl.when(i == 0)
         def _():
             in_order((a, b, c, d), s[Y], held)
 
-        base = pl.multiple_of((s[Z] ^ which) * HEAD, HEAD)
-        coming = held[h, pl.ds(base, HEAD), :]
-        later = held[h, pl.ds(2 * HEAD + base, HEAD), :]
-        cross = (
-            lax.dot_general(ready_ref[0], coming, AB_T, preferred_element_type=F32),
-            lax.dot_general(ready_ref[1], later, AB_T, preferred_element_type=F32),
-            dot(ready_ref[2], later),
-        )
-        grads = [(local_ref[j].astype(F32) + cross[j]).astype(BF16) for j in range(3)]
-        for k in range(heads):
-
-            @pl.when(h == k)
-            def _(k=k):
-                for j in range(3):
-                    start = (2 * j + k % 2) * HEAD
-                    (left, right)[k // 2][:, start : start + HEAD] = grads[j]
-
-    tile = pl.BlockSpec((3, tokens, HEAD), lambda h, s: (0, 0, h))
+        for which, (local_ref, ready_ref) in enumerate(((local_a, ready_a), (local_b, ready_b))):
+            for k in range(heads):
+
+                @pl.when(i == which * heads + k)
+                def _(k=k, which=which, local_ref=local_ref, ready_ref=ready_ref):
+                    base = pl.multiple_of((s[Z] ^ which) * HEAD, HEAD)
+                    coming = held[k, pl.ds(base, HEAD), :]
+                    later = held[k, pl.ds(2 * HEAD + base, HEAD), :]
+                    cross = (
+                        lax.dot_general(ready_ref[0], coming, AB_T, preferred_element_type=F32),
+                        lax.dot_general(ready_ref[1], later, AB_T, preferred_element_type=F32),
+                        dot(ready_ref[2], later),
+                    )
+                    out = outs[2 * which + k // 2]
+                    for j in range(3):
+                        start = (2 * j + k % 2) * HEAD
+                        total = local_ref[j].astype(F32) + cross[j]
+                        out[:, start : start + HEAD] = total.astype(BF16)
+
+    first = pl.BlockSpec((3, tokens, HEAD), lambda i, s: (0, 0, jnp.minimum(i, heads - 1)))
+    second = pl.BlockSpec((3, tokens, HEAD), lambda i, s: (0, 0, jnp.maximum(i - heads, 0)))
     side = shape((tokens, 3 * heads * HEAD // 2))
     return call(
         "whole_grads",
         body,
         table,
-        (heads,),
-        (local, ready, *states),
-        [tile, tile, *[whole(m) for m in states]],
-        [side, side],
-        [whole(side)] * 2,
-        12,
+        (2 * heads,),
+        (*own, *pair, *states),
+        [first, first, second, second, *[whole(m) for m in states]],
+        [side] * 4,
+        [whole(side)] * 4,
+        16,
         [pltpu.VMEM((4, *states[0].shape), BF16)],
     )
 
@@ -511,45 +514,43 @@
     return cut[:4], cut[4:]
 
 
-def final_sums(table, sides):
-    rows, cols = sides[0][0].shape
-
-    def body(s, *refs):
-        here, there = refs[-2:]
-        for k in range(2):
-            total = sum(ref[...].astype(F32) for ref in refs[k:8:2]).astype(BF16)
-            here[k] = total[: rows // 2]
-            there[k] = total[rows // 2 :]
-
-    operands = [x for both in zip(*sides) for x in both]
-    outs = [shape((2, rows // 2, cols))] * 2
+def final_sums(table, parts):
+    rows, cols = parts[0].shape
+
+    def body(s, a, b, c, d, here, there):
+        total = sum(ref[...].astype(F32) for ref in (a, b, c, d)).astype(BF16)
+        here[...] = total[: rows // 2]
+        there[...] = total[rows // 2 :]
+
+    outs = [shape((rows // 2, cols))] * 2
     return call(
         "final_sums",
         body,
         table,
         (1,),
-        operands,
-        [whole(x) for x in operands],
+        parts,
+        [whole(x) for x in parts],
         outs,
         [whole(o) for o in outs],
-        12,
+        8,
     )
 
 
 def finish(table, here, there):
-    _, rows, cols = here.shape
+    rows, cols = here[0].shape
     side = cols // 3
 
-    def body(s, here_ref, there_ref, out):
-        for ref, half in ((here_ref, s[Z]), (there_ref, 1 - s[Z])):
+    def body(s, *refs):
+        out = refs[-1]
+        for i, half in enumerate((s[Z], 1 - s[Z])):
             for k in range(2):
                 for j in range(3):
                     at = pl.ds(pl.multiple_of(half * 2 * side + k * side, side), side)
-                    out[j, :, at] = ref[k, :, j * side : (j + 1) * side].astype(F32)
+                    out[j, :, at] = refs[2 * i + k][:, j * side : (j + 1) * side].astype(F32)
 
     out = shape((3, rows, 4 * side), F32)
-    operands = (here, there)
-    return call("finish", body, table, (1,), operands, [whole(here)] * 2, out, whole(out), 8)
+    operands = (*here, *there)
+    return call("finish", body, table, (1,), operands, [whole(x) for x in operands], out, whole(out), 8)
 
 
 def swaps(pieces, left, right):
@@ -596,8 +597,6 @@
     far, side_core, qkv_own, turned = tied((far, side_core, qkv_own, turned))
     far_core = [send(x, "co", 1) for x in far]
     og_pair = send(tied((og_other, far))[0], "c0", 1)
-    local_own = local_grads(table, qkv_own, og_own, info, 0, per // 2, None)
-    far_core, local_own = tied((far_core, local_own))
     qkv_pair = project(
         table, [[side], [side_core], far, far_core], (2, 3, 0, 1), weight, None, note
     )
@@ -608,15 +607,15 @@
     to_y = shard_states(table, qkv_pair, og_pair, note, 1, to_y)
     at_y = [send(to_y[r], "c2", r) for r in (1, 3, 2)]
     qkv_own, _ = tied((qkv_own, to_y[0]))
-    local_own = local_grads(table, qkv_own, og_own, info, per // 2, per // 2, local_own)
-    second, _ = tied(([far, far_core, [side], [side_core]], to_y[0]))
-    turned.append(turn(table, second))
-    at_y, local_own, turned = tied((at_y, local_own, turned))
+    local_own = local_grads(table, qkv_own, og_own, info, 0, per, None)
+    at_y, local_own = tied((at_y, local_own))
     before, after, prior, later, ring = ring_y(table, [to_y[0], at_y[0], at_y[2], at_y[1]])
     at_x = [send(ring, "c1", r) for r in (1, 3, 2)]
     qkv_pair, _ = tied((qkv_pair, ring))
     local = local_grads(table, qkv_pair, og_pair, note, 0, per // 2, None)
-    at_x, local = tied((at_x, local))
+    second, _ = tied(([far, far_core, [side], [side_core]], ring))
+    turned.append(turn(table, second))
+    at_x, local, turned = tied((at_x, local, turned))
     back = arrivals(table, [ring, at_x[0], at_x[2], at_x[1]], before, after, prior, later)
     states = [send(back[r], "c2", r) for r in (1, 3, 2)]
     local, _ = tied((local, back[0]))
@@ -624,8 +623,7 @@
     states, turned, local = tied((states, turned, local))
     states = [back[0], states[0], states[2], states[1]]
 
-    left_own, right_own = whole_grads(table, 0, *local_own, states)
-    left_pair, right_pair = whole_grads(table, 1, *local, states)
+    left_own, right_own, left_pair, right_pair = whole_grads(table, local_own, local, states)
     lefts, rights = (left_own, left_pair), (right_own, right_pair)
     far_piece = weight_part(table, turned, lefts, rights, (2,), True)
     l_half, r_half = swaps(far_piece, "c1", "c2")
@@ -641,13 +639,13 @@
     own = weight_part(table, turned, lefts, rights, (0,), False)
     l_got, own = tied((l_got, own))
     l_cut, r_cut = cut_blocks(table, (own[0], *l_got), (own[1], *r_got))
-    l_got, r_got = [], []
-    for k, by in enumerate((1, 3, 2)):
-        l_got.append(send(l_cut[k], "c2", by))
-        r_got.append(send(r_cut[k], "c1", by))
-    here, there = final_sums(table, ((l_cut[3], *l_got), (r_cut[3], *r_got)))
-    there = send(there, "c0", 1)
-    return jnp.transpose(finish(table, here, there), (1, 0, 2))
+    l_got = [send(x, "c2", by) for x, by in zip(l_cut, (1, 3, 2))]
+    r_got = [send(x, "c1", by) for x, by in zip(r_cut, (1, 3, 2))]
+    l_here, l_there = final_sums(table, (l_cut[3], *l_got))
+    r_got, _ = tied((r_got, l_here))
+    r_here, r_there = final_sums(table, (r_cut[3], *r_got))
+    there = [send(x, "c0", 1) for x in (l_there, r_there)]
+    return jnp.transpose(finish(table, (l_here, r_here), there), (1, 0, 2))
 
 
 def solution(mesh):

time: 174 us -> 168 us (0.966)
  waiting for transfers between devices: 55.7 us -> 50.1 us
    ppermute x33 -> x34, waiting for transfers between devices: 54.9 us -> 49.2 us  [send(): lax.ppermute(x, axis, [(i, i ^ by) for i in range(lax.axis_size(axis))])]
    pallas_call x24 -> x23, Pallas kernels: 70.1 us -> 69.5 us  [call(): pl.pallas_call(body, grid_spec=pltpu.PrefetchScalarGridSpec(num_scalar_pr...]
    ppermute x33 -> x34, starting transfers between devices: 36.6 us -> 37.1 us  [send(): lax.ppermute(x, axis, [(i, i ^ by) for i in range(lax.axis_size(axis))])]
  transfers between devices with their start and end apart: 35 -> 36, of which waited for: 16 -> 20; matrix products, arithmetic and copies ran while one was open for 2% -> 2% of each run, Pallas kernels for 31% -> 33%
where the time goes in v8:
time: 168 us
  Pallas kernels  69.5 us (41%)
  waiting for transfers between devices  50.1 us (30%)
  starting transfers between devices  43.8 us (26%)
  other arithmetic  1.96 us (1%)
    pallas_call x23, Pallas kernels, call(): pl.pallas_call(body, grid_spec=pltpu.PrefetchScalarGridSpec(num_scalar_pr...  69.5 us
    ppermute x34, waiting for transfers between devices, send(): lax.ppermute(x, axis, [(i, i ^ by) for i in range(lax.axis_size(axis))])  49.2 us
    ppermute x34, starting transfers between devices, send(): lax.ppermute(x, axis, [(i, i ^ by) for i in range(lax.axis_size(axis))])  37.1 us
    ppermute x2, starting transfers between devices, across(): return lax.ppermute(x, ('c0', 'zl'), [(0, 3), (1, 2), (2, 1), (3, 0)])  6.75 us
  transfers between devices with their start and end apart: 36, of which 20 were waited for; matrix products, arithmetic and copies ran while one was open for 2% of the time, Pallas kernels for 33%

profile of v8, /device:TPU:0, one launch (start us, length us, event | category | flops | bytes accessed | tf_op | source)
XLA Modules:
  0.0 167.9 jit_solution(15275003861496123064)
XLA Ops:
  0.0 4.1 %collective-permute-start.1 = (bf16[512,768]{1,0:T(8,128)(2,1)}, bf16[512,768]{1,0:T(8,128)(2,1)S(1)}, u32[]{:S(2)}, u32[]{:S(2)}) collective-permute-start(bf16[512,768]{1,0:T(8,128)(2,1)} %refs_0_.2), channel_id=1, source_target_pairs={{0,66},{2,64},{64,2},{66,0},{1,67},{3,65},{65,3},{67,1},{4,70},{6,... | collective-permute-start | bytes 2359304 | tf_op jit(solution)/shard_map/ppermute | solution.py:27
  5.5 1.1 reduce-window.6
  7.0 1.6 collective-permute-start.3
  8.6 1.3 constant_dynamic-slice_fusion
  10.0 5.5 %project.3.refs_4_ = f32[3,512,512]{2,1,0:T(8,128)S(1)} custom-call(s32[6]{0:T(128)S(1)} %stack.27.s, bf16[512,768]{1,0:T(8,128)(2,1)S(1)} %copy-done, bf16[512,768]{1,0:T(8,128)(2,1)} %collective-permute-done.2.refs_1_, bf16[3,3072,1024]{2,1,0:T(8,128)(2,1)} %bitcast.31, bf16[3,3072,1024]{2,1,0:T(8,128)(2,1)} %bitcast.32), custom_call_target="tpu_custom_call" | custom-call | flops 1 | bytes 1 | tf_op jit(solution)/shard_map/project/pallas_call | solution.py:35
  15.5 8.6 %collective-permute-done.3.refs_10_.cum_ref = f32[8,512]{1,0:T(8,128)S(1)} collective-permute-done((f32[8,512]{1,0:T(8,128)S(1)}, f32[8,512]{1,0:T(8,128)S(1)}, u32[]{:S(2)}, u32[]{:S(2)}) %collective-permute-start.3) | collective-permute-done | bytes 16416 | tf_op jit(solution)/shard_map/ppermute | solution.py:23
  25.7 2.6 %collective-permute-start.5 = (bf16[256,768]{1,0:T(8,128)(2,1)S(1)}, bf16[256,768]{1,0:T(8,128)(2,1)S(1)}, u32[]{:S(2)}, u32[]{:S(2)}) collective-permute-start(bf16[256,768]{1,0:T(8,128)(2,1)S(1)} %get-tuple-element.132), channel_id=1, source_target_pairs={{0,66},{2,64},{64,2},{66,0},{1,67},{3,65},{65,3},{67,1},{4,70},{6,... | collective-permute-start | bytes 1179656 | tf_op jit(solution)/shard_map/ppermute | solution.py:27
  28.3 5.3 %project.4.qkv_ref = bf16[3,512,512]{2,1,0:T(8,128)(2,1)S(1)} custom-call(s32[6]{0:T(128)S(1)} %stack.27.s, bf16[512,768]{1,0:T(8,128)(2,1)S(1)} %collective-permute-done.b.refs_0_.refs_2_, bf16[512,768]{1,0:T(8,128)(2,1)S(1)} %collective-permute-done.7.refs_1_.refs_3_, bf16[3,3072,1024]{2,1,0:T(8,128)(2,1)} %bitcast.33, bf16[3,3072,1024]{2,1,0:T(8,128)(2,1)} %bitcast.34, ...), custom_call_target="tpu_custom_call" | custom-call | flops 1 | bytes 1 | tf_op jit(solution)/shard_map/project/pallas_call | solution.py:35
  33.6 3.2 %turn.2 = bf16[16,2,96,512]{3,2,1,0:T(8,128)(2,1)S(1)} custom-call(s32[6]{0:T(128)S(1)} %stack.27.s, bf16[512,768]{1,0:T(8,128)(2,1)S(1)} %copy-done, bf16[512,768]{1,0:T(8,128)(2,1)} %collective-permute-done.2.refs_1_, bf16[512,768]{1,0:T(8,128)(2,1)S(1)} %collective-permute-done.b.refs_0_.refs_2_, bf16[512,768]{1,0:T(8,128)(2,1)S(1)} %collective-permute-done.7.refs_1_.refs_3_), custom_call_target="tpu_custom_call" | custom-call | flops 1 | bytes 1 | tf_op jit(solution)/shard_map/turn/pallas_call | solution.py:35
  37.7 2.8 %collective-permute-start.8 = (bf16[512,512]{1,0:T(8,128)(2,1)S(1)}, bf16[512,512]{1,0:T(8,128)(2,1)S(1)}, u32[]{:S(2)}, u32[]{:S(2)}) collective-permute-start(bf16[512,512]{1,0:T(8,128)(2,1)S(1)} %get-tuple-element.141), channel_id=1, source_target_pairs={{0,64},{64,0},{1,65},{65,1},{2,66},{66,2},{3,67},{67,3},{4,68},{68... | collective-permute-start | bytes 1572872 | tf_op jit(solution)/shard_map/ppermute | solution.py:23
  41.0 1.2 collective-permute-done.9.refs_4_.refs_2_
  42.8 7.9 %project.5.qkv_ref = bf16[3,512,512]{2,1,0:T(8,128)(2,1)S(1)} custom-call(s32[6]{0:T(128)S(1)} %stack.27.s, bf16[512,768]{1,0:T(8,128)(2,1)S(1)} %collective-permute-done.1.a.refs_0_.refs_4_, bf16[512,768]{1,0:T(8,128)(2,1)S(1)} %collective-permute-done.6.refs_1_.refs_5_, bf16[256,768]{1,0:T(8,128)(2,1)S(1)} %collective-permute-done.4.refs_2_.refs_0_, ...), custom_call_target="tpu_custom_call" | custom-call | flops 1 | bytes 1 | tf_op jit(solution)/shard_map/project/pallas_call | solution.py:35
  50.7 2.3 %shard_states.2 = (bf16[528,128]{1,0:T(8,128)(2,1)S(1)}, bf16[528,128]{1,0:T(8,128)(2,1)S(1)}, bf16[528,128]{1,0:T(8,128)(2,1)S(1)}, bf16[528,128]{1,0:T(8,128)(2,1)S(1)}) custom-call(s32[6]{0:T(128)S(1)} %stack.27.s, bf16[3,512,512]{2,1,0:T(8,128)(2,1)S(1)} %project.4.qkv_ref, bf16[512,512]{1,0:T(8,128)(2,1)S(1)} %get-tuple-element.251.og_ref, ...), custom_call_target="tpu_custom_call" | custom-call | flops 1 | bytes 1 | tf_op jit(solution)/shard_map/shard_states/pallas_call | solution.py:35
  53.0 2.3 %shard_states.3 = (bf16[528,128]{1,0:T(8,128)(2,1)S(1)}, bf16[528,128]{1,0:T(8,128)(2,1)S(1)}, bf16[528,128]{1,0:T(8,128)(2,1)S(1)}, bf16[528,128]{1,0:T(8,128)(2,1)S(1)}) custom-call(s32[6]{0:T(128)S(1)} %stack.27.s, bf16[3,512,512]{2,1,0:T(8,128)(2,1)S(1)} %project.5.qkv_ref, bf16[512,512]{1,0:T(8,128)(2,1)S(1)} %collective-permute-done.8.og_ref, ...), custom_call_target="tpu_custom_call" | custom-call | flops 1 | bytes 1 | tf_op jit(solution)/shard_map/shard_states/pallas_call | solution.py:35
  55.4 1.7 collective-permute-start.11
  57.0 2.2 %collective-permute-start.12 = (bf16[528,128]{1,0:T(8,128)(2,1)S(1)}, bf16[528,128]{1,0:T(8,128)(2,1)S(1)}, u32[]{:S(2)}, u32[]{:S(2)}) collective-permute-start(bf16[528,128]{1,0:T(8,128)(2,1)S(1)} %get-tuple-element.158), channel_id=1, source_target_pairs={{0,12},{4,8},{8,4},{12,0},{1,13},{5,9},{9,5},{13,1},{2,14},{6,10},... | collective-permute-start | bytes 405512 | tf_op jit(solution)/shard_map/ppermute | solution.py:23
  59.9 5.9 %local_grads.3 = (bf16[3,512,512]{2,1,0:T(8,128)(2,1)S(1)}, bf16[3,512,512]{2,1,0:T(8,128)(2,1)S(1)}) custom-call(s32[6]{0:T(128)S(1)} %stack.27.s, bf16[3,512,512]{2,1,0:T(8,128)(2,1)S(1)} %project.4.qkv_ref, bf16[512,512]{1,0:T(8,128)(2,1)S(1)} %get-tuple-element.251.og_ref, f32[8,512]{1,0:T(8,128)S(1)} %concatenate.7.refs_5_.cum_ref), custom_call_target="tpu_custom_call" | custom-call | flops 1 | bytes 1 | tf_op jit(solution)/shard_map/local_grads/pallas_call | solution.py:35
  67.2 3.1 %collective-permute-start.16 = (bf16[528,128]{1,0:T(8,128)(2,1)S(1)}, bf16[528,128]{1,0:T(8,128)(2,1)S(1)}, u32[]{:S(2)}, u32[]{:S(2)}) collective-permute-start(bf16[528,128]{1,0:T(8,128)(2,1)S(1)} %get-tuple-element.166.a), channel_id=1, source_target_pairs={{0,32},{16,48},{32,0},{48,16},{1,33},{17,49},{33,1},{49,17},{2,34}... | collective-permute-start | bytes 405512 | tf_op jit(solution)/shard_map/ppermute | solution.py:23
  70.3 1.1 collective-permute-start.15
  71.4 3.2 %local_grads.4 = (bf16[3,512,512]{2,1,0:T(8,128)(2,1)S(1)}, bf16[3,512,512]{2,1,0:T(8,128)(2,1)S(1)}) custom-call(s32[6]{0:T(128)S(1)} %stack.27.s, bf16[3,512,512]{2,1,0:T(8,128)(2,1)S(1)} %project.5.qkv_ref, bf16[512,512]{1,0:T(8,128)(2,1)S(1)} %collective-permute-done.8.og_ref, f32[8,512]{1,0:T(8,128)S(1)} %collective-permute-done.3.refs_10_.cum_ref), custom_call_target="tpu_custom_call" | custom-call | flops 1 | bytes 1 | tf_op jit(solution)/shard_map/local_grads/pallas_call | solution.py:35
  74.7 2.0 %turn.3 = bf16[16,2,96,512]{3,2,1,0:T(8,128)(2,1)S(1)} custom-call(s32[6]{0:T(128)S(1)} %stack.27.s, bf16[256,768]{1,0:T(8,128)(2,1)S(1)} %collective-permute-done.4.refs_2_.refs_0_, bf16[256,768]{1,0:T(8,128)(2,1)S(1)} %collective-permute-done.5.refs_3_.refs_1_, bf16[256,768]{1,0:T(8,128)(2,1)S(1)} %collective-permute-done.9.refs_4_.refs_2_, ...), custom_call_target="tpu_custom_call" | custom-call | flops 1 | bytes 1 | tf_op jit(solution)/shard_map/turn/pallas_call | solution.py:35
  78.2 2.2 %collective-permute-start.18 = (bf16[512,128]{1,0:T(8,128)(2,1)S(1)}, bf16[512,128]{1,0:T(8,128)(2,1)S(1)}, u32[]{:S(2)}, u32[]{:S(2)}) collective-permute-start(bf16[512,128]{1,0:T(8,128)(2,1)S(1)} %get-tuple-element.185), channel_id=1, source_target_pairs={{0,12},{4,8},{8,4},{12,0},{1,13},{5,9},{9,5},{13,1},{2,14},{6,10},... | collective-permute-start | bytes 393224 | tf_op jit(solution)/shard_map/ppermute | solution.py:23
  80.4 1.4 collective-permute-start.19
  81.8 3.2 %local_grads.5 = (bf16[3,512,512]{2,1,0:T(8,128)(2,1)S(1)}, bf16[3,512,512]{2,1,0:T(8,128)(2,1)S(1)}) custom-call(s32[6]{0:T(128)S(1)} %stack.27.s, bf16[3,512,512]{2,1,0:T(8,128)(2,1)S(1)} %project.5.qkv_ref, bf16[512,512]{1,0:T(8,128)(2,1)S(1)} %collective-permute-done.8.og_ref, ...), custom_call_target="tpu_custom_call", output_to_operand_aliasing={{0}: (4, {}), {1}: (5, {})} | custom-call | flops 1 | bytes 1 | tf_op jit(solution)/shard_map/local_grads/pallas_call | solution.py:35
  85.7 1.4 collective-permute-done.19.c
  87.1 4.4 %whole_grads.1 = (bf16[512,768]{1,0:T(8,128)(2,1)S(1)}, bf16[512,768]{1,0:T(8,128)(2,1)S(1)}, bf16[512,768]{1,0:T(8,128)(2,1)S(1)}, bf16[512,768]{1,0:T(8,128)(2,1)S(1)}) custom-call(s32[6]{0:T(128)S(1)} %stack.27.s, bf16[3,512,512]{2,1,0:T(8,128)(2,1)S(1)} %get-tuple-element.198.local_a, bf16[3,512,512]{2,1,0:T(8,128)(2,1)S(1)} %get-tuple-element.199.ready_a, ...), custom_call_target="tpu_custom_call" | custom-call | flops 1 | bytes 1 | tf_op jit(solution)/shard_map/whole_grads/pallas_call | solution.py:35
  91.6 3.2 %weight_part.3 = (bf16[384,768]{1,0:T(8,128)(2,1)S(1)}, bf16[384,768]{1,0:T(8,128)(2,1)S(1)}, bf16[384,768]{1,0:T(8,128)(2,1)S(1)}, bf16[384,768]{1,0:T(8,128)(2,1)S(1)}) custom-call(s32[6]{0:T(128)S(1)} %stack.27.s, bf16[4,4,192,512]{3,2,1,0:T(8,128)(2,1)S(1)} %bitcast.19, bf16[4,4,192,512]{3,2,1,0:T(8,128)(2,1)S(1)} %bitcast.20, ...), custom_call_target="tpu_custom_call" | custom-call | flops 1 | bytes 1 | tf_op jit(solution)/shard_map/weight_part/pallas_call | solution.py:35
  94.7 2.6 %collective-permute-start.21 = (bf16[384,768]{1,0:T(8,128)(2,1)S(1)}, bf16[384,768]{1,0:T(8,128)(2,1)S(1)}, u32[]{:S(2)}, u32[]{:S(2)}) collective-permute-start(bf16[384,768]{1,0:T(8,128)(2,1)S(1)} %get-tuple-element.213), channel_id=1, source_target_pairs={{0,48},{16,32},{32,16},{48,0},{1,49},{17,33},{33,17},{49,1},{2,50}... | collective-permute-start | bytes 1769480 | tf_op jit(solution)/shard_map/ppermute | solution.py:23
  99.0 1.3 collective-permute-start.25
  100.3 8.4 %weight_part.4 = (bf16[768,768]{1,0:T(8,128)(2,1)S(1)}, bf16[768,768]{1,0:T(8,128)(2,1)S(1)}, bf16[768,768]{1,0:T(8,128)(2,1)S(1)}, bf16[768,768]{1,0:T(8,128)(2,1)S(1)}) custom-call(s32[6]{0:T(128)S(1)} %stack.27.s, bf16[4,4,192,512]{3,2,1,0:T(8,128)(2,1)S(1)} %bitcast.21, bf16[4,4,192,512]{3,2,1,0:T(8,128)(2,1)S(1)} %bitcast.22, ...), custom_call_target="tpu_custom_call" | custom-call | flops 1 | bytes 1 | tf_op jit(solution)/shard_map/weight_part/pallas_call | solution.py:35
  110.5 1.5 add_halves.2
  112.3 1.6 collective-permute-start.23
  114.0 1.5 add_halves.3
  115.4 1.3 collective-permute-start.27
  116.7 3.2 %weight_part.5 = (bf16[768,768]{1,0:T(8,128)(2,1)S(1)}, bf16[768,768]{1,0:T(8,128)(2,1)S(1)}) custom-call(s32[6]{0:T(128)S(1)} %stack.27.s, bf16[4,4,192,512]{3,2,1,0:T(8,128)(2,1)S(1)} %bitcast.23, bf16[4,4,192,512]{3,2,1,0:T(8,128)(2,1)S(1)} %bitcast.24, bf16[4,4,192,512]{3,2,1,0:T(8,128)(2,1)S(1)} %bitcast.29, bf16[4,4,192,512]{3,2,1,0:T(8,128)(2,1)S(1)} %bitcast.30, ...), custom_call_target="tpu_custom_call" | custom-call | flops 1 | bytes 1 | tf_op jit(solution)/shard_map/weight_part/pallas_call | solution.py:35
  119.9 18.2 %collective-permute-done.23.refs_2_ = bf16[768,768]{1,0:T(8,128)(2,1)S(1)} collective-permute-done((bf16[768,768]{1,0:T(8,128)(2,1)S(1)}, bf16[768,768]{1,0:T(8,128)(2,1)S(1)}, u32[]{:S(2)}, u32[]{:S(2)}) %collective-permute-start.23) | collective-permute-done | bytes 1179680 | tf_op jit(solution)/shard_map/ppermute | solution.py:23
  138.1 3.0 %collective-permute-done.27.refs_5_ = bf16[768,768]{1,0:T(8,128)(2,1)S(1)} collective-permute-done((bf16[768,768]{1,0:T(8,128)(2,1)S(1)}, bf16[768,768]{1,0:T(8,128)(2,1)S(1)}, u32[]{:S(2)}, u32[]{:S(2)}) %collective-permute-start.27) | collective-permute-done | bytes 1179680 | tf_op jit(solution)/shard_map/ppermute | solution.py:23
  141.2 1.4 cut_blocks.1
  142.9 2.0 %collective-permute-start.29 = (bf16[192,768]{1,0:T(8,128)(2,1)S(1)}, bf16[192,768]{1,0:T(8,128)(2,1)S(1)}, u32[]{:S(2)}, u32[]{:S(2)}) collective-permute-start(bf16[192,768]{1,0:T(8,128)(2,1)S(1)} %get-tuple-element.238), channel_id=1, source_target_pairs={{0,12},{4,8},{8,4},{12,0},{1,13},{5,9},{9,5},{13,1},{2,14},{6,10},... | collective-permute-start | bytes 884744 | tf_op jit(solution)/shard_map/ppermute | solution.py:23
  144.9 1.9 %collective-permute-start.30 = (bf16[192,768]{1,0:T(8,128)(2,1)S(1)}, bf16[192,768]{1,0:T(8,128)(2,1)S(1)}, u32[]{:S(2)}, u32[]{:S(2)}) collective-permute-start(bf16[192,768]{1,0:T(8,128)(2,1)S(1)} %get-tuple-element.239), channel_id=1, source_target_pairs={{0,8},{4,12},{8,0},{12,4},{1,9},{5,13},{9,1},{13,5},{2,10},{6,14},... | collective-permute-start | bytes 884744 | tf_op jit(solution)/shard_map/ppermute | solution.py:23
  147.7 1.7 %collective-permute-start.32 = (bf16[192,768]{1,0:T(8,128)(2,1)S(1)}, bf16[192,768]{1,0:T(8,128)(2,1)S(1)}, u32[]{:S(2)}, u32[]{:S(2)}) collective-permute-start(bf16[192,768]{1,0:T(8,128)(2,1)S(1)} %get-tuple-element.243), channel_id=1, source_target_pairs={{0,48},{16,32},{32,16},{48,0},{1,49},{17,33},{33,17},{49,1},{2,50}... | collective-permute-start | bytes 884744 | tf_op jit(solution)/shard_map/ppermute | solution.py:23
  150.6 1.9 %collective-permute-start.33 = (bf16[192,768]{1,0:T(8,128)(2,1)S(1)}, bf16[192,768]{1,0:T(8,128)(2,1)S(1)}, u32[]{:S(2)}, u32[]{:S(2)}) collective-permute-start(bf16[192,768]{1,0:T(8,128)(2,1)S(1)} %get-tuple-element.244), channel_id=1, source_target_pairs={{0,32},{16,48},{32,0},{48,16},{1,33},{17,49},{33,1},{49,17},{2,34}... | collective-permute-start | bytes 884744 | tf_op jit(solution)/shard_map/ppermute | solution.py:23
  153.1 1.9 %collective-permute-done.30.d = bf16[192,768]{1,0:T(8,128)(2,1)S(1)} collective-permute-done((bf16[192,768]{1,0:T(8,128)(2,1)S(1)}, bf16[192,768]{1,0:T(8,128)(2,1)S(1)}, u32[]{:S(2)}, u32[]{:S(2)}) %collective-permute-start.30) | collective-permute-done | bytes 294944 | tf_op jit(solution)/shard_map/ppermute | solution.py:23
  155.8 1.1 collective-permute-done.32.c
  156.9 2.0 %collective-permute-done.33.d = bf16[192,768]{1,0:T(8,128)(2,1)S(1)} collective-permute-done((bf16[192,768]{1,0:T(8,128)(2,1)S(1)}, bf16[192,768]{1,0:T(8,128)(2,1)S(1)}, u32[]{:S(2)}, u32[]{:S(2)}) %collective-permute-start.33) | collective-permute-done | bytes 294944 | tf_op jit(solution)/shard_map/ppermute | solution.py:23
  160.1 2.3 %collective-permute-done.34.refs_2_ = bf16[96,768]{1,0:T(8,128)(2,1)S(1)} collective-permute-done((bf16[96,768]{1,0:T(8,128)(2,1)S(1)}, bf16[96,768]{1,0:T(8,128)(2,1)S(1)}, u32[]{:S(2)}, u32[]{:S(2)}) %collective-permute-start.34) | collective-permute-done | bytes 147488 | tf_op jit(solution)/shard_map/ppermute | solution.py:23
  162.4 3.9 %collective-permute-done.35.refs_3_ = bf16[96,768]{1,0:T(8,128)(2,1)S(1)} collective-permute-done((bf16[96,768]{1,0:T(8,128)(2,1)S(1)}, bf16[96,768]{1,0:T(8,128)(2,1)S(1)}, u32[]{:S(2)}, u32[]{:S(2)}) %collective-permute-start.35) | collective-permute-done | bytes 147488 | tf_op jit(solution)/shard_map/ppermute | solution.py:23
  166.3 1.6 finish.1
  (61 shorter events, 17.8 us)
Async XLA Ops:
  0.0 10.0 %collective-permute-start.2 = (bf16[512,768]{1,0:T(8,128)(2,1)}, bf16[512,768]{1,0:T(8,128)(2,1)}, u32[]{:S(2)}, u32[]{:S(2)}) collective-permute-start(bf16[512,768]{1,0:T(8,128)(2,1)} %refs_0_.2), channel_id=1, source_target_pairs={{0,1},{1,0},{2,3},{3,2},{4,5},{5,4},{6,7},{7,6},{8,9},{9,8},{10,11... | collective-permute-start | bytes 2359304 | tf_op jit(solution)/shard_map/ppermute | solution.py:23
  0.0 24.1 %collective-permute-start.1 = (bf16[512,768]{1,0:T(8,128)(2,1)}, bf16[512,768]{1,0:T(8,128)(2,1)S(1)}, u32[]{:S(2)}, u32[]{:S(2)}) collective-permute-start(bf16[512,768]{1,0:T(8,128)(2,1)} %refs_0_.2), channel_id=1, source_target_pairs={{0,66},{2,64},{64,2},{66,0},{1,67},{3,65},{65,3},{67,1},{4,70},{6,... | collective-permute-start | bytes 2359304 | tf_op jit(solution)/shard_map/ppermute | solution.py:27
  4.1 20.1 %collective-permute-start = (bf16[512,768]{1,0:T(8,128)(2,1)}, bf16[512,768]{1,0:T(8,128)(2,1)S(1)}, u32[]{:S(2)}, u32[]{:S(2)}) collective-permute-start(bf16[512,768]{1,0:T(8,128)(2,1)} %refs_0_.2), channel_id=1, source_target_pairs={{0,2},{2,0},{1,3},{3,1},{4,6},{6,4},{5,7},{7,5},{8,10},{10,8},{9,1... | collective-permute-start | bytes 2359304 | tf_op jit(solution)/shard_map/ppermute | solution.py:23
  5.5 4.5 %copy-start = (bf16[512,768]{1,0:T(8,128)(2,1)S(1)}, bf16[512,768]{1,0:T(8,128)(2,1)}, u32[]{:S(2)}) copy-start(bf16[512,768]{1,0:T(8,128)(2,1)} %refs_0_.2) | copy-start | bytes 2359300
  7.0 17.1 %collective-permute-start.3 = (f32[8,512]{1,0:T(8,128)S(1)}, f32[8,512]{1,0:T(8,128)S(1)}, u32[]{:S(2)}, u32[]{:S(2)}) collective-permute-start(f32[8,512]{1,0:T(8,128)S(1)} %concatenate.6), channel_id=1, source_target_pairs={{0,64},{64,0},{1,65},{65,1},{2,66},{66,2},{3,67},{67,3},{4,68},{68... | collective-permute-start | bytes 49160 | tf_op jit(solution)/shard_map/ppermute | solution.py:23
  24.2 4.1 %collective-permute-start.7 = (bf16[512,768]{1,0:T(8,128)(2,1)S(1)}, bf16[512,768]{1,0:T(8,128)(2,1)S(1)}, u32[]{:S(2)}, u32[]{:S(2)}) collective-permute-start(bf16[512,768]{1,0:T(8,128)(2,1)S(1)} %collective-permute-done.b.refs_0_.refs_2_), channel_id=1, source_target_pairs={{0,1},{1,0},{2,3},{3,2},{4,5},{5,4},{6,7},{7,6},{8,9},{9,8},{10,11... | collective-permute-start | bytes 2359304 | tf_op jit(solution)/shard_map/ppermute | solution.py:23
  24.2 13.5 %collective-permute-start.6 = (bf16[512,768]{1,0:T(8,128)(2,1)S(1)}, bf16[512,768]{1,0:T(8,128)(2,1)S(1)}, u32[]{:S(2)}, u32[]{:S(2)}) collective-permute-start(bf16[512,768]{1,0:T(8,128)(2,1)S(1)} %collective-permute-done.1.a.refs_0_.refs_4_), channel_id=1, source_target_pairs={{0,1},{1,0},{2,3},{3,2},{4,5},{5,4},{6,7},{7,6},{8,9},{9,8},{10,11... | collective-permute-start | bytes 2359304 | tf_op jit(solution)/shard_map/ppermute | solution.py:23
  25.3 11.5 %collective-permute-start.4 = (bf16[256,768]{1,0:T(8,128)(2,1)S(1)}, bf16[256,768]{1,0:T(8,128)(2,1)S(1)}, u32[]{:S(2)}, u32[]{:S(2)}) collective-permute-start(bf16[256,768]{1,0:T(8,128)(2,1)S(1)} %get-tuple-element.131), channel_id=1, source_target_pairs={{0,2},{2,0},{1,3},{3,1},{4,6},{6,4},{5,7},{7,5},{8,10},{10,8},{9,1... | collective-permute-start | bytes 1179656 | tf_op jit(solution)/shard_map/ppermute | solution.py:23
  25.7 12.0 %collective-permute-start.5 = (bf16[256,768]{1,0:T(8,128)(2,1)S(1)}, bf16[256,768]{1,0:T(8,128)(2,1)S(1)}, u32[]{:S(2)}, u32[]{:S(2)}) collective-permute-start(bf16[256,768]{1,0:T(8,128)(2,1)S(1)} %get-tuple-element.132), channel_id=1, source_target_pairs={{0,66},{2,64},{64,2},{66,0},{1,67},{3,65},{65,3},{67,1},{4,70},{6,... | collective-permute-start | bytes 1179656 | tf_op jit(solution)/shard_map/ppermute | solution.py:27
  37.7 15.3 %collective-permute-start.8 = (bf16[512,512]{1,0:T(8,128)(2,1)S(1)}, bf16[512,512]{1,0:T(8,128)(2,1)S(1)}, u32[]{:S(2)}, u32[]{:S(2)}) collective-permute-start(bf16[512,512]{1,0:T(8,128)(2,1)S(1)} %get-tuple-element.141), channel_id=1, source_target_pairs={{0,64},{64,0},{1,65},{65,1},{2,66},{66,2},{3,67},{67,3},{4,68},{68... | collective-permute-start | bytes 1572872 | tf_op jit(solution)/shard_map/ppermute | solution.py:23
  40.5 1.7 %collective-permute-start.9 = (bf16[256,768]{1,0:T(8,128)(2,1)S(1)}, bf16[256,768]{1,0:T(8,128)(2,1)S(1)}, u32[]{:S(2)}, u32[]{:S(2)}) collective-permute-start(bf16[256,768]{1,0:T(8,128)(2,1)S(1)} %collective-permute-done.4.refs_2_.refs_0_), channel_id=1, source_target_pairs={{0,1},{1,0},{2,3},{3,2},{4,5},{5,4},{6,7},{7,6},{8,9},{9,8},{10,11... | collective-permute-start | bytes 1179656 | tf_op jit(solution)/shard_map/ppermute | solution.py:23
  40.5 2.3 %collective-permute-start.10 = (bf16[256,768]{1,0:T(8,128)(2,1)S(1)}, bf16[256,768]{1,0:T(8,128)(2,1)S(1)}, u32[]{:S(2)}, u32[]{:S(2)}) collective-permute-start(bf16[256,768]{1,0:T(8,128)(2,1)S(1)} %collective-permute-done.5.refs_3_.refs_1_), channel_id=1, source_target_pairs={{0,1},{1,0},{2,3},{3,2},{4,5},{5,4},{6,7},{7,6},{8,9},{9,8},{10,11... | collective-permute-start | bytes 1179656 | tf_op jit(solution)/shard_map/ppermute | solution.py:23
  55.4 10.4 %collective-permute-start.11 = (bf16[528,128]{1,0:T(8,128)(2,1)S(1)}, bf16[528,128]{1,0:T(8,128)(2,1)S(1)}, u32[]{:S(2)}, u32[]{:S(2)}) collective-permute-start(bf16[528,128]{1,0:T(8,128)(2,1)S(1)} %get-tuple-element.157), channel_id=1, source_target_pairs={{0,4},{4,0},{8,12},{12,8},{1,5},{5,1},{9,13},{13,9},{2,6},{6,2},{1... | collective-permute-start | bytes 405512 | tf_op jit(solution)/shard_map/ppermute | solution.py:23
  57.0 8.8 %collective-permute-start.12 = (bf16[528,128]{1,0:T(8,128)(2,1)S(1)}, bf16[528,128]{1,0:T(8,128)(2,1)S(1)}, u32[]{:S(2)}, u32[]{:S(2)}) collective-permute-start(bf16[528,128]{1,0:T(8,128)(2,1)S(1)} %get-tuple-element.158), channel_id=1, source_target_pairs={{0,12},{4,8},{8,4},{12,0},{1,13},{5,9},{9,5},{13,1},{2,14},{6,10},... | collective-permute-start | bytes 405512 | tf_op jit(solution)/shard_map/ppermute | solution.py:23
  59.2 7.3 %collective-permute-start.13 = (bf16[528,128]{1,0:T(8,128)(2,1)S(1)}, bf16[528,128]{1,0:T(8,128)(2,1)S(1)}, u32[]{:S(2)}, u32[]{:S(2)}) collective-permute-start(bf16[528,128]{1,0:T(8,128)(2,1)S(1)} %get-tuple-element.159), channel_id=1, source_target_pairs={{0,8},{4,12},{8,0},{12,4},{1,9},{5,13},{9,1},{13,5},{2,10},{6,14},... | collective-permute-start | bytes 405512 | tf_op jit(solution)/shard_map/ppermute | solution.py:23
  67.2 9.5 %collective-permute-start.16 = (bf16[528,128]{1,0:T(8,128)(2,1)S(1)}, bf16[528,128]{1,0:T(8,128)(2,1)S(1)}, u32[]{:S(2)}, u32[]{:S(2)}) collective-permute-start(bf16[528,128]{1,0:T(8,128)(2,1)S(1)} %get-tuple-element.166.a), channel_id=1, source_target_pairs={{0,32},{16,48},{32,0},{48,16},{1,33},{17,49},{33,1},{49,17},{2,34}... | collective-permute-start | bytes 405512 | tf_op jit(solution)/shard_map/ppermute | solution.py:23
  70.3 6.4 %collective-permute-start.15 = (bf16[528,128]{1,0:T(8,128)(2,1)S(1)}, bf16[528,128]{1,0:T(8,128)(2,1)S(1)}, u32[]{:S(2)}, u32[]{:S(2)}) collective-permute-start(bf16[528,128]{1,0:T(8,128)(2,1)S(1)} %get-tuple-element.166.a), channel_id=1, source_target_pairs={{0,48},{16,32},{32,16},{48,0},{1,49},{17,33},{33,17},{49,1},{2,50}... | collective-permute-start | bytes 405512 | tf_op jit(solution)/shard_map/ppermute | solution.py:23
  71.4 5.3 %collective-permute-start.14 = (bf16[528,128]{1,0:T(8,128)(2,1)S(1)}, bf16[528,128]{1,0:T(8,128)(2,1)S(1)}, u32[]{:S(2)}, u32[]{:S(2)}) collective-permute-start(bf16[528,128]{1,0:T(8,128)(2,1)S(1)} %get-tuple-element.166.a), channel_id=1, source_target_pairs={{0,16},{16,0},{32,48},{48,32},{1,17},{17,1},{33,49},{49,33},{2,18}... | collective-permute-start | bytes 405512 | tf_op jit(solution)/shard_map/ppermute | solution.py:23
  77.6 7.4 %collective-permute-start.17 = (bf16[512,128]{1,0:T(8,128)(2,1)S(1)}, bf16[512,128]{1,0:T(8,128)(2,1)S(1)}, u32[]{:S(2)}, u32[]{:S(2)}) collective-permute-start(bf16[512,128]{1,0:T(8,128)(2,1)S(1)} %get-tuple-element.184), channel_id=1, source_target_pairs={{0,4},{4,0},{8,12},{12,8},{1,5},{5,1},{9,13},{13,9},{2,6},{6,2},{1... | collective-permute-start | bytes 393224 | tf_op jit(solution)/shard_map/ppermute | solution.py:23
  78.2 7.5 %collective-permute-start.18 = (bf16[512,128]{1,0:T(8,128)(2,1)S(1)}, bf16[512,128]{1,0:T(8,128)(2,1)S(1)}, u32[]{:S(2)}, u32[]{:S(2)}) collective-permute-start(bf16[512,128]{1,0:T(8,128)(2,1)S(1)} %get-tuple-element.185), channel_id=1, source_target_pairs={{0,12},{4,8},{8,4},{12,0},{1,13},{5,9},{9,5},{13,1},{2,14},{6,10},... | collective-permute-start | bytes 393224 | tf_op jit(solution)/shard_map/ppermute | solution.py:23
  80.4 6.7 %collective-permute-start.19 = (bf16[512,128]{1,0:T(8,128)(2,1)S(1)}, bf16[512,128]{1,0:T(8,128)(2,1)S(1)}, u32[]{:S(2)}, u32[]{:S(2)}) collective-permute-start(bf16[512,128]{1,0:T(8,128)(2,1)S(1)} %get-tuple-element.186), channel_id=1, source_target_pairs={{0,8},{4,12},{8,0},{12,4},{1,9},{5,13},{9,1},{13,5},{2,10},{6,14},... | collective-permute-start | bytes 393224 | tf_op jit(solution)/shard_map/ppermute | solution.py:23
  94.7 14.8 %collective-permute-start.21 = (bf16[384,768]{1,0:T(8,128)(2,1)S(1)}, bf16[384,768]{1,0:T(8,128)(2,1)S(1)}, u32[]{:S(2)}, u32[]{:S(2)}) collective-permute-start(bf16[384,768]{1,0:T(8,128)(2,1)S(1)} %get-tuple-element.213), channel_id=1, source_target_pairs={{0,48},{16,32},{32,16},{48,0},{1,49},{17,33},{33,17},{49,1},{2,50}... | collective-permute-start | bytes 1769480 | tf_op jit(solution)/shard_map/ppermute | solution.py:23
  97.4 13.1 %collective-permute-start.20 = (bf16[384,768]{1,0:T(8,128)(2,1)S(1)}, bf16[384,768]{1,0:T(8,128)(2,1)S(1)}, u32[]{:S(2)}, u32[]{:S(2)}) collective-permute-start(bf16[384,768]{1,0:T(8,128)(2,1)S(1)} %get-tuple-element.209), channel_id=1, source_target_pairs={{0,16},{16,0},{32,48},{48,32},{1,17},{17,1},{33,49},{49,33},{2,18}... | collective-permute-start | bytes 1769480 | tf_op jit(solution)/shard_map/ppermute | solution.py:23
  98.1 14.2 %collective-permute-start.24 = (bf16[384,768]{1,0:T(8,128)(2,1)S(1)}, bf16[384,768]{1,0:T(8,128)(2,1)S(1)}, u32[]{:S(2)}, u32[]{:S(2)}) collective-permute-start(bf16[384,768]{1,0:T(8,128)(2,1)S(1)} %get-tuple-element.222), channel_id=1, source_target_pairs={{0,4},{4,0},{8,12},{12,8},{1,5},{5,1},{9,13},{13,9},{2,6},{6,2},{1... | collective-permute-start | bytes 1769480 | tf_op jit(solution)/shard_map/ppermute | solution.py:23
  99.0 13.4 %collective-permute-start.25 = (bf16[384,768]{1,0:T(8,128)(2,1)S(1)}, bf16[384,768]{1,0:T(8,128)(2,1)S(1)}, u32[]{:S(2)}, u32[]{:S(2)}) collective-permute-start(bf16[384,768]{1,0:T(8,128)(2,1)S(1)} %get-tuple-element.223), channel_id=1, source_target_pairs={{0,12},{4,8},{8,4},{12,0},{1,13},{5,9},{9,5},{13,1},{2,14},{6,10},... | collective-permute-start | bytes 1769480 | tf_op jit(solution)/shard_map/ppermute | solution.py:23
  111.9 26.2 %collective-permute-start.22 = (bf16[768,768]{1,0:T(8,128)(2,1)S(1)}, bf16[768,768]{1,0:T(8,128)(2,1)S(1)}, u32[]{:S(2)}, u32[]{:S(2)}) collective-permute-start(bf16[768,768]{1,0:T(8,128)(2,1)S(1)} %get-tuple-element.218), channel_id=1, source_target_pairs={{0,16},{16,0},{32,48},{48,32},{1,17},{17,1},{33,49},{49,33},{2,18}... | collective-permute-start | bytes 3538952 | tf_op jit(solution)/shard_map/ppermute | solution.py:23
  112.3 25.8 %collective-permute-start.23 = (bf16[768,768]{1,0:T(8,128)(2,1)S(1)}, bf16[768,768]{1,0:T(8,128)(2,1)S(1)}, u32[]{:S(2)}, u32[]{:S(2)}) collective-permute-start(bf16[768,768]{1,0:T(8,128)(2,1)S(1)} %get-tuple-element.219), channel_id=1, source_target_pairs={{0,48},{16,32},{32,16},{48,0},{1,49},{17,33},{33,17},{49,1},{2,50}... | collective-permute-start | bytes 3538952 | tf_op jit(solution)/shard_map/ppermute | solution.py:23
  115.4 25.7 %collective-permute-start.27 = (bf16[768,768]{1,0:T(8,128)(2,1)S(1)}, bf16[768,768]{1,0:T(8,128)(2,1)S(1)}, u32[]{:S(2)}, u32[]{:S(2)}) collective-permute-start(bf16[768,768]{1,0:T(8,128)(2,1)S(1)} %get-tuple-element.235), channel_id=1, source_target_pairs={{0,12},{4,8},{8,4},{12,0},{1,13},{5,9},{9,5},{13,1},{2,14},{6,10},... | collective-permute-start | bytes 3538952 | tf_op jit(solution)/shard_map/ppermute | solution.py:23
  116.7 24.5 %collective-permute-start.26 = (bf16[768,768]{1,0:T(8,128)(2,1)S(1)}, bf16[768,768]{1,0:T(8,128)(2,1)S(1)}, u32[]{:S(2)}, u32[]{:S(2)}) collective-permute-start(bf16[768,768]{1,0:T(8,128)(2,1)S(1)} %get-tuple-element.226), channel_id=1, source_target_pairs={{0,4},{4,0},{8,12},{12,8},{1,5},{5,1},{9,13},{13,9},{2,6},{6,2},{1... | collective-permute-start | bytes 3538952 | tf_op jit(solution)/shard_map/ppermute | solution.py:23
  142.6 8.0 %collective-permute-start.28 = (bf16[192,768]{1,0:T(8,128)(2,1)S(1)}, bf16[192,768]{1,0:T(8,128)(2,1)S(1)}, u32[]{:S(2)}, u32[]{:S(2)}) collective-permute-start(bf16[192,768]{1,0:T(8,128)(2,1)S(1)} %get-tuple-element.237), channel_id=1, source_target_pairs={{0,4},{4,0},{8,12},{12,8},{1,5},{5,1},{9,13},{13,9},{2,6},{6,2},{1... | collective-permute-start | bytes 884744 | tf_op jit(solution)/shard_map/ppermute | solution.py:23
  142.9 10.2 %collective-permute-start.29 = (bf16[192,768]{1,0:T(8,128)(2,1)S(1)}, bf16[192,768]{1,0:T(8,128)(2,1)S(1)}, u32[]{:S(2)}, u32[]{:S(2)}) collective-permute-start(bf16[192,768]{1,0:T(8,128)(2,1)S(1)} %get-tuple-element.238), channel_id=1, source_target_pairs={{0,12},{4,8},{8,4},{12,0},{1,13},{5,9},{9,5},{13,1},{2,14},{6,10},... | collective-permute-start | bytes 884744 | tf_op jit(solution)/shard_map/ppermute | solution.py:23
  144.9 10.1 %collective-permute-start.30 = (bf16[192,768]{1,0:T(8,128)(2,1)S(1)}, bf16[192,768]{1,0:T(8,128)(2,1)S(1)}, u32[]{:S(2)}, u32[]{:S(2)}) collective-permute-start(bf16[192,768]{1,0:T(8,128)(2,1)S(1)} %get-tuple-element.239), channel_id=1, source_target_pairs={{0,8},{4,12},{8,0},{12,4},{1,9},{5,13},{9,1},{13,5},{2,10},{6,14},... | collective-permute-start | bytes 884744 | tf_op jit(solution)/shard_map/ppermute | solution.py:23
  146.8 9.0 %collective-permute-start.31 = (bf16[192,768]{1,0:T(8,128)(2,1)S(1)}, bf16[192,768]{1,0:T(8,128)(2,1)S(1)}, u32[]{:S(2)}, u32[]{:S(2)}) collective-permute-start(bf16[192,768]{1,0:T(8,128)(2,1)S(1)} %get-tuple-element.242), channel_id=1, source_target_pairs={{0,16},{16,0},{32,48},{48,32},{1,17},{17,1},{33,49},{49,33},{2,18}... | collective-permute-start | bytes 884744 | tf_op jit(solution)/shard_map/ppermute | solution.py:23
  147.7 9.1 %collective-permute-start.32 = (bf16[192,768]{1,0:T(8,128)(2,1)S(1)}, bf16[192,768]{1,0:T(8,128)(2,1)S(1)}, u32[]{:S(2)}, u32[]{:S(2)}) collective-permute-start(bf16[192,768]{1,0:T(8,128)(2,1)S(1)} %get-tuple-element.243), channel_id=1, source_target_pairs={{0,48},{16,32},{32,16},{48,0},{1,49},{17,33},{33,17},{49,1},{2,50}... | collective-permute-start | bytes 884744 | tf_op jit(solution)/shard_map/ppermute | solution.py:23
  150.6 8.3 %collective-permute-start.33 = (bf16[192,768]{1,0:T(8,128)(2,1)S(1)}, bf16[192,768]{1,0:T(8,128)(2,1)S(1)}, u32[]{:S(2)}, u32[]{:S(2)}) collective-permute-start(bf16[192,768]{1,0:T(8,128)(2,1)S(1)} %get-tuple-element.244), channel_id=1, source_target_pairs={{0,32},{16,48},{32,0},{48,16},{1,33},{17,49},{33,1},{49,17},{2,34}... | collective-permute-start | bytes 884744 | tf_op jit(solution)/shard_map/ppermute | solution.py:23
  155.7 6.7 %collective-permute-start.34 = (bf16[96,768]{1,0:T(8,128)(2,1)S(1)}, bf16[96,768]{1,0:T(8,128)(2,1)S(1)}, u32[]{:S(2)}, u32[]{:S(2)}) collective-permute-start(bf16[96,768]{1,0:T(8,128)(2,1)S(1)} %get-tuple-element.249), channel_id=1, source_target_pairs={{0,64},{64,0},{1,65},{65,1},{2,66},{66,2},{3,67},{67,3},{4,68},{68... | collective-permute-start | bytes 442376 | tf_op jit(solution)/shard_map/ppermute | solution.py:23
  159.5 6.7 %collective-permute-start.35 = (bf16[96,768]{1,0:T(8,128)(2,1)S(1)}, bf16[96,768]{1,0:T(8,128)(2,1)S(1)}, u32[]{:S(2)}, u32[]{:S(2)}) collective-permute-start(bf16[96,768]{1,0:T(8,128)(2,1)S(1)} %get-tuple-element.250), channel_id=1, source_target_pairs={{0,64},{64,0},{1,65},{65,1},{2,66},{66,2},{3,67},{67,3},{4,68},{68... | collective-permute-start | bytes 442376 | tf_op jit(solution)/shard_map/ppermute | solution.py:23

commit v9 on v8

--- a/solution.py
+++ b/solution.py
@@ -487,31 +487,27 @@
     )
 
 
-def cut_blocks(table, left, right):
-    rows, cols = left[0].shape[0] // 4, left[0].shape[1]
-
-    def body(s, *refs):
-        for k, axis in enumerate((Y, X)):
-            a, b, c = refs[3 * k : 3 * k + 3]
-            for r, out in zip((1, 3, 2, 0), refs[6 + 4 * k : 10 + 4 * k]):
-                at = pl.ds(pl.multiple_of((s[axis] ^ r) * rows, rows), rows)
-                total = a[at, :].astype(F32) + b[at, :].astype(F32) + c[at, :].astype(F32)
-                out[...] = total.astype(BF16)
-
-    outs = [shape((rows, cols))] * 8
-    operands = (*left, *right)
-    cut = call(
+def cut_blocks(table, axis, parts):
+    rows, cols = parts[0].shape[0] // 4, parts[0].shape[1]
+
+    def body(s, a, b, c, *outs):
+        for r, out in zip((1, 3, 2, 0), outs):
+            at = pl.ds(pl.multiple_of((s[axis] ^ r) * rows, rows), rows)
+            total = a[at, :].astype(F32) + b[at, :].astype(F32) + c[at, :].astype(F32)
+            out[...] = total.astype(BF16)
+
+    outs = [shape((rows, cols))] * 4
+    return call(
         "cut_blocks",
         body,
         table,
         (1,),
-        operands,
-        [whole(x) for x in operands],
+        parts,
+        [whole(x) for x in parts],
         outs,
         [whole(o) for o in outs],
-        24,
-    )
-    return cut[:4], cut[4:]
+        16,
+    )
 
 
 def final_sums(table, parts):
@@ -597,12 +593,12 @@
     far, side_core, qkv_own, turned = tied((far, side_core, qkv_own, turned))
     far_core = [send(x, "co", 1) for x in far]
     og_pair = send(tied((og_other, far))[0], "c0", 1)
+    to_y = shard_states(table, qkv_own, og_own, info, 0, None)
+    far_core, to_y = tied((far_core, to_y))
     qkv_pair = project(
         table, [[side], [side_core], far, far_core], (2, 3, 0, 1), weight, None, note
     )
-    qkv_own, _ = tied((qkv_own, qkv_pair))
-    to_y = shard_states(table, qkv_own, og_own, info, 0, None)
-    og_pair, qkv_pair, to_y = tied((og_pair, qkv_pair, to_y))
+    og_pair, qkv_pair = tied((og_pair, qkv_pair))
 
     to_y = shard_states(table, qkv_pair, og_pair, note, 1, to_y)
     at_y = [send(to_y[r], "c2", r) for r in (1, 3, 2)]
@@ -638,13 +634,18 @@
     turned, _ = tied((turned, r_one))
     own = weight_part(table, turned, lefts, rights, (0,), False)
     l_got, own = tied((l_got, own))
-    l_cut, r_cut = cut_blocks(table, (own[0], *l_got), (own[1], *r_got))
+    l_cut = cut_blocks(table, Y, (own[0], *l_got))
+    r_got, _ = tied((r_got, l_cut[3]))
+    r_cut = cut_blocks(table, X, (own[1], *r_got))
     l_got = [send(x, "c2", by) for x, by in zip(l_cut, (1, 3, 2))]
     r_got = [send(x, "c1", by) for x, by in zip(r_cut, (1, 3, 2))]
+    l_got, _ = tied((l_got, r_cut[3]))
     l_here, l_there = final_sums(table, (l_cut[3], *l_got))
     r_got, _ = tied((r_got, l_here))
     r_here, r_there = final_sums(table, (r_cut[3], *r_got))
-    there = [send(x, "c0", 1) for x in (l_there, r_there)]
+    l_there = send(l_there, "c0", 1)
+    l_there, r_there = tied((l_there, r_there))
+    there = [l_there, send(r_there, "c0", 1)]
     return jnp.transpose(finish(table, (l_here, r_here), there), (1, 0, 2))
 
 

time: 168 us -> 168 us (level)
  waiting for transfers between devices: 50.1 us -> 48.1 us
    ppermute x34, waiting for transfers between devices: 49.2 us -> 47.2 us  [send(): lax.ppermute(x, axis, [(i, i ^ by) for i in range(lax.axis_size(axis))])]
    pallas_call x23 -> x24, Pallas kernels: 69.5 us -> 70.1 us  [call(): pl.pallas_call(body, grid_spec=pltpu.PrefetchScalarGridSpec(num_scalar_pr...]
  transfers between devices with their start and end apart: 36 -> 36, of which waited for: 20 -> 16; matrix products, arithmetic and copies ran while one was open for 2% -> 2% of each run, Pallas kernels for 33% -> 34%
where the time goes in v9:
time: 168 us
  Pallas kernels  70.1 us (42%)
  waiting for transfers between devices  48.1 us (29%)
  starting transfers between devices  45.4 us (27%)
  other arithmetic  1.96 us (1%)
    pallas_call x24, Pallas kernels, call(): pl.pallas_call(body, grid_spec=pltpu.PrefetchScalarGridSpec(num_scalar_pr...  70.1 us
    ppermute x34, waiting for transfers between devices, send(): lax.ppermute(x, axis, [(i, i ^ by) for i in range(lax.axis_size(axis))])  47.2 us
    ppermute x34, starting transfers between devices, send(): lax.ppermute(x, axis, [(i, i ^ by) for i in range(lax.axis_size(axis))])  38.6 us
    ppermute x2, starting transfers between devices, across(): return lax.ppermute(x, ('c0', 'zl'), [(0, 3), (1, 2), (2, 1), (3, 0)])  6.75 us
  transfers between devices with their start and end apart: 36, of which 16 were waited for; matrix products, arithmetic and copies ran while one was open for 2% of the time, Pallas kernels for 34%

profile of v9, /device:TPU:0, one launch (start us, length us, event | category | flops | bytes accessed | tf_op | source)
XLA Modules:
  0.0 168.0 jit_solution(10042555423522831578)
XLA Ops:
  0.0 4.1 %collective-permute-start.1 = (bf16[512,768]{1,0:T(8,128)(2,1)}, bf16[512,768]{1,0:T(8,128)(2,1)S(1)}, u32[]{:S(2)}, u32[]{:S(2)}) collective-permute-start(bf16[512,768]{1,0:T(8,128)(2,1)} %refs_0_.2), channel_id=1, source_target_pairs={{0,66},{2,64},{64,2},{66,0},{1,67},{3,65},{65,3},{67,1},{4,70},{6,... | collective-permute-start | bytes 2359304 | tf_op jit(solution)/shard_map/ppermute | solution.py:27
  5.5 1.1 reduce-window.6
  7.0 1.6 collective-permute-start.3
  8.6 1.3 constant_dynamic-slice_fusion
  10.0 5.5 %project.3.refs_4_ = f32[3,512,512]{2,1,0:T(8,128)S(1)} custom-call(s32[6]{0:T(128)S(1)} %stack.27.s, bf16[512,768]{1,0:T(8,128)(2,1)S(1)} %copy-done, bf16[512,768]{1,0:T(8,128)(2,1)} %collective-permute-done.2.refs_1_, bf16[3,3072,1024]{2,1,0:T(8,128)(2,1)} %bitcast.31, bf16[3,3072,1024]{2,1,0:T(8,128)(2,1)} %bitcast.32), custom_call_target="tpu_custom_call" | custom-call | flops 1 | bytes 1 | tf_op jit(solution)/shard_map/project/pallas_call | solution.py:35
  15.5 8.6 %collective-permute-done.3.refs_10_.cum_ref = f32[8,512]{1,0:T(8,128)S(1)} collective-permute-done((f32[8,512]{1,0:T(8,128)S(1)}, f32[8,512]{1,0:T(8,128)S(1)}, u32[]{:S(2)}, u32[]{:S(2)}) %collective-permute-start.3) | collective-permute-done | bytes 16416 | tf_op jit(solution)/shard_map/ppermute | solution.py:23
  25.7 2.6 %collective-permute-start.5 = (bf16[256,768]{1,0:T(8,128)(2,1)S(1)}, bf16[256,768]{1,0:T(8,128)(2,1)S(1)}, u32[]{:S(2)}, u32[]{:S(2)}) collective-permute-start(bf16[256,768]{1,0:T(8,128)(2,1)S(1)} %get-tuple-element.140), channel_id=1, source_target_pairs={{0,66},{2,64},{64,2},{66,0},{1,67},{3,65},{65,3},{67,1},{4,70},{6,... | collective-permute-start | bytes 1179656 | tf_op jit(solution)/shard_map/ppermute | solution.py:27
  28.3 5.3 %project.4.qkv_ref = bf16[3,512,512]{2,1,0:T(8,128)(2,1)S(1)} custom-call(s32[6]{0:T(128)S(1)} %stack.27.s, bf16[512,768]{1,0:T(8,128)(2,1)S(1)} %collective-permute-done.b.refs_0_.refs_2_, bf16[512,768]{1,0:T(8,128)(2,1)S(1)} %collective-permute-done.7.refs_1_.refs_3_, bf16[3,3072,1024]{2,1,0:T(8,128)(2,1)} %bitcast.33, bf16[3,3072,1024]{2,1,0:T(8,128)(2,1)} %bitcast.34, ...), custom_call_target="tpu_custom_call" | custom-call | flops 1 | bytes 1 | tf_op jit(solution)/shard_map/project/pallas_call | solution.py:35
  33.6 3.2 %turn.2 = bf16[16,2,96,512]{3,2,1,0:T(8,128)(2,1)S(1)} custom-call(s32[6]{0:T(128)S(1)} %stack.27.s, bf16[512,768]{1,0:T(8,128)(2,1)S(1)} %copy-done, bf16[512,768]{1,0:T(8,128)(2,1)} %collective-permute-done.2.refs_1_, bf16[512,768]{1,0:T(8,128)(2,1)S(1)} %collective-permute-done.b.refs_0_.refs_2_, bf16[512,768]{1,0:T(8,128)(2,1)S(1)} %collective-permute-done.7.refs_1_.refs_3_), custom_call_target="tpu_custom_call" | custom-call | flops 1 | bytes 1 | tf_op jit(solution)/shard_map/turn/pallas_call | solution.py:35
  37.7 2.8 %collective-permute-start.8 = (bf16[512,512]{1,0:T(8,128)(2,1)S(1)}, bf16[512,512]{1,0:T(8,128)(2,1)S(1)}, u32[]{:S(2)}, u32[]{:S(2)}) collective-permute-start(bf16[512,512]{1,0:T(8,128)(2,1)S(1)} %get-tuple-element.149), channel_id=1, source_target_pairs={{0,64},{64,0},{1,65},{65,1},{2,66},{66,2},{3,67},{67,3},{4,68},{68... | collective-permute-start | bytes 1572872 | tf_op jit(solution)/shard_map/ppermute | solution.py:23
  41.0 2.3 %shard_states.2 = (bf16[528,128]{1,0:T(8,128)(2,1)S(1)}, bf16[528,128]{1,0:T(8,128)(2,1)S(1)}, bf16[528,128]{1,0:T(8,128)(2,1)S(1)}, bf16[528,128]{1,0:T(8,128)(2,1)S(1)}) custom-call(s32[6]{0:T(128)S(1)} %stack.27.s, bf16[3,512,512]{2,1,0:T(8,128)(2,1)S(1)} %project.4.qkv_ref, bf16[512,512]{1,0:T(8,128)(2,1)S(1)} %get-tuple-element.267.og_ref, ...), custom_call_target="tpu_custom_call" | custom-call | flops 1 | bytes 1 | tf_op jit(solution)/shard_map/shard_states/pallas_call | solution.py:35
  43.4 7.9 %project.5.qkv_ref = bf16[3,512,512]{2,1,0:T(8,128)(2,1)S(1)} custom-call(s32[6]{0:T(128)S(1)} %stack.27.s, bf16[512,768]{1,0:T(8,128)(2,1)S(1)} %collective-permute-done.1.a.refs_0_.refs_4_, bf16[512,768]{1,0:T(8,128)(2,1)S(1)} %collective-permute-done.6.refs_1_.refs_5_, bf16[256,768]{1,0:T(8,128)(2,1)S(1)} %collective-permute-done.4.refs_2_.refs_0_, ...), custom_call_target="tpu_custom_call" | custom-call | flops 1 | bytes 1 | tf_op jit(solution)/shard_map/project/pallas_call | solution.py:35
  52.1 2.3 %shard_states.3 = (bf16[528,128]{1,0:T(8,128)(2,1)S(1)}, bf16[528,128]{1,0:T(8,128)(2,1)S(1)}, bf16[528,128]{1,0:T(8,128)(2,1)S(1)}, bf16[528,128]{1,0:T(8,128)(2,1)S(1)}) custom-call(s32[6]{0:T(128)S(1)} %stack.27.s, bf16[3,512,512]{2,1,0:T(8,128)(2,1)S(1)} %project.5.qkv_ref, bf16[512,512]{1,0:T(8,128)(2,1)S(1)} %collective-permute-done.8.og_ref, ...), custom_call_target="tpu_custom_call" | custom-call | flops 1 | bytes 1 | tf_op jit(solution)/shard_map/shard_states/pallas_call | solution.py:35
  54.4 1.7 collective-permute-start.11
  56.0 2.2 %collective-permute-start.12 = (bf16[528,128]{1,0:T(8,128)(2,1)S(1)}, bf16[528,128]{1,0:T(8,128)(2,1)S(1)}, u32[]{:S(2)}, u32[]{:S(2)}) collective-permute-start(bf16[528,128]{1,0:T(8,128)(2,1)S(1)} %get-tuple-element.167), channel_id=1, source_target_pairs={{0,12},{4,8},{8,4},{12,0},{1,13},{5,9},{9,5},{13,1},{2,14},{6,10},... | collective-permute-start | bytes 405512 | tf_op jit(solution)/shard_map/ppermute | solution.py:23
  59.0 5.9 %local_grads.3 = (bf16[3,512,512]{2,1,0:T(8,128)(2,1)S(1)}, bf16[3,512,512]{2,1,0:T(8,128)(2,1)S(1)}) custom-call(s32[6]{0:T(128)S(1)} %stack.27.s, bf16[3,512,512]{2,1,0:T(8,128)(2,1)S(1)} %project.4.qkv_ref, bf16[512,512]{1,0:T(8,128)(2,1)S(1)} %get-tuple-element.267.og_ref, f32[8,512]{1,0:T(8,128)S(1)} %concatenate.7.refs_5_.cum_ref), custom_call_target="tpu_custom_call" | custom-call | flops 1 | bytes 1 | tf_op jit(solution)/shard_map/local_grads/pallas_call | solution.py:35
  65.9 3.1 %collective-permute-start.16 = (bf16[528,128]{1,0:T(8,128)(2,1)S(1)}, bf16[528,128]{1,0:T(8,128)(2,1)S(1)}, u32[]{:S(2)}, u32[]{:S(2)}) collective-permute-start(bf16[528,128]{1,0:T(8,128)(2,1)S(1)} %get-tuple-element.175.a), channel_id=1, source_target_pairs={{0,32},{16,48},{32,0},{48,16},{1,33},{17,49},{33,1},{49,17},{2,34}... | collective-permute-start | bytes 405512 | tf_op jit(solution)/shard_map/ppermute | solution.py:23
  69.0 1.1 collective-permute-start.15
  70.1 3.2 %local_grads.4 = (bf16[3,512,512]{2,1,0:T(8,128)(2,1)S(1)}, bf16[3,512,512]{2,1,0:T(8,128)(2,1)S(1)}) custom-call(s32[6]{0:T(128)S(1)} %stack.27.s, bf16[3,512,512]{2,1,0:T(8,128)(2,1)S(1)} %project.5.qkv_ref, bf16[512,512]{1,0:T(8,128)(2,1)S(1)} %collective-permute-done.8.og_ref, f32[8,512]{1,0:T(8,128)S(1)} %collective-permute-done.3.refs_10_.cum_ref), custom_call_target="tpu_custom_call" | custom-call | flops 1 | bytes 1 | tf_op jit(solution)/shard_map/local_grads/pallas_call | solution.py:35
  73.4 2.0 %turn.3 = bf16[16,2,96,512]{3,2,1,0:T(8,128)(2,1)S(1)} custom-call(s32[6]{0:T(128)S(1)} %stack.27.s, bf16[256,768]{1,0:T(8,128)(2,1)S(1)} %collective-permute-done.4.refs_2_.refs_0_, bf16[256,768]{1,0:T(8,128)(2,1)S(1)} %collective-permute-done.5.refs_3_.refs_1_, bf16[256,768]{1,0:T(8,128)(2,1)S(1)} %collective-permute-done.9.refs_4_.refs_2_, ...), custom_call_target="tpu_custom_call" | custom-call | flops 1 | bytes 1 | tf_op jit(solution)/shard_map/turn/pallas_call | solution.py:35
  77.3 2.2 %collective-permute-start.18 = (bf16[512,128]{1,0:T(8,128)(2,1)S(1)}, bf16[512,128]{1,0:T(8,128)(2,1)S(1)}, u32[]{:S(2)}, u32[]{:S(2)}) collective-permute-start(bf16[512,128]{1,0:T(8,128)(2,1)S(1)} %get-tuple-element.194), channel_id=1, source_target_pairs={{0,12},{4,8},{8,4},{12,0},{1,13},{5,9},{9,5},{13,1},{2,14},{6,10},... | collective-permute-start | bytes 393224 | tf_op jit(solution)/shard_map/ppermute | solution.py:23
  79.4 1.0 collective-permute-start.19
  80.5 3.2 %local_grads.5 = (bf16[3,512,512]{2,1,0:T(8,128)(2,1)S(1)}, bf16[3,512,512]{2,1,0:T(8,128)(2,1)S(1)}) custom-call(s32[6]{0:T(128)S(1)} %stack.27.s, bf16[3,512,512]{2,1,0:T(8,128)(2,1)S(1)} %project.5.qkv_ref, bf16[512,512]{1,0:T(8,128)(2,1)S(1)} %collective-permute-done.8.og_ref, ...), custom_call_target="tpu_custom_call", output_to_operand_aliasing={{0}: (4, {}), {1}: (5, {})} | custom-call | flops 1 | bytes 1 | tf_op jit(solution)/shard_map/local_grads/pallas_call | solution.py:35
  84.2 1.8 %collective-permute-done.19.c = bf16[512,128]{1,0:T(8,128)(2,1)S(1)} collective-permute-done((bf16[512,128]{1,0:T(8,128)(2,1)S(1)}, bf16[512,128]{1,0:T(8,128)(2,1)S(1)}, u32[]{:S(2)}, u32[]{:S(2)}) %collective-permute-start.19) | collective-permute-done | bytes 131104 | tf_op jit(solution)/shard_map/ppermute | solution.py:23
  85.9 4.4 %whole_grads.1 = (bf16[512,768]{1,0:T(8,128)(2,1)S(1)}, bf16[512,768]{1,0:T(8,128)(2,1)S(1)}, bf16[512,768]{1,0:T(8,128)(2,1)S(1)}, bf16[512,768]{1,0:T(8,128)(2,1)S(1)}) custom-call(s32[6]{0:T(128)S(1)} %stack.27.s, bf16[3,512,512]{2,1,0:T(8,128)(2,1)S(1)} %get-tuple-element.207.local_a, bf16[3,512,512]{2,1,0:T(8,128)(2,1)S(1)} %get-tuple-element.208.ready_a, ...), custom_call_target="tpu_custom_call" | custom-call | flops 1 | bytes 1 | tf_op jit(solution)/shard_map/whole_grads/pallas_call | solution.py:35
  90.4 3.2 %weight_part.3 = (bf16[384,768]{1,0:T(8,128)(2,1)S(1)}, bf16[384,768]{1,0:T(8,128)(2,1)S(1)}, bf16[384,768]{1,0:T(8,128)(2,1)S(1)}, bf16[384,768]{1,0:T(8,128)(2,1)S(1)}) custom-call(s32[6]{0:T(128)S(1)} %stack.27.s, bf16[4,4,192,512]{3,2,1,0:T(8,128)(2,1)S(1)} %bitcast.19, bf16[4,4,192,512]{3,2,1,0:T(8,128)(2,1)S(1)} %bitcast.20, ...), custom_call_target="tpu_custom_call" | custom-call | flops 1 | bytes 1 | tf_op jit(solution)/shard_map/weight_part/pallas_call | solution.py:35
  93.5 2.2 %collective-permute-start.21 = (bf16[384,768]{1,0:T(8,128)(2,1)S(1)}, bf16[384,768]{1,0:T(8,128)(2,1)S(1)}, u32[]{:S(2)}, u32[]{:S(2)}) collective-permute-start(bf16[384,768]{1,0:T(8,128)(2,1)S(1)} %get-tuple-element.222), channel_id=1, source_target_pairs={{0,48},{16,32},{32,16},{48,0},{1,49},{17,33},{33,17},{49,1},{2,50}... | collective-permute-start | bytes 1769480 | tf_op jit(solution)/shard_map/ppermute | solution.py:23
  95.7 1.4 collective-permute-start.20
  98.7 8.4 %weight_part.4 = (bf16[768,768]{1,0:T(8,128)(2,1)S(1)}, bf16[768,768]{1,0:T(8,128)(2,1)S(1)}, bf16[768,768]{1,0:T(8,128)(2,1)S(1)}, bf16[768,768]{1,0:T(8,128)(2,1)S(1)}) custom-call(s32[6]{0:T(128)S(1)} %stack.27.s, bf16[4,4,192,512]{3,2,1,0:T(8,128)(2,1)S(1)} %bitcast.21, bf16[4,4,192,512]{3,2,1,0:T(8,128)(2,1)S(1)} %bitcast.22, ...), custom_call_target="tpu_custom_call" | custom-call | flops 1 | bytes 1 | tf_op jit(solution)/shard_map/weight_part/pallas_call | solution.py:35
  107.4 1.5 add_halves.2
  108.9 1.8 %collective-permute-start.23 = (bf16[768,768]{1,0:T(8,128)(2,1)S(1)}, bf16[768,768]{1,0:T(8,128)(2,1)S(1)}, u32[]{:S(2)}, u32[]{:S(2)}) collective-permute-start(bf16[768,768]{1,0:T(8,128)(2,1)S(1)} %get-tuple-element.228), channel_id=1, source_target_pairs={{0,48},{16,32},{32,16},{48,0},{1,49},{17,33},{33,17},{49,1},{2,50}... | collective-permute-start | bytes 3538952 | tf_op jit(solution)/shard_map/ppermute | solution.py:23
  110.7 1.5 add_halves.3
  112.2 1.5 collective-permute-start.30
  113.8 3.2 %weight_part.5 = (bf16[768,768]{1,0:T(8,128)(2,1)S(1)}, bf16[768,768]{1,0:T(8,128)(2,1)S(1)}) custom-call(s32[6]{0:T(128)S(1)} %stack.27.s, bf16[4,4,192,512]{3,2,1,0:T(8,128)(2,1)S(1)} %bitcast.23, bf16[4,4,192,512]{3,2,1,0:T(8,128)(2,1)S(1)} %bitcast.24, bf16[4,4,192,512]{3,2,1,0:T(8,128)(2,1)S(1)} %bitcast.29, bf16[4,4,192,512]{3,2,1,0:T(8,128)(2,1)S(1)} %bitcast.30, ...), custom_call_target="tpu_custom_call" | custom-call | flops 1 | bytes 1 | tf_op jit(solution)/shard_map/weight_part/pallas_call | solution.py:35
  117.0 17.5 %collective-permute-done.23.c = bf16[768,768]{1,0:T(8,128)(2,1)S(1)} collective-permute-done((bf16[768,768]{1,0:T(8,128)(2,1)S(1)}, bf16[768,768]{1,0:T(8,128)(2,1)S(1)}, u32[]{:S(2)}, u32[]{:S(2)}) %collective-permute-start.23) | collective-permute-done | bytes 1179680 | tf_op jit(solution)/shard_map/ppermute | solution.py:23
  135.5 1.7 %collective-permute-start.26 = (bf16[192,768]{1,0:T(8,128)(2,1)S(1)}, bf16[192,768]{1,0:T(8,128)(2,1)S(1)}, u32[]{:S(2)}, u32[]{:S(2)}) collective-permute-start(bf16[192,768]{1,0:T(8,128)(2,1)S(1)} %get-tuple-element.244), channel_id=1, source_target_pairs={{0,4},{4,0},{8,12},{12,8},{1,5},{5,1},{9,13},{13,9},{2,6},{6,2},{1... | collective-permute-start | bytes 884744 | tf_op jit(solution)/shard_map/ppermute | solution.py:23
  137.6 2.1 %collective-permute-start.28 = (bf16[192,768]{1,0:T(8,128)(2,1)S(1)}, bf16[192,768]{1,0:T(8,128)(2,1)S(1)}, u32[]{:S(2)}, u32[]{:S(2)}) collective-permute-start(bf16[192,768]{1,0:T(8,128)(2,1)S(1)} %get-tuple-element.246), channel_id=1, source_target_pairs={{0,8},{4,12},{8,0},{12,4},{1,9},{5,13},{9,1},{13,5},{2,10},{6,14},... | collective-permute-start | bytes 884744 | tf_op jit(solution)/shard_map/ppermute | solution.py:23
  139.7 1.1 collective-permute-done.29.b
  141.7 2.3 %collective-permute-start.31 = (bf16[192,768]{1,0:T(8,128)(2,1)S(1)}, bf16[192,768]{1,0:T(8,128)(2,1)S(1)}, u32[]{:S(2)}, u32[]{:S(2)}) collective-permute-start(bf16[192,768]{1,0:T(8,128)(2,1)S(1)} %get-tuple-element.256), channel_id=1, source_target_pairs={{0,16},{16,0},{32,48},{48,32},{1,17},{17,1},{33,49},{49,33},{2,18}... | collective-permute-start | bytes 884744 | tf_op jit(solution)/shard_map/ppermute | solution.py:23
  144.1 1.9 %collective-permute-start.32 = (bf16[192,768]{1,0:T(8,128)(2,1)S(1)}, bf16[192,768]{1,0:T(8,128)(2,1)S(1)}, u32[]{:S(2)}, u32[]{:S(2)}) collective-permute-start(bf16[192,768]{1,0:T(8,128)(2,1)S(1)} %get-tuple-element.257), channel_id=1, source_target_pairs={{0,48},{16,32},{32,16},{48,0},{1,49},{17,33},{33,17},{49,1},{2,50}... | collective-permute-start | bytes 884744 | tf_op jit(solution)/shard_map/ppermute | solution.py:23
  145.9 1.0 collective-permute-done.26.b
  146.9 2.4 %collective-permute-start.33 = (bf16[192,768]{1,0:T(8,128)(2,1)S(1)}, bf16[192,768]{1,0:T(8,128)(2,1)S(1)}, u32[]{:S(2)}, u32[]{:S(2)}) collective-permute-start(bf16[192,768]{1,0:T(8,128)(2,1)S(1)} %get-tuple-element.258), channel_id=1, source_target_pairs={{0,32},{16,48},{32,0},{48,16},{1,33},{17,49},{33,1},{49,17},{2,34}... | collective-permute-start | bytes 884744 | tf_op jit(solution)/shard_map/ppermute | solution.py:23
  149.3 1.8 %collective-permute-done.28.d = bf16[192,768]{1,0:T(8,128)(2,1)S(1)} collective-permute-done((bf16[192,768]{1,0:T(8,128)(2,1)S(1)}, bf16[192,768]{1,0:T(8,128)(2,1)S(1)}, u32[]{:S(2)}, u32[]{:S(2)}) %collective-permute-start.28) | collective-permute-done | bytes 294944 | tf_op jit(solution)/shard_map/ppermute | solution.py:23
  151.9 1.5 collective-permute-done.32.c
  153.4 1.8 %collective-permute-done.33.d = bf16[192,768]{1,0:T(8,128)(2,1)S(1)} collective-permute-done((bf16[192,768]{1,0:T(8,128)(2,1)S(1)}, bf16[192,768]{1,0:T(8,128)(2,1)S(1)}, u32[]{:S(2)}, u32[]{:S(2)}) %collective-permute-start.33) | collective-permute-done | bytes 294944 | tf_op jit(solution)/shard_map/ppermute | solution.py:23
  155.9 3.8 %collective-permute-done.34.refs_2_ = bf16[96,768]{1,0:T(8,128)(2,1)S(1)} collective-permute-done((bf16[96,768]{1,0:T(8,128)(2,1)S(1)}, bf16[96,768]{1,0:T(8,128)(2,1)S(1)}, u32[]{:S(2)}, u32[]{:S(2)}) %collective-permute-start.34) | collective-permute-done | bytes 147488 | tf_op jit(solution)/shard_map/ppermute | solution.py:23
  160.0 6.4 %collective-permute-done.35.refs_3_ = bf16[96,768]{1,0:T(8,128)(2,1)S(1)} collective-permute-done((bf16[96,768]{1,0:T(8,128)(2,1)S(1)}, bf16[96,768]{1,0:T(8,128)(2,1)S(1)}, u32[]{:S(2)}, u32[]{:S(2)}) %collective-permute-start.35) | collective-permute-done | bytes 147488 | tf_op jit(solution)/shard_map/ppermute | solution.py:23
  166.4 1.6 finish.1
  (62 shorter events, 15.1 us)
Async XLA Ops:
  0.0 10.0 %collective-permute-start.2 = (bf16[512,768]{1,0:T(8,128)(2,1)}, bf16[512,768]{1,0:T(8,128)(2,1)}, u32[]{:S(2)}, u32[]{:S(2)}) collective-permute-start(bf16[512,768]{1,0:T(8,128)(2,1)} %refs_0_.2), channel_id=1, source_target_pairs={{0,1},{1,0},{2,3},{3,2},{4,5},{5,4},{6,7},{7,6},{8,9},{9,8},{10,11... | collective-permute-start | bytes 2359304 | tf_op jit(solution)/shard_map/ppermute | solution.py:23
  0.0 24.1 %collective-permute-start.1 = (bf16[512,768]{1,0:T(8,128)(2,1)}, bf16[512,768]{1,0:T(8,128)(2,1)S(1)}, u32[]{:S(2)}, u32[]{:S(2)}) collective-permute-start(bf16[512,768]{1,0:T(8,128)(2,1)} %refs_0_.2), channel_id=1, source_target_pairs={{0,66},{2,64},{64,2},{66,0},{1,67},{3,65},{65,3},{67,1},{4,70},{6,... | collective-permute-start | bytes 2359304 | tf_op jit(solution)/shard_map/ppermute | solution.py:27
  4.1 20.1 %collective-permute-start = (bf16[512,768]{1,0:T(8,128)(2,1)}, bf16[512,768]{1,0:T(8,128)(2,1)S(1)}, u32[]{:S(2)}, u32[]{:S(2)}) collective-permute-start(bf16[512,768]{1,0:T(8,128)(2,1)} %refs_0_.2), channel_id=1, source_target_pairs={{0,2},{2,0},{1,3},{3,1},{4,6},{6,4},{5,7},{7,5},{8,10},{10,8},{9,1... | collective-permute-start | bytes 2359304 | tf_op jit(solution)/shard_map/ppermute | solution.py:23
  5.5 4.5 %copy-start = (bf16[512,768]{1,0:T(8,128)(2,1)S(1)}, bf16[512,768]{1,0:T(8,128)(2,1)}, u32[]{:S(2)}) copy-start(bf16[512,768]{1,0:T(8,128)(2,1)} %refs_0_.2) | copy-start | bytes 2359300
  7.0 17.1 %collective-permute-start.3 = (f32[8,512]{1,0:T(8,128)S(1)}, f32[8,512]{1,0:T(8,128)S(1)}, u32[]{:S(2)}, u32[]{:S(2)}) collective-permute-start(f32[8,512]{1,0:T(8,128)S(1)} %concatenate.6), channel_id=1, source_target_pairs={{0,64},{64,0},{1,65},{65,1},{2,66},{66,2},{3,67},{67,3},{4,68},{68... | collective-permute-start | bytes 49160 | tf_op jit(solution)/shard_map/ppermute | solution.py:23
  24.2 4.1 %collective-permute-start.7 = (bf16[512,768]{1,0:T(8,128)(2,1)S(1)}, bf16[512,768]{1,0:T(8,128)(2,1)S(1)}, u32[]{:S(2)}, u32[]{:S(2)}) collective-permute-start(bf16[512,768]{1,0:T(8,128)(2,1)S(1)} %collective-permute-done.b.refs_0_.refs_2_), channel_id=1, source_target_pairs={{0,1},{1,0},{2,3},{3,2},{4,5},{5,4},{6,7},{7,6},{8,9},{9,8},{10,11... | collective-permute-start | bytes 2359304 | tf_op jit(solution)/shard_map/ppermute | solution.py:23
  24.2 13.5 %collective-permute-start.6 = (bf16[512,768]{1,0:T(8,128)(2,1)S(1)}, bf16[512,768]{1,0:T(8,128)(2,1)S(1)}, u32[]{:S(2)}, u32[]{:S(2)}) collective-permute-start(bf16[512,768]{1,0:T(8,128)(2,1)S(1)} %collective-permute-done.1.a.refs_0_.refs_4_), channel_id=1, source_target_pairs={{0,1},{1,0},{2,3},{3,2},{4,5},{5,4},{6,7},{7,6},{8,9},{9,8},{10,11... | collective-permute-start | bytes 2359304 | tf_op jit(solution)/shard_map/ppermute | solution.py:23
  25.3 11.5 %collective-permute-start.4 = (bf16[256,768]{1,0:T(8,128)(2,1)S(1)}, bf16[256,768]{1,0:T(8,128)(2,1)S(1)}, u32[]{:S(2)}, u32[]{:S(2)}) collective-permute-start(bf16[256,768]{1,0:T(8,128)(2,1)S(1)} %get-tuple-element.139), channel_id=1, source_target_pairs={{0,2},{2,0},{1,3},{3,1},{4,6},{6,4},{5,7},{7,5},{8,10},{10,8},{9,1... | collective-permute-start | bytes 1179656 | tf_op jit(solution)/shard_map/ppermute | solution.py:23
  25.7 12.0 %collective-permute-start.5 = (bf16[256,768]{1,0:T(8,128)(2,1)S(1)}, bf16[256,768]{1,0:T(8,128)(2,1)S(1)}, u32[]{:S(2)}, u32[]{:S(2)}) collective-permute-start(bf16[256,768]{1,0:T(8,128)(2,1)S(1)} %get-tuple-element.140), channel_id=1, source_target_pairs={{0,66},{2,64},{64,2},{66,0},{1,67},{3,65},{65,3},{67,1},{4,70},{6,... | collective-permute-start | bytes 1179656 | tf_op jit(solution)/shard_map/ppermute | solution.py:27
  37.7 14.4 %collective-permute-start.8 = (bf16[512,512]{1,0:T(8,128)(2,1)S(1)}, bf16[512,512]{1,0:T(8,128)(2,1)S(1)}, u32[]{:S(2)}, u32[]{:S(2)}) collective-permute-start(bf16[512,512]{1,0:T(8,128)(2,1)S(1)} %get-tuple-element.149), channel_id=1, source_target_pairs={{0,64},{64,0},{1,65},{65,1},{2,66},{66,2},{3,67},{67,3},{4,68},{68... | collective-permute-start | bytes 1572872 | tf_op jit(solution)/shard_map/ppermute | solution.py:23
  40.5 2.8 %collective-permute-start.9 = (bf16[256,768]{1,0:T(8,128)(2,1)S(1)}, bf16[256,768]{1,0:T(8,128)(2,1)S(1)}, u32[]{:S(2)}, u32[]{:S(2)}) collective-permute-start(bf16[256,768]{1,0:T(8,128)(2,1)S(1)} %collective-permute-done.4.refs_2_.refs_0_), channel_id=1, source_target_pairs={{0,1},{1,0},{2,3},{3,2},{4,5},{5,4},{6,7},{7,6},{8,9},{9,8},{10,11... | collective-permute-start | bytes 1179656 | tf_op jit(solution)/shard_map/ppermute | solution.py:23
  40.5 2.8 %collective-permute-start.10 = (bf16[256,768]{1,0:T(8,128)(2,1)S(1)}, bf16[256,768]{1,0:T(8,128)(2,1)S(1)}, u32[]{:S(2)}, u32[]{:S(2)}) collective-permute-start(bf16[256,768]{1,0:T(8,128)(2,1)S(1)} %collective-permute-done.5.refs_3_.refs_1_), channel_id=1, source_target_pairs={{0,1},{1,0},{2,3},{3,2},{4,5},{5,4},{6,7},{7,6},{8,9},{9,8},{10,11... | collective-permute-start | bytes 1179656 | tf_op jit(solution)/shard_map/ppermute | solution.py:23
  54.4 10.4 %collective-permute-start.11 = (bf16[528,128]{1,0:T(8,128)(2,1)S(1)}, bf16[528,128]{1,0:T(8,128)(2,1)S(1)}, u32[]{:S(2)}, u32[]{:S(2)}) collective-permute-start(bf16[528,128]{1,0:T(8,128)(2,1)S(1)} %get-tuple-element.166), channel_id=1, source_target_pairs={{0,4},{4,0},{8,12},{12,8},{1,5},{5,1},{9,13},{13,9},{2,6},{6,2},{1... | collective-permute-start | bytes 405512 | tf_op jit(solution)/shard_map/ppermute | solution.py:23
  56.0 9.1 %collective-permute-start.12 = (bf16[528,128]{1,0:T(8,128)(2,1)S(1)}, bf16[528,128]{1,0:T(8,128)(2,1)S(1)}, u32[]{:S(2)}, u32[]{:S(2)}) collective-permute-start(bf16[528,128]{1,0:T(8,128)(2,1)S(1)} %get-tuple-element.167), channel_id=1, source_target_pairs={{0,12},{4,8},{8,4},{12,0},{1,13},{5,9},{9,5},{13,1},{2,14},{6,10},... | collective-permute-start | bytes 405512 | tf_op jit(solution)/shard_map/ppermute | solution.py:23
  58.2 6.9 %collective-permute-start.13 = (bf16[528,128]{1,0:T(8,128)(2,1)S(1)}, bf16[528,128]{1,0:T(8,128)(2,1)S(1)}, u32[]{:S(2)}, u32[]{:S(2)}) collective-permute-start(bf16[528,128]{1,0:T(8,128)(2,1)S(1)} %get-tuple-element.168), channel_id=1, source_target_pairs={{0,8},{4,12},{8,0},{12,4},{1,9},{5,13},{9,1},{13,5},{2,10},{6,14},... | collective-permute-start | bytes 405512 | tf_op jit(solution)/shard_map/ppermute | solution.py:23
  65.9 9.5 %collective-permute-start.16 = (bf16[528,128]{1,0:T(8,128)(2,1)S(1)}, bf16[528,128]{1,0:T(8,128)(2,1)S(1)}, u32[]{:S(2)}, u32[]{:S(2)}) collective-permute-start(bf16[528,128]{1,0:T(8,128)(2,1)S(1)} %get-tuple-element.175.a), channel_id=1, source_target_pairs={{0,32},{16,48},{32,0},{48,16},{1,33},{17,49},{33,1},{49,17},{2,34}... | collective-permute-start | bytes 405512 | tf_op jit(solution)/shard_map/ppermute | solution.py:23
  69.0 6.4 %collective-permute-start.15 = (bf16[528,128]{1,0:T(8,128)(2,1)S(1)}, bf16[528,128]{1,0:T(8,128)(2,1)S(1)}, u32[]{:S(2)}, u32[]{:S(2)}) collective-permute-start(bf16[528,128]{1,0:T(8,128)(2,1)S(1)} %get-tuple-element.175.a), channel_id=1, source_target_pairs={{0,48},{16,32},{32,16},{48,0},{1,49},{17,33},{33,17},{49,1},{2,50}... | collective-permute-start | bytes 405512 | tf_op jit(solution)/shard_map/ppermute | solution.py:23
  70.1 5.3 %collective-permute-start.14 = (bf16[528,128]{1,0:T(8,128)(2,1)S(1)}, bf16[528,128]{1,0:T(8,128)(2,1)S(1)}, u32[]{:S(2)}, u32[]{:S(2)}) collective-permute-start(bf16[528,128]{1,0:T(8,128)(2,1)S(1)} %get-tuple-element.175.a), channel_id=1, source_target_pairs={{0,16},{16,0},{32,48},{48,32},{1,17},{17,1},{33,49},{49,33},{2,18}... | collective-permute-start | bytes 405512 | tf_op jit(solution)/shard_map/ppermute | solution.py:23
  76.3 7.4 %collective-permute-start.17 = (bf16[512,128]{1,0:T(8,128)(2,1)S(1)}, bf16[512,128]{1,0:T(8,128)(2,1)S(1)}, u32[]{:S(2)}, u32[]{:S(2)}) collective-permute-start(bf16[512,128]{1,0:T(8,128)(2,1)S(1)} %get-tuple-element.193), channel_id=1, source_target_pairs={{0,4},{4,0},{8,12},{12,8},{1,5},{5,1},{9,13},{13,9},{2,6},{6,2},{1... | collective-permute-start | bytes 393224 | tf_op jit(solution)/shard_map/ppermute | solution.py:23
  77.3 6.9 %collective-permute-start.18 = (bf16[512,128]{1,0:T(8,128)(2,1)S(1)}, bf16[512,128]{1,0:T(8,128)(2,1)S(1)}, u32[]{:S(2)}, u32[]{:S(2)}) collective-permute-start(bf16[512,128]{1,0:T(8,128)(2,1)S(1)} %get-tuple-element.194), channel_id=1, source_target_pairs={{0,12},{4,8},{8,4},{12,0},{1,13},{5,9},{9,5},{13,1},{2,14},{6,10},... | collective-permute-start | bytes 393224 | tf_op jit(solution)/shard_map/ppermute | solution.py:23
  79.4 6.5 %collective-permute-start.19 = (bf16[512,128]{1,0:T(8,128)(2,1)S(1)}, bf16[512,128]{1,0:T(8,128)(2,1)S(1)}, u32[]{:S(2)}, u32[]{:S(2)}) collective-permute-start(bf16[512,128]{1,0:T(8,128)(2,1)S(1)} %get-tuple-element.195), channel_id=1, source_target_pairs={{0,8},{4,12},{8,0},{12,4},{1,9},{5,13},{9,1},{13,5},{2,10},{6,14},... | collective-permute-start | bytes 393224 | tf_op jit(solution)/shard_map/ppermute | solution.py:23
  93.5 13.9 %collective-permute-start.21 = (bf16[384,768]{1,0:T(8,128)(2,1)S(1)}, bf16[384,768]{1,0:T(8,128)(2,1)S(1)}, u32[]{:S(2)}, u32[]{:S(2)}) collective-permute-start(bf16[384,768]{1,0:T(8,128)(2,1)S(1)} %get-tuple-element.222), channel_id=1, source_target_pairs={{0,48},{16,32},{32,16},{48,0},{1,49},{17,33},{33,17},{49,1},{2,50}... | collective-permute-start | bytes 1769480 | tf_op jit(solution)/shard_map/ppermute | solution.py:23
  95.7 11.7 %collective-permute-start.20 = (bf16[384,768]{1,0:T(8,128)(2,1)S(1)}, bf16[384,768]{1,0:T(8,128)(2,1)S(1)}, u32[]{:S(2)}, u32[]{:S(2)}) collective-permute-start(bf16[384,768]{1,0:T(8,128)(2,1)S(1)} %get-tuple-element.218), channel_id=1, source_target_pairs={{0,16},{16,0},{32,48},{48,32},{1,17},{17,1},{33,49},{49,33},{2,18}... | collective-permute-start | bytes 1769480 | tf_op jit(solution)/shard_map/ppermute | solution.py:23
  97.1 13.6 %collective-permute-start.24 = (bf16[384,768]{1,0:T(8,128)(2,1)S(1)}, bf16[384,768]{1,0:T(8,128)(2,1)S(1)}, u32[]{:S(2)}, u32[]{:S(2)}) collective-permute-start(bf16[384,768]{1,0:T(8,128)(2,1)S(1)} %get-tuple-element.231), channel_id=1, source_target_pairs={{0,4},{4,0},{8,12},{12,8},{1,5},{5,1},{9,13},{13,9},{2,6},{6,2},{1... | collective-permute-start | bytes 1769480 | tf_op jit(solution)/shard_map/ppermute | solution.py:23
  97.8 12.9 %collective-permute-start.25 = (bf16[384,768]{1,0:T(8,128)(2,1)S(1)}, bf16[384,768]{1,0:T(8,128)(2,1)S(1)}, u32[]{:S(2)}, u32[]{:S(2)}) collective-permute-start(bf16[384,768]{1,0:T(8,128)(2,1)S(1)} %get-tuple-element.232), channel_id=1, source_target_pairs={{0,12},{4,8},{8,4},{12,0},{1,13},{5,9},{9,5},{13,1},{2,14},{6,10},... | collective-permute-start | bytes 1769480 | tf_op jit(solution)/shard_map/ppermute | solution.py:23
  108.9 25.6 %collective-permute-start.23 = (bf16[768,768]{1,0:T(8,128)(2,1)S(1)}, bf16[768,768]{1,0:T(8,128)(2,1)S(1)}, u32[]{:S(2)}, u32[]{:S(2)}) collective-permute-start(bf16[768,768]{1,0:T(8,128)(2,1)S(1)} %get-tuple-element.228), channel_id=1, source_target_pairs={{0,48},{16,32},{32,16},{48,0},{1,49},{17,33},{33,17},{49,1},{2,50}... | collective-permute-start | bytes 3538952 | tf_op jit(solution)/shard_map/ppermute | solution.py:23
  110.7 23.8 %collective-permute-start.22 = (bf16[768,768]{1,0:T(8,128)(2,1)S(1)}, bf16[768,768]{1,0:T(8,128)(2,1)S(1)}, u32[]{:S(2)}, u32[]{:S(2)}) collective-permute-start(bf16[768,768]{1,0:T(8,128)(2,1)S(1)} %get-tuple-element.227), channel_id=1, source_target_pairs={{0,16},{16,0},{32,48},{48,32},{1,17},{17,1},{33,49},{49,33},{2,18}... | collective-permute-start | bytes 3538952 | tf_op jit(solution)/shard_map/ppermute | solution.py:23
  112.2 27.5 %collective-permute-start.30 = (bf16[768,768]{1,0:T(8,128)(2,1)S(1)}, bf16[768,768]{1,0:T(8,128)(2,1)S(1)}, u32[]{:S(2)}, u32[]{:S(2)}) collective-permute-start(bf16[768,768]{1,0:T(8,128)(2,1)S(1)} %get-tuple-element.248), channel_id=1, source_target_pairs={{0,12},{4,8},{8,4},{12,0},{1,13},{5,9},{9,5},{13,1},{2,14},{6,10},... | collective-permute-start | bytes 3538952 | tf_op jit(solution)/shard_map/ppermute | solution.py:23
  113.7 27.1 %collective-permute-start.29 = (bf16[768,768]{1,0:T(8,128)(2,1)S(1)}, bf16[768,768]{1,0:T(8,128)(2,1)S(1)}, u32[]{:S(2)}, u32[]{:S(2)}) collective-permute-start(bf16[768,768]{1,0:T(8,128)(2,1)S(1)} %get-tuple-element.235), channel_id=1, source_target_pairs={{0,4},{4,0},{8,12},{12,8},{1,5},{5,1},{9,13},{13,9},{2,6},{6,2},{1... | collective-permute-start | bytes 3538952 | tf_op jit(solution)/shard_map/ppermute | solution.py:23
  135.5 11.4 %collective-permute-start.26 = (bf16[192,768]{1,0:T(8,128)(2,1)S(1)}, bf16[192,768]{1,0:T(8,128)(2,1)S(1)}, u32[]{:S(2)}, u32[]{:S(2)}) collective-permute-start(bf16[192,768]{1,0:T(8,128)(2,1)S(1)} %get-tuple-element.244), channel_id=1, source_target_pairs={{0,4},{4,0},{8,12},{12,8},{1,5},{5,1},{9,13},{13,9},{2,6},{6,2},{1... | collective-permute-start | bytes 884744 | tf_op jit(solution)/shard_map/ppermute | solution.py:23
  137.2 12.1 %collective-permute-start.27 = (bf16[192,768]{1,0:T(8,128)(2,1)S(1)}, bf16[192,768]{1,0:T(8,128)(2,1)S(1)}, u32[]{:S(2)}, u32[]{:S(2)}) collective-permute-start(bf16[192,768]{1,0:T(8,128)(2,1)S(1)} %get-tuple-element.245), channel_id=1, source_target_pairs={{0,12},{4,8},{8,4},{12,0},{1,13},{5,9},{9,5},{13,1},{2,14},{6,10},... | collective-permute-start | bytes 884744 | tf_op jit(solution)/shard_map/ppermute | solution.py:23
  137.6 13.5 %collective-permute-start.28 = (bf16[192,768]{1,0:T(8,128)(2,1)S(1)}, bf16[192,768]{1,0:T(8,128)(2,1)S(1)}, u32[]{:S(2)}, u32[]{:S(2)}) collective-permute-start(bf16[192,768]{1,0:T(8,128)(2,1)S(1)} %get-tuple-element.246), channel_id=1, source_target_pairs={{0,8},{4,12},{8,0},{12,4},{1,9},{5,13},{9,1},{13,5},{2,10},{6,14},... | collective-permute-start | bytes 884744 | tf_op jit(solution)/shard_map/ppermute | solution.py:23
  141.7 10.1 %collective-permute-start.31 = (bf16[192,768]{1,0:T(8,128)(2,1)S(1)}, bf16[192,768]{1,0:T(8,128)(2,1)S(1)}, u32[]{:S(2)}, u32[]{:S(2)}) collective-permute-start(bf16[192,768]{1,0:T(8,128)(2,1)S(1)} %get-tuple-element.256), channel_id=1, source_target_pairs={{0,16},{16,0},{32,48},{48,32},{1,17},{17,1},{33,49},{49,33},{2,18}... | collective-permute-start | bytes 884744 | tf_op jit(solution)/shard_map/ppermute | solution.py:23
  144.1 9.3 %collective-permute-start.32 = (bf16[192,768]{1,0:T(8,128)(2,1)S(1)}, bf16[192,768]{1,0:T(8,128)(2,1)S(1)}, u32[]{:S(2)}, u32[]{:S(2)}) collective-permute-start(bf16[192,768]{1,0:T(8,128)(2,1)S(1)} %get-tuple-element.257), channel_id=1, source_target_pairs={{0,48},{16,32},{32,16},{48,0},{1,49},{17,33},{33,17},{49,1},{2,50}... | collective-permute-start | bytes 884744 | tf_op jit(solution)/shard_map/ppermute | solution.py:23
  146.9 8.2 %collective-permute-start.33 = (bf16[192,768]{1,0:T(8,128)(2,1)S(1)}, bf16[192,768]{1,0:T(8,128)(2,1)S(1)}, u32[]{:S(2)}, u32[]{:S(2)}) collective-permute-start(bf16[192,768]{1,0:T(8,128)(2,1)S(1)} %get-tuple-element.258), channel_id=1, source_target_pairs={{0,32},{16,48},{32,0},{48,16},{1,33},{17,49},{33,1},{49,17},{2,34}... | collective-permute-start | bytes 884744 | tf_op jit(solution)/shard_map/ppermute | solution.py:23
  151.8 7.9 %collective-permute-start.34 = (bf16[96,768]{1,0:T(8,128)(2,1)S(1)}, bf16[96,768]{1,0:T(8,128)(2,1)S(1)}, u32[]{:S(2)}, u32[]{:S(2)}) collective-permute-start(bf16[96,768]{1,0:T(8,128)(2,1)S(1)} %get-tuple-element.263), channel_id=1, source_target_pairs={{0,64},{64,0},{1,65},{65,1},{2,66},{66,2},{3,67},{67,3},{4,68},{68... | collective-permute-start | bytes 442376 | tf_op jit(solution)/shard_map/ppermute | solution.py:23
  159.7 6.6 %collective-permute-start.35 = (bf16[96,768]{1,0:T(8,128)(2,1)S(1)}, bf16[96,768]{1,0:T(8,128)(2,1)S(1)}, u32[]{:S(2)}, u32[]{:S(2)}) collective-permute-start(bf16[96,768]{1,0:T(8,128)(2,1)S(1)} %get-tuple-element.266), channel_id=1, source_target_pairs={{0,64},{64,0},{1,65},{65,1},{2,66},{66,2},{3,67},{67,3},{4,68},{68... | collective-permute-start | bytes 442376 | tf_op jit(solution)/shard_map/ppermute | solution.py:23

commit v10 on v9

--- a/solution.py
+++ b/solution.py
@@ -471,13 +471,14 @@
         out_a[...] = (a[...].astype(F32) + u[...].astype(F32)).astype(BF16)
         out_b[...] = (b[...].astype(F32) + d[...].astype(F32)).astype(BF16)
 
-    first = pl.BlockSpec((n, cols), lambda i, s: (0, 0))
-    second = pl.BlockSpec((n, cols), lambda i, s: (1, 0))
+    steps = 4
+    first = pl.BlockSpec((n // steps, cols), lambda i, s: (i, 0))
+    second = pl.BlockSpec((n // steps, cols), lambda i, s: (i + steps, 0))
     return call(
         "add_halves",
         body,
         table,
-        (1,),
+        (steps,),
         (near_up, near_down, up, down),
         [first, second, first, first],
         [shape(near_up.shape), shape(near_down.shape)],
@@ -540,13 +541,13 @@
         out = refs[-1]
         for i, half in enumerate((s[Z], 1 - s[Z])):
             for k in range(2):
-                for j in range(3):
-                    at = pl.ds(pl.multiple_of(half * 2 * side + k * side, side), side)
-                    out[j, :, at] = refs[2 * i + k][:, j * side : (j + 1) * side].astype(F32)
+                at = pl.ds(pl.multiple_of(half * 2 * side + k * side, side), side)
+                out[0, :, at] = refs[2 * i + k][...].astype(F32)
 
     out = shape((3, rows, 4 * side), F32)
-    operands = (*here, *there)
-    return call("finish", body, table, (1,), operands, [whole(x) for x in operands], out, whole(out), 8)
+    part = pl.BlockSpec((rows, side), lambda j, s: (0, j))
+    spec = pl.BlockSpec((1, rows, 4 * side), lambda j, s: (j, 0, 0))
+    return call("finish", body, table, (3,), (*here, *there), [part] * 4, out, spec, 8)
 
 
 def swaps(pieces, left, right):
@@ -644,7 +645,7 @@
     r_got, _ = tied((r_got, l_here))
     r_here, r_there = final_sums(table, (r_cut[3], *r_got))
     l_there = send(l_there, "c0", 1)
-    l_there, r_there = tied((l_there, r_there))
+    l_there, r_here = tied((l_there, r_here))
     there = [l_there, send(r_there, "c0", 1)]
     return jnp.transpose(finish(table, (l_here, r_here), there), (1, 0, 2))
 

time: 168 us -> 168 us (level)
  starting transfers between devices: 45.4 us -> 48 us
  waiting for transfers between devices: 48.1 us -> 45.9 us
    ppermute x34, starting transfers between devices: 38.6 us -> 41.2 us  [send(): lax.ppermute(x, axis, [(i, i ^ by) for i in range(lax.axis_size(axis))])]
    ppermute x34, waiting for transfers between devices: 47.2 us -> 45 us  [send(): lax.ppermute(x, axis, [(i, i ^ by) for i in range(lax.axis_size(axis))])]
  transfers between devices with their start and end apart: 36 -> 36, of which waited for: 16 -> 14; matrix products, arithmetic and copies ran while one was open for 2% -> 2% of each run, Pallas kernels for 34% -> 33%
where the time goes in v10:
time: 168 us
  Pallas kernels  69.5 us (41%)
  starting transfers between devices  48 us (29%)
  waiting for transfers between devices  45.9 us (27%)
  other arithmetic  1.96 us (1%)
    pallas_call x24, Pallas kernels, call(): pl.pallas_call(body, grid_spec=pltpu.PrefetchScalarGridSpec(num_scalar_pr...  69.5 us
    ppermute x34, waiting for transfers between devices, send(): lax.ppermute(x, axis, [(i, i ^ by) for i in range(lax.axis_size(axis))])  45 us
    ppermute x34, starting transfers between devices, send(): lax.ppermute(x, axis, [(i, i ^ by) for i in range(lax.axis_size(axis))])  41.2 us
    ppermute x2, starting transfers between devices, across(): return lax.ppermute(x, ('c0', 'zl'), [(0, 3), (1, 2), (2, 1), (3, 0)])  6.75 us
  transfers between devices with their start and end apart: 36, of which 14 were waited for; matrix products, arithmetic and copies ran while one was open for 2% of the time, Pallas kernels for 33%

profile of v10, /device:TPU:0, one launch (start us, length us, event | category | flops | bytes accessed | tf_op | source)
XLA Modules:
  0.0 167.9 jit_solution(11994844958780356101)
XLA Ops:
  0.0 4.1 %collective-permute-start.1 = (bf16[512,768]{1,0:T(8,128)(2,1)}, bf16[512,768]{1,0:T(8,128)(2,1)S(1)}, u32[]{:S(2)}, u32[]{:S(2)}) collective-permute-start(bf16[512,768]{1,0:T(8,128)(2,1)} %refs_0_.2), channel_id=1, source_target_pairs={{0,66},{2,64},{64,2},{66,0},{1,67},{3,65},{65,3},{67,1},{4,70},{6,... | collective-permute-start | bytes 2359304 | tf_op jit(solution)/shard_map/ppermute | solution.py:27
  5.5 1.1 reduce-window.6
  7.0 1.6 collective-permute-start.3
  8.6 1.3 constant_dynamic-slice_fusion
  10.0 5.5 %project.3.refs_4_ = f32[3,512,512]{2,1,0:T(8,128)S(1)} custom-call(s32[6]{0:T(128)S(1)} %stack.27.s, bf16[512,768]{1,0:T(8,128)(2,1)S(1)} %copy-done, bf16[512,768]{1,0:T(8,128)(2,1)} %collective-permute-done.2.refs_1_, bf16[3,3072,1024]{2,1,0:T(8,128)(2,1)} %bitcast.31, bf16[3,3072,1024]{2,1,0:T(8,128)(2,1)} %bitcast.32), custom_call_target="tpu_custom_call" | custom-call | flops 1 | bytes 1 | tf_op jit(solution)/shard_map/project/pallas_call | solution.py:35
  15.5 8.6 %collective-permute-done.3.refs_10_.cum_ref = f32[8,512]{1,0:T(8,128)S(1)} collective-permute-done((f32[8,512]{1,0:T(8,128)S(1)}, f32[8,512]{1,0:T(8,128)S(1)}, u32[]{:S(2)}, u32[]{:S(2)}) %collective-permute-start.3) | collective-permute-done | bytes 16416 | tf_op jit(solution)/shard_map/ppermute | solution.py:23
  25.7 2.6 %collective-permute-start.5 = (bf16[256,768]{1,0:T(8,128)(2,1)S(1)}, bf16[256,768]{1,0:T(8,128)(2,1)S(1)}, u32[]{:S(2)}, u32[]{:S(2)}) collective-permute-start(bf16[256,768]{1,0:T(8,128)(2,1)S(1)} %get-tuple-element.140), channel_id=1, source_target_pairs={{0,66},{2,64},{64,2},{66,0},{1,67},{3,65},{65,3},{67,1},{4,70},{6,... | collective-permute-start | bytes 1179656 | tf_op jit(solution)/shard_map/ppermute | solution.py:27
  28.3 5.3 %project.4.qkv_ref = bf16[3,512,512]{2,1,0:T(8,128)(2,1)S(1)} custom-call(s32[6]{0:T(128)S(1)} %stack.27.s, bf16[512,768]{1,0:T(8,128)(2,1)S(1)} %collective-permute-done.b.refs_0_.refs_2_, bf16[512,768]{1,0:T(8,128)(2,1)S(1)} %collective-permute-done.7.refs_1_.refs_3_, bf16[3,3072,1024]{2,1,0:T(8,128)(2,1)} %bitcast.33, bf16[3,3072,1024]{2,1,0:T(8,128)(2,1)} %bitcast.34, ...), custom_call_target="tpu_custom_call" | custom-call | flops 1 | bytes 1 | tf_op jit(solution)/shard_map/project/pallas_call | solution.py:35
  33.6 3.2 %turn.2 = bf16[16,2,96,512]{3,2,1,0:T(8,128)(2,1)S(1)} custom-call(s32[6]{0:T(128)S(1)} %stack.27.s, bf16[512,768]{1,0:T(8,128)(2,1)S(1)} %copy-done, bf16[512,768]{1,0:T(8,128)(2,1)} %collective-permute-done.2.refs_1_, bf16[512,768]{1,0:T(8,128)(2,1)S(1)} %collective-permute-done.b.refs_0_.refs_2_, bf16[512,768]{1,0:T(8,128)(2,1)S(1)} %collective-permute-done.7.refs_1_.refs_3_), custom_call_target="tpu_custom_call" | custom-call | flops 1 | bytes 1 | tf_op jit(solution)/shard_map/turn/pallas_call | solution.py:35
  37.7 2.8 %collective-permute-start.8 = (bf16[512,512]{1,0:T(8,128)(2,1)S(1)}, bf16[512,512]{1,0:T(8,128)(2,1)S(1)}, u32[]{:S(2)}, u32[]{:S(2)}) collective-permute-start(bf16[512,512]{1,0:T(8,128)(2,1)S(1)} %get-tuple-element.149), channel_id=1, source_target_pairs={{0,64},{64,0},{1,65},{65,1},{2,66},{66,2},{3,67},{67,3},{4,68},{68... | collective-permute-start | bytes 1572872 | tf_op jit(solution)/shard_map/ppermute | solution.py:23
  41.0 2.3 %shard_states.2 = (bf16[528,128]{1,0:T(8,128)(2,1)S(1)}, bf16[528,128]{1,0:T(8,128)(2,1)S(1)}, bf16[528,128]{1,0:T(8,128)(2,1)S(1)}, bf16[528,128]{1,0:T(8,128)(2,1)S(1)}) custom-call(s32[6]{0:T(128)S(1)} %stack.27.s, bf16[3,512,512]{2,1,0:T(8,128)(2,1)S(1)} %project.4.qkv_ref, bf16[512,512]{1,0:T(8,128)(2,1)S(1)} %get-tuple-element.267.og_ref, ...), custom_call_target="tpu_custom_call" | custom-call | flops 1 | bytes 1 | tf_op jit(solution)/shard_map/shard_states/pallas_call | solution.py:35
  43.4 7.9 %project.5.qkv_ref = bf16[3,512,512]{2,1,0:T(8,128)(2,1)S(1)} custom-call(s32[6]{0:T(128)S(1)} %stack.27.s, bf16[512,768]{1,0:T(8,128)(2,1)S(1)} %collective-permute-done.1.a.refs_0_.refs_4_, bf16[512,768]{1,0:T(8,128)(2,1)S(1)} %collective-permute-done.6.refs_1_.refs_5_, bf16[256,768]{1,0:T(8,128)(2,1)S(1)} %collective-permute-done.4.refs_2_.refs_0_, ...), custom_call_target="tpu_custom_call" | custom-call | flops 1 | bytes 1 | tf_op jit(solution)/shard_map/project/pallas_call | solution.py:35
  52.1 2.3 %shard_states.3 = (bf16[528,128]{1,0:T(8,128)(2,1)S(1)}, bf16[528,128]{1,0:T(8,128)(2,1)S(1)}, bf16[528,128]{1,0:T(8,128)(2,1)S(1)}, bf16[528,128]{1,0:T(8,128)(2,1)S(1)}) custom-call(s32[6]{0:T(128)S(1)} %stack.27.s, bf16[3,512,512]{2,1,0:T(8,128)(2,1)S(1)} %project.5.qkv_ref, bf16[512,512]{1,0:T(8,128)(2,1)S(1)} %collective-permute-done.8.og_ref, ...), custom_call_target="tpu_custom_call" | custom-call | flops 1 | bytes 1 | tf_op jit(solution)/shard_map/shard_states/pallas_call | solution.py:35
  54.4 1.7 collective-permute-start.11
  56.0 2.2 %collective-permute-start.12 = (bf16[528,128]{1,0:T(8,128)(2,1)S(1)}, bf16[528,128]{1,0:T(8,128)(2,1)S(1)}, u32[]{:S(2)}, u32[]{:S(2)}) collective-permute-start(bf16[528,128]{1,0:T(8,128)(2,1)S(1)} %get-tuple-element.167), channel_id=1, source_target_pairs={{0,12},{4,8},{8,4},{12,0},{1,13},{5,9},{9,5},{13,1},{2,14},{6,10},... | collective-permute-start | bytes 405512 | tf_op jit(solution)/shard_map/ppermute | solution.py:23
  59.0 5.9 %local_grads.3 = (bf16[3,512,512]{2,1,0:T(8,128)(2,1)S(1)}, bf16[3,512,512]{2,1,0:T(8,128)(2,1)S(1)}) custom-call(s32[6]{0:T(128)S(1)} %stack.27.s, bf16[3,512,512]{2,1,0:T(8,128)(2,1)S(1)} %project.4.qkv_ref, bf16[512,512]{1,0:T(8,128)(2,1)S(1)} %get-tuple-element.267.og_ref, f32[8,512]{1,0:T(8,128)S(1)} %concatenate.7.refs_5_.cum_ref), custom_call_target="tpu_custom_call" | custom-call | flops 1 | bytes 1 | tf_op jit(solution)/shard_map/local_grads/pallas_call | solution.py:35
  65.9 3.1 %collective-permute-start.16 = (bf16[528,128]{1,0:T(8,128)(2,1)S(1)}, bf16[528,128]{1,0:T(8,128)(2,1)S(1)}, u32[]{:S(2)}, u32[]{:S(2)}) collective-permute-start(bf16[528,128]{1,0:T(8,128)(2,1)S(1)} %get-tuple-element.175.a), channel_id=1, source_target_pairs={{0,32},{16,48},{32,0},{48,16},{1,33},{17,49},{33,1},{49,17},{2,34}... | collective-permute-start | bytes 405512 | tf_op jit(solution)/shard_map/ppermute | solution.py:23
  69.0 1.1 collective-permute-start.15
  70.1 3.2 %local_grads.4 = (bf16[3,512,512]{2,1,0:T(8,128)(2,1)S(1)}, bf16[3,512,512]{2,1,0:T(8,128)(2,1)S(1)}) custom-call(s32[6]{0:T(128)S(1)} %stack.27.s, bf16[3,512,512]{2,1,0:T(8,128)(2,1)S(1)} %project.5.qkv_ref, bf16[512,512]{1,0:T(8,128)(2,1)S(1)} %collective-permute-done.8.og_ref, f32[8,512]{1,0:T(8,128)S(1)} %collective-permute-done.3.refs_10_.cum_ref), custom_call_target="tpu_custom_call" | custom-call | flops 1 | bytes 1 | tf_op jit(solution)/shard_map/local_grads/pallas_call | solution.py:35
  73.4 2.0 %turn.3 = bf16[16,2,96,512]{3,2,1,0:T(8,128)(2,1)S(1)} custom-call(s32[6]{0:T(128)S(1)} %stack.27.s, bf16[256,768]{1,0:T(8,128)(2,1)S(1)} %collective-permute-done.4.refs_2_.refs_0_, bf16[256,768]{1,0:T(8,128)(2,1)S(1)} %collective-permute-done.5.refs_3_.refs_1_, bf16[256,768]{1,0:T(8,128)(2,1)S(1)} %collective-permute-done.9.refs_4_.refs_2_, ...), custom_call_target="tpu_custom_call" | custom-call | flops 1 | bytes 1 | tf_op jit(solution)/shard_map/turn/pallas_call | solution.py:35
  76.3 1.0 collective-permute-start.17
  77.3 2.2 %collective-permute-start.18 = (bf16[512,128]{1,0:T(8,128)(2,1)S(1)}, bf16[512,128]{1,0:T(8,128)(2,1)S(1)}, u32[]{:S(2)}, u32[]{:S(2)}) collective-permute-start(bf16[512,128]{1,0:T(8,128)(2,1)S(1)} %get-tuple-element.194), channel_id=1, source_target_pairs={{0,12},{4,8},{8,4},{12,0},{1,13},{5,9},{9,5},{13,1},{2,14},{6,10},... | collective-permute-start | bytes 393224 | tf_op jit(solution)/shard_map/ppermute | solution.py:23
  79.4 1.0 collective-permute-start.19
  80.5 3.2 %local_grads.5 = (bf16[3,512,512]{2,1,0:T(8,128)(2,1)S(1)}, bf16[3,512,512]{2,1,0:T(8,128)(2,1)S(1)}) custom-call(s32[6]{0:T(128)S(1)} %stack.27.s, bf16[3,512,512]{2,1,0:T(8,128)(2,1)S(1)} %project.5.qkv_ref, bf16[512,512]{1,0:T(8,128)(2,1)S(1)} %collective-permute-done.8.og_ref, ...), custom_call_target="tpu_custom_call", output_to_operand_aliasing={{0}: (4, {}), {1}: (5, {})} | custom-call | flops 1 | bytes 1 | tf_op jit(solution)/shard_map/local_grads/pallas_call | solution.py:35
  84.2 1.8 %collective-permute-done.19.c = bf16[512,128]{1,0:T(8,128)(2,1)S(1)} collective-permute-done((bf16[512,128]{1,0:T(8,128)(2,1)S(1)}, bf16[512,128]{1,0:T(8,128)(2,1)S(1)}, u32[]{:S(2)}, u32[]{:S(2)}) %collective-permute-start.19) | collective-permute-done | bytes 131104 | tf_op jit(solution)/shard_map/ppermute | solution.py:23
  85.9 4.4 %whole_grads.1 = (bf16[512,768]{1,0:T(8,128)(2,1)S(1)}, bf16[512,768]{1,0:T(8,128)(2,1)S(1)}, bf16[512,768]{1,0:T(8,128)(2,1)S(1)}, bf16[512,768]{1,0:T(8,128)(2,1)S(1)}) custom-call(s32[6]{0:T(128)S(1)} %stack.27.s, bf16[3,512,512]{2,1,0:T(8,128)(2,1)S(1)} %get-tuple-element.207.local_a, bf16[3,512,512]{2,1,0:T(8,128)(2,1)S(1)} %get-tuple-element.208.ready_a, ...), custom_call_target="tpu_custom_call" | custom-call | flops 1 | bytes 1 | tf_op jit(solution)/shard_map/whole_grads/pallas_call | solution.py:35
  90.4 3.2 %weight_part.3 = (bf16[384,768]{1,0:T(8,128)(2,1)S(1)}, bf16[384,768]{1,0:T(8,128)(2,1)S(1)}, bf16[384,768]{1,0:T(8,128)(2,1)S(1)}, bf16[384,768]{1,0:T(8,128)(2,1)S(1)}) custom-call(s32[6]{0:T(128)S(1)} %stack.27.s, bf16[4,4,192,512]{3,2,1,0:T(8,128)(2,1)S(1)} %bitcast.19, bf16[4,4,192,512]{3,2,1,0:T(8,128)(2,1)S(1)} %bitcast.20, ...), custom_call_target="tpu_custom_call" | custom-call | flops 1 | bytes 1 | tf_op jit(solution)/shard_map/weight_part/pallas_call | solution.py:35
  93.5 2.2 %collective-permute-start.21 = (bf16[384,768]{1,0:T(8,128)(2,1)S(1)}, bf16[384,768]{1,0:T(8,128)(2,1)S(1)}, u32[]{:S(2)}, u32[]{:S(2)}) collective-permute-start(bf16[384,768]{1,0:T(8,128)(2,1)S(1)} %get-tuple-element.222), channel_id=1, source_target_pairs={{0,48},{16,32},{32,16},{48,0},{1,49},{17,33},{33,17},{49,1},{2,50}... | collective-permute-start | bytes 1769480 | tf_op jit(solution)/shard_map/ppermute | solution.py:23
  95.7 1.4 collective-permute-start.20
  97.8 0.9 collective-permute-start.25
  98.7 8.4 %weight_part.4 = (bf16[768,768]{1,0:T(8,128)(2,1)S(1)}, bf16[768,768]{1,0:T(8,128)(2,1)S(1)}, bf16[768,768]{1,0:T(8,128)(2,1)S(1)}, bf16[768,768]{1,0:T(8,128)(2,1)S(1)}) custom-call(s32[6]{0:T(128)S(1)} %stack.27.s, bf16[4,4,192,512]{3,2,1,0:T(8,128)(2,1)S(1)} %bitcast.21, bf16[4,4,192,512]{3,2,1,0:T(8,128)(2,1)S(1)} %bitcast.22, ...), custom_call_target="tpu_custom_call" | custom-call | flops 1 | bytes 1 | tf_op jit(solution)/shard_map/weight_part/pallas_call | solution.py:35
  108.4 1.8 %collective-permute-start.23 = (bf16[768,768]{1,0:T(8,128)(2,1)S(1)}, bf16[768,768]{1,0:T(8,128)(2,1)S(1)}, u32[]{:S(2)}, u32[]{:S(2)}) collective-permute-start(bf16[768,768]{1,0:T(8,128)(2,1)S(1)} %get-tuple-element.228), channel_id=1, source_target_pairs={{0,48},{16,32},{32,16},{48,0},{1,49},{17,33},{33,17},{49,1},{2,50}... | collective-permute-start | bytes 3538952 | tf_op jit(solution)/shard_map/ppermute | solution.py:23
  111.1 1.5 collective-permute-start.30
  112.7 3.2 %weight_part.5 = (bf16[768,768]{1,0:T(8,128)(2,1)S(1)}, bf16[768,768]{1,0:T(8,128)(2,1)S(1)}) custom-call(s32[6]{0:T(128)S(1)} %stack.27.s, bf16[4,4,192,512]{3,2,1,0:T(8,128)(2,1)S(1)} %bitcast.23, bf16[4,4,192,512]{3,2,1,0:T(8,128)(2,1)S(1)} %bitcast.24, bf16[4,4,192,512]{3,2,1,0:T(8,128)(2,1)S(1)} %bitcast.29, bf16[4,4,192,512]{3,2,1,0:T(8,128)(2,1)S(1)} %bitcast.30, ...), custom_call_target="tpu_custom_call" | custom-call | flops 1 | bytes 1 | tf_op jit(solution)/shard_map/weight_part/pallas_call | solution.py:35
  115.9 18.1 %collective-permute-done.23.c = bf16[768,768]{1,0:T(8,128)(2,1)S(1)} collective-permute-done((bf16[768,768]{1,0:T(8,128)(2,1)S(1)}, bf16[768,768]{1,0:T(8,128)(2,1)S(1)}, u32[]{:S(2)}, u32[]{:S(2)}) %collective-permute-start.23) | collective-permute-done | bytes 1179680 | tf_op jit(solution)/shard_map/ppermute | solution.py:23
  134.0 1.0 cut_blocks.2
  135.0 1.7 %collective-permute-start.26 = (bf16[192,768]{1,0:T(8,128)(2,1)S(1)}, bf16[192,768]{1,0:T(8,128)(2,1)S(1)}, u32[]{:S(2)}, u32[]{:S(2)}) collective-permute-start(bf16[192,768]{1,0:T(8,128)(2,1)S(1)} %get-tuple-element.244), channel_id=1, source_target_pairs={{0,4},{4,0},{8,12},{12,8},{1,5},{5,1},{9,13},{13,9},{2,6},{6,2},{1... | collective-permute-start | bytes 884744 | tf_op jit(solution)/shard_map/ppermute | solution.py:23
  136.7 2.5 %collective-permute-done.29.b = bf16[768,768]{1,0:T(8,128)(2,1)S(1)} collective-permute-done((bf16[768,768]{1,0:T(8,128)(2,1)S(1)}, bf16[768,768]{1,0:T(8,128)(2,1)S(1)}, u32[]{:S(2)}, u32[]{:S(2)}) %collective-permute-start.29) | collective-permute-done | bytes 1179680 | tf_op jit(solution)/shard_map/ppermute | solution.py:23
  139.1 3.3 %collective-permute-start.27 = (bf16[192,768]{1,0:T(8,128)(2,1)S(1)}, bf16[192,768]{1,0:T(8,128)(2,1)S(1)}, u32[]{:S(2)}, u32[]{:S(2)}) collective-permute-start(bf16[192,768]{1,0:T(8,128)(2,1)S(1)} %get-tuple-element.245), channel_id=1, source_target_pairs={{0,12},{4,8},{8,4},{12,0},{1,13},{5,9},{9,5},{13,1},{2,14},{6,10},... | collective-permute-start | bytes 884744 | tf_op jit(solution)/shard_map/ppermute | solution.py:23
  142.7 1.0 cut_blocks.3
  143.7 2.7 %collective-permute-start.32 = (bf16[192,768]{1,0:T(8,128)(2,1)S(1)}, bf16[192,768]{1,0:T(8,128)(2,1)S(1)}, u32[]{:S(2)}, u32[]{:S(2)}) collective-permute-start(bf16[192,768]{1,0:T(8,128)(2,1)S(1)} %get-tuple-element.257), channel_id=1, source_target_pairs={{0,16},{16,0},{32,48},{48,32},{1,17},{17,1},{33,49},{49,33},{2,18}... | collective-permute-start | bytes 884744 | tf_op jit(solution)/shard_map/ppermute | solution.py:23
  146.4 1.5 collective-permute-start.33
  148.5 2.5 %collective-permute-done.27.c = bf16[192,768]{1,0:T(8,128)(2,1)S(1)} collective-permute-done((bf16[192,768]{1,0:T(8,128)(2,1)S(1)}, bf16[192,768]{1,0:T(8,128)(2,1)S(1)}, u32[]{:S(2)}, u32[]{:S(2)}) %collective-permute-start.27) | collective-permute-done | bytes 294944 | tf_op jit(solution)/shard_map/ppermute | solution.py:23
  151.8 5.7 %collective-permute-done.33.c = bf16[192,768]{1,0:T(8,128)(2,1)S(1)} collective-permute-done((bf16[192,768]{1,0:T(8,128)(2,1)S(1)}, bf16[192,768]{1,0:T(8,128)(2,1)S(1)}, u32[]{:S(2)}, u32[]{:S(2)}) %collective-permute-start.33) | collective-permute-done | bytes 294944 | tf_op jit(solution)/shard_map/ppermute | solution.py:23
  158.6 3.2 %collective-permute-start.35 = (bf16[96,768]{1,0:T(8,128)(2,1)S(1)}, bf16[96,768]{1,0:T(8,128)(2,1)S(1)}, u32[]{:S(2)}, u32[]{:S(2)}) collective-permute-start(bf16[96,768]{1,0:T(8,128)(2,1)S(1)} %get-tuple-element.266), channel_id=1, source_target_pairs={{0,64},{64,0},{1,65},{65,1},{2,66},{66,2},{3,67},{67,3},{4,68},{68... | collective-permute-start | bytes 442376 | tf_op jit(solution)/shard_map/ppermute | solution.py:23
  161.8 2.3 %collective-permute-done.31.refs_2_ = bf16[96,768]{1,0:T(8,128)(2,1)S(1)} collective-permute-done((bf16[96,768]{1,0:T(8,128)(2,1)S(1)}, bf16[96,768]{1,0:T(8,128)(2,1)S(1)}, u32[]{:S(2)}, u32[]{:S(2)}) %collective-permute-start.31) | collective-permute-done | bytes 147488 | tf_op jit(solution)/shard_map/ppermute | solution.py:23
  164.1 1.6 collective-permute-done.35.refs_3_
  165.7 2.2 %finish.1 = f32[3,96,1024]{2,1,0:T(8,128)} custom-call(s32[6]{0:T(128)S(1)} %stack.27.s, bf16[96,768]{1,0:T(8,128)(2,1)S(1)} %get-tuple-element.255.refs_0_, bf16[96,768]{1,0:T(8,128)(2,1)S(1)} %get-tuple-element.264.refs_1_, bf16[96,768]{1,0:T(8,128)(2,1)S(1)} %collective-permute-done.31.refs_2_, bf16[96,768]{1,0:T(8,128)(2,1)S(1)} %collective-permute-done.35.refs_3_), custom_call_target="tpu_custom_call" | custom-call | flops 1 | bytes 1 | tf_op jit(solution)/shard_map/finish/pallas_call | solution.py:35
  (62 shorter events, 13.7 us)
Async XLA Ops:
  0.0 10.0 %collective-permute-start.2 = (bf16[512,768]{1,0:T(8,128)(2,1)}, bf16[512,768]{1,0:T(8,128)(2,1)}, u32[]{:S(2)}, u32[]{:S(2)}) collective-permute-start(bf16[512,768]{1,0:T(8,128)(2,1)} %refs_0_.2), channel_id=1, source_target_pairs={{0,1},{1,0},{2,3},{3,2},{4,5},{5,4},{6,7},{7,6},{8,9},{9,8},{10,11... | collective-permute-start | bytes 2359304 | tf_op jit(solution)/shard_map/ppermute | solution.py:23
  0.0 24.1 %collective-permute-start.1 = (bf16[512,768]{1,0:T(8,128)(2,1)}, bf16[512,768]{1,0:T(8,128)(2,1)S(1)}, u32[]{:S(2)}, u32[]{:S(2)}) collective-permute-start(bf16[512,768]{1,0:T(8,128)(2,1)} %refs_0_.2), channel_id=1, source_target_pairs={{0,66},{2,64},{64,2},{66,0},{1,67},{3,65},{65,3},{67,1},{4,70},{6,... | collective-permute-start | bytes 2359304 | tf_op jit(solution)/shard_map/ppermute | solution.py:27
  4.1 20.1 %collective-permute-start = (bf16[512,768]{1,0:T(8,128)(2,1)}, bf16[512,768]{1,0:T(8,128)(2,1)S(1)}, u32[]{:S(2)}, u32[]{:S(2)}) collective-permute-start(bf16[512,768]{1,0:T(8,128)(2,1)} %refs_0_.2), channel_id=1, source_target_pairs={{0,2},{2,0},{1,3},{3,1},{4,6},{6,4},{5,7},{7,5},{8,10},{10,8},{9,1... | collective-permute-start | bytes 2359304 | tf_op jit(solution)/shard_map/ppermute | solution.py:23
  5.5 4.5 %copy-start = (bf16[512,768]{1,0:T(8,128)(2,1)S(1)}, bf16[512,768]{1,0:T(8,128)(2,1)}, u32[]{:S(2)}) copy-start(bf16[512,768]{1,0:T(8,128)(2,1)} %refs_0_.2) | copy-start | bytes 2359300
  7.0 17.1 %collective-permute-start.3 = (f32[8,512]{1,0:T(8,128)S(1)}, f32[8,512]{1,0:T(8,128)S(1)}, u32[]{:S(2)}, u32[]{:S(2)}) collective-permute-start(f32[8,512]{1,0:T(8,128)S(1)} %concatenate.6), channel_id=1, source_target_pairs={{0,64},{64,0},{1,65},{65,1},{2,66},{66,2},{3,67},{67,3},{4,68},{68... | collective-permute-start | bytes 49160 | tf_op jit(solution)/shard_map/ppermute | solution.py:23
  24.2 4.1 %collective-permute-start.7 = (bf16[512,768]{1,0:T(8,128)(2,1)S(1)}, bf16[512,768]{1,0:T(8,128)(2,1)S(1)}, u32[]{:S(2)}, u32[]{:S(2)}) collective-permute-start(bf16[512,768]{1,0:T(8,128)(2,1)S(1)} %collective-permute-done.b.refs_0_.refs_2_), channel_id=1, source_target_pairs={{0,1},{1,0},{2,3},{3,2},{4,5},{5,4},{6,7},{7,6},{8,9},{9,8},{10,11... | collective-permute-start | bytes 2359304 | tf_op jit(solution)/shard_map/ppermute | solution.py:23
  24.2 13.5 %collective-permute-start.6 = (bf16[512,768]{1,0:T(8,128)(2,1)S(1)}, bf16[512,768]{1,0:T(8,128)(2,1)S(1)}, u32[]{:S(2)}, u32[]{:S(2)}) collective-permute-start(bf16[512,768]{1,0:T(8,128)(2,1)S(1)} %collective-permute-done.1.a.refs_0_.refs_4_), channel_id=1, source_target_pairs={{0,1},{1,0},{2,3},{3,2},{4,5},{5,4},{6,7},{7,6},{8,9},{9,8},{10,11... | collective-permute-start | bytes 2359304 | tf_op jit(solution)/shard_map/ppermute | solution.py:23
  25.3 11.5 %collective-permute-start.4 = (bf16[256,768]{1,0:T(8,128)(2,1)S(1)}, bf16[256,768]{1,0:T(8,128)(2,1)S(1)}, u32[]{:S(2)}, u32[]{:S(2)}) collective-permute-start(bf16[256,768]{1,0:T(8,128)(2,1)S(1)} %get-tuple-element.139), channel_id=1, source_target_pairs={{0,2},{2,0},{1,3},{3,1},{4,6},{6,4},{5,7},{7,5},{8,10},{10,8},{9,1... | collective-permute-start | bytes 1179656 | tf_op jit(solution)/shard_map/ppermute | solution.py:23
  25.7 12.0 %collective-permute-start.5 = (bf16[256,768]{1,0:T(8,128)(2,1)S(1)}, bf16[256,768]{1,0:T(8,128)(2,1)S(1)}, u32[]{:S(2)}, u32[]{:S(2)}) collective-permute-start(bf16[256,768]{1,0:T(8,128)(2,1)S(1)} %get-tuple-element.140), channel_id=1, source_target_pairs={{0,66},{2,64},{64,2},{66,0},{1,67},{3,65},{65,3},{67,1},{4,70},{6,... | collective-permute-start | bytes 1179656 | tf_op jit(solution)/shard_map/ppermute | solution.py:27
  37.7 14.4 %collective-permute-start.8 = (bf16[512,512]{1,0:T(8,128)(2,1)S(1)}, bf16[512,512]{1,0:T(8,128)(2,1)S(1)}, u32[]{:S(2)}, u32[]{:S(2)}) collective-permute-start(bf16[512,512]{1,0:T(8,128)(2,1)S(1)} %get-tuple-element.149), channel_id=1, source_target_pairs={{0,64},{64,0},{1,65},{65,1},{2,66},{66,2},{3,67},{67,3},{4,68},{68... | collective-permute-start | bytes 1572872 | tf_op jit(solution)/shard_map/ppermute | solution.py:23
  40.5 2.8 %collective-permute-start.9 = (bf16[256,768]{1,0:T(8,128)(2,1)S(1)}, bf16[256,768]{1,0:T(8,128)(2,1)S(1)}, u32[]{:S(2)}, u32[]{:S(2)}) collective-permute-start(bf16[256,768]{1,0:T(8,128)(2,1)S(1)} %collective-permute-done.4.refs_2_.refs_0_), channel_id=1, source_target_pairs={{0,1},{1,0},{2,3},{3,2},{4,5},{5,4},{6,7},{7,6},{8,9},{9,8},{10,11... | collective-permute-start | bytes 1179656 | tf_op jit(solution)/shard_map/ppermute | solution.py:23
  40.5 2.8 %collective-permute-start.10 = (bf16[256,768]{1,0:T(8,128)(2,1)S(1)}, bf16[256,768]{1,0:T(8,128)(2,1)S(1)}, u32[]{:S(2)}, u32[]{:S(2)}) collective-permute-start(bf16[256,768]{1,0:T(8,128)(2,1)S(1)} %collective-permute-done.5.refs_3_.refs_1_), channel_id=1, source_target_pairs={{0,1},{1,0},{2,3},{3,2},{4,5},{5,4},{6,7},{7,6},{8,9},{9,8},{10,11... | collective-permute-start | bytes 1179656 | tf_op jit(solution)/shard_map/ppermute | solution.py:23
  54.4 10.4 %collective-permute-start.11 = (bf16[528,128]{1,0:T(8,128)(2,1)S(1)}, bf16[528,128]{1,0:T(8,128)(2,1)S(1)}, u32[]{:S(2)}, u32[]{:S(2)}) collective-permute-start(bf16[528,128]{1,0:T(8,128)(2,1)S(1)} %get-tuple-element.166), channel_id=1, source_target_pairs={{0,4},{4,0},{8,12},{12,8},{1,5},{5,1},{9,13},{13,9},{2,6},{6,2},{1... | collective-permute-start | bytes 405512 | tf_op jit(solution)/shard_map/ppermute | solution.py:23
  56.0 9.1 %collective-permute-start.12 = (bf16[528,128]{1,0:T(8,128)(2,1)S(1)}, bf16[528,128]{1,0:T(8,128)(2,1)S(1)}, u32[]{:S(2)}, u32[]{:S(2)}) collective-permute-start(bf16[528,128]{1,0:T(8,128)(2,1)S(1)} %get-tuple-element.167), channel_id=1, source_target_pairs={{0,12},{4,8},{8,4},{12,0},{1,13},{5,9},{9,5},{13,1},{2,14},{6,10},... | collective-permute-start | bytes 405512 | tf_op jit(solution)/shard_map/ppermute | solution.py:23
  58.2 6.9 %collective-permute-start.13 = (bf16[528,128]{1,0:T(8,128)(2,1)S(1)}, bf16[528,128]{1,0:T(8,128)(2,1)S(1)}, u32[]{:S(2)}, u32[]{:S(2)}) collective-permute-start(bf16[528,128]{1,0:T(8,128)(2,1)S(1)} %get-tuple-element.168), channel_id=1, source_target_pairs={{0,8},{4,12},{8,0},{12,4},{1,9},{5,13},{9,1},{13,5},{2,10},{6,14},... | collective-permute-start | bytes 405512 | tf_op jit(solution)/shard_map/ppermute | solution.py:23
  65.9 9.5 %collective-permute-start.16 = (bf16[528,128]{1,0:T(8,128)(2,1)S(1)}, bf16[528,128]{1,0:T(8,128)(2,1)S(1)}, u32[]{:S(2)}, u32[]{:S(2)}) collective-permute-start(bf16[528,128]{1,0:T(8,128)(2,1)S(1)} %get-tuple-element.175.a), channel_id=1, source_target_pairs={{0,32},{16,48},{32,0},{48,16},{1,33},{17,49},{33,1},{49,17},{2,34}... | collective-permute-start | bytes 405512 | tf_op jit(solution)/shard_map/ppermute | solution.py:23
  69.0 6.4 %collective-permute-start.15 = (bf16[528,128]{1,0:T(8,128)(2,1)S(1)}, bf16[528,128]{1,0:T(8,128)(2,1)S(1)}, u32[]{:S(2)}, u32[]{:S(2)}) collective-permute-start(bf16[528,128]{1,0:T(8,128)(2,1)S(1)} %get-tuple-element.175.a), channel_id=1, source_target_pairs={{0,48},{16,32},{32,16},{48,0},{1,49},{17,33},{33,17},{49,1},{2,50}... | collective-permute-start | bytes 405512 | tf_op jit(solution)/shard_map/ppermute | solution.py:23
  70.1 5.3 %collective-permute-start.14 = (bf16[528,128]{1,0:T(8,128)(2,1)S(1)}, bf16[528,128]{1,0:T(8,128)(2,1)S(1)}, u32[]{:S(2)}, u32[]{:S(2)}) collective-permute-start(bf16[528,128]{1,0:T(8,128)(2,1)S(1)} %get-tuple-element.175.a), channel_id=1, source_target_pairs={{0,16},{16,0},{32,48},{48,32},{1,17},{17,1},{33,49},{49,33},{2,18}... | collective-permute-start | bytes 405512 | tf_op jit(solution)/shard_map/ppermute | solution.py:23
  76.3 7.4 %collective-permute-start.17 = (bf16[512,128]{1,0:T(8,128)(2,1)S(1)}, bf16[512,128]{1,0:T(8,128)(2,1)S(1)}, u32[]{:S(2)}, u32[]{:S(2)}) collective-permute-start(bf16[512,128]{1,0:T(8,128)(2,1)S(1)} %get-tuple-element.193), channel_id=1, source_target_pairs={{0,4},{4,0},{8,12},{12,8},{1,5},{5,1},{9,13},{13,9},{2,6},{6,2},{1... | collective-permute-start | bytes 393224 | tf_op jit(solution)/shard_map/ppermute | solution.py:23
  77.3 6.9 %collective-permute-start.18 = (bf16[512,128]{1,0:T(8,128)(2,1)S(1)}, bf16[512,128]{1,0:T(8,128)(2,1)S(1)}, u32[]{:S(2)}, u32[]{:S(2)}) collective-permute-start(bf16[512,128]{1,0:T(8,128)(2,1)S(1)} %get-tuple-element.194), channel_id=1, source_target_pairs={{0,12},{4,8},{8,4},{12,0},{1,13},{5,9},{9,5},{13,1},{2,14},{6,10},... | collective-permute-start | bytes 393224 | tf_op jit(solution)/shard_map/ppermute | solution.py:23
  79.4 6.5 %collective-permute-start.19 = (bf16[512,128]{1,0:T(8,128)(2,1)S(1)}, bf16[512,128]{1,0:T(8,128)(2,1)S(1)}, u32[]{:S(2)}, u32[]{:S(2)}) collective-permute-start(bf16[512,128]{1,0:T(8,128)(2,1)S(1)} %get-tuple-element.195), channel_id=1, source_target_pairs={{0,8},{4,12},{8,0},{12,4},{1,9},{5,13},{9,1},{13,5},{2,10},{6,14},... | collective-permute-start | bytes 393224 | tf_op jit(solution)/shard_map/ppermute | solution.py:23
  93.5 13.9 %collective-permute-start.21 = (bf16[384,768]{1,0:T(8,128)(2,1)S(1)}, bf16[384,768]{1,0:T(8,128)(2,1)S(1)}, u32[]{:S(2)}, u32[]{:S(2)}) collective-permute-start(bf16[384,768]{1,0:T(8,128)(2,1)S(1)} %get-tuple-element.222), channel_id=1, source_target_pairs={{0,48},{16,32},{32,16},{48,0},{1,49},{17,33},{33,17},{49,1},{2,50}... | collective-permute-start | bytes 1769480 | tf_op jit(solution)/shard_map/ppermute | solution.py:23
  95.7 11.7 %collective-permute-start.20 = (bf16[384,768]{1,0:T(8,128)(2,1)S(1)}, bf16[384,768]{1,0:T(8,128)(2,1)S(1)}, u32[]{:S(2)}, u32[]{:S(2)}) collective-permute-start(bf16[384,768]{1,0:T(8,128)(2,1)S(1)} %get-tuple-element.218), channel_id=1, source_target_pairs={{0,16},{16,0},{32,48},{48,32},{1,17},{17,1},{33,49},{49,33},{2,18}... | collective-permute-start | bytes 1769480 | tf_op jit(solution)/shard_map/ppermute | solution.py:23
  97.1 13.1 %collective-permute-start.24 = (bf16[384,768]{1,0:T(8,128)(2,1)S(1)}, bf16[384,768]{1,0:T(8,128)(2,1)S(1)}, u32[]{:S(2)}, u32[]{:S(2)}) collective-permute-start(bf16[384,768]{1,0:T(8,128)(2,1)S(1)} %get-tuple-element.231), channel_id=1, source_target_pairs={{0,4},{4,0},{8,12},{12,8},{1,5},{5,1},{9,13},{13,9},{2,6},{6,2},{1... | collective-permute-start | bytes 1769480 | tf_op jit(solution)/shard_map/ppermute | solution.py:23
  97.8 12.4 %collective-permute-start.25 = (bf16[384,768]{1,0:T(8,128)(2,1)S(1)}, bf16[384,768]{1,0:T(8,128)(2,1)S(1)}, u32[]{:S(2)}, u32[]{:S(2)}) collective-permute-start(bf16[384,768]{1,0:T(8,128)(2,1)S(1)} %get-tuple-element.232), channel_id=1, source_target_pairs={{0,12},{4,8},{8,4},{12,0},{1,13},{5,9},{9,5},{13,1},{2,14},{6,10},... | collective-permute-start | bytes 1769480 | tf_op jit(solution)/shard_map/ppermute | solution.py:23
  108.4 25.6 %collective-permute-start.23 = (bf16[768,768]{1,0:T(8,128)(2,1)S(1)}, bf16[768,768]{1,0:T(8,128)(2,1)S(1)}, u32[]{:S(2)}, u32[]{:S(2)}) collective-permute-start(bf16[768,768]{1,0:T(8,128)(2,1)S(1)} %get-tuple-element.228), channel_id=1, source_target_pairs={{0,48},{16,32},{32,16},{48,0},{1,49},{17,33},{33,17},{49,1},{2,50}... | collective-permute-start | bytes 3538952 | tf_op jit(solution)/shard_map/ppermute | solution.py:23
  110.2 23.8 %collective-permute-start.22 = (bf16[768,768]{1,0:T(8,128)(2,1)S(1)}, bf16[768,768]{1,0:T(8,128)(2,1)S(1)}, u32[]{:S(2)}, u32[]{:S(2)}) collective-permute-start(bf16[768,768]{1,0:T(8,128)(2,1)S(1)} %get-tuple-element.227), channel_id=1, source_target_pairs={{0,16},{16,0},{32,48},{48,32},{1,17},{17,1},{33,49},{49,33},{2,18}... | collective-permute-start | bytes 3538952 | tf_op jit(solution)/shard_map/ppermute | solution.py:23
  111.1 25.6 %collective-permute-start.30 = (bf16[768,768]{1,0:T(8,128)(2,1)S(1)}, bf16[768,768]{1,0:T(8,128)(2,1)S(1)}, u32[]{:S(2)}, u32[]{:S(2)}) collective-permute-start(bf16[768,768]{1,0:T(8,128)(2,1)S(1)} %get-tuple-element.248), channel_id=1, source_target_pairs={{0,12},{4,8},{8,4},{12,0},{1,13},{5,9},{9,5},{13,1},{2,14},{6,10},... | collective-permute-start | bytes 3538952 | tf_op jit(solution)/shard_map/ppermute | solution.py:23
  112.6 26.5 %collective-permute-start.29 = (bf16[768,768]{1,0:T(8,128)(2,1)S(1)}, bf16[768,768]{1,0:T(8,128)(2,1)S(1)}, u32[]{:S(2)}, u32[]{:S(2)}) collective-permute-start(bf16[768,768]{1,0:T(8,128)(2,1)S(1)} %get-tuple-element.235), channel_id=1, source_target_pairs={{0,4},{4,0},{8,12},{12,8},{1,5},{5,1},{9,13},{13,9},{2,6},{6,2},{1... | collective-permute-start | bytes 3538952 | tf_op jit(solution)/shard_map/ppermute | solution.py:23
  135.0 12.9 %collective-permute-start.26 = (bf16[192,768]{1,0:T(8,128)(2,1)S(1)}, bf16[192,768]{1,0:T(8,128)(2,1)S(1)}, u32[]{:S(2)}, u32[]{:S(2)}) collective-permute-start(bf16[192,768]{1,0:T(8,128)(2,1)S(1)} %get-tuple-element.244), channel_id=1, source_target_pairs={{0,4},{4,0},{8,12},{12,8},{1,5},{5,1},{9,13},{13,9},{2,6},{6,2},{1... | collective-permute-start | bytes 884744 | tf_op jit(solution)/shard_map/ppermute | solution.py:23
  139.1 11.9 %collective-permute-start.27 = (bf16[192,768]{1,0:T(8,128)(2,1)S(1)}, bf16[192,768]{1,0:T(8,128)(2,1)S(1)}, u32[]{:S(2)}, u32[]{:S(2)}) collective-permute-start(bf16[192,768]{1,0:T(8,128)(2,1)S(1)} %get-tuple-element.245), channel_id=1, source_target_pairs={{0,12},{4,8},{8,4},{12,0},{1,13},{5,9},{9,5},{13,1},{2,14},{6,10},... | collective-permute-start | bytes 884744 | tf_op jit(solution)/shard_map/ppermute | solution.py:23
  142.4 8.7 %collective-permute-start.28 = (bf16[192,768]{1,0:T(8,128)(2,1)S(1)}, bf16[192,768]{1,0:T(8,128)(2,1)S(1)}, u32[]{:S(2)}, u32[]{:S(2)}) collective-permute-start(bf16[192,768]{1,0:T(8,128)(2,1)S(1)} %get-tuple-element.246), channel_id=1, source_target_pairs={{0,8},{4,12},{8,0},{12,4},{1,9},{5,13},{9,1},{13,5},{2,10},{6,14},... | collective-permute-start | bytes 884744 | tf_op jit(solution)/shard_map/ppermute | solution.py:23
  143.7 8.1 %collective-permute-start.32 = (bf16[192,768]{1,0:T(8,128)(2,1)S(1)}, bf16[192,768]{1,0:T(8,128)(2,1)S(1)}, u32[]{:S(2)}, u32[]{:S(2)}) collective-permute-start(bf16[192,768]{1,0:T(8,128)(2,1)S(1)} %get-tuple-element.257), channel_id=1, source_target_pairs={{0,16},{16,0},{32,48},{48,32},{1,17},{17,1},{33,49},{49,33},{2,18}... | collective-permute-start | bytes 884744 | tf_op jit(solution)/shard_map/ppermute | solution.py:23
  146.4 11.1 %collective-permute-start.33 = (bf16[192,768]{1,0:T(8,128)(2,1)S(1)}, bf16[192,768]{1,0:T(8,128)(2,1)S(1)}, u32[]{:S(2)}, u32[]{:S(2)}) collective-permute-start(bf16[192,768]{1,0:T(8,128)(2,1)S(1)} %get-tuple-element.258), channel_id=1, source_target_pairs={{0,48},{16,32},{32,16},{48,0},{1,49},{17,33},{33,17},{49,1},{2,50}... | collective-permute-start | bytes 884744 | tf_op jit(solution)/shard_map/ppermute | solution.py:23
  147.9 9.6 %collective-permute-start.34 = (bf16[192,768]{1,0:T(8,128)(2,1)S(1)}, bf16[192,768]{1,0:T(8,128)(2,1)S(1)}, u32[]{:S(2)}, u32[]{:S(2)}) collective-permute-start(bf16[192,768]{1,0:T(8,128)(2,1)S(1)} %get-tuple-element.259), channel_id=1, source_target_pairs={{0,32},{16,48},{32,0},{48,16},{1,33},{17,49},{33,1},{49,17},{2,34}... | collective-permute-start | bytes 884744 | tf_op jit(solution)/shard_map/ppermute | solution.py:23
  157.5 6.6 %collective-permute-start.31 = (bf16[96,768]{1,0:T(8,128)(2,1)S(1)}, bf16[96,768]{1,0:T(8,128)(2,1)S(1)}, u32[]{:S(2)}, u32[]{:S(2)}) collective-permute-start(bf16[96,768]{1,0:T(8,128)(2,1)S(1)} %get-tuple-element.256), channel_id=1, source_target_pairs={{0,64},{64,0},{1,65},{65,1},{2,66},{66,2},{3,67},{67,3},{4,68},{68... | collective-permute-start | bytes 442376 | tf_op jit(solution)/shard_map/ppermute | solution.py:23
  158.6 7.1 %collective-permute-start.35 = (bf16[96,768]{1,0:T(8,128)(2,1)S(1)}, bf16[96,768]{1,0:T(8,128)(2,1)S(1)}, u32[]{:S(2)}, u32[]{:S(2)}) collective-permute-start(bf16[96,768]{1,0:T(8,128)(2,1)S(1)} %get-tuple-element.266), channel_id=1, source_target_pairs={{0,64},{64,0},{1,65},{65,1},{2,66},{66,2},{3,67},{67,3},{4,68},{68... | collective-permute-start | bytes 442376 | tf_op jit(solution)/shard_map/ppermute | solution.py:23

commit v11 on v8

--- a/solution.py
+++ b/solution.py
@@ -471,13 +471,14 @@
         out_a[...] = (a[...].astype(F32) + u[...].astype(F32)).astype(BF16)
         out_b[...] = (b[...].astype(F32) + d[...].astype(F32)).astype(BF16)
 
-    first = pl.BlockSpec((n, cols), lambda i, s: (0, 0))
-    second = pl.BlockSpec((n, cols), lambda i, s: (1, 0))
+    steps = 4
+    first = pl.BlockSpec((n // steps, cols), lambda i, s: (i, 0))
+    second = pl.BlockSpec((n // steps, cols), lambda i, s: (i + steps, 0))
     return call(
         "add_halves",
         body,
         table,
-        (1,),
+        (steps,),
         (near_up, near_down, up, down),
         [first, second, first, first],
         [shape(near_up.shape), shape(near_down.shape)],
@@ -597,12 +598,12 @@
     far, side_core, qkv_own, turned = tied((far, side_core, qkv_own, turned))
     far_core = [send(x, "co", 1) for x in far]
     og_pair = send(tied((og_other, far))[0], "c0", 1)
+    to_y = shard_states(table, qkv_own, og_own, info, 0, None)
+    far_core, to_y = tied((far_core, to_y))
     qkv_pair = project(
         table, [[side], [side_core], far, far_core], (2, 3, 0, 1), weight, None, note
     )
-    qkv_own, _ = tied((qkv_own, qkv_pair))
-    to_y = shard_states(table, qkv_own, og_own, info, 0, None)
-    og_pair, qkv_pair, to_y = tied((og_pair, qkv_pair, to_y))
+    og_pair, qkv_pair = tied((og_pair, qkv_pair))
 
     to_y = shard_states(table, qkv_pair, og_pair, note, 1, to_y)
     at_y = [send(to_y[r], "c2", r) for r in (1, 3, 2)]

time: 168 us -> 165 us (0.982)
  waiting for transfers between devices: 50.1 us -> 45.4 us
  starting transfers between devices: 43.8 us -> 46.1 us
    ppermute x34, waiting for transfers between devices: 49.2 us -> 44.5 us  [send(): lax.ppermute(x, axis, [(i, i ^ by) for i in range(lax.axis_size(axis))])]
    ppermute x34, starting transfers between devices: 37.1 us -> 39.4 us  [send(): lax.ppermute(x, axis, [(i, i ^ by) for i in range(lax.axis_size(axis))])]
  transfers between devices with their start and end apart: 36 -> 36, of which waited for: 20 -> 16; matrix products, arithmetic and copies ran while one was open for 2% -> 2% of each run, Pallas kernels for 33% -> 33%
where the time goes in v11:
time: 165 us; the launch traced here: 164 us
  Pallas kernels  68.4 us (41%)
  starting transfers between devices  46.1 us (28%)
  waiting for transfers between devices  45.4 us (28%)
  other arithmetic  1.96 us (1%)
    pallas_call x23, Pallas kernels, call(): pl.pallas_call(body, grid_spec=pltpu.PrefetchScalarGridSpec(num_scalar_pr...  68.4 us
    ppermute x34, waiting for transfers between devices, send(): lax.ppermute(x, axis, [(i, i ^ by) for i in range(lax.axis_size(axis))])  44.5 us
    ppermute x34, starting transfers between devices, send(): lax.ppermute(x, axis, [(i, i ^ by) for i in range(lax.axis_size(axis))])  39.4 us
    ppermute x2, starting transfers between devices, across(): return lax.ppermute(x, ('c0', 'zl'), [(0, 3), (1, 2), (2, 1), (3, 0)])  6.75 us
  transfers between devices with their start and end apart: 36, of which 16 were waited for; matrix products, arithmetic and copies ran while one was open for 2% of the time, Pallas kernels for 33%

profile of v11, /device:TPU:0, one launch (start us, length us, event | category | flops | bytes accessed | tf_op | source)
XLA Modules:
  0.0 164.4 jit_solution(18180783808178607436)
XLA Ops:
  0.0 4.1 %collective-permute-start.1 = (bf16[512,768]{1,0:T(8,128)(2,1)}, bf16[512,768]{1,0:T(8,128)(2,1)S(1)}, u32[]{:S(2)}, u32[]{:S(2)}) collective-permute-start(bf16[512,768]{1,0:T(8,128)(2,1)} %refs_0_.2), channel_id=1, source_target_pairs={{0,66},{2,64},{64,2},{66,0},{1,67},{3,65},{65,3},{67,1},{4,70},{6,... | collective-permute-start | bytes 2359304 | tf_op jit(solution)/shard_map/ppermute | solution.py:27
  5.5 1.1 reduce-window.6
  7.0 1.6 collective-permute-start.3
  8.6 1.3 constant_dynamic-slice_fusion
  10.0 5.5 %project.3.refs_4_ = f32[3,512,512]{2,1,0:T(8,128)S(1)} custom-call(s32[6]{0:T(128)S(1)} %stack.27.s, bf16[512,768]{1,0:T(8,128)(2,1)S(1)} %copy-done, bf16[512,768]{1,0:T(8,128)(2,1)} %collective-permute-done.2.refs_1_, bf16[3,3072,1024]{2,1,0:T(8,128)(2,1)} %bitcast.31, bf16[3,3072,1024]{2,1,0:T(8,128)(2,1)} %bitcast.32), custom_call_target="tpu_custom_call" | custom-call | flops 1 | bytes 1 | tf_op jit(solution)/shard_map/project/pallas_call | solution.py:35
  15.5 8.6 %collective-permute-done.3.refs_10_.cum_ref = f32[8,512]{1,0:T(8,128)S(1)} collective-permute-done((f32[8,512]{1,0:T(8,128)S(1)}, f32[8,512]{1,0:T(8,128)S(1)}, u32[]{:S(2)}, u32[]{:S(2)}) %collective-permute-start.3) | collective-permute-done | bytes 16416 | tf_op jit(solution)/shard_map/ppermute | solution.py:23
  25.7 2.6 %collective-permute-start.5 = (bf16[256,768]{1,0:T(8,128)(2,1)S(1)}, bf16[256,768]{1,0:T(8,128)(2,1)S(1)}, u32[]{:S(2)}, u32[]{:S(2)}) collective-permute-start(bf16[256,768]{1,0:T(8,128)(2,1)S(1)} %get-tuple-element.133), channel_id=1, source_target_pairs={{0,66},{2,64},{64,2},{66,0},{1,67},{3,65},{65,3},{67,1},{4,70},{6,... | collective-permute-start | bytes 1179656 | tf_op jit(solution)/shard_map/ppermute | solution.py:27
  28.3 5.3 %project.4.qkv_ref = bf16[3,512,512]{2,1,0:T(8,128)(2,1)S(1)} custom-call(s32[6]{0:T(128)S(1)} %stack.27.s, bf16[512,768]{1,0:T(8,128)(2,1)S(1)} %collective-permute-done.b.refs_0_.refs_2_, bf16[512,768]{1,0:T(8,128)(2,1)S(1)} %collective-permute-done.7.refs_1_.refs_3_, bf16[3,3072,1024]{2,1,0:T(8,128)(2,1)} %bitcast.33, bf16[3,3072,1024]{2,1,0:T(8,128)(2,1)} %bitcast.34, ...), custom_call_target="tpu_custom_call" | custom-call | flops 1 | bytes 1 | tf_op jit(solution)/shard_map/project/pallas_call | solution.py:35
  33.6 3.2 %turn.2 = bf16[16,2,96,512]{3,2,1,0:T(8,128)(2,1)S(1)} custom-call(s32[6]{0:T(128)S(1)} %stack.27.s, bf16[512,768]{1,0:T(8,128)(2,1)S(1)} %copy-done, bf16[512,768]{1,0:T(8,128)(2,1)} %collective-permute-done.2.refs_1_, bf16[512,768]{1,0:T(8,128)(2,1)S(1)} %collective-permute-done.b.refs_0_.refs_2_, bf16[512,768]{1,0:T(8,128)(2,1)S(1)} %collective-permute-done.7.refs_1_.refs_3_), custom_call_target="tpu_custom_call" | custom-call | flops 1 | bytes 1 | tf_op jit(solution)/shard_map/turn/pallas_call | solution.py:35
  37.7 2.8 %collective-permute-start.8 = (bf16[512,512]{1,0:T(8,128)(2,1)S(1)}, bf16[512,512]{1,0:T(8,128)(2,1)S(1)}, u32[]{:S(2)}, u32[]{:S(2)}) collective-permute-start(bf16[512,512]{1,0:T(8,128)(2,1)S(1)} %get-tuple-element.142), channel_id=1, source_target_pairs={{0,64},{64,0},{1,65},{65,1},{2,66},{66,2},{3,67},{67,3},{4,68},{68... | collective-permute-start | bytes 1572872 | tf_op jit(solution)/shard_map/ppermute | solution.py:23
  41.0 2.3 %shard_states.2 = (bf16[528,128]{1,0:T(8,128)(2,1)S(1)}, bf16[528,128]{1,0:T(8,128)(2,1)S(1)}, bf16[528,128]{1,0:T(8,128)(2,1)S(1)}, bf16[528,128]{1,0:T(8,128)(2,1)S(1)}) custom-call(s32[6]{0:T(128)S(1)} %stack.27.s, bf16[3,512,512]{2,1,0:T(8,128)(2,1)S(1)} %project.4.qkv_ref, bf16[512,512]{1,0:T(8,128)(2,1)S(1)} %get-tuple-element.253.og_ref, ...), custom_call_target="tpu_custom_call" | custom-call | flops 1 | bytes 1 | tf_op jit(solution)/shard_map/shard_states/pallas_call | solution.py:35
  43.4 7.9 %project.5.qkv_ref = bf16[3,512,512]{2,1,0:T(8,128)(2,1)S(1)} custom-call(s32[6]{0:T(128)S(1)} %stack.27.s, bf16[512,768]{1,0:T(8,128)(2,1)S(1)} %collective-permute-done.1.a.refs_0_.refs_4_, bf16[512,768]{1,0:T(8,128)(2,1)S(1)} %collective-permute-done.6.refs_1_.refs_5_, bf16[256,768]{1,0:T(8,128)(2,1)S(1)} %collective-permute-done.4.refs_2_.refs_0_, ...), custom_call_target="tpu_custom_call" | custom-call | flops 1 | bytes 1 | tf_op jit(solution)/shard_map/project/pallas_call | solution.py:35
  52.1 2.3 %shard_states.3 = (bf16[528,128]{1,0:T(8,128)(2,1)S(1)}, bf16[528,128]{1,0:T(8,128)(2,1)S(1)}, bf16[528,128]{1,0:T(8,128)(2,1)S(1)}, bf16[528,128]{1,0:T(8,128)(2,1)S(1)}) custom-call(s32[6]{0:T(128)S(1)} %stack.27.s, bf16[3,512,512]{2,1,0:T(8,128)(2,1)S(1)} %project.5.qkv_ref, bf16[512,512]{1,0:T(8,128)(2,1)S(1)} %collective-permute-done.8.og_ref, ...), custom_call_target="tpu_custom_call" | custom-call | flops 1 | bytes 1 | tf_op jit(solution)/shard_map/shard_states/pallas_call | solution.py:35
  54.4 1.7 %collective-permute-start.11 = (bf16[528,128]{1,0:T(8,128)(2,1)S(1)}, bf16[528,128]{1,0:T(8,128)(2,1)S(1)}, u32[]{:S(2)}, u32[]{:S(2)}) collective-permute-start(bf16[528,128]{1,0:T(8,128)(2,1)S(1)} %get-tuple-element.159), channel_id=1, source_target_pairs={{0,4},{4,0},{8,12},{12,8},{1,5},{5,1},{9,13},{13,9},{2,6},{6,2},{1... | collective-permute-start | bytes 405512 | tf_op jit(solution)/shard_map/ppermute | solution.py:23
  56.0 2.2 %collective-permute-start.12 = (bf16[528,128]{1,0:T(8,128)(2,1)S(1)}, bf16[528,128]{1,0:T(8,128)(2,1)S(1)}, u32[]{:S(2)}, u32[]{:S(2)}) collective-permute-start(bf16[528,128]{1,0:T(8,128)(2,1)S(1)} %get-tuple-element.160), channel_id=1, source_target_pairs={{0,12},{4,8},{8,4},{12,0},{1,13},{5,9},{9,5},{13,1},{2,14},{6,10},... | collective-permute-start | bytes 405512 | tf_op jit(solution)/shard_map/ppermute | solution.py:23
  59.0 5.9 %local_grads.3 = (bf16[3,512,512]{2,1,0:T(8,128)(2,1)S(1)}, bf16[3,512,512]{2,1,0:T(8,128)(2,1)S(1)}) custom-call(s32[6]{0:T(128)S(1)} %stack.27.s, bf16[3,512,512]{2,1,0:T(8,128)(2,1)S(1)} %project.4.qkv_ref, bf16[512,512]{1,0:T(8,128)(2,1)S(1)} %get-tuple-element.253.og_ref, f32[8,512]{1,0:T(8,128)S(1)} %concatenate.7.refs_5_.cum_ref), custom_call_target="tpu_custom_call" | custom-call | flops 1 | bytes 1 | tf_op jit(solution)/shard_map/local_grads/pallas_call | solution.py:35
  65.9 3.1 %collective-permute-start.16 = (bf16[528,128]{1,0:T(8,128)(2,1)S(1)}, bf16[528,128]{1,0:T(8,128)(2,1)S(1)}, u32[]{:S(2)}, u32[]{:S(2)}) collective-permute-start(bf16[528,128]{1,0:T(8,128)(2,1)S(1)} %get-tuple-element.168.a), channel_id=1, source_target_pairs={{0,32},{16,48},{32,0},{48,16},{1,33},{17,49},{33,1},{49,17},{2,34}... | collective-permute-start | bytes 405512 | tf_op jit(solution)/shard_map/ppermute | solution.py:23
  69.0 1.1 collective-permute-start.15
  70.1 3.2 %local_grads.4 = (bf16[3,512,512]{2,1,0:T(8,128)(2,1)S(1)}, bf16[3,512,512]{2,1,0:T(8,128)(2,1)S(1)}) custom-call(s32[6]{0:T(128)S(1)} %stack.27.s, bf16[3,512,512]{2,1,0:T(8,128)(2,1)S(1)} %project.5.qkv_ref, bf16[512,512]{1,0:T(8,128)(2,1)S(1)} %collective-permute-done.8.og_ref, f32[8,512]{1,0:T(8,128)S(1)} %collective-permute-done.3.refs_10_.cum_ref), custom_call_target="tpu_custom_call" | custom-call | flops 1 | bytes 1 | tf_op jit(solution)/shard_map/local_grads/pallas_call | solution.py:35
  73.4 2.0 %turn.3 = bf16[16,2,96,512]{3,2,1,0:T(8,128)(2,1)S(1)} custom-call(s32[6]{0:T(128)S(1)} %stack.27.s, bf16[256,768]{1,0:T(8,128)(2,1)S(1)} %collective-permute-done.4.refs_2_.refs_0_, bf16[256,768]{1,0:T(8,128)(2,1)S(1)} %collective-permute-done.5.refs_3_.refs_1_, bf16[256,768]{1,0:T(8,128)(2,1)S(1)} %collective-permute-done.9.refs_4_.refs_2_, ...), custom_call_target="tpu_custom_call" | custom-call | flops 1 | bytes 1 | tf_op jit(solution)/shard_map/turn/pallas_call | solution.py:35
  76.3 1.0 collective-permute-start.17
  77.3 2.2 %collective-permute-start.18 = (bf16[512,128]{1,0:T(8,128)(2,1)S(1)}, bf16[512,128]{1,0:T(8,128)(2,1)S(1)}, u32[]{:S(2)}, u32[]{:S(2)}) collective-permute-start(bf16[512,128]{1,0:T(8,128)(2,1)S(1)} %get-tuple-element.187), channel_id=1, source_target_pairs={{0,12},{4,8},{8,4},{12,0},{1,13},{5,9},{9,5},{13,1},{2,14},{6,10},... | collective-permute-start | bytes 393224 | tf_op jit(solution)/shard_map/ppermute | solution.py:23
  79.4 1.0 collective-permute-start.19
  80.5 3.2 %local_grads.5 = (bf16[3,512,512]{2,1,0:T(8,128)(2,1)S(1)}, bf16[3,512,512]{2,1,0:T(8,128)(2,1)S(1)}) custom-call(s32[6]{0:T(128)S(1)} %stack.27.s, bf16[3,512,512]{2,1,0:T(8,128)(2,1)S(1)} %project.5.qkv_ref, bf16[512,512]{1,0:T(8,128)(2,1)S(1)} %collective-permute-done.8.og_ref, ...), custom_call_target="tpu_custom_call", output_to_operand_aliasing={{0}: (4, {}), {1}: (5, {})} | custom-call | flops 1 | bytes 1 | tf_op jit(solution)/shard_map/local_grads/pallas_call | solution.py:35
  84.2 1.8 %collective-permute-done.19.c = bf16[512,128]{1,0:T(8,128)(2,1)S(1)} collective-permute-done((bf16[512,128]{1,0:T(8,128)(2,1)S(1)}, bf16[512,128]{1,0:T(8,128)(2,1)S(1)}, u32[]{:S(2)}, u32[]{:S(2)}) %collective-permute-start.19) | collective-permute-done | bytes 131104 | tf_op jit(solution)/shard_map/ppermute | solution.py:23
  85.9 4.4 %whole_grads.1 = (bf16[512,768]{1,0:T(8,128)(2,1)S(1)}, bf16[512,768]{1,0:T(8,128)(2,1)S(1)}, bf16[512,768]{1,0:T(8,128)(2,1)S(1)}, bf16[512,768]{1,0:T(8,128)(2,1)S(1)}) custom-call(s32[6]{0:T(128)S(1)} %stack.27.s, bf16[3,512,512]{2,1,0:T(8,128)(2,1)S(1)} %get-tuple-element.200.local_a, bf16[3,512,512]{2,1,0:T(8,128)(2,1)S(1)} %get-tuple-element.201.ready_a, ...), custom_call_target="tpu_custom_call" | custom-call | flops 1 | bytes 1 | tf_op jit(solution)/shard_map/whole_grads/pallas_call | solution.py:35
  90.4 3.2 %weight_part.3 = (bf16[384,768]{1,0:T(8,128)(2,1)S(1)}, bf16[384,768]{1,0:T(8,128)(2,1)S(1)}, bf16[384,768]{1,0:T(8,128)(2,1)S(1)}, bf16[384,768]{1,0:T(8,128)(2,1)S(1)}) custom-call(s32[6]{0:T(128)S(1)} %stack.27.s, bf16[4,4,192,512]{3,2,1,0:T(8,128)(2,1)S(1)} %bitcast.19, bf16[4,4,192,512]{3,2,1,0:T(8,128)(2,1)S(1)} %bitcast.20, ...), custom_call_target="tpu_custom_call" | custom-call | flops 1 | bytes 1 | tf_op jit(solution)/shard_map/weight_part/pallas_call | solution.py:35
  93.5 2.2 %collective-permute-start.21 = (bf16[384,768]{1,0:T(8,128)(2,1)S(1)}, bf16[384,768]{1,0:T(8,128)(2,1)S(1)}, u32[]{:S(2)}, u32[]{:S(2)}) collective-permute-start(bf16[384,768]{1,0:T(8,128)(2,1)S(1)} %get-tuple-element.215), channel_id=1, source_target_pairs={{0,48},{16,32},{32,16},{48,0},{1,49},{17,33},{33,17},{49,1},{2,50}... | collective-permute-start | bytes 1769480 | tf_op jit(solution)/shard_map/ppermute | solution.py:23
  95.7 1.4 collective-permute-start.20
  98.7 8.4 %weight_part.4 = (bf16[768,768]{1,0:T(8,128)(2,1)S(1)}, bf16[768,768]{1,0:T(8,128)(2,1)S(1)}, bf16[768,768]{1,0:T(8,128)(2,1)S(1)}, bf16[768,768]{1,0:T(8,128)(2,1)S(1)}) custom-call(s32[6]{0:T(128)S(1)} %stack.27.s, bf16[4,4,192,512]{3,2,1,0:T(8,128)(2,1)S(1)} %bitcast.21, bf16[4,4,192,512]{3,2,1,0:T(8,128)(2,1)S(1)} %bitcast.22, ...), custom_call_target="tpu_custom_call" | custom-call | flops 1 | bytes 1 | tf_op jit(solution)/shard_map/weight_part/pallas_call | solution.py:35
  108.4 1.0 collective-permute-start.22
  110.1 1.2 collective-permute-start.23
  112.2 1.0 collective-permute-start.27
  113.3 3.2 %weight_part.5 = (bf16[768,768]{1,0:T(8,128)(2,1)S(1)}, bf16[768,768]{1,0:T(8,128)(2,1)S(1)}) custom-call(s32[6]{0:T(128)S(1)} %stack.27.s, bf16[4,4,192,512]{3,2,1,0:T(8,128)(2,1)S(1)} %bitcast.23, bf16[4,4,192,512]{3,2,1,0:T(8,128)(2,1)S(1)} %bitcast.24, bf16[4,4,192,512]{3,2,1,0:T(8,128)(2,1)S(1)} %bitcast.29, bf16[4,4,192,512]{3,2,1,0:T(8,128)(2,1)S(1)} %bitcast.30, ...), custom_call_target="tpu_custom_call" | custom-call | flops 1 | bytes 1 | tf_op jit(solution)/shard_map/weight_part/pallas_call | solution.py:35
  116.5 17.6 %collective-permute-done.23.refs_2_ = bf16[768,768]{1,0:T(8,128)(2,1)S(1)} collective-permute-done((bf16[768,768]{1,0:T(8,128)(2,1)S(1)}, bf16[768,768]{1,0:T(8,128)(2,1)S(1)}, u32[]{:S(2)}, u32[]{:S(2)}) %collective-permute-start.23) | collective-permute-done | bytes 1179680 | tf_op jit(solution)/shard_map/ppermute | solution.py:23
  134.1 2.2 %collective-permute-done.27.refs_5_ = bf16[768,768]{1,0:T(8,128)(2,1)S(1)} collective-permute-done((bf16[768,768]{1,0:T(8,128)(2,1)S(1)}, bf16[768,768]{1,0:T(8,128)(2,1)S(1)}, u32[]{:S(2)}, u32[]{:S(2)}) %collective-permute-start.27) | collective-permute-done | bytes 1179680 | tf_op jit(solution)/shard_map/ppermute | solution.py:23
  136.3 1.6 collective-permute-done.26.refs_4_
  137.9 1.4 cut_blocks.1
  139.5 1.9 %collective-permute-start.29 = (bf16[192,768]{1,0:T(8,128)(2,1)S(1)}, bf16[192,768]{1,0:T(8,128)(2,1)S(1)}, u32[]{:S(2)}, u32[]{:S(2)}) collective-permute-start(bf16[192,768]{1,0:T(8,128)(2,1)S(1)} %get-tuple-element.240), channel_id=1, source_target_pairs={{0,12},{4,8},{8,4},{12,0},{1,13},{5,9},{9,5},{13,1},{2,14},{6,10},... | collective-permute-start | bytes 884744 | tf_op jit(solution)/shard_map/ppermute | solution.py:23
  141.4 2.0 %collective-permute-start.30 = (bf16[192,768]{1,0:T(8,128)(2,1)S(1)}, bf16[192,768]{1,0:T(8,128)(2,1)S(1)}, u32[]{:S(2)}, u32[]{:S(2)}) collective-permute-start(bf16[192,768]{1,0:T(8,128)(2,1)S(1)} %get-tuple-element.241), channel_id=1, source_target_pairs={{0,8},{4,12},{8,0},{12,4},{1,9},{5,13},{9,1},{13,5},{2,10},{6,14},... | collective-permute-start | bytes 884744 | tf_op jit(solution)/shard_map/ppermute | solution.py:23
  144.2 1.4 collective-permute-start.32
  146.4 1.2 collective-permute-start.33
  147.7 3.1 %collective-permute-done.29.c = bf16[192,768]{1,0:T(8,128)(2,1)S(1)} collective-permute-done((bf16[192,768]{1,0:T(8,128)(2,1)S(1)}, bf16[192,768]{1,0:T(8,128)(2,1)S(1)}, u32[]{:S(2)}, u32[]{:S(2)}) %collective-permute-start.29) | collective-permute-done | bytes 294944 | tf_op jit(solution)/shard_map/ppermute | solution.py:23
  151.4 2.0 %collective-permute-start.34 = (bf16[96,768]{1,0:T(8,128)(2,1)S(1)}, bf16[96,768]{1,0:T(8,128)(2,1)S(1)}, u32[]{:S(2)}, u32[]{:S(2)}) collective-permute-start(bf16[96,768]{1,0:T(8,128)(2,1)S(1)} %get-tuple-element.251), channel_id=1, source_target_pairs={{0,64},{64,0},{1,65},{65,1},{2,66},{66,2},{3,67},{67,3},{4,68},{68... | collective-permute-start | bytes 442376 | tf_op jit(solution)/shard_map/ppermute | solution.py:23
  153.4 1.9 %collective-permute-done.32.c = bf16[192,768]{1,0:T(8,128)(2,1)S(1)} collective-permute-done((bf16[192,768]{1,0:T(8,128)(2,1)S(1)}, bf16[192,768]{1,0:T(8,128)(2,1)S(1)}, u32[]{:S(2)}, u32[]{:S(2)}) %collective-permute-start.32) | collective-permute-done | bytes 294944 | tf_op jit(solution)/shard_map/ppermute | solution.py:23
  156.0 2.3 %collective-permute-start.35 = (bf16[96,768]{1,0:T(8,128)(2,1)S(1)}, bf16[96,768]{1,0:T(8,128)(2,1)S(1)}, u32[]{:S(2)}, u32[]{:S(2)}) collective-permute-start(bf16[96,768]{1,0:T(8,128)(2,1)S(1)} %get-tuple-element.252), channel_id=1, source_target_pairs={{0,64},{64,0},{1,65},{65,1},{2,66},{66,2},{3,67},{67,3},{4,68},{68... | collective-permute-start | bytes 442376 | tf_op jit(solution)/shard_map/ppermute | solution.py:23
  158.3 4.4 %collective-permute-done.35.refs_3_ = bf16[96,768]{1,0:T(8,128)(2,1)S(1)} collective-permute-done((bf16[96,768]{1,0:T(8,128)(2,1)S(1)}, bf16[96,768]{1,0:T(8,128)(2,1)S(1)}, u32[]{:S(2)}, u32[]{:S(2)}) %collective-permute-start.35) | collective-permute-done | bytes 147488 | tf_op jit(solution)/shard_map/ppermute | solution.py:23
  162.7 1.6 finish.1
  (61 shorter events, 15.7 us)
Async XLA Ops:
  0.0 10.0 %collective-permute-start.2 = (bf16[512,768]{1,0:T(8,128)(2,1)}, bf16[512,768]{1,0:T(8,128)(2,1)}, u32[]{:S(2)}, u32[]{:S(2)}) collective-permute-start(bf16[512,768]{1,0:T(8,128)(2,1)} %refs_0_.2), channel_id=1, source_target_pairs={{0,1},{1,0},{2,3},{3,2},{4,5},{5,4},{6,7},{7,6},{8,9},{9,8},{10,11... | collective-permute-start | bytes 2359304 | tf_op jit(solution)/shard_map/ppermute | solution.py:23
  0.0 24.1 %collective-permute-start.1 = (bf16[512,768]{1,0:T(8,128)(2,1)}, bf16[512,768]{1,0:T(8,128)(2,1)S(1)}, u32[]{:S(2)}, u32[]{:S(2)}) collective-permute-start(bf16[512,768]{1,0:T(8,128)(2,1)} %refs_0_.2), channel_id=1, source_target_pairs={{0,66},{2,64},{64,2},{66,0},{1,67},{3,65},{65,3},{67,1},{4,70},{6,... | collective-permute-start | bytes 2359304 | tf_op jit(solution)/shard_map/ppermute | solution.py:27
  4.1 20.1 %collective-permute-start = (bf16[512,768]{1,0:T(8,128)(2,1)}, bf16[512,768]{1,0:T(8,128)(2,1)S(1)}, u32[]{:S(2)}, u32[]{:S(2)}) collective-permute-start(bf16[512,768]{1,0:T(8,128)(2,1)} %refs_0_.2), channel_id=1, source_target_pairs={{0,2},{2,0},{1,3},{3,1},{4,6},{6,4},{5,7},{7,5},{8,10},{10,8},{9,1... | collective-permute-start | bytes 2359304 | tf_op jit(solution)/shard_map/ppermute | solution.py:23
  5.5 4.5 %copy-start = (bf16[512,768]{1,0:T(8,128)(2,1)S(1)}, bf16[512,768]{1,0:T(8,128)(2,1)}, u32[]{:S(2)}) copy-start(bf16[512,768]{1,0:T(8,128)(2,1)} %refs_0_.2) | copy-start | bytes 2359300
  7.0 17.1 %collective-permute-start.3 = (f32[8,512]{1,0:T(8,128)S(1)}, f32[8,512]{1,0:T(8,128)S(1)}, u32[]{:S(2)}, u32[]{:S(2)}) collective-permute-start(f32[8,512]{1,0:T(8,128)S(1)} %concatenate.6), channel_id=1, source_target_pairs={{0,64},{64,0},{1,65},{65,1},{2,66},{66,2},{3,67},{67,3},{4,68},{68... | collective-permute-start | bytes 49160 | tf_op jit(solution)/shard_map/ppermute | solution.py:23
  24.2 4.1 %collective-permute-start.7 = (bf16[512,768]{1,0:T(8,128)(2,1)S(1)}, bf16[512,768]{1,0:T(8,128)(2,1)S(1)}, u32[]{:S(2)}, u32[]{:S(2)}) collective-permute-start(bf16[512,768]{1,0:T(8,128)(2,1)S(1)} %collective-permute-done.b.refs_0_.refs_2_), channel_id=1, source_target_pairs={{0,1},{1,0},{2,3},{3,2},{4,5},{5,4},{6,7},{7,6},{8,9},{9,8},{10,11... | collective-permute-start | bytes 2359304 | tf_op jit(solution)/shard_map/ppermute | solution.py:23
  24.2 13.5 %collective-permute-start.6 = (bf16[512,768]{1,0:T(8,128)(2,1)S(1)}, bf16[512,768]{1,0:T(8,128)(2,1)S(1)}, u32[]{:S(2)}, u32[]{:S(2)}) collective-permute-start(bf16[512,768]{1,0:T(8,128)(2,1)S(1)} %collective-permute-done.1.a.refs_0_.refs_4_), channel_id=1, source_target_pairs={{0,1},{1,0},{2,3},{3,2},{4,5},{5,4},{6,7},{7,6},{8,9},{9,8},{10,11... | collective-permute-start | bytes 2359304 | tf_op jit(solution)/shard_map/ppermute | solution.py:23
  25.3 11.5 %collective-permute-start.4 = (bf16[256,768]{1,0:T(8,128)(2,1)S(1)}, bf16[256,768]{1,0:T(8,128)(2,1)S(1)}, u32[]{:S(2)}, u32[]{:S(2)}) collective-permute-start(bf16[256,768]{1,0:T(8,128)(2,1)S(1)} %get-tuple-element.132), channel_id=1, source_target_pairs={{0,2},{2,0},{1,3},{3,1},{4,6},{6,4},{5,7},{7,5},{8,10},{10,8},{9,1... | collective-permute-start | bytes 1179656 | tf_op jit(solution)/shard_map/ppermute | solution.py:23
  25.7 12.0 %collective-permute-start.5 = (bf16[256,768]{1,0:T(8,128)(2,1)S(1)}, bf16[256,768]{1,0:T(8,128)(2,1)S(1)}, u32[]{:S(2)}, u32[]{:S(2)}) collective-permute-start(bf16[256,768]{1,0:T(8,128)(2,1)S(1)} %get-tuple-element.133), channel_id=1, source_target_pairs={{0,66},{2,64},{64,2},{66,0},{1,67},{3,65},{65,3},{67,1},{4,70},{6,... | collective-permute-start | bytes 1179656 | tf_op jit(solution)/shard_map/ppermute | solution.py:27
  37.7 14.4 %collective-permute-start.8 = (bf16[512,512]{1,0:T(8,128)(2,1)S(1)}, bf16[512,512]{1,0:T(8,128)(2,1)S(1)}, u32[]{:S(2)}, u32[]{:S(2)}) collective-permute-start(bf16[512,512]{1,0:T(8,128)(2,1)S(1)} %get-tuple-element.142), channel_id=1, source_target_pairs={{0,64},{64,0},{1,65},{65,1},{2,66},{66,2},{3,67},{67,3},{4,68},{68... | collective-permute-start | bytes 1572872 | tf_op jit(solution)/shard_map/ppermute | solution.py:23
  40.5 2.8 %collective-permute-start.9 = (bf16[256,768]{1,0:T(8,128)(2,1)S(1)}, bf16[256,768]{1,0:T(8,128)(2,1)S(1)}, u32[]{:S(2)}, u32[]{:S(2)}) collective-permute-start(bf16[256,768]{1,0:T(8,128)(2,1)S(1)} %collective-permute-done.4.refs_2_.refs_0_), channel_id=1, source_target_pairs={{0,1},{1,0},{2,3},{3,2},{4,5},{5,4},{6,7},{7,6},{8,9},{9,8},{10,11... | collective-permute-start | bytes 1179656 | tf_op jit(solution)/shard_map/ppermute | solution.py:23
  40.5 2.8 %collective-permute-start.10 = (bf16[256,768]{1,0:T(8,128)(2,1)S(1)}, bf16[256,768]{1,0:T(8,128)(2,1)S(1)}, u32[]{:S(2)}, u32[]{:S(2)}) collective-permute-start(bf16[256,768]{1,0:T(8,128)(2,1)S(1)} %collective-permute-done.5.refs_3_.refs_1_), channel_id=1, source_target_pairs={{0,1},{1,0},{2,3},{3,2},{4,5},{5,4},{6,7},{7,6},{8,9},{9,8},{10,11... | collective-permute-start | bytes 1179656 | tf_op jit(solution)/shard_map/ppermute | solution.py:23
  54.4 10.4 %collective-permute-start.11 = (bf16[528,128]{1,0:T(8,128)(2,1)S(1)}, bf16[528,128]{1,0:T(8,128)(2,1)S(1)}, u32[]{:S(2)}, u32[]{:S(2)}) collective-permute-start(bf16[528,128]{1,0:T(8,128)(2,1)S(1)} %get-tuple-element.159), channel_id=1, source_target_pairs={{0,4},{4,0},{8,12},{12,8},{1,5},{5,1},{9,13},{13,9},{2,6},{6,2},{1... | collective-permute-start | bytes 405512 | tf_op jit(solution)/shard_map/ppermute | solution.py:23
  56.0 9.1 %collective-permute-start.12 = (bf16[528,128]{1,0:T(8,128)(2,1)S(1)}, bf16[528,128]{1,0:T(8,128)(2,1)S(1)}, u32[]{:S(2)}, u32[]{:S(2)}) collective-permute-start(bf16[528,128]{1,0:T(8,128)(2,1)S(1)} %get-tuple-element.160), channel_id=1, source_target_pairs={{0,12},{4,8},{8,4},{12,0},{1,13},{5,9},{9,5},{13,1},{2,14},{6,10},... | collective-permute-start | bytes 405512 | tf_op jit(solution)/shard_map/ppermute | solution.py:23
  58.2 6.9 %collective-permute-start.13 = (bf16[528,128]{1,0:T(8,128)(2,1)S(1)}, bf16[528,128]{1,0:T(8,128)(2,1)S(1)}, u32[]{:S(2)}, u32[]{:S(2)}) collective-permute-start(bf16[528,128]{1,0:T(8,128)(2,1)S(1)} %get-tuple-element.161), channel_id=1, source_target_pairs={{0,8},{4,12},{8,0},{12,4},{1,9},{5,13},{9,1},{13,5},{2,10},{6,14},... | collective-permute-start | bytes 405512 | tf_op jit(solution)/shard_map/ppermute | solution.py:23
  65.9 9.5 %collective-permute-start.16 = (bf16[528,128]{1,0:T(8,128)(2,1)S(1)}, bf16[528,128]{1,0:T(8,128)(2,1)S(1)}, u32[]{:S(2)}, u32[]{:S(2)}) collective-permute-start(bf16[528,128]{1,0:T(8,128)(2,1)S(1)} %get-tuple-element.168.a), channel_id=1, source_target_pairs={{0,32},{16,48},{32,0},{48,16},{1,33},{17,49},{33,1},{49,17},{2,34}... | collective-permute-start | bytes 405512 | tf_op jit(solution)/shard_map/ppermute | solution.py:23
  69.0 6.4 %collective-permute-start.15 = (bf16[528,128]{1,0:T(8,128)(2,1)S(1)}, bf16[528,128]{1,0:T(8,128)(2,1)S(1)}, u32[]{:S(2)}, u32[]{:S(2)}) collective-permute-start(bf16[528,128]{1,0:T(8,128)(2,1)S(1)} %get-tuple-element.168.a), channel_id=1, source_target_pairs={{0,48},{16,32},{32,16},{48,0},{1,49},{17,33},{33,17},{49,1},{2,50}... | collective-permute-start | bytes 405512 | tf_op jit(solution)/shard_map/ppermute | solution.py:23
  70.1 5.3 %collective-permute-start.14 = (bf16[528,128]{1,0:T(8,128)(2,1)S(1)}, bf16[528,128]{1,0:T(8,128)(2,1)S(1)}, u32[]{:S(2)}, u32[]{:S(2)}) collective-permute-start(bf16[528,128]{1,0:T(8,128)(2,1)S(1)} %get-tuple-element.168.a), channel_id=1, source_target_pairs={{0,16},{16,0},{32,48},{48,32},{1,17},{17,1},{33,49},{49,33},{2,18}... | collective-permute-start | bytes 405512 | tf_op jit(solution)/shard_map/ppermute | solution.py:23
  76.3 7.4 %collective-permute-start.17 = (bf16[512,128]{1,0:T(8,128)(2,1)S(1)}, bf16[512,128]{1,0:T(8,128)(2,1)S(1)}, u32[]{:S(2)}, u32[]{:S(2)}) collective-permute-start(bf16[512,128]{1,0:T(8,128)(2,1)S(1)} %get-tuple-element.186), channel_id=1, source_target_pairs={{0,4},{4,0},{8,12},{12,8},{1,5},{5,1},{9,13},{13,9},{2,6},{6,2},{1... | collective-permute-start | bytes 393224 | tf_op jit(solution)/shard_map/ppermute | solution.py:23
  77.3 6.9 %collective-permute-start.18 = (bf16[512,128]{1,0:T(8,128)(2,1)S(1)}, bf16[512,128]{1,0:T(8,128)(2,1)S(1)}, u32[]{:S(2)}, u32[]{:S(2)}) collective-permute-start(bf16[512,128]{1,0:T(8,128)(2,1)S(1)} %get-tuple-element.187), channel_id=1, source_target_pairs={{0,12},{4,8},{8,4},{12,0},{1,13},{5,9},{9,5},{13,1},{2,14},{6,10},... | collective-permute-start | bytes 393224 | tf_op jit(solution)/shard_map/ppermute | solution.py:23
  79.4 6.5 %collective-permute-start.19 = (bf16[512,128]{1,0:T(8,128)(2,1)S(1)}, bf16[512,128]{1,0:T(8,128)(2,1)S(1)}, u32[]{:S(2)}, u32[]{:S(2)}) collective-permute-start(bf16[512,128]{1,0:T(8,128)(2,1)S(1)} %get-tuple-element.188), channel_id=1, source_target_pairs={{0,8},{4,12},{8,0},{12,4},{1,9},{5,13},{9,1},{13,5},{2,10},{6,14},... | collective-permute-start | bytes 393224 | tf_op jit(solution)/shard_map/ppermute | solution.py:23
  93.5 13.9 %collective-permute-start.21 = (bf16[384,768]{1,0:T(8,128)(2,1)S(1)}, bf16[384,768]{1,0:T(8,128)(2,1)S(1)}, u32[]{:S(2)}, u32[]{:S(2)}) collective-permute-start(bf16[384,768]{1,0:T(8,128)(2,1)S(1)} %get-tuple-element.215), channel_id=1, source_target_pairs={{0,48},{16,32},{32,16},{48,0},{1,49},{17,33},{33,17},{49,1},{2,50}... | collective-permute-start | bytes 1769480 | tf_op jit(solution)/shard_map/ppermute | solution.py:23
  95.7 11.7 %collective-permute-start.20 = (bf16[384,768]{1,0:T(8,128)(2,1)S(1)}, bf16[384,768]{1,0:T(8,128)(2,1)S(1)}, u32[]{:S(2)}, u32[]{:S(2)}) collective-permute-start(bf16[384,768]{1,0:T(8,128)(2,1)S(1)} %get-tuple-element.211), channel_id=1, source_target_pairs={{0,16},{16,0},{32,48},{48,32},{1,17},{17,1},{33,49},{49,33},{2,18}... | collective-permute-start | bytes 1769480 | tf_op jit(solution)/shard_map/ppermute | solution.py:23
  97.1 12.3 %collective-permute-start.24 = (bf16[384,768]{1,0:T(8,128)(2,1)S(1)}, bf16[384,768]{1,0:T(8,128)(2,1)S(1)}, u32[]{:S(2)}, u32[]{:S(2)}) collective-permute-start(bf16[384,768]{1,0:T(8,128)(2,1)S(1)} %get-tuple-element.224), channel_id=1, source_target_pairs={{0,4},{4,0},{8,12},{12,8},{1,5},{5,1},{9,13},{13,9},{2,6},{6,2},{1... | collective-permute-start | bytes 1769480 | tf_op jit(solution)/shard_map/ppermute | solution.py:23
  97.8 12.3 %collective-permute-start.25 = (bf16[384,768]{1,0:T(8,128)(2,1)S(1)}, bf16[384,768]{1,0:T(8,128)(2,1)S(1)}, u32[]{:S(2)}, u32[]{:S(2)}) collective-permute-start(bf16[384,768]{1,0:T(8,128)(2,1)S(1)} %get-tuple-element.225), channel_id=1, source_target_pairs={{0,12},{4,8},{8,4},{12,0},{1,13},{5,9},{9,5},{13,1},{2,14},{6,10},... | collective-permute-start | bytes 1769480 | tf_op jit(solution)/shard_map/ppermute | solution.py:23
  108.4 25.8 %collective-permute-start.22 = (bf16[768,768]{1,0:T(8,128)(2,1)S(1)}, bf16[768,768]{1,0:T(8,128)(2,1)S(1)}, u32[]{:S(2)}, u32[]{:S(2)}) collective-permute-start(bf16[768,768]{1,0:T(8,128)(2,1)S(1)} %get-tuple-element.220), channel_id=1, source_target_pairs={{0,16},{16,0},{32,48},{48,32},{1,17},{17,1},{33,49},{49,33},{2,18}... | collective-permute-start | bytes 3538952 | tf_op jit(solution)/shard_map/ppermute | solution.py:23
  110.1 24.0 %collective-permute-start.23 = (bf16[768,768]{1,0:T(8,128)(2,1)S(1)}, bf16[768,768]{1,0:T(8,128)(2,1)S(1)}, u32[]{:S(2)}, u32[]{:S(2)}) collective-permute-start(bf16[768,768]{1,0:T(8,128)(2,1)S(1)} %get-tuple-element.221), channel_id=1, source_target_pairs={{0,48},{16,32},{32,16},{48,0},{1,49},{17,33},{33,17},{49,1},{2,50}... | collective-permute-start | bytes 3538952 | tf_op jit(solution)/shard_map/ppermute | solution.py:23
  112.2 24.1 %collective-permute-start.27 = (bf16[768,768]{1,0:T(8,128)(2,1)S(1)}, bf16[768,768]{1,0:T(8,128)(2,1)S(1)}, u32[]{:S(2)}, u32[]{:S(2)}) collective-permute-start(bf16[768,768]{1,0:T(8,128)(2,1)S(1)} %get-tuple-element.237), channel_id=1, source_target_pairs={{0,12},{4,8},{8,4},{12,0},{1,13},{5,9},{9,5},{13,1},{2,14},{6,10},... | collective-permute-start | bytes 3538952 | tf_op jit(solution)/shard_map/ppermute | solution.py:23
  113.2 24.7 %collective-permute-start.26 = (bf16[768,768]{1,0:T(8,128)(2,1)S(1)}, bf16[768,768]{1,0:T(8,128)(2,1)S(1)}, u32[]{:S(2)}, u32[]{:S(2)}) collective-permute-start(bf16[768,768]{1,0:T(8,128)(2,1)S(1)} %get-tuple-element.228), channel_id=1, source_target_pairs={{0,4},{4,0},{8,12},{12,8},{1,5},{5,1},{9,13},{13,9},{2,6},{6,2},{1... | collective-permute-start | bytes 3538952 | tf_op jit(solution)/shard_map/ppermute | solution.py:23
  139.2 7.2 %collective-permute-start.28 = (bf16[192,768]{1,0:T(8,128)(2,1)S(1)}, bf16[192,768]{1,0:T(8,128)(2,1)S(1)}, u32[]{:S(2)}, u32[]{:S(2)}) collective-permute-start(bf16[192,768]{1,0:T(8,128)(2,1)S(1)} %get-tuple-element.239), channel_id=1, source_target_pairs={{0,4},{4,0},{8,12},{12,8},{1,5},{5,1},{9,13},{13,9},{2,6},{6,2},{1... | collective-permute-start | bytes 884744 | tf_op jit(solution)/shard_map/ppermute | solution.py:23
  139.5 11.2 %collective-permute-start.29 = (bf16[192,768]{1,0:T(8,128)(2,1)S(1)}, bf16[192,768]{1,0:T(8,128)(2,1)S(1)}, u32[]{:S(2)}, u32[]{:S(2)}) collective-permute-start(bf16[192,768]{1,0:T(8,128)(2,1)S(1)} %get-tuple-element.240), channel_id=1, source_target_pairs={{0,12},{4,8},{8,4},{12,0},{1,13},{5,9},{9,5},{13,1},{2,14},{6,10},... | collective-permute-start | bytes 884744 | tf_op jit(solution)/shard_map/ppermute | solution.py:23
  141.4 9.3 %collective-permute-start.30 = (bf16[192,768]{1,0:T(8,128)(2,1)S(1)}, bf16[192,768]{1,0:T(8,128)(2,1)S(1)}, u32[]{:S(2)}, u32[]{:S(2)}) collective-permute-start(bf16[192,768]{1,0:T(8,128)(2,1)S(1)} %get-tuple-element.241), channel_id=1, source_target_pairs={{0,8},{4,12},{8,0},{12,4},{1,9},{5,13},{9,1},{13,5},{2,10},{6,14},... | collective-permute-start | bytes 884744 | tf_op jit(solution)/shard_map/ppermute | solution.py:23
  143.4 10.0 %collective-permute-start.31 = (bf16[192,768]{1,0:T(8,128)(2,1)S(1)}, bf16[192,768]{1,0:T(8,128)(2,1)S(1)}, u32[]{:S(2)}, u32[]{:S(2)}) collective-permute-start(bf16[192,768]{1,0:T(8,128)(2,1)S(1)} %get-tuple-element.244), channel_id=1, source_target_pairs={{0,16},{16,0},{32,48},{48,32},{1,17},{17,1},{33,49},{49,33},{2,18}... | collective-permute-start | bytes 884744 | tf_op jit(solution)/shard_map/ppermute | solution.py:23
  144.2 11.1 %collective-permute-start.32 = (bf16[192,768]{1,0:T(8,128)(2,1)S(1)}, bf16[192,768]{1,0:T(8,128)(2,1)S(1)}, u32[]{:S(2)}, u32[]{:S(2)}) collective-permute-start(bf16[192,768]{1,0:T(8,128)(2,1)S(1)} %get-tuple-element.245), channel_id=1, source_target_pairs={{0,48},{16,32},{32,16},{48,0},{1,49},{17,33},{33,17},{49,1},{2,50}... | collective-permute-start | bytes 884744 | tf_op jit(solution)/shard_map/ppermute | solution.py:23
  146.4 8.9 %collective-permute-start.33 = (bf16[192,768]{1,0:T(8,128)(2,1)S(1)}, bf16[192,768]{1,0:T(8,128)(2,1)S(1)}, u32[]{:S(2)}, u32[]{:S(2)}) collective-permute-start(bf16[192,768]{1,0:T(8,128)(2,1)S(1)} %get-tuple-element.246), channel_id=1, source_target_pairs={{0,32},{16,48},{32,0},{48,16},{1,33},{17,49},{33,1},{49,17},{2,34}... | collective-permute-start | bytes 884744 | tf_op jit(solution)/shard_map/ppermute | solution.py:23
  151.4 6.9 %collective-permute-start.34 = (bf16[96,768]{1,0:T(8,128)(2,1)S(1)}, bf16[96,768]{1,0:T(8,128)(2,1)S(1)}, u32[]{:S(2)}, u32[]{:S(2)}) collective-permute-start(bf16[96,768]{1,0:T(8,128)(2,1)S(1)} %get-tuple-element.251), channel_id=1, source_target_pairs={{0,64},{64,0},{1,65},{65,1},{2,66},{66,2},{3,67},{67,3},{4,68},{68... | collective-permute-start | bytes 442376 | tf_op jit(solution)/shard_map/ppermute | solution.py:23
  156.0 6.7 %collective-permute-start.35 = (bf16[96,768]{1,0:T(8,128)(2,1)S(1)}, bf16[96,768]{1,0:T(8,128)(2,1)S(1)}, u32[]{:S(2)}, u32[]{:S(2)}) collective-permute-start(bf16[96,768]{1,0:T(8,128)(2,1)S(1)} %get-tuple-element.252), channel_id=1, source_target_pairs={{0,64},{64,0},{1,65},{65,1},{2,66},{66,2},{3,67},{67,3},{4,68},{68... | collective-permute-start | bytes 442376 | tf_op jit(solution)/shard_map/ppermute | solution.py:23

commit v12 on v11

--- a/solution.py
+++ b/solution.py
@@ -426,34 +426,41 @@
     tokens, cols = lefts[0].shape
     rows = turned[0].shape[2]
 
+    n = 2 if split else 1
+
     def body(s, own_x, own_y, pair_x, pair_y, left_a, left_b, right_a, right_b, *outs):
         r = pl.program_id(0)
+        count = len(outs) // 2
         for side, (a, b, ga, gb) in enumerate(
             ((own_x, pair_x, left_a, left_b), (own_y, pair_y, right_a, right_b))
         ):
-            acc = dot(a[...].reshape(4 * rows, tokens), ga[...])
-            acc += dot(b[...].reshape(4 * rows, tokens), gb[...])
+            acc = dot(a[...].reshape(4 * rows // n, tokens), ga[...])
+            acc += dot(b[...].reshape(4 * rows // n, tokens), gb[...])
             acc = acc.astype(BF16)
-            if split:
-                outs[2 * side][...] = acc[: 2 * rows]
-                outs[2 * side + 1][...] = acc[2 * rows :]
-                continue
-            for k in range(len(places)):
+            for k in range(count):
 
                 @pl.when(r == k)
                 def _(k=k, acc=acc, side=side):
-                    outs[side * len(places) + k][...] = acc
+                    outs[side * count + k][...] = acc
 
     step = places[1] - places[0] if len(places) > 1 else 0
-    by_x = pl.BlockSpec((1, 4, rows, tokens), lambda r, s: (s[X] ^ (places[0] + step * r), 0, 0, 0))
-    by_y = pl.BlockSpec((4, 1, rows, tokens), lambda r, s: (0, s[Y] ^ (places[0] + step * r), 0, 0))
-    outs = [shape((2 * rows if split else 4 * rows, cols))] * (4 if split else 2 * len(places))
+    if split:
+        by_x = pl.BlockSpec((1, 2, rows, tokens), lambda r, s: (s[X] ^ places[0], r, 0, 0))
+        by_y = pl.BlockSpec((2, 1, rows, tokens), lambda r, s: (r, s[Y] ^ places[0], 0, 0))
+    else:
+        by_x = pl.BlockSpec(
+            (1, 4, rows, tokens), lambda r, s: (s[X] ^ (places[0] + step * r), 0, 0, 0)
+        )
+        by_y = pl.BlockSpec(
+            (4, 1, rows, tokens), lambda r, s: (0, s[Y] ^ (places[0] + step * r), 0, 0)
+        )
+    outs = [shape((4 * rows // n, cols))] * (4 if split else 2 * len(places))
     operands = (turned[0], turned[0], turned[1], turned[1], *lefts, *rights)
     return call(
         "weight_part",
         body,
         table,
-        (len(places),),
+        (n * len(places),),
         operands,
         [by_x, by_y, by_x, by_y, *[whole(x) for x in (*lefts, *rights)]],
         outs,
@@ -492,22 +499,28 @@
     rows, cols = left[0].shape[0] // 4, left[0].shape[1]
 
     def body(s, *refs):
-        for k, axis in enumerate((Y, X)):
-            a, b, c = refs[3 * k : 3 * k + 3]
-            for r, out in zip((1, 3, 2, 0), refs[6 + 4 * k : 10 + 4 * k]):
-                at = pl.ds(pl.multiple_of((s[axis] ^ r) * rows, rows), rows)
-                total = a[at, :].astype(F32) + b[at, :].astype(F32) + c[at, :].astype(F32)
-                out[...] = total.astype(BF16)
+        i = pl.program_id(0)
+        for side in range(2):
+            a, b, c = (ref[...].astype(F32) for ref in refs[3 * side : 3 * side + 3])
+            total = (a + b + c).astype(BF16)
+            for k, at in enumerate((0, 2, 1, 3)):
+
+                @pl.when(i == at)
+                def _(k=k, side=side, total=total):
+                    refs[6 + 4 * side + k][...] = total
 
     outs = [shape((rows, cols))] * 8
-    operands = (*left, *right)
+    specs = [
+        pl.BlockSpec((rows, cols), lambda i, s, axis=axis: (s[axis] ^ ((i + 1) % 4), 0))
+        for axis in (Y, X)
+    ]
     cut = call(
         "cut_blocks",
         body,
         table,
-        (1,),
-        operands,
-        [whole(x) for x in operands],
+        (4,),
+        (*left, *right),
+        [specs[0]] * 3 + [specs[1]] * 3,
         outs,
         [whole(o) for o in outs],
         24,

time: 165 us -> 167 us (1.012)
  Pallas kernels: 68.4 us -> 71.1 us
    pallas_call x23, Pallas kernels: 68.4 us -> 71.1 us  [call(): pl.pallas_call(body, grid_spec=pltpu.PrefetchScalarGridSpec(num_scalar_pr...]
  transfers between devices with their start and end apart: 36 -> 36, of which waited for: 16 -> 17; matrix products, arithmetic and copies ran while one was open for 2% -> 2% of each run, Pallas kernels for 33% -> 32%
where the time goes in v12:
time: 167 us
  Pallas kernels  71.1 us (43%)
  starting transfers between devices  45.7 us (27%)
  waiting for transfers between devices  45.5 us (27%)
  other arithmetic  1.96 us (1%)
    pallas_call x23, Pallas kernels, call(): pl.pallas_call(body, grid_spec=pltpu.PrefetchScalarGridSpec(num_scalar_pr...  71.1 us
    ppermute x34, waiting for transfers between devices, send(): lax.ppermute(x, axis, [(i, i ^ by) for i in range(lax.axis_size(axis))])  44.6 us
    ppermute x34, starting transfers between devices, send(): lax.ppermute(x, axis, [(i, i ^ by) for i in range(lax.axis_size(axis))])  38.9 us
    ppermute x2, starting transfers between devices, across(): return lax.ppermute(x, ('c0', 'zl'), [(0, 3), (1, 2), (2, 1), (3, 0)])  6.75 us
  transfers between devices with their start and end apart: 36, of which 17 were waited for; matrix products, arithmetic and copies ran while one was open for 2% of the time, Pallas kernels for 32%

profile of v12, /device:TPU:0, one launch (start us, length us, event | category | flops | bytes accessed | tf_op | source)
XLA Modules:
  0.0 166.7 jit_solution(3885040939675891466)
XLA Ops:
  0.0 4.1 %collective-permute-start.1 = (bf16[512,768]{1,0:T(8,128)(2,1)}, bf16[512,768]{1,0:T(8,128)(2,1)S(1)}, u32[]{:S(2)}, u32[]{:S(2)}) collective-permute-start(bf16[512,768]{1,0:T(8,128)(2,1)} %refs_0_.2), channel_id=1, source_target_pairs={{0,66},{2,64},{64,2},{66,0},{1,67},{3,65},{65,3},{67,1},{4,70},{6,... | collective-permute-start | bytes 2359304 | tf_op jit(solution)/shard_map/ppermute | solution.py:27
  5.5 1.1 reduce-window.6
  7.0 1.6 collective-permute-start.3
  8.6 1.3 constant_dynamic-slice_fusion
  10.0 5.5 %project.3.refs_4_ = f32[3,512,512]{2,1,0:T(8,128)S(1)} custom-call(s32[6]{0:T(128)S(1)} %stack.27.s, bf16[512,768]{1,0:T(8,128)(2,1)S(1)} %copy-done, bf16[512,768]{1,0:T(8,128)(2,1)} %collective-permute-done.2.refs_1_, bf16[3,3072,1024]{2,1,0:T(8,128)(2,1)} %bitcast.31, bf16[3,3072,1024]{2,1,0:T(8,128)(2,1)} %bitcast.32), custom_call_target="tpu_custom_call" | custom-call | flops 1 | bytes 1 | tf_op jit(solution)/shard_map/project/pallas_call | solution.py:35
  15.5 8.6 %collective-permute-done.3.refs_10_.cum_ref = f32[8,512]{1,0:T(8,128)S(1)} collective-permute-done((f32[8,512]{1,0:T(8,128)S(1)}, f32[8,512]{1,0:T(8,128)S(1)}, u32[]{:S(2)}, u32[]{:S(2)}) %collective-permute-start.3) | collective-permute-done | bytes 16416 | tf_op jit(solution)/shard_map/ppermute | solution.py:23
  25.7 2.6 %collective-permute-start.5 = (bf16[256,768]{1,0:T(8,128)(2,1)S(1)}, bf16[256,768]{1,0:T(8,128)(2,1)S(1)}, u32[]{:S(2)}, u32[]{:S(2)}) collective-permute-start(bf16[256,768]{1,0:T(8,128)(2,1)S(1)} %get-tuple-element.133), channel_id=1, source_target_pairs={{0,66},{2,64},{64,2},{66,0},{1,67},{3,65},{65,3},{67,1},{4,70},{6,... | collective-permute-start | bytes 1179656 | tf_op jit(solution)/shard_map/ppermute | solution.py:27
  28.3 5.3 %project.4.qkv_ref = bf16[3,512,512]{2,1,0:T(8,128)(2,1)S(1)} custom-call(s32[6]{0:T(128)S(1)} %stack.27.s, bf16[512,768]{1,0:T(8,128)(2,1)S(1)} %collective-permute-done.b.refs_0_.refs_2_, bf16[512,768]{1,0:T(8,128)(2,1)S(1)} %collective-permute-done.7.refs_1_.refs_3_, bf16[3,3072,1024]{2,1,0:T(8,128)(2,1)} %bitcast.33, bf16[3,3072,1024]{2,1,0:T(8,128)(2,1)} %bitcast.34, ...), custom_call_target="tpu_custom_call" | custom-call | flops 1 | bytes 1 | tf_op jit(solution)/shard_map/project/pallas_call | solution.py:35
  33.6 3.2 %turn.2 = bf16[16,2,96,512]{3,2,1,0:T(8,128)(2,1)S(1)} custom-call(s32[6]{0:T(128)S(1)} %stack.27.s, bf16[512,768]{1,0:T(8,128)(2,1)S(1)} %copy-done, bf16[512,768]{1,0:T(8,128)(2,1)} %collective-permute-done.2.refs_1_, bf16[512,768]{1,0:T(8,128)(2,1)S(1)} %collective-permute-done.b.refs_0_.refs_2_, bf16[512,768]{1,0:T(8,128)(2,1)S(1)} %collective-permute-done.7.refs_1_.refs_3_), custom_call_target="tpu_custom_call" | custom-call | flops 1 | bytes 1 | tf_op jit(solution)/shard_map/turn/pallas_call | solution.py:35
  37.7 2.8 %collective-permute-start.8 = (bf16[512,512]{1,0:T(8,128)(2,1)S(1)}, bf16[512,512]{1,0:T(8,128)(2,1)S(1)}, u32[]{:S(2)}, u32[]{:S(2)}) collective-permute-start(bf16[512,512]{1,0:T(8,128)(2,1)S(1)} %get-tuple-element.142), channel_id=1, source_target_pairs={{0,64},{64,0},{1,65},{65,1},{2,66},{66,2},{3,67},{67,3},{4,68},{68... | collective-permute-start | bytes 1572872 | tf_op jit(solution)/shard_map/ppermute | solution.py:23
  41.0 2.3 %shard_states.2 = (bf16[528,128]{1,0:T(8,128)(2,1)S(1)}, bf16[528,128]{1,0:T(8,128)(2,1)S(1)}, bf16[528,128]{1,0:T(8,128)(2,1)S(1)}, bf16[528,128]{1,0:T(8,128)(2,1)S(1)}) custom-call(s32[6]{0:T(128)S(1)} %stack.27.s, bf16[3,512,512]{2,1,0:T(8,128)(2,1)S(1)} %project.4.qkv_ref, bf16[512,512]{1,0:T(8,128)(2,1)S(1)} %get-tuple-element.253.og_ref, ...), custom_call_target="tpu_custom_call" | custom-call | flops 1 | bytes 1 | tf_op jit(solution)/shard_map/shard_states/pallas_call | solution.py:35
  43.4 7.9 %project.5.qkv_ref = bf16[3,512,512]{2,1,0:T(8,128)(2,1)S(1)} custom-call(s32[6]{0:T(128)S(1)} %stack.27.s, bf16[512,768]{1,0:T(8,128)(2,1)S(1)} %collective-permute-done.1.a.refs_0_.refs_4_, bf16[512,768]{1,0:T(8,128)(2,1)S(1)} %collective-permute-done.6.refs_1_.refs_5_, bf16[256,768]{1,0:T(8,128)(2,1)S(1)} %collective-permute-done.4.refs_2_.refs_0_, ...), custom_call_target="tpu_custom_call" | custom-call | flops 1 | bytes 1 | tf_op jit(solution)/shard_map/project/pallas_call | solution.py:35
  52.1 2.3 %shard_states.3 = (bf16[528,128]{1,0:T(8,128)(2,1)S(1)}, bf16[528,128]{1,0:T(8,128)(2,1)S(1)}, bf16[528,128]{1,0:T(8,128)(2,1)S(1)}, bf16[528,128]{1,0:T(8,128)(2,1)S(1)}) custom-call(s32[6]{0:T(128)S(1)} %stack.27.s, bf16[3,512,512]{2,1,0:T(8,128)(2,1)S(1)} %project.5.qkv_ref, bf16[512,512]{1,0:T(8,128)(2,1)S(1)} %collective-permute-done.8.og_ref, ...), custom_call_target="tpu_custom_call" | custom-call | flops 1 | bytes 1 | tf_op jit(solution)/shard_map/shard_states/pallas_call | solution.py:35
  54.4 1.7 collective-permute-start.11
  56.0 2.2 %collective-permute-start.12 = (bf16[528,128]{1,0:T(8,128)(2,1)S(1)}, bf16[528,128]{1,0:T(8,128)(2,1)S(1)}, u32[]{:S(2)}, u32[]{:S(2)}) collective-permute-start(bf16[528,128]{1,0:T(8,128)(2,1)S(1)} %get-tuple-element.160), channel_id=1, source_target_pairs={{0,12},{4,8},{8,4},{12,0},{1,13},{5,9},{9,5},{13,1},{2,14},{6,10},... | collective-permute-start | bytes 405512 | tf_op jit(solution)/shard_map/ppermute | solution.py:23
  59.0 5.9 %local_grads.3 = (bf16[3,512,512]{2,1,0:T(8,128)(2,1)S(1)}, bf16[3,512,512]{2,1,0:T(8,128)(2,1)S(1)}) custom-call(s32[6]{0:T(128)S(1)} %stack.27.s, bf16[3,512,512]{2,1,0:T(8,128)(2,1)S(1)} %project.4.qkv_ref, bf16[512,512]{1,0:T(8,128)(2,1)S(1)} %get-tuple-element.253.og_ref, f32[8,512]{1,0:T(8,128)S(1)} %concatenate.7.refs_5_.cum_ref), custom_call_target="tpu_custom_call" | custom-call | flops 1 | bytes 1 | tf_op jit(solution)/shard_map/local_grads/pallas_call | solution.py:35
  65.9 3.1 %collective-permute-start.16 = (bf16[528,128]{1,0:T(8,128)(2,1)S(1)}, bf16[528,128]{1,0:T(8,128)(2,1)S(1)}, u32[]{:S(2)}, u32[]{:S(2)}) collective-permute-start(bf16[528,128]{1,0:T(8,128)(2,1)S(1)} %get-tuple-element.168.a), channel_id=1, source_target_pairs={{0,32},{16,48},{32,0},{48,16},{1,33},{17,49},{33,1},{49,17},{2,34}... | collective-permute-start | bytes 405512 | tf_op jit(solution)/shard_map/ppermute | solution.py:23
  69.0 1.1 collective-permute-start.15
  70.1 3.2 %local_grads.4 = (bf16[3,512,512]{2,1,0:T(8,128)(2,1)S(1)}, bf16[3,512,512]{2,1,0:T(8,128)(2,1)S(1)}) custom-call(s32[6]{0:T(128)S(1)} %stack.27.s, bf16[3,512,512]{2,1,0:T(8,128)(2,1)S(1)} %project.5.qkv_ref, bf16[512,512]{1,0:T(8,128)(2,1)S(1)} %collective-permute-done.8.og_ref, f32[8,512]{1,0:T(8,128)S(1)} %collective-permute-done.3.refs_10_.cum_ref), custom_call_target="tpu_custom_call" | custom-call | flops 1 | bytes 1 | tf_op jit(solution)/shard_map/local_grads/pallas_call | solution.py:35
  73.4 2.0 %turn.3 = bf16[16,2,96,512]{3,2,1,0:T(8,128)(2,1)S(1)} custom-call(s32[6]{0:T(128)S(1)} %stack.27.s, bf16[256,768]{1,0:T(8,128)(2,1)S(1)} %collective-permute-done.4.refs_2_.refs_0_, bf16[256,768]{1,0:T(8,128)(2,1)S(1)} %collective-permute-done.5.refs_3_.refs_1_, bf16[256,768]{1,0:T(8,128)(2,1)S(1)} %collective-permute-done.9.refs_4_.refs_2_, ...), custom_call_target="tpu_custom_call" | custom-call | flops 1 | bytes 1 | tf_op jit(solution)/shard_map/turn/pallas_call | solution.py:35
  76.3 1.0 collective-permute-start.17
  77.3 2.2 %collective-permute-start.18 = (bf16[512,128]{1,0:T(8,128)(2,1)S(1)}, bf16[512,128]{1,0:T(8,128)(2,1)S(1)}, u32[]{:S(2)}, u32[]{:S(2)}) collective-permute-start(bf16[512,128]{1,0:T(8,128)(2,1)S(1)} %get-tuple-element.187), channel_id=1, source_target_pairs={{0,12},{4,8},{8,4},{12,0},{1,13},{5,9},{9,5},{13,1},{2,14},{6,10},... | collective-permute-start | bytes 393224 | tf_op jit(solution)/shard_map/ppermute | solution.py:23
  79.4 1.0 collective-permute-start.19
  80.5 3.2 %local_grads.5 = (bf16[3,512,512]{2,1,0:T(8,128)(2,1)S(1)}, bf16[3,512,512]{2,1,0:T(8,128)(2,1)S(1)}) custom-call(s32[6]{0:T(128)S(1)} %stack.27.s, bf16[3,512,512]{2,1,0:T(8,128)(2,1)S(1)} %project.5.qkv_ref, bf16[512,512]{1,0:T(8,128)(2,1)S(1)} %collective-permute-done.8.og_ref, ...), custom_call_target="tpu_custom_call", output_to_operand_aliasing={{0}: (4, {}), {1}: (5, {})} | custom-call | flops 1 | bytes 1 | tf_op jit(solution)/shard_map/local_grads/pallas_call | solution.py:35
  84.2 1.8 %collective-permute-done.19.c = bf16[512,128]{1,0:T(8,128)(2,1)S(1)} collective-permute-done((bf16[512,128]{1,0:T(8,128)(2,1)S(1)}, bf16[512,128]{1,0:T(8,128)(2,1)S(1)}, u32[]{:S(2)}, u32[]{:S(2)}) %collective-permute-start.19) | collective-permute-done | bytes 131104 | tf_op jit(solution)/shard_map/ppermute | solution.py:23
  85.9 4.4 %whole_grads.1 = (bf16[512,768]{1,0:T(8,128)(2,1)S(1)}, bf16[512,768]{1,0:T(8,128)(2,1)S(1)}, bf16[512,768]{1,0:T(8,128)(2,1)S(1)}, bf16[512,768]{1,0:T(8,128)(2,1)S(1)}) custom-call(s32[6]{0:T(128)S(1)} %stack.27.s, bf16[3,512,512]{2,1,0:T(8,128)(2,1)S(1)} %get-tuple-element.200.local_a, bf16[3,512,512]{2,1,0:T(8,128)(2,1)S(1)} %get-tuple-element.201.ready_a, ...), custom_call_target="tpu_custom_call" | custom-call | flops 1 | bytes 1 | tf_op jit(solution)/shard_map/whole_grads/pallas_call | solution.py:35
  90.4 4.9 %weight_part.3 = (bf16[384,768]{1,0:T(8,128)(2,1)S(1)}, bf16[384,768]{1,0:T(8,128)(2,1)S(1)}, bf16[384,768]{1,0:T(8,128)(2,1)S(1)}, bf16[384,768]{1,0:T(8,128)(2,1)S(1)}) custom-call(s32[6]{0:T(128)S(1)} %stack.27.s, bf16[4,4,192,512]{3,2,1,0:T(8,128)(2,1)S(1)} %bitcast.19, bf16[4,4,192,512]{3,2,1,0:T(8,128)(2,1)S(1)} %bitcast.20, ...), custom_call_target="tpu_custom_call" | custom-call | flops 1 | bytes 1 | tf_op jit(solution)/shard_map/weight_part/pallas_call | solution.py:35
  95.2 2.2 %collective-permute-start.21 = (bf16[384,768]{1,0:T(8,128)(2,1)S(1)}, bf16[384,768]{1,0:T(8,128)(2,1)S(1)}, u32[]{:S(2)}, u32[]{:S(2)}) collective-permute-start(bf16[384,768]{1,0:T(8,128)(2,1)S(1)} %get-tuple-element.215), channel_id=1, source_target_pairs={{0,48},{16,32},{32,16},{48,0},{1,49},{17,33},{33,17},{49,1},{2,50}... | collective-permute-start | bytes 1769480 | tf_op jit(solution)/shard_map/ppermute | solution.py:23
  97.4 1.4 collective-permute-start.20
  100.4 8.4 %weight_part.4 = (bf16[768,768]{1,0:T(8,128)(2,1)S(1)}, bf16[768,768]{1,0:T(8,128)(2,1)S(1)}, bf16[768,768]{1,0:T(8,128)(2,1)S(1)}, bf16[768,768]{1,0:T(8,128)(2,1)S(1)}) custom-call(s32[6]{0:T(128)S(1)} %stack.27.s, bf16[4,4,192,512]{3,2,1,0:T(8,128)(2,1)S(1)} %bitcast.21, bf16[4,4,192,512]{3,2,1,0:T(8,128)(2,1)S(1)} %bitcast.22, ...), custom_call_target="tpu_custom_call" | custom-call | flops 1 | bytes 1 | tf_op jit(solution)/shard_map/weight_part/pallas_call | solution.py:35
  110.1 1.0 collective-permute-start.22
  111.8 1.2 collective-permute-start.23
  113.9 1.2 collective-permute-start.27
  115.3 3.2 %weight_part.5 = (bf16[768,768]{1,0:T(8,128)(2,1)S(1)}, bf16[768,768]{1,0:T(8,128)(2,1)S(1)}) custom-call(s32[6]{0:T(128)S(1)} %stack.27.s, bf16[4,4,192,512]{3,2,1,0:T(8,128)(2,1)S(1)} %bitcast.23, bf16[4,4,192,512]{3,2,1,0:T(8,128)(2,1)S(1)} %bitcast.24, bf16[4,4,192,512]{3,2,1,0:T(8,128)(2,1)S(1)} %bitcast.29, bf16[4,4,192,512]{3,2,1,0:T(8,128)(2,1)S(1)} %bitcast.30, ...), custom_call_target="tpu_custom_call" | custom-call | flops 1 | bytes 1 | tf_op jit(solution)/shard_map/weight_part/pallas_call | solution.py:35
  118.4 17.6 %collective-permute-done.23.refs_2_ = bf16[768,768]{1,0:T(8,128)(2,1)S(1)} collective-permute-done((bf16[768,768]{1,0:T(8,128)(2,1)S(1)}, bf16[768,768]{1,0:T(8,128)(2,1)S(1)}, u32[]{:S(2)}, u32[]{:S(2)}) %collective-permute-start.23) | collective-permute-done | bytes 1179680 | tf_op jit(solution)/shard_map/ppermute | solution.py:23
  136.0 2.2 %collective-permute-done.27.refs_5_ = bf16[768,768]{1,0:T(8,128)(2,1)S(1)} collective-permute-done((bf16[768,768]{1,0:T(8,128)(2,1)S(1)}, bf16[768,768]{1,0:T(8,128)(2,1)S(1)}, u32[]{:S(2)}, u32[]{:S(2)}) %collective-permute-start.27) | collective-permute-done | bytes 1179680 | tf_op jit(solution)/shard_map/ppermute | solution.py:23
  138.9 2.3 %cut_blocks.1 = (bf16[192,768]{1,0:T(8,128)(2,1)S(1)}, bf16[192,768]{1,0:T(8,128)(2,1)S(1)}, bf16[192,768]{1,0:T(8,128)(2,1)S(1)}, bf16[192,768]{1,0:T(8,128)(2,...) custom-call(s32[6]{0:T(128)S(1)} %stack.27.s, ...), custom_call_target="tpu_custom_call" | custom-call | flops 1 | bytes 1 | tf_op jit(solution)/shard_map/cut_blocks/pallas_call | solution.py:35
  141.6 1.8 %collective-permute-start.29 = (bf16[192,768]{1,0:T(8,128)(2,1)S(1)}, bf16[192,768]{1,0:T(8,128)(2,1)S(1)}, u32[]{:S(2)}, u32[]{:S(2)}) collective-permute-start(bf16[192,768]{1,0:T(8,128)(2,1)S(1)} %get-tuple-element.240), channel_id=1, source_target_pairs={{0,12},{4,8},{8,4},{12,0},{1,13},{5,9},{9,5},{13,1},{2,14},{6,10},... | collective-permute-start | bytes 884744 | tf_op jit(solution)/shard_map/ppermute | solution.py:23
  143.4 2.0 %collective-permute-start.30 = (bf16[192,768]{1,0:T(8,128)(2,1)S(1)}, bf16[192,768]{1,0:T(8,128)(2,1)S(1)}, u32[]{:S(2)}, u32[]{:S(2)}) collective-permute-start(bf16[192,768]{1,0:T(8,128)(2,1)S(1)} %get-tuple-element.241), channel_id=1, source_target_pairs={{0,8},{4,12},{8,0},{12,4},{1,9},{5,13},{9,1},{13,5},{2,10},{6,14},... | collective-permute-start | bytes 884744 | tf_op jit(solution)/shard_map/ppermute | solution.py:23
  145.4 1.1 collective-permute-start.31
  146.5 1.0 collective-permute-start.32
  148.4 1.2 collective-permute-start.33
  149.6 3.4 %collective-permute-done.29.c = bf16[192,768]{1,0:T(8,128)(2,1)S(1)} collective-permute-done((bf16[192,768]{1,0:T(8,128)(2,1)S(1)}, bf16[192,768]{1,0:T(8,128)(2,1)S(1)}, u32[]{:S(2)}, u32[]{:S(2)}) %collective-permute-start.29) | collective-permute-done | bytes 294944 | tf_op jit(solution)/shard_map/ppermute | solution.py:23
  153.7 1.8 %collective-permute-start.34 = (bf16[96,768]{1,0:T(8,128)(2,1)S(1)}, bf16[96,768]{1,0:T(8,128)(2,1)S(1)}, u32[]{:S(2)}, u32[]{:S(2)}) collective-permute-start(bf16[96,768]{1,0:T(8,128)(2,1)S(1)} %get-tuple-element.251), channel_id=1, source_target_pairs={{0,64},{64,0},{1,65},{65,1},{2,66},{66,2},{3,67},{67,3},{4,68},{68... | collective-permute-start | bytes 442376 | tf_op jit(solution)/shard_map/ppermute | solution.py:23
  155.6 2.1 %collective-permute-done.32.c = bf16[192,768]{1,0:T(8,128)(2,1)S(1)} collective-permute-done((bf16[192,768]{1,0:T(8,128)(2,1)S(1)}, bf16[192,768]{1,0:T(8,128)(2,1)S(1)}, u32[]{:S(2)}, u32[]{:S(2)}) %collective-permute-start.32) | collective-permute-done | bytes 294944 | tf_op jit(solution)/shard_map/ppermute | solution.py:23
  158.3 2.0 %collective-permute-start.35 = (bf16[96,768]{1,0:T(8,128)(2,1)S(1)}, bf16[96,768]{1,0:T(8,128)(2,1)S(1)}, u32[]{:S(2)}, u32[]{:S(2)}) collective-permute-start(bf16[96,768]{1,0:T(8,128)(2,1)S(1)} %get-tuple-element.252), channel_id=1, source_target_pairs={{0,64},{64,0},{1,65},{65,1},{2,66},{66,2},{3,67},{67,3},{4,68},{68... | collective-permute-start | bytes 442376 | tf_op jit(solution)/shard_map/ppermute | solution.py:23
  160.4 4.6 %collective-permute-done.35.refs_3_ = bf16[96,768]{1,0:T(8,128)(2,1)S(1)} collective-permute-done((bf16[96,768]{1,0:T(8,128)(2,1)S(1)}, bf16[96,768]{1,0:T(8,128)(2,1)S(1)}, u32[]{:S(2)}, u32[]{:S(2)}) %collective-permute-start.35) | collective-permute-done | bytes 147488 | tf_op jit(solution)/shard_map/ppermute | solution.py:23
  165.0 1.6 finish.1
  (61 shorter events, 16.0 us)
Async XLA Ops:
  0.0 10.0 %collective-permute-start.2 = (bf16[512,768]{1,0:T(8,128)(2,1)}, bf16[512,768]{1,0:T(8,128)(2,1)}, u32[]{:S(2)}, u32[]{:S(2)}) collective-permute-start(bf16[512,768]{1,0:T(8,128)(2,1)} %refs_0_.2), channel_id=1, source_target_pairs={{0,1},{1,0},{2,3},{3,2},{4,5},{5,4},{6,7},{7,6},{8,9},{9,8},{10,11... | collective-permute-start | bytes 2359304 | tf_op jit(solution)/shard_map/ppermute | solution.py:23
  0.0 24.1 %collective-permute-start.1 = (bf16[512,768]{1,0:T(8,128)(2,1)}, bf16[512,768]{1,0:T(8,128)(2,1)S(1)}, u32[]{:S(2)}, u32[]{:S(2)}) collective-permute-start(bf16[512,768]{1,0:T(8,128)(2,1)} %refs_0_.2), channel_id=1, source_target_pairs={{0,66},{2,64},{64,2},{66,0},{1,67},{3,65},{65,3},{67,1},{4,70},{6,... | collective-permute-start | bytes 2359304 | tf_op jit(solution)/shard_map/ppermute | solution.py:27
  4.1 20.1 %collective-permute-start = (bf16[512,768]{1,0:T(8,128)(2,1)}, bf16[512,768]{1,0:T(8,128)(2,1)S(1)}, u32[]{:S(2)}, u32[]{:S(2)}) collective-permute-start(bf16[512,768]{1,0:T(8,128)(2,1)} %refs_0_.2), channel_id=1, source_target_pairs={{0,2},{2,0},{1,3},{3,1},{4,6},{6,4},{5,7},{7,5},{8,10},{10,8},{9,1... | collective-permute-start | bytes 2359304 | tf_op jit(solution)/shard_map/ppermute | solution.py:23
  5.5 4.5 %copy-start = (bf16[512,768]{1,0:T(8,128)(2,1)S(1)}, bf16[512,768]{1,0:T(8,128)(2,1)}, u32[]{:S(2)}) copy-start(bf16[512,768]{1,0:T(8,128)(2,1)} %refs_0_.2) | copy-start | bytes 2359300
  7.0 17.1 %collective-permute-start.3 = (f32[8,512]{1,0:T(8,128)S(1)}, f32[8,512]{1,0:T(8,128)S(1)}, u32[]{:S(2)}, u32[]{:S(2)}) collective-permute-start(f32[8,512]{1,0:T(8,128)S(1)} %concatenate.6), channel_id=1, source_target_pairs={{0,64},{64,0},{1,65},{65,1},{2,66},{66,2},{3,67},{67,3},{4,68},{68... | collective-permute-start | bytes 49160 | tf_op jit(solution)/shard_map/ppermute | solution.py:23
  24.2 4.1 %collective-permute-start.7 = (bf16[512,768]{1,0:T(8,128)(2,1)S(1)}, bf16[512,768]{1,0:T(8,128)(2,1)S(1)}, u32[]{:S(2)}, u32[]{:S(2)}) collective-permute-start(bf16[512,768]{1,0:T(8,128)(2,1)S(1)} %collective-permute-done.b.refs_0_.refs_2_), channel_id=1, source_target_pairs={{0,1},{1,0},{2,3},{3,2},{4,5},{5,4},{6,7},{7,6},{8,9},{9,8},{10,11... | collective-permute-start | bytes 2359304 | tf_op jit(solution)/shard_map/ppermute | solution.py:23
  24.2 13.5 %collective-permute-start.6 = (bf16[512,768]{1,0:T(8,128)(2,1)S(1)}, bf16[512,768]{1,0:T(8,128)(2,1)S(1)}, u32[]{:S(2)}, u32[]{:S(2)}) collective-permute-start(bf16[512,768]{1,0:T(8,128)(2,1)S(1)} %collective-permute-done.1.a.refs_0_.refs_4_), channel_id=1, source_target_pairs={{0,1},{1,0},{2,3},{3,2},{4,5},{5,4},{6,7},{7,6},{8,9},{9,8},{10,11... | collective-permute-start | bytes 2359304 | tf_op jit(solution)/shard_map/ppermute | solution.py:23
  25.3 11.5 %collective-permute-start.4 = (bf16[256,768]{1,0:T(8,128)(2,1)S(1)}, bf16[256,768]{1,0:T(8,128)(2,1)S(1)}, u32[]{:S(2)}, u32[]{:S(2)}) collective-permute-start(bf16[256,768]{1,0:T(8,128)(2,1)S(1)} %get-tuple-element.132), channel_id=1, source_target_pairs={{0,2},{2,0},{1,3},{3,1},{4,6},{6,4},{5,7},{7,5},{8,10},{10,8},{9,1... | collective-permute-start | bytes 1179656 | tf_op jit(solution)/shard_map/ppermute | solution.py:23
  25.7 12.0 %collective-permute-start.5 = (bf16[256,768]{1,0:T(8,128)(2,1)S(1)}, bf16[256,768]{1,0:T(8,128)(2,1)S(1)}, u32[]{:S(2)}, u32[]{:S(2)}) collective-permute-start(bf16[256,768]{1,0:T(8,128)(2,1)S(1)} %get-tuple-element.133), channel_id=1, source_target_pairs={{0,66},{2,64},{64,2},{66,0},{1,67},{3,65},{65,3},{67,1},{4,70},{6,... | collective-permute-start | bytes 1179656 | tf_op jit(solution)/shard_map/ppermute | solution.py:27
  37.7 14.4 %collective-permute-start.8 = (bf16[512,512]{1,0:T(8,128)(2,1)S(1)}, bf16[512,512]{1,0:T(8,128)(2,1)S(1)}, u32[]{:S(2)}, u32[]{:S(2)}) collective-permute-start(bf16[512,512]{1,0:T(8,128)(2,1)S(1)} %get-tuple-element.142), channel_id=1, source_target_pairs={{0,64},{64,0},{1,65},{65,1},{2,66},{66,2},{3,67},{67,3},{4,68},{68... | collective-permute-start | bytes 1572872 | tf_op jit(solution)/shard_map/ppermute | solution.py:23
  40.5 2.8 %collective-permute-start.9 = (bf16[256,768]{1,0:T(8,128)(2,1)S(1)}, bf16[256,768]{1,0:T(8,128)(2,1)S(1)}, u32[]{:S(2)}, u32[]{:S(2)}) collective-permute-start(bf16[256,768]{1,0:T(8,128)(2,1)S(1)} %collective-permute-done.4.refs_2_.refs_0_), channel_id=1, source_target_pairs={{0,1},{1,0},{2,3},{3,2},{4,5},{5,4},{6,7},{7,6},{8,9},{9,8},{10,11... | collective-permute-start | bytes 1179656 | tf_op jit(solution)/shard_map/ppermute | solution.py:23
  40.5 2.8 %collective-permute-start.10 = (bf16[256,768]{1,0:T(8,128)(2,1)S(1)}, bf16[256,768]{1,0:T(8,128)(2,1)S(1)}, u32[]{:S(2)}, u32[]{:S(2)}) collective-permute-start(bf16[256,768]{1,0:T(8,128)(2,1)S(1)} %collective-permute-done.5.refs_3_.refs_1_), channel_id=1, source_target_pairs={{0,1},{1,0},{2,3},{3,2},{4,5},{5,4},{6,7},{7,6},{8,9},{9,8},{10,11... | collective-permute-start | bytes 1179656 | tf_op jit(solution)/shard_map/ppermute | solution.py:23
  54.4 10.4 %collective-permute-start.11 = (bf16[528,128]{1,0:T(8,128)(2,1)S(1)}, bf16[528,128]{1,0:T(8,128)(2,1)S(1)}, u32[]{:S(2)}, u32[]{:S(2)}) collective-permute-start(bf16[528,128]{1,0:T(8,128)(2,1)S(1)} %get-tuple-element.159), channel_id=1, source_target_pairs={{0,4},{4,0},{8,12},{12,8},{1,5},{5,1},{9,13},{13,9},{2,6},{6,2},{1... | collective-permute-start | bytes 405512 | tf_op jit(solution)/shard_map/ppermute | solution.py:23
  56.0 9.1 %collective-permute-start.12 = (bf16[528,128]{1,0:T(8,128)(2,1)S(1)}, bf16[528,128]{1,0:T(8,128)(2,1)S(1)}, u32[]{:S(2)}, u32[]{:S(2)}) collective-permute-start(bf16[528,128]{1,0:T(8,128)(2,1)S(1)} %get-tuple-element.160), channel_id=1, source_target_pairs={{0,12},{4,8},{8,4},{12,0},{1,13},{5,9},{9,5},{13,1},{2,14},{6,10},... | collective-permute-start | bytes 405512 | tf_op jit(solution)/shard_map/ppermute | solution.py:23
  58.2 6.9 %collective-permute-start.13 = (bf16[528,128]{1,0:T(8,128)(2,1)S(1)}, bf16[528,128]{1,0:T(8,128)(2,1)S(1)}, u32[]{:S(2)}, u32[]{:S(2)}) collective-permute-start(bf16[528,128]{1,0:T(8,128)(2,1)S(1)} %get-tuple-element.161), channel_id=1, source_target_pairs={{0,8},{4,12},{8,0},{12,4},{1,9},{5,13},{9,1},{13,5},{2,10},{6,14},... | collective-permute-start | bytes 405512 | tf_op jit(solution)/shard_map/ppermute | solution.py:23
  65.9 9.5 %collective-permute-start.16 = (bf16[528,128]{1,0:T(8,128)(2,1)S(1)}, bf16[528,128]{1,0:T(8,128)(2,1)S(1)}, u32[]{:S(2)}, u32[]{:S(2)}) collective-permute-start(bf16[528,128]{1,0:T(8,128)(2,1)S(1)} %get-tuple-element.168.a), channel_id=1, source_target_pairs={{0,32},{16,48},{32,0},{48,16},{1,33},{17,49},{33,1},{49,17},{2,34}... | collective-permute-start | bytes 405512 | tf_op jit(solution)/shard_map/ppermute | solution.py:23
  69.0 6.4 %collective-permute-start.15 = (bf16[528,128]{1,0:T(8,128)(2,1)S(1)}, bf16[528,128]{1,0:T(8,128)(2,1)S(1)}, u32[]{:S(2)}, u32[]{:S(2)}) collective-permute-start(bf16[528,128]{1,0:T(8,128)(2,1)S(1)} %get-tuple-element.168.a), channel_id=1, source_target_pairs={{0,48},{16,32},{32,16},{48,0},{1,49},{17,33},{33,17},{49,1},{2,50}... | collective-permute-start | bytes 405512 | tf_op jit(solution)/shard_map/ppermute | solution.py:23
  70.1 5.3 %collective-permute-start.14 = (bf16[528,128]{1,0:T(8,128)(2,1)S(1)}, bf16[528,128]{1,0:T(8,128)(2,1)S(1)}, u32[]{:S(2)}, u32[]{:S(2)}) collective-permute-start(bf16[528,128]{1,0:T(8,128)(2,1)S(1)} %get-tuple-element.168.a), channel_id=1, source_target_pairs={{0,16},{16,0},{32,48},{48,32},{1,17},{17,1},{33,49},{49,33},{2,18}... | collective-permute-start | bytes 405512 | tf_op jit(solution)/shard_map/ppermute | solution.py:23
  76.3 7.4 %collective-permute-start.17 = (bf16[512,128]{1,0:T(8,128)(2,1)S(1)}, bf16[512,128]{1,0:T(8,128)(2,1)S(1)}, u32[]{:S(2)}, u32[]{:S(2)}) collective-permute-start(bf16[512,128]{1,0:T(8,128)(2,1)S(1)} %get-tuple-element.186), channel_id=1, source_target_pairs={{0,4},{4,0},{8,12},{12,8},{1,5},{5,1},{9,13},{13,9},{2,6},{6,2},{1... | collective-permute-start | bytes 393224 | tf_op jit(solution)/shard_map/ppermute | solution.py:23
  77.3 6.9 %collective-permute-start.18 = (bf16[512,128]{1,0:T(8,128)(2,1)S(1)}, bf16[512,128]{1,0:T(8,128)(2,1)S(1)}, u32[]{:S(2)}, u32[]{:S(2)}) collective-permute-start(bf16[512,128]{1,0:T(8,128)(2,1)S(1)} %get-tuple-element.187), channel_id=1, source_target_pairs={{0,12},{4,8},{8,4},{12,0},{1,13},{5,9},{9,5},{13,1},{2,14},{6,10},... | collective-permute-start | bytes 393224 | tf_op jit(solution)/shard_map/ppermute | solution.py:23
  79.4 6.5 %collective-permute-start.19 = (bf16[512,128]{1,0:T(8,128)(2,1)S(1)}, bf16[512,128]{1,0:T(8,128)(2,1)S(1)}, u32[]{:S(2)}, u32[]{:S(2)}) collective-permute-start(bf16[512,128]{1,0:T(8,128)(2,1)S(1)} %get-tuple-element.188), channel_id=1, source_target_pairs={{0,8},{4,12},{8,0},{12,4},{1,9},{5,13},{9,1},{13,5},{2,10},{6,14},... | collective-permute-start | bytes 393224 | tf_op jit(solution)/shard_map/ppermute | solution.py:23
  95.2 13.9 %collective-permute-start.21 = (bf16[384,768]{1,0:T(8,128)(2,1)S(1)}, bf16[384,768]{1,0:T(8,128)(2,1)S(1)}, u32[]{:S(2)}, u32[]{:S(2)}) collective-permute-start(bf16[384,768]{1,0:T(8,128)(2,1)S(1)} %get-tuple-element.215), channel_id=1, source_target_pairs={{0,48},{16,32},{32,16},{48,0},{1,49},{17,33},{33,17},{49,1},{2,50}... | collective-permute-start | bytes 1769480 | tf_op jit(solution)/shard_map/ppermute | solution.py:23
  97.4 11.7 %collective-permute-start.20 = (bf16[384,768]{1,0:T(8,128)(2,1)S(1)}, bf16[384,768]{1,0:T(8,128)(2,1)S(1)}, u32[]{:S(2)}, u32[]{:S(2)}) collective-permute-start(bf16[384,768]{1,0:T(8,128)(2,1)S(1)} %get-tuple-element.211), channel_id=1, source_target_pairs={{0,16},{16,0},{32,48},{48,32},{1,17},{17,1},{33,49},{49,33},{2,18}... | collective-permute-start | bytes 1769480 | tf_op jit(solution)/shard_map/ppermute | solution.py:23
  98.8 12.2 %collective-permute-start.24 = (bf16[384,768]{1,0:T(8,128)(2,1)S(1)}, bf16[384,768]{1,0:T(8,128)(2,1)S(1)}, u32[]{:S(2)}, u32[]{:S(2)}) collective-permute-start(bf16[384,768]{1,0:T(8,128)(2,1)S(1)} %get-tuple-element.224), channel_id=1, source_target_pairs={{0,4},{4,0},{8,12},{12,8},{1,5},{5,1},{9,13},{13,9},{2,6},{6,2},{1... | collective-permute-start | bytes 1769480 | tf_op jit(solution)/shard_map/ppermute | solution.py:23
  99.5 12.3 %collective-permute-start.25 = (bf16[384,768]{1,0:T(8,128)(2,1)S(1)}, bf16[384,768]{1,0:T(8,128)(2,1)S(1)}, u32[]{:S(2)}, u32[]{:S(2)}) collective-permute-start(bf16[384,768]{1,0:T(8,128)(2,1)S(1)} %get-tuple-element.225), channel_id=1, source_target_pairs={{0,12},{4,8},{8,4},{12,0},{1,13},{5,9},{9,5},{13,1},{2,14},{6,10},... | collective-permute-start | bytes 1769480 | tf_op jit(solution)/shard_map/ppermute | solution.py:23
  110.1 26.0 %collective-permute-start.22 = (bf16[768,768]{1,0:T(8,128)(2,1)S(1)}, bf16[768,768]{1,0:T(8,128)(2,1)S(1)}, u32[]{:S(2)}, u32[]{:S(2)}) collective-permute-start(bf16[768,768]{1,0:T(8,128)(2,1)S(1)} %get-tuple-element.220), channel_id=1, source_target_pairs={{0,16},{16,0},{32,48},{48,32},{1,17},{17,1},{33,49},{49,33},{2,18}... | collective-permute-start | bytes 3538952 | tf_op jit(solution)/shard_map/ppermute | solution.py:23
  111.8 24.2 %collective-permute-start.23 = (bf16[768,768]{1,0:T(8,128)(2,1)S(1)}, bf16[768,768]{1,0:T(8,128)(2,1)S(1)}, u32[]{:S(2)}, u32[]{:S(2)}) collective-permute-start(bf16[768,768]{1,0:T(8,128)(2,1)S(1)} %get-tuple-element.221), channel_id=1, source_target_pairs={{0,48},{16,32},{32,16},{48,0},{1,49},{17,33},{33,17},{49,1},{2,50}... | collective-permute-start | bytes 3538952 | tf_op jit(solution)/shard_map/ppermute | solution.py:23
  113.9 24.3 %collective-permute-start.27 = (bf16[768,768]{1,0:T(8,128)(2,1)S(1)}, bf16[768,768]{1,0:T(8,128)(2,1)S(1)}, u32[]{:S(2)}, u32[]{:S(2)}) collective-permute-start(bf16[768,768]{1,0:T(8,128)(2,1)S(1)} %get-tuple-element.237), channel_id=1, source_target_pairs={{0,12},{4,8},{8,4},{12,0},{1,13},{5,9},{9,5},{13,1},{2,14},{6,10},... | collective-permute-start | bytes 3538952 | tf_op jit(solution)/shard_map/ppermute | solution.py:23
  115.1 23.8 %collective-permute-start.26 = (bf16[768,768]{1,0:T(8,128)(2,1)S(1)}, bf16[768,768]{1,0:T(8,128)(2,1)S(1)}, u32[]{:S(2)}, u32[]{:S(2)}) collective-permute-start(bf16[768,768]{1,0:T(8,128)(2,1)S(1)} %get-tuple-element.228), channel_id=1, source_target_pairs={{0,4},{4,0},{8,12},{12,8},{1,5},{5,1},{9,13},{13,9},{2,6},{6,2},{1... | collective-permute-start | bytes 3538952 | tf_op jit(solution)/shard_map/ppermute | solution.py:23
  141.2 7.2 %collective-permute-start.28 = (bf16[192,768]{1,0:T(8,128)(2,1)S(1)}, bf16[192,768]{1,0:T(8,128)(2,1)S(1)}, u32[]{:S(2)}, u32[]{:S(2)}) collective-permute-start(bf16[192,768]{1,0:T(8,128)(2,1)S(1)} %get-tuple-element.239), channel_id=1, source_target_pairs={{0,4},{4,0},{8,12},{12,8},{1,5},{5,1},{9,13},{13,9},{2,6},{6,2},{1... | collective-permute-start | bytes 884744 | tf_op jit(solution)/shard_map/ppermute | solution.py:23
  141.6 11.4 %collective-permute-start.29 = (bf16[192,768]{1,0:T(8,128)(2,1)S(1)}, bf16[192,768]{1,0:T(8,128)(2,1)S(1)}, u32[]{:S(2)}, u32[]{:S(2)}) collective-permute-start(bf16[192,768]{1,0:T(8,128)(2,1)S(1)} %get-tuple-element.240), channel_id=1, source_target_pairs={{0,12},{4,8},{8,4},{12,0},{1,13},{5,9},{9,5},{13,1},{2,14},{6,10},... | collective-permute-start | bytes 884744 | tf_op jit(solution)/shard_map/ppermute | solution.py:23
  143.4 9.7 %collective-permute-start.30 = (bf16[192,768]{1,0:T(8,128)(2,1)S(1)}, bf16[192,768]{1,0:T(8,128)(2,1)S(1)}, u32[]{:S(2)}, u32[]{:S(2)}) collective-permute-start(bf16[192,768]{1,0:T(8,128)(2,1)S(1)} %get-tuple-element.241), channel_id=1, source_target_pairs={{0,8},{4,12},{8,0},{12,4},{1,9},{5,13},{9,1},{13,5},{2,10},{6,14},... | collective-permute-start | bytes 884744 | tf_op jit(solution)/shard_map/ppermute | solution.py:23
  145.4 10.2 %collective-permute-start.31 = (bf16[192,768]{1,0:T(8,128)(2,1)S(1)}, bf16[192,768]{1,0:T(8,128)(2,1)S(1)}, u32[]{:S(2)}, u32[]{:S(2)}) collective-permute-start(bf16[192,768]{1,0:T(8,128)(2,1)S(1)} %get-tuple-element.244), channel_id=1, source_target_pairs={{0,16},{16,0},{32,48},{48,32},{1,17},{17,1},{33,49},{49,33},{2,18}... | collective-permute-start | bytes 884744 | tf_op jit(solution)/shard_map/ppermute | solution.py:23
  146.5 11.1 %collective-permute-start.32 = (bf16[192,768]{1,0:T(8,128)(2,1)S(1)}, bf16[192,768]{1,0:T(8,128)(2,1)S(1)}, u32[]{:S(2)}, u32[]{:S(2)}) collective-permute-start(bf16[192,768]{1,0:T(8,128)(2,1)S(1)} %get-tuple-element.245), channel_id=1, source_target_pairs={{0,48},{16,32},{32,16},{48,0},{1,49},{17,33},{33,17},{49,1},{2,50}... | collective-permute-start | bytes 884744 | tf_op jit(solution)/shard_map/ppermute | solution.py:23
  148.4 9.2 %collective-permute-start.33 = (bf16[192,768]{1,0:T(8,128)(2,1)S(1)}, bf16[192,768]{1,0:T(8,128)(2,1)S(1)}, u32[]{:S(2)}, u32[]{:S(2)}) collective-permute-start(bf16[192,768]{1,0:T(8,128)(2,1)S(1)} %get-tuple-element.246), channel_id=1, source_target_pairs={{0,32},{16,48},{32,0},{48,16},{1,33},{17,49},{33,1},{49,17},{2,34}... | collective-permute-start | bytes 884744 | tf_op jit(solution)/shard_map/ppermute | solution.py:23
  153.7 6.7 %collective-permute-start.34 = (bf16[96,768]{1,0:T(8,128)(2,1)S(1)}, bf16[96,768]{1,0:T(8,128)(2,1)S(1)}, u32[]{:S(2)}, u32[]{:S(2)}) collective-permute-start(bf16[96,768]{1,0:T(8,128)(2,1)S(1)} %get-tuple-element.251), channel_id=1, source_target_pairs={{0,64},{64,0},{1,65},{65,1},{2,66},{66,2},{3,67},{67,3},{4,68},{68... | collective-permute-start | bytes 442376 | tf_op jit(solution)/shard_map/ppermute | solution.py:23
  158.3 6.7 %collective-permute-start.35 = (bf16[96,768]{1,0:T(8,128)(2,1)S(1)}, bf16[96,768]{1,0:T(8,128)(2,1)S(1)}, u32[]{:S(2)}, u32[]{:S(2)}) collective-permute-start(bf16[96,768]{1,0:T(8,128)(2,1)S(1)} %get-tuple-element.252), channel_id=1, source_target_pairs={{0,64},{64,0},{1,65},{65,1},{2,66},{66,2},{3,67},{67,3},{4,68},{68... | collective-permute-start | bytes 442376 | tf_op jit(solution)/shard_map/ppermute | solution.py:23

commit v13 on v11

--- a/solution.py
+++ b/solution.py
@@ -606,11 +606,11 @@
     og_pair, qkv_pair = tied((og_pair, qkv_pair))
 
     to_y = shard_states(table, qkv_pair, og_pair, note, 1, to_y)
-    at_y = [send(to_y[r], "c2", r) for r in (1, 3, 2)]
+    at_y = [send(to_y[r], "c2", r) for r in (2, 1, 3)]
     qkv_own, _ = tied((qkv_own, to_y[0]))
     local_own = local_grads(table, qkv_own, og_own, info, 0, per, None)
     at_y, local_own = tied((at_y, local_own))
-    before, after, prior, later, ring = ring_y(table, [to_y[0], at_y[0], at_y[2], at_y[1]])
+    before, after, prior, later, ring = ring_y(table, [to_y[0], at_y[1], at_y[0], at_y[2]])
     at_x = [send(ring, "c1", r) for r in (1, 3, 2)]
     qkv_pair, _ = tied((qkv_pair, ring))
     local = local_grads(table, qkv_pair, og_pair, note, 0, per // 2, None)
@@ -618,11 +618,11 @@
     turned.append(turn(table, second))
     at_x, local, turned = tied((at_x, local, turned))
     back = arrivals(table, [ring, at_x[0], at_x[2], at_x[1]], before, after, prior, later)
-    states = [send(back[r], "c2", r) for r in (1, 3, 2)]
+    states = [send(back[r], "c2", r) for r in (2, 1, 3)]
     local, _ = tied((local, back[0]))
     local = local_grads(table, qkv_pair, og_pair, note, per // 2, per // 2, local)
     states, turned, local = tied((states, turned, local))
-    states = [back[0], states[0], states[2], states[1]]
+    states = [back[0], states[1], states[0], states[2]]
 
     left_own, right_own, left_pair, right_pair = whole_grads(table, local_own, local, states)
     lefts, rights = (left_own, left_pair), (right_own, right_pair)

time: 165 us -> 164 us (level)
  transfers between devices with their start and end apart: 36 -> 36, of which waited for: 16 -> 17; matrix products, arithmetic and copies ran while one was open for 2% -> 2% of each run, Pallas kernels for 33% -> 33%
where the time goes in v13:
time: 164 us
  Pallas kernels  68.4 us (42%)
  starting transfers between devices  46.1 us (28%)
  waiting for transfers between devices  45 us (27%)
  other arithmetic  1.96 us (1%)
    pallas_call x23, Pallas kernels, call(): pl.pallas_call(body, grid_spec=pltpu.PrefetchScalarGridSpec(num_scalar_pr...  68.4 us
    ppermute x34, waiting for transfers between devices, send(): lax.ppermute(x, axis, [(i, i ^ by) for i in range(lax.axis_size(axis))])  44.1 us
    ppermute x34, starting transfers between devices, send(): lax.ppermute(x, axis, [(i, i ^ by) for i in range(lax.axis_size(axis))])  39.3 us
    ppermute x2, starting transfers between devices, across(): return lax.ppermute(x, ('c0', 'zl'), [(0, 3), (1, 2), (2, 1), (3, 0)])  6.75 us
  transfers between devices with their start and end apart: 36, of which 17 were waited for; matrix products, arithmetic and copies ran while one was open for 2% of the time, Pallas kernels for 33%

profile of v13, /device:TPU:0, one launch (start us, length us, event | category | flops | bytes accessed | tf_op | source)
XLA Modules:
  0.0 164.0 jit_solution(13723587153090885940)
XLA Ops:
  0.0 4.1 %collective-permute-start.1 = (bf16[512,768]{1,0:T(8,128)(2,1)}, bf16[512,768]{1,0:T(8,128)(2,1)S(1)}, u32[]{:S(2)}, u32[]{:S(2)}) collective-permute-start(bf16[512,768]{1,0:T(8,128)(2,1)} %refs_0_.2), channel_id=1, source_target_pairs={{0,66},{2,64},{64,2},{66,0},{1,67},{3,65},{65,3},{67,1},{4,70},{6,... | collective-permute-start | bytes 2359304 | tf_op jit(solution)/shard_map/ppermute | solution.py:27
  5.5 1.1 reduce-window.6
  7.0 1.6 collective-permute-start.3
  8.6 1.3 constant_dynamic-slice_fusion
  10.0 5.5 %project.3.refs_4_ = f32[3,512,512]{2,1,0:T(8,128)S(1)} custom-call(s32[6]{0:T(128)S(1)} %stack.27.s, bf16[512,768]{1,0:T(8,128)(2,1)S(1)} %copy-done, bf16[512,768]{1,0:T(8,128)(2,1)} %collective-permute-done.2.refs_1_, bf16[3,3072,1024]{2,1,0:T(8,128)(2,1)} %bitcast.31, bf16[3,3072,1024]{2,1,0:T(8,128)(2,1)} %bitcast.32), custom_call_target="tpu_custom_call" | custom-call | flops 1 | bytes 1 | tf_op jit(solution)/shard_map/project/pallas_call | solution.py:35
  15.5 8.6 %collective-permute-done.3.refs_10_.cum_ref = f32[8,512]{1,0:T(8,128)S(1)} collective-permute-done((f32[8,512]{1,0:T(8,128)S(1)}, f32[8,512]{1,0:T(8,128)S(1)}, u32[]{:S(2)}, u32[]{:S(2)}) %collective-permute-start.3) | collective-permute-done | bytes 16416 | tf_op jit(solution)/shard_map/ppermute | solution.py:23
  25.7 2.6 %collective-permute-start.5 = (bf16[256,768]{1,0:T(8,128)(2,1)S(1)}, bf16[256,768]{1,0:T(8,128)(2,1)S(1)}, u32[]{:S(2)}, u32[]{:S(2)}) collective-permute-start(bf16[256,768]{1,0:T(8,128)(2,1)S(1)} %get-tuple-element.133), channel_id=1, source_target_pairs={{0,66},{2,64},{64,2},{66,0},{1,67},{3,65},{65,3},{67,1},{4,70},{6,... | collective-permute-start | bytes 1179656 | tf_op jit(solution)/shard_map/ppermute | solution.py:27
  28.3 5.3 %project.4.qkv_ref = bf16[3,512,512]{2,1,0:T(8,128)(2,1)S(1)} custom-call(s32[6]{0:T(128)S(1)} %stack.27.s, bf16[512,768]{1,0:T(8,128)(2,1)S(1)} %collective-permute-done.b.refs_0_.refs_2_, bf16[512,768]{1,0:T(8,128)(2,1)S(1)} %collective-permute-done.7.refs_1_.refs_3_, bf16[3,3072,1024]{2,1,0:T(8,128)(2,1)} %bitcast.33, bf16[3,3072,1024]{2,1,0:T(8,128)(2,1)} %bitcast.34, ...), custom_call_target="tpu_custom_call" | custom-call | flops 1 | bytes 1 | tf_op jit(solution)/shard_map/project/pallas_call | solution.py:35
  33.6 3.2 %turn.2 = bf16[16,2,96,512]{3,2,1,0:T(8,128)(2,1)S(1)} custom-call(s32[6]{0:T(128)S(1)} %stack.27.s, bf16[512,768]{1,0:T(8,128)(2,1)S(1)} %copy-done, bf16[512,768]{1,0:T(8,128)(2,1)} %collective-permute-done.2.refs_1_, bf16[512,768]{1,0:T(8,128)(2,1)S(1)} %collective-permute-done.b.refs_0_.refs_2_, bf16[512,768]{1,0:T(8,128)(2,1)S(1)} %collective-permute-done.7.refs_1_.refs_3_), custom_call_target="tpu_custom_call" | custom-call | flops 1 | bytes 1 | tf_op jit(solution)/shard_map/turn/pallas_call | solution.py:35
  37.7 2.8 %collective-permute-start.8 = (bf16[512,512]{1,0:T(8,128)(2,1)S(1)}, bf16[512,512]{1,0:T(8,128)(2,1)S(1)}, u32[]{:S(2)}, u32[]{:S(2)}) collective-permute-start(bf16[512,512]{1,0:T(8,128)(2,1)S(1)} %get-tuple-element.142), channel_id=1, source_target_pairs={{0,64},{64,0},{1,65},{65,1},{2,66},{66,2},{3,67},{67,3},{4,68},{68... | collective-permute-start | bytes 1572872 | tf_op jit(solution)/shard_map/ppermute | solution.py:23
  41.0 2.3 %shard_states.2 = (bf16[528,128]{1,0:T(8,128)(2,1)S(1)}, bf16[528,128]{1,0:T(8,128)(2,1)S(1)}, bf16[528,128]{1,0:T(8,128)(2,1)S(1)}, bf16[528,128]{1,0:T(8,128)(2,1)S(1)}) custom-call(s32[6]{0:T(128)S(1)} %stack.27.s, bf16[3,512,512]{2,1,0:T(8,128)(2,1)S(1)} %project.4.qkv_ref, bf16[512,512]{1,0:T(8,128)(2,1)S(1)} %get-tuple-element.253.og_ref, ...), custom_call_target="tpu_custom_call" | custom-call | flops 1 | bytes 1 | tf_op jit(solution)/shard_map/shard_states/pallas_call | solution.py:35
  43.4 7.9 %project.5.qkv_ref = bf16[3,512,512]{2,1,0:T(8,128)(2,1)S(1)} custom-call(s32[6]{0:T(128)S(1)} %stack.27.s, bf16[512,768]{1,0:T(8,128)(2,1)S(1)} %collective-permute-done.1.a.refs_0_.refs_4_, bf16[512,768]{1,0:T(8,128)(2,1)S(1)} %collective-permute-done.6.refs_1_.refs_5_, bf16[256,768]{1,0:T(8,128)(2,1)S(1)} %collective-permute-done.4.refs_2_.refs_0_, ...), custom_call_target="tpu_custom_call" | custom-call | flops 1 | bytes 1 | tf_op jit(solution)/shard_map/project/pallas_call | solution.py:35
  52.1 2.3 %shard_states.3 = (bf16[528,128]{1,0:T(8,128)(2,1)S(1)}, bf16[528,128]{1,0:T(8,128)(2,1)S(1)}, bf16[528,128]{1,0:T(8,128)(2,1)S(1)}, bf16[528,128]{1,0:T(8,128)(2,1)S(1)}) custom-call(s32[6]{0:T(128)S(1)} %stack.27.s, bf16[3,512,512]{2,1,0:T(8,128)(2,1)S(1)} %project.5.qkv_ref, bf16[512,512]{1,0:T(8,128)(2,1)S(1)} %collective-permute-done.8.og_ref, ...), custom_call_target="tpu_custom_call" | custom-call | flops 1 | bytes 1 | tf_op jit(solution)/shard_map/shard_states/pallas_call | solution.py:35
  54.4 3.3 %collective-permute-start.11 = (bf16[528,128]{1,0:T(8,128)(2,1)S(1)}, bf16[528,128]{1,0:T(8,128)(2,1)S(1)}, u32[]{:S(2)}, u32[]{:S(2)}) collective-permute-start(bf16[528,128]{1,0:T(8,128)(2,1)S(1)} %get-tuple-element.159), channel_id=1, source_target_pairs={{0,8},{4,12},{8,0},{12,4},{1,9},{5,13},{9,1},{13,5},{2,10},{6,14},... | collective-permute-start | bytes 405512 | tf_op jit(solution)/shard_map/ppermute | solution.py:23
  58.7 5.9 %local_grads.3 = (bf16[3,512,512]{2,1,0:T(8,128)(2,1)S(1)}, bf16[3,512,512]{2,1,0:T(8,128)(2,1)S(1)}) custom-call(s32[6]{0:T(128)S(1)} %stack.27.s, bf16[3,512,512]{2,1,0:T(8,128)(2,1)S(1)} %project.4.qkv_ref, bf16[512,512]{1,0:T(8,128)(2,1)S(1)} %get-tuple-element.253.og_ref, f32[8,512]{1,0:T(8,128)S(1)} %concatenate.7.refs_5_.cum_ref), custom_call_target="tpu_custom_call" | custom-call | flops 1 | bytes 1 | tf_op jit(solution)/shard_map/local_grads/pallas_call | solution.py:35
  65.4 3.1 %collective-permute-start.16 = (bf16[528,128]{1,0:T(8,128)(2,1)S(1)}, bf16[528,128]{1,0:T(8,128)(2,1)S(1)}, u32[]{:S(2)}, u32[]{:S(2)}) collective-permute-start(bf16[528,128]{1,0:T(8,128)(2,1)S(1)} %get-tuple-element.168.a), channel_id=1, source_target_pairs={{0,32},{16,48},{32,0},{48,16},{1,33},{17,49},{33,1},{49,17},{2,34}... | collective-permute-start | bytes 405512 | tf_op jit(solution)/shard_map/ppermute | solution.py:23
  68.5 1.1 collective-permute-start.15
  69.6 3.2 %local_grads.4 = (bf16[3,512,512]{2,1,0:T(8,128)(2,1)S(1)}, bf16[3,512,512]{2,1,0:T(8,128)(2,1)S(1)}) custom-call(s32[6]{0:T(128)S(1)} %stack.27.s, bf16[3,512,512]{2,1,0:T(8,128)(2,1)S(1)} %project.5.qkv_ref, bf16[512,512]{1,0:T(8,128)(2,1)S(1)} %collective-permute-done.8.og_ref, f32[8,512]{1,0:T(8,128)S(1)} %collective-permute-done.3.refs_10_.cum_ref), custom_call_target="tpu_custom_call" | custom-call | flops 1 | bytes 1 | tf_op jit(solution)/shard_map/local_grads/pallas_call | solution.py:35
  72.8 2.0 %turn.3 = bf16[16,2,96,512]{3,2,1,0:T(8,128)(2,1)S(1)} custom-call(s32[6]{0:T(128)S(1)} %stack.27.s, bf16[256,768]{1,0:T(8,128)(2,1)S(1)} %collective-permute-done.4.refs_2_.refs_0_, bf16[256,768]{1,0:T(8,128)(2,1)S(1)} %collective-permute-done.5.refs_3_.refs_1_, bf16[256,768]{1,0:T(8,128)(2,1)S(1)} %collective-permute-done.9.refs_4_.refs_2_, ...), custom_call_target="tpu_custom_call" | custom-call | flops 1 | bytes 1 | tf_op jit(solution)/shard_map/turn/pallas_call | solution.py:35
  75.8 3.1 %collective-permute-start.17 = (bf16[512,128]{1,0:T(8,128)(2,1)S(1)}, bf16[512,128]{1,0:T(8,128)(2,1)S(1)}, u32[]{:S(2)}, u32[]{:S(2)}) collective-permute-start(bf16[512,128]{1,0:T(8,128)(2,1)S(1)} %get-tuple-element.186), channel_id=1, source_target_pairs={{0,8},{4,12},{8,0},{12,4},{1,9},{5,13},{9,1},{13,5},{2,10},{6,14},... | collective-permute-start | bytes 393224 | tf_op jit(solution)/shard_map/ppermute | solution.py:23
  79.9 3.2 %local_grads.5 = (bf16[3,512,512]{2,1,0:T(8,128)(2,1)S(1)}, bf16[3,512,512]{2,1,0:T(8,128)(2,1)S(1)}) custom-call(s32[6]{0:T(128)S(1)} %stack.27.s, bf16[3,512,512]{2,1,0:T(8,128)(2,1)S(1)} %project.5.qkv_ref, bf16[512,512]{1,0:T(8,128)(2,1)S(1)} %collective-permute-done.8.og_ref, ...), custom_call_target="tpu_custom_call", output_to_operand_aliasing={{0}: (4, {}), {1}: (5, {})} | custom-call | flops 1 | bytes 1 | tf_op jit(solution)/shard_map/local_grads/pallas_call | solution.py:35
  83.9 1.8 %collective-permute-done.19.d = bf16[512,128]{1,0:T(8,128)(2,1)S(1)} collective-permute-done((bf16[512,128]{1,0:T(8,128)(2,1)S(1)}, bf16[512,128]{1,0:T(8,128)(2,1)S(1)}, u32[]{:S(2)}, u32[]{:S(2)}) %collective-permute-start.19) | collective-permute-done | bytes 131104 | tf_op jit(solution)/shard_map/ppermute | solution.py:23
  85.7 4.4 %whole_grads.1 = (bf16[512,768]{1,0:T(8,128)(2,1)S(1)}, bf16[512,768]{1,0:T(8,128)(2,1)S(1)}, bf16[512,768]{1,0:T(8,128)(2,1)S(1)}, bf16[512,768]{1,0:T(8,128)(2,1)S(1)}) custom-call(s32[6]{0:T(128)S(1)} %stack.27.s, bf16[3,512,512]{2,1,0:T(8,128)(2,1)S(1)} %get-tuple-element.200.local_a, bf16[3,512,512]{2,1,0:T(8,128)(2,1)S(1)} %get-tuple-element.201.ready_a, ...), custom_call_target="tpu_custom_call" | custom-call | flops 1 | bytes 1 | tf_op jit(solution)/shard_map/whole_grads/pallas_call | solution.py:35
  90.2 3.2 %weight_part.3 = (bf16[384,768]{1,0:T(8,128)(2,1)S(1)}, bf16[384,768]{1,0:T(8,128)(2,1)S(1)}, bf16[384,768]{1,0:T(8,128)(2,1)S(1)}, bf16[384,768]{1,0:T(8,128)(2,1)S(1)}) custom-call(s32[6]{0:T(128)S(1)} %stack.27.s, bf16[4,4,192,512]{3,2,1,0:T(8,128)(2,1)S(1)} %bitcast.19, bf16[4,4,192,512]{3,2,1,0:T(8,128)(2,1)S(1)} %bitcast.20, ...), custom_call_target="tpu_custom_call" | custom-call | flops 1 | bytes 1 | tf_op jit(solution)/shard_map/weight_part/pallas_call | solution.py:35
  93.3 2.2 %collective-permute-start.21 = (bf16[384,768]{1,0:T(8,128)(2,1)S(1)}, bf16[384,768]{1,0:T(8,128)(2,1)S(1)}, u32[]{:S(2)}, u32[]{:S(2)}) collective-permute-start(bf16[384,768]{1,0:T(8,128)(2,1)S(1)} %get-tuple-element.215), channel_id=1, source_target_pairs={{0,48},{16,32},{32,16},{48,0},{1,49},{17,33},{33,17},{49,1},{2,50}... | collective-permute-start | bytes 1769480 | tf_op jit(solution)/shard_map/ppermute | solution.py:23
  95.5 1.4 collective-permute-start.20
  97.1 1.5 collective-permute-start.25
  98.5 8.4 %weight_part.4 = (bf16[768,768]{1,0:T(8,128)(2,1)S(1)}, bf16[768,768]{1,0:T(8,128)(2,1)S(1)}, bf16[768,768]{1,0:T(8,128)(2,1)S(1)}, bf16[768,768]{1,0:T(8,128)(2,1)S(1)}) custom-call(s32[6]{0:T(128)S(1)} %stack.27.s, bf16[4,4,192,512]{3,2,1,0:T(8,128)(2,1)S(1)} %bitcast.21, bf16[4,4,192,512]{3,2,1,0:T(8,128)(2,1)S(1)} %bitcast.22, ...), custom_call_target="tpu_custom_call" | custom-call | flops 1 | bytes 1 | tf_op jit(solution)/shard_map/weight_part/pallas_call | solution.py:35
  108.0 0.9 add_halves.2
  108.9 1.5 collective-permute-start.22
  110.4 1.1 collective-permute-start.23
  113.2 3.2 %weight_part.5 = (bf16[768,768]{1,0:T(8,128)(2,1)S(1)}, bf16[768,768]{1,0:T(8,128)(2,1)S(1)}) custom-call(s32[6]{0:T(128)S(1)} %stack.27.s, bf16[4,4,192,512]{3,2,1,0:T(8,128)(2,1)S(1)} %bitcast.23, bf16[4,4,192,512]{3,2,1,0:T(8,128)(2,1)S(1)} %bitcast.24, bf16[4,4,192,512]{3,2,1,0:T(8,128)(2,1)S(1)} %bitcast.29, bf16[4,4,192,512]{3,2,1,0:T(8,128)(2,1)S(1)} %bitcast.30, ...), custom_call_target="tpu_custom_call" | custom-call | flops 1 | bytes 1 | tf_op jit(solution)/shard_map/weight_part/pallas_call | solution.py:35
  116.3 18.7 %collective-permute-done.23.refs_2_ = bf16[768,768]{1,0:T(8,128)(2,1)S(1)} collective-permute-done((bf16[768,768]{1,0:T(8,128)(2,1)S(1)}, bf16[768,768]{1,0:T(8,128)(2,1)S(1)}, u32[]{:S(2)}, u32[]{:S(2)}) %collective-permute-start.23) | collective-permute-done | bytes 1179680 | tf_op jit(solution)/shard_map/ppermute | solution.py:23
  135.0 2.0 %collective-permute-done.27.refs_5_ = bf16[768,768]{1,0:T(8,128)(2,1)S(1)} collective-permute-done((bf16[768,768]{1,0:T(8,128)(2,1)S(1)}, bf16[768,768]{1,0:T(8,128)(2,1)S(1)}, u32[]{:S(2)}, u32[]{:S(2)}) %collective-permute-start.27) | collective-permute-done | bytes 1179680 | tf_op jit(solution)/shard_map/ppermute | solution.py:23
  137.3 1.4 cut_blocks.1
  139.2 2.4 %collective-permute-start.29 = (bf16[192,768]{1,0:T(8,128)(2,1)S(1)}, bf16[192,768]{1,0:T(8,128)(2,1)S(1)}, u32[]{:S(2)}, u32[]{:S(2)}) collective-permute-start(bf16[192,768]{1,0:T(8,128)(2,1)S(1)} %get-tuple-element.240), channel_id=1, source_target_pairs={{0,12},{4,8},{8,4},{12,0},{1,13},{5,9},{9,5},{13,1},{2,14},{6,10},... | collective-permute-start | bytes 884744 | tf_op jit(solution)/shard_map/ppermute | solution.py:23
  141.7 1.2 collective-permute-start.30
  142.9 0.9 collective-permute-start.31
  143.8 1.7 %collective-permute-start.32 = (bf16[192,768]{1,0:T(8,128)(2,1)S(1)}, bf16[192,768]{1,0:T(8,128)(2,1)S(1)}, u32[]{:S(2)}, u32[]{:S(2)}) collective-permute-start(bf16[192,768]{1,0:T(8,128)(2,1)S(1)} %get-tuple-element.245), channel_id=1, source_target_pairs={{0,48},{16,32},{32,16},{48,0},{1,49},{17,33},{33,17},{49,1},{2,50}... | collective-permute-start | bytes 884744 | tf_op jit(solution)/shard_map/ppermute | solution.py:23
  146.0 2.0 %collective-permute-start.33 = (bf16[192,768]{1,0:T(8,128)(2,1)S(1)}, bf16[192,768]{1,0:T(8,128)(2,1)S(1)}, u32[]{:S(2)}, u32[]{:S(2)}) collective-permute-start(bf16[192,768]{1,0:T(8,128)(2,1)S(1)} %get-tuple-element.246), channel_id=1, source_target_pairs={{0,32},{16,48},{32,0},{48,16},{1,33},{17,49},{33,1},{49,17},{2,34}... | collective-permute-start | bytes 884744 | tf_op jit(solution)/shard_map/ppermute | solution.py:23
  148.0 1.1 collective-permute-done.29.c
  149.1 1.7 %collective-permute-done.30.d = bf16[192,768]{1,0:T(8,128)(2,1)S(1)} collective-permute-done((bf16[192,768]{1,0:T(8,128)(2,1)S(1)}, bf16[192,768]{1,0:T(8,128)(2,1)S(1)}, u32[]{:S(2)}, u32[]{:S(2)}) %collective-permute-start.30) | collective-permute-done | bytes 294944 | tf_op jit(solution)/shard_map/ppermute | solution.py:23
  151.5 1.8 %collective-permute-start.34 = (bf16[96,768]{1,0:T(8,128)(2,1)S(1)}, bf16[96,768]{1,0:T(8,128)(2,1)S(1)}, u32[]{:S(2)}, u32[]{:S(2)}) collective-permute-start(bf16[96,768]{1,0:T(8,128)(2,1)S(1)} %get-tuple-element.251), channel_id=1, source_target_pairs={{0,64},{64,0},{1,65},{65,1},{2,66},{66,2},{3,67},{67,3},{4,68},{68... | collective-permute-start | bytes 442376 | tf_op jit(solution)/shard_map/ppermute | solution.py:23
  153.3 1.6 collective-permute-done.33.d
  155.6 1.6 collective-permute-start.35
  157.2 1.0 collective-permute-done.34.refs_2_
  158.3 4.1 %collective-permute-done.35.refs_3_ = bf16[96,768]{1,0:T(8,128)(2,1)S(1)} collective-permute-done((bf16[96,768]{1,0:T(8,128)(2,1)S(1)}, bf16[96,768]{1,0:T(8,128)(2,1)S(1)}, u32[]{:S(2)}, u32[]{:S(2)}) %collective-permute-start.35) | collective-permute-done | bytes 147488 | tf_op jit(solution)/shard_map/ppermute | solution.py:23
  162.3 1.6 finish.1
  (61 shorter events, 14.9 us)
Async XLA Ops:
  0.0 10.0 %collective-permute-start.2 = (bf16[512,768]{1,0:T(8,128)(2,1)}, bf16[512,768]{1,0:T(8,128)(2,1)}, u32[]{:S(2)}, u32[]{:S(2)}) collective-permute-start(bf16[512,768]{1,0:T(8,128)(2,1)} %refs_0_.2), channel_id=1, source_target_pairs={{0,1},{1,0},{2,3},{3,2},{4,5},{5,4},{6,7},{7,6},{8,9},{9,8},{10,11... | collective-permute-start | bytes 2359304 | tf_op jit(solution)/shard_map/ppermute | solution.py:23
  0.0 24.1 %collective-permute-start.1 = (bf16[512,768]{1,0:T(8,128)(2,1)}, bf16[512,768]{1,0:T(8,128)(2,1)S(1)}, u32[]{:S(2)}, u32[]{:S(2)}) collective-permute-start(bf16[512,768]{1,0:T(8,128)(2,1)} %refs_0_.2), channel_id=1, source_target_pairs={{0,66},{2,64},{64,2},{66,0},{1,67},{3,65},{65,3},{67,1},{4,70},{6,... | collective-permute-start | bytes 2359304 | tf_op jit(solution)/shard_map/ppermute | solution.py:27
  4.1 20.1 %collective-permute-start = (bf16[512,768]{1,0:T(8,128)(2,1)}, bf16[512,768]{1,0:T(8,128)(2,1)S(1)}, u32[]{:S(2)}, u32[]{:S(2)}) collective-permute-start(bf16[512,768]{1,0:T(8,128)(2,1)} %refs_0_.2), channel_id=1, source_target_pairs={{0,2},{2,0},{1,3},{3,1},{4,6},{6,4},{5,7},{7,5},{8,10},{10,8},{9,1... | collective-permute-start | bytes 2359304 | tf_op jit(solution)/shard_map/ppermute | solution.py:23
  5.5 4.5 %copy-start = (bf16[512,768]{1,0:T(8,128)(2,1)S(1)}, bf16[512,768]{1,0:T(8,128)(2,1)}, u32[]{:S(2)}) copy-start(bf16[512,768]{1,0:T(8,128)(2,1)} %refs_0_.2) | copy-start | bytes 2359300
  7.0 17.1 %collective-permute-start.3 = (f32[8,512]{1,0:T(8,128)S(1)}, f32[8,512]{1,0:T(8,128)S(1)}, u32[]{:S(2)}, u32[]{:S(2)}) collective-permute-start(f32[8,512]{1,0:T(8,128)S(1)} %concatenate.6), channel_id=1, source_target_pairs={{0,64},{64,0},{1,65},{65,1},{2,66},{66,2},{3,67},{67,3},{4,68},{68... | collective-permute-start | bytes 49160 | tf_op jit(solution)/shard_map/ppermute | solution.py:23
  24.2 4.1 %collective-permute-start.7 = (bf16[512,768]{1,0:T(8,128)(2,1)S(1)}, bf16[512,768]{1,0:T(8,128)(2,1)S(1)}, u32[]{:S(2)}, u32[]{:S(2)}) collective-permute-start(bf16[512,768]{1,0:T(8,128)(2,1)S(1)} %collective-permute-done.b.refs_0_.refs_2_), channel_id=1, source_target_pairs={{0,1},{1,0},{2,3},{3,2},{4,5},{5,4},{6,7},{7,6},{8,9},{9,8},{10,11... | collective-permute-start | bytes 2359304 | tf_op jit(solution)/shard_map/ppermute | solution.py:23
  24.2 13.5 %collective-permute-start.6 = (bf16[512,768]{1,0:T(8,128)(2,1)S(1)}, bf16[512,768]{1,0:T(8,128)(2,1)S(1)}, u32[]{:S(2)}, u32[]{:S(2)}) collective-permute-start(bf16[512,768]{1,0:T(8,128)(2,1)S(1)} %collective-permute-done.1.a.refs_0_.refs_4_), channel_id=1, source_target_pairs={{0,1},{1,0},{2,3},{3,2},{4,5},{5,4},{6,7},{7,6},{8,9},{9,8},{10,11... | collective-permute-start | bytes 2359304 | tf_op jit(solution)/shard_map/ppermute | solution.py:23
  25.3 11.5 %collective-permute-start.4 = (bf16[256,768]{1,0:T(8,128)(2,1)S(1)}, bf16[256,768]{1,0:T(8,128)(2,1)S(1)}, u32[]{:S(2)}, u32[]{:S(2)}) collective-permute-start(bf16[256,768]{1,0:T(8,128)(2,1)S(1)} %get-tuple-element.132), channel_id=1, source_target_pairs={{0,2},{2,0},{1,3},{3,1},{4,6},{6,4},{5,7},{7,5},{8,10},{10,8},{9,1... | collective-permute-start | bytes 1179656 | tf_op jit(solution)/shard_map/ppermute | solution.py:23
  25.7 12.0 %collective-permute-start.5 = (bf16[256,768]{1,0:T(8,128)(2,1)S(1)}, bf16[256,768]{1,0:T(8,128)(2,1)S(1)}, u32[]{:S(2)}, u32[]{:S(2)}) collective-permute-start(bf16[256,768]{1,0:T(8,128)(2,1)S(1)} %get-tuple-element.133), channel_id=1, source_target_pairs={{0,66},{2,64},{64,2},{66,0},{1,67},{3,65},{65,3},{67,1},{4,70},{6,... | collective-permute-start | bytes 1179656 | tf_op jit(solution)/shard_map/ppermute | solution.py:27
  37.7 14.4 %collective-permute-start.8 = (bf16[512,512]{1,0:T(8,128)(2,1)S(1)}, bf16[512,512]{1,0:T(8,128)(2,1)S(1)}, u32[]{:S(2)}, u32[]{:S(2)}) collective-permute-start(bf16[512,512]{1,0:T(8,128)(2,1)S(1)} %get-tuple-element.142), channel_id=1, source_target_pairs={{0,64},{64,0},{1,65},{65,1},{2,66},{66,2},{3,67},{67,3},{4,68},{68... | collective-permute-start | bytes 1572872 | tf_op jit(solution)/shard_map/ppermute | solution.py:23
  40.5 2.8 %collective-permute-start.9 = (bf16[256,768]{1,0:T(8,128)(2,1)S(1)}, bf16[256,768]{1,0:T(8,128)(2,1)S(1)}, u32[]{:S(2)}, u32[]{:S(2)}) collective-permute-start(bf16[256,768]{1,0:T(8,128)(2,1)S(1)} %collective-permute-done.4.refs_2_.refs_0_), channel_id=1, source_target_pairs={{0,1},{1,0},{2,3},{3,2},{4,5},{5,4},{6,7},{7,6},{8,9},{9,8},{10,11... | collective-permute-start | bytes 1179656 | tf_op jit(solution)/shard_map/ppermute | solution.py:23
  40.5 2.8 %collective-permute-start.10 = (bf16[256,768]{1,0:T(8,128)(2,1)S(1)}, bf16[256,768]{1,0:T(8,128)(2,1)S(1)}, u32[]{:S(2)}, u32[]{:S(2)}) collective-permute-start(bf16[256,768]{1,0:T(8,128)(2,1)S(1)} %collective-permute-done.5.refs_3_.refs_1_), channel_id=1, source_target_pairs={{0,1},{1,0},{2,3},{3,2},{4,5},{5,4},{6,7},{7,6},{8,9},{9,8},{10,11... | collective-permute-start | bytes 1179656 | tf_op jit(solution)/shard_map/ppermute | solution.py:23
  54.4 10.2 %collective-permute-start.11 = (bf16[528,128]{1,0:T(8,128)(2,1)S(1)}, bf16[528,128]{1,0:T(8,128)(2,1)S(1)}, u32[]{:S(2)}, u32[]{:S(2)}) collective-permute-start(bf16[528,128]{1,0:T(8,128)(2,1)S(1)} %get-tuple-element.159), channel_id=1, source_target_pairs={{0,8},{4,12},{8,0},{12,4},{1,9},{5,13},{9,1},{13,5},{2,10},{6,14},... | collective-permute-start | bytes 405512 | tf_op jit(solution)/shard_map/ppermute | solution.py:23
  57.7 6.9 %collective-permute-start.12 = (bf16[528,128]{1,0:T(8,128)(2,1)S(1)}, bf16[528,128]{1,0:T(8,128)(2,1)S(1)}, u32[]{:S(2)}, u32[]{:S(2)}) collective-permute-start(bf16[528,128]{1,0:T(8,128)(2,1)S(1)} %get-tuple-element.160), channel_id=1, source_target_pairs={{0,4},{4,0},{8,12},{12,8},{1,5},{5,1},{9,13},{13,9},{2,6},{6,2},{1... | collective-permute-start | bytes 405512 | tf_op jit(solution)/shard_map/ppermute | solution.py:23
  58.3 6.3 %collective-permute-start.13 = (bf16[528,128]{1,0:T(8,128)(2,1)S(1)}, bf16[528,128]{1,0:T(8,128)(2,1)S(1)}, u32[]{:S(2)}, u32[]{:S(2)}) collective-permute-start(bf16[528,128]{1,0:T(8,128)(2,1)S(1)} %get-tuple-element.161), channel_id=1, source_target_pairs={{0,12},{4,8},{8,4},{12,0},{1,13},{5,9},{9,5},{13,1},{2,14},{6,10},... | collective-permute-start | bytes 405512 | tf_op jit(solution)/shard_map/ppermute | solution.py:23
  65.4 9.5 %collective-permute-start.16 = (bf16[528,128]{1,0:T(8,128)(2,1)S(1)}, bf16[528,128]{1,0:T(8,128)(2,1)S(1)}, u32[]{:S(2)}, u32[]{:S(2)}) collective-permute-start(bf16[528,128]{1,0:T(8,128)(2,1)S(1)} %get-tuple-element.168.a), channel_id=1, source_target_pairs={{0,32},{16,48},{32,0},{48,16},{1,33},{17,49},{33,1},{49,17},{2,34}... | collective-permute-start | bytes 405512 | tf_op jit(solution)/shard_map/ppermute | solution.py:23
  68.5 6.4 %collective-permute-start.15 = (bf16[528,128]{1,0:T(8,128)(2,1)S(1)}, bf16[528,128]{1,0:T(8,128)(2,1)S(1)}, u32[]{:S(2)}, u32[]{:S(2)}) collective-permute-start(bf16[528,128]{1,0:T(8,128)(2,1)S(1)} %get-tuple-element.168.a), channel_id=1, source_target_pairs={{0,48},{16,32},{32,16},{48,0},{1,49},{17,33},{33,17},{49,1},{2,50}... | collective-permute-start | bytes 405512 | tf_op jit(solution)/shard_map/ppermute | solution.py:23
  69.6 5.3 %collective-permute-start.14 = (bf16[528,128]{1,0:T(8,128)(2,1)S(1)}, bf16[528,128]{1,0:T(8,128)(2,1)S(1)}, u32[]{:S(2)}, u32[]{:S(2)}) collective-permute-start(bf16[528,128]{1,0:T(8,128)(2,1)S(1)} %get-tuple-element.168.a), channel_id=1, source_target_pairs={{0,16},{16,0},{32,48},{48,32},{1,17},{17,1},{33,49},{49,33},{2,18}... | collective-permute-start | bytes 405512 | tf_op jit(solution)/shard_map/ppermute | solution.py:23
  75.8 7.4 %collective-permute-start.17 = (bf16[512,128]{1,0:T(8,128)(2,1)S(1)}, bf16[512,128]{1,0:T(8,128)(2,1)S(1)}, u32[]{:S(2)}, u32[]{:S(2)}) collective-permute-start(bf16[512,128]{1,0:T(8,128)(2,1)S(1)} %get-tuple-element.186), channel_id=1, source_target_pairs={{0,8},{4,12},{8,0},{12,4},{1,9},{5,13},{9,1},{13,5},{2,10},{6,14},... | collective-permute-start | bytes 393224 | tf_op jit(solution)/shard_map/ppermute | solution.py:23
  78.9 5.0 %collective-permute-start.18 = (bf16[512,128]{1,0:T(8,128)(2,1)S(1)}, bf16[512,128]{1,0:T(8,128)(2,1)S(1)}, u32[]{:S(2)}, u32[]{:S(2)}) collective-permute-start(bf16[512,128]{1,0:T(8,128)(2,1)S(1)} %get-tuple-element.187), channel_id=1, source_target_pairs={{0,4},{4,0},{8,12},{12,8},{1,5},{5,1},{9,13},{13,9},{2,6},{6,2},{1... | collective-permute-start | bytes 393224 | tf_op jit(solution)/shard_map/ppermute | solution.py:23
  79.6 6.2 %collective-permute-start.19 = (bf16[512,128]{1,0:T(8,128)(2,1)S(1)}, bf16[512,128]{1,0:T(8,128)(2,1)S(1)}, u32[]{:S(2)}, u32[]{:S(2)}) collective-permute-start(bf16[512,128]{1,0:T(8,128)(2,1)S(1)} %get-tuple-element.188), channel_id=1, source_target_pairs={{0,12},{4,8},{8,4},{12,0},{1,13},{5,9},{9,5},{13,1},{2,14},{6,10},... | collective-permute-start | bytes 393224 | tf_op jit(solution)/shard_map/ppermute | solution.py:23
  93.3 14.4 %collective-permute-start.21 = (bf16[384,768]{1,0:T(8,128)(2,1)S(1)}, bf16[384,768]{1,0:T(8,128)(2,1)S(1)}, u32[]{:S(2)}, u32[]{:S(2)}) collective-permute-start(bf16[384,768]{1,0:T(8,128)(2,1)S(1)} %get-tuple-element.215), channel_id=1, source_target_pairs={{0,48},{16,32},{32,16},{48,0},{1,49},{17,33},{33,17},{49,1},{2,50}... | collective-permute-start | bytes 1769480 | tf_op jit(solution)/shard_map/ppermute | solution.py:23
  95.5 12.5 %collective-permute-start.20 = (bf16[384,768]{1,0:T(8,128)(2,1)S(1)}, bf16[384,768]{1,0:T(8,128)(2,1)S(1)}, u32[]{:S(2)}, u32[]{:S(2)}) collective-permute-start(bf16[384,768]{1,0:T(8,128)(2,1)S(1)} %get-tuple-element.211), channel_id=1, source_target_pairs={{0,16},{16,0},{32,48},{48,32},{1,17},{17,1},{33,49},{49,33},{2,18}... | collective-permute-start | bytes 1769480 | tf_op jit(solution)/shard_map/ppermute | solution.py:23
  96.9 13.5 %collective-permute-start.24 = (bf16[384,768]{1,0:T(8,128)(2,1)S(1)}, bf16[384,768]{1,0:T(8,128)(2,1)S(1)}, u32[]{:S(2)}, u32[]{:S(2)}) collective-permute-start(bf16[384,768]{1,0:T(8,128)(2,1)S(1)} %get-tuple-element.224), channel_id=1, source_target_pairs={{0,4},{4,0},{8,12},{12,8},{1,5},{5,1},{9,13},{13,9},{2,6},{6,2},{1... | collective-permute-start | bytes 1769480 | tf_op jit(solution)/shard_map/ppermute | solution.py:23
  97.1 13.4 %collective-permute-start.25 = (bf16[384,768]{1,0:T(8,128)(2,1)S(1)}, bf16[384,768]{1,0:T(8,128)(2,1)S(1)}, u32[]{:S(2)}, u32[]{:S(2)}) collective-permute-start(bf16[384,768]{1,0:T(8,128)(2,1)S(1)} %get-tuple-element.225), channel_id=1, source_target_pairs={{0,12},{4,8},{8,4},{12,0},{1,13},{5,9},{9,5},{13,1},{2,14},{6,10},... | collective-permute-start | bytes 1769480 | tf_op jit(solution)/shard_map/ppermute | solution.py:23
  108.9 26.1 %collective-permute-start.22 = (bf16[768,768]{1,0:T(8,128)(2,1)S(1)}, bf16[768,768]{1,0:T(8,128)(2,1)S(1)}, u32[]{:S(2)}, u32[]{:S(2)}) collective-permute-start(bf16[768,768]{1,0:T(8,128)(2,1)S(1)} %get-tuple-element.220), channel_id=1, source_target_pairs={{0,16},{16,0},{32,48},{48,32},{1,17},{17,1},{33,49},{49,33},{2,18}... | collective-permute-start | bytes 3538952 | tf_op jit(solution)/shard_map/ppermute | solution.py:23
  110.4 24.6 %collective-permute-start.23 = (bf16[768,768]{1,0:T(8,128)(2,1)S(1)}, bf16[768,768]{1,0:T(8,128)(2,1)S(1)}, u32[]{:S(2)}, u32[]{:S(2)}) collective-permute-start(bf16[768,768]{1,0:T(8,128)(2,1)S(1)} %get-tuple-element.221), channel_id=1, source_target_pairs={{0,48},{16,32},{32,16},{48,0},{1,49},{17,33},{33,17},{49,1},{2,50}... | collective-permute-start | bytes 3538952 | tf_op jit(solution)/shard_map/ppermute | solution.py:23
  112.4 24.6 %collective-permute-start.27 = (bf16[768,768]{1,0:T(8,128)(2,1)S(1)}, bf16[768,768]{1,0:T(8,128)(2,1)S(1)}, u32[]{:S(2)}, u32[]{:S(2)}) collective-permute-start(bf16[768,768]{1,0:T(8,128)(2,1)S(1)} %get-tuple-element.237), channel_id=1, source_target_pairs={{0,12},{4,8},{8,4},{12,0},{1,13},{5,9},{9,5},{13,1},{2,14},{6,10},... | collective-permute-start | bytes 3538952 | tf_op jit(solution)/shard_map/ppermute | solution.py:23
  112.6 24.7 %collective-permute-start.26 = (bf16[768,768]{1,0:T(8,128)(2,1)S(1)}, bf16[768,768]{1,0:T(8,128)(2,1)S(1)}, u32[]{:S(2)}, u32[]{:S(2)}) collective-permute-start(bf16[768,768]{1,0:T(8,128)(2,1)S(1)} %get-tuple-element.228), channel_id=1, source_target_pairs={{0,4},{4,0},{8,12},{12,8},{1,5},{5,1},{9,13},{13,9},{2,6},{6,2},{1... | collective-permute-start | bytes 3538952 | tf_op jit(solution)/shard_map/ppermute | solution.py:23
  138.7 7.3 %collective-permute-start.28 = (bf16[192,768]{1,0:T(8,128)(2,1)S(1)}, bf16[192,768]{1,0:T(8,128)(2,1)S(1)}, u32[]{:S(2)}, u32[]{:S(2)}) collective-permute-start(bf16[192,768]{1,0:T(8,128)(2,1)S(1)} %get-tuple-element.239), channel_id=1, source_target_pairs={{0,4},{4,0},{8,12},{12,8},{1,5},{5,1},{9,13},{13,9},{2,6},{6,2},{1... | collective-permute-start | bytes 884744 | tf_op jit(solution)/shard_map/ppermute | solution.py:23
  139.2 9.9 %collective-permute-start.29 = (bf16[192,768]{1,0:T(8,128)(2,1)S(1)}, bf16[192,768]{1,0:T(8,128)(2,1)S(1)}, u32[]{:S(2)}, u32[]{:S(2)}) collective-permute-start(bf16[192,768]{1,0:T(8,128)(2,1)S(1)} %get-tuple-element.240), channel_id=1, source_target_pairs={{0,12},{4,8},{8,4},{12,0},{1,13},{5,9},{9,5},{13,1},{2,14},{6,10},... | collective-permute-start | bytes 884744 | tf_op jit(solution)/shard_map/ppermute | solution.py:23
  141.7 9.2 %collective-permute-start.30 = (bf16[192,768]{1,0:T(8,128)(2,1)S(1)}, bf16[192,768]{1,0:T(8,128)(2,1)S(1)}, u32[]{:S(2)}, u32[]{:S(2)}) collective-permute-start(bf16[192,768]{1,0:T(8,128)(2,1)S(1)} %get-tuple-element.241), channel_id=1, source_target_pairs={{0,8},{4,12},{8,0},{12,4},{1,9},{5,13},{9,1},{13,5},{2,10},{6,14},... | collective-permute-start | bytes 884744 | tf_op jit(solution)/shard_map/ppermute | solution.py:23
  142.9 10.5 %collective-permute-start.31 = (bf16[192,768]{1,0:T(8,128)(2,1)S(1)}, bf16[192,768]{1,0:T(8,128)(2,1)S(1)}, u32[]{:S(2)}, u32[]{:S(2)}) collective-permute-start(bf16[192,768]{1,0:T(8,128)(2,1)S(1)} %get-tuple-element.244), channel_id=1, source_target_pairs={{0,16},{16,0},{32,48},{48,32},{1,17},{17,1},{33,49},{49,33},{2,18}... | collective-permute-start | bytes 884744 | tf_op jit(solution)/shard_map/ppermute | solution.py:23
  143.8 9.5 %collective-permute-start.32 = (bf16[192,768]{1,0:T(8,128)(2,1)S(1)}, bf16[192,768]{1,0:T(8,128)(2,1)S(1)}, u32[]{:S(2)}, u32[]{:S(2)}) collective-permute-start(bf16[192,768]{1,0:T(8,128)(2,1)S(1)} %get-tuple-element.245), channel_id=1, source_target_pairs={{0,48},{16,32},{32,16},{48,0},{1,49},{17,33},{33,17},{49,1},{2,50}... | collective-permute-start | bytes 884744 | tf_op jit(solution)/shard_map/ppermute | solution.py:23
  146.0 8.9 %collective-permute-start.33 = (bf16[192,768]{1,0:T(8,128)(2,1)S(1)}, bf16[192,768]{1,0:T(8,128)(2,1)S(1)}, u32[]{:S(2)}, u32[]{:S(2)}) collective-permute-start(bf16[192,768]{1,0:T(8,128)(2,1)S(1)} %get-tuple-element.246), channel_id=1, source_target_pairs={{0,32},{16,48},{32,0},{48,16},{1,33},{17,49},{33,1},{49,17},{2,34}... | collective-permute-start | bytes 884744 | tf_op jit(solution)/shard_map/ppermute | solution.py:23
  151.5 6.7 %collective-permute-start.34 = (bf16[96,768]{1,0:T(8,128)(2,1)S(1)}, bf16[96,768]{1,0:T(8,128)(2,1)S(1)}, u32[]{:S(2)}, u32[]{:S(2)}) collective-permute-start(bf16[96,768]{1,0:T(8,128)(2,1)S(1)} %get-tuple-element.251), channel_id=1, source_target_pairs={{0,64},{64,0},{1,65},{65,1},{2,66},{66,2},{3,67},{67,3},{4,68},{68... | collective-permute-start | bytes 442376 | tf_op jit(solution)/shard_map/ppermute | solution.py:23
  155.6 6.7 %collective-permute-start.35 = (bf16[96,768]{1,0:T(8,128)(2,1)S(1)}, bf16[96,768]{1,0:T(8,128)(2,1)S(1)}, u32[]{:S(2)}, u32[]{:S(2)}) collective-permute-start(bf16[96,768]{1,0:T(8,128)(2,1)S(1)} %get-tuple-element.252), channel_id=1, source_target_pairs={{0,64},{64,0},{1,65},{65,1},{2,66},{66,2},{3,67},{67,3},{4,68},{68... | collective-permute-start | bytes 442376 | tf_op jit(solution)/shard_map/ppermute | solution.py:23

commit v14 on v13

--- a/solution.py
+++ b/solution.py
@@ -614,13 +614,13 @@
     at_x = [send(ring, "c1", r) for r in (1, 3, 2)]
     qkv_pair, _ = tied((qkv_pair, ring))
     local = local_grads(table, qkv_pair, og_pair, note, 0, per // 2, None)
-    second, _ = tied(([far, far_core, [side], [side_core]], ring))
-    turned.append(turn(table, second))
-    at_x, local, turned = tied((at_x, local, turned))
+    at_x, local = tied((at_x, local))
     back = arrivals(table, [ring, at_x[0], at_x[2], at_x[1]], before, after, prior, later)
     states = [send(back[r], "c2", r) for r in (2, 1, 3)]
     local, _ = tied((local, back[0]))
     local = local_grads(table, qkv_pair, og_pair, note, per // 2, per // 2, local)
+    second, _ = tied(([far, far_core, [side], [side_core]], back[0]))
+    turned.append(turn(table, second))
     states, turned, local = tied((states, turned, local))
     states = [back[0], states[1], states[0], states[2]]
 

time: 164 us -> 165 us (level)
  transfers between devices with their start and end apart: 36 -> 36, of which waited for: 17 -> 16; matrix products, arithmetic and copies ran while one was open for 2% -> 2% of each run, Pallas kernels for 33% -> 33%
where the time goes in v14:
time: 165 us
  Pallas kernels  68.4 us (41%)
  starting transfers between devices  47.2 us (29%)
  waiting for transfers between devices  44.5 us (27%)
  other arithmetic  1.96 us (1%)
    pallas_call x23, Pallas kernels, call(): pl.pallas_call(body, grid_spec=pltpu.PrefetchScalarGridSpec(num_scalar_pr...  68.4 us
    ppermute x34, waiting for transfers between devices, send(): lax.ppermute(x, axis, [(i, i ^ by) for i in range(lax.axis_size(axis))])  43.6 us
    ppermute x34, starting transfers between devices, send(): lax.ppermute(x, axis, [(i, i ^ by) for i in range(lax.axis_size(axis))])  40.4 us
    ppermute x2, starting transfers between devices, across(): return lax.ppermute(x, ('c0', 'zl'), [(0, 3), (1, 2), (2, 1), (3, 0)])  6.75 us
  transfers between devices with their start and end apart: 36, of which 16 were waited for; matrix products, arithmetic and copies ran while one was open for 2% of the time, Pallas kernels for 33%

profile of v14, /device:TPU:0, one launch (start us, length us, event | category | flops | bytes accessed | tf_op | source)
XLA Modules:
  0.0 164.5 jit_solution(1198778871182036022)
XLA Ops:
  0.0 4.1 %collective-permute-start.1 = (bf16[512,768]{1,0:T(8,128)(2,1)}, bf16[512,768]{1,0:T(8,128)(2,1)S(1)}, u32[]{:S(2)}, u32[]{:S(2)}) collective-permute-start(bf16[512,768]{1,0:T(8,128)(2,1)} %refs_0_.2), channel_id=1, source_target_pairs={{0,66},{2,64},{64,2},{66,0},{1,67},{3,65},{65,3},{67,1},{4,70},{6,... | collective-permute-start | bytes 2359304 | tf_op jit(solution)/shard_map/ppermute | solution.py:27
  5.5 1.1 reduce-window.6
  7.0 1.6 collective-permute-start.3
  8.6 1.3 constant_dynamic-slice_fusion
  10.0 5.5 %project.3.refs_4_ = f32[3,512,512]{2,1,0:T(8,128)S(1)} custom-call(s32[6]{0:T(128)S(1)} %stack.27.s, bf16[512,768]{1,0:T(8,128)(2,1)S(1)} %copy-done, bf16[512,768]{1,0:T(8,128)(2,1)} %collective-permute-done.2.refs_1_, bf16[3,3072,1024]{2,1,0:T(8,128)(2,1)} %bitcast.31, bf16[3,3072,1024]{2,1,0:T(8,128)(2,1)} %bitcast.32), custom_call_target="tpu_custom_call" | custom-call | flops 1 | bytes 1 | tf_op jit(solution)/shard_map/project/pallas_call | solution.py:35
  15.5 8.6 %collective-permute-done.3.refs_10_.cum_ref = f32[8,512]{1,0:T(8,128)S(1)} collective-permute-done((f32[8,512]{1,0:T(8,128)S(1)}, f32[8,512]{1,0:T(8,128)S(1)}, u32[]{:S(2)}, u32[]{:S(2)}) %collective-permute-start.3) | collective-permute-done | bytes 16416 | tf_op jit(solution)/shard_map/ppermute | solution.py:23
  25.7 2.6 %collective-permute-start.5 = (bf16[256,768]{1,0:T(8,128)(2,1)S(1)}, bf16[256,768]{1,0:T(8,128)(2,1)S(1)}, u32[]{:S(2)}, u32[]{:S(2)}) collective-permute-start(bf16[256,768]{1,0:T(8,128)(2,1)S(1)} %get-tuple-element.131), channel_id=1, source_target_pairs={{0,66},{2,64},{64,2},{66,0},{1,67},{3,65},{65,3},{67,1},{4,70},{6,... | collective-permute-start | bytes 1179656 | tf_op jit(solution)/shard_map/ppermute | solution.py:27
  28.3 5.3 %project.4.qkv_ref = bf16[3,512,512]{2,1,0:T(8,128)(2,1)S(1)} custom-call(s32[6]{0:T(128)S(1)} %stack.27.s, bf16[512,768]{1,0:T(8,128)(2,1)S(1)} %collective-permute-done.b.refs_0_.refs_2_, bf16[512,768]{1,0:T(8,128)(2,1)S(1)} %collective-permute-done.7.refs_1_.refs_3_, bf16[3,3072,1024]{2,1,0:T(8,128)(2,1)} %bitcast.33, bf16[3,3072,1024]{2,1,0:T(8,128)(2,1)} %bitcast.34, ...), custom_call_target="tpu_custom_call" | custom-call | flops 1 | bytes 1 | tf_op jit(solution)/shard_map/project/pallas_call | solution.py:35
  33.6 3.2 %turn.2 = bf16[16,2,96,512]{3,2,1,0:T(8,128)(2,1)S(1)} custom-call(s32[6]{0:T(128)S(1)} %stack.27.s, bf16[512,768]{1,0:T(8,128)(2,1)S(1)} %copy-done, bf16[512,768]{1,0:T(8,128)(2,1)} %collective-permute-done.2.refs_1_, bf16[512,768]{1,0:T(8,128)(2,1)S(1)} %collective-permute-done.b.refs_0_.refs_2_, bf16[512,768]{1,0:T(8,128)(2,1)S(1)} %collective-permute-done.7.refs_1_.refs_3_), custom_call_target="tpu_custom_call" | custom-call | flops 1 | bytes 1 | tf_op jit(solution)/shard_map/turn/pallas_call | solution.py:35
  37.7 2.8 %collective-permute-start.8 = (bf16[512,512]{1,0:T(8,128)(2,1)S(1)}, bf16[512,512]{1,0:T(8,128)(2,1)S(1)}, u32[]{:S(2)}, u32[]{:S(2)}) collective-permute-start(bf16[512,512]{1,0:T(8,128)(2,1)S(1)} %get-tuple-element.140), channel_id=1, source_target_pairs={{0,64},{64,0},{1,65},{65,1},{2,66},{66,2},{3,67},{67,3},{4,68},{68... | collective-permute-start | bytes 1572872 | tf_op jit(solution)/shard_map/ppermute | solution.py:23
  41.0 2.3 %shard_states.2 = (bf16[528,128]{1,0:T(8,128)(2,1)S(1)}, bf16[528,128]{1,0:T(8,128)(2,1)S(1)}, bf16[528,128]{1,0:T(8,128)(2,1)S(1)}, bf16[528,128]{1,0:T(8,128)(2,1)S(1)}) custom-call(s32[6]{0:T(128)S(1)} %stack.27.s, bf16[3,512,512]{2,1,0:T(8,128)(2,1)S(1)} %project.4.qkv_ref, bf16[512,512]{1,0:T(8,128)(2,1)S(1)} %get-tuple-element.249.og_ref, ...), custom_call_target="tpu_custom_call" | custom-call | flops 1 | bytes 1 | tf_op jit(solution)/shard_map/shard_states/pallas_call | solution.py:35
  43.4 7.9 %project.5.qkv_ref = bf16[3,512,512]{2,1,0:T(8,128)(2,1)S(1)} custom-call(s32[6]{0:T(128)S(1)} %stack.27.s, bf16[512,768]{1,0:T(8,128)(2,1)S(1)} %collective-permute-done.1.a.refs_0_.refs_4_, bf16[512,768]{1,0:T(8,128)(2,1)S(1)} %collective-permute-done.6.refs_1_.refs_5_, bf16[256,768]{1,0:T(8,128)(2,1)S(1)} %collective-permute-done.4.refs_2_.refs_0_, ...), custom_call_target="tpu_custom_call" | custom-call | flops 1 | bytes 1 | tf_op jit(solution)/shard_map/project/pallas_call | solution.py:35
  52.1 2.3 %shard_states.3 = (bf16[528,128]{1,0:T(8,128)(2,1)S(1)}, bf16[528,128]{1,0:T(8,128)(2,1)S(1)}, bf16[528,128]{1,0:T(8,128)(2,1)S(1)}, bf16[528,128]{1,0:T(8,128)(2,1)S(1)}) custom-call(s32[6]{0:T(128)S(1)} %stack.27.s, bf16[3,512,512]{2,1,0:T(8,128)(2,1)S(1)} %project.5.qkv_ref, bf16[512,512]{1,0:T(8,128)(2,1)S(1)} %collective-permute-done.8.og_ref, ...), custom_call_target="tpu_custom_call" | custom-call | flops 1 | bytes 1 | tf_op jit(solution)/shard_map/shard_states/pallas_call | solution.py:35
  54.4 3.3 %collective-permute-start.11 = (bf16[528,128]{1,0:T(8,128)(2,1)S(1)}, bf16[528,128]{1,0:T(8,128)(2,1)S(1)}, u32[]{:S(2)}, u32[]{:S(2)}) collective-permute-start(bf16[528,128]{1,0:T(8,128)(2,1)S(1)} %get-tuple-element.157), channel_id=1, source_target_pairs={{0,8},{4,12},{8,0},{12,4},{1,9},{5,13},{9,1},{13,5},{2,10},{6,14},... | collective-permute-start | bytes 405512 | tf_op jit(solution)/shard_map/ppermute | solution.py:23
  58.7 5.9 %local_grads.3 = (bf16[3,512,512]{2,1,0:T(8,128)(2,1)S(1)}, bf16[3,512,512]{2,1,0:T(8,128)(2,1)S(1)}) custom-call(s32[6]{0:T(128)S(1)} %stack.27.s, bf16[3,512,512]{2,1,0:T(8,128)(2,1)S(1)} %project.4.qkv_ref, bf16[512,512]{1,0:T(8,128)(2,1)S(1)} %get-tuple-element.249.og_ref, f32[8,512]{1,0:T(8,128)S(1)} %concatenate.7.refs_5_.cum_ref), custom_call_target="tpu_custom_call" | custom-call | flops 1 | bytes 1 | tf_op jit(solution)/shard_map/local_grads/pallas_call | solution.py:35
  65.4 3.1 %collective-permute-start.16 = (bf16[528,128]{1,0:T(8,128)(2,1)S(1)}, bf16[528,128]{1,0:T(8,128)(2,1)S(1)}, u32[]{:S(2)}, u32[]{:S(2)}) collective-permute-start(bf16[528,128]{1,0:T(8,128)(2,1)S(1)} %get-tuple-element.166.a), channel_id=1, source_target_pairs={{0,32},{16,48},{32,0},{48,16},{1,33},{17,49},{33,1},{49,17},{2,34}... | collective-permute-start | bytes 405512 | tf_op jit(solution)/shard_map/ppermute | solution.py:23
  68.5 1.1 collective-permute-start.15
  69.6 3.2 %local_grads.4 = (bf16[3,512,512]{2,1,0:T(8,128)(2,1)S(1)}, bf16[3,512,512]{2,1,0:T(8,128)(2,1)S(1)}) custom-call(s32[6]{0:T(128)S(1)} %stack.27.s, bf16[3,512,512]{2,1,0:T(8,128)(2,1)S(1)} %project.5.qkv_ref, bf16[512,512]{1,0:T(8,128)(2,1)S(1)} %collective-permute-done.8.og_ref, f32[8,512]{1,0:T(8,128)S(1)} %collective-permute-done.3.refs_10_.cum_ref), custom_call_target="tpu_custom_call" | custom-call | flops 1 | bytes 1 | tf_op jit(solution)/shard_map/local_grads/pallas_call | solution.py:35
  72.8 2.0 %collective-permute-done.15.d = bf16[528,128]{1,0:T(8,128)(2,1)S(1)} collective-permute-done((bf16[528,128]{1,0:T(8,128)(2,1)S(1)}, bf16[528,128]{1,0:T(8,128)(2,1)S(1)}, u32[]{:S(2)}, u32[]{:S(2)}) %collective-permute-start.15) | collective-permute-done | bytes 135200 | tf_op jit(solution)/shard_map/ppermute | solution.py:23
  75.7 3.0 %collective-permute-start.17 = (bf16[512,128]{1,0:T(8,128)(2,1)S(1)}, bf16[512,128]{1,0:T(8,128)(2,1)S(1)}, u32[]{:S(2)}, u32[]{:S(2)}) collective-permute-start(bf16[512,128]{1,0:T(8,128)(2,1)S(1)} %get-tuple-element.177), channel_id=1, source_target_pairs={{0,8},{4,12},{8,0},{12,4},{1,9},{5,13},{9,1},{13,5},{2,10},{6,14},... | collective-permute-start | bytes 393224 | tf_op jit(solution)/shard_map/ppermute | solution.py:23
  79.9 3.2 %local_grads.5 = (bf16[3,512,512]{2,1,0:T(8,128)(2,1)S(1)}, bf16[3,512,512]{2,1,0:T(8,128)(2,1)S(1)}) custom-call(s32[6]{0:T(128)S(1)} %stack.27.s, bf16[3,512,512]{2,1,0:T(8,128)(2,1)S(1)} %project.5.qkv_ref, bf16[512,512]{1,0:T(8,128)(2,1)S(1)} %collective-permute-done.8.og_ref, ...), custom_call_target="tpu_custom_call", output_to_operand_aliasing={{0}: (4, {}), {1}: (5, {})} | custom-call | flops 1 | bytes 1 | tf_op jit(solution)/shard_map/local_grads/pallas_call | solution.py:35
  83.1 2.0 %turn.3 = bf16[16,2,96,512]{3,2,1,0:T(8,128)(2,1)S(1)} custom-call(s32[6]{0:T(128)S(1)} %stack.27.s, bf16[256,768]{1,0:T(8,128)(2,1)S(1)} %collective-permute-done.4.refs_2_.refs_0_, bf16[256,768]{1,0:T(8,128)(2,1)S(1)} %collective-permute-done.5.refs_3_.refs_1_, bf16[256,768]{1,0:T(8,128)(2,1)S(1)} %collective-permute-done.9.refs_4_.refs_2_, ...), custom_call_target="tpu_custom_call" | custom-call | flops 1 | bytes 1 | tf_op jit(solution)/shard_map/turn/pallas_call | solution.py:35
  85.5 4.4 %whole_grads.1 = (bf16[512,768]{1,0:T(8,128)(2,1)S(1)}, bf16[512,768]{1,0:T(8,128)(2,1)S(1)}, bf16[512,768]{1,0:T(8,128)(2,1)S(1)}, bf16[512,768]{1,0:T(8,128)(2,1)S(1)}) custom-call(s32[6]{0:T(128)S(1)} %stack.27.s, bf16[3,512,512]{2,1,0:T(8,128)(2,1)S(1)} %get-tuple-element.196.local_a, bf16[3,512,512]{2,1,0:T(8,128)(2,1)S(1)} %get-tuple-element.197.ready_a, ...), custom_call_target="tpu_custom_call" | custom-call | flops 1 | bytes 1 | tf_op jit(solution)/shard_map/whole_grads/pallas_call | solution.py:35
  90.0 3.2 %weight_part.3 = (bf16[384,768]{1,0:T(8,128)(2,1)S(1)}, bf16[384,768]{1,0:T(8,128)(2,1)S(1)}, bf16[384,768]{1,0:T(8,128)(2,1)S(1)}, bf16[384,768]{1,0:T(8,128)(2,1)S(1)}) custom-call(s32[6]{0:T(128)S(1)} %stack.27.s, bf16[4,4,192,512]{3,2,1,0:T(8,128)(2,1)S(1)} %bitcast.19, bf16[4,4,192,512]{3,2,1,0:T(8,128)(2,1)S(1)} %bitcast.20, ...), custom_call_target="tpu_custom_call" | custom-call | flops 1 | bytes 1 | tf_op jit(solution)/shard_map/weight_part/pallas_call | solution.py:35
  93.2 2.1 %collective-permute-start.21 = (bf16[384,768]{1,0:T(8,128)(2,1)S(1)}, bf16[384,768]{1,0:T(8,128)(2,1)S(1)}, u32[]{:S(2)}, u32[]{:S(2)}) collective-permute-start(bf16[384,768]{1,0:T(8,128)(2,1)S(1)} %get-tuple-element.211), channel_id=1, source_target_pairs={{0,48},{16,32},{32,16},{48,0},{1,49},{17,33},{33,17},{49,1},{2,50}... | collective-permute-start | bytes 1769480 | tf_op jit(solution)/shard_map/ppermute | solution.py:23
  96.2 2.2 %collective-permute-start.25 = (bf16[384,768]{1,0:T(8,128)(2,1)S(1)}, bf16[384,768]{1,0:T(8,128)(2,1)S(1)}, u32[]{:S(2)}, u32[]{:S(2)}) collective-permute-start(bf16[384,768]{1,0:T(8,128)(2,1)S(1)} %get-tuple-element.221), channel_id=1, source_target_pairs={{0,12},{4,8},{8,4},{12,0},{1,13},{5,9},{9,5},{13,1},{2,14},{6,10},... | collective-permute-start | bytes 1769480 | tf_op jit(solution)/shard_map/ppermute | solution.py:23
  98.4 8.4 %weight_part.4 = (bf16[768,768]{1,0:T(8,128)(2,1)S(1)}, bf16[768,768]{1,0:T(8,128)(2,1)S(1)}, bf16[768,768]{1,0:T(8,128)(2,1)S(1)}, bf16[768,768]{1,0:T(8,128)(2,1)S(1)}) custom-call(s32[6]{0:T(128)S(1)} %stack.27.s, bf16[4,4,192,512]{3,2,1,0:T(8,128)(2,1)S(1)} %bitcast.21, bf16[4,4,192,512]{3,2,1,0:T(8,128)(2,1)S(1)} %bitcast.22, ...), custom_call_target="tpu_custom_call" | custom-call | flops 1 | bytes 1 | tf_op jit(solution)/shard_map/weight_part/pallas_call | solution.py:35
  106.8 0.9 collective-permute-done.21.d
  108.6 1.2 collective-permute-start.22
  109.8 1.2 collective-permute-start.23
  111.9 2.0 %collective-permute-start.27 = (bf16[768,768]{1,0:T(8,128)(2,1)S(1)}, bf16[768,768]{1,0:T(8,128)(2,1)S(1)}, u32[]{:S(2)}, u32[]{:S(2)}) collective-permute-start(bf16[768,768]{1,0:T(8,128)(2,1)S(1)} %get-tuple-element.233), channel_id=1, source_target_pairs={{0,12},{4,8},{8,4},{12,0},{1,13},{5,9},{9,5},{13,1},{2,14},{6,10},... | collective-permute-start | bytes 3538952 | tf_op jit(solution)/shard_map/ppermute | solution.py:23
  114.0 3.2 %weight_part.5 = (bf16[768,768]{1,0:T(8,128)(2,1)S(1)}, bf16[768,768]{1,0:T(8,128)(2,1)S(1)}) custom-call(s32[6]{0:T(128)S(1)} %stack.27.s, bf16[4,4,192,512]{3,2,1,0:T(8,128)(2,1)S(1)} %bitcast.23, bf16[4,4,192,512]{3,2,1,0:T(8,128)(2,1)S(1)} %bitcast.24, bf16[4,4,192,512]{3,2,1,0:T(8,128)(2,1)S(1)} %bitcast.29, bf16[4,4,192,512]{3,2,1,0:T(8,128)(2,1)S(1)} %bitcast.30, ...), custom_call_target="tpu_custom_call" | custom-call | flops 1 | bytes 1 | tf_op jit(solution)/shard_map/weight_part/pallas_call | solution.py:35
  117.2 17.9 %collective-permute-done.23.refs_2_ = bf16[768,768]{1,0:T(8,128)(2,1)S(1)} collective-permute-done((bf16[768,768]{1,0:T(8,128)(2,1)S(1)}, bf16[768,768]{1,0:T(8,128)(2,1)S(1)}, u32[]{:S(2)}, u32[]{:S(2)}) %collective-permute-start.23) | collective-permute-done | bytes 1179680 | tf_op jit(solution)/shard_map/ppermute | solution.py:23
  135.0 2.3 %collective-permute-done.27.refs_5_ = bf16[768,768]{1,0:T(8,128)(2,1)S(1)} collective-permute-done((bf16[768,768]{1,0:T(8,128)(2,1)S(1)}, bf16[768,768]{1,0:T(8,128)(2,1)S(1)}, u32[]{:S(2)}, u32[]{:S(2)}) %collective-permute-start.27) | collective-permute-done | bytes 1179680 | tf_op jit(solution)/shard_map/ppermute | solution.py:23
  137.8 1.4 cut_blocks.1
  139.6 1.9 %collective-permute-start.29 = (bf16[192,768]{1,0:T(8,128)(2,1)S(1)}, bf16[192,768]{1,0:T(8,128)(2,1)S(1)}, u32[]{:S(2)}, u32[]{:S(2)}) collective-permute-start(bf16[192,768]{1,0:T(8,128)(2,1)S(1)} %get-tuple-element.236), channel_id=1, source_target_pairs={{0,12},{4,8},{8,4},{12,0},{1,13},{5,9},{9,5},{13,1},{2,14},{6,10},... | collective-permute-start | bytes 884744 | tf_op jit(solution)/shard_map/ppermute | solution.py:23
  141.5 1.9 %collective-permute-start.30 = (bf16[192,768]{1,0:T(8,128)(2,1)S(1)}, bf16[192,768]{1,0:T(8,128)(2,1)S(1)}, u32[]{:S(2)}, u32[]{:S(2)}) collective-permute-start(bf16[192,768]{1,0:T(8,128)(2,1)S(1)} %get-tuple-element.237), channel_id=1, source_target_pairs={{0,8},{4,12},{8,0},{12,4},{1,9},{5,13},{9,1},{13,5},{2,10},{6,14},... | collective-permute-start | bytes 884744 | tf_op jit(solution)/shard_map/ppermute | solution.py:23
  143.4 1.0 collective-permute-start.31
  144.4 1.2 collective-permute-start.32
  145.6 1.2 collective-permute-done.28.b
  146.8 2.0 %collective-permute-start.33 = (bf16[192,768]{1,0:T(8,128)(2,1)S(1)}, bf16[192,768]{1,0:T(8,128)(2,1)S(1)}, u32[]{:S(2)}, u32[]{:S(2)}) collective-permute-start(bf16[192,768]{1,0:T(8,128)(2,1)S(1)} %get-tuple-element.242), channel_id=1, source_target_pairs={{0,32},{16,48},{32,0},{48,16},{1,33},{17,49},{33,1},{49,17},{2,34}... | collective-permute-start | bytes 884744 | tf_op jit(solution)/shard_map/ppermute | solution.py:23
  149.3 1.9 %collective-permute-done.30.d = bf16[192,768]{1,0:T(8,128)(2,1)S(1)} collective-permute-done((bf16[192,768]{1,0:T(8,128)(2,1)S(1)}, bf16[192,768]{1,0:T(8,128)(2,1)S(1)}, u32[]{:S(2)}, u32[]{:S(2)}) %collective-permute-start.30) | collective-permute-done | bytes 294944 | tf_op jit(solution)/shard_map/ppermute | solution.py:23
  151.9 2.3 %collective-permute-start.34 = (bf16[96,768]{1,0:T(8,128)(2,1)S(1)}, bf16[96,768]{1,0:T(8,128)(2,1)S(1)}, u32[]{:S(2)}, u32[]{:S(2)}) collective-permute-start(bf16[96,768]{1,0:T(8,128)(2,1)S(1)} %get-tuple-element.247), channel_id=1, source_target_pairs={{0,64},{64,0},{1,65},{65,1},{2,66},{66,2},{3,67},{67,3},{4,68},{68... | collective-permute-start | bytes 442376 | tf_op jit(solution)/shard_map/ppermute | solution.py:23
  154.2 1.3 collective-permute-done.32.c
  156.2 1.5 collective-permute-start.35
  157.7 0.9 collective-permute-done.34.refs_2_
  158.6 4.3 %collective-permute-done.35.refs_3_ = bf16[96,768]{1,0:T(8,128)(2,1)S(1)} collective-permute-done((bf16[96,768]{1,0:T(8,128)(2,1)S(1)}, bf16[96,768]{1,0:T(8,128)(2,1)S(1)}, u32[]{:S(2)}, u32[]{:S(2)}) %collective-permute-start.35) | collective-permute-done | bytes 147488 | tf_op jit(solution)/shard_map/ppermute | solution.py:23
  162.9 1.6 finish.1
  (61 shorter events, 14.5 us)
Async XLA Ops:
  0.0 10.0 %collective-permute-start.2 = (bf16[512,768]{1,0:T(8,128)(2,1)}, bf16[512,768]{1,0:T(8,128)(2,1)}, u32[]{:S(2)}, u32[]{:S(2)}) collective-permute-start(bf16[512,768]{1,0:T(8,128)(2,1)} %refs_0_.2), channel_id=1, source_target_pairs={{0,1},{1,0},{2,3},{3,2},{4,5},{5,4},{6,7},{7,6},{8,9},{9,8},{10,11... | collective-permute-start | bytes 2359304 | tf_op jit(solution)/shard_map/ppermute | solution.py:23
  0.0 24.1 %collective-permute-start.1 = (bf16[512,768]{1,0:T(8,128)(2,1)}, bf16[512,768]{1,0:T(8,128)(2,1)S(1)}, u32[]{:S(2)}, u32[]{:S(2)}) collective-permute-start(bf16[512,768]{1,0:T(8,128)(2,1)} %refs_0_.2), channel_id=1, source_target_pairs={{0,66},{2,64},{64,2},{66,0},{1,67},{3,65},{65,3},{67,1},{4,70},{6,... | collective-permute-start | bytes 2359304 | tf_op jit(solution)/shard_map/ppermute | solution.py:27
  4.1 20.1 %collective-permute-start = (bf16[512,768]{1,0:T(8,128)(2,1)}, bf16[512,768]{1,0:T(8,128)(2,1)S(1)}, u32[]{:S(2)}, u32[]{:S(2)}) collective-permute-start(bf16[512,768]{1,0:T(8,128)(2,1)} %refs_0_.2), channel_id=1, source_target_pairs={{0,2},{2,0},{1,3},{3,1},{4,6},{6,4},{5,7},{7,5},{8,10},{10,8},{9,1... | collective-permute-start | bytes 2359304 | tf_op jit(solution)/shard_map/ppermute | solution.py:23
  5.5 4.5 %copy-start = (bf16[512,768]{1,0:T(8,128)(2,1)S(1)}, bf16[512,768]{1,0:T(8,128)(2,1)}, u32[]{:S(2)}) copy-start(bf16[512,768]{1,0:T(8,128)(2,1)} %refs_0_.2) | copy-start | bytes 2359300
  7.0 17.1 %collective-permute-start.3 = (f32[8,512]{1,0:T(8,128)S(1)}, f32[8,512]{1,0:T(8,128)S(1)}, u32[]{:S(2)}, u32[]{:S(2)}) collective-permute-start(f32[8,512]{1,0:T(8,128)S(1)} %concatenate.6), channel_id=1, source_target_pairs={{0,64},{64,0},{1,65},{65,1},{2,66},{66,2},{3,67},{67,3},{4,68},{68... | collective-permute-start | bytes 49160 | tf_op jit(solution)/shard_map/ppermute | solution.py:23
  24.2 4.1 %collective-permute-start.7 = (bf16[512,768]{1,0:T(8,128)(2,1)S(1)}, bf16[512,768]{1,0:T(8,128)(2,1)S(1)}, u32[]{:S(2)}, u32[]{:S(2)}) collective-permute-start(bf16[512,768]{1,0:T(8,128)(2,1)S(1)} %collective-permute-done.b.refs_0_.refs_2_), channel_id=1, source_target_pairs={{0,1},{1,0},{2,3},{3,2},{4,5},{5,4},{6,7},{7,6},{8,9},{9,8},{10,11... | collective-permute-start | bytes 2359304 | tf_op jit(solution)/shard_map/ppermute | solution.py:23
  24.2 13.5 %collective-permute-start.6 = (bf16[512,768]{1,0:T(8,128)(2,1)S(1)}, bf16[512,768]{1,0:T(8,128)(2,1)S(1)}, u32[]{:S(2)}, u32[]{:S(2)}) collective-permute-start(bf16[512,768]{1,0:T(8,128)(2,1)S(1)} %collective-permute-done.1.a.refs_0_.refs_4_), channel_id=1, source_target_pairs={{0,1},{1,0},{2,3},{3,2},{4,5},{5,4},{6,7},{7,6},{8,9},{9,8},{10,11... | collective-permute-start | bytes 2359304 | tf_op jit(solution)/shard_map/ppermute | solution.py:23
  25.3 11.5 %collective-permute-start.4 = (bf16[256,768]{1,0:T(8,128)(2,1)S(1)}, bf16[256,768]{1,0:T(8,128)(2,1)S(1)}, u32[]{:S(2)}, u32[]{:S(2)}) collective-permute-start(bf16[256,768]{1,0:T(8,128)(2,1)S(1)} %get-tuple-element.130), channel_id=1, source_target_pairs={{0,2},{2,0},{1,3},{3,1},{4,6},{6,4},{5,7},{7,5},{8,10},{10,8},{9,1... | collective-permute-start | bytes 1179656 | tf_op jit(solution)/shard_map/ppermute | solution.py:23
  25.7 12.0 %collective-permute-start.5 = (bf16[256,768]{1,0:T(8,128)(2,1)S(1)}, bf16[256,768]{1,0:T(8,128)(2,1)S(1)}, u32[]{:S(2)}, u32[]{:S(2)}) collective-permute-start(bf16[256,768]{1,0:T(8,128)(2,1)S(1)} %get-tuple-element.131), channel_id=1, source_target_pairs={{0,66},{2,64},{64,2},{66,0},{1,67},{3,65},{65,3},{67,1},{4,70},{6,... | collective-permute-start | bytes 1179656 | tf_op jit(solution)/shard_map/ppermute | solution.py:27
  37.7 14.4 %collective-permute-start.8 = (bf16[512,512]{1,0:T(8,128)(2,1)S(1)}, bf16[512,512]{1,0:T(8,128)(2,1)S(1)}, u32[]{:S(2)}, u32[]{:S(2)}) collective-permute-start(bf16[512,512]{1,0:T(8,128)(2,1)S(1)} %get-tuple-element.140), channel_id=1, source_target_pairs={{0,64},{64,0},{1,65},{65,1},{2,66},{66,2},{3,67},{67,3},{4,68},{68... | collective-permute-start | bytes 1572872 | tf_op jit(solution)/shard_map/ppermute | solution.py:23
  40.5 2.8 %collective-permute-start.9 = (bf16[256,768]{1,0:T(8,128)(2,1)S(1)}, bf16[256,768]{1,0:T(8,128)(2,1)S(1)}, u32[]{:S(2)}, u32[]{:S(2)}) collective-permute-start(bf16[256,768]{1,0:T(8,128)(2,1)S(1)} %collective-permute-done.4.refs_2_.refs_0_), channel_id=1, source_target_pairs={{0,1},{1,0},{2,3},{3,2},{4,5},{5,4},{6,7},{7,6},{8,9},{9,8},{10,11... | collective-permute-start | bytes 1179656 | tf_op jit(solution)/shard_map/ppermute | solution.py:23
  40.5 2.8 %collective-permute-start.10 = (bf16[256,768]{1,0:T(8,128)(2,1)S(1)}, bf16[256,768]{1,0:T(8,128)(2,1)S(1)}, u32[]{:S(2)}, u32[]{:S(2)}) collective-permute-start(bf16[256,768]{1,0:T(8,128)(2,1)S(1)} %collective-permute-done.5.refs_3_.refs_1_), channel_id=1, source_target_pairs={{0,1},{1,0},{2,3},{3,2},{4,5},{5,4},{6,7},{7,6},{8,9},{9,8},{10,11... | collective-permute-start | bytes 1179656 | tf_op jit(solution)/shard_map/ppermute | solution.py:23
  54.4 10.2 %collective-permute-start.11 = (bf16[528,128]{1,0:T(8,128)(2,1)S(1)}, bf16[528,128]{1,0:T(8,128)(2,1)S(1)}, u32[]{:S(2)}, u32[]{:S(2)}) collective-permute-start(bf16[528,128]{1,0:T(8,128)(2,1)S(1)} %get-tuple-element.157), channel_id=1, source_target_pairs={{0,8},{4,12},{8,0},{12,4},{1,9},{5,13},{9,1},{13,5},{2,10},{6,14},... | collective-permute-start | bytes 405512 | tf_op jit(solution)/shard_map/ppermute | solution.py:23
  57.7 6.9 %collective-permute-start.12 = (bf16[528,128]{1,0:T(8,128)(2,1)S(1)}, bf16[528,128]{1,0:T(8,128)(2,1)S(1)}, u32[]{:S(2)}, u32[]{:S(2)}) collective-permute-start(bf16[528,128]{1,0:T(8,128)(2,1)S(1)} %get-tuple-element.158), channel_id=1, source_target_pairs={{0,4},{4,0},{8,12},{12,8},{1,5},{5,1},{9,13},{13,9},{2,6},{6,2},{1... | collective-permute-start | bytes 405512 | tf_op jit(solution)/shard_map/ppermute | solution.py:23
  58.3 6.3 %collective-permute-start.13 = (bf16[528,128]{1,0:T(8,128)(2,1)S(1)}, bf16[528,128]{1,0:T(8,128)(2,1)S(1)}, u32[]{:S(2)}, u32[]{:S(2)}) collective-permute-start(bf16[528,128]{1,0:T(8,128)(2,1)S(1)} %get-tuple-element.159), channel_id=1, source_target_pairs={{0,12},{4,8},{8,4},{12,0},{1,13},{5,9},{9,5},{13,1},{2,14},{6,10},... | collective-permute-start | bytes 405512 | tf_op jit(solution)/shard_map/ppermute | solution.py:23
  65.4 7.5 %collective-permute-start.16 = (bf16[528,128]{1,0:T(8,128)(2,1)S(1)}, bf16[528,128]{1,0:T(8,128)(2,1)S(1)}, u32[]{:S(2)}, u32[]{:S(2)}) collective-permute-start(bf16[528,128]{1,0:T(8,128)(2,1)S(1)} %get-tuple-element.166.a), channel_id=1, source_target_pairs={{0,32},{16,48},{32,0},{48,16},{1,33},{17,49},{33,1},{49,17},{2,34}... | collective-permute-start | bytes 405512 | tf_op jit(solution)/shard_map/ppermute | solution.py:23
  68.5 6.4 %collective-permute-start.15 = (bf16[528,128]{1,0:T(8,128)(2,1)S(1)}, bf16[528,128]{1,0:T(8,128)(2,1)S(1)}, u32[]{:S(2)}, u32[]{:S(2)}) collective-permute-start(bf16[528,128]{1,0:T(8,128)(2,1)S(1)} %get-tuple-element.166.a), channel_id=1, source_target_pairs={{0,48},{16,32},{32,16},{48,0},{1,49},{17,33},{33,17},{49,1},{2,50}... | collective-permute-start | bytes 405512 | tf_op jit(solution)/shard_map/ppermute | solution.py:23
  69.6 5.3 %collective-permute-start.14 = (bf16[528,128]{1,0:T(8,128)(2,1)S(1)}, bf16[528,128]{1,0:T(8,128)(2,1)S(1)}, u32[]{:S(2)}, u32[]{:S(2)}) collective-permute-start(bf16[528,128]{1,0:T(8,128)(2,1)S(1)} %get-tuple-element.166.a), channel_id=1, source_target_pairs={{0,16},{16,0},{32,48},{48,32},{1,17},{17,1},{33,49},{49,33},{2,18}... | collective-permute-start | bytes 405512 | tf_op jit(solution)/shard_map/ppermute | solution.py:23
  75.7 9.5 %collective-permute-start.17 = (bf16[512,128]{1,0:T(8,128)(2,1)S(1)}, bf16[512,128]{1,0:T(8,128)(2,1)S(1)}, u32[]{:S(2)}, u32[]{:S(2)}) collective-permute-start(bf16[512,128]{1,0:T(8,128)(2,1)S(1)} %get-tuple-element.177), channel_id=1, source_target_pairs={{0,8},{4,12},{8,0},{12,4},{1,9},{5,13},{9,1},{13,5},{2,10},{6,14},... | collective-permute-start | bytes 393224 | tf_op jit(solution)/shard_map/ppermute | solution.py:23
  78.7 6.5 %collective-permute-start.18 = (bf16[512,128]{1,0:T(8,128)(2,1)S(1)}, bf16[512,128]{1,0:T(8,128)(2,1)S(1)}, u32[]{:S(2)}, u32[]{:S(2)}) collective-permute-start(bf16[512,128]{1,0:T(8,128)(2,1)S(1)} %get-tuple-element.178), channel_id=1, source_target_pairs={{0,4},{4,0},{8,12},{12,8},{1,5},{5,1},{9,13},{13,9},{2,6},{6,2},{1... | collective-permute-start | bytes 393224 | tf_op jit(solution)/shard_map/ppermute | solution.py:23
  79.4 6.2 %collective-permute-start.19 = (bf16[512,128]{1,0:T(8,128)(2,1)S(1)}, bf16[512,128]{1,0:T(8,128)(2,1)S(1)}, u32[]{:S(2)}, u32[]{:S(2)}) collective-permute-start(bf16[512,128]{1,0:T(8,128)(2,1)S(1)} %get-tuple-element.179), channel_id=1, source_target_pairs={{0,12},{4,8},{8,4},{12,0},{1,13},{5,9},{9,5},{13,1},{2,14},{6,10},... | collective-permute-start | bytes 393224 | tf_op jit(solution)/shard_map/ppermute | solution.py:23
  93.2 14.6 %collective-permute-start.21 = (bf16[384,768]{1,0:T(8,128)(2,1)S(1)}, bf16[384,768]{1,0:T(8,128)(2,1)S(1)}, u32[]{:S(2)}, u32[]{:S(2)}) collective-permute-start(bf16[384,768]{1,0:T(8,128)(2,1)S(1)} %get-tuple-element.211), channel_id=1, source_target_pairs={{0,48},{16,32},{32,16},{48,0},{1,49},{17,33},{33,17},{49,1},{2,50}... | collective-permute-start | bytes 1769480 | tf_op jit(solution)/shard_map/ppermute | solution.py:23
  95.2 12.5 %collective-permute-start.20 = (bf16[384,768]{1,0:T(8,128)(2,1)S(1)}, bf16[384,768]{1,0:T(8,128)(2,1)S(1)}, u32[]{:S(2)}, u32[]{:S(2)}) collective-permute-start(bf16[384,768]{1,0:T(8,128)(2,1)S(1)} %get-tuple-element.207), channel_id=1, source_target_pairs={{0,16},{16,0},{32,48},{48,32},{1,17},{17,1},{33,49},{49,33},{2,18}... | collective-permute-start | bytes 1769480 | tf_op jit(solution)/shard_map/ppermute | solution.py:23
  95.2 14.6 %collective-permute-start.24 = (bf16[384,768]{1,0:T(8,128)(2,1)S(1)}, bf16[384,768]{1,0:T(8,128)(2,1)S(1)}, u32[]{:S(2)}, u32[]{:S(2)}) collective-permute-start(bf16[384,768]{1,0:T(8,128)(2,1)S(1)} %get-tuple-element.220), channel_id=1, source_target_pairs={{0,4},{4,0},{8,12},{12,8},{1,5},{5,1},{9,13},{13,9},{2,6},{6,2},{1... | collective-permute-start | bytes 1769480 | tf_op jit(solution)/shard_map/ppermute | solution.py:23
  96.2 13.6 %collective-permute-start.25 = (bf16[384,768]{1,0:T(8,128)(2,1)S(1)}, bf16[384,768]{1,0:T(8,128)(2,1)S(1)}, u32[]{:S(2)}, u32[]{:S(2)}) collective-permute-start(bf16[384,768]{1,0:T(8,128)(2,1)S(1)} %get-tuple-element.221), channel_id=1, source_target_pairs={{0,12},{4,8},{8,4},{12,0},{1,13},{5,9},{9,5},{13,1},{2,14},{6,10},... | collective-permute-start | bytes 1769480 | tf_op jit(solution)/shard_map/ppermute | solution.py:23
  108.6 26.4 %collective-permute-start.22 = (bf16[768,768]{1,0:T(8,128)(2,1)S(1)}, bf16[768,768]{1,0:T(8,128)(2,1)S(1)}, u32[]{:S(2)}, u32[]{:S(2)}) collective-permute-start(bf16[768,768]{1,0:T(8,128)(2,1)S(1)} %get-tuple-element.216), channel_id=1, source_target_pairs={{0,16},{16,0},{32,48},{48,32},{1,17},{17,1},{33,49},{49,33},{2,18}... | collective-permute-start | bytes 3538952 | tf_op jit(solution)/shard_map/ppermute | solution.py:23
  109.8 25.2 %collective-permute-start.23 = (bf16[768,768]{1,0:T(8,128)(2,1)S(1)}, bf16[768,768]{1,0:T(8,128)(2,1)S(1)}, u32[]{:S(2)}, u32[]{:S(2)}) collective-permute-start(bf16[768,768]{1,0:T(8,128)(2,1)S(1)} %get-tuple-element.217), channel_id=1, source_target_pairs={{0,48},{16,32},{32,16},{48,0},{1,49},{17,33},{33,17},{49,1},{2,50}... | collective-permute-start | bytes 3538952 | tf_op jit(solution)/shard_map/ppermute | solution.py:23
  111.9 25.4 %collective-permute-start.27 = (bf16[768,768]{1,0:T(8,128)(2,1)S(1)}, bf16[768,768]{1,0:T(8,128)(2,1)S(1)}, u32[]{:S(2)}, u32[]{:S(2)}) collective-permute-start(bf16[768,768]{1,0:T(8,128)(2,1)S(1)} %get-tuple-element.233), channel_id=1, source_target_pairs={{0,12},{4,8},{8,4},{12,0},{1,13},{5,9},{9,5},{13,1},{2,14},{6,10},... | collective-permute-start | bytes 3538952 | tf_op jit(solution)/shard_map/ppermute | solution.py:23
  114.0 23.9 %collective-permute-start.26 = (bf16[768,768]{1,0:T(8,128)(2,1)S(1)}, bf16[768,768]{1,0:T(8,128)(2,1)S(1)}, u32[]{:S(2)}, u32[]{:S(2)}) collective-permute-start(bf16[768,768]{1,0:T(8,128)(2,1)S(1)} %get-tuple-element.224), channel_id=1, source_target_pairs={{0,4},{4,0},{8,12},{12,8},{1,5},{5,1},{9,13},{13,9},{2,6},{6,2},{1... | collective-permute-start | bytes 3538952 | tf_op jit(solution)/shard_map/ppermute | solution.py:23
  139.2 7.6 %collective-permute-start.28 = (bf16[192,768]{1,0:T(8,128)(2,1)S(1)}, bf16[192,768]{1,0:T(8,128)(2,1)S(1)}, u32[]{:S(2)}, u32[]{:S(2)}) collective-permute-start(bf16[192,768]{1,0:T(8,128)(2,1)S(1)} %get-tuple-element.235), channel_id=1, source_target_pairs={{0,4},{4,0},{8,12},{12,8},{1,5},{5,1},{9,13},{13,9},{2,6},{6,2},{1... | collective-permute-start | bytes 884744 | tf_op jit(solution)/shard_map/ppermute | solution.py:23
  139.6 9.7 %collective-permute-start.29 = (bf16[192,768]{1,0:T(8,128)(2,1)S(1)}, bf16[192,768]{1,0:T(8,128)(2,1)S(1)}, u32[]{:S(2)}, u32[]{:S(2)}) collective-permute-start(bf16[192,768]{1,0:T(8,128)(2,1)S(1)} %get-tuple-element.236), channel_id=1, source_target_pairs={{0,12},{4,8},{8,4},{12,0},{1,13},{5,9},{9,5},{13,1},{2,14},{6,10},... | collective-permute-start | bytes 884744 | tf_op jit(solution)/shard_map/ppermute | solution.py:23
  141.5 9.7 %collective-permute-start.30 = (bf16[192,768]{1,0:T(8,128)(2,1)S(1)}, bf16[192,768]{1,0:T(8,128)(2,1)S(1)}, u32[]{:S(2)}, u32[]{:S(2)}) collective-permute-start(bf16[192,768]{1,0:T(8,128)(2,1)S(1)} %get-tuple-element.237), channel_id=1, source_target_pairs={{0,8},{4,12},{8,0},{12,4},{1,9},{5,13},{9,1},{13,5},{2,10},{6,14},... | collective-permute-start | bytes 884744 | tf_op jit(solution)/shard_map/ppermute | solution.py:23
  143.4 10.8 %collective-permute-start.31 = (bf16[192,768]{1,0:T(8,128)(2,1)S(1)}, bf16[192,768]{1,0:T(8,128)(2,1)S(1)}, u32[]{:S(2)}, u32[]{:S(2)}) collective-permute-start(bf16[192,768]{1,0:T(8,128)(2,1)S(1)} %get-tuple-element.240), channel_id=1, source_target_pairs={{0,16},{16,0},{32,48},{48,32},{1,17},{17,1},{33,49},{49,33},{2,18}... | collective-permute-start | bytes 884744 | tf_op jit(solution)/shard_map/ppermute | solution.py:23
  144.4 11.1 %collective-permute-start.32 = (bf16[192,768]{1,0:T(8,128)(2,1)S(1)}, bf16[192,768]{1,0:T(8,128)(2,1)S(1)}, u32[]{:S(2)}, u32[]{:S(2)}) collective-permute-start(bf16[192,768]{1,0:T(8,128)(2,1)S(1)} %get-tuple-element.241), channel_id=1, source_target_pairs={{0,48},{16,32},{32,16},{48,0},{1,49},{17,33},{33,17},{49,1},{2,50}... | collective-permute-start | bytes 884744 | tf_op jit(solution)/shard_map/ppermute | solution.py:23
  146.8 8.7 %collective-permute-start.33 = (bf16[192,768]{1,0:T(8,128)(2,1)S(1)}, bf16[192,768]{1,0:T(8,128)(2,1)S(1)}, u32[]{:S(2)}, u32[]{:S(2)}) collective-permute-start(bf16[192,768]{1,0:T(8,128)(2,1)S(1)} %get-tuple-element.242), channel_id=1, source_target_pairs={{0,32},{16,48},{32,0},{48,16},{1,33},{17,49},{33,1},{49,17},{2,34}... | collective-permute-start | bytes 884744 | tf_op jit(solution)/shard_map/ppermute | solution.py:23
  151.9 6.7 %collective-permute-start.34 = (bf16[96,768]{1,0:T(8,128)(2,1)S(1)}, bf16[96,768]{1,0:T(8,128)(2,1)S(1)}, u32[]{:S(2)}, u32[]{:S(2)}) collective-permute-start(bf16[96,768]{1,0:T(8,128)(2,1)S(1)} %get-tuple-element.247), channel_id=1, source_target_pairs={{0,64},{64,0},{1,65},{65,1},{2,66},{66,2},{3,67},{67,3},{4,68},{68... | collective-permute-start | bytes 442376 | tf_op jit(solution)/shard_map/ppermute | solution.py:23
  156.2 6.7 %collective-permute-start.35 = (bf16[96,768]{1,0:T(8,128)(2,1)S(1)}, bf16[96,768]{1,0:T(8,128)(2,1)S(1)}, u32[]{:S(2)}, u32[]{:S(2)}) collective-permute-start(bf16[96,768]{1,0:T(8,128)(2,1)S(1)} %get-tuple-element.248), channel_id=1, source_target_pairs={{0,64},{64,0},{1,65},{65,1},{2,66},{66,2},{3,67},{67,3},{4,68},{68... | collective-permute-start | bytes 442376 | tf_op jit(solution)/shard_map/ppermute | solution.py:23
